TPU v7x, 32 devices: a whole 2x2x4 slice. The times are simulated.
32 devices in a mesh: groups: 2 (over y), rows: 4 (over z), blocks: 2 (over x), cols: 2 (over core).
Axes of the slice: x: 2, y: 2, z: 4, core: 2. Of those that a mesh axis runs over, the one named last changes fastest.
Arguments:
- inputs: bfloat16 [4096, 1024], P(('groups', 'rows')), parts along dimension 0, may hold values from -6 to 6
- projection: bfloat16 [1024, 8192], P(None, ('groups', 'blocks', 'cols')), parts along dimension 1, may hold values from -0.1875 to 0.1875
- phases: bfloat16 [8192], P(('groups', 'blocks', 'cols')), parts along dimension 0, may hold values from -3.140625 to 3.140625
- inverse_blocks: float32 [4, 2048, 2048], P(('groups', 'blocks'), 'rows'), parts along dimension 0, as said below
- labels: int32 [4096], P(('groups', 'rows')), parts along dimension 0, may hold values from 0 to 999
- predictions: float32 [4096, 1000], P(('groups', 'rows'), 'cols'), parts along dimension 0, may hold values from -4 to 4
- coefficients: float32 [8192, 1000], P(('groups', 'blocks', 'rows'), 'cols'), parts along dimension 0, may hold values from -3 to 3
Outputs:
- new_coefficients: float32 [8192, 1000], P(('groups', 'blocks', 'rows'), 'cols'), parts along dimension 0
- new_predictions: float32 [4096, 1000], P(('groups', 'rows'), 'cols'), parts along dimension 0
There are 2 independent parts, one for each index of `groups`. A program takes and returns all parts, laid end to end along the dimension named above; each array names one. Nothing has to cross between parts.
Inputs may be any that keep to these rules, and one draw needn't show every extreme that they name: `inverse_blocks`: one dense preconditioner for each feature block.
All inputs are finite; a program needn't handle non-finite values.
Results may differ from a plain program's by a relative error of at most 0.0029.
Values may be sent and summed in bfloat16 or wider, within the bound.
No kernel may reach another device: no remote copies, remote signals or barrier semaphores. Data moves between devices by JAX's collectives and lax.ppermute only.
A program may use at most 64 MiB of HBM per device.

v0:
```python
import jax
import jax.numpy as jnp
from jax import lax
from jax.sharding import PartitionSpec as P

DAMPING = 0.5


def cosine_features(inputs, projection, phases):
    angles = (
        jnp.dot(inputs, projection, preferred_element_type=jnp.float32)
        + phases.astype(jnp.float32)[None, :]
    )
    return jnp.cos(angles).astype(jnp.bfloat16)


def shards(inputs, projection, phases, inverse_blocks, labels, predictions, coefficients):
    out_width = predictions.shape[1]
    classes = lax.axis_index("cols") * out_width + jnp.arange(out_width, dtype=jnp.int32)
    onehot = (labels[:, None] == classes[None, :]).astype(jnp.float32)
    residual = (onehot - predictions).astype(jnp.bfloat16)
    half_features = cosine_features(inputs, projection, phases)
    features_full = lax.all_gather(half_features, "cols", axis=1, tiled=True)
    local_inverse = inverse_blocks[0]
    column_slice = features_full
    own_gradient = lax.psum_scatter(
        lax.dot_general(
            column_slice, residual, (((0,), (0,)), ((), ())), preferred_element_type=jnp.float32
        ),
        "rows",
        scatter_dimension=0,
        tiled=True,
    )
    gradient = lax.all_gather(own_gradient, "rows", axis=0, tiled=True)
    solved = jnp.dot(local_inverse, gradient, precision=lax.Precision.HIGHEST)
    step_update = DAMPING * solved
    new_coefficients = coefficients + step_update
    column_slice = features_full
    contribution = jnp.dot(
        column_slice,
        lax.all_gather(step_update.astype(jnp.bfloat16), "rows", axis=0, tiled=True),
        preferred_element_type=jnp.float32,
    )
    summed = lax.psum(contribution, "blocks")
    return (new_coefficients, predictions + summed)


def solution(mesh):
    return jax.shard_map(
        shards,
        mesh=mesh,
        in_specs=(
            P(("groups", "rows"), None),
            P(None, ("groups", "blocks", "cols")),
            P(("groups", "blocks", "cols")),
            P(("groups", "blocks"), "rows", None),
            P(("groups", "rows")),
            P(("groups", "rows"), "cols"),
            P(("groups", "blocks", "rows"), "cols"),
        ),
        out_specs=(P(("groups", "blocks", "rows"), "cols"), P(("groups", "rows"), "cols")),
        check_vma=False,
    )
```

profile of v0, /device:TPU:0, one launch (start us, length us, event | category | flops | bytes accessed | tf_op | source)
XLA Modules:
  0.0 311.2 jit_solution(1773116370345842166)
XLA Ops:
  7.2 0.0 copy-start
  7.2 0.0 all-gather.4.cloned.1.call-start
  7.2 0.8 convert_element_type.15
  8.0 0.7 copy-done
  8.8 0.0 copy-start.1
  8.8 0.0 copy-start.2
  8.8 9.8 %cosine_convert_fusion = bf16[512,1024]{1,0:T(8,128)(2,1)} fusion(bf16[512,1024]{1,0:T(8,128)(2,1)} %param.7, bf16[1024,1024]{1,0:T(8,128)(2,1)S(1)} %copy-done, f32[1024]{0:T(1024)S(1)} %convert_element_type.15), kind=kOutput, calls=%fused_computation.2 | convolution fusion | flops 1074790400 | bytes 4198400 | tf_op jit(solution)/shard_map/dot_general | solution.py:11
  18.6 0.0 all-gather.4.cloned.1.call-update
  18.6 0.0 reduce-scatter.2.cloned.1.call-start
  18.7 13.4 %all-gather.4.cloned.1.call-done = bf16[512,2048]{1,0:T(8,128)(2,1)} async-done(((bf16[512,1024]{1,0:T(8,128)(2,1)}), bf16[512,2048]{1,0:T(8,128)(2,1)}) %all-gather.4.cloned.1.call-update) | async-done | bytes 2097168 | tf_op jit(solution)/shard_map/all_gather | solution.py:23
  32.1 0.0 copy-done.1
  32.1 0.0 copy-done.2
  32.1 5.0 %fusion.8 = f32[2048,500]{1,0:T(8,128)} fusion(bf16[512,2048]{1,0:T(8,128)(2,1)} %all-gather.4.cloned.1.call-done, f32[512,500]{0,1:T(8,128)S(1)} %copy-done.1, s32[512]{0:T(512)S(1)} %copy-done.2, s32[500]{0:T(512)S(1)} %iota_add_fusion), kind=kOutput, calls=%fused_computation.6 | convolution fusion | flops 1049600000 | bytes 7221200 | tf_op jit(solution)/shard_map/dot_general | solution.py:27
  37.0 0.0 reduce-scatter.2.cloned.1.call-update
  37.0 0.0 all-gather.6.cloned.1.call-start
  37.1 78.0 %reduce-scatter.2.cloned.1.call-done = f32[512,500]{1,0:T(8,128)} async-done(((f32[2048,500]{1,0:T(8,128)}), f32[512,500]{1,0:T(8,128)}) %reduce-scatter.2.cloned.1.call-update) | async-done | bytes 1024016 | tf_op jit(solution)/shard_map/reduce_scatter | solution.py:26
  115.1 0.0 all-gather.6.cloned.1.call-update
  115.2 0.2 all-gather.8.cloned.1.call-start
  115.4 82.7 %all-gather.6.cloned.1.call-done = f32[2048,500]{1,0:T(8,128)} async-done(((f32[512,500]{1,0:T(8,128)}), f32[2048,500]{1,0:T(8,128)}) %all-gather.6.cloned.1.call-update) | async-done | bytes 4096016 | tf_op jit(solution)/shard_map/all_gather | solution.py:34
  198.1 17.2 %fusion.11 = (bf16[512,500]{0,1:T(8,128)(2,1)}, f32[512,500]{0,1:T(8,128)}) fusion(f32[512,500]{0,1:T(8,128)} %param.13, f32[2048,500]{1,0:T(8,128)} %all-gather.6.cloned.1.call-done, f32[1,512,2048]{2,1,0:T(8,128)} %param.10), kind=kOutput, calls=%fused_computation.10 | convolution fusion | flops 6292224000 | bytes 10850304 | tf_op jit(solution)/shard_map/dot_general | solution.py:35
  215.3 0.0 all-gather.8.cloned.1.call-update
  215.3 0.0 all-reduce.2.cloned.1.call-start
  215.4 43.9 %all-gather.8.cloned.1.call-done = bf16[2048,500]{0,1:T(8,128)(2,1)} async-done(((bf16[512,500]{0,1:T(8,128)(2,1)}), bf16[2048,500]{0,1:T(8,128)(2,1)}) %all-gather.8.cloned.1.call-update) | async-done | bytes 2048016 | tf_op jit(solution)/shard_map/all_gather | solution.py:41
  259.3 4.4 %fusion.12 = f32[512,500]{0,1:T(8,128)} fusion(bf16[512,2048]{1,0:T(8,128)(2,1)} %all-gather.4.cloned.1.call-done, bf16[2048,500]{0,1:T(8,128)(2,1)} %all-gather.8.cloned.1.call-done), kind=kOutput, calls=%fused_computation.11 | convolution fusion | flops 1048576000 | bytes 5169152 | tf_op jit(solution)/shard_map/dot_general | solution.py:39
  263.7 0.0 all-reduce.2.cloned.1.call-update
  263.8 38.6 %all-reduce.2.cloned.1.call-done = f32[512,500]{0,1:T(8,128)} async-done(((f32[512,500]{0,1:T(8,128)}), f32[512,500]{0,1:T(8,128)}) %all-reduce.2.cloned.1.call-update) | async-done | bytes 1024016 | tf_op jit(solution)/shard_map/psum | solution.py:44
  302.3 2.4 add.33
  (1 shorter events, 0.0 us)
Async XLA Ops:
  7.2 1.6 copy-start
  7.2 24.9 %all-gather.4.cloned.1.call-start = ((), (), s32[]{:S(2)}) async-start(), calls=%async_computation.1 | async-start | bytes 3145728 | tf_op jit(solution)/shard_map/all_gather | solution.py:23
  8.8 23.3 %copy-start.1 = (f32[512,500]{0,1:T(8,128)S(1)}, f32[512,500]{0,1:T(8,128)}, u32[]{:S(2)}) copy-start(f32[512,500]{0,1:T(8,128)} %param.12) | copy-start | bytes 3072004
  8.8 23.3 %copy-start.2 = (s32[512]{0:T(512)S(1)}, s32[512]{0:T(512)}, u32[]{:S(2)}) copy-start(s32[512]{0:T(512)} %param.11) | copy-start | bytes 6148
  18.6 96.5 %reduce-scatter.2.cloned.1.call-start = ((), (), s32[]{:S(2)}) async-start(), calls=%async_computation.2 | async-start | bytes 5242880 | tf_op jit(solution)/shard_map/reduce_scatter | solution.py:26
  37.0 161.1 %all-gather.6.cloned.1.call-start = ((), (), s32[]{:S(2)}) async-start(), calls=%async_computation.3 | async-start | bytes 5242880 | tf_op jit(solution)/shard_map/all_gather | solution.py:34
  115.2 144.1 %all-gather.8.cloned.1.call-start = ((), (), s32[]{:S(2)}) async-start(), calls=%async_computation.4 | async-start | bytes 2580480 | tf_op jit(solution)/shard_map/all_gather | solution.py:41
  215.3 87.0 %all-reduce.2.cloned.1.call-start = ((), (), s32[]{:S(2)}) async-start(), calls=%async_computation.5 | async-start | bytes 2064384 | tf_op jit(solution)/shard_map/psum | solution.py:44
Sparse Core Ops, SparseCore 0:
  18.7 13.2 all-gather.3
  37.2 77.9 reduce-scatter.1
  116.8 81.2 all-gather.5
  215.4 43.8 all-gather.7
  263.9 38.3 all-reduce.1
where the time goes:
time: 311 us
  waiting for transfers between devices  257 us (83%)
  matrix products  36.4 us (12%)
  between operations  13.8 us (4%)
  other arithmetic  3.21 us (1%)
    all_gather x1, waiting for transfers between devices, shards(): gradient = lax.all_gather(own_gradient, 'rows', axis=0, tiled=True)  82.7 us
    reduce_scatter x1, waiting for transfers between devices, shards(): lax.psum_scatter(lax.dot_general(column_slice, residual, (((0,), (0,)), (...  78 us
    all_gather x1, waiting for transfers between devices, shards(): lax.all_gather(step_update.astype(jnp.bfloat16), 'rows', axis=0, tiled=True)  43.9 us
    psum x1, waiting for transfers between devices, shards(): summed = lax.psum(contribution, 'blocks')  38.6 us
    dot_general x1, matrix products, shards(): solved = jnp.dot(local_inverse, gradient, precision=lax.Precision.HIGHEST)  17.2 us
    all_gather x1, waiting for transfers between devices, shards(): features_full = lax.all_gather(half_features, 'cols', axis=1, tiled=True)  13.4 us
    dot_general x1, matrix products, cosine_features(): jnp.dot(inputs, projection, preferred_element_type=jnp.float32)  9.81 us
  transfers between devices with their start and end apart: 5, of which 5 were waited for; matrix products, arithmetic and copies ran while one was open for 0% of the time, Pallas kernels for 0%

commit v1 on v0

v1 whole, which is shorter than its diff:
```python
import functools

import jax
import jax.numpy as jnp
from jax import lax
from jax.experimental import pallas as pl
from jax.experimental.pallas import tpu as pltpu
from jax.sharding import PartitionSpec as P

DAMPING = 0.5
F32, BF16 = jnp.float32, jnp.bfloat16
LANES = 128

COS_TERMS = (
    0.9999999887556631, -0.49999988843399, 0.04166648574334225, -0.001388778673619495,
    2.4769518189949842e-05, -2.7075418374484127e-07, 1.7231808612122658e-09,
)
INV_TWO_PI = 0.15915494309189535
TWO_PI_HIGH = 6.28125
TWO_PI_LOW = 0.0019353071795864769


def cosine(angles):
    turns = jnp.round(angles * INV_TWO_PI)
    rest = (angles - turns * TWO_PI_HIGH) - turns * TWO_PI_LOW
    square = rest * rest
    result = jnp.full_like(square, COS_TERMS[-1])
    for term in COS_TERMS[-2::-1]:
        result = result * square + term
    return result


def dot(a, b):
    return jnp.dot(a, b, preferred_element_type=F32)


def dot_nt(a, b):
    return lax.dot_general(a, b, (((1,), (1,)), ((), ())), preferred_element_type=F32)


def params(n_grid, vmem_mib=48):
    return pltpu.CompilerParams(
        dimension_semantics=("arbitrary",) * n_grid, vmem_limit_bytes=vmem_mib << 20
    )


def residual_kernel(place, labels, predictions, out, wide):
    width = predictions.shape[1]
    wide[...] = jnp.zeros_like(wide)
    wide[:, :width] = predictions[...]
    flipped = wide[...].T
    classes = lax.broadcasted_iota(jnp.int32, flipped.shape, 0)
    hit = (classes + place[2] * width == labels[0]).astype(F32)
    out[...] = jnp.where(classes < width, hit - flipped, 0.0).astype(BF16)


def residual_block(place, labels, predictions, padded, rows):
    width = predictions.shape[1]
    part = rows // 2
    pick = lambda j, p: 2 * p[1] + (j ^ p[2])
    return pl.pallas_call(
        residual_kernel,
        out_shape=jax.ShapeDtypeStruct((padded, rows), BF16),
        grid_spec=pltpu.PrefetchScalarGridSpec(
            num_scalar_prefetch=1,
            grid=(2,),
            in_specs=[
                pl.BlockSpec((1, 1, part), lambda j, p: (pick(j, p), 0, 0)),
                pl.BlockSpec((part, width), lambda j, p: (pick(j, p), 0)),
            ],
            out_specs=pl.BlockSpec((padded, part), lambda j, p: (0, j)),
            scratch_shapes=[pltpu.VMEM((part, padded), F32)],
        ),
        compiler_params=params(1),
        name="residual",
    )(place, labels.reshape(-1, 1, part), predictions)


def features_kernel(n_rows, tiles, place, *refs):
    rows, (w_own, w_other, p_own, p_other, out) = refs[:n_rows], refs[n_rows:]
    step = pl.program_id(0)

    def body(weights, phases):
        start = 0
        for ref in rows:
            angles = dot(ref[...], weights[...]) + phases[...].astype(F32)
            out[start:start + ref.shape[0], :] = cosine(angles).astype(BF16)
            start += ref.shape[0]

    @pl.when(step < tiles)
    def _():
        body(w_own, p_own)

    @pl.when(step >= tiles)
    def _():
        body(w_other, p_other)


def features(place, rows, weights, phases, tile=512):
    depth, half = weights[0].shape
    tiles = half // tile
    total = sum(r.shape[0] for r in rows)
    own = lambda i, p: (0, jnp.minimum(i, tiles - 1))
    other = lambda i, p: (0, jnp.maximum(i - tiles, 0))

    def where(i, p):
        second = (i >= tiles).astype(jnp.int32)
        return (0, (p[2] ^ second) * tiles + (i - second * tiles))

    return pl.pallas_call(
        functools.partial(features_kernel, len(rows), tiles),
        out_shape=jax.ShapeDtypeStruct((total, 2 * half), BF16),
        grid_spec=pltpu.PrefetchScalarGridSpec(
            num_scalar_prefetch=1,
            grid=(2 * tiles,),
            in_specs=[pl.BlockSpec(r.shape, lambda i, p: (0, 0)) for r in rows]
            + [
                pl.BlockSpec((depth, tile), own),
                pl.BlockSpec((depth, tile), other),
                pl.BlockSpec((1, tile), own),
                pl.BlockSpec((1, tile), other),
            ],
            out_specs=pl.BlockSpec((total, tile), where),
        ),
        compiler_params=params(1),
        name="features",
    )(place, *rows, *weights, *phases)


def joined(pieces, part):
    sides = [[r[:, i * part:(i + 1) * part] for r in pieces] for i in (0, 1)]
    return [s[0] if len(s) == 1 else jnp.concatenate(s, axis=1) for s in sides]


def gradient_of(groups, refs, part):
    total, at = None, 0
    for count, stacked in groups:
        pieces = [refs[at + i][...] for i in range(count)]
        if stacked:
            pieces = [jnp.concatenate(pieces, axis=0)]
        first, second = joined(pieces, part)
        mine, theirs = refs[at + count][...], refs[at + count + 1][...]
        at += count + 2
        if first.shape[1] < 256:
            products = [dot(jnp.concatenate([first, second], axis=1), jnp.concatenate([mine, theirs], axis=0))]
        else:
            products = [dot(first, mine), dot(second, theirs)]
        for product in products:
            total = product if total is None else total + product
    return total


def flat(groups):
    return [a for pieces, mine, theirs in groups for a in (*pieces, mine, theirs)]


def shape_of(groups, stacked):
    return [(len(g[0]), s) for g, s in zip(groups, stacked)]


def group_specs(groups, tile):
    specs = []
    for pieces, mine, theirs in groups:
        specs += [pl.BlockSpec(r.shape, lambda k: (0, 0)) for r in pieces]
        specs += [pl.BlockSpec((f.shape[0], tile), lambda k: (0, k)) for f in (mine, theirs)]
    return specs


def gradient_kernel(form, part, *refs):
    refs[-1][...] = gradient_of(form, refs[:-1], part)


def gradient(groups, stacked, part, padded, tile=512):
    n_feat = groups[0][1].shape[1]
    return pl.pallas_call(
        functools.partial(gradient_kernel, shape_of(groups, stacked), part),
        out_shape=jax.ShapeDtypeStruct((padded, n_feat), F32),
        grid=(n_feat // tile,),
        in_specs=group_specs(groups, tile),
        out_specs=pl.BlockSpec((padded, tile), lambda k: (0, k)),
        compiler_params=params(1),
        name="gradient",
    )(*flat(groups))


def high_low(x):
    high = x.astype(BF16)
    return high, (x - high.astype(F32)).astype(BF16)


def solve_kernel(form, part, *refs):
    *pieces, partial_gradient, inverse, coefficients, new, sent, total = refs
    k = pl.program_id(0)
    g_high, g_low = high_low(partial_gradient[...] + gradient_of(form, pieces, part))
    p_high, p_low = high_low(inverse[...])
    product = dot_nt(p_high, g_high) + (dot_nt(p_low, g_high) + dot_nt(p_high, g_low))

    @pl.when(k == 0)
    def _():
        total[...] = product

    @pl.when(k > 0)
    def _():
        total[...] += product

    @pl.when(k == pl.num_programs(0) - 1)
    def _():
        update = DAMPING * total[...]
        new[...] = coefficients[...] + update[:, :new.shape[1]]
        sent[...] = update.astype(BF16)


def solve(groups, stacked, part, partial_gradient, inverse, coefficients, tile=512):
    padded, n_feat = partial_gradient.shape
    slice_rows, width = coefficients.shape
    return pl.pallas_call(
        functools.partial(solve_kernel, shape_of(groups, stacked), part),
        out_shape=(
            jax.ShapeDtypeStruct((slice_rows, width), F32),
            jax.ShapeDtypeStruct((slice_rows, padded), BF16),
        ),
        grid=(n_feat // tile,),
        in_specs=group_specs(groups, tile)
        + [
            pl.BlockSpec((padded, tile), lambda k: (0, k)),
            pl.BlockSpec((slice_rows, tile), lambda k: (0, k)),
            pl.BlockSpec((slice_rows, width), lambda k: (0, 0)),
        ],
        out_specs=(
            pl.BlockSpec((slice_rows, width), lambda k: (0, 0)),
            pl.BlockSpec((slice_rows, padded), lambda k: (0, 0)),
        ),
        scratch_shapes=[pltpu.VMEM((slice_rows, padded), F32)],
        compiler_params=params(1),
        name="solve",
    )(*flat(groups), partial_gradient, inverse, coefficients)


def change(body, place, mine, theirs, sent, received, out_shapes, name):
    depth = sent.shape[0]
    own_slice = lambda i, p: (0, p[0])
    whole = lambda i, p: (0, 0)

    def kernel(place, *refs):
        body(*refs)

    return pl.pallas_call(
        kernel,
        out_shape=tuple(jax.ShapeDtypeStruct(s, BF16) for s in out_shapes),
        grid_spec=pltpu.PrefetchScalarGridSpec(
            num_scalar_prefetch=1,
            grid=(1,),
            in_specs=[pl.BlockSpec((f.shape[0], depth), own_slice) for f in (mine, theirs)]
            + [pl.BlockSpec(a.shape, whole) for a in (sent, *received)],
            out_specs=tuple(pl.BlockSpec(s, whole) for s in out_shapes),
        ),
        compiler_params=params(1),
        name=name,
    )(place, mine, theirs, sent, *received)


def far_body(mine, theirs, sent, a, b):
    a[...] = dot(mine[...], sent[...]).astype(BF16)
    b[...] = dot(theirs[...], sent[...]).astype(BF16)


def third_body(mine, theirs, sent, in_e, in_o, out_e, out_o):
    part = in_e.shape[0]
    mine, theirs = dot(mine[...], sent[...]), dot(theirs[...], sent[...])
    out_e[:part] = mine[:part].astype(BF16)
    out_e[part:] = (theirs[:part] + in_o[...].astype(F32)).astype(BF16)
    out_o[:part] = (mine[part:] + in_e[...].astype(F32)).astype(BF16)
    out_o[part:] = theirs[part:].astype(BF16)


def middle_body(mine, theirs, sent, in_e, in_o, out_e, out_o):
    part = in_e.shape[0] // 2
    mine, theirs = dot(mine[...], sent[...]), dot(theirs[...], sent[...])
    came_e, came_o = in_e[...].astype(F32), in_o[...].astype(F32)
    out_e[:part] = (mine[:part] + came_e[:part]).astype(BF16)
    out_e[part:] = (theirs[:part] + came_e[part:]).astype(BF16)
    out_o[:part] = (mine[part:] + came_o[:part]).astype(BF16)
    out_o[part:] = (theirs[part:] + came_o[part:]).astype(BF16)


def last_body(mine, theirs, sent, in_e, in_o, out):
    part = mine.shape[0]
    came = in_e[...].astype(F32) + in_o[...].astype(F32)
    out[:part] = (dot(mine[...], sent[...]) + came[:part]).astype(BF16)
    out[part:] = (dot(theirs[...], sent[...]) + came[part:]).astype(BF16)


def apply_kernel(place, predictions, own, other, new):
    width = new.shape[1]
    mine = pl.program_id(0) // 2 == place[1]

    @pl.when(mine)
    def _():
        new[...] = predictions[...] + own[:, :width].astype(F32)

    @pl.when(jnp.logical_not(mine))
    def _():
        new[...] = predictions[...] + other[:, :width].astype(F32)


def apply_change(place, predictions, own, other):
    rows, width = predictions.shape
    part = rows // 4
    whole = lambda i, p: (i, 0)
    source = lambda i, p: ((i % 2) ^ p[2], 0)
    return pl.pallas_call(
        apply_kernel,
        out_shape=jax.ShapeDtypeStruct((rows, width), F32),
        grid_spec=pltpu.PrefetchScalarGridSpec(
            num_scalar_prefetch=1,
            grid=(4,),
            in_specs=[
                pl.BlockSpec((part, width), whole),
                pl.BlockSpec((part, own.shape[1]), source),
                pl.BlockSpec((part, own.shape[1]), source),
            ],
            out_specs=pl.BlockSpec((part, width), whole),
        ),
        compiler_params=params(1),
        name="apply",
    )(place, predictions, own, other)


def swap(x, axes, pairs):
    return lax.ppermute(x, axes, [p for a, b in pairs for p in ((a, b), (b, a))])


def ring_shards(n_rows, inputs, projection, phases, inverse_blocks, labels, predictions, coefficients):
    ring = [2 * z for z in range(n_rows)] + [2 * z + 1 for z in reversed(range(n_rows))]
    size = len(ring)
    even = [(ring[i], ring[i + 1]) for i in range(0, size, 2)]
    odd = [(ring[i], ring[(i + 1) % size]) for i in range(1, size, 2)]
    E = lambda x: swap(x, ("rows", "blocks"), even)
    O = lambda x: swap(x, ("rows", "blocks"), odd)
    C = lambda x: swap(x, "cols", [(0, 1)])

    z, x, c = (lax.axis_index(a) for a in ("rows", "blocks", "cols"))
    place = jnp.stack([z, x, c]).astype(jnp.int32)
    local_rows, width = predictions.shape
    part = local_rows // 4
    padded = -(-width // LANES) * LANES

    weights = (projection, C(projection))
    phases = phases[None, :]
    phases = (phases, C(phases))

    x0 = lax.dynamic_slice_in_dim(inputs, (2 * x + c) * part, part, 0)
    r0 = residual_block(place, labels, predictions, padded, 2 * part)

    def around(own):
        half = own.shape[0] // 2
        e1, o1 = E(own), O(own)
        e2, o2 = E(o1), O(e1)
        e3, o3 = E(o2), O(e2)
        e4, o4 = E(o3[:half]), O(e3[half:])
        return (e1, o1), (e2, o2), (e3, o3), (e4, o4)

    xs = ((x0,),) + around(x0)
    rs = ((r0,),) + around(r0)
    groups = []
    for rows_in, residual_in in zip(xs, rs):
        mine = features(place, rows_in, weights, phases)
        groups.append((residual_in, mine, C(mine)))
    partial_gradient = gradient(groups[:3], (False,) * 3, part, padded)
    new_coefficients, sent = solve(
        groups[3:], (False, True), part, partial_gradient, inverse_blocks[0], coefficients
    )

    step = lambda body, k, received, shapes, name: change(
        body, place, groups[k][1], groups[k][2], sent, received, shapes, name
    )
    piece, block = (part, padded), (2 * part, padded)
    a4, b4 = step(far_body, 4, (), (piece, piece), "far")
    e3, o3 = step(third_body, 3, (E(a4), O(b4)), (block, block), "third")
    e2, o2 = step(middle_body, 2, (O(o3), E(e3)), (block, block), "second")
    e1, o1 = step(middle_body, 1, (O(o2), E(e2)), (block, block), "first")
    (own,) = step(last_body, 0, (E(e1), O(o1)), (block,), "last")
    other = swap(own, "blocks", [(0, 1)])
    return new_coefficients, apply_change(place, predictions, own, other)


def plain_shards(inputs, projection, phases, inverse_blocks, labels, predictions, coefficients):
    out_width = predictions.shape[1]
    classes = lax.axis_index("cols") * out_width + jnp.arange(out_width, dtype=jnp.int32)
    onehot = (labels[:, None] == classes[None, :]).astype(F32)
    residual = (onehot - predictions).astype(BF16)
    angles = dot(inputs, projection) + phases.astype(F32)[None, :]
    half_features = jnp.cos(angles).astype(BF16)
    features_full = lax.all_gather(half_features, "cols", axis=1, tiled=True)
    own_gradient = lax.psum_scatter(
        lax.dot_general(features_full, residual, (((0,), (0,)), ((), ())), preferred_element_type=F32),
        "rows", scatter_dimension=0, tiled=True,
    )
    gradient_full = lax.all_gather(own_gradient, "rows", axis=0, tiled=True)
    update = DAMPING * jnp.dot(inverse_blocks[0], gradient_full, precision=lax.Precision.HIGHEST)
    sent = lax.all_gather(update.astype(BF16), "rows", axis=0, tiled=True)
    summed = lax.psum(dot(features_full, sent), "blocks")
    return coefficients + update, predictions + summed


def solution(mesh):
    n_rows, n_blocks = mesh.shape["rows"], mesh.shape["blocks"]
    small_ring = n_blocks == 2 and n_rows == 4 and mesh.shape["cols"] == 2
    shards = functools.partial(ring_shards, n_rows) if small_ring else plain_shards
    return jax.shard_map(
        shards,
        mesh=mesh,
        in_specs=(
            P(("groups", "rows"), None),
            P(None, ("groups", "blocks", "cols")),
            P(("groups", "blocks", "cols")),
            P(("groups", "blocks"), "rows", None),
            P(("groups", "rows")),
            P(("groups", "rows"), "cols"),
            P(("groups", "blocks", "rows"), "cols"),
        ),
        out_specs=(P(("groups", "blocks", "rows"), "cols"), P(("groups", "rows"), "cols")),
        check_vma=False,
    )
```

time: 311 us -> 148 us (0.48)
  waiting for transfers between devices: 257 us -> 36.7 us
  Pallas kernels: 0 us -> 54.9 us
  matrix products: 36.4 us -> 0 us
  starting transfers between devices: 0.38 us -> 31.1 us
  local copies, waits for them, and re-layouts: 0.74 us -> 23.5 us
  between operations: 13.8 us -> 0.99 us
  other arithmetic: 3.21 us -> 0.08 us
    all_gather x3 -> x0, waiting for transfers between devices: 140 us -> none  [the longest x1 82.7 us: shards(): gradient = lax.all_gather(own_gradient, 'rows', axis=0, tiled=True)]
    reduce_scatter x1 -> x0, waiting for transfers between devices: 78 us -> none  [shards(): lax.psum_scatter(lax.dot_general(column_slice, residual, (((0,), (0,)), (...]
    pallas_call x0 -> x14, Pallas kernels: none -> 54.9 us  [the longest x5 28.4 us: features(): pl.pallas_call(functools.partial(features_kernel, len(rows), tiles), out_...]
    psum x1 -> x0, waiting for transfers between devices: 38.6 us -> none  [shards(): summed = lax.psum(contribution, 'blocks')]
    ppermute x0 -> x32, waiting for transfers between devices: none -> 36.7 us  [swap(): lax.ppermute(x, axes, [p for a, b in pairs for p in ((a, b), (b, a))])]
    dot_general x4 -> x0, matrix products: 36.4 us -> none  [the longest x1 17.2 us: shards(): solved = jnp.dot(local_inverse, gradient, precision=lax.Precision.HIGHEST)]
    ppermute x0 -> x32, starting transfers between devices: none -> 31.1 us  [swap(): lax.ppermute(x, axes, [p for a, b in pairs for p in ((a, b), (b, a))])]
    unnamed x6 -> x70, local copies, waits for them, and re-layouts: 0.74 us -> 22.7 us
  transfers between devices with their start and end apart: 5 -> 32, of which waited for: 5 -> 13; matrix products, arithmetic and copies ran while one was open for 0% -> 5% of each run, Pallas kernels for 0% -> 24%
where the time goes in v1:
time: 148 us; the launch traced here: 147 us
  Pallas kernels  54.9 us (37%)
  waiting for transfers between devices  36.7 us (25%)
  starting transfers between devices  31.1 us (21%)
  local copies, waits for them, and re-layouts  23.5 us (16%)
    ppermute x32, waiting for transfers between devices, swap(): lax.ppermute(x, axes, [p for a, b in pairs for p in ((a, b), (b, a))])  36.7 us
    ppermute x32, starting transfers between devices, swap(): lax.ppermute(x, axes, [p for a, b in pairs for p in ((a, b), (b, a))])  31.1 us
    pallas_call x5, Pallas kernels, features(): pl.pallas_call(functools.partial(features_kernel, len(rows), tiles), out_...  28.4 us
    unnamed x70, local copies, waits for them, and re-layouts  22.7 us
    pallas_call x1, Pallas kernels, solve(): pl.pallas_call(functools.partial(solve_kernel, shape_of(groups, stacked),...  9.05 us
    pallas_call x5, Pallas kernels, change(): pl.pallas_call(kernel, out_shape=tuple((jax.ShapeDtypeStruct(s, BF16) for...  7.66 us
    pallas_call x1, Pallas kernels, gradient(): pl.pallas_call(functools.partial(gradient_kernel, shape_of(groups, stacke...  6.34 us
  transfers between devices with their start and end apart: 32, of which 13 were waited for; matrix products, arithmetic and copies ran while one was open for 5% of the time, Pallas kernels for 24%

profile of v1, /device:TPU:0, one launch (start us, length us, event | category | flops | bytes accessed | tf_op | source)
XLA Modules:
  0.0 147.2 jit_solution(9498058606453276805)
XLA Ops:
  1.9 3.0 %collective-permute-start.9 = (bf16[128,1024]{1,0:T(8,128)(2,1)S(1)}, bf16[128,1024]{1,0:T(8,128)(2,1)}, u32[]{:S(2)}, u32[]{:S(2)}) collective-permute-start(bf16[128,1024]{1,0:T(8,128)(2,1)S(1)} %constant_dynamic-slice_fusion.refs_0_), channel_id=1, source_target_pairs={{4,8},{8,4},{12,14},{14,12},{10,6},{6,10},{2,0},{0,2},{5,9},{9,5},... | collective-permute-start | bytes 786440 | tf_op jit(solution)/shard_map/ppermute | solution.py:330
  4.9 1.7 %collective-permute-start.6 = (bf16[128,1024]{1,0:T(8,128)(2,1)S(1)}, bf16[128,1024]{1,0:T(8,128)(2,1)}, u32[]{:S(2)}, u32[]{:S(2)}) collective-permute-start(bf16[128,1024]{1,0:T(8,128)(2,1)S(1)} %constant_dynamic-slice_fusion.refs_0_), channel_id=1, source_target_pairs={{0,4},{4,0},{8,12},{12,8},{14,10},{10,14},{6,2},{2,6},{1,5},{5,1},... | collective-permute-start | bytes 786440 | tf_op jit(solution)/shard_map/ppermute | solution.py:330
  6.5 2.6 %copy.9.predictions = f32[512,500]{1,0:T(8,128)} copy(f32[512,500]{0,1:T(8,128)} %param.12) | data formatting | bytes 2048000 | tf_op args[5]
  13.5 1.6 %collective-permute-start.10 = (bf16[128,1024]{1,0:T(8,128)(2,1)}, bf16[128,1024]{1,0:T(8,128)(2,1)S(1)}, u32[]{:S(2)}, u32[]{:S(2)}) collective-permute-start(bf16[128,1024]{1,0:T(8,128)(2,1)} %collective-permute-done.9.refs_1_), channel_id=1, source_target_pairs={{0,4},{4,0},{8,12},{12,8},{14,10},{10,14},{6,2},{2,6},{1,5},{5,1},... | collective-permute-start | bytes 786440 | tf_op jit(solution)/shard_map/ppermute | solution.py:330
  18.8 2.5 %collective-permute-done.3.refs_4_ = bf16[512,256]{1,0:T(8,128)(2,1)S(1)} collective-permute-done((bf16[512,256]{1,0:T(8,128)(2,1)S(1)}, bf16[512,256]{1,0:T(8,128)(2,1)S(1)}, u32[]{:S(2)}, u32[]{:S(2)}) %collective-permute-start.3) | collective-permute-done | bytes 262176 | tf_op jit(solution)/shard_map/ppermute | solution.py:330
  22.9 4.0 %collective-permute-done.7.refs_1_ = bf16[128,1024]{1,0:T(8,128)(2,1)S(1)} collective-permute-done((bf16[128,1024]{1,0:T(8,128)(2,1)}, bf16[128,1024]{1,0:T(8,128)(2,1)S(1)}, u32[]{:S(2)}, u32[]{:S(2)}) %collective-permute-start.7) | collective-permute-done | bytes 262176 | tf_op jit(solution)/shard_map/ppermute | solution.py:330
  28.5 5.6 %features.8.refs_5_.refs_0_ = bf16[256,2048]{1,0:T(8,128)(2,1)S(1)} custom-call(s32[3]{0:T(128)S(1)} %pad_add_fusion.place, bf16[128,1024]{1,0:T(8,128)(2,1)} %collective-permute-done.6.refs_0_, bf16[128,1024]{1,0:T(8,128)(2,1)} %collective-permute-done.9.refs_1_, bf16[1024,1024]{1,0:T(8,128)(2,1)S(1)} %copy-done.1, ...), custom_call_target="tpu_custom_call" | custom-call | tf_op jit(solution)/shard_map/features/pallas_call | solution.py:110
  35.7 6.2 %features.9.refs_9_.refs_0_ = bf16[256,2048]{1,0:T(8,128)(2,1)} custom-call(s32[3]{0:T(128)S(1)} %pad_add_fusion.place, bf16[128,1024]{1,0:T(8,128)(2,1)S(1)} %collective-permute-done.10.refs_0_, bf16[128,1024]{1,0:T(8,128)(2,1)S(1)} %collective-permute-done.7.refs_1_, bf16[1024,1024]{1,0:T(8,128)(2,1)S(1)} %copy-done.1, ...), custom_call_target="tpu_custom_call" | custom-call | tf_op jit(solution)/shard_map/features/pallas_call | solution.py:110
  42.2 6.2 %features.5.refs_2_.refs_0_ = bf16[256,2048]{1,0:T(8,128)(2,1)} custom-call(s32[3]{0:T(128)S(1)} %pad_add_fusion.place, bf16[128,1024]{1,0:T(8,128)(2,1)S(1)} %collective-permute-done.8.refs_0_, bf16[128,1024]{1,0:T(8,128)(2,1)S(1)} %collective-permute-done.11.refs_1_, bf16[1024,1024]{1,0:T(8,128)(2,1)S(1)} %copy-done.1, ...), custom_call_target="tpu_custom_call" | custom-call | tf_op jit(solution)/shard_map/features/pallas_call | solution.py:110
  48.7 1.8 %collective-permute-start.17 = (bf16[64,1024]{1,0:T(8,128)(2,1)S(1)}, bf16[64,1024]{1,0:T(8,128)(2,1)S(1)}, u32[]{:S(2)}, u32[]{:S(2)}) collective-permute-start(bf16[64,1024]{1,0:T(8,128)(2,1)S(1)} %slice.18), channel_id=1, source_target_pairs={{0,4},{4,0},{8,12},{12,8},{14,10},{10,14},{6,2},{2,6},{1,5},{5,1},... | collective-permute-start | bytes 393224 | tf_op jit(solution)/shard_map/ppermute | solution.py:330
  51.4 3.0 %collective-permute-done.17.refs_0_ = bf16[64,1024]{1,0:T(8,128)(2,1)S(1)} collective-permute-done((bf16[64,1024]{1,0:T(8,128)(2,1)S(1)}, bf16[64,1024]{1,0:T(8,128)(2,1)S(1)}, u32[]{:S(2)}, u32[]{:S(2)}) %collective-permute-start.17) | collective-permute-done | bytes 131104 | tf_op jit(solution)/shard_map/ppermute | solution.py:330
  54.4 1.7 %collective-permute-start.2 = (bf16[512,256]{1,0:T(8,128)(2,1)S(1)}, bf16[512,256]{1,0:T(8,128)(2,1)S(1)}, u32[]{:S(2)}, u32[]{:S(2)}) collective-permute-start(bf16[512,256]{1,0:T(8,128)(2,1)S(1)} %collective-permute-done.1.refs_8_), channel_id=1, source_target_pairs={{0,4},{4,0},{8,12},{12,8},{14,10},{10,14},{6,2},{2,6},{1,5},{5,1},... | collective-permute-start | bytes 786440 | tf_op jit(solution)/shard_map/ppermute | solution.py:330
  56.2 4.6 %features.7.refs_1_.refs_0_ = bf16[128,2048]{1,0:T(8,128)(2,1)S(1)} custom-call(s32[3]{0:T(128)S(1)} %pad_add_fusion.place, bf16[128,1024]{1,0:T(8,128)(2,1)S(1)} %constant_dynamic-slice_fusion.refs_0_, bf16[1024,1024]{1,0:T(8,128)(2,1)S(1)} %copy-done.1, bf16[1024,1024]{1,0:T(8,128)(2,1)} %collective-permute-done.12.refs_3_.refs_2_, ...), custom_call_target="tpu_custom_call" | custom-call | tf_op jit(solution)/shard_map/features/pallas_call | solution.py:110
  60.9 5.8 %features.6.refs_6_.refs_0_ = bf16[128,2048]{1,0:T(8,128)(2,1)} custom-call(s32[3]{0:T(128)S(1)} %pad_add_fusion.place, bf16[64,1024]{1,0:T(8,128)(2,1)S(1)} %collective-permute-done.17.refs_0_, bf16[64,1024]{1,0:T(8,128)(2,1)S(1)} %collective-permute-done.18.refs_1_, bf16[1024,1024]{1,0:T(8,128)(2,1)S(1)} %copy-done.1, ...), custom_call_target="tpu_custom_call" | custom-call | tf_op jit(solution)/shard_map/features/pallas_call | solution.py:110
  70.1 2.6 %copy.10.refs_10_ = f32[512,500]{1,0:T(8,128)} copy(f32[512,500]{0,1:T(8,128)} %param.13) | data formatting | bytes 2048000 | tf_op args[6]
  81.0 6.3 %gradient.1.refs_8_ = f32[512,2048]{1,0:T(8,128)} custom-call(bf16[512,256]{1,0:T(8,128)(2,1)S(1)} %copy-done.17, bf16[128,2048]{1,0:T(8,128)(2,1)S(1)} %copy-done.8, bf16[128,2048]{1,0:T(8,128)(2,1)S(1)} %copy-done.14, bf16[512,256]{1,0:T(8,128)(2,1)S(1)} %copy-done.25, bf16[512,256]{1,0:T(8,128)(2,1)S(1)} %copy-done.23, bf16[256,2048]{1,0:T(8,128)(2,1)S(1)} %copy-done.5, ...), custom_call_target="tpu_custom_call" | custom-call | tf_op jit(solution)/shard_map/gradient/pallas_call | solution.py:175
  89.0 9.1 %solve.1 = (f32[512,500]{1,0:T(8,128)S(1)}, bf16[512,512]{1,0:T(8,128)(2,1)S(1)}) custom-call(bf16[512,256]{1,0:T(8,128)(2,1)S(1)} %copy-done.21, bf16[512,256]{1,0:T(8,128)(2,1)S(1)} %copy-done.19, bf16[256,2048]{1,0:T(8,128)(2,1)} %features.5.refs_2_.refs_0_, bf16[256,2048]{1,0:T(8,128)(2,1)} %collective-permute-done.14.refs_3_.refs_1_, ...), custom_call_target="tpu_custom_call" | custom-call | tf_op jit(solution)/shard_map/solve/pallas_call | solution.py:216
  98.1 1.8 %far.1 = (bf16[128,512]{1,0:T(8,128)(2,1)S(1)}, bf16[128,512]{1,0:T(8,128)(2,1)S(1)}) custom-call(s32[3]{0:T(128)S(1)} %pad_add_fusion.place, bf16[128,2048]{1,0:T(8,128)(2,1)} %features.6.refs_6_.refs_0_, bf16[128,2048]{1,0:T(8,128)(2,1)S(1)} %collective-permute-done.19.refs_7_.refs_1_, bf16[512,512]{1,0:T(8,128)(2,1)S(1)} %get-tuple-element.13.refs_2_), custom_call_target="tpu_custom_call" | custom-call | tf_op jit(solution)/shard_map/far/pallas_call | solution.py:247
  99.9 1.7 %collective-permute-start.23 = (bf16[128,512]{1,0:T(8,128)(2,1)S(1)}, bf16[128,512]{1,0:T(8,128)(2,1)S(1)}, u32[]{:S(2)}, u32[]{:S(2)}) collective-permute-start(bf16[128,512]{1,0:T(8,128)(2,1)S(1)} %get-tuple-element.14), channel_id=1, source_target_pairs={{0,4},{4,0},{8,12},{12,8},{14,10},{10,14},{6,2},{2,6},{1,5},{5,1},... | collective-permute-start | bytes 393224 | tf_op jit(solution)/shard_map/ppermute | solution.py:330
  102.1 2.8 %collective-permute-done.23.refs_3_ = bf16[128,512]{1,0:T(8,128)(2,1)S(1)} collective-permute-done((bf16[128,512]{1,0:T(8,128)(2,1)S(1)}, bf16[128,512]{1,0:T(8,128)(2,1)S(1)}, u32[]{:S(2)}, u32[]{:S(2)}) %collective-permute-start.23) | collective-permute-done | bytes 131104 | tf_op jit(solution)/shard_map/ppermute | solution.py:330
  104.9 1.6 %collective-permute-done.24.refs_4_ = bf16[128,512]{1,0:T(8,128)(2,1)S(1)} collective-permute-done((bf16[128,512]{1,0:T(8,128)(2,1)S(1)}, bf16[128,512]{1,0:T(8,128)(2,1)S(1)}, u32[]{:S(2)}, u32[]{:S(2)}) %collective-permute-start.24) | collective-permute-done | bytes 131104 | tf_op jit(solution)/shard_map/ppermute | solution.py:330
  106.5 2.0 %third.1 = (bf16[256,512]{1,0:T(8,128)(2,1)S(1)}, bf16[256,512]{1,0:T(8,128)(2,1)S(1)}) custom-call(s32[3]{0:T(128)S(1)} %pad_add_fusion.place, bf16[256,2048]{1,0:T(8,128)(2,1)} %features.5.refs_2_.refs_0_, bf16[256,2048]{1,0:T(8,128)(2,1)} %collective-permute-done.14.refs_3_.refs_1_, bf16[512,512]{1,0:T(8,128)(2,1)S(1)} %get-tuple-element.13.refs_2_, ...), custom_call_target="tpu_custom_call" | custom-call | tf_op jit(solution)/shard_map/third/pallas_call | solution.py:247
  109.2 1.7 %collective-permute-start.26 = (bf16[256,512]{1,0:T(8,128)(2,1)S(1)}, bf16[256,512]{1,0:T(8,128)(2,1)S(1)}, u32[]{:S(2)}, u32[]{:S(2)}) collective-permute-start(bf16[256,512]{1,0:T(8,128)(2,1)S(1)} %get-tuple-element.17), channel_id=1, source_target_pairs={{0,4},{4,0},{8,12},{12,8},{14,10},{10,14},{6,2},{2,6},{1,5},{5,1},... | collective-permute-start | bytes 786440 | tf_op jit(solution)/shard_map/ppermute | solution.py:330
  110.8 4.3 %collective-permute-done.25.refs_3_ = bf16[256,512]{1,0:T(8,128)(2,1)S(1)} collective-permute-done((bf16[256,512]{1,0:T(8,128)(2,1)S(1)}, bf16[256,512]{1,0:T(8,128)(2,1)S(1)}, u32[]{:S(2)}, u32[]{:S(2)}) %collective-permute-start.25) | collective-permute-done | bytes 262176 | tf_op jit(solution)/shard_map/ppermute | solution.py:330
  115.6 2.0 %second.1 = (bf16[256,512]{1,0:T(8,128)(2,1)S(1)}, bf16[256,512]{1,0:T(8,128)(2,1)S(1)}) custom-call(s32[3]{0:T(128)S(1)} %pad_add_fusion.place, bf16[256,2048]{1,0:T(8,128)(2,1)} %features.9.refs_9_.refs_0_, bf16[256,2048]{1,0:T(8,128)(2,1)} %collective-permute-done.22.refs_10_.refs_1_, bf16[512,512]{1,0:T(8,128)(2,1)S(1)} %get-tuple-element.13.refs_2_, ...), custom_call_target="tpu_custom_call" | custom-call | tf_op jit(solution)/shard_map/second/pallas_call | solution.py:247
  119.6 4.5 %collective-permute-done.27.refs_3_ = bf16[256,512]{1,0:T(8,128)(2,1)S(1)} collective-permute-done((bf16[256,512]{1,0:T(8,128)(2,1)S(1)}, bf16[256,512]{1,0:T(8,128)(2,1)S(1)}, u32[]{:S(2)}, u32[]{:S(2)}) %collective-permute-start.27) | collective-permute-done | bytes 262176 | tf_op jit(solution)/shard_map/ppermute | solution.py:330
  124.0 1.6 %collective-permute-done.28.refs_4_ = bf16[256,512]{1,0:T(8,128)(2,1)S(1)} collective-permute-done((bf16[256,512]{1,0:T(8,128)(2,1)S(1)}, bf16[256,512]{1,0:T(8,128)(2,1)S(1)}, u32[]{:S(2)}, u32[]{:S(2)}) %collective-permute-start.28) | collective-permute-done | bytes 262176 | tf_op jit(solution)/shard_map/ppermute | solution.py:330
  128.8 4.3 %collective-permute-done.29.refs_3_ = bf16[256,512]{1,0:T(8,128)(2,1)S(1)} collective-permute-done((bf16[256,512]{1,0:T(8,128)(2,1)S(1)}, bf16[256,512]{1,0:T(8,128)(2,1)S(1)}, u32[]{:S(2)}, u32[]{:S(2)}) %collective-permute-start.29) | collective-permute-done | bytes 262176 | tf_op jit(solution)/shard_map/ppermute | solution.py:330
  133.1 2.8 %collective-permute-done.30.refs_4_ = bf16[256,512]{1,0:T(8,128)(2,1)S(1)} collective-permute-done((bf16[256,512]{1,0:T(8,128)(2,1)S(1)}, bf16[256,512]{1,0:T(8,128)(2,1)S(1)}, u32[]{:S(2)}, u32[]{:S(2)}) %collective-permute-start.30) | collective-permute-done | bytes 262176 | tf_op jit(solution)/shard_map/ppermute | solution.py:330
  136.8 1.6 %collective-permute-start.31 = (bf16[256,512]{1,0:T(8,128)(2,1)S(1)}, bf16[256,512]{1,0:T(8,128)(2,1)}, u32[]{:S(2)}, u32[]{:S(2)}) collective-permute-start(bf16[256,512]{1,0:T(8,128)(2,1)S(1)} %last.1.own), channel_id=1, source_target_pairs={{0,2},{2,0},{1,3},{3,1},{4,6},{6,4},{5,7},{7,5},{8,10},{10,8},{9,1... | collective-permute-start | bytes 786440 | tf_op jit(solution)/shard_map/ppermute | solution.py:330
  139.7 3.7 %collective-permute-done.31.other = bf16[256,512]{1,0:T(8,128)(2,1)} collective-permute-done((bf16[256,512]{1,0:T(8,128)(2,1)S(1)}, bf16[256,512]{1,0:T(8,128)(2,1)}, u32[]{:S(2)}, u32[]{:S(2)}) %collective-permute-start.31) | collective-permute-done | bytes 262176 | tf_op jit(solution)/shard_map/ppermute | solution.py:330
  143.3 2.5 %apply.1 = f32[512,500]{1,0:T(8,128)S(1)} custom-call(s32[3]{0:T(128)S(1)} %pad_add_fusion.place, f32[512,500]{1,0:T(8,128)S(1)} %copy-done.3, bf16[256,512]{1,0:T(8,128)(2,1)S(1)} %last.1.own, bf16[256,512]{1,0:T(8,128)(2,1)} %collective-permute-done.31.other), custom_call_target="tpu_custom_call" | custom-call | tf_op jit(solution)/shard_map/apply/pallas_call | solution.py:311
  (123 shorter events, 39.1 us)
Async XLA Ops:
  0.7 27.8 %collective-permute-start.12 = (bf16[1024,1024]{1,0:T(8,128)(2,1)}, bf16[1024,1024]{1,0:T(8,128)(2,1)}, u32[]{:S(2)}, u32[]{:S(2)}) collective-permute-start(bf16[1024,1024]{1,0:T(8,128)(2,1)} %refs_2_.7), channel_id=1, source_target_pairs={{0,1},{1,0},{2,3},{3,2},{4,5},{5,4},{6,7},{7,6},{8,9},{9,8},{10,11... | collective-permute-start | bytes 6291464 | tf_op jit(solution)/shard_map/ppermute | solution.py:330
  1.9 11.7 %collective-permute-start.9 = (bf16[128,1024]{1,0:T(8,128)(2,1)S(1)}, bf16[128,1024]{1,0:T(8,128)(2,1)}, u32[]{:S(2)}, u32[]{:S(2)}) collective-permute-start(bf16[128,1024]{1,0:T(8,128)(2,1)S(1)} %constant_dynamic-slice_fusion.refs_0_), channel_id=1, source_target_pairs={{4,8},{8,4},{12,14},{14,12},{10,6},{6,10},{2,0},{0,2},{5,9},{9,5},... | collective-permute-start | bytes 786440 | tf_op jit(solution)/shard_map/ppermute | solution.py:330
  4.9 10.2 %collective-permute-start.6 = (bf16[128,1024]{1,0:T(8,128)(2,1)S(1)}, bf16[128,1024]{1,0:T(8,128)(2,1)}, u32[]{:S(2)}, u32[]{:S(2)}) collective-permute-start(bf16[128,1024]{1,0:T(8,128)(2,1)S(1)} %constant_dynamic-slice_fusion.refs_0_), channel_id=1, source_target_pairs={{0,4},{4,0},{8,12},{12,8},{14,10},{10,14},{6,2},{2,6},{1,5},{5,1},... | collective-permute-start | bytes 786440 | tf_op jit(solution)/shard_map/ppermute | solution.py:330
  12.0 9.3 %collective-permute-start.3 = (bf16[512,256]{1,0:T(8,128)(2,1)S(1)}, bf16[512,256]{1,0:T(8,128)(2,1)S(1)}, u32[]{:S(2)}, u32[]{:S(2)}) collective-permute-start(bf16[512,256]{1,0:T(8,128)(2,1)S(1)} %residual.1.refs_0_), channel_id=1, source_target_pairs={{4,8},{8,4},{12,14},{14,12},{10,6},{6,10},{2,0},{0,2},{5,9},{9,5},... | collective-permute-start | bytes 786440 | tf_op jit(solution)/shard_map/ppermute | solution.py:330
  13.5 8.8 %collective-permute-start.10 = (bf16[128,1024]{1,0:T(8,128)(2,1)}, bf16[128,1024]{1,0:T(8,128)(2,1)S(1)}, u32[]{:S(2)}, u32[]{:S(2)}) collective-permute-start(bf16[128,1024]{1,0:T(8,128)(2,1)} %collective-permute-done.9.refs_1_), channel_id=1, source_target_pairs={{0,4},{4,0},{8,12},{12,8},{14,10},{10,14},{6,2},{2,6},{1,5},{5,1},... | collective-permute-start | bytes 786440 | tf_op jit(solution)/shard_map/ppermute | solution.py:330
  15.1 11.8 %collective-permute-start.7 = (bf16[128,1024]{1,0:T(8,128)(2,1)}, bf16[128,1024]{1,0:T(8,128)(2,1)S(1)}, u32[]{:S(2)}, u32[]{:S(2)}) collective-permute-start(bf16[128,1024]{1,0:T(8,128)(2,1)} %collective-permute-done.6.refs_0_), channel_id=1, source_target_pairs={{4,8},{8,4},{12,14},{14,12},{10,6},{6,10},{2,0},{0,2},{5,9},{9,5},... | collective-permute-start | bytes 786440 | tf_op jit(solution)/shard_map/ppermute | solution.py:330
  16.3 1.2 collective-permute-start.13
  17.5 10.4 %collective-permute-start = (bf16[512,256]{1,0:T(8,128)(2,1)S(1)}, bf16[512,256]{1,0:T(8,128)(2,1)S(1)}, u32[]{:S(2)}, u32[]{:S(2)}) collective-permute-start(bf16[512,256]{1,0:T(8,128)(2,1)S(1)} %residual.1.refs_0_), channel_id=1, source_target_pairs={{0,4},{4,0},{8,12},{12,8},{14,10},{10,14},{6,2},{2,6},{1,5},{5,1},... | collective-permute-start | bytes 786440 | tf_op jit(solution)/shard_map/ppermute | solution.py:330
  21.3 12.9 %collective-permute-start.4 = (bf16[512,256]{1,0:T(8,128)(2,1)S(1)}, bf16[512,256]{1,0:T(8,128)(2,1)S(1)}, u32[]{:S(2)}, u32[]{:S(2)}) collective-permute-start(bf16[512,256]{1,0:T(8,128)(2,1)S(1)} %collective-permute-done.3.refs_4_), channel_id=1, source_target_pairs={{0,4},{4,0},{8,12},{12,8},{14,10},{10,14},{6,2},{2,6},{1,5},{5,1},... | collective-permute-start | bytes 786440 | tf_op jit(solution)/shard_map/ppermute | solution.py:330
  22.3 19.6 %collective-permute-start.11 = (bf16[128,1024]{1,0:T(8,128)(2,1)S(1)}, bf16[128,1024]{1,0:T(8,128)(2,1)S(1)}, u32[]{:S(2)}, u32[]{:S(2)}) collective-permute-start(bf16[128,1024]{1,0:T(8,128)(2,1)S(1)} %collective-permute-done.10.refs_0_), channel_id=1, source_target_pairs={{4,8},{8,4},{12,14},{14,12},{10,6},{6,10},{2,0},{0,2},{5,9},{9,5},... | collective-permute-start | bytes 786440 | tf_op jit(solution)/shard_map/ppermute | solution.py:330
  26.9 15.3 %collective-permute-start.8 = (bf16[128,1024]{1,0:T(8,128)(2,1)S(1)}, bf16[128,1024]{1,0:T(8,128)(2,1)S(1)}, u32[]{:S(2)}, u32[]{:S(2)}) collective-permute-start(bf16[128,1024]{1,0:T(8,128)(2,1)S(1)} %collective-permute-done.7.refs_1_), channel_id=1, source_target_pairs={{0,4},{4,0},{8,12},{12,8},{14,10},{10,14},{6,2},{2,6},{1,5},{5,1},... | collective-permute-start | bytes 786440 | tf_op jit(solution)/shard_map/ppermute | solution.py:330
  27.9 20.8 %collective-permute-start.1 = (bf16[512,256]{1,0:T(8,128)(2,1)S(1)}, bf16[512,256]{1,0:T(8,128)(2,1)S(1)}, u32[]{:S(2)}, u32[]{:S(2)}) collective-permute-start(bf16[512,256]{1,0:T(8,128)(2,1)S(1)} %collective-permute-done.refs_3_), channel_id=1, source_target_pairs={{4,8},{8,4},{12,14},{14,12},{10,6},{6,10},{2,0},{0,2},{5,9},{9,5},... | collective-permute-start | bytes 786440 | tf_op jit(solution)/shard_map/ppermute | solution.py:330
  34.1 34.3 %collective-permute-start.21 = (bf16[256,2048]{1,0:T(8,128)(2,1)S(1)}, bf16[256,2048]{1,0:T(8,128)(2,1)S(1)}, u32[]{:S(2)}, u32[]{:S(2)}) collective-permute-start(bf16[256,2048]{1,0:T(8,128)(2,1)S(1)} %features.8.refs_5_.refs_0_), channel_id=1, source_target_pairs={{0,1},{1,0},{2,3},{3,2},{4,5},{5,4},{6,7},{7,6},{8,9},{9,8},{10,11... | collective-permute-start | bytes 3145736 | tf_op jit(solution)/shard_map/ppermute | solution.py:330
  34.2 16.4 %collective-permute-start.5 = (bf16[512,256]{1,0:T(8,128)(2,1)S(1)}, bf16[512,256]{1,0:T(8,128)(2,1)S(1)}, u32[]{:S(2)}, u32[]{:S(2)}) collective-permute-start(bf16[512,256]{1,0:T(8,128)(2,1)S(1)} %collective-permute-done.4.refs_7_), channel_id=1, source_target_pairs={{4,8},{8,4},{12,14},{14,12},{10,6},{6,10},{2,0},{0,2},{5,9},{9,5},... | collective-permute-start | bytes 786440 | tf_op jit(solution)/shard_map/ppermute | solution.py:330
  41.9 30.8 %collective-permute-start.22 = (bf16[256,2048]{1,0:T(8,128)(2,1)}, bf16[256,2048]{1,0:T(8,128)(2,1)}, u32[]{:S(2)}, u32[]{:S(2)}) collective-permute-start(bf16[256,2048]{1,0:T(8,128)(2,1)} %features.9.refs_9_.refs_0_), channel_id=1, source_target_pairs={{0,1},{1,0},{2,3},{3,2},{4,5},{5,4},{6,7},{7,6},{8,9},{9,8},{10,11... | collective-permute-start | bytes 3145736 | tf_op jit(solution)/shard_map/ppermute | solution.py:330
  48.4 39.7 %collective-permute-start.14 = (bf16[256,2048]{1,0:T(8,128)(2,1)}, bf16[256,2048]{1,0:T(8,128)(2,1)}, u32[]{:S(2)}, u32[]{:S(2)}) collective-permute-start(bf16[256,2048]{1,0:T(8,128)(2,1)} %features.5.refs_2_.refs_0_), channel_id=1, source_target_pairs={{0,1},{1,0},{2,3},{3,2},{4,5},{5,4},{6,7},{7,6},{8,9},{9,8},{10,11... | collective-permute-start | bytes 3145736 | tf_op jit(solution)/shard_map/ppermute | solution.py:330
  48.7 5.7 %collective-permute-start.17 = (bf16[64,1024]{1,0:T(8,128)(2,1)S(1)}, bf16[64,1024]{1,0:T(8,128)(2,1)S(1)}, u32[]{:S(2)}, u32[]{:S(2)}) collective-permute-start(bf16[64,1024]{1,0:T(8,128)(2,1)S(1)} %slice.18), channel_id=1, source_target_pairs={{0,4},{4,0},{8,12},{12,8},{14,10},{10,14},{6,2},{2,6},{1,5},{5,1},... | collective-permute-start | bytes 393224 | tf_op jit(solution)/shard_map/ppermute | solution.py:330
  50.6 10.2 %collective-permute-start.18 = (bf16[64,1024]{1,0:T(8,128)(2,1)S(1)}, bf16[64,1024]{1,0:T(8,128)(2,1)S(1)}, u32[]{:S(2)}, u32[]{:S(2)}) collective-permute-start(bf16[64,1024]{1,0:T(8,128)(2,1)S(1)} %slice.19), channel_id=1, source_target_pairs={{4,8},{8,4},{12,14},{14,12},{10,6},{6,10},{2,0},{0,2},{5,9},{9,5},... | collective-permute-start | bytes 393224 | tf_op jit(solution)/shard_map/ppermute | solution.py:330
  54.4 12.3 %collective-permute-start.2 = (bf16[512,256]{1,0:T(8,128)(2,1)S(1)}, bf16[512,256]{1,0:T(8,128)(2,1)S(1)}, u32[]{:S(2)}, u32[]{:S(2)}) collective-permute-start(bf16[512,256]{1,0:T(8,128)(2,1)S(1)} %collective-permute-done.1.refs_8_), channel_id=1, source_target_pairs={{0,4},{4,0},{8,12},{12,8},{14,10},{10,14},{6,2},{2,6},{1,5},{5,1},... | collective-permute-start | bytes 786440 | tf_op jit(solution)/shard_map/ppermute | solution.py:330
  60.8 6.5 %collective-permute-start.20 = (bf16[128,2048]{1,0:T(8,128)(2,1)S(1)}, bf16[128,2048]{1,0:T(8,128)(2,1)S(1)}, u32[]{:S(2)}, u32[]{:S(2)}) collective-permute-start(bf16[128,2048]{1,0:T(8,128)(2,1)S(1)} %features.7.refs_1_.refs_0_), channel_id=1, source_target_pairs={{0,1},{1,0},{2,3},{3,2},{4,5},{5,4},{6,7},{7,6},{8,9},{9,8},{10,11... | collective-permute-start | bytes 1572872 | tf_op jit(solution)/shard_map/ppermute | solution.py:330
  66.7 21.3 %collective-permute-start.19 = (bf16[128,2048]{1,0:T(8,128)(2,1)}, bf16[128,2048]{1,0:T(8,128)(2,1)S(1)}, u32[]{:S(2)}, u32[]{:S(2)}) collective-permute-start(bf16[128,2048]{1,0:T(8,128)(2,1)} %features.6.refs_6_.refs_0_), channel_id=1, source_target_pairs={{0,1},{1,0},{2,3},{3,2},{4,5},{5,4},{6,7},{7,6},{8,9},{9,8},{10,11... | collective-permute-start | bytes 1572872 | tf_op jit(solution)/shard_map/ppermute | solution.py:330
  68.1 19.3 %collective-permute-start.15 = (bf16[256,256]{1,0:T(8,128)(2,1)S(1)}, bf16[256,256]{1,0:T(8,128)(2,1)S(1)}, u32[]{:S(2)}, u32[]{:S(2)}) collective-permute-start(bf16[256,256]{1,0:T(8,128)(2,1)S(1)} %slice.16), channel_id=1, source_target_pairs={{0,4},{4,0},{8,12},{12,8},{14,10},{10,14},{6,2},{2,6},{1,5},{5,1},... | collective-permute-start | bytes 393224 | tf_op jit(solution)/shard_map/ppermute | solution.py:330
  69.4 18.0 %collective-permute-start.16 = (bf16[256,256]{1,0:T(8,128)(2,1)S(1)}, bf16[256,256]{1,0:T(8,128)(2,1)S(1)}, u32[]{:S(2)}, u32[]{:S(2)}) collective-permute-start(bf16[256,256]{1,0:T(8,128)(2,1)S(1)} %slice.17), channel_id=1, source_target_pairs={{4,8},{8,4},{12,14},{14,12},{10,6},{6,10},{2,0},{0,2},{5,9},{9,5},... | collective-permute-start | bytes 393224 | tf_op jit(solution)/shard_map/ppermute | solution.py:330
  99.9 5.0 %collective-permute-start.23 = (bf16[128,512]{1,0:T(8,128)(2,1)S(1)}, bf16[128,512]{1,0:T(8,128)(2,1)S(1)}, u32[]{:S(2)}, u32[]{:S(2)}) collective-permute-start(bf16[128,512]{1,0:T(8,128)(2,1)S(1)} %get-tuple-element.14), channel_id=1, source_target_pairs={{0,4},{4,0},{8,12},{12,8},{14,10},{10,14},{6,2},{2,6},{1,5},{5,1},... | collective-permute-start | bytes 393224 | tf_op jit(solution)/shard_map/ppermute | solution.py:330
  101.5 5.0 %collective-permute-start.24 = (bf16[128,512]{1,0:T(8,128)(2,1)S(1)}, bf16[128,512]{1,0:T(8,128)(2,1)S(1)}, u32[]{:S(2)}, u32[]{:S(2)}) collective-permute-start(bf16[128,512]{1,0:T(8,128)(2,1)S(1)} %get-tuple-element.15), channel_id=1, source_target_pairs={{4,8},{8,4},{12,14},{14,12},{10,6},{6,10},{2,0},{0,2},{5,9},{9,5},... | collective-permute-start | bytes 393224 | tf_op jit(solution)/shard_map/ppermute | solution.py:330
  108.5 6.6 %collective-permute-start.25 = (bf16[256,512]{1,0:T(8,128)(2,1)S(1)}, bf16[256,512]{1,0:T(8,128)(2,1)S(1)}, u32[]{:S(2)}, u32[]{:S(2)}) collective-permute-start(bf16[256,512]{1,0:T(8,128)(2,1)S(1)} %get-tuple-element.16), channel_id=1, source_target_pairs={{4,8},{8,4},{12,14},{14,12},{10,6},{6,10},{2,0},{0,2},{5,9},{9,5},... | collective-permute-start | bytes 786440 | tf_op jit(solution)/shard_map/ppermute | solution.py:330
  109.2 6.4 %collective-permute-start.26 = (bf16[256,512]{1,0:T(8,128)(2,1)S(1)}, bf16[256,512]{1,0:T(8,128)(2,1)S(1)}, u32[]{:S(2)}, u32[]{:S(2)}) collective-permute-start(bf16[256,512]{1,0:T(8,128)(2,1)S(1)} %get-tuple-element.17), channel_id=1, source_target_pairs={{0,4},{4,0},{8,12},{12,8},{14,10},{10,14},{6,2},{2,6},{1,5},{5,1},... | collective-permute-start | bytes 786440 | tf_op jit(solution)/shard_map/ppermute | solution.py:330
  117.6 6.4 %collective-permute-start.27 = (bf16[256,512]{1,0:T(8,128)(2,1)S(1)}, bf16[256,512]{1,0:T(8,128)(2,1)S(1)}, u32[]{:S(2)}, u32[]{:S(2)}) collective-permute-start(bf16[256,512]{1,0:T(8,128)(2,1)S(1)} %get-tuple-element.18), channel_id=1, source_target_pairs={{4,8},{8,4},{12,14},{14,12},{10,6},{6,10},{2,0},{0,2},{5,9},{9,5},... | collective-permute-start | bytes 786440 | tf_op jit(solution)/shard_map/ppermute | solution.py:330
  119.1 6.6 %collective-permute-start.28 = (bf16[256,512]{1,0:T(8,128)(2,1)S(1)}, bf16[256,512]{1,0:T(8,128)(2,1)S(1)}, u32[]{:S(2)}, u32[]{:S(2)}) collective-permute-start(bf16[256,512]{1,0:T(8,128)(2,1)S(1)} %get-tuple-element.19), channel_id=1, source_target_pairs={{0,4},{4,0},{8,12},{12,8},{14,10},{10,14},{6,2},{2,6},{1,5},{5,1},... | collective-permute-start | bytes 786440 | tf_op jit(solution)/shard_map/ppermute | solution.py:330
  126.7 6.4 %collective-permute-start.29 = (bf16[256,512]{1,0:T(8,128)(2,1)S(1)}, bf16[256,512]{1,0:T(8,128)(2,1)S(1)}, u32[]{:S(2)}, u32[]{:S(2)}) collective-permute-start(bf16[256,512]{1,0:T(8,128)(2,1)S(1)} %get-tuple-element.20), channel_id=1, source_target_pairs={{0,4},{4,0},{8,12},{12,8},{14,10},{10,14},{6,2},{2,6},{1,5},{5,1},... | collective-permute-start | bytes 786440 | tf_op jit(solution)/shard_map/ppermute | solution.py:330
  127.4 8.6 %collective-permute-start.30 = (bf16[256,512]{1,0:T(8,128)(2,1)S(1)}, bf16[256,512]{1,0:T(8,128)(2,1)S(1)}, u32[]{:S(2)}, u32[]{:S(2)}) collective-permute-start(bf16[256,512]{1,0:T(8,128)(2,1)S(1)} %get-tuple-element.21), channel_id=1, source_target_pairs={{4,8},{8,4},{12,14},{14,12},{10,6},{6,10},{2,0},{0,2},{5,9},{9,5},... | collective-permute-start | bytes 786440 | tf_op jit(solution)/shard_map/ppermute | solution.py:330
  136.8 6.5 %collective-permute-start.31 = (bf16[256,512]{1,0:T(8,128)(2,1)S(1)}, bf16[256,512]{1,0:T(8,128)(2,1)}, u32[]{:S(2)}, u32[]{:S(2)}) collective-permute-start(bf16[256,512]{1,0:T(8,128)(2,1)S(1)} %last.1.own), channel_id=1, source_target_pairs={{0,2},{2,0},{1,3},{3,1},{4,6},{6,4},{5,7},{7,5},{8,10},{10,8},{9,1... | collective-permute-start | bytes 786440 | tf_op jit(solution)/shard_map/ppermute | solution.py:330
  (33 other events, 318.4 us)

commit v2 on v0

v2 whole, which is shorter than its diff:
```python
import functools

import jax
import jax.numpy as jnp
from jax import lax
from jax.experimental import pallas as pl
from jax.experimental.pallas import tpu as pltpu
from jax.sharding import PartitionSpec as P

DAMPING = 0.5
F32, BF16 = jnp.float32, jnp.bfloat16
LANES = 128

COS_TERMS = (
    0.9999999887556631, -0.49999988843399, 0.04166648574334225, -0.001388778673619495,
    2.4769518189949842e-05, -2.7075418374484127e-07, 1.7231808612122658e-09,
)
INV_TWO_PI = 0.15915494309189535
TWO_PI_HIGH = 6.28125
TWO_PI_LOW = 0.0019353071795864769


def cosine(angles):
    turns = jnp.round(angles * INV_TWO_PI)
    rest = (angles - turns * TWO_PI_HIGH) - turns * TWO_PI_LOW
    square = rest * rest
    result = jnp.full_like(square, COS_TERMS[-1])
    for term in COS_TERMS[-2::-1]:
        result = result * square + term
    return result


def dot(a, b):
    return jnp.dot(a, b, preferred_element_type=F32)


def dot_nt(a, b):
    return lax.dot_general(a, b, (((1,), (1,)), ((), ())), preferred_element_type=F32)


def call(kernel, out_shapes, place, args, name, vmem_mib=56):
    vmem = pl.BlockSpec(memory_space=pltpu.VMEM)
    single = isinstance(out_shapes, jax.ShapeDtypeStruct)
    return pl.pallas_call(
        kernel,
        out_shape=out_shapes,
        in_specs=[pl.BlockSpec(memory_space=pltpu.SMEM)] + [vmem] * len(args),
        out_specs=vmem if single else (vmem,) * len(out_shapes),
        compiler_params=pltpu.CompilerParams(vmem_limit_bytes=vmem_mib << 20),
        name=name,
    )(place, *args)


def like(shape, dtype=BF16):
    return jax.ShapeDtypeStruct(tuple(shape), dtype)


def lanes(index, size):
    return pl.ds(pl.multiple_of(index * size, size), size)


def residual_kernel(place, labels, predictions, out):
    width = predictions.shape[0]
    part = out.shape[1] // 2
    out[...] = jnp.zeros_like(out)
    for j in (0, 1):
        own = lanes(2 * place[1] + (place[2] ^ j), part)
        classes = lax.broadcasted_iota(jnp.int32, (width, part), 0) + place[2] * width
        hit = (classes == labels[:, own]).astype(F32)
        out[:width, j * part:(j + 1) * part] = (hit - predictions[:, own]).astype(BF16)


def features_kernel(n_rows, place, *refs):
    rows, (w_own, w_other, p_own, p_other, out) = refs[:n_rows], refs[n_rows:]
    inputs = rows[0][...] if n_rows == 1 else jnp.concatenate([r[...] for r in rows], axis=0)
    half = w_own.shape[1]
    for i, (weights, phases) in enumerate(((w_own, p_own), (w_other, p_other))):
        angles = dot(inputs, weights[...]) + phases[...].astype(F32)
        out[:, lanes(place[2] ^ i, half)] = cosine(angles).astype(BF16)


def features(place, rows, weights, phases):
    total = sum(r.shape[0] for r in rows)
    return call(
        functools.partial(features_kernel, len(rows)),
        like((total, 2 * weights[0].shape[1])), place, (*rows, *weights, *phases), "features",
    )


def joined(pieces, part):
    sides = [[r[:, i * part:(i + 1) * part] for r in pieces] for i in (0, 1)]
    return [s[0] if len(s) == 1 else jnp.concatenate(s, axis=1) for s in sides]


def gradient_of(groups, refs, part, at_features):
    total, at = None, 0
    for count, stacked in groups:
        pieces = [refs[at + i][...] for i in range(count)]
        if stacked:
            pieces = [jnp.concatenate(pieces, axis=0)]
        first, second = joined(pieces, part)
        mine, theirs = refs[at + count][:, at_features], refs[at + count + 1][:, at_features]
        at += count + 2
        if first.shape[1] < 256:
            products = [dot(jnp.concatenate([first, second], axis=1), jnp.concatenate([mine, theirs], axis=0))]
        else:
            products = [dot(first, mine), dot(second, theirs)]
        for product in products:
            total = product if total is None else total + product
    return total


def flat(groups):
    return [a for pieces, mine, theirs in groups for a in (*pieces, mine, theirs)]


def shape_of(groups, stacked):
    return [(len(g[0]), s) for g, s in zip(groups, stacked)]


TILE = 512


def gradient_kernel(form, part, earlier, place, *refs):
    *pieces, out = refs
    for k in range(0, out.shape[1], TILE):
        at = slice(k, k + TILE)
        total = gradient_of(form, pieces[earlier:], part, at)
        out[:, at] = pieces[0][:, at] + total if earlier else total


def gradient(place, groups, stacked, part, padded, earlier=()):
    n_feat = groups[0][1].shape[1]
    return call(
        functools.partial(gradient_kernel, shape_of(groups, stacked), part, len(earlier)),
        like((padded, n_feat), F32), place, (*earlier, *flat(groups)), "gradient",
    )


def high_low(x):
    high = x.astype(BF16)
    return high, (x - high.astype(F32)).astype(BF16)


def solve_kernel(form, part, place, *refs):
    *pieces, partial_gradient, inverse, coefficients, new, sent = refs
    total = None
    for k in range(0, inverse.shape[1], TILE):
        at = slice(k, k + TILE)
        g_high, g_low = high_low(partial_gradient[:, at] + gradient_of(form, pieces, part, at))
        p_high, p_low = high_low(inverse[:, at])
        product = dot_nt(g_high, p_high) + (dot_nt(g_high, p_low) + dot_nt(g_low, p_high))
        total = product if total is None else total + product
    update = DAMPING * total
    new[...] = coefficients[...] + update[:new.shape[0]]
    sent[...] = update.astype(BF16)


def solve(place, groups, stacked, part, partial_gradient, inverse, coefficients):
    outs = (like(coefficients.shape, F32), like((partial_gradient.shape[0], coefficients.shape[1])))
    return call(
        functools.partial(solve_kernel, shape_of(groups, stacked), part),
        outs, place, (*flat(groups), partial_gradient, inverse, coefficients), "solve",
    )


def own_change(place, sent, features_ref):
    depth = sent.shape[1]
    return dot_nt(sent[...], features_ref[:, lanes(place[0], depth)])


def far_kernel(place, sent, mine, theirs, a, b):
    a[...] = own_change(place, sent, mine).astype(BF16)
    b[...] = own_change(place, sent, theirs).astype(BF16)


def third_kernel(place, sent, mine, theirs, in_e, in_o, out_e, out_o):
    part = in_e.shape[1]
    mine, theirs = own_change(place, sent, mine), own_change(place, sent, theirs)
    out_e[:, :part] = mine[:, :part].astype(BF16)
    out_e[:, part:] = (theirs[:, :part] + in_o[...].astype(F32)).astype(BF16)
    out_o[:, :part] = (mine[:, part:] + in_e[...].astype(F32)).astype(BF16)
    out_o[:, part:] = theirs[:, part:].astype(BF16)


def middle_kernel(place, sent, mine, theirs, in_e, in_o, out_e, out_o):
    part = in_e.shape[1] // 2
    for i, own in enumerate((mine, theirs)):
        own = own_change(place, sent, own)
        at = slice(i * part, (i + 1) * part)
        out_e[:, at] = (own[:, :part] + in_e[:, at].astype(F32)).astype(BF16)
        out_o[:, at] = (own[:, part:] + in_o[:, at].astype(F32)).astype(BF16)


def last_kernel(place, sent, mine, theirs, in_e, in_o, out):
    part = in_e.shape[1] // 2
    for i, own in enumerate((mine, theirs)):
        at = slice(i * part, (i + 1) * part)
        came = in_e[:, at].astype(F32) + in_o[:, at].astype(F32)
        out[:, at] = (own_change(place, sent, own) + came).astype(BF16)


def apply_kernel(place, predictions, own, other, new):
    width, part = new.shape[0], own.shape[1] // 2
    for i, source in enumerate((own, other)):
        for j in (0, 1):
            at = lanes(2 * (place[1] ^ i) + (place[2] ^ j), part)
            new[:, at] = predictions[:, at] + source[:width, j * part:(j + 1) * part].astype(F32)


def swap(x, axes, pairs):
    return lax.ppermute(x, axes, [p for a, b in pairs for p in ((a, b), (b, a))])


def ring_shards(n_rows, inputs, projection, phases, inverse_blocks, labels, predictions, coefficients):
    ring = [2 * z for z in range(n_rows)] + [2 * z + 1 for z in reversed(range(n_rows))]
    size = len(ring)
    even = [(ring[i], ring[i + 1]) for i in range(0, size, 2)]
    odd = [(ring[i], ring[(i + 1) % size]) for i in range(1, size, 2)]
    E = lambda x: swap(x, ("rows", "blocks"), even)
    O = lambda x: swap(x, ("rows", "blocks"), odd)
    C = lambda x: swap(x, "cols", [(0, 1)])

    z, x, c = (lax.axis_index(a) for a in ("rows", "blocks", "cols"))
    place = jnp.stack([z, x, c]).astype(jnp.int32)
    local_rows, width = predictions.shape
    part = local_rows // 4
    padded = -(-width // LANES) * LANES

    weights = (projection, C(projection))
    phases = phases[None, :]
    phases = (phases, C(phases))
    predictions, coefficients = predictions.T, coefficients.T

    x0 = lax.dynamic_slice_in_dim(inputs, (2 * x + c) * part, part, 0)
    r0 = call(
        residual_kernel, like((padded, 2 * part)), place, (labels[None, :], predictions), "residual"
    )

    def around(own):
        half = own.shape[0] // 2
        e1, o1 = E(own), O(own)
        e2, o2 = E(o1), O(e1)
        e3, o3 = E(o2), O(e2)
        e4, o4 = E(o3[:half]), O(e3[half:])
        return (e1, o1), (e2, o2), (e3, o3), (e4, o4)

    xs = ((x0,),) + around(x0)
    rs = ((r0,),) + around(r0)
    groups = []
    for rows_in, residual_in in zip(xs, rs):
        mine = features(place, rows_in, weights, phases)
        groups.append((residual_in, mine, C(mine)))
    first = gradient(place, groups[:3], (False,) * 3, part, padded)
    first = gradient(place, groups[3:4], (False,), part, padded, (first,))
    new_coefficients, sent = solve(place, groups[4:], (True,), part, first, inverse_blocks[0], coefficients)

    def step(kernel, k, received, shapes, name):
        return call(kernel, tuple(like(s) for s in shapes), place, (sent, *groups[k][1:], *received), name)

    piece, block = (padded, part), (padded, 2 * part)
    a4, b4 = step(far_kernel, 4, (), (piece, piece), "far")
    e3, o3 = step(third_kernel, 3, (E(a4), O(b4)), (block, block), "third")
    e2, o2 = step(middle_kernel, 2, (O(o3), E(e3)), (block, block), "second")
    e1, o1 = step(middle_kernel, 1, (O(o2), E(e2)), (block, block), "first")
    (own,) = step(last_kernel, 0, (E(e1), O(o1)), (block,), "last")
    other = swap(own, "blocks", [(0, 1)])
    new = call(apply_kernel, like(predictions.shape, F32), place, (predictions, own, other), "apply")
    return new_coefficients.T, new.T


def plain_shards(inputs, projection, phases, inverse_blocks, labels, predictions, coefficients):
    out_width = predictions.shape[1]
    classes = lax.axis_index("cols") * out_width + jnp.arange(out_width, dtype=jnp.int32)
    onehot = (labels[:, None] == classes[None, :]).astype(F32)
    residual = (onehot - predictions).astype(BF16)
    angles = dot(inputs, projection) + phases.astype(F32)[None, :]
    half_features = jnp.cos(angles).astype(BF16)
    features_full = lax.all_gather(half_features, "cols", axis=1, tiled=True)
    own_gradient = lax.psum_scatter(
        lax.dot_general(features_full, residual, (((0,), (0,)), ((), ())), preferred_element_type=F32),
        "rows", scatter_dimension=0, tiled=True,
    )
    gradient_full = lax.all_gather(own_gradient, "rows", axis=0, tiled=True)
    update = DAMPING * jnp.dot(inverse_blocks[0], gradient_full, precision=lax.Precision.HIGHEST)
    sent = lax.all_gather(update.astype(BF16), "rows", axis=0, tiled=True)
    summed = lax.psum(dot(features_full, sent), "blocks")
    return coefficients + update, predictions + summed


def solution(mesh):
    n_rows, n_blocks = mesh.shape["rows"], mesh.shape["blocks"]
    small_ring = n_blocks == 2 and n_rows == 4 and mesh.shape["cols"] == 2
    shards = functools.partial(ring_shards, n_rows) if small_ring else plain_shards
    return jax.shard_map(
        shards,
        mesh=mesh,
        in_specs=(
            P(("groups", "rows"), None),
            P(None, ("groups", "blocks", "cols")),
            P(("groups", "blocks", "cols")),
            P(("groups", "blocks"), "rows", None),
            P(("groups", "rows")),
            P(("groups", "rows"), "cols"),
            P(("groups", "blocks", "rows"), "cols"),
        ),
        out_specs=(P(("groups", "blocks", "rows"), "cols"), P(("groups", "rows"), "cols")),
        check_vma=False,
    )
```

time: 311 us -> 154 us (0.50)
  waiting for transfers between devices: 257 us -> 34.3 us
  Pallas kernels: 0 us -> 68.9 us
  matrix products: 36.4 us -> 0 us
  starting transfers between devices: 0.38 us -> 36.5 us
  between operations: 13.8 us -> 0.9 us
  local copies, waits for them, and re-layouts: 0.74 us -> 12.6 us
    all_gather x3 -> x0, waiting for transfers between devices: 140 us -> none  [the longest x1 82.7 us: shards(): gradient = lax.all_gather(own_gradient, 'rows', axis=0, tiled=True)]
    reduce_scatter x1 -> x0, waiting for transfers between devices: 78 us -> none  [shards(): lax.psum_scatter(lax.dot_general(column_slice, residual, (((0,), (0,)), (...]
    pallas_call x0 -> x15, Pallas kernels: none -> 68.9 us  [call(): pl.pallas_call(kernel, out_shape=out_shapes, in_specs=[pl.BlockSpec(memor...]
    psum x1 -> x0, waiting for transfers between devices: 38.6 us -> none  [shards(): summed = lax.psum(contribution, 'blocks')]
    ppermute x0 -> x32, starting transfers between devices: none -> 36.5 us  [swap(): lax.ppermute(x, axes, [p for a, b in pairs for p in ((a, b), (b, a))])]
    dot_general x4 -> x0, matrix products: 36.4 us -> none  [the longest x1 17.2 us: shards(): solved = jnp.dot(local_inverse, gradient, precision=lax.Precision.HIGHEST)]
    ppermute x0 -> x32, waiting for transfers between devices: none -> 34.3 us  [swap(): lax.ppermute(x, axes, [p for a, b in pairs for p in ((a, b), (b, a))])]
    unnamed x6 -> x64, local copies, waits for them, and re-layouts: 0.74 us -> 10.1 us
  transfers between devices with their start and end apart: 5 -> 32, of which waited for: 5 -> 14; matrix products, arithmetic and copies ran while one was open for 0% -> 2% of each run, Pallas kernels for 0% -> 28%
where the time goes in v2:
time: 154 us
  Pallas kernels  68.9 us (45%)
  starting transfers between devices  36.5 us (24%)
  waiting for transfers between devices  34.3 us (22%)
  local copies, waits for them, and re-layouts  12.6 us (8%)
    pallas_call x15, Pallas kernels, call(): pl.pallas_call(kernel, out_shape=out_shapes, in_specs=[pl.BlockSpec(memor...  68.9 us
    ppermute x32, starting transfers between devices, swap(): lax.ppermute(x, axes, [p for a, b in pairs for p in ((a, b), (b, a))])  36.5 us
    ppermute x32, waiting for transfers between devices, swap(): lax.ppermute(x, axes, [p for a, b in pairs for p in ((a, b), (b, a))])  34.3 us
    unnamed x64, local copies, waits for them, and re-layouts  10.1 us
  transfers between devices with their start and end apart: 32, of which 14 were waited for; matrix products, arithmetic and copies ran while one was open for 2% of the time, Pallas kernels for 28%

profile of v2, /device:TPU:0, one launch (start us, length us, event | category | flops | bytes accessed | tf_op | source)
XLA Modules:
  0.0 153.8 jit_solution(18001026886721808980)
XLA Ops:
  1.9 3.1 %collective-permute-start.12 = (bf16[128,1024]{1,0:T(8,128)(2,1)S(1)}, bf16[128,1024]{1,0:T(8,128)(2,1)}, u32[]{:S(2)}, u32[]{:S(2)}) collective-permute-start(bf16[128,1024]{1,0:T(8,128)(2,1)S(1)} %constant_dynamic-slice_fusion.refs_0_), channel_id=1, source_target_pairs={{0,4},{4,0},{8,12},{12,8},{14,10},{10,14},{6,2},{2,6},{1,5},{5,1},... | collective-permute-start | bytes 786440 | tf_op jit(solution)/shard_map/ppermute | solution.py:212
  7.0 2.0 %residual.1.refs_0_ = bf16[512,256]{1,0:T(8,128)(2,1)} custom-call(s32[3]{0:T(128)} %pad_add_fusion.place, s32[1,512]{1,0:T(1,128)} %bitcast.14, f32[500,512]{1,0:T(8,128)} %bitcast.10), custom_call_target="tpu_custom_call" | custom-call | tf_op jit(solution)/shard_map/residual/pallas_call | solution.py:44
  9.1 1.7 %collective-permute-start.4 = (bf16[512,256]{1,0:T(8,128)(2,1)}, bf16[512,256]{1,0:T(8,128)(2,1)S(1)}, u32[]{:S(2)}, u32[]{:S(2)}) collective-permute-start(bf16[512,256]{1,0:T(8,128)(2,1)} %residual.1.refs_0_), channel_id=1, source_target_pairs={{0,4},{4,0},{8,12},{12,8},{14,10},{10,14},{6,2},{2,6},{1,5},{5,1},... | collective-permute-start | bytes 786440 | tf_op jit(solution)/shard_map/ppermute | solution.py:212
  11.5 1.9 %collective-permute-start.13 = (bf16[128,1024]{1,0:T(8,128)(2,1)}, bf16[128,1024]{1,0:T(8,128)(2,1)S(1)}, u32[]{:S(2)}, u32[]{:S(2)}) collective-permute-start(bf16[128,1024]{1,0:T(8,128)(2,1)} %collective-permute-done.12.refs_0_), channel_id=1, source_target_pairs={{4,8},{8,4},{12,14},{14,12},{10,6},{6,10},{2,0},{0,2},{5,9},{9,5},... | collective-permute-start | bytes 786440 | tf_op jit(solution)/shard_map/ppermute | solution.py:212
  13.4 2.5 %collective-permute-start.9 = (bf16[128,1024]{1,0:T(8,128)(2,1)}, bf16[128,1024]{1,0:T(8,128)(2,1)S(1)}, u32[]{:S(2)}, u32[]{:S(2)}) collective-permute-start(bf16[128,1024]{1,0:T(8,128)(2,1)} %collective-permute-done.8.refs_1_), channel_id=1, source_target_pairs={{0,4},{4,0},{8,12},{12,8},{14,10},{10,14},{6,2},{2,6},{1,5},{5,1},... | collective-permute-start | bytes 786440 | tf_op jit(solution)/shard_map/ppermute | solution.py:212
  19.8 1.6 %collective-permute-start.14 = (bf16[128,1024]{1,0:T(8,128)(2,1)S(1)}, bf16[128,1024]{1,0:T(8,128)(2,1)S(1)}, u32[]{:S(2)}, u32[]{:S(2)}) collective-permute-start(bf16[128,1024]{1,0:T(8,128)(2,1)S(1)} %collective-permute-done.13.refs_1_), channel_id=1, source_target_pairs={{0,4},{4,0},{8,12},{12,8},{14,10},{10,14},{6,2},{2,6},{1,5},{5,1},... | collective-permute-start | bytes 786440 | tf_op jit(solution)/shard_map/ppermute | solution.py:212
  21.4 1.6 %collective-permute-done.9.refs_0_ = bf16[128,1024]{1,0:T(8,128)(2,1)S(1)} collective-permute-done((bf16[128,1024]{1,0:T(8,128)(2,1)}, bf16[128,1024]{1,0:T(8,128)(2,1)S(1)}, u32[]{:S(2)}, u32[]{:S(2)}) %collective-permute-start.9) | collective-permute-done | bytes 262176 | tf_op jit(solution)/shard_map/ppermute | solution.py:212
  23.0 1.9 %collective-permute-start.10 = (bf16[128,1024]{1,0:T(8,128)(2,1)S(1)}, bf16[128,1024]{1,0:T(8,128)(2,1)S(1)}, u32[]{:S(2)}, u32[]{:S(2)}) collective-permute-start(bf16[128,1024]{1,0:T(8,128)(2,1)S(1)} %collective-permute-done.9.refs_0_), channel_id=1, source_target_pairs={{4,8},{8,4},{12,14},{14,12},{10,6},{6,10},{2,0},{0,2},{5,9},{9,5},... | collective-permute-start | bytes 786440 | tf_op jit(solution)/shard_map/ppermute | solution.py:212
  24.9 2.1 %collective-permute-done.refs_4_ = bf16[512,256]{1,0:T(8,128)(2,1)S(1)} collective-permute-done((bf16[512,256]{1,0:T(8,128)(2,1)}, bf16[512,256]{1,0:T(8,128)(2,1)S(1)}, u32[]{:S(2)}, u32[]{:S(2)}) %collective-permute-start) | collective-permute-done | bytes 262176 | tf_op jit(solution)/shard_map/ppermute | solution.py:212
  29.4 5.9 %features.7.refs_5_.mine = bf16[256,2048]{1,0:T(8,128)(2,1)} custom-call(s32[3]{0:T(128)} %pad_add_fusion.place, bf16[128,1024]{1,0:T(8,128)(2,1)} %collective-permute-done.12.refs_0_, bf16[128,1024]{1,0:T(8,128)(2,1)} %collective-permute-done.8.refs_1_, bf16[1024,1024]{1,0:T(8,128)(2,1)} %refs_2_.7, bf16[1024,1024]{1,0:T(8,128)(2,1)} %copy-done.1, ...), custom_call_target="tpu_custom_call" | custom-call | tf_op jit(solution)/shard_map/features/pallas_call | solution.py:44
  36.4 5.9 %features.8.refs_9_.mine = bf16[256,2048]{1,0:T(8,128)(2,1)} custom-call(s32[3]{0:T(128)} %pad_add_fusion.place, bf16[128,1024]{1,0:T(8,128)(2,1)} %copy-done.15, bf16[128,1024]{1,0:T(8,128)(2,1)} %copy-done.16, bf16[1024,1024]{1,0:T(8,128)(2,1)} %refs_2_.7, bf16[1024,1024]{1,0:T(8,128)(2,1)} %copy-done.1, bf16[1,1024]{1,0:T(2,128)(2,1)} %copy-done.24, ...), custom_call_target="tpu_custom_call" | custom-call | tf_op jit(solution)/shard_map/features/pallas_call | solution.py:44
  43.7 5.9 %features.9.refs_3_.mine = bf16[256,2048]{1,0:T(8,128)(2,1)} custom-call(s32[3]{0:T(128)} %pad_add_fusion.place, bf16[128,1024]{1,0:T(8,128)(2,1)} %copy-done.11, bf16[128,1024]{1,0:T(8,128)(2,1)} %copy-done.10, bf16[1024,1024]{1,0:T(8,128)(2,1)} %refs_2_.7, bf16[1024,1024]{1,0:T(8,128)(2,1)} %copy-done.1, bf16[1,1024]{1,0:T(2,128)(2,1)} %copy-done.24, ...), custom_call_target="tpu_custom_call" | custom-call | tf_op jit(solution)/shard_map/features/pallas_call | solution.py:44
  50.7 1.6 %collective-permute-start.15 = (bf16[64,1024]{1,0:T(8,128)(2,1)S(1)}, bf16[64,1024]{1,0:T(8,128)(2,1)S(1)}, u32[]{:S(2)}, u32[]{:S(2)}) collective-permute-start(bf16[64,1024]{1,0:T(8,128)(2,1)S(1)} %slice.19), channel_id=1, source_target_pairs={{4,8},{8,4},{12,14},{14,12},{10,6},{6,10},{2,0},{0,2},{5,9},{9,5},... | collective-permute-start | bytes 393224 | tf_op jit(solution)/shard_map/ppermute | solution.py:212
  53.2 1.7 %collective-permute-start.11 = (bf16[64,1024]{1,0:T(8,128)(2,1)S(1)}, bf16[64,1024]{1,0:T(8,128)(2,1)S(1)}, u32[]{:S(2)}, u32[]{:S(2)}) collective-permute-start(bf16[64,1024]{1,0:T(8,128)(2,1)S(1)} %slice.18), channel_id=1, source_target_pairs={{0,4},{4,0},{8,12},{12,8},{14,10},{10,14},{6,2},{2,6},{1,5},{5,1},... | collective-permute-start | bytes 393224 | tf_op jit(solution)/shard_map/ppermute | solution.py:212
  54.9 1.7 %collective-permute-done.15.refs_1_ = bf16[64,1024]{1,0:T(8,128)(2,1)S(1)} collective-permute-done((bf16[64,1024]{1,0:T(8,128)(2,1)S(1)}, bf16[64,1024]{1,0:T(8,128)(2,1)S(1)}, u32[]{:S(2)}, u32[]{:S(2)}) %collective-permute-start.15) | collective-permute-done | bytes 131104 | tf_op jit(solution)/shard_map/ppermute | solution.py:212
  58.1 4.4 %features.6.refs_1_.mine = bf16[128,2048]{1,0:T(8,128)(2,1)} custom-call(s32[3]{0:T(128)} %pad_add_fusion.place, bf16[128,1024]{1,0:T(8,128)(2,1)} %copy-done.7, bf16[1024,1024]{1,0:T(8,128)(2,1)} %refs_2_.7, bf16[1024,1024]{1,0:T(8,128)(2,1)} %copy-done.1, bf16[1,1024]{1,0:T(2,128)(2,1)} %copy-done.24, bf16[1,1024]{1,0:T(2,128)(2,1)} %copy-done.31), custom_call_target="tpu_custom_call" | custom-call | tf_op jit(solution)/shard_map/features/pallas_call | solution.py:44
  63.1 4.4 %features.5.refs_2_.mine = bf16[128,2048]{1,0:T(8,128)(2,1)} custom-call(s32[3]{0:T(128)} %pad_add_fusion.place, bf16[64,1024]{1,0:T(8,128)(2,1)} %copy-done.28, bf16[64,1024]{1,0:T(8,128)(2,1)} %copy-done.27, bf16[1024,1024]{1,0:T(8,128)(2,1)} %refs_2_.7, bf16[1024,1024]{1,0:T(8,128)(2,1)} %copy-done.1, bf16[1,1024]{1,0:T(2,128)(2,1)} %copy-done.24, ...), custom_call_target="tpu_custom_call" | custom-call | tf_op jit(solution)/shard_map/features/pallas_call | solution.py:44
  70.6 7.9 %gradient.2.refs_0_ = f32[512,2048]{1,0:T(8,128)} custom-call(s32[3]{0:T(128)} %pad_add_fusion.place, bf16[512,256]{1,0:T(8,128)(2,1)} %residual.1.refs_0_, bf16[128,2048]{1,0:T(8,128)(2,1)} %features.6.refs_1_.mine, bf16[128,2048]{1,0:T(8,128)(2,1)} %copy-done.5, bf16[512,256]{1,0:T(8,128)(2,1)} %copy-done.12, bf16[512,256]{1,0:T(8,128)(2,1)} %copy-done.13, ...), custom_call_target="tpu_custom_call" | custom-call | tf_op jit(solution)/shard_map/gradient/pallas_call | solution.py:44
  79.6 6.2 %gradient.3.refs_4_ = f32[512,2048]{1,0:T(8,128)} custom-call(s32[3]{0:T(128)} %pad_add_fusion.place, f32[512,2048]{1,0:T(8,128)} %gradient.2.refs_0_, bf16[512,256]{1,0:T(8,128)(2,1)} %copy-done.8, bf16[512,256]{1,0:T(8,128)(2,1)} %copy-done.9, bf16[256,2048]{1,0:T(8,128)(2,1)} %features.9.refs_3_.mine, bf16[256,2048]{1,0:T(8,128)(2,1)} %copy-done.2), custom_call_target="tpu_custom_call" | custom-call | tf_op jit(solution)/shard_map/gradient/pallas_call | solution.py:44
  86.7 9.2 %solve.1 = (f32[500,512]{1,0:T(8,128)}, bf16[512,512]{1,0:T(8,128)(2,1)}) custom-call(s32[3]{0:T(128)} %pad_add_fusion.place, bf16[256,256]{1,0:T(8,128)(2,1)} %copy-done.26, bf16[256,256]{1,0:T(8,128)(2,1)} %copy-done.25, bf16[128,2048]{1,0:T(8,128)(2,1)} %features.5.refs_2_.mine, bf16[128,2048]{1,0:T(8,128)(2,1)} %copy-done.6, ...), custom_call_target="tpu_custom_call" | custom-call | tf_op jit(solution)/shard_map/solve/pallas_call | solution.py:44
  95.9 2.5 %far.1 = (bf16[512,128]{1,0:T(8,128)(2,1)}, bf16[512,128]{1,0:T(8,128)(2,1)}) custom-call(s32[3]{0:T(128)} %pad_add_fusion.place, bf16[512,512]{1,0:T(8,128)(2,1)} %get-tuple-element.13.sent, bf16[128,2048]{1,0:T(8,128)(2,1)} %features.5.refs_2_.mine, bf16[128,2048]{1,0:T(8,128)(2,1)} %copy-done.6), custom_call_target="tpu_custom_call" | custom-call | tf_op jit(solution)/shard_map/far/pallas_call | solution.py:44
  100.7 3.4 %collective-permute-done.23.in_e = bf16[512,128]{1,0:T(8,128)(2,1)S(1)} collective-permute-done((bf16[512,128]{1,0:T(8,128)(2,1)}, bf16[512,128]{1,0:T(8,128)(2,1)S(1)}, u32[]{:S(2)}, u32[]{:S(2)}) %collective-permute-start.23) | collective-permute-done | bytes 131104 | tf_op jit(solution)/shard_map/ppermute | solution.py:212
  105.7 3.0 %third.1 = (bf16[512,256]{1,0:T(8,128)(2,1)}, bf16[512,256]{1,0:T(8,128)(2,1)}) custom-call(s32[3]{0:T(128)} %pad_add_fusion.place, bf16[512,512]{1,0:T(8,128)(2,1)} %get-tuple-element.13.sent, bf16[256,2048]{1,0:T(8,128)(2,1)} %features.9.refs_3_.mine, bf16[256,2048]{1,0:T(8,128)(2,1)} %copy-done.2, bf16[512,128]{1,0:T(8,128)(2,1)} %copy-done.29, ...), custom_call_target="tpu_custom_call" | custom-call | tf_op jit(solution)/shard_map/third/pallas_call | solution.py:44
  109.8 1.6 %collective-permute-start.26 = (bf16[512,256]{1,0:T(8,128)(2,1)}, bf16[512,256]{1,0:T(8,128)(2,1)S(1)}, u32[]{:S(2)}, u32[]{:S(2)}) collective-permute-start(bf16[512,256]{1,0:T(8,128)(2,1)} %get-tuple-element.17), channel_id=1, source_target_pairs={{0,4},{4,0},{8,12},{12,8},{14,10},{10,14},{6,2},{2,6},{1,5},{5,1},... | collective-permute-start | bytes 786440 | tf_op jit(solution)/shard_map/ppermute | solution.py:212
  111.3 5.0 %collective-permute-done.25.in_e = bf16[512,256]{1,0:T(8,128)(2,1)S(1)} collective-permute-done((bf16[512,256]{1,0:T(8,128)(2,1)}, bf16[512,256]{1,0:T(8,128)(2,1)S(1)}, u32[]{:S(2)}, u32[]{:S(2)}) %collective-permute-start.25) | collective-permute-done | bytes 262176 | tf_op jit(solution)/shard_map/ppermute | solution.py:212
  118.0 3.1 %second.1 = (bf16[512,256]{1,0:T(8,128)(2,1)}, bf16[512,256]{1,0:T(8,128)(2,1)}) custom-call(s32[3]{0:T(128)} %pad_add_fusion.place, bf16[512,512]{1,0:T(8,128)(2,1)} %get-tuple-element.13.sent, bf16[256,2048]{1,0:T(8,128)(2,1)} %features.8.refs_9_.mine, bf16[256,2048]{1,0:T(8,128)(2,1)} %copy-done.4, bf16[512,256]{1,0:T(8,128)(2,1)} %copy-done.19, ...), custom_call_target="tpu_custom_call" | custom-call | tf_op jit(solution)/shard_map/second/pallas_call | solution.py:44
  123.7 4.1 %collective-permute-done.27.in_e = bf16[512,256]{1,0:T(8,128)(2,1)S(1)} collective-permute-done((bf16[512,256]{1,0:T(8,128)(2,1)}, bf16[512,256]{1,0:T(8,128)(2,1)S(1)}, u32[]{:S(2)}, u32[]{:S(2)}) %collective-permute-start.27) | collective-permute-done | bytes 262176 | tf_op jit(solution)/shard_map/ppermute | solution.py:212
  129.4 3.1 %first.1 = (bf16[512,256]{1,0:T(8,128)(2,1)}, bf16[512,256]{1,0:T(8,128)(2,1)}) custom-call(s32[3]{0:T(128)} %pad_add_fusion.place, bf16[512,512]{1,0:T(8,128)(2,1)} %get-tuple-element.13.sent, bf16[256,2048]{1,0:T(8,128)(2,1)} %features.7.refs_5_.mine, bf16[256,2048]{1,0:T(8,128)(2,1)} %copy-done.3, bf16[512,256]{1,0:T(8,128)(2,1)} %copy-done.20, ...), custom_call_target="tpu_custom_call" | custom-call | tf_op jit(solution)/shard_map/first/pallas_call | solution.py:44
  134.9 4.2 %collective-permute-done.29.in_e = bf16[512,256]{1,0:T(8,128)(2,1)S(1)} collective-permute-done((bf16[512,256]{1,0:T(8,128)(2,1)}, bf16[512,256]{1,0:T(8,128)(2,1)S(1)}, u32[]{:S(2)}, u32[]{:S(2)}) %collective-permute-start.29) | collective-permute-done | bytes 262176 | tf_op jit(solution)/shard_map/ppermute | solution.py:212
  141.4 2.7 %last.1.own = bf16[512,256]{1,0:T(8,128)(2,1)} custom-call(s32[3]{0:T(128)} %pad_add_fusion.place, bf16[512,512]{1,0:T(8,128)(2,1)} %get-tuple-element.13.sent, bf16[128,2048]{1,0:T(8,128)(2,1)} %features.6.refs_1_.mine, bf16[128,2048]{1,0:T(8,128)(2,1)} %copy-done.5, bf16[512,256]{1,0:T(8,128)(2,1)} %copy-done.17, bf16[512,256]{1,0:T(8,128)(2,1)} %copy-done.18), custom_call_target="tpu_custom_call" | custom-call | tf_op jit(solution)/shard_map/last/pallas_call | solution.py:44
  144.8 5.8 %collective-permute-done.31.other = bf16[512,256]{1,0:T(8,128)(2,1)S(1)} collective-permute-done((bf16[512,256]{1,0:T(8,128)(2,1)}, bf16[512,256]{1,0:T(8,128)(2,1)S(1)}, u32[]{:S(2)}, u32[]{:S(2)}) %collective-permute-start.31) | collective-permute-done | bytes 262176 | tf_op jit(solution)/shard_map/ppermute | solution.py:212
  151.3 2.5 %apply.1 = f32[500,512]{1,0:T(8,128)} custom-call(s32[3]{0:T(128)} %pad_add_fusion.place, f32[500,512]{1,0:T(8,128)} %bitcast.11, bf16[512,256]{1,0:T(8,128)(2,1)} %last.1.own, bf16[512,256]{1,0:T(8,128)(2,1)} %copy-done.23), custom_call_target="tpu_custom_call" | custom-call | tf_op jit(solution)/shard_map/apply/pallas_call | solution.py:44
  (118 shorter events, 38.7 us)
Async XLA Ops:
  0.6 27.4 %collective-permute-start.16 = (bf16[1024,1024]{1,0:T(8,128)(2,1)}, bf16[1024,1024]{1,0:T(8,128)(2,1)S(1)}, u32[]{:S(2)}, u32[]{:S(2)}) collective-permute-start(bf16[1024,1024]{1,0:T(8,128)(2,1)} %refs_2_.7), channel_id=1, source_target_pairs={{0,1},{1,0},{2,3},{3,2},{4,5},{5,4},{6,7},{7,6},{8,9},{9,8},{10,11... | collective-permute-start | bytes 6291464 | tf_op jit(solution)/shard_map/ppermute | solution.py:212
  1.9 9.6 %collective-permute-start.12 = (bf16[128,1024]{1,0:T(8,128)(2,1)S(1)}, bf16[128,1024]{1,0:T(8,128)(2,1)}, u32[]{:S(2)}, u32[]{:S(2)}) collective-permute-start(bf16[128,1024]{1,0:T(8,128)(2,1)S(1)} %constant_dynamic-slice_fusion.refs_0_), channel_id=1, source_target_pairs={{0,4},{4,0},{8,12},{12,8},{14,10},{10,14},{6,2},{2,6},{1,5},{5,1},... | collective-permute-start | bytes 786440 | tf_op jit(solution)/shard_map/ppermute | solution.py:212
  5.0 8.4 %collective-permute-start.8 = (bf16[128,1024]{1,0:T(8,128)(2,1)S(1)}, bf16[128,1024]{1,0:T(8,128)(2,1)}, u32[]{:S(2)}, u32[]{:S(2)}) collective-permute-start(bf16[128,1024]{1,0:T(8,128)(2,1)S(1)} %constant_dynamic-slice_fusion.refs_0_), channel_id=1, source_target_pairs={{4,8},{8,4},{12,14},{14,12},{10,6},{6,10},{2,0},{0,2},{5,9},{9,5},... | collective-permute-start | bytes 786440 | tf_op jit(solution)/shard_map/ppermute | solution.py:212
  9.1 10.1 %collective-permute-start.4 = (bf16[512,256]{1,0:T(8,128)(2,1)}, bf16[512,256]{1,0:T(8,128)(2,1)S(1)}, u32[]{:S(2)}, u32[]{:S(2)}) collective-permute-start(bf16[512,256]{1,0:T(8,128)(2,1)} %residual.1.refs_0_), channel_id=1, source_target_pairs={{0,4},{4,0},{8,12},{12,8},{14,10},{10,14},{6,2},{2,6},{1,5},{5,1},... | collective-permute-start | bytes 786440 | tf_op jit(solution)/shard_map/ppermute | solution.py:212
  11.5 8.3 %collective-permute-start.13 = (bf16[128,1024]{1,0:T(8,128)(2,1)}, bf16[128,1024]{1,0:T(8,128)(2,1)S(1)}, u32[]{:S(2)}, u32[]{:S(2)}) collective-permute-start(bf16[128,1024]{1,0:T(8,128)(2,1)} %collective-permute-done.12.refs_0_), channel_id=1, source_target_pairs={{4,8},{8,4},{12,14},{14,12},{10,6},{6,10},{2,0},{0,2},{5,9},{9,5},... | collective-permute-start | bytes 786440 | tf_op jit(solution)/shard_map/ppermute | solution.py:212
  13.4 9.7 %collective-permute-start.9 = (bf16[128,1024]{1,0:T(8,128)(2,1)}, bf16[128,1024]{1,0:T(8,128)(2,1)S(1)}, u32[]{:S(2)}, u32[]{:S(2)}) collective-permute-start(bf16[128,1024]{1,0:T(8,128)(2,1)} %collective-permute-done.8.refs_1_), channel_id=1, source_target_pairs={{0,4},{4,0},{8,12},{12,8},{14,10},{10,14},{6,2},{2,6},{1,5},{5,1},... | collective-permute-start | bytes 786440 | tf_op jit(solution)/shard_map/ppermute | solution.py:212
  16.5 1.2 collective-permute-start.17
  17.7 9.4 %collective-permute-start = (bf16[512,256]{1,0:T(8,128)(2,1)}, bf16[512,256]{1,0:T(8,128)(2,1)S(1)}, u32[]{:S(2)}, u32[]{:S(2)}) collective-permute-start(bf16[512,256]{1,0:T(8,128)(2,1)} %residual.1.refs_0_), channel_id=1, source_target_pairs={{4,8},{8,4},{12,14},{14,12},{10,6},{6,10},{2,0},{0,2},{5,9},{9,5},... | collective-permute-start | bytes 786440 | tf_op jit(solution)/shard_map/ppermute | solution.py:212
  19.2 16.1 %collective-permute-start.5 = (bf16[512,256]{1,0:T(8,128)(2,1)S(1)}, bf16[512,256]{1,0:T(8,128)(2,1)S(1)}, u32[]{:S(2)}, u32[]{:S(2)}) collective-permute-start(bf16[512,256]{1,0:T(8,128)(2,1)S(1)} %collective-permute-done.4.refs_3_), channel_id=1, source_target_pairs={{4,8},{8,4},{12,14},{14,12},{10,6},{6,10},{2,0},{0,2},{5,9},{9,5},... | collective-permute-start | bytes 786440 | tf_op jit(solution)/shard_map/ppermute | solution.py:212
  19.8 22.5 %collective-permute-start.14 = (bf16[128,1024]{1,0:T(8,128)(2,1)S(1)}, bf16[128,1024]{1,0:T(8,128)(2,1)S(1)}, u32[]{:S(2)}, u32[]{:S(2)}) collective-permute-start(bf16[128,1024]{1,0:T(8,128)(2,1)S(1)} %collective-permute-done.13.refs_1_), channel_id=1, source_target_pairs={{0,4},{4,0},{8,12},{12,8},{14,10},{10,14},{6,2},{2,6},{1,5},{5,1},... | collective-permute-start | bytes 786440 | tf_op jit(solution)/shard_map/ppermute | solution.py:212
  23.0 19.5 %collective-permute-start.10 = (bf16[128,1024]{1,0:T(8,128)(2,1)S(1)}, bf16[128,1024]{1,0:T(8,128)(2,1)S(1)}, u32[]{:S(2)}, u32[]{:S(2)}) collective-permute-start(bf16[128,1024]{1,0:T(8,128)(2,1)S(1)} %collective-permute-done.9.refs_0_), channel_id=1, source_target_pairs={{4,8},{8,4},{12,14},{14,12},{10,6},{6,10},{2,0},{0,2},{5,9},{9,5},... | collective-permute-start | bytes 786440 | tf_op jit(solution)/shard_map/ppermute | solution.py:212
  27.1 23.7 %collective-permute-start.1 = (bf16[512,256]{1,0:T(8,128)(2,1)S(1)}, bf16[512,256]{1,0:T(8,128)(2,1)}, u32[]{:S(2)}, u32[]{:S(2)}) collective-permute-start(bf16[512,256]{1,0:T(8,128)(2,1)S(1)} %collective-permute-done.refs_4_), channel_id=1, source_target_pairs={{0,4},{4,0},{8,12},{12,8},{14,10},{10,14},{6,2},{2,6},{1,5},{5,1},... | collective-permute-start | bytes 786440 | tf_op jit(solution)/shard_map/ppermute | solution.py:212
  35.3 33.0 %collective-permute-start.20 = (bf16[256,2048]{1,0:T(8,128)(2,1)}, bf16[256,2048]{1,0:T(8,128)(2,1)S(1)}, u32[]{:S(2)}, u32[]{:S(2)}) collective-permute-start(bf16[256,2048]{1,0:T(8,128)(2,1)} %features.7.refs_5_.mine), channel_id=1, source_target_pairs={{0,1},{1,0},{2,3},{3,2},{4,5},{5,4},{6,7},{7,6},{8,9},{9,8},{10,11... | collective-permute-start | bytes 3145736 | tf_op jit(solution)/shard_map/ppermute | solution.py:212
  35.3 17.9 %collective-permute-start.6 = (bf16[512,256]{1,0:T(8,128)(2,1)S(1)}, bf16[512,256]{1,0:T(8,128)(2,1)S(1)}, u32[]{:S(2)}, u32[]{:S(2)}) collective-permute-start(bf16[512,256]{1,0:T(8,128)(2,1)S(1)} %collective-permute-done.5.refs_8_), channel_id=1, source_target_pairs={{0,4},{4,0},{8,12},{12,8},{14,10},{10,14},{6,2},{2,6},{1,5},{5,1},... | collective-permute-start | bytes 786440 | tf_op jit(solution)/shard_map/ppermute | solution.py:212
  42.3 27.3 %collective-permute-start.21 = (bf16[256,2048]{1,0:T(8,128)(2,1)}, bf16[256,2048]{1,0:T(8,128)(2,1)S(1)}, u32[]{:S(2)}, u32[]{:S(2)}) collective-permute-start(bf16[256,2048]{1,0:T(8,128)(2,1)} %features.8.refs_9_.mine), channel_id=1, source_target_pairs={{0,1},{1,0},{2,3},{3,2},{4,5},{5,4},{6,7},{7,6},{8,9},{9,8},{10,11... | collective-permute-start | bytes 3145736 | tf_op jit(solution)/shard_map/ppermute | solution.py:212
  49.6 28.9 %collective-permute-start.22 = (bf16[256,2048]{1,0:T(8,128)(2,1)}, bf16[256,2048]{1,0:T(8,128)(2,1)S(1)}, u32[]{:S(2)}, u32[]{:S(2)}) collective-permute-start(bf16[256,2048]{1,0:T(8,128)(2,1)} %features.9.refs_3_.mine), channel_id=1, source_target_pairs={{0,1},{1,0},{2,3},{3,2},{4,5},{5,4},{6,7},{7,6},{8,9},{9,8},{10,11... | collective-permute-start | bytes 3145736 | tf_op jit(solution)/shard_map/ppermute | solution.py:212
  50.7 5.8 %collective-permute-start.15 = (bf16[64,1024]{1,0:T(8,128)(2,1)S(1)}, bf16[64,1024]{1,0:T(8,128)(2,1)S(1)}, u32[]{:S(2)}, u32[]{:S(2)}) collective-permute-start(bf16[64,1024]{1,0:T(8,128)(2,1)S(1)} %slice.19), channel_id=1, source_target_pairs={{4,8},{8,4},{12,14},{14,12},{10,6},{6,10},{2,0},{0,2},{5,9},{9,5},... | collective-permute-start | bytes 393224 | tf_op jit(solution)/shard_map/ppermute | solution.py:212
  53.2 9.2 %collective-permute-start.11 = (bf16[64,1024]{1,0:T(8,128)(2,1)S(1)}, bf16[64,1024]{1,0:T(8,128)(2,1)S(1)}, u32[]{:S(2)}, u32[]{:S(2)}) collective-permute-start(bf16[64,1024]{1,0:T(8,128)(2,1)S(1)} %slice.18), channel_id=1, source_target_pairs={{0,4},{4,0},{8,12},{12,8},{14,10},{10,14},{6,2},{2,6},{1,5},{5,1},... | collective-permute-start | bytes 393224 | tf_op jit(solution)/shard_map/ppermute | solution.py:212
  56.6 11.0 %collective-permute-start.2 = (bf16[512,256]{1,0:T(8,128)(2,1)}, bf16[512,256]{1,0:T(8,128)(2,1)S(1)}, u32[]{:S(2)}, u32[]{:S(2)}) collective-permute-start(bf16[512,256]{1,0:T(8,128)(2,1)} %collective-permute-done.1.refs_7_), channel_id=1, source_target_pairs={{4,8},{8,4},{12,14},{14,12},{10,6},{6,10},{2,0},{0,2},{5,9},{9,5},... | collective-permute-start | bytes 786440 | tf_op jit(solution)/shard_map/ppermute | solution.py:212
  62.5 5.2 %collective-permute-start.19 = (bf16[128,2048]{1,0:T(8,128)(2,1)}, bf16[128,2048]{1,0:T(8,128)(2,1)S(1)}, u32[]{:S(2)}, u32[]{:S(2)}) collective-permute-start(bf16[128,2048]{1,0:T(8,128)(2,1)} %features.6.refs_1_.mine), channel_id=1, source_target_pairs={{0,1},{1,0},{2,3},{3,2},{4,5},{5,4},{6,7},{7,6},{8,9},{9,8},{10,11... | collective-permute-start | bytes 1572872 | tf_op jit(solution)/shard_map/ppermute | solution.py:212
  67.6 18.2 %collective-permute-start.18 = (bf16[128,2048]{1,0:T(8,128)(2,1)}, bf16[128,2048]{1,0:T(8,128)(2,1)S(1)}, u32[]{:S(2)}, u32[]{:S(2)}) collective-permute-start(bf16[128,2048]{1,0:T(8,128)(2,1)} %features.5.refs_2_.mine), channel_id=1, source_target_pairs={{0,1},{1,0},{2,3},{3,2},{4,5},{5,4},{6,7},{7,6},{8,9},{9,8},{10,11... | collective-permute-start | bytes 1572872 | tf_op jit(solution)/shard_map/ppermute | solution.py:212
  67.7 18.0 %collective-permute-start.7 = (bf16[256,256]{1,0:T(8,128)(2,1)S(1)}, bf16[256,256]{1,0:T(8,128)(2,1)S(1)}, u32[]{:S(2)}, u32[]{:S(2)}) collective-permute-start(bf16[256,256]{1,0:T(8,128)(2,1)S(1)} %slice.17), channel_id=1, source_target_pairs={{4,8},{8,4},{12,14},{14,12},{10,6},{6,10},{2,0},{0,2},{5,9},{9,5},... | collective-permute-start | bytes 393224 | tf_op jit(solution)/shard_map/ppermute | solution.py:212
  68.3 17.5 %collective-permute-start.3 = (bf16[256,256]{1,0:T(8,128)(2,1)S(1)}, bf16[256,256]{1,0:T(8,128)(2,1)S(1)}, u32[]{:S(2)}, u32[]{:S(2)}) collective-permute-start(bf16[256,256]{1,0:T(8,128)(2,1)S(1)} %slice.16), channel_id=1, source_target_pairs={{0,4},{4,0},{8,12},{12,8},{14,10},{10,14},{6,2},{2,6},{1,5},{5,1},... | collective-permute-start | bytes 393224 | tf_op jit(solution)/shard_map/ppermute | solution.py:212
  98.4 5.6 %collective-permute-start.23 = (bf16[512,128]{1,0:T(8,128)(2,1)}, bf16[512,128]{1,0:T(8,128)(2,1)S(1)}, u32[]{:S(2)}, u32[]{:S(2)}) collective-permute-start(bf16[512,128]{1,0:T(8,128)(2,1)} %get-tuple-element.14), channel_id=1, source_target_pairs={{0,4},{4,0},{8,12},{12,8},{14,10},{10,14},{6,2},{2,6},{1,5},{5,1},... | collective-permute-start | bytes 393224 | tf_op jit(solution)/shard_map/ppermute | solution.py:212
  99.4 5.6 %collective-permute-start.24 = (bf16[512,128]{1,0:T(8,128)(2,1)}, bf16[512,128]{1,0:T(8,128)(2,1)S(1)}, u32[]{:S(2)}, u32[]{:S(2)}) collective-permute-start(bf16[512,128]{1,0:T(8,128)(2,1)} %get-tuple-element.15), channel_id=1, source_target_pairs={{4,8},{8,4},{12,14},{14,12},{10,6},{6,10},{2,0},{0,2},{5,9},{9,5},... | collective-permute-start | bytes 393224 | tf_op jit(solution)/shard_map/ppermute | solution.py:212
  108.7 7.6 %collective-permute-start.25 = (bf16[512,256]{1,0:T(8,128)(2,1)}, bf16[512,256]{1,0:T(8,128)(2,1)S(1)}, u32[]{:S(2)}, u32[]{:S(2)}) collective-permute-start(bf16[512,256]{1,0:T(8,128)(2,1)} %get-tuple-element.16), channel_id=1, source_target_pairs={{4,8},{8,4},{12,14},{14,12},{10,6},{6,10},{2,0},{0,2},{5,9},{9,5},... | collective-permute-start | bytes 786440 | tf_op jit(solution)/shard_map/ppermute | solution.py:212
  109.8 7.5 %collective-permute-start.26 = (bf16[512,256]{1,0:T(8,128)(2,1)}, bf16[512,256]{1,0:T(8,128)(2,1)S(1)}, u32[]{:S(2)}, u32[]{:S(2)}) collective-permute-start(bf16[512,256]{1,0:T(8,128)(2,1)} %get-tuple-element.17), channel_id=1, source_target_pairs={{0,4},{4,0},{8,12},{12,8},{14,10},{10,14},{6,2},{2,6},{1,5},{5,1},... | collective-permute-start | bytes 786440 | tf_op jit(solution)/shard_map/ppermute | solution.py:212
  121.1 6.6 %collective-permute-start.27 = (bf16[512,256]{1,0:T(8,128)(2,1)}, bf16[512,256]{1,0:T(8,128)(2,1)S(1)}, u32[]{:S(2)}, u32[]{:S(2)}) collective-permute-start(bf16[512,256]{1,0:T(8,128)(2,1)} %get-tuple-element.18), channel_id=1, source_target_pairs={{4,8},{8,4},{12,14},{14,12},{10,6},{6,10},{2,0},{0,2},{5,9},{9,5},... | collective-permute-start | bytes 786440 | tf_op jit(solution)/shard_map/ppermute | solution.py:212
  122.1 6.6 %collective-permute-start.28 = (bf16[512,256]{1,0:T(8,128)(2,1)}, bf16[512,256]{1,0:T(8,128)(2,1)S(1)}, u32[]{:S(2)}, u32[]{:S(2)}) collective-permute-start(bf16[512,256]{1,0:T(8,128)(2,1)} %get-tuple-element.19), channel_id=1, source_target_pairs={{0,4},{4,0},{8,12},{12,8},{14,10},{10,14},{6,2},{2,6},{1,5},{5,1},... | collective-permute-start | bytes 786440 | tf_op jit(solution)/shard_map/ppermute | solution.py:212
  132.5 6.6 %collective-permute-start.29 = (bf16[512,256]{1,0:T(8,128)(2,1)}, bf16[512,256]{1,0:T(8,128)(2,1)S(1)}, u32[]{:S(2)}, u32[]{:S(2)}) collective-permute-start(bf16[512,256]{1,0:T(8,128)(2,1)} %get-tuple-element.20), channel_id=1, source_target_pairs={{0,4},{4,0},{8,12},{12,8},{14,10},{10,14},{6,2},{2,6},{1,5},{5,1},... | collective-permute-start | bytes 786440 | tf_op jit(solution)/shard_map/ppermute | solution.py:212
  134.1 6.6 %collective-permute-start.30 = (bf16[512,256]{1,0:T(8,128)(2,1)}, bf16[512,256]{1,0:T(8,128)(2,1)S(1)}, u32[]{:S(2)}, u32[]{:S(2)}) collective-permute-start(bf16[512,256]{1,0:T(8,128)(2,1)} %get-tuple-element.21), channel_id=1, source_target_pairs={{4,8},{8,4},{12,14},{14,12},{10,6},{6,10},{2,0},{0,2},{5,9},{9,5},... | collective-permute-start | bytes 786440 | tf_op jit(solution)/shard_map/ppermute | solution.py:212
  144.0 6.6 %collective-permute-start.31 = (bf16[512,256]{1,0:T(8,128)(2,1)}, bf16[512,256]{1,0:T(8,128)(2,1)S(1)}, u32[]{:S(2)}, u32[]{:S(2)}) collective-permute-start(bf16[512,256]{1,0:T(8,128)(2,1)} %last.1.own), channel_id=1, source_target_pairs={{0,2},{2,0},{1,3},{3,1},{4,6},{6,4},{5,7},{7,5},{8,10},{10,8},{9,1... | collective-permute-start | bytes 786440 | tf_op jit(solution)/shard_map/ppermute | solution.py:212
  (32 other events, 241.9 us)

commit v3 on v2

--- a/solution.py
+++ b/solution.py
@@ -38,7 +38,7 @@
     return lax.dot_general(a, b, (((1,), (1,)), ((), ())), preferred_element_type=F32)
 
 
-def call(kernel, out_shapes, place, args, name, vmem_mib=56):
+def call(kernel, out_shapes, place, args, name, vmem_mib):
     vmem = pl.BlockSpec(memory_space=pltpu.VMEM)
     single = isinstance(out_shapes, jax.ShapeDtypeStruct)
     return pl.pallas_call(
@@ -83,7 +83,7 @@
     total = sum(r.shape[0] for r in rows)
     return call(
         functools.partial(features_kernel, len(rows)),
-        like((total, 2 * weights[0].shape[1])), place, (*rows, *weights, *phases), "features",
+        like((total, 2 * weights[0].shape[1])), place, (*rows, *weights, *phases), "features", 14,
     )
 
 
@@ -133,7 +133,7 @@
     n_feat = groups[0][1].shape[1]
     return call(
         functools.partial(gradient_kernel, shape_of(groups, stacked), part, len(earlier)),
-        like((padded, n_feat), F32), place, (*earlier, *flat(groups)), "gradient",
+        like((padded, n_feat), F32), place, (*earlier, *flat(groups)), "gradient", 20,
     )
 
 
@@ -160,7 +160,7 @@
     outs = (like(coefficients.shape, F32), like((partial_gradient.shape[0], coefficients.shape[1])))
     return call(
         functools.partial(solve_kernel, shape_of(groups, stacked), part),
-        outs, place, (*flat(groups), partial_gradient, inverse, coefficients), "solve",
+        outs, place, (*flat(groups), partial_gradient, inverse, coefficients), "solve", 24,
     )
 
 
@@ -234,7 +234,7 @@
 
     x0 = lax.dynamic_slice_in_dim(inputs, (2 * x + c) * part, part, 0)
     r0 = call(
-        residual_kernel, like((padded, 2 * part)), place, (labels[None, :], predictions), "residual"
+        residual_kernel, like((padded, 2 * part)), place, (labels[None, :], predictions), "residual", 6
     )
 
     def around(own):
@@ -256,7 +256,7 @@
     new_coefficients, sent = solve(place, groups[4:], (True,), part, first, inverse_blocks[0], coefficients)
 
     def step(kernel, k, received, shapes, name):
-        return call(kernel, tuple(like(s) for s in shapes), place, (sent, *groups[k][1:], *received), name)
+        return call(kernel, tuple(like(s) for s in shapes), place, (sent, *groups[k][1:], *received), name, 8)
 
     piece, block = (padded, part), (padded, 2 * part)
     a4, b4 = step(far_kernel, 4, (), (piece, piece), "far")
@@ -265,7 +265,7 @@
     e1, o1 = step(middle_kernel, 1, (O(o2), E(e2)), (block, block), "first")
     (own,) = step(last_kernel, 0, (E(e1), O(o1)), (block,), "last")
     other = swap(own, "blocks", [(0, 1)])
-    new = call(apply_kernel, like(predictions.shape, F32), place, (predictions, own, other), "apply")
+    new = call(apply_kernel, like(predictions.shape, F32), place, (predictions, own, other), "apply", 6)
     return new_coefficients.T, new.T
 
 

time: 154 us -> 113 us (0.73)
  Pallas kernels: 68.9 us -> 31.6 us
  local copies, waits for them, and re-layouts: 12.6 us -> 5.57 us
  waiting for transfers between devices: 34.3 us -> 37.5 us
    pallas_call x15, Pallas kernels: 68.9 us -> 31.6 us  [call(): pl.pallas_call(kernel, out_shape=out_shapes, in_specs=[pl.BlockSpec(memor...]
    unnamed x64 -> x16, local copies, waits for them, and re-layouts: 10.1 us -> 4.83 us
    ppermute x32, waiting for transfers between devices: 34.3 us -> 37.5 us  [swap(): lax.ppermute(x, axes, [p for a, b in pairs for p in ((a, b), (b, a))])]
    slice x4, local copies, waits for them, and re-layouts: 1.85 us -> 0.04 us  [around(): e4, o4 = (E(o3[:half]), O(e3[half:]))]
  transfers between devices with their start and end apart: 32 -> 32, of which waited for: 14 -> 15; matrix products, arithmetic and copies ran while one was open for 2% -> 1% of each run, Pallas kernels for 28% -> 17%
where the time goes in v3:
time: 113 us; the launch traced here: 112 us
  waiting for transfers between devices  37.5 us (33%)
  starting transfers between devices  36.6 us (32%)
  Pallas kernels  31.6 us (28%)
  local copies, waits for them, and re-layouts  5.57 us (5%)
    ppermute x32, waiting for transfers between devices, swap(): lax.ppermute(x, axes, [p for a, b in pairs for p in ((a, b), (b, a))])  37.5 us
    ppermute x32, starting transfers between devices, swap(): lax.ppermute(x, axes, [p for a, b in pairs for p in ((a, b), (b, a))])  36.6 us
    pallas_call x15, Pallas kernels, call(): pl.pallas_call(kernel, out_shape=out_shapes, in_specs=[pl.BlockSpec(memor...  31.6 us
    unnamed x16, local copies, waits for them, and re-layouts  4.83 us
  transfers between devices with their start and end apart: 32, of which 15 were waited for; matrix products, arithmetic and copies ran while one was open for 1% of the time, Pallas kernels for 17%

profile of v3, /device:TPU:0, one launch (start us, length us, event | category | flops | bytes accessed | tf_op | source)
XLA Modules:
  0.0 112.3 jit_solution(5149643730554430823)
XLA Ops:
  1.9 3.1 %collective-permute-start.12 = (bf16[128,1024]{1,0:T(8,128)(2,1)S(1)}, bf16[128,1024]{1,0:T(8,128)(2,1)}, u32[]{:S(2)}, u32[]{:S(2)}) collective-permute-start(bf16[128,1024]{1,0:T(8,128)(2,1)S(1)} %constant_dynamic-slice_fusion.refs_0_), channel_id=1, source_target_pairs={{0,4},{4,0},{8,12},{12,8},{14,10},{10,14},{6,2},{2,6},{1,5},{5,1},... | collective-permute-start | bytes 786440 | tf_op jit(solution)/shard_map/ppermute | solution.py:212
  5.0 1.5 %collective-permute-start.8 = (bf16[128,1024]{1,0:T(8,128)(2,1)S(1)}, bf16[128,1024]{1,0:T(8,128)(2,1)}, u32[]{:S(2)}, u32[]{:S(2)}) collective-permute-start(bf16[128,1024]{1,0:T(8,128)(2,1)S(1)} %constant_dynamic-slice_fusion.refs_0_), channel_id=1, source_target_pairs={{4,8},{8,4},{12,14},{14,12},{10,6},{6,10},{2,0},{0,2},{5,9},{9,5},... | collective-permute-start | bytes 786440 | tf_op jit(solution)/shard_map/ppermute | solution.py:212
  9.1 1.7 %collective-permute-start.4 = (bf16[512,256]{1,0:T(8,128)(2,1)S(1)}, bf16[512,256]{1,0:T(8,128)(2,1)S(1)}, u32[]{:S(2)}, u32[]{:S(2)}) collective-permute-start(bf16[512,256]{1,0:T(8,128)(2,1)S(1)} %residual.1.refs_0_), channel_id=1, source_target_pairs={{0,4},{4,0},{8,12},{12,8},{14,10},{10,14},{6,2},{2,6},{1,5},{5,1},... | collective-permute-start | bytes 786440 | tf_op jit(solution)/shard_map/ppermute | solution.py:212
  11.6 1.9 %collective-permute-start.13 = (bf16[128,1024]{1,0:T(8,128)(2,1)}, bf16[128,1024]{1,0:T(8,128)(2,1)S(1)}, u32[]{:S(2)}, u32[]{:S(2)}) collective-permute-start(bf16[128,1024]{1,0:T(8,128)(2,1)} %collective-permute-done.12.refs_0_), channel_id=1, source_target_pairs={{4,8},{8,4},{12,14},{14,12},{10,6},{6,10},{2,0},{0,2},{5,9},{9,5},... | collective-permute-start | bytes 786440 | tf_op jit(solution)/shard_map/ppermute | solution.py:212
  13.5 2.4 %collective-permute-start.9 = (bf16[128,1024]{1,0:T(8,128)(2,1)}, bf16[128,1024]{1,0:T(8,128)(2,1)S(1)}, u32[]{:S(2)}, u32[]{:S(2)}) collective-permute-start(bf16[128,1024]{1,0:T(8,128)(2,1)} %collective-permute-done.8.refs_1_), channel_id=1, source_target_pairs={{0,4},{4,0},{8,12},{12,8},{14,10},{10,14},{6,2},{2,6},{1,5},{5,1},... | collective-permute-start | bytes 786440 | tf_op jit(solution)/shard_map/ppermute | solution.py:212
  19.7 1.6 %collective-permute-start.14 = (bf16[128,1024]{1,0:T(8,128)(2,1)S(1)}, bf16[128,1024]{1,0:T(8,128)(2,1)S(1)}, u32[]{:S(2)}, u32[]{:S(2)}) collective-permute-start(bf16[128,1024]{1,0:T(8,128)(2,1)S(1)} %collective-permute-done.13.refs_1_), channel_id=1, source_target_pairs={{0,4},{4,0},{8,12},{12,8},{14,10},{10,14},{6,2},{2,6},{1,5},{5,1},... | collective-permute-start | bytes 786440 | tf_op jit(solution)/shard_map/ppermute | solution.py:212
  21.4 1.6 %collective-permute-done.9.refs_0_ = bf16[128,1024]{1,0:T(8,128)(2,1)S(1)} collective-permute-done((bf16[128,1024]{1,0:T(8,128)(2,1)}, bf16[128,1024]{1,0:T(8,128)(2,1)S(1)}, u32[]{:S(2)}, u32[]{:S(2)}) %collective-permute-start.9) | collective-permute-done | bytes 262176 | tf_op jit(solution)/shard_map/ppermute | solution.py:212
  23.0 1.8 %collective-permute-start.10 = (bf16[128,1024]{1,0:T(8,128)(2,1)S(1)}, bf16[128,1024]{1,0:T(8,128)(2,1)S(1)}, u32[]{:S(2)}, u32[]{:S(2)}) collective-permute-start(bf16[128,1024]{1,0:T(8,128)(2,1)S(1)} %collective-permute-done.9.refs_0_), channel_id=1, source_target_pairs={{4,8},{8,4},{12,14},{14,12},{10,6},{6,10},{2,0},{0,2},{5,9},{9,5},... | collective-permute-start | bytes 786440 | tf_op jit(solution)/shard_map/ppermute | solution.py:212
  24.8 2.0 %collective-permute-done.refs_4_ = bf16[512,256]{1,0:T(8,128)(2,1)S(1)} collective-permute-done((bf16[512,256]{1,0:T(8,128)(2,1)S(1)}, bf16[512,256]{1,0:T(8,128)(2,1)S(1)}, u32[]{:S(2)}, u32[]{:S(2)}) %collective-permute-start) | collective-permute-done | bytes 262176 | tf_op jit(solution)/shard_map/ppermute | solution.py:212
  27.9 1.6 %copy-done.1 = bf16[1024,1024]{1,0:T(8,128)(2,1)S(1)} copy-done((bf16[1024,1024]{1,0:T(8,128)(2,1)S(1)}, bf16[1024,1024]{1,0:T(8,128)(2,1)}, u32[]{:S(2)}) %copy-start.1) | copy-done | bytes 2097176
  29.5 3.5 %features.7.refs_5_.mine = bf16[256,2048]{1,0:T(8,128)(2,1)S(1)} custom-call(s32[3]{0:T(128)S(1)} %pad_add_fusion.place, bf16[128,1024]{1,0:T(8,128)(2,1)} %collective-permute-done.12.refs_0_, bf16[128,1024]{1,0:T(8,128)(2,1)} %collective-permute-done.8.refs_1_, bf16[1024,1024]{1,0:T(8,128)(2,1)S(1)} %copy-done.1, ...), custom_call_target="tpu_custom_call" | custom-call | tf_op jit(solution)/shard_map/features/pallas_call | solution.py:44
  34.2 3.0 %features.8.refs_9_.mine = bf16[256,2048]{1,0:T(8,128)(2,1)S(1)} custom-call(s32[3]{0:T(128)S(1)} %pad_add_fusion.place, bf16[128,1024]{1,0:T(8,128)(2,1)S(1)} %collective-permute-done.9.refs_0_, bf16[128,1024]{1,0:T(8,128)(2,1)S(1)} %collective-permute-done.13.refs_1_, bf16[1024,1024]{1,0:T(8,128)(2,1)S(1)} %copy-done.1, ...), custom_call_target="tpu_custom_call" | custom-call | tf_op jit(solution)/shard_map/features/pallas_call | solution.py:44
  37.5 3.0 %features.9.refs_3_.mine = bf16[256,2048]{1,0:T(8,128)(2,1)S(1)} custom-call(s32[3]{0:T(128)S(1)} %pad_add_fusion.place, bf16[128,1024]{1,0:T(8,128)(2,1)S(1)} %collective-permute-done.14.refs_0_, bf16[128,1024]{1,0:T(8,128)(2,1)S(1)} %collective-permute-done.10.refs_1_, bf16[1024,1024]{1,0:T(8,128)(2,1)S(1)} %copy-done.1, ...), custom_call_target="tpu_custom_call" | custom-call | tf_op jit(solution)/shard_map/features/pallas_call | solution.py:44
  41.0 1.6 %collective-permute-start.15 = (bf16[64,1024]{1,0:T(8,128)(2,1)S(1)}, bf16[64,1024]{1,0:T(8,128)(2,1)S(1)}, u32[]{:S(2)}, u32[]{:S(2)}) collective-permute-start(bf16[64,1024]{1,0:T(8,128)(2,1)S(1)} %slice.19), channel_id=1, source_target_pairs={{4,8},{8,4},{12,14},{14,12},{10,6},{6,10},{2,0},{0,2},{5,9},{9,5},... | collective-permute-start | bytes 393224 | tf_op jit(solution)/shard_map/ppermute | solution.py:212
  42.6 1.6 %collective-permute-start.11 = (bf16[64,1024]{1,0:T(8,128)(2,1)S(1)}, bf16[64,1024]{1,0:T(8,128)(2,1)S(1)}, u32[]{:S(2)}, u32[]{:S(2)}) collective-permute-start(bf16[64,1024]{1,0:T(8,128)(2,1)S(1)} %slice.18), channel_id=1, source_target_pairs={{0,4},{4,0},{8,12},{12,8},{14,10},{10,14},{6,2},{2,6},{1,5},{5,1},... | collective-permute-start | bytes 393224 | tf_op jit(solution)/shard_map/ppermute | solution.py:212
  44.2 2.4 %collective-permute-done.15.refs_1_ = bf16[64,1024]{1,0:T(8,128)(2,1)S(1)} collective-permute-done((bf16[64,1024]{1,0:T(8,128)(2,1)S(1)}, bf16[64,1024]{1,0:T(8,128)(2,1)S(1)}, u32[]{:S(2)}, u32[]{:S(2)}) %collective-permute-start.15) | collective-permute-done | bytes 131104 | tf_op jit(solution)/shard_map/ppermute | solution.py:212
  48.1 1.8 %features.6.refs_1_.mine = bf16[128,2048]{1,0:T(8,128)(2,1)S(1)} custom-call(s32[3]{0:T(128)S(1)} %pad_add_fusion.place, bf16[128,1024]{1,0:T(8,128)(2,1)S(1)} %constant_dynamic-slice_fusion.refs_0_, bf16[1024,1024]{1,0:T(8,128)(2,1)S(1)} %copy-done.1, bf16[1024,1024]{1,0:T(8,128)(2,1)S(1)} %collective-permute-done.16.refs_3_.refs_2_, ...), custom_call_target="tpu_custom_call" | custom-call | tf_op jit(solution)/shard_map/features/pallas_call | solution.py:44
  50.1 1.8 %features.5.refs_2_.mine = bf16[128,2048]{1,0:T(8,128)(2,1)S(1)} custom-call(s32[3]{0:T(128)S(1)} %pad_add_fusion.place, bf16[64,1024]{1,0:T(8,128)(2,1)S(1)} %collective-permute-done.11.refs_0_, bf16[64,1024]{1,0:T(8,128)(2,1)S(1)} %collective-permute-done.15.refs_1_, bf16[1024,1024]{1,0:T(8,128)(2,1)S(1)} %copy-done.2, ...), custom_call_target="tpu_custom_call" | custom-call | tf_op jit(solution)/shard_map/features/pallas_call | solution.py:44
  51.9 2.3 %collective-permute-done.2.refs_2_ = bf16[512,256]{1,0:T(8,128)(2,1)S(1)} collective-permute-done((bf16[512,256]{1,0:T(8,128)(2,1)S(1)}, bf16[512,256]{1,0:T(8,128)(2,1)S(1)}, u32[]{:S(2)}, u32[]{:S(2)}) %collective-permute-start.2) | collective-permute-done | bytes 262176 | tf_op jit(solution)/shard_map/ppermute | solution.py:212
  54.2 1.6 %collective-permute-start.7 = (bf16[256,256]{1,0:T(8,128)(2,1)S(1)}, bf16[256,256]{1,0:T(8,128)(2,1)S(1)}, u32[]{:S(2)}, u32[]{:S(2)}) collective-permute-start(bf16[256,256]{1,0:T(8,128)(2,1)S(1)} %slice.17), channel_id=1, source_target_pairs={{4,8},{8,4},{12,14},{14,12},{10,6},{6,10},{2,0},{0,2},{5,9},{9,5},... | collective-permute-start | bytes 393224 | tf_op jit(solution)/shard_map/ppermute | solution.py:212
  55.8 1.6 %collective-permute-start.3 = (bf16[256,256]{1,0:T(8,128)(2,1)S(1)}, bf16[256,256]{1,0:T(8,128)(2,1)S(1)}, u32[]{:S(2)}, u32[]{:S(2)}) collective-permute-start(bf16[256,256]{1,0:T(8,128)(2,1)S(1)} %slice.16), channel_id=1, source_target_pairs={{0,4},{4,0},{8,12},{12,8},{14,10},{10,14},{6,2},{2,6},{1,5},{5,1},... | collective-permute-start | bytes 393224 | tf_op jit(solution)/shard_map/ppermute | solution.py:212
  57.3 3.6 %gradient.2.refs_0_ = f32[512,2048]{1,0:T(8,128)S(1)} custom-call(s32[3]{0:T(128)S(1)} %pad_add_fusion.place, bf16[512,256]{1,0:T(8,128)(2,1)S(1)} %residual.1.refs_0_, bf16[128,2048]{1,0:T(8,128)(2,1)S(1)} %features.6.refs_1_.mine, bf16[128,2048]{1,0:T(8,128)(2,1)S(1)} %collective-permute-done.19.refs_2_.theirs, ...), custom_call_target="tpu_custom_call" | custom-call | tf_op jit(solution)/shard_map/gradient/pallas_call | solution.py:44
  60.9 1.8 %gradient.3.refs_4_ = f32[512,2048]{1,0:T(8,128)S(1)} custom-call(s32[3]{0:T(128)S(1)} %pad_add_fusion.place, f32[512,2048]{1,0:T(8,128)S(1)} %gradient.2.refs_0_, bf16[512,256]{1,0:T(8,128)(2,1)S(1)} %collective-permute-done.6.refs_1_, bf16[512,256]{1,0:T(8,128)(2,1)S(1)} %collective-permute-done.2.refs_2_, bf16[256,2048]{1,0:T(8,128)(2,1)S(1)} %features.9.refs_3_.mine, ...), custom_call_target="tpu_custom_call" | custom-call | tf_op jit(solution)/shard_map/gradient/pallas_call | solution.py:44
  63.4 5.6 %solve.1 = (f32[500,512]{1,0:T(8,128)}, bf16[512,512]{1,0:T(8,128)(2,1)S(1)}) custom-call(s32[3]{0:T(128)S(1)} %pad_add_fusion.place, bf16[256,256]{1,0:T(8,128)(2,1)S(1)} %collective-permute-done.3.refs_0_, bf16[256,256]{1,0:T(8,128)(2,1)S(1)} %collective-permute-done.7.refs_1_, bf16[128,2048]{1,0:T(8,128)(2,1)S(1)} %features.5.refs_2_.mine, ...), custom_call_target="tpu_custom_call" | custom-call | tf_op jit(solution)/shard_map/solve/pallas_call | solution.py:44
  71.1 4.3 %collective-permute-done.23.in_e = bf16[512,128]{1,0:T(8,128)(2,1)S(1)} collective-permute-done((bf16[512,128]{1,0:T(8,128)(2,1)S(1)}, bf16[512,128]{1,0:T(8,128)(2,1)S(1)}, u32[]{:S(2)}, u32[]{:S(2)}) %collective-permute-start.23) | collective-permute-done | bytes 131104 | tf_op jit(solution)/shard_map/ppermute | solution.py:212
  77.3 1.8 %collective-permute-start.26 = (bf16[512,256]{1,0:T(8,128)(2,1)S(1)}, bf16[512,256]{1,0:T(8,128)(2,1)S(1)}, u32[]{:S(2)}, u32[]{:S(2)}) collective-permute-start(bf16[512,256]{1,0:T(8,128)(2,1)S(1)} %get-tuple-element.17), channel_id=1, source_target_pairs={{0,4},{4,0},{8,12},{12,8},{14,10},{10,14},{6,2},{2,6},{1,5},{5,1},... | collective-permute-start | bytes 786440 | tf_op jit(solution)/shard_map/ppermute | solution.py:212
  79.1 4.7 %collective-permute-done.25.in_e = bf16[512,256]{1,0:T(8,128)(2,1)S(1)} collective-permute-done((bf16[512,256]{1,0:T(8,128)(2,1)S(1)}, bf16[512,256]{1,0:T(8,128)(2,1)S(1)}, u32[]{:S(2)}, u32[]{:S(2)}) %collective-permute-start.25) | collective-permute-done | bytes 262176 | tf_op jit(solution)/shard_map/ppermute | solution.py:212
  88.1 3.7 %collective-permute-done.27.in_e = bf16[512,256]{1,0:T(8,128)(2,1)S(1)} collective-permute-done((bf16[512,256]{1,0:T(8,128)(2,1)S(1)}, bf16[512,256]{1,0:T(8,128)(2,1)S(1)}, u32[]{:S(2)}, u32[]{:S(2)}) %collective-permute-start.27) | collective-permute-done | bytes 262176 | tf_op jit(solution)/shard_map/ppermute | solution.py:212
  96.3 4.2 %collective-permute-done.29.in_e = bf16[512,256]{1,0:T(8,128)(2,1)S(1)} collective-permute-done((bf16[512,256]{1,0:T(8,128)(2,1)S(1)}, bf16[512,256]{1,0:T(8,128)(2,1)S(1)}, u32[]{:S(2)}, u32[]{:S(2)}) %collective-permute-start.29) | collective-permute-done | bytes 262176 | tf_op jit(solution)/shard_map/ppermute | solution.py:212
  100.5 2.7 %collective-permute-done.30.in_o = bf16[512,256]{1,0:T(8,128)(2,1)S(1)} collective-permute-done((bf16[512,256]{1,0:T(8,128)(2,1)S(1)}, bf16[512,256]{1,0:T(8,128)(2,1)S(1)}, u32[]{:S(2)}, u32[]{:S(2)}) %collective-permute-start.30) | collective-permute-done | bytes 262176 | tf_op jit(solution)/shard_map/ppermute | solution.py:212
  105.0 5.6 %collective-permute-done.31.other = bf16[512,256]{1,0:T(8,128)(2,1)S(1)} collective-permute-done((bf16[512,256]{1,0:T(8,128)(2,1)S(1)}, bf16[512,256]{1,0:T(8,128)(2,1)S(1)}, u32[]{:S(2)}, u32[]{:S(2)}) %collective-permute-start.31) | collective-permute-done | bytes 262176 | tf_op jit(solution)/shard_map/ppermute | solution.py:212
  110.6 1.7 %apply.1 = f32[500,512]{1,0:T(8,128)} custom-call(s32[3]{0:T(128)S(1)} %pad_add_fusion.place, f32[500,512]{1,0:T(8,128)S(1)} %bitcast.11, bf16[512,256]{1,0:T(8,128)(2,1)S(1)} %last.1.own, bf16[512,256]{1,0:T(8,128)(2,1)S(1)} %collective-permute-done.31.other), custom_call_target="tpu_custom_call" | custom-call | tf_op jit(solution)/shard_map/apply/pallas_call | solution.py:44
  (70 shorter events, 28.1 us)
Async XLA Ops:
  0.6 27.2 %collective-permute-start.16 = (bf16[1024,1024]{1,0:T(8,128)(2,1)}, bf16[1024,1024]{1,0:T(8,128)(2,1)S(1)}, u32[]{:S(2)}, u32[]{:S(2)}) collective-permute-start(bf16[1024,1024]{1,0:T(8,128)(2,1)} %refs_2_.7), channel_id=1, source_target_pairs={{0,1},{1,0},{2,3},{3,2},{4,5},{5,4},{6,7},{7,6},{8,9},{9,8},{10,11... | collective-permute-start | bytes 6291464 | tf_op jit(solution)/shard_map/ppermute | solution.py:212
  1.9 9.7 %collective-permute-start.12 = (bf16[128,1024]{1,0:T(8,128)(2,1)S(1)}, bf16[128,1024]{1,0:T(8,128)(2,1)}, u32[]{:S(2)}, u32[]{:S(2)}) collective-permute-start(bf16[128,1024]{1,0:T(8,128)(2,1)S(1)} %constant_dynamic-slice_fusion.refs_0_), channel_id=1, source_target_pairs={{0,4},{4,0},{8,12},{12,8},{14,10},{10,14},{6,2},{2,6},{1,5},{5,1},... | collective-permute-start | bytes 786440 | tf_op jit(solution)/shard_map/ppermute | solution.py:212
  5.0 8.5 %collective-permute-start.8 = (bf16[128,1024]{1,0:T(8,128)(2,1)S(1)}, bf16[128,1024]{1,0:T(8,128)(2,1)}, u32[]{:S(2)}, u32[]{:S(2)}) collective-permute-start(bf16[128,1024]{1,0:T(8,128)(2,1)S(1)} %constant_dynamic-slice_fusion.refs_0_), channel_id=1, source_target_pairs={{4,8},{8,4},{12,14},{14,12},{10,6},{6,10},{2,0},{0,2},{5,9},{9,5},... | collective-permute-start | bytes 786440 | tf_op jit(solution)/shard_map/ppermute | solution.py:212
  9.1 10.1 %collective-permute-start.4 = (bf16[512,256]{1,0:T(8,128)(2,1)S(1)}, bf16[512,256]{1,0:T(8,128)(2,1)S(1)}, u32[]{:S(2)}, u32[]{:S(2)}) collective-permute-start(bf16[512,256]{1,0:T(8,128)(2,1)S(1)} %residual.1.refs_0_), channel_id=1, source_target_pairs={{0,4},{4,0},{8,12},{12,8},{14,10},{10,14},{6,2},{2,6},{1,5},{5,1},... | collective-permute-start | bytes 786440 | tf_op jit(solution)/shard_map/ppermute | solution.py:212
  11.6 8.2 %collective-permute-start.13 = (bf16[128,1024]{1,0:T(8,128)(2,1)}, bf16[128,1024]{1,0:T(8,128)(2,1)S(1)}, u32[]{:S(2)}, u32[]{:S(2)}) collective-permute-start(bf16[128,1024]{1,0:T(8,128)(2,1)} %collective-permute-done.12.refs_0_), channel_id=1, source_target_pairs={{4,8},{8,4},{12,14},{14,12},{10,6},{6,10},{2,0},{0,2},{5,9},{9,5},... | collective-permute-start | bytes 786440 | tf_op jit(solution)/shard_map/ppermute | solution.py:212
  13.5 9.5 %collective-permute-start.9 = (bf16[128,1024]{1,0:T(8,128)(2,1)}, bf16[128,1024]{1,0:T(8,128)(2,1)S(1)}, u32[]{:S(2)}, u32[]{:S(2)}) collective-permute-start(bf16[128,1024]{1,0:T(8,128)(2,1)} %collective-permute-done.8.refs_1_), channel_id=1, source_target_pairs={{0,4},{4,0},{8,12},{12,8},{14,10},{10,14},{6,2},{2,6},{1,5},{5,1},... | collective-permute-start | bytes 786440 | tf_op jit(solution)/shard_map/ppermute | solution.py:212
  16.5 1.2 %collective-permute-start.17 = (bf16[1,1024]{1,0:T(2,128)(2,1)S(1)}, bf16[1,1024]{1,0:T(2,128)(2,1)S(1)}, u32[]{:S(2)}, u32[]{:S(2)}) collective-permute-start(bf16[1,1024]{1,0:T(2,128)(2,1)S(1)} %broadcast_in_dim.7.refs_4_.refs_3_), channel_id=1, source_target_pairs={{0,1},{1,0},{2,3},{3,2},{4,5},{5,4},{6,7},{7,6},{8,9},{9,8},{10,11... | collective-permute-start | bytes 6152 | tf_op jit(solution)/shard_map/ppermute | solution.py:212
  17.7 9.2 %collective-permute-start = (bf16[512,256]{1,0:T(8,128)(2,1)S(1)}, bf16[512,256]{1,0:T(8,128)(2,1)S(1)}, u32[]{:S(2)}, u32[]{:S(2)}) collective-permute-start(bf16[512,256]{1,0:T(8,128)(2,1)S(1)} %residual.1.refs_0_), channel_id=1, source_target_pairs={{4,8},{8,4},{12,14},{14,12},{10,6},{6,10},{2,0},{0,2},{5,9},{9,5},... | collective-permute-start | bytes 786440 | tf_op jit(solution)/shard_map/ppermute | solution.py:212
  19.2 13.9 %collective-permute-start.5 = (bf16[512,256]{1,0:T(8,128)(2,1)S(1)}, bf16[512,256]{1,0:T(8,128)(2,1)S(1)}, u32[]{:S(2)}, u32[]{:S(2)}) collective-permute-start(bf16[512,256]{1,0:T(8,128)(2,1)S(1)} %collective-permute-done.4.refs_3_), channel_id=1, source_target_pairs={{4,8},{8,4},{12,14},{14,12},{10,6},{6,10},{2,0},{0,2},{5,9},{9,5},... | collective-permute-start | bytes 786440 | tf_op jit(solution)/shard_map/ppermute | solution.py:212
  19.7 17.5 %collective-permute-start.14 = (bf16[128,1024]{1,0:T(8,128)(2,1)S(1)}, bf16[128,1024]{1,0:T(8,128)(2,1)S(1)}, u32[]{:S(2)}, u32[]{:S(2)}) collective-permute-start(bf16[128,1024]{1,0:T(8,128)(2,1)S(1)} %collective-permute-done.13.refs_1_), channel_id=1, source_target_pairs={{0,4},{4,0},{8,12},{12,8},{14,10},{10,14},{6,2},{2,6},{1,5},{5,1},... | collective-permute-start | bytes 786440 | tf_op jit(solution)/shard_map/ppermute | solution.py:212
  23.0 14.5 %collective-permute-start.10 = (bf16[128,1024]{1,0:T(8,128)(2,1)S(1)}, bf16[128,1024]{1,0:T(8,128)(2,1)S(1)}, u32[]{:S(2)}, u32[]{:S(2)}) collective-permute-start(bf16[128,1024]{1,0:T(8,128)(2,1)S(1)} %collective-permute-done.9.refs_0_), channel_id=1, source_target_pairs={{4,8},{8,4},{12,14},{14,12},{10,6},{6,10},{2,0},{0,2},{5,9},{9,5},... | collective-permute-start | bytes 786440 | tf_op jit(solution)/shard_map/ppermute | solution.py:212
  26.9 14.1 %collective-permute-start.1 = (bf16[512,256]{1,0:T(8,128)(2,1)S(1)}, bf16[512,256]{1,0:T(8,128)(2,1)S(1)}, u32[]{:S(2)}, u32[]{:S(2)}) collective-permute-start(bf16[512,256]{1,0:T(8,128)(2,1)S(1)} %collective-permute-done.refs_4_), channel_id=1, source_target_pairs={{0,4},{4,0},{8,12},{12,8},{14,10},{10,14},{6,2},{2,6},{1,5},{5,1},... | collective-permute-start | bytes 786440 | tf_op jit(solution)/shard_map/ppermute | solution.py:212
  33.0 22.8 %collective-permute-start.20 = (bf16[256,2048]{1,0:T(8,128)(2,1)S(1)}, bf16[256,2048]{1,0:T(8,128)(2,1)S(1)}, u32[]{:S(2)}, u32[]{:S(2)}) collective-permute-start(bf16[256,2048]{1,0:T(8,128)(2,1)S(1)} %features.7.refs_5_.mine), channel_id=1, source_target_pairs={{0,1},{1,0},{2,3},{3,2},{4,5},{5,4},{6,7},{7,6},{8,9},{9,8},{10,11... | collective-permute-start | bytes 3145736 | tf_op jit(solution)/shard_map/ppermute | solution.py:212
  33.1 9.5 %collective-permute-start.6 = (bf16[512,256]{1,0:T(8,128)(2,1)S(1)}, bf16[512,256]{1,0:T(8,128)(2,1)S(1)}, u32[]{:S(2)}, u32[]{:S(2)}) collective-permute-start(bf16[512,256]{1,0:T(8,128)(2,1)S(1)} %collective-permute-done.5.refs_8_), channel_id=1, source_target_pairs={{0,4},{4,0},{8,12},{12,8},{14,10},{10,14},{6,2},{2,6},{1,5},{5,1},... | collective-permute-start | bytes 786440 | tf_op jit(solution)/shard_map/ppermute | solution.py:212
  37.3 20.1 %collective-permute-start.21 = (bf16[256,2048]{1,0:T(8,128)(2,1)S(1)}, bf16[256,2048]{1,0:T(8,128)(2,1)S(1)}, u32[]{:S(2)}, u32[]{:S(2)}) collective-permute-start(bf16[256,2048]{1,0:T(8,128)(2,1)S(1)} %features.8.refs_9_.mine), channel_id=1, source_target_pairs={{0,1},{1,0},{2,3},{3,2},{4,5},{5,4},{6,7},{7,6},{8,9},{9,8},{10,11... | collective-permute-start | bytes 3145736 | tf_op jit(solution)/shard_map/ppermute | solution.py:212
  40.6 20.4 %collective-permute-start.22 = (bf16[256,2048]{1,0:T(8,128)(2,1)S(1)}, bf16[256,2048]{1,0:T(8,128)(2,1)S(1)}, u32[]{:S(2)}, u32[]{:S(2)}) collective-permute-start(bf16[256,2048]{1,0:T(8,128)(2,1)S(1)} %features.9.refs_3_.mine), channel_id=1, source_target_pairs={{0,1},{1,0},{2,3},{3,2},{4,5},{5,4},{6,7},{7,6},{8,9},{9,8},{10,11... | collective-permute-start | bytes 3145736 | tf_op jit(solution)/shard_map/ppermute | solution.py:212
  41.0 5.6 %collective-permute-start.15 = (bf16[64,1024]{1,0:T(8,128)(2,1)S(1)}, bf16[64,1024]{1,0:T(8,128)(2,1)S(1)}, u32[]{:S(2)}, u32[]{:S(2)}) collective-permute-start(bf16[64,1024]{1,0:T(8,128)(2,1)S(1)} %slice.19), channel_id=1, source_target_pairs={{4,8},{8,4},{12,14},{14,12},{10,6},{6,10},{2,0},{0,2},{5,9},{9,5},... | collective-permute-start | bytes 393224 | tf_op jit(solution)/shard_map/ppermute | solution.py:212
  42.6 7.4 %collective-permute-start.11 = (bf16[64,1024]{1,0:T(8,128)(2,1)S(1)}, bf16[64,1024]{1,0:T(8,128)(2,1)S(1)}, u32[]{:S(2)}, u32[]{:S(2)}) collective-permute-start(bf16[64,1024]{1,0:T(8,128)(2,1)S(1)} %slice.18), channel_id=1, source_target_pairs={{0,4},{4,0},{8,12},{12,8},{14,10},{10,14},{6,2},{2,6},{1,5},{5,1},... | collective-permute-start | bytes 393224 | tf_op jit(solution)/shard_map/ppermute | solution.py:212
  46.6 7.5 %collective-permute-start.2 = (bf16[512,256]{1,0:T(8,128)(2,1)S(1)}, bf16[512,256]{1,0:T(8,128)(2,1)S(1)}, u32[]{:S(2)}, u32[]{:S(2)}) collective-permute-start(bf16[512,256]{1,0:T(8,128)(2,1)S(1)} %collective-permute-done.1.refs_7_), channel_id=1, source_target_pairs={{4,8},{8,4},{12,14},{14,12},{10,6},{6,10},{2,0},{0,2},{5,9},{9,5},... | collective-permute-start | bytes 786440 | tf_op jit(solution)/shard_map/ppermute | solution.py:212
  50.0 4.2 %collective-permute-start.19 = (bf16[128,2048]{1,0:T(8,128)(2,1)S(1)}, bf16[128,2048]{1,0:T(8,128)(2,1)S(1)}, u32[]{:S(2)}, u32[]{:S(2)}) collective-permute-start(bf16[128,2048]{1,0:T(8,128)(2,1)S(1)} %features.6.refs_1_.mine), channel_id=1, source_target_pairs={{0,1},{1,0},{2,3},{3,2},{4,5},{5,4},{6,7},{7,6},{8,9},{9,8},{10,11... | collective-permute-start | bytes 1572872 | tf_op jit(solution)/shard_map/ppermute | solution.py:212
  54.2 8.6 %collective-permute-start.18 = (bf16[128,2048]{1,0:T(8,128)(2,1)S(1)}, bf16[128,2048]{1,0:T(8,128)(2,1)S(1)}, u32[]{:S(2)}, u32[]{:S(2)}) collective-permute-start(bf16[128,2048]{1,0:T(8,128)(2,1)S(1)} %features.5.refs_2_.mine), channel_id=1, source_target_pairs={{0,1},{1,0},{2,3},{3,2},{4,5},{5,4},{6,7},{7,6},{8,9},{9,8},{10,11... | collective-permute-start | bytes 1572872 | tf_op jit(solution)/shard_map/ppermute | solution.py:212
  54.2 8.5 %collective-permute-start.7 = (bf16[256,256]{1,0:T(8,128)(2,1)S(1)}, bf16[256,256]{1,0:T(8,128)(2,1)S(1)}, u32[]{:S(2)}, u32[]{:S(2)}) collective-permute-start(bf16[256,256]{1,0:T(8,128)(2,1)S(1)} %slice.17), channel_id=1, source_target_pairs={{4,8},{8,4},{12,14},{14,12},{10,6},{6,10},{2,0},{0,2},{5,9},{9,5},... | collective-permute-start | bytes 393224 | tf_op jit(solution)/shard_map/ppermute | solution.py:212
  55.8 7.0 %collective-permute-start.3 = (bf16[256,256]{1,0:T(8,128)(2,1)S(1)}, bf16[256,256]{1,0:T(8,128)(2,1)S(1)}, u32[]{:S(2)}, u32[]{:S(2)}) collective-permute-start(bf16[256,256]{1,0:T(8,128)(2,1)S(1)} %slice.16), channel_id=1, source_target_pairs={{0,4},{4,0},{8,12},{12,8},{14,10},{10,14},{6,2},{2,6},{1,5},{5,1},... | collective-permute-start | bytes 393224 | tf_op jit(solution)/shard_map/ppermute | solution.py:212
  70.0 5.4 %collective-permute-start.23 = (bf16[512,128]{1,0:T(8,128)(2,1)S(1)}, bf16[512,128]{1,0:T(8,128)(2,1)S(1)}, u32[]{:S(2)}, u32[]{:S(2)}) collective-permute-start(bf16[512,128]{1,0:T(8,128)(2,1)S(1)} %get-tuple-element.14), channel_id=1, source_target_pairs={{0,4},{4,0},{8,12},{12,8},{14,10},{10,14},{6,2},{2,6},{1,5},{5,1},... | collective-permute-start | bytes 393224 | tf_op jit(solution)/shard_map/ppermute | solution.py:212
  70.6 5.1 %collective-permute-start.24 = (bf16[512,128]{1,0:T(8,128)(2,1)S(1)}, bf16[512,128]{1,0:T(8,128)(2,1)S(1)}, u32[]{:S(2)}, u32[]{:S(2)}) collective-permute-start(bf16[512,128]{1,0:T(8,128)(2,1)S(1)} %get-tuple-element.15), channel_id=1, source_target_pairs={{4,8},{8,4},{12,14},{14,12},{10,6},{6,10},{2,0},{0,2},{5,9},{9,5},... | collective-permute-start | bytes 393224 | tf_op jit(solution)/shard_map/ppermute | solution.py:212
  76.6 7.2 %collective-permute-start.25 = (bf16[512,256]{1,0:T(8,128)(2,1)S(1)}, bf16[512,256]{1,0:T(8,128)(2,1)S(1)}, u32[]{:S(2)}, u32[]{:S(2)}) collective-permute-start(bf16[512,256]{1,0:T(8,128)(2,1)S(1)} %get-tuple-element.16), channel_id=1, source_target_pairs={{4,8},{8,4},{12,14},{14,12},{10,6},{6,10},{2,0},{0,2},{5,9},{9,5},... | collective-permute-start | bytes 786440 | tf_op jit(solution)/shard_map/ppermute | solution.py:212
  77.3 7.0 %collective-permute-start.26 = (bf16[512,256]{1,0:T(8,128)(2,1)S(1)}, bf16[512,256]{1,0:T(8,128)(2,1)S(1)}, u32[]{:S(2)}, u32[]{:S(2)}) collective-permute-start(bf16[512,256]{1,0:T(8,128)(2,1)S(1)} %get-tuple-element.17), channel_id=1, source_target_pairs={{0,4},{4,0},{8,12},{12,8},{14,10},{10,14},{6,2},{2,6},{1,5},{5,1},... | collective-permute-start | bytes 786440 | tf_op jit(solution)/shard_map/ppermute | solution.py:212
  85.4 6.4 %collective-permute-start.27 = (bf16[512,256]{1,0:T(8,128)(2,1)S(1)}, bf16[512,256]{1,0:T(8,128)(2,1)S(1)}, u32[]{:S(2)}, u32[]{:S(2)}) collective-permute-start(bf16[512,256]{1,0:T(8,128)(2,1)S(1)} %get-tuple-element.18), channel_id=1, source_target_pairs={{4,8},{8,4},{12,14},{14,12},{10,6},{6,10},{2,0},{0,2},{5,9},{9,5},... | collective-permute-start | bytes 786440 | tf_op jit(solution)/shard_map/ppermute | solution.py:212
  86.7 6.4 %collective-permute-start.28 = (bf16[512,256]{1,0:T(8,128)(2,1)S(1)}, bf16[512,256]{1,0:T(8,128)(2,1)S(1)}, u32[]{:S(2)}, u32[]{:S(2)}) collective-permute-start(bf16[512,256]{1,0:T(8,128)(2,1)S(1)} %get-tuple-element.19), channel_id=1, source_target_pairs={{0,4},{4,0},{8,12},{12,8},{14,10},{10,14},{6,2},{2,6},{1,5},{5,1},... | collective-permute-start | bytes 786440 | tf_op jit(solution)/shard_map/ppermute | solution.py:212
  94.0 6.4 %collective-permute-start.29 = (bf16[512,256]{1,0:T(8,128)(2,1)S(1)}, bf16[512,256]{1,0:T(8,128)(2,1)S(1)}, u32[]{:S(2)}, u32[]{:S(2)}) collective-permute-start(bf16[512,256]{1,0:T(8,128)(2,1)S(1)} %get-tuple-element.20), channel_id=1, source_target_pairs={{0,4},{4,0},{8,12},{12,8},{14,10},{10,14},{6,2},{2,6},{1,5},{5,1},... | collective-permute-start | bytes 786440 | tf_op jit(solution)/shard_map/ppermute | solution.py:212
  95.5 7.7 %collective-permute-start.30 = (bf16[512,256]{1,0:T(8,128)(2,1)S(1)}, bf16[512,256]{1,0:T(8,128)(2,1)S(1)}, u32[]{:S(2)}, u32[]{:S(2)}) collective-permute-start(bf16[512,256]{1,0:T(8,128)(2,1)S(1)} %get-tuple-element.21), channel_id=1, source_target_pairs={{4,8},{8,4},{12,14},{14,12},{10,6},{6,10},{2,0},{0,2},{5,9},{9,5},... | collective-permute-start | bytes 786440 | tf_op jit(solution)/shard_map/ppermute | solution.py:212
  104.2 6.4 %collective-permute-start.31 = (bf16[512,256]{1,0:T(8,128)(2,1)S(1)}, bf16[512,256]{1,0:T(8,128)(2,1)S(1)}, u32[]{:S(2)}, u32[]{:S(2)}) collective-permute-start(bf16[512,256]{1,0:T(8,128)(2,1)S(1)} %last.1.own), channel_id=1, source_target_pairs={{0,2},{2,0},{1,3},{3,1},{4,6},{6,4},{5,7},{7,5},{8,10},{10,8},{9,1... | collective-permute-start | bytes 786440 | tf_op jit(solution)/shard_map/ppermute | solution.py:212
  (8 other events, 52.2 us)

commit v4 on v3

v4 whole, which is shorter than its diff:
```python
import functools

import jax
import jax.numpy as jnp
from jax import lax
from jax.experimental import pallas as pl
from jax.experimental.pallas import tpu as pltpu
from jax.sharding import PartitionSpec as P

DAMPING = 0.5
F32, BF16 = jnp.float32, jnp.bfloat16
LANES = 128

COS_TERMS = (
    0.9999999887556631, -0.49999988843399, 0.04166648574334225, -0.001388778673619495,
    2.4769518189949842e-05, -2.7075418374484127e-07, 1.7231808612122658e-09,
)
INV_TWO_PI = 0.15915494309189535
TWO_PI_HIGH = 6.28125
TWO_PI_LOW = 0.0019353071795864769


def cosine(angles):
    turns = jnp.round(angles * INV_TWO_PI)
    rest = (angles - turns * TWO_PI_HIGH) - turns * TWO_PI_LOW
    square = rest * rest
    result = jnp.full_like(square, COS_TERMS[-1])
    for term in COS_TERMS[-2::-1]:
        result = result * square + term
    return result


def dot(a, b):
    return jnp.dot(a, b, preferred_element_type=F32)


def dot_nt(a, b):
    return lax.dot_general(a, b, (((1,), (1,)), ((), ())), preferred_element_type=F32)


def call(kernel, out_shapes, place, args, name, vmem_mib, scratch=()):
    vmem = pl.BlockSpec(memory_space=pltpu.VMEM)
    single = isinstance(out_shapes, jax.ShapeDtypeStruct)
    return pl.pallas_call(
        kernel,
        out_shape=out_shapes,
        in_specs=[pl.BlockSpec(memory_space=pltpu.SMEM)] + [vmem] * len(args),
        out_specs=vmem if single else (vmem,) * len(out_shapes),
        scratch_shapes=scratch,
        compiler_params=pltpu.CompilerParams(vmem_limit_bytes=vmem_mib << 20),
        name=name,
    )(place, *args)


def like(shape, dtype=BF16):
    return jax.ShapeDtypeStruct(tuple(shape), dtype)


def lanes(index, size):
    return pl.ds(pl.multiple_of(index * size, size), size)


def message_kernel(place, inputs, labels, predictions, out):
    width = predictions.shape[0]
    part = out.shape[0] - LANES
    start = pl.multiple_of((2 * place[1] + place[2]) * part, part)
    out[:part] = inputs[pl.ds(start, part)]
    for i, k in enumerate(range(0, width, LANES)):
        size = min(LANES, width - k)
        if size < LANES:
            out[part:, 2 * part * i:2 * part * (i + 1)] = jnp.zeros((LANES, 2 * part), BF16)
        for j in (0, 1):
            own = lanes(2 * place[1] + (place[2] ^ j), part)
            classes = lax.broadcasted_iota(jnp.int32, (size, part), 0) + (place[2] * width + k)
            hit = (classes == labels[:, own]).astype(F32)
            at = slice(part * (2 * i + j), part * (2 * i + j + 1))
            out[part:part + size, at] = (hit - predictions[k:k + size, own]).astype(BF16)


def high_low(x):
    high = x.astype(BF16)
    return high, (x - high.astype(F32)).astype(BF16)


def split_kernel(place, x, high, low):
    high[...], low[...] = high_low(x[...])


TILE = 512


def block_kernel(n_rows, place, *refs):
    rows, (w_own, w_other, p_own, p_other, high, low, out, feats) = refs[:n_rows], refs[n_rows:]
    part = feats.shape[0] // n_rows
    inputs = [r[:part] for r in rows]
    inputs = inputs[0] if n_rows == 1 else jnp.concatenate(inputs, axis=0)
    half, depth = w_own.shape[1], high.shape[0]
    total = None
    for i, (weights, phases) in enumerate(((w_own, p_own), (w_other, p_other))):
        for k in range(0, half, TILE):
            at = pl.ds(pl.multiple_of((place[2] ^ i) * half + k, TILE), TILE)
            angles = dot(inputs, weights[:, k:k + TILE]) + phases[:, k:k + TILE].astype(F32)
            tile = cosine(angles).astype(BF16)
            feats[:, at] = tile
            product = dot_nt(tile, high[:, at]) + dot_nt(tile, low[:, at])
            total = product if total is None else total + product
    out[:, :depth], out[:, depth:2 * depth] = high_low(total)
    out[:, 2 * depth:] = feats[:, lanes(place[0], depth)]


def residual_of(ref, part):
    pieces = ref[ref.shape[0] - LANES:]
    pieces = [pieces[:, k:k + 2 * part] for k in range(0, pieces.shape[1], 2 * part)]
    return jnp.concatenate(pieces, axis=0)


def product_of(counts, refs, depth):
    total, at = None, 0
    for count in counts:
        mine, theirs = refs[at + count], refs[at + count + 1]
        part = mine.shape[0] // count
        pieces = [residual_of(refs[at + i], part) for i in range(count)]
        at += count + 2
        if count == 1:
            products = [dot(pieces[0], jnp.concatenate([mine[:, :2 * depth], theirs[:, :2 * depth]], axis=0))]
        else:
            sides = [jnp.concatenate([p[:, i * part:(i + 1) * part] for p in pieces], axis=1) for i in (0, 1)]
            products = [dot(side, q[:, :2 * depth]) for side, q in zip(sides, (mine, theirs))]
        for product in products:
            product = product[:, :depth] + product[:, depth:]
            total = product if total is None else total + product
    return total


def flat(groups):
    return [a for pieces, mine, theirs in groups for a in (*pieces, mine, theirs)]


def begin_kernel(counts, place, *refs):
    *pieces, out = refs
    out[...] = product_of(counts, pieces, out.shape[1])


def update_kernel(counts, place, *refs):
    *pieces, begun, coefficients, new, sent = refs
    update = DAMPING * (begun[...] + product_of(counts, pieces, begun.shape[1]))
    new[...] = coefficients[...] + update[:new.shape[0]]
    sent[...] = update.astype(BF16)


def own_change(sent, mine, theirs, rows=slice(None)):
    depth = sent.shape[1]
    pieces = [f[rows, 2 * depth:] for f in (mine, theirs)]
    return dot_nt(sent[...], jnp.concatenate(pieces, axis=0))


def far_kernel(place, sent, mine, out):
    out[...] = dot_nt(sent[...], mine[:, 2 * sent.shape[1]:]).astype(BF16)


def third_kernel(which, place, sent, mine, theirs, came, out):
    part = came.shape[1]
    own = own_change(sent, mine, theirs, slice(which * part, (which + 1) * part))
    for i in (0, 1):
        at = slice(i * part, (i + 1) * part)
        total = own[:, at] + came[...].astype(F32) if i != which else own[:, at]
        out[:, at] = total.astype(BF16)


def middle_kernel(which, place, sent, mine, theirs, came, out):
    part = came.shape[1] // 2
    own = own_change(sent, mine, theirs, slice(which * part, (which + 1) * part))
    out[...] = (own + came[...].astype(F32)).astype(BF16)


def last_kernel(place, sent, mine, theirs, in_a, in_b, out):
    came = in_a[...].astype(F32) + in_b[...].astype(F32)
    out[...] = (own_change(sent, mine, theirs) + came).astype(BF16)


def apply_kernel(place, predictions, own, other, new):
    width, part = new.shape[0], own.shape[1] // 2
    for i, source in enumerate((own, other)):
        for j in (0, 1):
            at = lanes(2 * (place[1] ^ i) + (place[2] ^ j), part)
            new[:, at] = predictions[:, at] + source[:width, j * part:(j + 1) * part].astype(F32)


def swap(x, axes, pairs):
    return lax.ppermute(x, axes, [p for a, b in pairs for p in ((a, b), (b, a))])


def ring_shards(n_rows, inputs, projection, phases, inverse_blocks, labels, predictions, coefficients):
    ring = [2 * z for z in range(n_rows)] + [2 * z + 1 for z in reversed(range(n_rows))]
    size = len(ring)
    even = [(ring[i], ring[i + 1]) for i in range(0, size, 2)]
    odd = [(ring[i], ring[(i + 1) % size]) for i in range(1, size, 2)]
    E = lambda x: swap(x, ("rows", "blocks"), even)
    O = lambda x: swap(x, ("rows", "blocks"), odd)
    C = lambda x: swap(x, "cols", [(0, 1)])

    z, x, c = (lax.axis_index(a) for a in ("rows", "blocks", "cols"))
    place = jnp.stack([z, x, c]).astype(jnp.int32)
    local_rows, width = predictions.shape
    part = local_rows // 4
    padded = -(-width // LANES) * LANES

    weights = (projection, C(projection))
    phases = phases[None, :]
    phases = (phases, C(phases))
    predictions, coefficients = predictions.T, coefficients.T
    depth = coefficients.shape[1]

    sent0 = call(
        message_kernel, like((part + LANES, inputs.shape[1])), place,
        (inputs, labels[None, :], predictions), "message", 8,
    )
    e1, o1 = E(sent0), O(sent0)
    e2, o2 = E(o1), O(e1)
    e3, o3 = E(o2), O(e2)
    e4, o4 = E(o3[:part]), O(e3[part:])
    inverse = call(
        split_kernel, (like(inverse_blocks.shape[1:]),) * 2, place, (inverse_blocks[0],), "split", 14
    )

    def block(*rows):
        out = like((len(rows) * part, 3 * depth))
        scratch = (pltpu.VMEM((len(rows) * part, 2 * projection.shape[1]), BF16),)
        args = (*rows, *weights, *phases, *inverse)
        mine = call(functools.partial(block_kernel, len(rows)), out, place, args, "block", 16, scratch)
        return mine, C(mine)

    b0, b1, b2, b3, b4 = block(sent0), block(e1, o1), block(e2, o2), block(e3, o3), block(e4)
    begun = call(
        functools.partial(begin_kernel, (1, 2, 2)), like((padded, depth), F32), place,
        flat([((sent0,), *b0), ((e1, o1), *b1), ((e2, o2), *b2)]), "begin", 14,
    )
    new_coefficients, sent = call(
        functools.partial(update_kernel, (2, 1)),
        (like(coefficients.shape, F32), like((padded, depth))), place,
        (*flat([((e3, o3), *b3), ((o4,), *b4)]), begun, coefficients), "update", 14,
    )

    piece, whole = like((padded, part)), like((padded, 2 * part))

    def hop(kernel, which, k, came, name):
        return call(functools.partial(kernel, which), whole, place, (sent, *k, came), name, 6)

    far_a = call(far_kernel, piece, place, (sent, b4[0]), "far", 6)
    far_b = call(far_kernel, piece, place, (sent, b4[1]), "far", 6)
    way_a, way_b = E(far_a), O(far_b)
    way_a, way_b = O(hop(third_kernel, 1, b3, way_a, "third")), E(hop(third_kernel, 0, b3, way_b, "third"))
    way_a, way_b = E(hop(middle_kernel, 0, b2, way_a, "second")), O(hop(middle_kernel, 1, b2, way_b, "second"))
    way_a, way_b = O(hop(middle_kernel, 1, b1, way_a, "first")), E(hop(middle_kernel, 0, b1, way_b, "first"))
    own = call(last_kernel, whole, place, (sent, *b0, way_a, way_b), "last", 6)
    other = swap(own, "blocks", [(0, 1)])
    new = call(apply_kernel, like(predictions.shape, F32), place, (predictions, own, other), "apply", 6)
    return new_coefficients.T, new.T


def plain_shards(inputs, projection, phases, inverse_blocks, labels, predictions, coefficients):
    out_width = predictions.shape[1]
    classes = lax.axis_index("cols") * out_width + jnp.arange(out_width, dtype=jnp.int32)
    onehot = (labels[:, None] == classes[None, :]).astype(F32)
    residual = (onehot - predictions).astype(BF16)
    angles = dot(inputs, projection) + phases.astype(F32)[None, :]
    half_features = jnp.cos(angles).astype(BF16)
    features_full = lax.all_gather(half_features, "cols", axis=1, tiled=True)
    own_gradient = lax.psum_scatter(
        lax.dot_general(features_full, residual, (((0,), (0,)), ((), ())), preferred_element_type=F32),
        "rows", scatter_dimension=0, tiled=True,
    )
    gradient_full = lax.all_gather(own_gradient, "rows", axis=0, tiled=True)
    update = DAMPING * jnp.dot(inverse_blocks[0], gradient_full, precision=lax.Precision.HIGHEST)
    sent = lax.all_gather(update.astype(BF16), "rows", axis=0, tiled=True)
    summed = lax.psum(dot(features_full, sent), "blocks")
    return coefficients + update, predictions + summed


def solution(mesh):
    n_rows, n_blocks = mesh.shape["rows"], mesh.shape["blocks"]
    small_ring = n_blocks == 2 and n_rows == 4 and mesh.shape["cols"] == 2
    shards = functools.partial(ring_shards, n_rows) if small_ring else plain_shards
    return jax.shard_map(
        shards,
        mesh=mesh,
        in_specs=(
            P(("groups", "rows"), None),
            P(None, ("groups", "blocks", "cols")),
            P(("groups", "blocks", "cols")),
            P(("groups", "blocks"), "rows", None),
            P(("groups", "rows")),
            P(("groups", "rows"), "cols"),
            P(("groups", "blocks", "rows"), "cols"),
        ),
        out_specs=(P(("groups", "blocks", "rows"), "cols"), P(("groups", "rows"), "cols")),
        check_vma=False,
    )
```

time: 113 us -> 125 us (1.11)
  waiting for transfers between devices: 37.5 us -> 59.4 us
  starting transfers between devices: 36.6 us -> 23.5 us
  Pallas kernels: 31.6 us -> 35.7 us
    ppermute x32 -> x24, waiting for transfers between devices: 37.5 us -> 59.4 us  [swap(): lax.ppermute(x, axes, [p for a, b in pairs for p in ((a, b), (b, a))])]
    ppermute x32 -> x24, starting transfers between devices: 36.6 us -> 23.5 us  [swap(): lax.ppermute(x, axes, [p for a, b in pairs for p in ((a, b), (b, a))])]
    pallas_call x15 -> x19, Pallas kernels: 31.6 us -> 35.7 us  [call(): pl.pallas_call(kernel, out_shape=out_shapes, in_specs=[pl.BlockSpec(memor...]
  transfers between devices with their start and end apart: 32 -> 24, of which waited for: 15 -> 12; matrix products, arithmetic and copies ran while one was open for 1% -> 0% of each run, Pallas kernels for 17% -> 24%
where the time goes in v4:
time: 125 us
  waiting for transfers between devices  59.4 us (48%)
  Pallas kernels  35.7 us (29%)
  starting transfers between devices  23.5 us (19%)
  local copies, waits for them, and re-layouts  5.58 us (4%)
    ppermute x24, waiting for transfers between devices, swap(): lax.ppermute(x, axes, [p for a, b in pairs for p in ((a, b), (b, a))])  59.4 us
    pallas_call x19, Pallas kernels, call(): pl.pallas_call(kernel, out_shape=out_shapes, in_specs=[pl.BlockSpec(memor...  35.7 us
    ppermute x24, starting transfers between devices, swap(): lax.ppermute(x, axes, [p for a, b in pairs for p in ((a, b), (b, a))])  23.5 us
    unnamed x16, local copies, waits for them, and re-layouts  5.54 us
  transfers between devices with their start and end apart: 24, of which 12 were waited for; matrix products, arithmetic and copies ran while one was open for 0% of the time, Pallas kernels for 24%

profile of v4, /device:TPU:0, one launch (start us, length us, event | category | flops | bytes accessed | tf_op | source)
XLA Modules:
  0.0 125.1 jit_solution(5118382499357939246)
XLA Ops:
  2.5 1.2 copy-done.4
  5.0 2.6 %collective-permute-start.3 = (bf16[256,1024]{1,0:T(8,128)(2,1)S(1)}, bf16[256,1024]{1,0:T(8,128)(2,1)S(1)}, u32[]{:S(2)}, u32[]{:S(2)}) collective-permute-start(bf16[256,1024]{1,0:T(8,128)(2,1)S(1)} %message.1.refs_0_), channel_id=1, source_target_pairs={{4,8},{8,4},{12,14},{14,12},{10,6},{6,10},{2,0},{0,2},{5,9},{9,5},... | collective-permute-start | bytes 1572872 | tf_op jit(solution)/shard_map/ppermute | solution.py:190
  7.6 1.7 %collective-permute-start = (bf16[256,1024]{1,0:T(8,128)(2,1)S(1)}, bf16[256,1024]{1,0:T(8,128)(2,1)S(1)}, u32[]{:S(2)}, u32[]{:S(2)}) collective-permute-start(bf16[256,1024]{1,0:T(8,128)(2,1)S(1)} %message.1.refs_0_), channel_id=1, source_target_pairs={{0,4},{4,0},{8,12},{12,8},{14,10},{10,14},{6,2},{2,6},{1,5},{5,1},... | collective-permute-start | bytes 1572872 | tf_op jit(solution)/shard_map/ppermute | solution.py:190
  9.3 10.9 %collective-permute-done.3.refs_1_.refs_4_ = bf16[256,1024]{1,0:T(8,128)(2,1)S(1)} collective-permute-done((bf16[256,1024]{1,0:T(8,128)(2,1)S(1)}, bf16[256,1024]{1,0:T(8,128)(2,1)S(1)}, u32[]{:S(2)}, u32[]{:S(2)}) %collective-permute-start.3) | collective-permute-done | bytes 524320 | tf_op jit(solution)/shard_map/ppermute | solution.py:190
  20.2 1.8 %collective-permute-start.4 = (bf16[256,1024]{1,0:T(8,128)(2,1)S(1)}, bf16[256,1024]{1,0:T(8,128)(2,1)S(1)}, u32[]{:S(2)}, u32[]{:S(2)}) collective-permute-start(bf16[256,1024]{1,0:T(8,128)(2,1)S(1)} %collective-permute-done.3.refs_1_.refs_4_), channel_id=1, source_target_pairs={{0,4},{4,0},{8,12},{12,8},{14,10},{10,14},{6,2},{2,6},{1,5},{5,1},... | collective-permute-start | bytes 1572872 | tf_op jit(solution)/shard_map/ppermute | solution.py:190
  22.0 1.5 %collective-permute-start.1 = (bf16[256,1024]{1,0:T(8,128)(2,1)S(1)}, bf16[256,1024]{1,0:T(8,128)(2,1)S(1)}, u32[]{:S(2)}, u32[]{:S(2)}) collective-permute-start(bf16[256,1024]{1,0:T(8,128)(2,1)S(1)} %collective-permute-done.refs_0_.refs_3_), channel_id=1, source_target_pairs={{4,8},{8,4},{12,14},{14,12},{10,6},{6,10},{2,0},{0,2},{5,9},{9,5},... | collective-permute-start | bytes 1572872 | tf_op jit(solution)/shard_map/ppermute | solution.py:190
  23.5 10.4 %collective-permute-done.4.refs_0_.refs_7_ = bf16[256,1024]{1,0:T(8,128)(2,1)S(1)} collective-permute-done((bf16[256,1024]{1,0:T(8,128)(2,1)S(1)}, bf16[256,1024]{1,0:T(8,128)(2,1)S(1)}, u32[]{:S(2)}, u32[]{:S(2)}) %collective-permute-start.4) | collective-permute-done | bytes 524320 | tf_op jit(solution)/shard_map/ppermute | solution.py:190
  33.9 1.5 %collective-permute-start.5 = (bf16[256,1024]{1,0:T(8,128)(2,1)S(1)}, bf16[256,1024]{1,0:T(8,128)(2,1)S(1)}, u32[]{:S(2)}, u32[]{:S(2)}) collective-permute-start(bf16[256,1024]{1,0:T(8,128)(2,1)S(1)} %collective-permute-done.4.refs_0_.refs_7_), channel_id=1, source_target_pairs={{4,8},{8,4},{12,14},{14,12},{10,6},{6,10},{2,0},{0,2},{5,9},{9,5},... | collective-permute-start | bytes 1572872 | tf_op jit(solution)/shard_map/ppermute | solution.py:190
  35.5 1.7 %collective-permute-start.2 = (bf16[256,1024]{1,0:T(8,128)(2,1)S(1)}, bf16[256,1024]{1,0:T(8,128)(2,1)S(1)}, u32[]{:S(2)}, u32[]{:S(2)}) collective-permute-start(bf16[256,1024]{1,0:T(8,128)(2,1)S(1)} %collective-permute-done.1.refs_1_.refs_8_), channel_id=1, source_target_pairs={{0,4},{4,0},{8,12},{12,8},{14,10},{10,14},{6,2},{2,6},{1,5},{5,1},... | collective-permute-start | bytes 1572872 | tf_op jit(solution)/shard_map/ppermute | solution.py:190
  37.2 2.2 %copy-done.1 = f32[1,512,2048]{2,1,0:T(8,128)S(1)} copy-done((f32[1,512,2048]{2,1,0:T(8,128)S(1)}, f32[1,512,2048]{2,1,0:T(8,128)}, u32[]{:S(2)}) %copy-start.1) | copy-done | bytes 4194328
  39.4 1.4 %split.1 = (bf16[512,2048]{1,0:T(8,128)(2,1)S(1)}, bf16[512,2048]{1,0:T(8,128)(2,1)S(1)}) custom-call(s32[3]{0:T(128)S(1)} %pad_add_fusion.place, f32[512,2048]{1,0:T(8,128)S(1)} %bitcast.9), custom_call_target="tpu_custom_call" | custom-call | tf_op jit(solution)/shard_map/split/pallas_call | solution.py:44
  41.0 4.3 %block.9.refs_9_.mine = bf16[256,1536]{1,0:T(8,128)(2,1)S(1)} custom-call(s32[3]{0:T(128)S(1)} %pad_add_fusion.place, bf16[256,1024]{1,0:T(8,128)(2,1)S(1)} %collective-permute-done.4.refs_0_.refs_7_, bf16[256,1024]{1,0:T(8,128)(2,1)S(1)} %collective-permute-done.1.refs_1_.refs_8_, bf16[1024,1024]{1,0:T(8,128)(2,1)S(1)} %copy-done, ...), custom_call_target="tpu_custom_call" | custom-call | tf_op jit(solution)/shard_map/block/pallas_call | solution.py:44
  45.9 4.3 %block.8.refs_5_.mine = bf16[256,1536]{1,0:T(8,128)(2,1)S(1)} custom-call(s32[3]{0:T(128)S(1)} %pad_add_fusion.place, bf16[256,1024]{1,0:T(8,128)(2,1)S(1)} %collective-permute-done.refs_0_.refs_3_, bf16[256,1024]{1,0:T(8,128)(2,1)S(1)} %collective-permute-done.3.refs_1_.refs_4_, bf16[1024,1024]{1,0:T(8,128)(2,1)S(1)} %copy-done, ...), custom_call_target="tpu_custom_call" | custom-call | tf_op jit(solution)/shard_map/block/pallas_call | solution.py:44
  50.3 4.3 %block.5.refs_2_.mine = bf16[256,1536]{1,0:T(8,128)(2,1)S(1)} custom-call(s32[3]{0:T(128)S(1)} %pad_add_fusion.place, bf16[256,1024]{1,0:T(8,128)(2,1)S(1)} %collective-permute-done.2.refs_0_, bf16[256,1024]{1,0:T(8,128)(2,1)S(1)} %collective-permute-done.5.refs_1_, bf16[1024,1024]{1,0:T(8,128)(2,1)S(1)} %copy-done, ...), custom_call_target="tpu_custom_call" | custom-call | tf_op jit(solution)/shard_map/block/pallas_call | solution.py:44
  55.2 3.5 %block.7.refs_1_.mine = bf16[128,1536]{1,0:T(8,128)(2,1)S(1)} custom-call(s32[3]{0:T(128)S(1)} %pad_add_fusion.place, bf16[256,1024]{1,0:T(8,128)(2,1)S(1)} %message.1.refs_0_, bf16[1024,1024]{1,0:T(8,128)(2,1)S(1)} %copy-done, bf16[1024,1024]{1,0:T(8,128)(2,1)S(1)} %collective-permute-done.6.refs_3_.refs_2_, ...), custom_call_target="tpu_custom_call" | custom-call | tf_op jit(solution)/shard_map/block/pallas_call | solution.py:44
  59.2 8.3 %collective-permute-done.10.refs_0_ = bf16[128,1024]{1,0:T(8,128)(2,1)S(1)} collective-permute-done((bf16[128,1024]{1,0:T(8,128)(2,1)S(1)}, bf16[128,1024]{1,0:T(8,128)(2,1)S(1)}, u32[]{:S(2)}, u32[]{:S(2)}) %collective-permute-start.10) | collective-permute-done | bytes 262176 | tf_op jit(solution)/shard_map/ppermute | solution.py:190
  67.5 3.3 %block.6.refs_5_.mine = bf16[128,1536]{1,0:T(8,128)(2,1)S(1)} custom-call(s32[3]{0:T(128)S(1)} %pad_add_fusion.place, bf16[128,1024]{1,0:T(8,128)(2,1)S(1)} %collective-permute-done.10.refs_0_, bf16[1024,1024]{1,0:T(8,128)(2,1)S(1)} %copy-done, bf16[1024,1024]{1,0:T(8,128)(2,1)S(1)} %collective-permute-done.6.refs_3_.refs_2_, ...), custom_call_target="tpu_custom_call" | custom-call | tf_op jit(solution)/shard_map/block/pallas_call | solution.py:44
  71.0 1.5 %collective-permute-start.9 = (bf16[128,1024]{1,0:T(8,128)(2,1)S(1)}, bf16[128,1024]{1,0:T(8,128)(2,1)S(1)}, u32[]{:S(2)}, u32[]{:S(2)}) collective-permute-start(bf16[128,1024]{1,0:T(8,128)(2,1)S(1)} %slice.8), channel_id=1, source_target_pairs={{4,8},{8,4},{12,14},{14,12},{10,6},{6,10},{2,0},{0,2},{5,9},{9,5},... | collective-permute-start | bytes 786440 | tf_op jit(solution)/shard_map/ppermute | solution.py:190
  72.5 2.1 %begin.1.refs_7_ = f32[512,512]{1,0:T(8,128)S(1)} custom-call(s32[3]{0:T(128)S(1)} %pad_add_fusion.place, bf16[256,1024]{1,0:T(8,128)(2,1)S(1)} %message.1.refs_0_, bf16[128,1536]{1,0:T(8,128)(2,1)S(1)} %block.7.refs_1_.mine, bf16[128,1536]{1,0:T(8,128)(2,1)S(1)} %collective-permute-done.12.refs_2_.theirs, ...), custom_call_target="tpu_custom_call" | custom-call | tf_op jit(solution)/shard_map/begin/pallas_call | solution.py:44
  74.6 5.2 %collective-permute-done.9.refs_4_ = bf16[128,1024]{1,0:T(8,128)(2,1)S(1)} collective-permute-done((bf16[128,1024]{1,0:T(8,128)(2,1)S(1)}, bf16[128,1024]{1,0:T(8,128)(2,1)S(1)}, u32[]{:S(2)}, u32[]{:S(2)}) %collective-permute-start.9) | collective-permute-done | bytes 262176 | tf_op jit(solution)/shard_map/ppermute | solution.py:190
  79.7 2.5 %update.1 = (f32[500,512]{1,0:T(8,128)}, bf16[512,512]{1,0:T(8,128)(2,1)S(1)}) custom-call(s32[3]{0:T(128)S(1)} %pad_add_fusion.place, bf16[256,1024]{1,0:T(8,128)(2,1)S(1)} %collective-permute-done.2.refs_0_, bf16[256,1024]{1,0:T(8,128)(2,1)S(1)} %collective-permute-done.5.refs_1_, bf16[256,1536]{1,0:T(8,128)(2,1)S(1)} %block.5.refs_2_.mine, ...), custom_call_target="tpu_custom_call" | custom-call | tf_op jit(solution)/shard_map/update/pallas_call | solution.py:44
  83.1 1.5 %collective-permute-start.19 = (bf16[512,128]{1,0:T(8,128)(2,1)S(1)}, bf16[512,128]{1,0:T(8,128)(2,1)S(1)}, u32[]{:S(2)}, u32[]{:S(2)}) collective-permute-start(bf16[512,128]{1,0:T(8,128)(2,1)S(1)} %far.3), channel_id=1, source_target_pairs={{4,8},{8,4},{12,14},{14,12},{10,6},{6,10},{2,0},{0,2},{5,9},{9,5},... | collective-permute-start | bytes 393224 | tf_op jit(solution)/shard_map/ppermute | solution.py:190
  85.4 1.6 %collective-permute-start.15 = (bf16[512,128]{1,0:T(8,128)(2,1)S(1)}, bf16[512,128]{1,0:T(8,128)(2,1)S(1)}, u32[]{:S(2)}, u32[]{:S(2)}) collective-permute-start(bf16[512,128]{1,0:T(8,128)(2,1)S(1)} %far.2), channel_id=1, source_target_pairs={{0,4},{4,0},{8,12},{12,8},{14,10},{10,14},{6,2},{2,6},{1,5},{5,1},... | collective-permute-start | bytes 393224 | tf_op jit(solution)/shard_map/ppermute | solution.py:190
  89.1 1.6 %collective-permute-start.20 = (bf16[512,256]{1,0:T(8,128)(2,1)S(1)}, bf16[512,256]{1,0:T(8,128)(2,1)S(1)}, u32[]{:S(2)}, u32[]{:S(2)}) collective-permute-start(bf16[512,256]{1,0:T(8,128)(2,1)S(1)} %third.3), channel_id=1, source_target_pairs={{0,4},{4,0},{8,12},{12,8},{14,10},{10,14},{6,2},{2,6},{1,5},{5,1},... | collective-permute-start | bytes 786440 | tf_op jit(solution)/shard_map/ppermute | solution.py:190
  92.1 4.1 %collective-permute-done.20.came = bf16[512,256]{1,0:T(8,128)(2,1)S(1)} collective-permute-done((bf16[512,256]{1,0:T(8,128)(2,1)S(1)}, bf16[512,256]{1,0:T(8,128)(2,1)S(1)}, u32[]{:S(2)}, u32[]{:S(2)}) %collective-permute-start.20) | collective-permute-done | bytes 262176 | tf_op jit(solution)/shard_map/ppermute | solution.py:190
  97.1 1.5 %collective-permute-start.21 = (bf16[512,256]{1,0:T(8,128)(2,1)S(1)}, bf16[512,256]{1,0:T(8,128)(2,1)S(1)}, u32[]{:S(2)}, u32[]{:S(2)}) collective-permute-start(bf16[512,256]{1,0:T(8,128)(2,1)S(1)} %second.3), channel_id=1, source_target_pairs={{4,8},{8,4},{12,14},{14,12},{10,6},{6,10},{2,0},{0,2},{5,9},{9,5},... | collective-permute-start | bytes 786440 | tf_op jit(solution)/shard_map/ppermute | solution.py:190
  101.2 3.1 %collective-permute-done.21.came = bf16[512,256]{1,0:T(8,128)(2,1)S(1)} collective-permute-done((bf16[512,256]{1,0:T(8,128)(2,1)S(1)}, bf16[512,256]{1,0:T(8,128)(2,1)S(1)}, u32[]{:S(2)}, u32[]{:S(2)}) %collective-permute-start.21) | collective-permute-done | bytes 262176 | tf_op jit(solution)/shard_map/ppermute | solution.py:190
  106.2 1.6 %collective-permute-done.17.came = bf16[512,256]{1,0:T(8,128)(2,1)S(1)} collective-permute-done((bf16[512,256]{1,0:T(8,128)(2,1)S(1)}, bf16[512,256]{1,0:T(8,128)(2,1)S(1)}, u32[]{:S(2)}, u32[]{:S(2)}) %collective-permute-start.17) | collective-permute-done | bytes 262176 | tf_op jit(solution)/shard_map/ppermute | solution.py:190
  108.8 3.7 %collective-permute-done.22.in_b = bf16[512,256]{1,0:T(8,128)(2,1)S(1)} collective-permute-done((bf16[512,256]{1,0:T(8,128)(2,1)S(1)}, bf16[512,256]{1,0:T(8,128)(2,1)S(1)}, u32[]{:S(2)}, u32[]{:S(2)}) %collective-permute-start.22) | collective-permute-done | bytes 262176 | tf_op jit(solution)/shard_map/ppermute | solution.py:190
  112.4 3.7 %collective-permute-done.18.in_a = bf16[512,256]{1,0:T(8,128)(2,1)S(1)} collective-permute-done((bf16[512,256]{1,0:T(8,128)(2,1)S(1)}, bf16[512,256]{1,0:T(8,128)(2,1)S(1)}, u32[]{:S(2)}, u32[]{:S(2)}) %collective-permute-start.18) | collective-permute-done | bytes 262176 | tf_op jit(solution)/shard_map/ppermute | solution.py:190
  117.1 6.4 %collective-permute-done.23.other = bf16[512,256]{1,0:T(8,128)(2,1)S(1)} collective-permute-done((bf16[512,256]{1,0:T(8,128)(2,1)S(1)}, bf16[512,256]{1,0:T(8,128)(2,1)S(1)}, u32[]{:S(2)}, u32[]{:S(2)}) %collective-permute-start.23) | collective-permute-done | bytes 262176 | tf_op jit(solution)/shard_map/ppermute | solution.py:190
  123.5 1.7 %apply.1 = f32[500,512]{1,0:T(8,128)} custom-call(s32[3]{0:T(128)S(1)} %pad_add_fusion.place, f32[500,512]{1,0:T(8,128)S(1)} %bitcast.11, bf16[512,256]{1,0:T(8,128)(2,1)S(1)} %last.1.own, bf16[512,256]{1,0:T(8,128)(2,1)S(1)} %collective-permute-done.23.other), custom_call_target="tpu_custom_call" | custom-call | tf_op jit(solution)/shard_map/apply/pallas_call | solution.py:44
  (55 shorter events, 17.6 us)
Async XLA Ops:
  0.6 36.5 %copy-start.7 = (bf16[1024]{0:T(1024)(128)(2,1)S(1)}, bf16[1024]{0:T(1024)(128)(2,1)}, u32[]{:S(2)}) copy-start(bf16[1024]{0:T(1024)(128)(2,1)} %param.9) | copy-start | bytes 6148
  0.6 40.1 %collective-permute-start.6 = (bf16[1024,1024]{1,0:T(8,128)(2,1)}, bf16[1024,1024]{1,0:T(8,128)(2,1)S(1)}, u32[]{:S(2)}, u32[]{:S(2)}) collective-permute-start(bf16[1024,1024]{1,0:T(8,128)(2,1)} %refs_2_.5), channel_id=1, source_target_pairs={{0,1},{1,0},{2,3},{3,2},{4,5},{5,4},{6,7},{7,6},{8,9},{9,8},{10,11... | collective-permute-start | bytes 6291464 | tf_op jit(solution)/shard_map/ppermute | solution.py:190
  1.2 1.2 copy-start.2
  2.5 1.2 copy-start.4
  3.7 0.7 copy-start.6
  5.0 15.1 %collective-permute-start.3 = (bf16[256,1024]{1,0:T(8,128)(2,1)S(1)}, bf16[256,1024]{1,0:T(8,128)(2,1)S(1)}, u32[]{:S(2)}, u32[]{:S(2)}) collective-permute-start(bf16[256,1024]{1,0:T(8,128)(2,1)S(1)} %message.1.refs_0_), channel_id=1, source_target_pairs={{4,8},{8,4},{12,14},{14,12},{10,6},{6,10},{2,0},{0,2},{5,9},{9,5},... | collective-permute-start | bytes 1572872 | tf_op jit(solution)/shard_map/ppermute | solution.py:190
  7.6 14.4 %collective-permute-start = (bf16[256,1024]{1,0:T(8,128)(2,1)S(1)}, bf16[256,1024]{1,0:T(8,128)(2,1)S(1)}, u32[]{:S(2)}, u32[]{:S(2)}) collective-permute-start(bf16[256,1024]{1,0:T(8,128)(2,1)S(1)} %message.1.refs_0_), channel_id=1, source_target_pairs={{0,4},{4,0},{8,12},{12,8},{14,10},{10,14},{6,2},{2,6},{1,5},{5,1},... | collective-permute-start | bytes 1572872 | tf_op jit(solution)/shard_map/ppermute | solution.py:190
  20.2 13.7 %collective-permute-start.4 = (bf16[256,1024]{1,0:T(8,128)(2,1)S(1)}, bf16[256,1024]{1,0:T(8,128)(2,1)S(1)}, u32[]{:S(2)}, u32[]{:S(2)}) collective-permute-start(bf16[256,1024]{1,0:T(8,128)(2,1)S(1)} %collective-permute-done.3.refs_1_.refs_4_), channel_id=1, source_target_pairs={{0,4},{4,0},{8,12},{12,8},{14,10},{10,14},{6,2},{2,6},{1,5},{5,1},... | collective-permute-start | bytes 1572872 | tf_op jit(solution)/shard_map/ppermute | solution.py:190
  22.0 13.4 %collective-permute-start.1 = (bf16[256,1024]{1,0:T(8,128)(2,1)S(1)}, bf16[256,1024]{1,0:T(8,128)(2,1)S(1)}, u32[]{:S(2)}, u32[]{:S(2)}) collective-permute-start(bf16[256,1024]{1,0:T(8,128)(2,1)S(1)} %collective-permute-done.refs_0_.refs_3_), channel_id=1, source_target_pairs={{4,8},{8,4},{12,14},{14,12},{10,6},{6,10},{2,0},{0,2},{5,9},{9,5},... | collective-permute-start | bytes 1572872 | tf_op jit(solution)/shard_map/ppermute | solution.py:190
  33.9 16.4 %collective-permute-start.5 = (bf16[256,1024]{1,0:T(8,128)(2,1)S(1)}, bf16[256,1024]{1,0:T(8,128)(2,1)S(1)}, u32[]{:S(2)}, u32[]{:S(2)}) collective-permute-start(bf16[256,1024]{1,0:T(8,128)(2,1)S(1)} %collective-permute-done.4.refs_0_.refs_7_), channel_id=1, source_target_pairs={{4,8},{8,4},{12,14},{14,12},{10,6},{6,10},{2,0},{0,2},{5,9},{9,5},... | collective-permute-start | bytes 1572872 | tf_op jit(solution)/shard_map/ppermute | solution.py:190
  35.5 14.9 %collective-permute-start.2 = (bf16[256,1024]{1,0:T(8,128)(2,1)S(1)}, bf16[256,1024]{1,0:T(8,128)(2,1)S(1)}, u32[]{:S(2)}, u32[]{:S(2)}) collective-permute-start(bf16[256,1024]{1,0:T(8,128)(2,1)S(1)} %collective-permute-done.1.refs_1_.refs_8_), channel_id=1, source_target_pairs={{0,4},{4,0},{8,12},{12,8},{14,10},{10,14},{6,2},{2,6},{1,5},{5,1},... | collective-permute-start | bytes 1572872 | tf_op jit(solution)/shard_map/ppermute | solution.py:190
  37.1 3.6 %collective-permute-start.7 = (bf16[1,1024]{1,0:T(2,128)(2,1)S(1)}, bf16[1,1024]{1,0:T(2,128)(2,1)S(1)}, u32[]{:S(2)}, u32[]{:S(2)}) collective-permute-start(bf16[1,1024]{1,0:T(2,128)(2,1)S(1)} %broadcast_in_dim.7.refs_4_.refs_3_), channel_id=1, source_target_pairs={{0,1},{1,0},{2,3},{3,2},{4,5},{5,4},{6,7},{7,6},{8,9},{9,8},{10,11... | collective-permute-start | bytes 6152 | tf_op jit(solution)/shard_map/ppermute | solution.py:190
  37.2 2.2 %copy-start.1 = (f32[1,512,2048]{2,1,0:T(8,128)S(1)}, f32[1,512,2048]{2,1,0:T(8,128)}, u32[]{:S(2)}) copy-start(f32[1,512,2048]{2,1,0:T(8,128)} %param.10) | copy-start | bytes 12582916
  39.4 1.6 %copy-start = (bf16[1024,1024]{1,0:T(8,128)(2,1)S(1)}, bf16[1024,1024]{1,0:T(8,128)(2,1)}, u32[]{:S(2)}) copy-start(bf16[1024,1024]{1,0:T(8,128)(2,1)} %refs_2_.5) | copy-start | bytes 6291460
  45.3 27.2 %collective-permute-start.14 = (bf16[256,1536]{1,0:T(8,128)(2,1)S(1)}, bf16[256,1536]{1,0:T(8,128)(2,1)S(1)}, u32[]{:S(2)}, u32[]{:S(2)}) collective-permute-start(bf16[256,1536]{1,0:T(8,128)(2,1)S(1)} %block.9.refs_9_.mine), channel_id=1, source_target_pairs={{0,1},{1,0},{2,3},{3,2},{4,5},{5,4},{6,7},{7,6},{8,9},{9,8},{10,11... | collective-permute-start | bytes 2359304 | tf_op jit(solution)/shard_map/ppermute | solution.py:190
  50.2 22.3 %collective-permute-start.13 = (bf16[256,1536]{1,0:T(8,128)(2,1)S(1)}, bf16[256,1536]{1,0:T(8,128)(2,1)S(1)}, u32[]{:S(2)}, u32[]{:S(2)}) collective-permute-start(bf16[256,1536]{1,0:T(8,128)(2,1)S(1)} %block.8.refs_5_.mine), channel_id=1, source_target_pairs={{0,1},{1,0},{2,3},{3,2},{4,5},{5,4},{6,7},{7,6},{8,9},{9,8},{10,11... | collective-permute-start | bytes 2359304 | tf_op jit(solution)/shard_map/ppermute | solution.py:190
  54.7 25.1 %collective-permute-start.8 = (bf16[256,1536]{1,0:T(8,128)(2,1)S(1)}, bf16[256,1536]{1,0:T(8,128)(2,1)S(1)}, u32[]{:S(2)}, u32[]{:S(2)}) collective-permute-start(bf16[256,1536]{1,0:T(8,128)(2,1)S(1)} %block.5.refs_2_.mine), channel_id=1, source_target_pairs={{0,1},{1,0},{2,3},{3,2},{4,5},{5,4},{6,7},{7,6},{8,9},{9,8},{10,11... | collective-permute-start | bytes 2359304 | tf_op jit(solution)/shard_map/ppermute | solution.py:190
  58.7 12.2 %collective-permute-start.12 = (bf16[128,1536]{1,0:T(8,128)(2,1)S(1)}, bf16[128,1536]{1,0:T(8,128)(2,1)S(1)}, u32[]{:S(2)}, u32[]{:S(2)}) collective-permute-start(bf16[128,1536]{1,0:T(8,128)(2,1)S(1)} %block.7.refs_1_.mine), channel_id=1, source_target_pairs={{0,1},{1,0},{2,3},{3,2},{4,5},{5,4},{6,7},{7,6},{8,9},{9,8},{10,11... | collective-permute-start | bytes 1179656 | tf_op jit(solution)/shard_map/ppermute | solution.py:190
  58.8 8.7 %collective-permute-start.10 = (bf16[128,1024]{1,0:T(8,128)(2,1)S(1)}, bf16[128,1024]{1,0:T(8,128)(2,1)S(1)}, u32[]{:S(2)}, u32[]{:S(2)}) collective-permute-start(bf16[128,1024]{1,0:T(8,128)(2,1)S(1)} %slice.9), channel_id=1, source_target_pairs={{0,4},{4,0},{8,12},{12,8},{14,10},{10,14},{6,2},{2,6},{1,5},{5,1},... | collective-permute-start | bytes 786440 | tf_op jit(solution)/shard_map/ppermute | solution.py:190
  70.8 8.9 %collective-permute-start.11 = (bf16[128,1536]{1,0:T(8,128)(2,1)S(1)}, bf16[128,1536]{1,0:T(8,128)(2,1)S(1)}, u32[]{:S(2)}, u32[]{:S(2)}) collective-permute-start(bf16[128,1536]{1,0:T(8,128)(2,1)S(1)} %block.6.refs_5_.mine), channel_id=1, source_target_pairs={{0,1},{1,0},{2,3},{3,2},{4,5},{5,4},{6,7},{7,6},{8,9},{9,8},{10,11... | collective-permute-start | bytes 1179656 | tf_op jit(solution)/shard_map/ppermute | solution.py:190
  70.9 8.8 %copy-start.5 = (f32[512,500]{0,1:T(8,128)S(1)}, f32[512,500]{0,1:T(8,128)}, u32[]{:S(2)}) copy-start(f32[512,500]{0,1:T(8,128)} %param.13) | copy-start | bytes 3072004
  71.0 8.8 %collective-permute-start.9 = (bf16[128,1024]{1,0:T(8,128)(2,1)S(1)}, bf16[128,1024]{1,0:T(8,128)(2,1)S(1)}, u32[]{:S(2)}, u32[]{:S(2)}) collective-permute-start(bf16[128,1024]{1,0:T(8,128)(2,1)S(1)} %slice.8), channel_id=1, source_target_pairs={{4,8},{8,4},{12,14},{14,12},{10,6},{6,10},{2,0},{0,2},{5,9},{9,5},... | collective-permute-start | bytes 786440 | tf_op jit(solution)/shard_map/ppermute | solution.py:190
  83.1 5.2 %collective-permute-start.19 = (bf16[512,128]{1,0:T(8,128)(2,1)S(1)}, bf16[512,128]{1,0:T(8,128)(2,1)S(1)}, u32[]{:S(2)}, u32[]{:S(2)}) collective-permute-start(bf16[512,128]{1,0:T(8,128)(2,1)S(1)} %far.3), channel_id=1, source_target_pairs={{4,8},{8,4},{12,14},{14,12},{10,6},{6,10},{2,0},{0,2},{5,9},{9,5},... | collective-permute-start | bytes 393224 | tf_op jit(solution)/shard_map/ppermute | solution.py:190
  85.4 5.3 %collective-permute-start.15 = (bf16[512,128]{1,0:T(8,128)(2,1)S(1)}, bf16[512,128]{1,0:T(8,128)(2,1)S(1)}, u32[]{:S(2)}, u32[]{:S(2)}) collective-permute-start(bf16[512,128]{1,0:T(8,128)(2,1)S(1)} %far.2), channel_id=1, source_target_pairs={{0,4},{4,0},{8,12},{12,8},{14,10},{10,14},{6,2},{2,6},{1,5},{5,1},... | collective-permute-start | bytes 393224 | tf_op jit(solution)/shard_map/ppermute | solution.py:190
  89.1 7.1 %collective-permute-start.20 = (bf16[512,256]{1,0:T(8,128)(2,1)S(1)}, bf16[512,256]{1,0:T(8,128)(2,1)S(1)}, u32[]{:S(2)}, u32[]{:S(2)}) collective-permute-start(bf16[512,256]{1,0:T(8,128)(2,1)S(1)} %third.3), channel_id=1, source_target_pairs={{0,4},{4,0},{8,12},{12,8},{14,10},{10,14},{6,2},{2,6},{1,5},{5,1},... | collective-permute-start | bytes 786440 | tf_op jit(solution)/shard_map/ppermute | solution.py:190
  91.6 7.9 %collective-permute-start.16 = (bf16[512,256]{1,0:T(8,128)(2,1)S(1)}, bf16[512,256]{1,0:T(8,128)(2,1)S(1)}, u32[]{:S(2)}, u32[]{:S(2)}) collective-permute-start(bf16[512,256]{1,0:T(8,128)(2,1)S(1)} %third.2), channel_id=1, source_target_pairs={{4,8},{8,4},{12,14},{14,12},{10,6},{6,10},{2,0},{0,2},{5,9},{9,5},... | collective-permute-start | bytes 786440 | tf_op jit(solution)/shard_map/ppermute | solution.py:190
  97.1 7.2 %collective-permute-start.21 = (bf16[512,256]{1,0:T(8,128)(2,1)S(1)}, bf16[512,256]{1,0:T(8,128)(2,1)S(1)}, u32[]{:S(2)}, u32[]{:S(2)}) collective-permute-start(bf16[512,256]{1,0:T(8,128)(2,1)S(1)} %second.3), channel_id=1, source_target_pairs={{4,8},{8,4},{12,14},{14,12},{10,6},{6,10},{2,0},{0,2},{5,9},{9,5},... | collective-permute-start | bytes 786440 | tf_op jit(solution)/shard_map/ppermute | solution.py:190
  100.4 7.5 %collective-permute-start.17 = (bf16[512,256]{1,0:T(8,128)(2,1)S(1)}, bf16[512,256]{1,0:T(8,128)(2,1)S(1)}, u32[]{:S(2)}, u32[]{:S(2)}) collective-permute-start(bf16[512,256]{1,0:T(8,128)(2,1)S(1)} %second.2), channel_id=1, source_target_pairs={{0,4},{4,0},{8,12},{12,8},{14,10},{10,14},{6,2},{2,6},{1,5},{5,1},... | collective-permute-start | bytes 786440 | tf_op jit(solution)/shard_map/ppermute | solution.py:190
  105.1 18.3 %copy-start.3 = (f32[512,500]{0,1:T(8,128)S(1)}, f32[512,500]{0,1:T(8,128)}, u32[]{:S(2)}) copy-start(f32[512,500]{0,1:T(8,128)} %param.12) | copy-start | bytes 3072004
  105.1 7.3 %collective-permute-start.22 = (bf16[512,256]{1,0:T(8,128)(2,1)S(1)}, bf16[512,256]{1,0:T(8,128)(2,1)S(1)}, u32[]{:S(2)}, u32[]{:S(2)}) collective-permute-start(bf16[512,256]{1,0:T(8,128)(2,1)S(1)} %first.3), channel_id=1, source_target_pairs={{0,4},{4,0},{8,12},{12,8},{14,10},{10,14},{6,2},{2,6},{1,5},{5,1},... | collective-permute-start | bytes 786440 | tf_op jit(solution)/shard_map/ppermute | solution.py:190
  108.7 7.4 %collective-permute-start.18 = (bf16[512,256]{1,0:T(8,128)(2,1)S(1)}, bf16[512,256]{1,0:T(8,128)(2,1)S(1)}, u32[]{:S(2)}, u32[]{:S(2)}) collective-permute-start(bf16[512,256]{1,0:T(8,128)(2,1)S(1)} %first.2), channel_id=1, source_target_pairs={{4,8},{8,4},{12,14},{14,12},{10,6},{6,10},{2,0},{0,2},{5,9},{9,5},... | collective-permute-start | bytes 786440 | tf_op jit(solution)/shard_map/ppermute | solution.py:190
  117.0 6.4 %collective-permute-start.23 = (bf16[512,256]{1,0:T(8,128)(2,1)S(1)}, bf16[512,256]{1,0:T(8,128)(2,1)S(1)}, u32[]{:S(2)}, u32[]{:S(2)}) collective-permute-start(bf16[512,256]{1,0:T(8,128)(2,1)S(1)} %last.1.own), channel_id=1, source_target_pairs={{0,2},{2,0},{1,3},{3,1},{4,6},{6,4},{5,7},{7,5},{8,10},{10,8},{9,1... | collective-permute-start | bytes 786440 | tf_op jit(solution)/shard_map/ppermute | solution.py:190

commit v5 on v4

--- a/solution.py
+++ b/solution.py
@@ -38,7 +38,7 @@
     return lax.dot_general(a, b, (((1,), (1,)), ((), ())), preferred_element_type=F32)
 
 
-def call(kernel, out_shapes, place, args, name, vmem_mib, scratch=()):
+def call(kernel, out_shapes, place, args, name, vmem_mib, mflops, scratch=()):
     vmem = pl.BlockSpec(memory_space=pltpu.VMEM)
     single = isinstance(out_shapes, jax.ShapeDtypeStruct)
     return pl.pallas_call(
@@ -47,6 +47,9 @@
         in_specs=[pl.BlockSpec(memory_space=pltpu.SMEM)] + [vmem] * len(args),
         out_specs=vmem if single else (vmem,) * len(out_shapes),
         scratch_shapes=scratch,
+        cost_estimate=pl.CostEstimate(
+            flops=mflops * 10**6, transcendentals=0, bytes_accessed=sum(a.size * a.dtype.itemsize for a in args)
+        ),
         compiler_params=pltpu.CompilerParams(vmem_limit_bytes=vmem_mib << 20),
         name=name,
     )(place, *args)
@@ -136,9 +139,10 @@
     return [a for pieces, mine, theirs in groups for a in (*pieces, mine, theirs)]
 
 
-def begin_kernel(counts, place, *refs):
+def begin_kernel(counts, earlier, place, *refs):
     *pieces, out = refs
-    out[...] = product_of(counts, pieces, out.shape[1])
+    total = product_of(counts, pieces[earlier:], out.shape[1])
+    out[...] = pieces[0][...] + total if earlier else total
 
 
 def update_kernel(counts, place, *refs):
@@ -188,6 +192,10 @@
 
 def swap(x, axes, pairs):
     return lax.ppermute(x, axes, [p for a, b in pairs for p in ((a, b), (b, a))])
+
+
+def after(arrays, *others):
+    return lax.optimization_barrier((*arrays, *others))[:len(arrays)]
 
 
 def ring_shards(n_rows, inputs, projection, phases, inverse_blocks, labels, predictions, coefficients):
@@ -213,48 +221,65 @@
 
     sent0 = call(
         message_kernel, like((part + LANES, inputs.shape[1])), place,
-        (inputs, labels[None, :], predictions), "message", 8,
-    )
-    e1, o1 = E(sent0), O(sent0)
-    e2, o2 = E(o1), O(e1)
-    e3, o3 = E(o2), O(e2)
-    e4, o4 = E(o3[:part]), O(e3[part:])
+        (inputs, labels[None, :], predictions), "message", 8, 300,
+    )
     inverse = call(
-        split_kernel, (like(inverse_blocks.shape[1:]),) * 2, place, (inverse_blocks[0],), "split", 14
+        split_kernel, (like(inverse_blocks.shape[1:]),) * 2, place, (inverse_blocks[0],), "split", 14, 500
     )
 
     def block(*rows):
         out = like((len(rows) * part, 3 * depth))
         scratch = (pltpu.VMEM((len(rows) * part, 2 * projection.shape[1]), BF16),)
         args = (*rows, *weights, *phases, *inverse)
-        mine = call(functools.partial(block_kernel, len(rows)), out, place, args, "block", 16, scratch)
+        mine = call(
+            functools.partial(block_kernel, len(rows)), out, place, args, "block", 16, 2000 * len(rows), scratch
+        )
         return mine, C(mine)
 
-    b0, b1, b2, b3, b4 = block(sent0), block(e1, o1), block(e2, o2), block(e3, o3), block(e4)
-    begun = call(
-        functools.partial(begin_kernel, (1, 2, 2)), like((padded, depth), F32), place,
-        flat([((sent0,), *b0), ((e1, o1), *b1), ((e2, o2), *b2)]), "begin", 14,
-    )
+    def begin(groups, *earlier):
+        counts = tuple(len(g[0]) for g in groups)
+        return call(
+            functools.partial(begin_kernel, counts, len(earlier)), like((padded, depth), F32), place,
+            (*earlier, *flat(groups)), "begin", 14, 1400,
+        )
+
+    e1, o1 = E(sent0), O(sent0)
+    b0 = block(sent0)
+    e1, o1 = after((e1, o1), b0[0])
+    e2, o2 = E(o1), O(e1)
+    b1 = block(e1, o1)
+    e2, o2 = after((e2, o2), b1[0])
+    e3, o3 = E(o2), O(e2)
+    b2 = block(e2, o2)
+    begun = begin([((sent0,), *b0), ((e1, o1), *b1)])
+    e3, o3 = after((e3, o3), b2[0], begun)
+    rows4, residual4 = o3[:part], e3[part:]
+    e4, o4 = E(rows4), O(residual4)
+    e3, o3 = after((e3, o3), rows4, residual4)
+    b3 = block(e3, o3)
+    begun = begin([((e2, o2), *b2), ((e3, o3), *b3)], begun)
+    e4, o4 = after((e4, o4), begun)
+    b4 = block(e4)
     new_coefficients, sent = call(
-        functools.partial(update_kernel, (2, 1)),
+        functools.partial(update_kernel, (1,)),
         (like(coefficients.shape, F32), like((padded, depth))), place,
-        (*flat([((e3, o3), *b3), ((o4,), *b4)]), begun, coefficients), "update", 14,
+        (*flat([((o4,), *b4)]), begun, coefficients), "update", 14, 800,
     )
 
     piece, whole = like((padded, part)), like((padded, 2 * part))
 
     def hop(kernel, which, k, came, name):
-        return call(functools.partial(kernel, which), whole, place, (sent, *k, came), name, 6)
-
-    far_a = call(far_kernel, piece, place, (sent, b4[0]), "far", 6)
-    far_b = call(far_kernel, piece, place, (sent, b4[1]), "far", 6)
+        return call(functools.partial(kernel, which), whole, place, (sent, *k, came), name, 6, 150)
+
+    far_a = call(far_kernel, piece, place, (sent, b4[0]), "far", 6, 70)
+    far_b = call(far_kernel, piece, place, (sent, b4[1]), "far", 6, 70)
     way_a, way_b = E(far_a), O(far_b)
     way_a, way_b = O(hop(third_kernel, 1, b3, way_a, "third")), E(hop(third_kernel, 0, b3, way_b, "third"))
     way_a, way_b = E(hop(middle_kernel, 0, b2, way_a, "second")), O(hop(middle_kernel, 1, b2, way_b, "second"))
     way_a, way_b = O(hop(middle_kernel, 1, b1, way_a, "first")), E(hop(middle_kernel, 0, b1, way_b, "first"))
-    own = call(last_kernel, whole, place, (sent, *b0, way_a, way_b), "last", 6)
+    own = call(last_kernel, whole, place, (sent, *b0, way_a, way_b), "last", 6, 150)
     other = swap(own, "blocks", [(0, 1)])
-    new = call(apply_kernel, like(predictions.shape, F32), place, (predictions, own, other), "apply", 6)
+    new = call(apply_kernel, like(predictions.shape, F32), place, (predictions, own, other), "apply", 6, 100)
     return new_coefficients.T, new.T
 
 

time: 125 us -> 113 us (0.904)
  waiting for transfers between devices: 59.4 us -> 48.5 us
  starting transfers between devices: 23.5 us -> 21 us
    ppermute x24, waiting for transfers between devices: 59.4 us -> 48.5 us  [swap(): lax.ppermute(x, axes, [p for a, b in pairs for p in ((a, b), (b, a))])]
    ppermute x24, starting transfers between devices: 23.5 us -> 21 us  [swap(): lax.ppermute(x, axes, [p for a, b in pairs for p in ((a, b), (b, a))])]
    pallas_call x19 -> x20, Pallas kernels: 35.7 us -> 36.4 us  [call(): pl.pallas_call(kernel, out_shape=out_shapes, in_specs=[pl.BlockSpec(memor...]
  transfers between devices with their start and end apart: 24 -> 24, of which waited for: 12 -> 17; matrix products, arithmetic and copies ran while one was open for 0% -> 0% of each run, Pallas kernels for 24% -> 25%
where the time goes in v5:
time: 113 us; the launch traced here: 112 us
  waiting for transfers between devices  48.5 us (43%)
  Pallas kernels  36.4 us (32%)
  starting transfers between devices  21 us (19%)
  local copies, waits for them, and re-layouts  5.58 us (5%)
    ppermute x24, waiting for transfers between devices, swap(): lax.ppermute(x, axes, [p for a, b in pairs for p in ((a, b), (b, a))])  48.5 us
    pallas_call x20, Pallas kernels, call(): pl.pallas_call(kernel, out_shape=out_shapes, in_specs=[pl.BlockSpec(memor...  36.4 us
    ppermute x24, starting transfers between devices, swap(): lax.ppermute(x, axes, [p for a, b in pairs for p in ((a, b), (b, a))])  21 us
    unnamed x16, local copies, waits for them, and re-layouts  5.54 us
  transfers between devices with their start and end apart: 24, of which 17 were waited for; matrix products, arithmetic and copies ran while one was open for 0% of the time, Pallas kernels for 25%

profile of v5, /device:TPU:0, one launch (start us, length us, event | category | flops | bytes accessed | tf_op | source)
XLA Modules:
  0.0 112.5 jit_solution(15417534816277372813)
XLA Ops:
  5.0 2.6 %collective-permute-start.1 = (bf16[256,1024]{1,0:T(8,128)(2,1)S(1)}, bf16[256,1024]{1,0:T(8,128)(2,1)S(1)}, u32[]{:S(2)}, u32[]{:S(2)}) collective-permute-start(bf16[256,1024]{1,0:T(8,128)(2,1)S(1)} %message.1.refs_0_), channel_id=1, source_target_pairs={{4,8},{8,4},{12,14},{14,12},{10,6},{6,10},{2,0},{0,2},{5,9},{9,5},... | collective-permute-start | bytes 1572872 | tf_op jit(solution)/shard_map/ppermute | solution.py:194
  7.6 1.7 %collective-permute-start = (bf16[256,1024]{1,0:T(8,128)(2,1)S(1)}, bf16[256,1024]{1,0:T(8,128)(2,1)S(1)}, u32[]{:S(2)}, u32[]{:S(2)}) collective-permute-start(bf16[256,1024]{1,0:T(8,128)(2,1)S(1)} %message.1.refs_0_), channel_id=1, source_target_pairs={{0,4},{4,0},{8,12},{12,8},{14,10},{10,14},{6,2},{2,6},{1,5},{5,1},... | collective-permute-start | bytes 1572872 | tf_op jit(solution)/shard_map/ppermute | solution.py:194
  9.4 2.2 %copy-done.1 = f32[1,512,2048]{2,1,0:T(8,128)S(1)} copy-done((f32[1,512,2048]{2,1,0:T(8,128)S(1)}, f32[1,512,2048]{2,1,0:T(8,128)}, u32[]{:S(2)}) %copy-start.1) | copy-done | bytes 4194328
  11.5 1.4 %split.1 = (bf16[512,2048]{1,0:T(8,128)(2,1)S(1)}, bf16[512,2048]{1,0:T(8,128)(2,1)S(1)}) custom-call(s32[3]{0:T(128)S(1)} %pad_add_fusion.place, f32[512,2048]{1,0:T(8,128)S(1)} %bitcast.9), custom_call_target="tpu_custom_call" | custom-call | flops 500000000 | bytes 4194304 | tf_op jit(solution)/shard_map/split/pallas_call | solution.py:44
  13.1 3.3 %block.5.refs_1_.mine = bf16[128,1536]{1,0:T(8,128)(2,1)S(1)} custom-call(s32[3]{0:T(128)S(1)} %pad_add_fusion.place, bf16[256,1024]{1,0:T(8,128)(2,1)S(1)} %message.1.refs_0_, bf16[1024,1024]{1,0:T(8,128)(2,1)S(1)} %copy-done, bf16[1024,1024]{1,0:T(8,128)(2,1)S(1)} %collective-permute-done.2.refs_2_.refs_3_, ...), custom_call_target="tpu_custom_call" | custom-call | flops 2000000000 | bytes 8916992 | tf_op jit(solution)/shard_map/block/pallas_call | solution.py:44
  16.4 3.7 %collective-permute-done.1.refs_1_.refs_4_ = bf16[256,1024]{1,0:T(8,128)(2,1)S(1)} collective-permute-done((bf16[256,1024]{1,0:T(8,128)(2,1)S(1)}, bf16[256,1024]{1,0:T(8,128)(2,1)S(1)}, u32[]{:S(2)}, u32[]{:S(2)}) %collective-permute-start.1) | collective-permute-done | bytes 524320 | tf_op jit(solution)/shard_map/ppermute | solution.py:194
  20.2 1.5 %collective-permute-done.refs_0_.refs_3_ = bf16[256,1024]{1,0:T(8,128)(2,1)S(1)} collective-permute-done((bf16[256,1024]{1,0:T(8,128)(2,1)S(1)}, bf16[256,1024]{1,0:T(8,128)(2,1)S(1)}, u32[]{:S(2)}, u32[]{:S(2)}) %collective-permute-start) | collective-permute-done | bytes 524320 | tf_op jit(solution)/shard_map/ppermute | solution.py:194
  21.6 1.7 %collective-permute-start.4 = (bf16[256,1024]{1,0:T(8,128)(2,1)S(1)}, bf16[256,1024]{1,0:T(8,128)(2,1)S(1)}, u32[]{:S(2)}, u32[]{:S(2)}) collective-permute-start(bf16[256,1024]{1,0:T(8,128)(2,1)S(1)} %collective-permute-done.1.refs_1_.refs_4_), channel_id=1, source_target_pairs={{0,4},{4,0},{8,12},{12,8},{14,10},{10,14},{6,2},{2,6},{1,5},{5,1},... | collective-permute-start | bytes 1572872 | tf_op jit(solution)/shard_map/ppermute | solution.py:194
  23.3 1.5 %collective-permute-start.5 = (bf16[256,1024]{1,0:T(8,128)(2,1)S(1)}, bf16[256,1024]{1,0:T(8,128)(2,1)S(1)}, u32[]{:S(2)}, u32[]{:S(2)}) collective-permute-start(bf16[256,1024]{1,0:T(8,128)(2,1)S(1)} %collective-permute-done.refs_0_.refs_3_), channel_id=1, source_target_pairs={{4,8},{8,4},{12,14},{14,12},{10,6},{6,10},{2,0},{0,2},{5,9},{9,5},... | collective-permute-start | bytes 1572872 | tf_op jit(solution)/shard_map/ppermute | solution.py:194
  24.8 4.3 %block.6.refs_5_.mine = bf16[256,1536]{1,0:T(8,128)(2,1)S(1)} custom-call(s32[3]{0:T(128)S(1)} %pad_add_fusion.place, bf16[256,1024]{1,0:T(8,128)(2,1)S(1)} %collective-permute-done.refs_0_.refs_3_, bf16[256,1024]{1,0:T(8,128)(2,1)S(1)} %collective-permute-done.1.refs_1_.refs_4_, bf16[1024,1024]{1,0:T(8,128)(2,1)S(1)} %copy-done, ...), custom_call_target="tpu_custom_call" | custom-call | flops 4000000000 | bytes 9441280 | tf_op jit(solution)/shard_map/block/pallas_call | solution.py:44
  29.7 5.1 %collective-permute-done.4.refs_0_.refs_1_ = bf16[256,1024]{1,0:T(8,128)(2,1)S(1)} collective-permute-done((bf16[256,1024]{1,0:T(8,128)(2,1)S(1)}, bf16[256,1024]{1,0:T(8,128)(2,1)S(1)}, u32[]{:S(2)}, u32[]{:S(2)}) %collective-permute-start.4) | collective-permute-done | bytes 524320 | tf_op jit(solution)/shard_map/ppermute | solution.py:194
  34.8 1.4 %collective-permute-done.5.refs_1_.refs_2_ = bf16[256,1024]{1,0:T(8,128)(2,1)S(1)} collective-permute-done((bf16[256,1024]{1,0:T(8,128)(2,1)S(1)}, bf16[256,1024]{1,0:T(8,128)(2,1)S(1)}, u32[]{:S(2)}, u32[]{:S(2)}) %collective-permute-start.5) | collective-permute-done | bytes 524320 | tf_op jit(solution)/shard_map/ppermute | solution.py:194
  36.2 1.3 %collective-permute-start.6 = (bf16[256,1024]{1,0:T(8,128)(2,1)S(1)}, bf16[256,1024]{1,0:T(8,128)(2,1)S(1)}, u32[]{:S(2)}, u32[]{:S(2)}) collective-permute-start(bf16[256,1024]{1,0:T(8,128)(2,1)S(1)} %collective-permute-done.5.refs_1_.refs_2_), channel_id=1, source_target_pairs={{0,4},{4,0},{8,12},{12,8},{14,10},{10,14},{6,2},{2,6},{1,5},{5,1},... | collective-permute-start | bytes 1572872 | tf_op jit(solution)/shard_map/ppermute | solution.py:194
  38.3 4.3 %block.7.refs_3_.mine = bf16[256,1536]{1,0:T(8,128)(2,1)S(1)} custom-call(s32[3]{0:T(128)S(1)} %pad_add_fusion.place, bf16[256,1024]{1,0:T(8,128)(2,1)S(1)} %collective-permute-done.4.refs_0_.refs_1_, bf16[256,1024]{1,0:T(8,128)(2,1)S(1)} %collective-permute-done.5.refs_1_.refs_2_, bf16[1024,1024]{1,0:T(8,128)(2,1)S(1)} %copy-done, ...), custom_call_target="tpu_custom_call" | custom-call | flops 4000000000 | bytes 9441280 | tf_op jit(solution)/shard_map/block/pallas_call | solution.py:44
  42.8 1.5 %begin.2.refs_0_ = f32[512,512]{1,0:T(8,128)S(1)} custom-call(s32[3]{0:T(128)S(1)} %pad_add_fusion.place, bf16[256,1024]{1,0:T(8,128)(2,1)S(1)} %message.1.refs_0_, bf16[128,1536]{1,0:T(8,128)(2,1)S(1)} %block.5.refs_1_.mine, bf16[128,1536]{1,0:T(8,128)(2,1)S(1)} %collective-permute-done.8.refs_2_.theirs, ...), custom_call_target="tpu_custom_call" | custom-call | flops 1400000000 | bytes 3932160 | tf_op jit(solution)/shard_map/begin/pallas_call | solution.py:44
  44.3 4.0 %collective-permute-done.6.refs_0_.refs_5_ = bf16[256,1024]{1,0:T(8,128)(2,1)S(1)} collective-permute-done((bf16[256,1024]{1,0:T(8,128)(2,1)S(1)}, bf16[256,1024]{1,0:T(8,128)(2,1)S(1)}, u32[]{:S(2)}, u32[]{:S(2)}) %collective-permute-start.6) | collective-permute-done | bytes 524320 | tf_op jit(solution)/shard_map/ppermute | solution.py:194
  49.6 4.5 %block.8.refs_7_.mine = bf16[256,1536]{1,0:T(8,128)(2,1)S(1)} custom-call(s32[3]{0:T(128)S(1)} %pad_add_fusion.place, bf16[256,1024]{1,0:T(8,128)(2,1)S(1)} %collective-permute-done.6.refs_0_.refs_5_, bf16[256,1024]{1,0:T(8,128)(2,1)S(1)} %collective-permute-done.7.refs_1_.refs_6_, bf16[1024,1024]{1,0:T(8,128)(2,1)S(1)} %copy-done, ...), custom_call_target="tpu_custom_call" | custom-call | flops 4000000000 | bytes 9441280 | tf_op jit(solution)/shard_map/block/pallas_call | solution.py:44
  55.1 1.6 %collective-permute-start.10 = (bf16[128,1024]{1,0:T(8,128)(2,1)S(1)}, bf16[128,1024]{1,0:T(8,128)(2,1)S(1)}, u32[]{:S(2)}, u32[]{:S(2)}) collective-permute-start(bf16[128,1024]{1,0:T(8,128)(2,1)S(1)} %slice.6), channel_id=1, source_target_pairs={{0,4},{4,0},{8,12},{12,8},{14,10},{10,14},{6,2},{2,6},{1,5},{5,1},... | collective-permute-start | bytes 786440 | tf_op jit(solution)/shard_map/ppermute | solution.py:194
  56.7 1.8 %begin.3.refs_3_ = f32[512,512]{1,0:T(8,128)S(1)} custom-call(s32[3]{0:T(128)S(1)} %pad_add_fusion.place, f32[512,512]{1,0:T(8,128)S(1)} %begin.2.refs_0_, bf16[256,1024]{1,0:T(8,128)(2,1)S(1)} %collective-permute-done.4.refs_0_.refs_1_, bf16[256,1024]{1,0:T(8,128)(2,1)S(1)} %collective-permute-done.5.refs_1_.refs_2_, ...), custom_call_target="tpu_custom_call" | custom-call | flops 1400000000 | bytes 6291456 | tf_op jit(solution)/shard_map/begin/pallas_call | solution.py:44
  58.5 4.4 %collective-permute-done.11.refs_0_ = bf16[128,1024]{1,0:T(8,128)(2,1)S(1)} collective-permute-done((bf16[128,1024]{1,0:T(8,128)(2,1)S(1)}, bf16[128,1024]{1,0:T(8,128)(2,1)S(1)}, u32[]{:S(2)}, u32[]{:S(2)}) %collective-permute-start.11) | collective-permute-done | bytes 262176 | tf_op jit(solution)/shard_map/ppermute | solution.py:194
  63.5 3.3 %block.9.refs_1_.mine = bf16[128,1536]{1,0:T(8,128)(2,1)S(1)} custom-call(s32[3]{0:T(128)S(1)} %pad_add_fusion.place, bf16[128,1024]{1,0:T(8,128)(2,1)S(1)} %collective-permute-done.10.refs_0_, bf16[1024,1024]{1,0:T(8,128)(2,1)S(1)} %copy-done, bf16[1024,1024]{1,0:T(8,128)(2,1)S(1)} %collective-permute-done.2.refs_2_.refs_3_, ...), custom_call_target="tpu_custom_call" | custom-call | flops 2000000000 | bytes 8654848 | tf_op jit(solution)/shard_map/block/pallas_call | solution.py:44
  66.9 1.7 %collective-permute-done.14.refs_2_.mine = bf16[128,1536]{1,0:T(8,128)(2,1)S(1)} collective-permute-done((bf16[128,1536]{1,0:T(8,128)(2,1)S(1)}, bf16[128,1536]{1,0:T(8,128)(2,1)S(1)}, u32[]{:S(2)}, u32[]{:S(2)}) %collective-permute-start.14) | collective-permute-done | bytes 393248 | tf_op jit(solution)/shard_map/ppermute | solution.py:194
  68.6 2.0 %update.1 = (f32[500,512]{1,0:T(8,128)}, bf16[512,512]{1,0:T(8,128)(2,1)S(1)}) custom-call(s32[3]{0:T(128)S(1)} %pad_add_fusion.place, bf16[128,1024]{1,0:T(8,128)(2,1)S(1)} %collective-permute-done.11.refs_0_, bf16[128,1536]{1,0:T(8,128)(2,1)S(1)} %block.9.refs_1_.mine, bf16[128,1536]{1,0:T(8,128)(2,1)S(1)} %collective-permute-done.14.refs_2_.mine, ...), custom_call_target="tpu_custom_call" | custom-call | flops 800000000 | bytes 3121152 | tf_op jit(solution)/shard_map/update/pallas_call | solution.py:44
  74.2 2.7 %collective-permute-done.19.came = bf16[512,128]{1,0:T(8,128)(2,1)S(1)} collective-permute-done((bf16[512,128]{1,0:T(8,128)(2,1)S(1)}, bf16[512,128]{1,0:T(8,128)(2,1)S(1)}, u32[]{:S(2)}, u32[]{:S(2)}) %collective-permute-start.19) | collective-permute-done | bytes 131104 | tf_op jit(solution)/shard_map/ppermute | solution.py:194
  77.8 1.7 %collective-permute-start.20 = (bf16[512,256]{1,0:T(8,128)(2,1)S(1)}, bf16[512,256]{1,0:T(8,128)(2,1)S(1)}, u32[]{:S(2)}, u32[]{:S(2)}) collective-permute-start(bf16[512,256]{1,0:T(8,128)(2,1)S(1)} %third.3), channel_id=1, source_target_pairs={{0,4},{4,0},{8,12},{12,8},{14,10},{10,14},{6,2},{2,6},{1,5},{5,1},... | collective-permute-start | bytes 786440 | tf_op jit(solution)/shard_map/ppermute | solution.py:194
  80.8 4.7 %collective-permute-done.20.came = bf16[512,256]{1,0:T(8,128)(2,1)S(1)} collective-permute-done((bf16[512,256]{1,0:T(8,128)(2,1)S(1)}, bf16[512,256]{1,0:T(8,128)(2,1)S(1)}, u32[]{:S(2)}, u32[]{:S(2)}) %collective-permute-start.20) | collective-permute-done | bytes 262176 | tf_op jit(solution)/shard_map/ppermute | solution.py:194
  89.2 4.1 %collective-permute-done.21.came = bf16[512,256]{1,0:T(8,128)(2,1)S(1)} collective-permute-done((bf16[512,256]{1,0:T(8,128)(2,1)S(1)}, bf16[512,256]{1,0:T(8,128)(2,1)S(1)}, u32[]{:S(2)}, u32[]{:S(2)}) %collective-permute-start.21) | collective-permute-done | bytes 262176 | tf_op jit(solution)/shard_map/ppermute | solution.py:194
  94.2 1.3 %collective-permute-start.22 = (bf16[512,256]{1,0:T(8,128)(2,1)S(1)}, bf16[512,256]{1,0:T(8,128)(2,1)S(1)}, u32[]{:S(2)}, u32[]{:S(2)}) collective-permute-start(bf16[512,256]{1,0:T(8,128)(2,1)S(1)} %first.3), channel_id=1, source_target_pairs={{0,4},{4,0},{8,12},{12,8},{14,10},{10,14},{6,2},{2,6},{1,5},{5,1},... | collective-permute-start | bytes 786440 | tf_op jit(solution)/shard_map/ppermute | solution.py:194
  97.1 3.8 %collective-permute-done.22.in_b = bf16[512,256]{1,0:T(8,128)(2,1)S(1)} collective-permute-done((bf16[512,256]{1,0:T(8,128)(2,1)S(1)}, bf16[512,256]{1,0:T(8,128)(2,1)S(1)}, u32[]{:S(2)}, u32[]{:S(2)}) %collective-permute-start.22) | collective-permute-done | bytes 262176 | tf_op jit(solution)/shard_map/ppermute | solution.py:194
  100.9 2.6 %collective-permute-done.18.in_a = bf16[512,256]{1,0:T(8,128)(2,1)S(1)} collective-permute-done((bf16[512,256]{1,0:T(8,128)(2,1)S(1)}, bf16[512,256]{1,0:T(8,128)(2,1)S(1)}, u32[]{:S(2)}, u32[]{:S(2)}) %collective-permute-start.18) | collective-permute-done | bytes 262176 | tf_op jit(solution)/shard_map/ppermute | solution.py:194
  104.7 6.1 %collective-permute-done.23.other = bf16[512,256]{1,0:T(8,128)(2,1)S(1)} collective-permute-done((bf16[512,256]{1,0:T(8,128)(2,1)S(1)}, bf16[512,256]{1,0:T(8,128)(2,1)S(1)}, u32[]{:S(2)}, u32[]{:S(2)}) %collective-permute-start.23) | collective-permute-done | bytes 262176 | tf_op jit(solution)/shard_map/ppermute | solution.py:194
  110.8 1.7 %apply.1 = f32[500,512]{1,0:T(8,128)} custom-call(s32[3]{0:T(128)S(1)} %pad_add_fusion.place, f32[500,512]{1,0:T(8,128)S(1)} %bitcast.11, bf16[512,256]{1,0:T(8,128)(2,1)S(1)} %last.1.own, bf16[512,256]{1,0:T(8,128)(2,1)S(1)} %collective-permute-done.23.other), custom_call_target="tpu_custom_call" | custom-call | flops 100000000 | bytes 1548288 | tf_op jit(solution)/shard_map/apply/pallas_call | solution.py:44
  (56 shorter events, 22.2 us)
Async XLA Ops:
  0.6 8.6 %copy-start.7 = (bf16[1024]{0:T(1024)(128)(2,1)S(1)}, bf16[1024]{0:T(1024)(128)(2,1)}, u32[]{:S(2)}) copy-start(bf16[1024]{0:T(1024)(128)(2,1)} %param.9) | copy-start | bytes 6148
  0.6 12.3 %collective-permute-start.2 = (bf16[1024,1024]{1,0:T(8,128)(2,1)}, bf16[1024,1024]{1,0:T(8,128)(2,1)S(1)}, u32[]{:S(2)}, u32[]{:S(2)}) collective-permute-start(bf16[1024,1024]{1,0:T(8,128)(2,1)} %refs_1_.3), channel_id=1, source_target_pairs={{0,1},{1,0},{2,3},{3,2},{4,5},{5,4},{6,7},{7,6},{8,9},{9,8},{10,11... | collective-permute-start | bytes 6291464 | tf_op jit(solution)/shard_map/ppermute | solution.py:194
  1.2 1.2 %copy-start.2 = (f32[512,500]{0,1:T(8,128)S(1)}, f32[512,500]{0,1:T(8,128)}, u32[]{:S(2)}) copy-start(f32[512,500]{0,1:T(8,128)} %param.12) | copy-start | bytes 3072004
  2.5 1.2 %copy-start.4 = (bf16[512,1024]{1,0:T(8,128)(2,1)S(1)}, bf16[512,1024]{1,0:T(8,128)(2,1)}, u32[]{:S(2)}) copy-start(bf16[512,1024]{1,0:T(8,128)(2,1)} %inputs.1) | copy-start | bytes 3145732
  3.7 0.7 copy-start.6
  5.0 15.1 %collective-permute-start.1 = (bf16[256,1024]{1,0:T(8,128)(2,1)S(1)}, bf16[256,1024]{1,0:T(8,128)(2,1)S(1)}, u32[]{:S(2)}, u32[]{:S(2)}) collective-permute-start(bf16[256,1024]{1,0:T(8,128)(2,1)S(1)} %message.1.refs_0_), channel_id=1, source_target_pairs={{4,8},{8,4},{12,14},{14,12},{10,6},{6,10},{2,0},{0,2},{5,9},{9,5},... | collective-permute-start | bytes 1572872 | tf_op jit(solution)/shard_map/ppermute | solution.py:194
  7.6 14.0 %collective-permute-start = (bf16[256,1024]{1,0:T(8,128)(2,1)S(1)}, bf16[256,1024]{1,0:T(8,128)(2,1)S(1)}, u32[]{:S(2)}, u32[]{:S(2)}) collective-permute-start(bf16[256,1024]{1,0:T(8,128)(2,1)S(1)} %message.1.refs_0_), channel_id=1, source_target_pairs={{0,4},{4,0},{8,12},{12,8},{14,10},{10,14},{6,2},{2,6},{1,5},{5,1},... | collective-permute-start | bytes 1572872 | tf_op jit(solution)/shard_map/ppermute | solution.py:194
  9.3 3.6 %collective-permute-start.3 = (bf16[1,1024]{1,0:T(2,128)(2,1)S(1)}, bf16[1,1024]{1,0:T(2,128)(2,1)S(1)}, u32[]{:S(2)}, u32[]{:S(2)}) collective-permute-start(bf16[1,1024]{1,0:T(2,128)(2,1)S(1)} %broadcast_in_dim.7.refs_3_.refs_4_), channel_id=1, source_target_pairs={{0,1},{1,0},{2,3},{3,2},{4,5},{5,4},{6,7},{7,6},{8,9},{9,8},{10,11... | collective-permute-start | bytes 6152 | tf_op jit(solution)/shard_map/ppermute | solution.py:194
  9.3 2.2 %copy-start.1 = (f32[1,512,2048]{2,1,0:T(8,128)S(1)}, f32[1,512,2048]{2,1,0:T(8,128)}, u32[]{:S(2)}) copy-start(f32[1,512,2048]{2,1,0:T(8,128)} %param.10) | copy-start | bytes 12582916
  11.5 1.6 %copy-start = (bf16[1024,1024]{1,0:T(8,128)(2,1)S(1)}, bf16[1024,1024]{1,0:T(8,128)(2,1)}, u32[]{:S(2)}) copy-start(bf16[1024,1024]{1,0:T(8,128)(2,1)} %refs_1_.3) | copy-start | bytes 6291460
  21.6 13.2 %collective-permute-start.4 = (bf16[256,1024]{1,0:T(8,128)(2,1)S(1)}, bf16[256,1024]{1,0:T(8,128)(2,1)S(1)}, u32[]{:S(2)}, u32[]{:S(2)}) collective-permute-start(bf16[256,1024]{1,0:T(8,128)(2,1)S(1)} %collective-permute-done.1.refs_1_.refs_4_), channel_id=1, source_target_pairs={{0,4},{4,0},{8,12},{12,8},{14,10},{10,14},{6,2},{2,6},{1,5},{5,1},... | collective-permute-start | bytes 1572872 | tf_op jit(solution)/shard_map/ppermute | solution.py:194
  23.3 12.9 %collective-permute-start.5 = (bf16[256,1024]{1,0:T(8,128)(2,1)S(1)}, bf16[256,1024]{1,0:T(8,128)(2,1)S(1)}, u32[]{:S(2)}, u32[]{:S(2)}) collective-permute-start(bf16[256,1024]{1,0:T(8,128)(2,1)S(1)} %collective-permute-done.refs_0_.refs_3_), channel_id=1, source_target_pairs={{4,8},{8,4},{12,14},{14,12},{10,6},{6,10},{2,0},{0,2},{5,9},{9,5},... | collective-permute-start | bytes 1572872 | tf_op jit(solution)/shard_map/ppermute | solution.py:194
  29.1 13.6 %collective-permute-start.9 = (bf16[256,1536]{1,0:T(8,128)(2,1)S(1)}, bf16[256,1536]{1,0:T(8,128)(2,1)S(1)}, u32[]{:S(2)}, u32[]{:S(2)}) collective-permute-start(bf16[256,1536]{1,0:T(8,128)(2,1)S(1)} %block.6.refs_5_.mine), channel_id=1, source_target_pairs={{0,1},{1,0},{2,3},{3,2},{4,5},{5,4},{6,7},{7,6},{8,9},{9,8},{10,11... | collective-permute-start | bytes 2359304 | tf_op jit(solution)/shard_map/ppermute | solution.py:194
  29.2 13.5 %collective-permute-start.8 = (bf16[128,1536]{1,0:T(8,128)(2,1)S(1)}, bf16[128,1536]{1,0:T(8,128)(2,1)S(1)}, u32[]{:S(2)}, u32[]{:S(2)}) collective-permute-start(bf16[128,1536]{1,0:T(8,128)(2,1)S(1)} %block.5.refs_1_.mine), channel_id=1, source_target_pairs={{0,1},{1,0},{2,3},{3,2},{4,5},{5,4},{6,7},{7,6},{8,9},{9,8},{10,11... | collective-permute-start | bytes 1179656 | tf_op jit(solution)/shard_map/ppermute | solution.py:194
  36.2 12.0 %collective-permute-start.6 = (bf16[256,1024]{1,0:T(8,128)(2,1)S(1)}, bf16[256,1024]{1,0:T(8,128)(2,1)S(1)}, u32[]{:S(2)}, u32[]{:S(2)}) collective-permute-start(bf16[256,1024]{1,0:T(8,128)(2,1)S(1)} %collective-permute-done.5.refs_1_.refs_2_), channel_id=1, source_target_pairs={{0,4},{4,0},{8,12},{12,8},{14,10},{10,14},{6,2},{2,6},{1,5},{5,1},... | collective-permute-start | bytes 1572872 | tf_op jit(solution)/shard_map/ppermute | solution.py:194
  37.6 12.0 %collective-permute-start.7 = (bf16[256,1024]{1,0:T(8,128)(2,1)S(1)}, bf16[256,1024]{1,0:T(8,128)(2,1)S(1)}, u32[]{:S(2)}, u32[]{:S(2)}) collective-permute-start(bf16[256,1024]{1,0:T(8,128)(2,1)S(1)} %collective-permute-done.4.refs_0_.refs_1_), channel_id=1, source_target_pairs={{4,8},{8,4},{12,14},{14,12},{10,6},{6,10},{2,0},{0,2},{5,9},{9,5},... | collective-permute-start | bytes 1572872 | tf_op jit(solution)/shard_map/ppermute | solution.py:194
  42.7 14.0 %collective-permute-start.12 = (bf16[256,1536]{1,0:T(8,128)(2,1)S(1)}, bf16[256,1536]{1,0:T(8,128)(2,1)S(1)}, u32[]{:S(2)}, u32[]{:S(2)}) collective-permute-start(bf16[256,1536]{1,0:T(8,128)(2,1)S(1)} %block.7.refs_3_.mine), channel_id=1, source_target_pairs={{0,1},{1,0},{2,3},{3,2},{4,5},{5,4},{6,7},{7,6},{8,9},{9,8},{10,11... | collective-permute-start | bytes 2359304 | tf_op jit(solution)/shard_map/ppermute | solution.py:194
  54.1 2.6 %collective-permute-start.13 = (bf16[256,1536]{1,0:T(8,128)(2,1)S(1)}, bf16[256,1536]{1,0:T(8,128)(2,1)S(1)}, u32[]{:S(2)}, u32[]{:S(2)}) collective-permute-start(bf16[256,1536]{1,0:T(8,128)(2,1)S(1)} %block.8.refs_7_.mine), channel_id=1, source_target_pairs={{0,1},{1,0},{2,3},{3,2},{4,5},{5,4},{6,7},{7,6},{8,9},{9,8},{10,11... | collective-permute-start | bytes 2359304 | tf_op jit(solution)/shard_map/ppermute | solution.py:194
  54.2 8.7 %collective-permute-start.11 = (bf16[128,1024]{1,0:T(8,128)(2,1)S(1)}, bf16[128,1024]{1,0:T(8,128)(2,1)S(1)}, u32[]{:S(2)}, u32[]{:S(2)}) collective-permute-start(bf16[128,1024]{1,0:T(8,128)(2,1)S(1)} %slice.7), channel_id=1, source_target_pairs={{4,8},{8,4},{12,14},{14,12},{10,6},{6,10},{2,0},{0,2},{5,9},{9,5},... | collective-permute-start | bytes 786440 | tf_op jit(solution)/shard_map/ppermute | solution.py:194
  55.1 8.4 %collective-permute-start.10 = (bf16[128,1024]{1,0:T(8,128)(2,1)S(1)}, bf16[128,1024]{1,0:T(8,128)(2,1)S(1)}, u32[]{:S(2)}, u32[]{:S(2)}) collective-permute-start(bf16[128,1024]{1,0:T(8,128)(2,1)S(1)} %slice.6), channel_id=1, source_target_pairs={{0,4},{4,0},{8,12},{12,8},{14,10},{10,14},{6,2},{2,6},{1,5},{5,1},... | collective-permute-start | bytes 786440 | tf_op jit(solution)/shard_map/ppermute | solution.py:194
  58.5 10.1 %copy-start.5 = (f32[512,500]{0,1:T(8,128)S(1)}, f32[512,500]{0,1:T(8,128)}, u32[]{:S(2)}) copy-start(f32[512,500]{0,1:T(8,128)} %param.13) | copy-start | bytes 3072004
  66.8 1.8 %collective-permute-start.14 = (bf16[128,1536]{1,0:T(8,128)(2,1)S(1)}, bf16[128,1536]{1,0:T(8,128)(2,1)S(1)}, u32[]{:S(2)}, u32[]{:S(2)}) collective-permute-start(bf16[128,1536]{1,0:T(8,128)(2,1)S(1)} %block.9.refs_1_.mine), channel_id=1, source_target_pairs={{0,1},{1,0},{2,3},{3,2},{4,5},{5,4},{6,7},{7,6},{8,9},{9,8},{10,11... | collective-permute-start | bytes 1179656 | tf_op jit(solution)/shard_map/ppermute | solution.py:194
  71.4 5.6 %collective-permute-start.19 = (bf16[512,128]{1,0:T(8,128)(2,1)S(1)}, bf16[512,128]{1,0:T(8,128)(2,1)S(1)}, u32[]{:S(2)}, u32[]{:S(2)}) collective-permute-start(bf16[512,128]{1,0:T(8,128)(2,1)S(1)} %far.3), channel_id=1, source_target_pairs={{4,8},{8,4},{12,14},{14,12},{10,6},{6,10},{2,0},{0,2},{5,9},{9,5},... | collective-permute-start | bytes 393224 | tf_op jit(solution)/shard_map/ppermute | solution.py:194
  73.5 6.0 %collective-permute-start.15 = (bf16[512,128]{1,0:T(8,128)(2,1)S(1)}, bf16[512,128]{1,0:T(8,128)(2,1)S(1)}, u32[]{:S(2)}, u32[]{:S(2)}) collective-permute-start(bf16[512,128]{1,0:T(8,128)(2,1)S(1)} %far.2), channel_id=1, source_target_pairs={{0,4},{4,0},{8,12},{12,8},{14,10},{10,14},{6,2},{2,6},{1,5},{5,1},... | collective-permute-start | bytes 393224 | tf_op jit(solution)/shard_map/ppermute | solution.py:194
  77.8 7.6 %collective-permute-start.20 = (bf16[512,256]{1,0:T(8,128)(2,1)S(1)}, bf16[512,256]{1,0:T(8,128)(2,1)S(1)}, u32[]{:S(2)}, u32[]{:S(2)}) collective-permute-start(bf16[512,256]{1,0:T(8,128)(2,1)S(1)} %third.3), channel_id=1, source_target_pairs={{0,4},{4,0},{8,12},{12,8},{14,10},{10,14},{6,2},{2,6},{1,5},{5,1},... | collective-permute-start | bytes 786440 | tf_op jit(solution)/shard_map/ppermute | solution.py:194
  80.4 7.6 %collective-permute-start.16 = (bf16[512,256]{1,0:T(8,128)(2,1)S(1)}, bf16[512,256]{1,0:T(8,128)(2,1)S(1)}, u32[]{:S(2)}, u32[]{:S(2)}) collective-permute-start(bf16[512,256]{1,0:T(8,128)(2,1)S(1)} %third.2), channel_id=1, source_target_pairs={{4,8},{8,4},{12,14},{14,12},{10,6},{6,10},{2,0},{0,2},{5,9},{9,5},... | collective-permute-start | bytes 786440 | tf_op jit(solution)/shard_map/ppermute | solution.py:194
  86.3 7.0 %collective-permute-start.21 = (bf16[512,256]{1,0:T(8,128)(2,1)S(1)}, bf16[512,256]{1,0:T(8,128)(2,1)S(1)}, u32[]{:S(2)}, u32[]{:S(2)}) collective-permute-start(bf16[512,256]{1,0:T(8,128)(2,1)S(1)} %second.3), channel_id=1, source_target_pairs={{4,8},{8,4},{12,14},{14,12},{10,6},{6,10},{2,0},{0,2},{5,9},{9,5},... | collective-permute-start | bytes 786440 | tf_op jit(solution)/shard_map/ppermute | solution.py:194
  88.8 7.0 %collective-permute-start.17 = (bf16[512,256]{1,0:T(8,128)(2,1)S(1)}, bf16[512,256]{1,0:T(8,128)(2,1)S(1)}, u32[]{:S(2)}, u32[]{:S(2)}) collective-permute-start(bf16[512,256]{1,0:T(8,128)(2,1)S(1)} %second.2), channel_id=1, source_target_pairs={{0,4},{4,0},{8,12},{12,8},{14,10},{10,14},{6,2},{2,6},{1,5},{5,1},... | collective-permute-start | bytes 786440 | tf_op jit(solution)/shard_map/ppermute | solution.py:194
  94.2 16.6 %copy-start.3 = (f32[512,500]{0,1:T(8,128)S(1)}, f32[512,500]{0,1:T(8,128)}, u32[]{:S(2)}) copy-start(f32[512,500]{0,1:T(8,128)} %param.12) | copy-start | bytes 3072004
  94.2 6.7 %collective-permute-start.22 = (bf16[512,256]{1,0:T(8,128)(2,1)S(1)}, bf16[512,256]{1,0:T(8,128)(2,1)S(1)}, u32[]{:S(2)}, u32[]{:S(2)}) collective-permute-start(bf16[512,256]{1,0:T(8,128)(2,1)S(1)} %first.3), channel_id=1, source_target_pairs={{0,4},{4,0},{8,12},{12,8},{14,10},{10,14},{6,2},{2,6},{1,5},{5,1},... | collective-permute-start | bytes 786440 | tf_op jit(solution)/shard_map/ppermute | solution.py:194
  96.7 6.8 %collective-permute-start.18 = (bf16[512,256]{1,0:T(8,128)(2,1)S(1)}, bf16[512,256]{1,0:T(8,128)(2,1)S(1)}, u32[]{:S(2)}, u32[]{:S(2)}) collective-permute-start(bf16[512,256]{1,0:T(8,128)(2,1)S(1)} %first.2), channel_id=1, source_target_pairs={{4,8},{8,4},{12,14},{14,12},{10,6},{6,10},{2,0},{0,2},{5,9},{9,5},... | collective-permute-start | bytes 786440 | tf_op jit(solution)/shard_map/ppermute | solution.py:194
  104.4 6.4 %collective-permute-start.23 = (bf16[512,256]{1,0:T(8,128)(2,1)S(1)}, bf16[512,256]{1,0:T(8,128)(2,1)S(1)}, u32[]{:S(2)}, u32[]{:S(2)}) collective-permute-start(bf16[512,256]{1,0:T(8,128)(2,1)S(1)} %last.1.own), channel_id=1, source_target_pairs={{0,2},{2,0},{1,3},{3,1},{4,6},{6,4},{5,7},{7,5},{8,10},{10,8},{9,1... | collective-permute-start | bytes 786440 | tf_op jit(solution)/shard_map/ppermute | solution.py:194

commit v6 on v5

v6 whole, which is shorter than its diff:
```python
import functools

import jax
import jax.numpy as jnp
from jax import lax
from jax.experimental import pallas as pl
from jax.experimental.pallas import tpu as pltpu
from jax.sharding import PartitionSpec as P

DAMPING = 0.5
F32, BF16 = jnp.float32, jnp.bfloat16
LANES = 128

COS_TERMS = (
    0.9999999887556631, -0.49999988843399, 0.04166648574334225, -0.001388778673619495,
    2.4769518189949842e-05, -2.7075418374484127e-07, 1.7231808612122658e-09,
)
INV_TWO_PI = 0.15915494309189535
TWO_PI_HIGH = 6.28125
TWO_PI_LOW = 0.0019353071795864769


def cosine(angles):
    turns = jnp.round(angles * INV_TWO_PI)
    rest = (angles - turns * TWO_PI_HIGH) - turns * TWO_PI_LOW
    square = rest * rest
    result = jnp.full_like(square, COS_TERMS[-1])
    for term in COS_TERMS[-2::-1]:
        result = result * square + term
    return result


def dot(a, b):
    return jnp.dot(a, b, preferred_element_type=F32)


def dot_nt(a, b):
    return lax.dot_general(a, b, (((1,), (1,)), ((), ())), preferred_element_type=F32)


def call(kernel, out_shapes, place, args, name, vmem_mib, mflops, scratch=()):
    vmem = pl.BlockSpec(memory_space=pltpu.VMEM)
    single = isinstance(out_shapes, jax.ShapeDtypeStruct)
    return pl.pallas_call(
        kernel,
        out_shape=out_shapes,
        in_specs=[pl.BlockSpec(memory_space=pltpu.SMEM)] + [vmem] * len(args),
        out_specs=vmem if single else (vmem,) * len(out_shapes),
        scratch_shapes=scratch,
        cost_estimate=pl.CostEstimate(
            flops=mflops * 10**6, transcendentals=0, bytes_accessed=sum(a.size * a.dtype.itemsize for a in args)
        ),
        compiler_params=pltpu.CompilerParams(vmem_limit_bytes=vmem_mib << 20),
        name=name,
    )(place, *args)


def like(shape, dtype=BF16):
    return jax.ShapeDtypeStruct(tuple(shape), dtype)


def lanes(index, size):
    return pl.ds(pl.multiple_of(index * size, size), size)


def inputs_kernel(place, inputs, out):
    part = out.shape[0] // 2
    for j in (0, 1):
        start = pl.multiple_of((2 * place[1] + (place[2] ^ j)) * part, part)
        out[j * part:(j + 1) * part] = inputs[pl.ds(start, part)]


def residual_kernel(place, labels, predictions, own, given):
    width = predictions.shape[0]
    part = own.shape[1] // 2
    tail = own.shape[0] - width
    own[width:], given[width:] = (jnp.zeros((tail, 2 * part), BF16),) * 2
    for j in (0, 1):
        at = lanes(2 * place[1] + (place[2] ^ j), part)
        classes = lax.broadcasted_iota(jnp.int32, (width, part), 0) + place[2] * width
        residual = ((classes == labels[:, at]).astype(F32) - predictions[:, at]).astype(BF16)
        own[:width, j * part:(j + 1) * part] = residual
        given[:width, (1 - j) * part:(2 - j) * part] = residual


def high_low(x):
    high = x.astype(BF16)
    return high, (x - high.astype(F32)).astype(BF16)


def split_kernel(place, x, high, low):
    high[...], low[...] = high_low(x[...])


TILE = 512


def block_kernel(place, rows, w_own, w_other, p_own, p_other, high, low, out, own_slice, feats):
    inputs = rows[:feats.shape[0]]
    half, depth = w_own.shape[1], high.shape[0]
    total = None
    for i, (weights, phases) in enumerate(((w_own, p_own), (w_other, p_other))):
        for k in range(0, half, TILE):
            at = pl.ds(pl.multiple_of((place[2] ^ i) * half + k, TILE), TILE)
            angles = dot(inputs, weights[:, k:k + TILE]) + phases[:, k:k + TILE].astype(F32)
            tile = cosine(angles).astype(BF16)
            feats[:, at] = tile
            product = dot_nt(tile, high[:, at]) + dot_nt(tile, low[:, at])
            total = product if total is None else total + product
    out[:, :depth], out[:, depth:] = high_low(total)
    own_slice[...] = feats[:, lanes(place[0], depth)]


def product_of(refs, classes):
    total, short = None, None
    for residual, q in zip(refs[::2], refs[1::2]):
        left, right = residual[:classes], q[...]
        if right.shape[0] < 256:
            if short is None:
                short = left[:, :right.shape[0]], right
                continue
            at = slice(0, right.shape[0]) if left.shape[1] == right.shape[0] else slice(right.shape[0], None)
            left = jnp.concatenate([short[0], left[:, at]], axis=1)
            right = jnp.concatenate([short[1], right], axis=0)
            short = None
        product = dot(left, right)
        depth = product.shape[1] // 2
        product = product[:, :depth] + product[:, depth:]
        total = product if total is None else total + product
    return total


def begin_kernel(earlier, place, *refs):
    *pieces, out = refs
    total = product_of(pieces[earlier:], out.shape[0])
    out[...] = pieces[0][...] + total if earlier else total


def update_kernel(place, begun, coefficients, *refs):
    *pieces, new, sent = refs
    update = DAMPING * (begun[...] + product_of(pieces, begun.shape[0]))
    new[...] = coefficients[...] + update[:new.shape[0]]
    sent[...] = update.astype(BF16)


def far_kernel(place, sent, feats, out):
    out[...] = dot_nt(sent[...], feats[...]).astype(BF16)


def hop_kernel(place, sent, feats, came, out):
    total = dot_nt(sent[...], feats[...])
    size = came.shape[1]
    out[:, :size] = (total[:, :size] + came[...].astype(F32)).astype(BF16)
    if size < out.shape[1]:
        out[:, size:] = total[:, size:].astype(BF16)


def last_kernel(place, sent, mine, theirs, came, given, out):
    part = mine.shape[0]
    total = dot_nt(sent[...], jnp.concatenate([mine[...], theirs[...]], axis=0)) + came[...].astype(F32)
    for i in (0, 1):
        at, there = slice(i * part, (i + 1) * part), slice((1 - i) * part, (2 - i) * part)
        out[:, at] = (total[:, at] + given[:, there].astype(F32)).astype(BF16)


def apply_kernel(place, predictions, own, other, new):
    width, part = new.shape[0], own.shape[1] // 2
    for i, source in enumerate((own, other)):
        for j in (0, 1):
            at = lanes(2 * (place[1] ^ i) + (place[2] ^ j), part)
            new[:, at] = predictions[:, at] + source[:width, j * part:(j + 1) * part].astype(F32)


def swap(x, axes, pairs):
    return lax.ppermute(x, axes, [p for a, b in pairs for p in ((a, b), (b, a))])


def after(arrays, *others):
    return lax.optimization_barrier((*arrays, *others))[:len(arrays)]


def ring_shards(n_rows, inputs, projection, phases, inverse_blocks, labels, predictions, coefficients):
    ring = [2 * z for z in range(n_rows)] + [2 * z + 1 for z in reversed(range(n_rows))]
    size = len(ring)
    even = [(ring[i], ring[i + 1]) for i in range(0, size, 2)]
    odd = [(ring[i], ring[(i + 1) % size]) for i in range(1, size, 2)]
    ways = [[(2 * a + c, 2 * b + c) for c, pairs in enumerate(way) for a, b in pairs]
            for way in ((even, odd), (odd, even))]
    S = lambda x: swap(x, ("rows", "blocks", "cols"), ways[0])
    T = lambda x: swap(x, ("rows", "blocks", "cols"), ways[1])
    C = lambda x: swap(x, "cols", [(0, 1)])

    place = jnp.stack([lax.axis_index(a) for a in ("rows", "blocks", "cols")]).astype(jnp.int32)
    local_rows, width = predictions.shape
    part = local_rows // 4
    padded = -(-width // LANES) * LANES
    predictions, coefficients = predictions.T, coefficients.T
    depth = coefficients.shape[1]

    x0 = call(inputs_kernel, like((2 * part, inputs.shape[1])), place, (inputs,), "inputs", 6, 100)
    own, given = call(
        residual_kernel, (like((padded, 2 * part)),) * 2, place, (labels[None, :], predictions), "residual", 6, 300
    )
    r0 = jnp.concatenate([own, C(given)], axis=0)
    weights = (projection, C(projection))
    phases = phases[None, :]
    phases = (phases, C(phases))
    inverse = call(
        split_kernel, (like(inverse_blocks.shape[1:]),) * 2, place, (inverse_blocks[0],), "split", 14, 500
    )

    def block(rows, size):
        scratch = (pltpu.VMEM((size, 2 * projection.shape[1]), BF16),)
        return call(
            block_kernel, (like((size, 2 * depth)), like((size, depth))), place,
            (rows, *weights, *phases, *inverse), "block", 16, size, scratch,
        )

    def begin(pairs, *earlier):
        return call(
            functools.partial(begin_kernel, len(earlier)), like((padded, depth), F32), place,
            (*earlier, *[a for pair in pairs for a in pair]), "begin", 14, 200,
        )

    x1, r1 = S(x0), S(r0)
    q0, f0 = block(x0, part)
    (x1,) = after((x1,), q0)
    x2 = T(x1)
    q1, f1 = block(x1, 2 * part)
    (r1,) = after((r1,), q1)
    r2 = T(r1)
    (x2,) = after((x2,), q1)
    x3 = S(x2)
    q2, f2 = block(x2, 2 * part)
    (r2,) = after((r2,), q2)
    r3 = S(r2)
    theirs = lambda r: C(r[padded:])
    q0_other, f0_other = C(q0), C(f0)
    begun = begin([(r0, q0), (r0, q0_other), (r1, q1), (theirs(r1), C(q1))])
    (x3,) = after((x3,), begun, f0_other)
    x4 = T(x3[:part])
    q3, f3 = block(x3, 2 * part)
    (r3,) = after((r3,), q3)
    r4 = T(r3[:, :part])
    begun = begin([(r2, q2), (theirs(r2), C(q2)), (r3, q3), (theirs(r3), C(q3))], begun)
    (x4,) = after((x4,), begun)
    q4, f4 = block(x4, part)
    new_coefficients, sent = call(
        update_kernel, (like(coefficients.shape, F32), like((padded, depth))), place,
        (begun, coefficients, r4, q4, theirs(r4), C(q4)), "update", 14, 800,
    )

    piece, whole = like((padded, part)), like((padded, 2 * part))
    far = lambda u: call(far_kernel, piece, place, (u, f4), "far", 6, 70)
    first = far(sent)
    updates = (sent, *after((C(sent),), first))
    moving = [T(first), T(far(updates[1]))]
    for way, feats in ((S, f3), (T, f2), (S, f1)):
        moving = [
            way(call(hop_kernel, whole, place, (u, feats, m), "hop", 6, 150)) for u, m in zip(updates, moving)
        ]
    own = call(last_kernel, whole, place, (sent, f0, f0_other, moving[0], C(moving[1])), "last", 6, 150)
    other = swap(own, "blocks", [(0, 1)])
    new = call(apply_kernel, like(predictions.shape, F32), place, (predictions, own, other), "apply", 6, 100)
    return new_coefficients.T, new.T


def plain_shards(inputs, projection, phases, inverse_blocks, labels, predictions, coefficients):
    out_width = predictions.shape[1]
    classes = lax.axis_index("cols") * out_width + jnp.arange(out_width, dtype=jnp.int32)
    onehot = (labels[:, None] == classes[None, :]).astype(F32)
    residual = (onehot - predictions).astype(BF16)
    angles = dot(inputs, projection) + phases.astype(F32)[None, :]
    half_features = jnp.cos(angles).astype(BF16)
    features_full = lax.all_gather(half_features, "cols", axis=1, tiled=True)
    own_gradient = lax.psum_scatter(
        lax.dot_general(features_full, residual, (((0,), (0,)), ((), ())), preferred_element_type=F32),
        "rows", scatter_dimension=0, tiled=True,
    )
    gradient_full = lax.all_gather(own_gradient, "rows", axis=0, tiled=True)
    update = DAMPING * jnp.dot(inverse_blocks[0], gradient_full, precision=lax.Precision.HIGHEST)
    sent = lax.all_gather(update.astype(BF16), "rows", axis=0, tiled=True)
    summed = lax.psum(dot(features_full, sent), "blocks")
    return coefficients + update, predictions + summed


def solution(mesh):
    n_rows, n_blocks = mesh.shape["rows"], mesh.shape["blocks"]
    small_ring = n_blocks == 2 and n_rows == 4 and mesh.shape["cols"] == 2
    shards = functools.partial(ring_shards, n_rows) if small_ring else plain_shards
    return jax.shard_map(
        shards,
        mesh=mesh,
        in_specs=(
            P(("groups", "rows"), None),
            P(None, ("groups", "blocks", "cols")),
            P(("groups", "blocks", "cols")),
            P(("groups", "blocks"), "rows", None),
            P(("groups", "rows")),
            P(("groups", "rows"), "cols"),
            P(("groups", "blocks", "rows"), "cols"),
        ),
        out_specs=(P(("groups", "blocks", "rows"), "cols"), P(("groups", "rows"), "cols")),
        check_vma=False,
    )
```

time: 113 us -> 111 us (0.982)
  waiting for transfers between devices: 48.5 us -> 34.8 us
  starting transfers between devices: 21 us -> 32.6 us
    ppermute x24 -> x32, waiting for transfers between devices: 48.5 us -> 34.8 us  [swap(): lax.ppermute(x, axes, [p for a, b in pairs for p in ((a, b), (b, a))])]
    ppermute x24 -> x32, starting transfers between devices: 21 us -> 32.6 us  [swap(): lax.ppermute(x, axes, [p for a, b in pairs for p in ((a, b), (b, a))])]
    pallas_call x20 -> x21, Pallas kernels: 36.4 us -> 37 us  [call(): pl.pallas_call(kernel, out_shape=out_shapes, in_specs=[pl.BlockSpec(memor...]
    unnamed x16 -> x17, local copies, waits for them, and re-layouts: 5.54 us -> 5.56 us
  transfers between devices with their start and end apart: 24 -> 32, of which waited for: 17 -> 12; matrix products, arithmetic and copies ran while one was open for 0% -> 0% of each run, Pallas kernels for 25% -> 28%
where the time goes in v6:
time: 111 us
  Pallas kernels  37 us (33%)
  waiting for transfers between devices  34.8 us (31%)
  starting transfers between devices  32.6 us (29%)
  local copies, waits for them, and re-layouts  5.68 us (5%)
    pallas_call x21, Pallas kernels, call(): pl.pallas_call(kernel, out_shape=out_shapes, in_specs=[pl.BlockSpec(memor...  37 us
    ppermute x32, waiting for transfers between devices, swap(): lax.ppermute(x, axes, [p for a, b in pairs for p in ((a, b), (b, a))])  34.8 us
    ppermute x32, starting transfers between devices, swap(): lax.ppermute(x, axes, [p for a, b in pairs for p in ((a, b), (b, a))])  32.6 us
    unnamed x17, local copies, waits for them, and re-layouts  5.56 us
  transfers between devices with their start and end apart: 32, of which 12 were waited for; matrix products, arithmetic and copies ran while one was open for 0% of the time, Pallas kernels for 28%

profile of v6, /device:TPU:0, one launch (start us, length us, event | category | flops | bytes accessed | tf_op | source)
XLA Modules:
  0.0 111.2 jit_solution(4966257210532271643)
XLA Ops:
  5.7 3.1 %collective-permute-start.5 = (bf16[256,1024]{1,0:T(8,128)(2,1)S(1)}, bf16[256,1024]{1,0:T(8,128)(2,1)S(1)}, u32[]{:S(2)}, u32[]{:S(2)}) collective-permute-start(bf16[256,1024]{1,0:T(8,128)(2,1)S(1)} %inputs.2.rows), channel_id=1, source_target_pairs={{0,4},{4,0},{8,12},{12,8},{14,10},{10,14},{6,2},{2,6},{5,9},{9,5},... | collective-permute-start | bytes 1572872 | tf_op jit(solution)/shard_map/ppermute | solution.py:175
  9.1 2.2 %copy-done.1 = f32[1,512,2048]{2,1,0:T(8,128)S(1)} copy-done((f32[1,512,2048]{2,1,0:T(8,128)S(1)}, f32[1,512,2048]{2,1,0:T(8,128)}, u32[]{:S(2)}) %copy-start.1) | copy-done | bytes 4194328
  12.8 3.3 %block.5 = (bf16[128,1024]{1,0:T(8,128)(2,1)S(1)}, bf16[128,512]{1,0:T(8,128)(2,1)S(1)}) custom-call(s32[3]{0:T(128)S(1)} %pad_add_fusion.place, bf16[256,1024]{1,0:T(8,128)(2,1)S(1)} %inputs.2.rows, bf16[1024,1024]{1,0:T(8,128)(2,1)S(1)} %copy-done, bf16[1024,1024]{1,0:T(8,128)(2,1)S(1)} %collective-permute-done.1.w_other, ...), custom_call_target="tpu_custom_call" | custom-call | flops 128000000 | bytes 8916992 | tf_op jit(solution)/shard_map/block/pallas_call | solution.py:44
  16.2 2.0 %collective-permute-start.9 = (bf16[256,1024]{1,0:T(8,128)(2,1)S(1)}, bf16[256,1024]{1,0:T(8,128)(2,1)S(1)}, u32[]{:S(2)}, u32[]{:S(2)}) collective-permute-start(bf16[256,1024]{1,0:T(8,128)(2,1)S(1)} %collective-permute-done.5.rows), channel_id=1, source_target_pairs={{4,8},{8,4},{12,14},{14,12},{10,6},{6,10},{2,0},{0,2},{1,5},{5,1},... | collective-permute-start | bytes 1572872 | tf_op jit(solution)/shard_map/ppermute | solution.py:175
  18.1 4.3 %block.6 = (bf16[256,1024]{1,0:T(8,128)(2,1)S(1)}, bf16[256,512]{1,0:T(8,128)(2,1)S(1)}) custom-call(s32[3]{0:T(128)S(1)} %pad_add_fusion.place, bf16[256,1024]{1,0:T(8,128)(2,1)S(1)} %collective-permute-done.5.rows, bf16[1024,1024]{1,0:T(8,128)(2,1)S(1)} %copy-done, bf16[1024,1024]{1,0:T(8,128)(2,1)S(1)} %collective-permute-done.1.w_other, ...), custom_call_target="tpu_custom_call" | custom-call | flops 256000000 | bytes 8916992 | tf_op jit(solution)/shard_map/block/pallas_call | solution.py:44
  23.6 2.2 %collective-permute-start.8 = (bf16[1024,256]{1,0:T(8,128)(2,1)S(1)}, bf16[1024,256]{1,0:T(8,128)(2,1)S(1)}, u32[]{:S(2)}, u32[]{:S(2)}) collective-permute-start(bf16[1024,256]{1,0:T(8,128)(2,1)S(1)} %collective-permute-done.4.refs_4_), channel_id=1, source_target_pairs={{4,8},{8,4},{12,14},{14,12},{10,6},{6,10},{2,0},{0,2},{1,5},{5,1},... | collective-permute-start | bytes 1572872 | tf_op jit(solution)/shard_map/ppermute | solution.py:175
  26.5 1.8 %collective-permute-start.13 = (bf16[256,1024]{1,0:T(8,128)(2,1)S(1)}, bf16[256,1024]{1,0:T(8,128)(2,1)S(1)}, u32[]{:S(2)}, u32[]{:S(2)}) collective-permute-start(bf16[256,1024]{1,0:T(8,128)(2,1)S(1)} %collective-permute-done.9.rows), channel_id=1, source_target_pairs={{0,4},{4,0},{8,12},{12,8},{14,10},{10,14},{6,2},{2,6},{5,9},{9,5},... | collective-permute-start | bytes 1572872 | tf_op jit(solution)/shard_map/ppermute | solution.py:175
  28.9 4.3 %block.7 = (bf16[256,1024]{1,0:T(8,128)(2,1)S(1)}, bf16[256,512]{1,0:T(8,128)(2,1)S(1)}) custom-call(s32[3]{0:T(128)S(1)} %pad_add_fusion.place, bf16[256,1024]{1,0:T(8,128)(2,1)S(1)} %collective-permute-done.9.rows, bf16[1024,1024]{1,0:T(8,128)(2,1)S(1)} %copy-done, bf16[1024,1024]{1,0:T(8,128)(2,1)S(1)} %collective-permute-done.1.w_other, ...), custom_call_target="tpu_custom_call" | custom-call | flops 256000000 | bytes 8916992 | tf_op jit(solution)/shard_map/block/pallas_call | solution.py:44
  33.2 2.7 %collective-permute-done.8.refs_1_ = bf16[1024,256]{1,0:T(8,128)(2,1)S(1)} collective-permute-done((bf16[1024,256]{1,0:T(8,128)(2,1)S(1)}, bf16[1024,256]{1,0:T(8,128)(2,1)S(1)}, u32[]{:S(2)}, u32[]{:S(2)}) %collective-permute-start.8) | collective-permute-done | bytes 524320 | tf_op jit(solution)/shard_map/ppermute | solution.py:175
  36.0 2.4 %collective-permute-start.12 = (bf16[1024,256]{1,0:T(8,128)(2,1)S(1)}, bf16[1024,256]{1,0:T(8,128)(2,1)S(1)}, u32[]{:S(2)}, u32[]{:S(2)}) collective-permute-start(bf16[1024,256]{1,0:T(8,128)(2,1)S(1)} %collective-permute-done.8.refs_1_), channel_id=1, source_target_pairs={{0,4},{4,0},{8,12},{12,8},{14,10},{10,14},{6,2},{2,6},{5,9},{9,5},... | collective-permute-start | bytes 1572872 | tf_op jit(solution)/shard_map/ppermute | solution.py:175
  38.9 1.5 %begin.2.refs_0_ = f32[512,512]{1,0:T(8,128)S(1)} custom-call(s32[3]{0:T(128)S(1)} %pad_add_fusion.place, bf16[1024,256]{1,0:T(8,128)(2,1)S(1)} %constant_dynamic-update-slice_fusion.refs_0_.refs_2_, bf16[128,1024]{1,0:T(8,128)(2,1)S(1)} %get-tuple-element.30.refs_1_, bf16[1024,256]{1,0:T(8,128)(2,1)S(1)} %constant_dynamic-update-slice_fusion.refs_0_.refs_2_, ...), custom_call_target="tpu_custom_call" | custom-call | flops 200000000 | bytes 3407872 | tf_op jit(solution)/shard_map/begin/pallas_call | solution.py:44
  40.4 4.5 %block.8 = (bf16[256,1024]{1,0:T(8,128)(2,1)S(1)}, bf16[256,512]{1,0:T(8,128)(2,1)S(1)}) custom-call(s32[3]{0:T(128)S(1)} %pad_add_fusion.place, bf16[256,1024]{1,0:T(8,128)(2,1)S(1)} %collective-permute-done.13.rows, bf16[1024,1024]{1,0:T(8,128)(2,1)S(1)} %copy-done, bf16[1024,1024]{1,0:T(8,128)(2,1)S(1)} %collective-permute-done.1.w_other, ...), custom_call_target="tpu_custom_call" | custom-call | flops 256000000 | bytes 8916992 | tf_op jit(solution)/shard_map/block/pallas_call | solution.py:44
  45.8 1.8 %collective-permute-start.18 = (bf16[128,1024]{1,0:T(8,128)(2,1)S(1)}, bf16[128,1024]{1,0:T(8,128)(2,1)S(1)}, u32[]{:S(2)}, u32[]{:S(2)}) collective-permute-start(bf16[128,1024]{1,0:T(8,128)(2,1)S(1)} %slice.22), channel_id=1, source_target_pairs={{4,8},{8,4},{12,14},{14,12},{10,6},{6,10},{2,0},{0,2},{1,5},{5,1},... | collective-permute-start | bytes 786440 | tf_op jit(solution)/shard_map/ppermute | solution.py:175
  48.8 1.8 %begin.3.begun = f32[512,512]{1,0:T(8,128)S(1)} custom-call(s32[3]{0:T(128)S(1)} %pad_add_fusion.place, f32[512,512]{1,0:T(8,128)S(1)} %begin.2.refs_0_, bf16[1024,256]{1,0:T(8,128)(2,1)S(1)} %collective-permute-done.8.refs_1_, bf16[256,1024]{1,0:T(8,128)(2,1)S(1)} %get-tuple-element.35.refs_2_, bf16[512,256]{1,0:T(8,128)(2,1)S(1)} %collective-permute-done.10.refs_3_, ...), custom_call_target="tpu_custom_call" | custom-call | flops 200000000 | bytes 4718592 | tf_op jit(solution)/shard_map/begin/pallas_call | solution.py:44
  50.6 1.6 %collective-permute-done.18.rows = bf16[128,1024]{1,0:T(8,128)(2,1)S(1)} collective-permute-done((bf16[128,1024]{1,0:T(8,128)(2,1)S(1)}, bf16[128,1024]{1,0:T(8,128)(2,1)S(1)}, u32[]{:S(2)}, u32[]{:S(2)}) %collective-permute-start.18) | collective-permute-done | bytes 262176 | tf_op jit(solution)/shard_map/ppermute | solution.py:175
  52.2 3.3 %block.9 = (bf16[128,1024]{1,0:T(8,128)(2,1)S(1)}, bf16[128,512]{1,0:T(8,128)(2,1)S(1)}) custom-call(s32[3]{0:T(128)S(1)} %pad_add_fusion.place, bf16[128,1024]{1,0:T(8,128)(2,1)S(1)} %collective-permute-done.18.rows, bf16[1024,1024]{1,0:T(8,128)(2,1)S(1)} %copy-done, bf16[1024,1024]{1,0:T(8,128)(2,1)S(1)} %collective-permute-done.1.w_other, ...), custom_call_target="tpu_custom_call" | custom-call | flops 128000000 | bytes 8654848 | tf_op jit(solution)/shard_map/block/pallas_call | solution.py:44
  57.3 2.0 %update.1 = (f32[500,512]{1,0:T(8,128)}, bf16[512,512]{1,0:T(8,128)(2,1)S(1)}) custom-call(s32[3]{0:T(128)S(1)} %pad_add_fusion.place, f32[512,512]{1,0:T(8,128)S(1)} %begin.3.begun, f32[500,512]{1,0:T(8,128)S(1)} %bitcast.10, bf16[1024,128]{1,0:T(8,128)(2,1)S(1)} %collective-permute-done.17.refs_0_, bf16[128,1024]{1,0:T(8,128)(2,1)S(1)} %get-tuple-element.42.refs_1_, ...), custom_call_target="tpu_custom_call" | custom-call | flops 800000000 | bytes 2990080 | tf_op jit(solution)/shard_map/update/pallas_call | solution.py:44
  62.1 1.8 %collective-permute-start.26 = (bf16[512,128]{1,0:T(8,128)(2,1)S(1)}, bf16[512,128]{1,0:T(8,128)(2,1)S(1)}, u32[]{:S(2)}, u32[]{:S(2)}) collective-permute-start(bf16[512,128]{1,0:T(8,128)(2,1)S(1)} %far.3), channel_id=1, source_target_pairs={{4,8},{8,4},{12,14},{14,12},{10,6},{6,10},{2,0},{0,2},{1,5},{5,1},... | collective-permute-start | bytes 393224 | tf_op jit(solution)/shard_map/ppermute | solution.py:175
  63.9 3.2 %collective-permute-done.26.came = bf16[512,128]{1,0:T(8,128)(2,1)S(1)} collective-permute-done((bf16[512,128]{1,0:T(8,128)(2,1)S(1)}, bf16[512,128]{1,0:T(8,128)(2,1)S(1)}, u32[]{:S(2)}, u32[]{:S(2)}) %collective-permute-start.26) | collective-permute-done | bytes 131104 | tf_op jit(solution)/shard_map/ppermute | solution.py:175
  68.0 1.9 %collective-permute-start.27 = (bf16[512,256]{1,0:T(8,128)(2,1)S(1)}, bf16[512,256]{1,0:T(8,128)(2,1)S(1)}, u32[]{:S(2)}, u32[]{:S(2)}) collective-permute-start(bf16[512,256]{1,0:T(8,128)(2,1)S(1)} %hop.9), channel_id=1, source_target_pairs={{0,4},{4,0},{8,12},{12,8},{14,10},{10,14},{6,2},{2,6},{5,9},{9,5},... | collective-permute-start | bytes 786440 | tf_op jit(solution)/shard_map/ppermute | solution.py:175
  69.9 1.5 %collective-permute-start.21 = (bf16[512,128]{1,0:T(8,128)(2,1)S(1)}, bf16[512,128]{1,0:T(8,128)(2,1)S(1)}, u32[]{:S(2)}, u32[]{:S(2)}) collective-permute-start(bf16[512,128]{1,0:T(8,128)(2,1)S(1)} %far.2), channel_id=1, source_target_pairs={{4,8},{8,4},{12,14},{14,12},{10,6},{6,10},{2,0},{0,2},{1,5},{5,1},... | collective-permute-start | bytes 393224 | tf_op jit(solution)/shard_map/ppermute | solution.py:175
  71.4 3.5 %collective-permute-done.21.came = bf16[512,128]{1,0:T(8,128)(2,1)S(1)} collective-permute-done((bf16[512,128]{1,0:T(8,128)(2,1)S(1)}, bf16[512,128]{1,0:T(8,128)(2,1)S(1)}, u32[]{:S(2)}, u32[]{:S(2)}) %collective-permute-start.21) | collective-permute-done | bytes 131104 | tf_op jit(solution)/shard_map/ppermute | solution.py:175
  77.9 1.5 %collective-permute-start.28 = (bf16[512,256]{1,0:T(8,128)(2,1)S(1)}, bf16[512,256]{1,0:T(8,128)(2,1)S(1)}, u32[]{:S(2)}, u32[]{:S(2)}) collective-permute-start(bf16[512,256]{1,0:T(8,128)(2,1)S(1)} %hop.10), channel_id=1, source_target_pairs={{4,8},{8,4},{12,14},{14,12},{10,6},{6,10},{2,0},{0,2},{1,5},{5,1},... | collective-permute-start | bytes 786440 | tf_op jit(solution)/shard_map/ppermute | solution.py:175
  79.4 5.3 %collective-permute-done.22.came = bf16[512,256]{1,0:T(8,128)(2,1)S(1)} collective-permute-done((bf16[512,256]{1,0:T(8,128)(2,1)S(1)}, bf16[512,256]{1,0:T(8,128)(2,1)S(1)}, u32[]{:S(2)}, u32[]{:S(2)}) %collective-permute-start.22) | collective-permute-done | bytes 262176 | tf_op jit(solution)/shard_map/ppermute | solution.py:175
  85.7 1.7 %collective-permute-start.23 = (bf16[512,256]{1,0:T(8,128)(2,1)S(1)}, bf16[512,256]{1,0:T(8,128)(2,1)S(1)}, u32[]{:S(2)}, u32[]{:S(2)}) collective-permute-start(bf16[512,256]{1,0:T(8,128)(2,1)S(1)} %hop.7), channel_id=1, source_target_pairs={{4,8},{8,4},{12,14},{14,12},{10,6},{6,10},{2,0},{0,2},{1,5},{5,1},... | collective-permute-start | bytes 786440 | tf_op jit(solution)/shard_map/ppermute | solution.py:175
  88.3 1.7 %collective-permute-start.29 = (bf16[512,256]{1,0:T(8,128)(2,1)S(1)}, bf16[512,256]{1,0:T(8,128)(2,1)S(1)}, u32[]{:S(2)}, u32[]{:S(2)}) collective-permute-start(bf16[512,256]{1,0:T(8,128)(2,1)S(1)} %hop.11), channel_id=1, source_target_pairs={{0,4},{4,0},{8,12},{12,8},{14,10},{10,14},{6,2},{2,6},{5,9},{9,5},... | collective-permute-start | bytes 786440 | tf_op jit(solution)/shard_map/ppermute | solution.py:175
  90.0 4.9 %collective-permute-done.23.came = bf16[512,256]{1,0:T(8,128)(2,1)S(1)} collective-permute-done((bf16[512,256]{1,0:T(8,128)(2,1)S(1)}, bf16[512,256]{1,0:T(8,128)(2,1)S(1)}, u32[]{:S(2)}, u32[]{:S(2)}) %collective-permute-start.23) | collective-permute-done | bytes 262176 | tf_op jit(solution)/shard_map/ppermute | solution.py:175
  95.8 1.4 %collective-permute-start.24 = (bf16[512,256]{1,0:T(8,128)(2,1)S(1)}, bf16[512,256]{1,0:T(8,128)(2,1)S(1)}, u32[]{:S(2)}, u32[]{:S(2)}) collective-permute-start(bf16[512,256]{1,0:T(8,128)(2,1)S(1)} %hop.8), channel_id=1, source_target_pairs={{0,4},{4,0},{8,12},{12,8},{14,10},{10,14},{6,2},{2,6},{5,9},{9,5},... | collective-permute-start | bytes 786440 | tf_op jit(solution)/shard_map/ppermute | solution.py:175
  97.1 5.1 %collective-permute-done.24.came = bf16[512,256]{1,0:T(8,128)(2,1)S(1)} collective-permute-done((bf16[512,256]{1,0:T(8,128)(2,1)S(1)}, bf16[512,256]{1,0:T(8,128)(2,1)S(1)}, u32[]{:S(2)}, u32[]{:S(2)}) %collective-permute-start.24) | collective-permute-done | bytes 262176 | tf_op jit(solution)/shard_map/ppermute | solution.py:175
  103.1 1.8 %collective-permute-start.31 = (bf16[512,256]{1,0:T(8,128)(2,1)S(1)}, bf16[512,256]{1,0:T(8,128)(2,1)S(1)}, u32[]{:S(2)}, u32[]{:S(2)}) collective-permute-start(bf16[512,256]{1,0:T(8,128)(2,1)S(1)} %last.1.own), channel_id=1, source_target_pairs={{0,2},{2,0},{1,3},{3,1},{4,6},{6,4},{5,7},{7,5},{8,10},{10,8},{9,1... | collective-permute-start | bytes 786440 | tf_op jit(solution)/shard_map/ppermute | solution.py:175
  104.9 4.6 %collective-permute-done.31.other = bf16[512,256]{1,0:T(8,128)(2,1)S(1)} collective-permute-done((bf16[512,256]{1,0:T(8,128)(2,1)S(1)}, bf16[512,256]{1,0:T(8,128)(2,1)S(1)}, u32[]{:S(2)}, u32[]{:S(2)}) %collective-permute-start.31) | collective-permute-done | bytes 262176 | tf_op jit(solution)/shard_map/ppermute | solution.py:175
  109.5 1.7 %apply.1 = f32[500,512]{1,0:T(8,128)} custom-call(s32[3]{0:T(128)S(1)} %pad_add_fusion.place, f32[500,512]{1,0:T(8,128)S(1)} %bitcast.12, bf16[512,256]{1,0:T(8,128)(2,1)S(1)} %last.1.own, bf16[512,256]{1,0:T(8,128)(2,1)S(1)} %collective-permute-done.31.other), custom_call_target="tpu_custom_call" | custom-call | flops 100000000 | bytes 1548288 | tf_op jit(solution)/shard_map/apply/pallas_call | solution.py:44
  (79 shorter events, 23.6 us)
Async XLA Ops:
  0.6 12.0 %collective-permute-start.1 = (bf16[1024,1024]{1,0:T(8,128)(2,1)}, bf16[1024,1024]{1,0:T(8,128)(2,1)S(1)}, u32[]{:S(2)}, u32[]{:S(2)}) collective-permute-start(bf16[1024,1024]{1,0:T(8,128)(2,1)} %w_own.9), channel_id=1, source_target_pairs={{0,1},{1,0},{2,3},{3,2},{4,5},{5,4},{6,7},{7,6},{8,9},{9,8},{10,11... | collective-permute-start | bytes 6291464 | tf_op jit(solution)/shard_map/ppermute | solution.py:175
  3.8 5.0 %collective-permute-start = (bf16[512,256]{1,0:T(8,128)(2,1)S(1)}, bf16[512,256]{1,0:T(8,128)(2,1)S(1)}, u32[]{:S(2)}, u32[]{:S(2)}) collective-permute-start(bf16[512,256]{1,0:T(8,128)(2,1)S(1)} %get-tuple-element.27), channel_id=1, source_target_pairs={{0,1},{1,0},{2,3},{3,2},{4,5},{5,4},{6,7},{7,6},{8,9},{9,8},{10,11... | collective-permute-start | bytes 786440 | tf_op jit(solution)/shard_map/ppermute | solution.py:175
  5.7 10.4 %collective-permute-start.5 = (bf16[256,1024]{1,0:T(8,128)(2,1)S(1)}, bf16[256,1024]{1,0:T(8,128)(2,1)S(1)}, u32[]{:S(2)}, u32[]{:S(2)}) collective-permute-start(bf16[256,1024]{1,0:T(8,128)(2,1)S(1)} %inputs.2.rows), channel_id=1, source_target_pairs={{0,4},{4,0},{8,12},{12,8},{14,10},{10,14},{6,2},{2,6},{5,9},{9,5},... | collective-permute-start | bytes 1572872 | tf_op jit(solution)/shard_map/ppermute | solution.py:175
  8.9 14.7 %collective-permute-start.4 = (bf16[1024,256]{1,0:T(8,128)(2,1)S(1)}, bf16[1024,256]{1,0:T(8,128)(2,1)S(1)}, u32[]{:S(2)}, u32[]{:S(2)}) collective-permute-start(bf16[1024,256]{1,0:T(8,128)(2,1)S(1)} %constant_dynamic-update-slice_fusion.refs_0_.refs_2_), channel_id=1, source_target_pairs={{0,4},{4,0},{8,12},{12,8},{14,10},{10,14},{6,2},{2,6},{5,9},{9,5},... | collective-permute-start | bytes 1572872 | tf_op jit(solution)/shard_map/ppermute | solution.py:175
  9.0 3.6 %collective-permute-start.2 = (bf16[1,1024]{1,0:T(2,128)(2,1)S(1)}, bf16[1,1024]{1,0:T(2,128)(2,1)S(1)}, u32[]{:S(2)}, u32[]{:S(2)}) collective-permute-start(bf16[1,1024]{1,0:T(2,128)(2,1)S(1)} %broadcast_in_dim.7.p_own), channel_id=1, source_target_pairs={{0,1},{1,0},{2,3},{3,2},{4,5},{5,4},{6,7},{7,6},{8,9},{9,8},{10,11... | collective-permute-start | bytes 6152 | tf_op jit(solution)/shard_map/ppermute | solution.py:175
  16.2 10.3 %collective-permute-start.9 = (bf16[256,1024]{1,0:T(8,128)(2,1)S(1)}, bf16[256,1024]{1,0:T(8,128)(2,1)S(1)}, u32[]{:S(2)}, u32[]{:S(2)}) collective-permute-start(bf16[256,1024]{1,0:T(8,128)(2,1)S(1)} %collective-permute-done.5.rows), channel_id=1, source_target_pairs={{4,8},{8,4},{12,14},{14,12},{10,6},{6,10},{2,0},{0,2},{1,5},{5,1},... | collective-permute-start | bytes 1572872 | tf_op jit(solution)/shard_map/ppermute | solution.py:175
  23.6 12.4 %collective-permute-start.8 = (bf16[1024,256]{1,0:T(8,128)(2,1)S(1)}, bf16[1024,256]{1,0:T(8,128)(2,1)S(1)}, u32[]{:S(2)}, u32[]{:S(2)}) collective-permute-start(bf16[1024,256]{1,0:T(8,128)(2,1)S(1)} %collective-permute-done.4.refs_4_), channel_id=1, source_target_pairs={{4,8},{8,4},{12,14},{14,12},{10,6},{6,10},{2,0},{0,2},{1,5},{5,1},... | collective-permute-start | bytes 1572872 | tf_op jit(solution)/shard_map/ppermute | solution.py:175
  25.8 13.1 %collective-permute-start.7 = (bf16[256,1024]{1,0:T(8,128)(2,1)S(1)}, bf16[256,1024]{1,0:T(8,128)(2,1)S(1)}, u32[]{:S(2)}, u32[]{:S(2)}) collective-permute-start(bf16[256,1024]{1,0:T(8,128)(2,1)S(1)} %get-tuple-element.32.refs_5_), channel_id=1, source_target_pairs={{0,1},{1,0},{2,3},{3,2},{4,5},{5,4},{6,7},{7,6},{8,9},{9,8},{10,11... | collective-permute-start | bytes 1572872 | tf_op jit(solution)/shard_map/ppermute | solution.py:175
  26.5 14.0 %collective-permute-start.13 = (bf16[256,1024]{1,0:T(8,128)(2,1)S(1)}, bf16[256,1024]{1,0:T(8,128)(2,1)S(1)}, u32[]{:S(2)}, u32[]{:S(2)}) collective-permute-start(bf16[256,1024]{1,0:T(8,128)(2,1)S(1)} %collective-permute-done.9.rows), channel_id=1, source_target_pairs={{0,4},{4,0},{8,12},{12,8},{14,10},{10,14},{6,2},{2,6},{5,9},{9,5},... | collective-permute-start | bytes 1572872 | tf_op jit(solution)/shard_map/ppermute | solution.py:175
  28.3 10.1 %collective-permute-start.6 = (bf16[512,256]{1,0:T(8,128)(2,1)S(1)}, bf16[512,256]{1,0:T(8,128)(2,1)S(1)}, u32[]{:S(2)}, u32[]{:S(2)}) collective-permute-start(bf16[512,256]{1,0:T(8,128)(2,1)S(1)} %slice.18), channel_id=1, source_target_pairs={{0,1},{1,0},{2,3},{3,2},{4,5},{5,4},{6,7},{7,6},{8,9},{9,8},{10,11... | collective-permute-start | bytes 786440 | tf_op jit(solution)/shard_map/ppermute | solution.py:175
  28.8 9.6 %collective-permute-start.3 = (bf16[128,1024]{1,0:T(8,128)(2,1)S(1)}, bf16[128,1024]{1,0:T(8,128)(2,1)S(1)}, u32[]{:S(2)}, u32[]{:S(2)}) collective-permute-start(bf16[128,1024]{1,0:T(8,128)(2,1)S(1)} %get-tuple-element.30.refs_1_), channel_id=1, source_target_pairs={{0,1},{1,0},{2,3},{3,2},{4,5},{5,4},{6,7},{7,6},{8,9},{9,8},{10,11... | collective-permute-start | bytes 786440 | tf_op jit(solution)/shard_map/ppermute | solution.py:175
  36.0 9.6 %collective-permute-start.12 = (bf16[1024,256]{1,0:T(8,128)(2,1)S(1)}, bf16[1024,256]{1,0:T(8,128)(2,1)S(1)}, u32[]{:S(2)}, u32[]{:S(2)}) collective-permute-start(bf16[1024,256]{1,0:T(8,128)(2,1)S(1)} %collective-permute-done.8.refs_1_), channel_id=1, source_target_pairs={{0,4},{4,0},{8,12},{12,8},{14,10},{10,14},{6,2},{2,6},{5,9},{9,5},... | collective-permute-start | bytes 1572872 | tf_op jit(solution)/shard_map/ppermute | solution.py:175
  38.4 2.0 %collective-permute-start.14 = (bf16[128,512]{1,0:T(8,128)(2,1)S(1)}, bf16[128,512]{1,0:T(8,128)(2,1)S(1)}, u32[]{:S(2)}, u32[]{:S(2)}) collective-permute-start(bf16[128,512]{1,0:T(8,128)(2,1)S(1)} %get-tuple-element.37.mine), channel_id=1, source_target_pairs={{0,1},{1,0},{2,3},{3,2},{4,5},{5,4},{6,7},{7,6},{8,9},{9,8},{10,11... | collective-permute-start | bytes 393224 | tf_op jit(solution)/shard_map/ppermute | solution.py:175
  38.4 10.4 %collective-permute-start.11 = (bf16[256,1024]{1,0:T(8,128)(2,1)S(1)}, bf16[256,1024]{1,0:T(8,128)(2,1)S(1)}, u32[]{:S(2)}, u32[]{:S(2)}) collective-permute-start(bf16[256,1024]{1,0:T(8,128)(2,1)S(1)} %get-tuple-element.35.refs_2_), channel_id=1, source_target_pairs={{0,1},{1,0},{2,3},{3,2},{4,5},{5,4},{6,7},{7,6},{8,9},{9,8},{10,11... | collective-permute-start | bytes 1572872 | tf_op jit(solution)/shard_map/ppermute | solution.py:175
  45.0 3.9 %collective-permute-start.16 = (bf16[256,1024]{1,0:T(8,128)(2,1)S(1)}, bf16[256,1024]{1,0:T(8,128)(2,1)S(1)}, u32[]{:S(2)}, u32[]{:S(2)}) collective-permute-start(bf16[256,1024]{1,0:T(8,128)(2,1)S(1)} %get-tuple-element.39.refs_6_), channel_id=1, source_target_pairs={{0,1},{1,0},{2,3},{3,2},{4,5},{5,4},{6,7},{7,6},{8,9},{9,8},{10,11... | collective-permute-start | bytes 1572872 | tf_op jit(solution)/shard_map/ppermute | solution.py:175
  45.1 2.6 %collective-permute-start.10 = (bf16[512,256]{1,0:T(8,128)(2,1)S(1)}, bf16[512,256]{1,0:T(8,128)(2,1)S(1)}, u32[]{:S(2)}, u32[]{:S(2)}) collective-permute-start(bf16[512,256]{1,0:T(8,128)(2,1)S(1)} %slice.19), channel_id=1, source_target_pairs={{0,1},{1,0},{2,3},{3,2},{4,5},{5,4},{6,7},{7,6},{8,9},{9,8},{10,11... | collective-permute-start | bytes 786440 | tf_op jit(solution)/shard_map/ppermute | solution.py:175
  45.6 3.2 %collective-permute-start.15 = (bf16[512,256]{1,0:T(8,128)(2,1)S(1)}, bf16[512,256]{1,0:T(8,128)(2,1)S(1)}, u32[]{:S(2)}, u32[]{:S(2)}) collective-permute-start(bf16[512,256]{1,0:T(8,128)(2,1)S(1)} %slice.20), channel_id=1, source_target_pairs={{0,1},{1,0},{2,3},{3,2},{4,5},{5,4},{6,7},{7,6},{8,9},{9,8},{10,11... | collective-permute-start | bytes 786440 | tf_op jit(solution)/shard_map/ppermute | solution.py:175
  45.8 6.4 %collective-permute-start.18 = (bf16[128,1024]{1,0:T(8,128)(2,1)S(1)}, bf16[128,1024]{1,0:T(8,128)(2,1)S(1)}, u32[]{:S(2)}, u32[]{:S(2)}) collective-permute-start(bf16[128,1024]{1,0:T(8,128)(2,1)S(1)} %slice.22), channel_id=1, source_target_pairs={{4,8},{8,4},{12,14},{14,12},{10,6},{6,10},{2,0},{0,2},{1,5},{5,1},... | collective-permute-start | bytes 786440 | tf_op jit(solution)/shard_map/ppermute | solution.py:175
  47.7 7.9 %collective-permute-start.17 = (bf16[1024,128]{1,0:T(8,128)(2,1)S(1)}, bf16[1024,128]{1,0:T(8,128)(2,1)S(1)}, u32[]{:S(2)}, u32[]{:S(2)}) collective-permute-start(bf16[1024,128]{1,0:T(8,128)(2,1)S(1)} %slice.21), channel_id=1, source_target_pairs={{4,8},{8,4},{12,14},{14,12},{10,6},{6,10},{2,0},{0,2},{1,5},{5,1},... | collective-permute-start | bytes 786440 | tf_op jit(solution)/shard_map/ppermute | solution.py:175
  55.6 1.8 %collective-permute-start.20 = (bf16[128,1024]{1,0:T(8,128)(2,1)S(1)}, bf16[128,1024]{1,0:T(8,128)(2,1)S(1)}, u32[]{:S(2)}, u32[]{:S(2)}) collective-permute-start(bf16[128,1024]{1,0:T(8,128)(2,1)S(1)} %get-tuple-element.42.refs_1_), channel_id=1, source_target_pairs={{0,1},{1,0},{2,3},{3,2},{4,5},{5,4},{6,7},{7,6},{8,9},{9,8},{10,11... | collective-permute-start | bytes 786440 | tf_op jit(solution)/shard_map/ppermute | solution.py:175
  55.7 1.7 %collective-permute-start.19 = (bf16[512,128]{1,0:T(8,128)(2,1)S(1)}, bf16[512,128]{1,0:T(8,128)(2,1)S(1)}, u32[]{:S(2)}, u32[]{:S(2)}) collective-permute-start(bf16[512,128]{1,0:T(8,128)(2,1)S(1)} %slice.24), channel_id=1, source_target_pairs={{0,1},{1,0},{2,3},{3,2},{4,5},{5,4},{6,7},{7,6},{8,9},{9,8},{10,11... | collective-permute-start | bytes 393224 | tf_op jit(solution)/shard_map/ppermute | solution.py:175
  59.3 1.9 %collective-permute-start.25 = (bf16[512,512]{1,0:T(8,128)(2,1)S(1)}, bf16[512,512]{1,0:T(8,128)(2,1)S(1)}, u32[]{:S(2)}, u32[]{:S(2)}) collective-permute-start(bf16[512,512]{1,0:T(8,128)(2,1)S(1)} %get-tuple-element.44.sent), channel_id=1, source_target_pairs={{0,1},{1,0},{2,3},{3,2},{4,5},{5,4},{6,7},{7,6},{8,9},{9,8},{10,11... | collective-permute-start | bytes 1572872 | tf_op jit(solution)/shard_map/ppermute | solution.py:175
  62.1 5.0 %collective-permute-start.26 = (bf16[512,128]{1,0:T(8,128)(2,1)S(1)}, bf16[512,128]{1,0:T(8,128)(2,1)S(1)}, u32[]{:S(2)}, u32[]{:S(2)}) collective-permute-start(bf16[512,128]{1,0:T(8,128)(2,1)S(1)} %far.3), channel_id=1, source_target_pairs={{4,8},{8,4},{12,14},{14,12},{10,6},{6,10},{2,0},{0,2},{1,5},{5,1},... | collective-permute-start | bytes 393224 | tf_op jit(solution)/shard_map/ppermute | solution.py:175
  68.0 9.1 %collective-permute-start.27 = (bf16[512,256]{1,0:T(8,128)(2,1)S(1)}, bf16[512,256]{1,0:T(8,128)(2,1)S(1)}, u32[]{:S(2)}, u32[]{:S(2)}) collective-permute-start(bf16[512,256]{1,0:T(8,128)(2,1)S(1)} %hop.9), channel_id=1, source_target_pairs={{0,4},{4,0},{8,12},{12,8},{14,10},{10,14},{6,2},{2,6},{5,9},{9,5},... | collective-permute-start | bytes 786440 | tf_op jit(solution)/shard_map/ppermute | solution.py:175
  69.9 5.0 %collective-permute-start.21 = (bf16[512,128]{1,0:T(8,128)(2,1)S(1)}, bf16[512,128]{1,0:T(8,128)(2,1)S(1)}, u32[]{:S(2)}, u32[]{:S(2)}) collective-permute-start(bf16[512,128]{1,0:T(8,128)(2,1)S(1)} %far.2), channel_id=1, source_target_pairs={{4,8},{8,4},{12,14},{14,12},{10,6},{6,10},{2,0},{0,2},{1,5},{5,1},... | collective-permute-start | bytes 393224 | tf_op jit(solution)/shard_map/ppermute | solution.py:175
  75.7 9.0 %collective-permute-start.22 = (bf16[512,256]{1,0:T(8,128)(2,1)S(1)}, bf16[512,256]{1,0:T(8,128)(2,1)S(1)}, u32[]{:S(2)}, u32[]{:S(2)}) collective-permute-start(bf16[512,256]{1,0:T(8,128)(2,1)S(1)} %hop.6), channel_id=1, source_target_pairs={{0,4},{4,0},{8,12},{12,8},{14,10},{10,14},{6,2},{2,6},{5,9},{9,5},... | collective-permute-start | bytes 786440 | tf_op jit(solution)/shard_map/ppermute | solution.py:175
  77.9 9.5 %collective-permute-start.28 = (bf16[512,256]{1,0:T(8,128)(2,1)S(1)}, bf16[512,256]{1,0:T(8,128)(2,1)S(1)}, u32[]{:S(2)}, u32[]{:S(2)}) collective-permute-start(bf16[512,256]{1,0:T(8,128)(2,1)S(1)} %hop.10), channel_id=1, source_target_pairs={{4,8},{8,4},{12,14},{14,12},{10,6},{6,10},{2,0},{0,2},{1,5},{5,1},... | collective-permute-start | bytes 786440 | tf_op jit(solution)/shard_map/ppermute | solution.py:175
  85.7 9.2 %collective-permute-start.23 = (bf16[512,256]{1,0:T(8,128)(2,1)S(1)}, bf16[512,256]{1,0:T(8,128)(2,1)S(1)}, u32[]{:S(2)}, u32[]{:S(2)}) collective-permute-start(bf16[512,256]{1,0:T(8,128)(2,1)S(1)} %hop.7), channel_id=1, source_target_pairs={{4,8},{8,4},{12,14},{14,12},{10,6},{6,10},{2,0},{0,2},{1,5},{5,1},... | collective-permute-start | bytes 786440 | tf_op jit(solution)/shard_map/ppermute | solution.py:175
  88.3 8.8 %collective-permute-start.29 = (bf16[512,256]{1,0:T(8,128)(2,1)S(1)}, bf16[512,256]{1,0:T(8,128)(2,1)S(1)}, u32[]{:S(2)}, u32[]{:S(2)}) collective-permute-start(bf16[512,256]{1,0:T(8,128)(2,1)S(1)} %hop.11), channel_id=1, source_target_pairs={{0,4},{4,0},{8,12},{12,8},{14,10},{10,14},{6,2},{2,6},{5,9},{9,5},... | collective-permute-start | bytes 786440 | tf_op jit(solution)/shard_map/ppermute | solution.py:175
  95.8 6.4 %collective-permute-start.24 = (bf16[512,256]{1,0:T(8,128)(2,1)S(1)}, bf16[512,256]{1,0:T(8,128)(2,1)S(1)}, u32[]{:S(2)}, u32[]{:S(2)}) collective-permute-start(bf16[512,256]{1,0:T(8,128)(2,1)S(1)} %hop.8), channel_id=1, source_target_pairs={{0,4},{4,0},{8,12},{12,8},{14,10},{10,14},{6,2},{2,6},{5,9},{9,5},... | collective-permute-start | bytes 786440 | tf_op jit(solution)/shard_map/ppermute | solution.py:175
  97.1 5.1 %collective-permute-start.30 = (bf16[512,256]{1,0:T(8,128)(2,1)S(1)}, bf16[512,256]{1,0:T(8,128)(2,1)S(1)}, u32[]{:S(2)}, u32[]{:S(2)}) collective-permute-start(bf16[512,256]{1,0:T(8,128)(2,1)S(1)} %collective-permute-done.29), channel_id=1, source_target_pairs={{0,1},{1,0},{2,3},{3,2},{4,5},{5,4},{6,7},{7,6},{8,9},{9,8},{10,11... | collective-permute-start | bytes 786440 | tf_op jit(solution)/shard_map/ppermute | solution.py:175
  103.1 6.4 %collective-permute-start.31 = (bf16[512,256]{1,0:T(8,128)(2,1)S(1)}, bf16[512,256]{1,0:T(8,128)(2,1)S(1)}, u32[]{:S(2)}, u32[]{:S(2)}) collective-permute-start(bf16[512,256]{1,0:T(8,128)(2,1)S(1)} %last.1.own), channel_id=1, source_target_pairs={{0,2},{2,0},{1,3},{3,1},{4,6},{6,4},{5,7},{7,5},{8,10},{10,8},{9,1... | collective-permute-start | bytes 786440 | tf_op jit(solution)/shard_map/ppermute | solution.py:175
  (8 other events, 44.1 us)

commit v7 on v6

--- a/solution.py
+++ b/solution.py
@@ -11,23 +11,20 @@
 F32, BF16 = jnp.float32, jnp.bfloat16
 LANES = 128
 
-COS_TERMS = (
-    0.9999999887556631, -0.49999988843399, 0.04166648574334225, -0.001388778673619495,
-    2.4769518189949842e-05, -2.7075418374484127e-07, 1.7231808612122658e-09,
+SINE_TERMS = (
+    6.283185280127733, -41.341680582549685, 81.60247253767959, -76.5810396203459, 39.75848375303386
 )
-INV_TWO_PI = 0.15915494309189535
-TWO_PI_HIGH = 6.28125
-TWO_PI_LOW = 0.0019353071795864769
-
-
-def cosine(angles):
-    turns = jnp.round(angles * INV_TWO_PI)
-    rest = (angles - turns * TWO_PI_HIGH) - turns * TWO_PI_LOW
-    square = rest * rest
-    result = jnp.full_like(square, COS_TERMS[-1])
-    for term in COS_TERMS[-2::-1]:
+TURNS = 0.15915494309189535
+
+
+def cosine(angles, phases):
+    turns = angles * TURNS + phases.astype(F32) * TURNS
+    quarter = 0.25 - jnp.abs(turns - jnp.round(turns))
+    square = quarter * quarter
+    result = square * SINE_TERMS[-1] + SINE_TERMS[-2]
+    for term in SINE_TERMS[-3::-1]:
         result = result * square + term
-    return result
+    return result * quarter
 
 
 def dot(a, b):
@@ -38,18 +35,17 @@
     return lax.dot_general(a, b, (((1,), (1,)), ((), ())), preferred_element_type=F32)
 
 
-def call(kernel, out_shapes, place, args, name, vmem_mib, mflops, scratch=()):
-    vmem = pl.BlockSpec(memory_space=pltpu.VMEM)
+def call(kernel, out_shapes, place, args, name, vmem_mib, scratch=(), in_place=None, out_place=pltpu.VMEM, aliases={}):
+    spaces = in_place or (pltpu.VMEM,) * len(args)
+    vmem = pl.BlockSpec(memory_space=out_place)
     single = isinstance(out_shapes, jax.ShapeDtypeStruct)
     return pl.pallas_call(
         kernel,
         out_shape=out_shapes,
-        in_specs=[pl.BlockSpec(memory_space=pltpu.SMEM)] + [vmem] * len(args),
+        in_specs=[pl.BlockSpec(memory_space=m) for m in (pltpu.SMEM, *spaces)],
         out_specs=vmem if single else (vmem,) * len(out_shapes),
         scratch_shapes=scratch,
-        cost_estimate=pl.CostEstimate(
-            flops=mflops * 10**6, transcendentals=0, bytes_accessed=sum(a.size * a.dtype.itemsize for a in args)
-        ),
+        input_output_aliases=aliases,
         compiler_params=pltpu.CompilerParams(vmem_limit_bytes=vmem_mib << 20),
         name=name,
     )(place, *args)
@@ -63,24 +59,32 @@
     return pl.ds(pl.multiple_of(index * size, size), size)
 
 
-def inputs_kernel(place, inputs, out):
-    part = out.shape[0] // 2
-    for j in (0, 1):
-        start = pl.multiple_of((2 * place[1] + (place[2] ^ j)) * part, part)
-        out[j * part:(j + 1) * part] = inputs[pl.ds(start, part)]
-
-
-def residual_kernel(place, labels, predictions, own, given):
+def prepare_kernel(place, inputs, labels, predictions, rows, own, given, wide, tags, sems):
     width = predictions.shape[0]
     part = own.shape[1] // 2
+    copies = []
+    for j in (0, 1):
+        block = 2 * place[1] + (place[2] ^ j)
+        at, there = lanes(block, part), slice(j * part, (j + 1) * part)
+        copies += [
+            pltpu.make_async_copy(predictions.at[:, at], wide.at[:, there], sems.at[3 * j]),
+            pltpu.make_async_copy(labels.at[:, at], tags.at[:, there], sems.at[3 * j + 1]),
+            pltpu.make_async_copy(inputs.at[at], rows.at[there], sems.at[3 * j + 2]),
+        ]
+    for copy in copies:
+        copy.start()
     tail = own.shape[0] - width
     own[width:], given[width:] = (jnp.zeros((tail, 2 * part), BF16),) * 2
     for j in (0, 1):
-        at = lanes(2 * place[1] + (place[2] ^ j), part)
+        copies[3 * j].wait()
+        copies[3 * j + 1].wait()
+        there = slice(j * part, (j + 1) * part)
         classes = lax.broadcasted_iota(jnp.int32, (width, part), 0) + place[2] * width
-        residual = ((classes == labels[:, at]).astype(F32) - predictions[:, at]).astype(BF16)
-        own[:width, j * part:(j + 1) * part] = residual
+        residual = ((classes == tags[:, there]).astype(F32) - wide[:, there]).astype(BF16)
+        own[:width, there] = residual
         given[:width, (1 - j) * part:(2 - j) * part] = residual
+    for j in (0, 1):
+        copies[3 * j + 2].wait()
 
 
 def high_low(x):
@@ -102,8 +106,7 @@
     for i, (weights, phases) in enumerate(((w_own, p_own), (w_other, p_other))):
         for k in range(0, half, TILE):
             at = pl.ds(pl.multiple_of((place[2] ^ i) * half + k, TILE), TILE)
-            angles = dot(inputs, weights[:, k:k + TILE]) + phases[:, k:k + TILE].astype(F32)
-            tile = cosine(angles).astype(BF16)
+            tile = cosine(dot(inputs, weights[:, k:k + TILE]), phases[:, k:k + TILE]).astype(BF16)
             feats[:, at] = tile
             product = dot_nt(tile, high[:, at]) + dot_nt(tile, low[:, at])
             total = product if total is None else total + product
@@ -136,11 +139,11 @@
     out[...] = pieces[0][...] + total if earlier else total
 
 
-def update_kernel(place, begun, coefficients, *refs):
-    *pieces, new, sent = refs
-    update = DAMPING * (begun[...] + product_of(pieces, begun.shape[0]))
-    new[...] = coefficients[...] + update[:new.shape[0]]
-    sent[...] = update.astype(BF16)
+def update_kernel(place, begun, *refs):
+    *pieces, update, sent = refs
+    total = DAMPING * (begun[...] + product_of(pieces, begun.shape[0]))
+    update[...] = total
+    sent[...] = total.astype(BF16)
 
 
 def far_kernel(place, sent, feats, out):
@@ -163,12 +166,17 @@
         out[:, at] = (total[:, at] + given[:, there].astype(F32)).astype(BF16)
 
 
-def apply_kernel(place, predictions, own, other, new):
-    width, part = new.shape[0], own.shape[1] // 2
-    for i, source in enumerate((own, other)):
-        for j in (0, 1):
-            at = lanes(2 * (place[1] ^ i) + (place[2] ^ j), part)
-            new[:, at] = predictions[:, at] + source[:width, j * part:(j + 1) * part].astype(F32)
+def apply_kernel(which, place, predictions, change, *refs):
+    new, total, sems = refs[-3:]
+    width, part = total.shape[0], total.shape[1] // 2
+    copies = []
+    for j in (0, 1):
+        at, there = lanes(2 * (place[1] ^ which) + (place[2] ^ j), part), slice(j * part, (j + 1) * part)
+        total[:, there] = predictions[:, at] + change[:width, there].astype(F32)
+        copies.append(pltpu.make_async_copy(total.at[:, there], new.at[:, at], sems.at[j]))
+        copies[j].start()
+    for copy in copies:
+        copy.wait()
 
 
 def swap(x, axes, pairs):
@@ -197,29 +205,35 @@
     predictions, coefficients = predictions.T, coefficients.T
     depth = coefficients.shape[1]
 
-    x0 = call(inputs_kernel, like((2 * part, inputs.shape[1])), place, (inputs,), "inputs", 6, 100)
-    own, given = call(
-        residual_kernel, (like((padded, 2 * part)),) * 2, place, (labels[None, :], predictions), "residual", 6, 300
-    )
-    r0 = jnp.concatenate([own, C(given)], axis=0)
+    dma = pltpu.SemaphoreType.DMA
+    block_rows = like((2 * part, inputs.shape[1]))
+    x0, own, given = call(
+        prepare_kernel, (block_rows, *(like((padded, 2 * part)),) * 2), place,
+        tuple(pltpu.with_memory_space_constraint(a, pltpu.HBM) for a in (inputs, labels[None, :], predictions)),
+        "prepare", 6,
+        (pltpu.VMEM((width, 2 * part), F32), pltpu.VMEM((1, 2 * part), jnp.int32), dma((6,))), (pltpu.HBM,) * 3,
+    )
+    given = C(given)
+    (x0,) = after((x0,), given)
+    r0 = jnp.concatenate([own, given], axis=0)
     weights = (projection, C(projection))
     phases = phases[None, :]
     phases = (phases, C(phases))
     inverse = call(
-        split_kernel, (like(inverse_blocks.shape[1:]),) * 2, place, (inverse_blocks[0],), "split", 14, 500
+        split_kernel, (like(inverse_blocks.shape[1:]),) * 2, place, (inverse_blocks[0],), "split", 14
     )
 
     def block(rows, size):
         scratch = (pltpu.VMEM((size, 2 * projection.shape[1]), BF16),)
         return call(
             block_kernel, (like((size, 2 * depth)), like((size, depth))), place,
-            (rows, *weights, *phases, *inverse), "block", 16, size, scratch,
+            (rows, *weights, *phases, *inverse), "block", 16, scratch,
         )
 
     def begin(pairs, *earlier):
         return call(
             functools.partial(begin_kernel, len(earlier)), like((padded, depth), F32), place,
-            (*earlier, *[a for pair in pairs for a in pair]), "begin", 14, 200,
+            (*earlier, *[a for pair in pairs for a in pair]), "begin", 14,
         )
 
     x1, r1 = S(x0), S(r0)
@@ -245,24 +259,35 @@
     begun = begin([(r2, q2), (theirs(r2), C(q2)), (r3, q3), (theirs(r3), C(q3))], begun)
     (x4,) = after((x4,), begun)
     q4, f4 = block(x4, part)
-    new_coefficients, sent = call(
-        update_kernel, (like(coefficients.shape, F32), like((padded, depth))), place,
-        (begun, coefficients, r4, q4, theirs(r4), C(q4)), "update", 14, 800,
+    update, sent = call(
+        update_kernel, (like((padded, depth), F32), like((padded, depth))), place,
+        (begun, r4, q4, theirs(r4), C(q4)), "update", 14,
     )
 
     piece, whole = like((padded, part)), like((padded, 2 * part))
-    far = lambda u: call(far_kernel, piece, place, (u, f4), "far", 6, 70)
+    far = lambda u: call(far_kernel, piece, place, (u, f4), "far", 6)
+    hop = lambda u, feats, came: call(hop_kernel, whole, place, (u, feats, came), "hop", 6)
     first = far(sent)
-    updates = (sent, *after((C(sent),), first))
-    moving = [T(first), T(far(updates[1]))]
+    sent_other, first = after((C(sent), first), first)
+    first, second = T(first), T(far(sent_other))
+    (second,) = after((second,), first)
     for way, feats in ((S, f3), (T, f2), (S, f1)):
-        moving = [
-            way(call(hop_kernel, whole, place, (u, feats, m), "hop", 6, 150)) for u, m in zip(updates, moving)
-        ]
-    own = call(last_kernel, whole, place, (sent, f0, f0_other, moving[0], C(moving[1])), "last", 6, 150)
-    other = swap(own, "blocks", [(0, 1)])
-    new = call(apply_kernel, like(predictions.shape, F32), place, (predictions, own, other), "apply", 6, 100)
-    return new_coefficients.T, new.T
+        second_sum = hop(sent_other, feats, second)
+        (first,) = after((first,), second_sum)
+        first_sum = hop(sent, feats, first)
+        second, first = way(second_sum), way(first_sum)
+        (second,) = after((second,), first_sum)
+    own = call(last_kernel, whole, place, (sent, f0, f0_other, first, C(second)), "last", 6)
+    new = None
+    for i in (0, 1):
+        change = swap(own, "blocks", [(0, 1)]) if i else own
+        earlier = (new,) if i else ()
+        new = call(
+            functools.partial(apply_kernel, i), like(predictions.shape, F32), place,
+            (predictions, change, *earlier), "apply", 6, (pltpu.VMEM((width, 2 * part), F32), dma((2,))),
+            (pltpu.VMEM, pltpu.VMEM, *(pl.ANY,) * i), pl.ANY, {3: 0} if i else {},
+        )
+    return (coefficients + update[:width]).T, new.T
 
 
 def plain_shards(inputs, projection, phases, inverse_blocks, labels, predictions, coefficients):

time: 111 us -> 104 us (0.937)
  starting transfers between devices: 32.6 us -> 29.2 us
  local copies, waits for them, and re-layouts: 5.68 us -> 2.56 us
  waiting for transfers between devices: 34.8 us -> 32.5 us
  other arithmetic: 0.08 us -> 1.24 us
    ppermute x32, starting transfers between devices: 32.6 us -> 29.2 us  [swap(): lax.ppermute(x, axes, [p for a, b in pairs for p in ((a, b), (b, a))])]
    unnamed x17 -> x11, local copies, waits for them, and re-layouts: 5.56 us -> 2.43 us
    ppermute x32, waiting for transfers between devices: 34.8 us -> 32.5 us  [swap(): lax.ppermute(x, axes, [p for a, b in pairs for p in ((a, b), (b, a))])]
    transpose x0 -> x1, other arithmetic: none -> 1.16 us  [ring_shards(): return ((coefficients + update[:width]).T, new.T)]
  transfers between devices with their start and end apart: 32 -> 32, of which waited for: 12 -> 16; matrix products, arithmetic and copies ran while one was open for 0% -> 1% of each run, Pallas kernels for 28% -> 31%
where the time goes in v7:
time: 104 us
  Pallas kernels  37.1 us (36%)
  waiting for transfers between devices  32.5 us (31%)
  starting transfers between devices  29.2 us (28%)
  local copies, waits for them, and re-layouts  2.56 us (2%)
  other arithmetic  1.24 us (1%)
  between operations  1.13 us (1%)
    pallas_call x21, Pallas kernels, call(): pl.pallas_call(kernel, out_shape=out_shapes, in_specs=[pl.BlockSpec(memor...  37.1 us
    ppermute x32, waiting for transfers between devices, swap(): lax.ppermute(x, axes, [p for a, b in pairs for p in ((a, b), (b, a))])  32.5 us
    ppermute x32, starting transfers between devices, swap(): lax.ppermute(x, axes, [p for a, b in pairs for p in ((a, b), (b, a))])  29.2 us
    unnamed x11, local copies, waits for them, and re-layouts  2.43 us
  transfers between devices with their start and end apart: 32, of which 16 were waited for; matrix products, arithmetic and copies ran while one was open for 1% of the time, Pallas kernels for 31%

profile of v7, /device:TPU:0, one launch (start us, length us, event | category | flops | bytes accessed | tf_op | source)
XLA Modules:
  0.0 103.7 jit_solution(15608570477759924151)
XLA Ops:
  1.2 1.9 %prepare.1 = (bf16[256,1024]{1,0:T(8,128)(2,1)S(1)}, bf16[512,256]{1,0:T(8,128)(2,1)S(1)}, bf16[512,256]{1,0:T(8,128)(2,1)S(1)}) custom-call(s32[3]{0:T(128)S(1)} %pad_add_fusion.place, bf16[512,1024]{1,0:T(8,128)(2,1)} %inputs.1, s32[1,512]{1,0:T(1,128)} %bitcast.18, f32[500,512]{1,0:T(8,128)} %bitcast.13), custom_call_target="tpu_custom_call" | custom-call | tf_op jit(solution)/shard_map/prepare/pallas_call | solution.py:42
  3.3 2.0 %collective-permute-done = bf16[512,256]{1,0:T(8,128)(2,1)S(1)} collective-permute-done((bf16[512,256]{1,0:T(8,128)(2,1)S(1)}, bf16[512,256]{1,0:T(8,128)(2,1)S(1)}, u32[]{:S(2)}, u32[]{:S(2)}) %collective-permute-start) | collective-permute-done | bytes 262176 | tf_op jit(solution)/shard_map/ppermute | solution.py:183
  5.3 2.9 %collective-permute-start.5 = (bf16[256,1024]{1,0:T(8,128)(2,1)S(1)}, bf16[256,1024]{1,0:T(8,128)(2,1)S(1)}, u32[]{:S(2)}, u32[]{:S(2)}) collective-permute-start(bf16[256,1024]{1,0:T(8,128)(2,1)S(1)} %get-tuple-element.39.rows), channel_id=1, source_target_pairs={{0,4},{4,0},{8,12},{12,8},{14,10},{10,14},{6,2},{2,6},{5,9},{9,5},... | collective-permute-start | bytes 1572872 | tf_op jit(solution)/shard_map/ppermute | solution.py:183
  8.5 2.2 %copy-done.2 = f32[1,512,2048]{2,1,0:T(8,128)S(1)} copy-done((f32[1,512,2048]{2,1,0:T(8,128)S(1)}, f32[1,512,2048]{2,1,0:T(8,128)}, u32[]{:S(2)}) %copy-start.2) | copy-done | bytes 4194328
  12.3 3.3 %block.5 = (bf16[128,1024]{1,0:T(8,128)(2,1)S(1)}, bf16[128,512]{1,0:T(8,128)(2,1)S(1)}) custom-call(s32[3]{0:T(128)S(1)} %pad_add_fusion.place, bf16[256,1024]{1,0:T(8,128)(2,1)S(1)} %get-tuple-element.39.rows, bf16[1024,1024]{1,0:T(8,128)(2,1)S(1)} %copy-done, bf16[1024,1024]{1,0:T(8,128)(2,1)S(1)} %collective-permute-done.1.w_other, ...), custom_call_target="tpu_custom_call" | custom-call | tf_op jit(solution)/shard_map/block/pallas_call | solution.py:42
  15.6 2.0 %collective-permute-start.9 = (bf16[256,1024]{1,0:T(8,128)(2,1)S(1)}, bf16[256,1024]{1,0:T(8,128)(2,1)S(1)}, u32[]{:S(2)}, u32[]{:S(2)}) collective-permute-start(bf16[256,1024]{1,0:T(8,128)(2,1)S(1)} %collective-permute-done.5.rows), channel_id=1, source_target_pairs={{4,8},{8,4},{12,14},{14,12},{10,6},{6,10},{2,0},{0,2},{1,5},{5,1},... | collective-permute-start | bytes 1572872 | tf_op jit(solution)/shard_map/ppermute | solution.py:183
  17.6 4.1 %block.6 = (bf16[256,1024]{1,0:T(8,128)(2,1)S(1)}, bf16[256,512]{1,0:T(8,128)(2,1)S(1)}) custom-call(s32[3]{0:T(128)S(1)} %pad_add_fusion.place, bf16[256,1024]{1,0:T(8,128)(2,1)S(1)} %collective-permute-done.5.rows, bf16[1024,1024]{1,0:T(8,128)(2,1)S(1)} %copy-done, bf16[1024,1024]{1,0:T(8,128)(2,1)S(1)} %collective-permute-done.1.w_other, ...), custom_call_target="tpu_custom_call" | custom-call | tf_op jit(solution)/shard_map/block/pallas_call | solution.py:42
  23.0 2.2 %collective-permute-start.8 = (bf16[1024,256]{1,0:T(8,128)(2,1)S(1)}, bf16[1024,256]{1,0:T(8,128)(2,1)S(1)}, u32[]{:S(2)}, u32[]{:S(2)}) collective-permute-start(bf16[1024,256]{1,0:T(8,128)(2,1)S(1)} %collective-permute-done.4.refs_4_), channel_id=1, source_target_pairs={{4,8},{8,4},{12,14},{14,12},{10,6},{6,10},{2,0},{0,2},{1,5},{5,1},... | collective-permute-start | bytes 1572872 | tf_op jit(solution)/shard_map/ppermute | solution.py:183
  26.0 1.8 %collective-permute-start.13 = (bf16[256,1024]{1,0:T(8,128)(2,1)S(1)}, bf16[256,1024]{1,0:T(8,128)(2,1)S(1)}, u32[]{:S(2)}, u32[]{:S(2)}) collective-permute-start(bf16[256,1024]{1,0:T(8,128)(2,1)S(1)} %collective-permute-done.9.rows), channel_id=1, source_target_pairs={{0,4},{4,0},{8,12},{12,8},{14,10},{10,14},{6,2},{2,6},{5,9},{9,5},... | collective-permute-start | bytes 1572872 | tf_op jit(solution)/shard_map/ppermute | solution.py:183
  28.4 4.1 %block.7 = (bf16[256,1024]{1,0:T(8,128)(2,1)S(1)}, bf16[256,512]{1,0:T(8,128)(2,1)S(1)}) custom-call(s32[3]{0:T(128)S(1)} %pad_add_fusion.place, bf16[256,1024]{1,0:T(8,128)(2,1)S(1)} %collective-permute-done.9.rows, bf16[1024,1024]{1,0:T(8,128)(2,1)S(1)} %copy-done, bf16[1024,1024]{1,0:T(8,128)(2,1)S(1)} %collective-permute-done.1.w_other, ...), custom_call_target="tpu_custom_call" | custom-call | tf_op jit(solution)/shard_map/block/pallas_call | solution.py:42
  32.5 2.9 %collective-permute-done.8.refs_1_ = bf16[1024,256]{1,0:T(8,128)(2,1)S(1)} collective-permute-done((bf16[1024,256]{1,0:T(8,128)(2,1)S(1)}, bf16[1024,256]{1,0:T(8,128)(2,1)S(1)}, u32[]{:S(2)}, u32[]{:S(2)}) %collective-permute-start.8) | collective-permute-done | bytes 524320 | tf_op jit(solution)/shard_map/ppermute | solution.py:183
  35.4 2.4 %collective-permute-start.12 = (bf16[1024,256]{1,0:T(8,128)(2,1)S(1)}, bf16[1024,256]{1,0:T(8,128)(2,1)S(1)}, u32[]{:S(2)}, u32[]{:S(2)}) collective-permute-start(bf16[1024,256]{1,0:T(8,128)(2,1)S(1)} %collective-permute-done.8.refs_1_), channel_id=1, source_target_pairs={{0,4},{4,0},{8,12},{12,8},{14,10},{10,14},{6,2},{2,6},{5,9},{9,5},... | collective-permute-start | bytes 1572872 | tf_op jit(solution)/shard_map/ppermute | solution.py:183
  38.3 1.5 %begin.2.refs_0_ = f32[512,512]{1,0:T(8,128)S(1)} custom-call(s32[3]{0:T(128)S(1)} %pad_add_fusion.place, bf16[1024,256]{1,0:T(8,128)(2,1)S(1)} %constant_dynamic-update-slice_fusion.refs_0_.refs_2_, bf16[128,1024]{1,0:T(8,128)(2,1)S(1)} %get-tuple-element.42.refs_1_, bf16[1024,256]{1,0:T(8,128)(2,1)S(1)} %constant_dynamic-update-slice_fusion.refs_0_.refs_2_, ...), custom_call_target="tpu_custom_call" | custom-call | tf_op jit(solution)/shard_map/begin/pallas_call | solution.py:42
  39.8 4.3 %block.8 = (bf16[256,1024]{1,0:T(8,128)(2,1)S(1)}, bf16[256,512]{1,0:T(8,128)(2,1)S(1)}) custom-call(s32[3]{0:T(128)S(1)} %pad_add_fusion.place, bf16[256,1024]{1,0:T(8,128)(2,1)S(1)} %collective-permute-done.13.rows, bf16[1024,1024]{1,0:T(8,128)(2,1)S(1)} %copy-done, bf16[1024,1024]{1,0:T(8,128)(2,1)S(1)} %collective-permute-done.1.w_other, ...), custom_call_target="tpu_custom_call" | custom-call | tf_op jit(solution)/shard_map/block/pallas_call | solution.py:42
  45.0 2.0 %collective-permute-start.18 = (bf16[128,1024]{1,0:T(8,128)(2,1)S(1)}, bf16[128,1024]{1,0:T(8,128)(2,1)S(1)}, u32[]{:S(2)}, u32[]{:S(2)}) collective-permute-start(bf16[128,1024]{1,0:T(8,128)(2,1)S(1)} %slice.25), channel_id=1, source_target_pairs={{4,8},{8,4},{12,14},{14,12},{10,6},{6,10},{2,0},{0,2},{1,5},{5,1},... | collective-permute-start | bytes 786440 | tf_op jit(solution)/shard_map/ppermute | solution.py:183
  47.9 1.8 %begin.3.begun = f32[512,512]{1,0:T(8,128)S(1)} custom-call(s32[3]{0:T(128)S(1)} %pad_add_fusion.place, f32[512,512]{1,0:T(8,128)S(1)} %begin.2.refs_0_, bf16[1024,256]{1,0:T(8,128)(2,1)S(1)} %collective-permute-done.8.refs_1_, bf16[256,1024]{1,0:T(8,128)(2,1)S(1)} %get-tuple-element.47.refs_2_, bf16[512,256]{1,0:T(8,128)(2,1)S(1)} %collective-permute-done.10.refs_3_, ...), custom_call_target="tpu_custom_call" | custom-call | tf_op jit(solution)/shard_map/begin/pallas_call | solution.py:42
  49.7 1.7 %collective-permute-done.18.rows = bf16[128,1024]{1,0:T(8,128)(2,1)S(1)} collective-permute-done((bf16[128,1024]{1,0:T(8,128)(2,1)S(1)}, bf16[128,1024]{1,0:T(8,128)(2,1)S(1)}, u32[]{:S(2)}, u32[]{:S(2)}) %collective-permute-start.18) | collective-permute-done | bytes 262176 | tf_op jit(solution)/shard_map/ppermute | solution.py:183
  51.5 3.3 %block.9 = (bf16[128,1024]{1,0:T(8,128)(2,1)S(1)}, bf16[128,512]{1,0:T(8,128)(2,1)S(1)}) custom-call(s32[3]{0:T(128)S(1)} %pad_add_fusion.place, bf16[128,1024]{1,0:T(8,128)(2,1)S(1)} %collective-permute-done.18.rows, bf16[1024,1024]{1,0:T(8,128)(2,1)S(1)} %copy-done, bf16[1024,1024]{1,0:T(8,128)(2,1)S(1)} %collective-permute-done.1.w_other, ...), custom_call_target="tpu_custom_call" | custom-call | tf_op jit(solution)/shard_map/block/pallas_call | solution.py:42
  60.4 2.0 %collective-permute-start.23 = (bf16[512,128]{1,0:T(8,128)(2,1)S(1)}, bf16[512,128]{1,0:T(8,128)(2,1)S(1)}, u32[]{:S(2)}, u32[]{:S(2)}) collective-permute-start(bf16[512,128]{1,0:T(8,128)(2,1)S(1)} %far.3), channel_id=1, source_target_pairs={{4,8},{8,4},{12,14},{14,12},{10,6},{6,10},{2,0},{0,2},{1,5},{5,1},... | collective-permute-start | bytes 393224 | tf_op jit(solution)/shard_map/ppermute | solution.py:183
  62.5 2.9 %collective-permute-done.23.came = bf16[512,128]{1,0:T(8,128)(2,1)S(1)} collective-permute-done((bf16[512,128]{1,0:T(8,128)(2,1)S(1)}, bf16[512,128]{1,0:T(8,128)(2,1)S(1)}, u32[]{:S(2)}, u32[]{:S(2)}) %collective-permute-start.23) | collective-permute-done | bytes 131104 | tf_op jit(solution)/shard_map/ppermute | solution.py:183
  65.4 2.0 %collective-permute-done.22.came = bf16[512,128]{1,0:T(8,128)(2,1)S(1)} collective-permute-done((bf16[512,128]{1,0:T(8,128)(2,1)S(1)}, bf16[512,128]{1,0:T(8,128)(2,1)S(1)}, u32[]{:S(2)}, u32[]{:S(2)}) %collective-permute-start.22) | collective-permute-done | bytes 131104 | tf_op jit(solution)/shard_map/ppermute | solution.py:183
  68.3 1.7 %collective-permute-start.25 = (bf16[512,256]{1,0:T(8,128)(2,1)S(1)}, bf16[512,256]{1,0:T(8,128)(2,1)S(1)}, u32[]{:S(2)}, u32[]{:S(2)}) collective-permute-start(bf16[512,256]{1,0:T(8,128)(2,1)S(1)} %hop.6), channel_id=1, source_target_pairs={{0,4},{4,0},{8,12},{12,8},{14,10},{10,14},{6,2},{2,6},{5,9},{9,5},... | collective-permute-start | bytes 786440 | tf_op jit(solution)/shard_map/ppermute | solution.py:183
  71.3 3.4 %collective-permute-done.25.came = bf16[512,256]{1,0:T(8,128)(2,1)S(1)} collective-permute-done((bf16[512,256]{1,0:T(8,128)(2,1)S(1)}, bf16[512,256]{1,0:T(8,128)(2,1)S(1)}, u32[]{:S(2)}, u32[]{:S(2)}) %collective-permute-start.25) | collective-permute-done | bytes 262176 | tf_op jit(solution)/shard_map/ppermute | solution.py:183
  75.6 1.5 %collective-permute-start.27 = (bf16[512,256]{1,0:T(8,128)(2,1)S(1)}, bf16[512,256]{1,0:T(8,128)(2,1)S(1)}, u32[]{:S(2)}, u32[]{:S(2)}) collective-permute-start(bf16[512,256]{1,0:T(8,128)(2,1)S(1)} %hop.8), channel_id=1, source_target_pairs={{4,8},{8,4},{12,14},{14,12},{10,6},{6,10},{2,0},{0,2},{1,5},{5,1},... | collective-permute-start | bytes 786440 | tf_op jit(solution)/shard_map/ppermute | solution.py:183
  77.0 1.4 %collective-permute-done.24.came = bf16[512,256]{1,0:T(8,128)(2,1)S(1)} collective-permute-done((bf16[512,256]{1,0:T(8,128)(2,1)S(1)}, bf16[512,256]{1,0:T(8,128)(2,1)S(1)}, u32[]{:S(2)}, u32[]{:S(2)}) %collective-permute-start.24) | collective-permute-done | bytes 262176 | tf_op jit(solution)/shard_map/ppermute | solution.py:183
  80.5 1.5 %collective-permute-done.27.came = bf16[512,256]{1,0:T(8,128)(2,1)S(1)} collective-permute-done((bf16[512,256]{1,0:T(8,128)(2,1)S(1)}, bf16[512,256]{1,0:T(8,128)(2,1)S(1)}, u32[]{:S(2)}, u32[]{:S(2)}) %collective-permute-start.27) | collective-permute-done | bytes 262176 | tf_op jit(solution)/shard_map/ppermute | solution.py:183
  82.9 1.7 %collective-permute-start.29 = (bf16[512,256]{1,0:T(8,128)(2,1)S(1)}, bf16[512,256]{1,0:T(8,128)(2,1)S(1)}, u32[]{:S(2)}, u32[]{:S(2)}) collective-permute-start(bf16[512,256]{1,0:T(8,128)(2,1)S(1)} %hop.10), channel_id=1, source_target_pairs={{0,4},{4,0},{8,12},{12,8},{14,10},{10,14},{6,2},{2,6},{5,9},{9,5},... | collective-permute-start | bytes 786440 | tf_op jit(solution)/shard_map/ppermute | solution.py:183
  84.6 2.9 %collective-permute-done.26.came = bf16[512,256]{1,0:T(8,128)(2,1)S(1)} collective-permute-done((bf16[512,256]{1,0:T(8,128)(2,1)S(1)}, bf16[512,256]{1,0:T(8,128)(2,1)S(1)}, u32[]{:S(2)}, u32[]{:S(2)}) %collective-permute-start.26) | collective-permute-done | bytes 262176 | tf_op jit(solution)/shard_map/ppermute | solution.py:183
  88.4 1.7 %collective-permute-start.28 = (bf16[512,256]{1,0:T(8,128)(2,1)S(1)}, bf16[512,256]{1,0:T(8,128)(2,1)S(1)}, u32[]{:S(2)}, u32[]{:S(2)}) collective-permute-start(bf16[512,256]{1,0:T(8,128)(2,1)S(1)} %hop.11), channel_id=1, source_target_pairs={{0,4},{4,0},{8,12},{12,8},{14,10},{10,14},{6,2},{2,6},{5,9},{9,5},... | collective-permute-start | bytes 786440 | tf_op jit(solution)/shard_map/ppermute | solution.py:183
  90.1 4.7 %collective-permute-done.28.came = bf16[512,256]{1,0:T(8,128)(2,1)S(1)} collective-permute-done((bf16[512,256]{1,0:T(8,128)(2,1)S(1)}, bf16[512,256]{1,0:T(8,128)(2,1)S(1)}, u32[]{:S(2)}, u32[]{:S(2)}) %collective-permute-start.28) | collective-permute-done | bytes 262176 | tf_op jit(solution)/shard_map/ppermute | solution.py:183
  99.4 2.8 %collective-permute-done.31.change = bf16[512,256]{1,0:T(8,128)(2,1)S(1)} collective-permute-done((bf16[512,256]{1,0:T(8,128)(2,1)S(1)}, bf16[512,256]{1,0:T(8,128)(2,1)S(1)}, u32[]{:S(2)}, u32[]{:S(2)}) %collective-permute-start.31) | collective-permute-done | bytes 262176 | tf_op jit(solution)/shard_map/ppermute | solution.py:183
  102.1 1.4 %apply.3 = f32[500,512]{1,0:T(8,128)} custom-call(s32[3]{0:T(128)S(1)} %pad_add_fusion.place, f32[500,512]{1,0:T(8,128)S(1)} %bitcast.15, bf16[512,256]{1,0:T(8,128)(2,1)S(1)} %collective-permute-done.31.change, f32[500,512]{1,0:T(8,128)} %apply.2.refs_0_), custom_call_target="tpu_custom_call", output_to_operand_aliasing={{}: (3, {})} | custom-call | tf_op jit(solution)/shard_map/apply/pallas_call | solution.py:42
  (74 shorter events, 24.5 us)
Async XLA Ops:
  0.6 11.4 %collective-permute-start.1 = (bf16[1024,1024]{1,0:T(8,128)(2,1)}, bf16[1024,1024]{1,0:T(8,128)(2,1)S(1)}, u32[]{:S(2)}, u32[]{:S(2)}) collective-permute-start(bf16[1024,1024]{1,0:T(8,128)(2,1)} %w_own.9), channel_id=1, source_target_pairs={{0,1},{1,0},{2,3},{3,2},{4,5},{5,4},{6,7},{7,6},{8,9},{9,8},{10,11... | collective-permute-start | bytes 6291464 | tf_op jit(solution)/shard_map/ppermute | solution.py:183
  3.2 2.2 %collective-permute-start = (bf16[512,256]{1,0:T(8,128)(2,1)S(1)}, bf16[512,256]{1,0:T(8,128)(2,1)S(1)}, u32[]{:S(2)}, u32[]{:S(2)}) collective-permute-start(bf16[512,256]{1,0:T(8,128)(2,1)S(1)} %get-tuple-element.37), channel_id=1, source_target_pairs={{0,1},{1,0},{2,3},{3,2},{4,5},{5,4},{6,7},{7,6},{8,9},{9,8},{10,11... | collective-permute-start | bytes 786440 | tf_op jit(solution)/shard_map/ppermute | solution.py:183
  5.3 10.3 %collective-permute-start.5 = (bf16[256,1024]{1,0:T(8,128)(2,1)S(1)}, bf16[256,1024]{1,0:T(8,128)(2,1)S(1)}, u32[]{:S(2)}, u32[]{:S(2)}) collective-permute-start(bf16[256,1024]{1,0:T(8,128)(2,1)S(1)} %get-tuple-element.39.rows), channel_id=1, source_target_pairs={{0,4},{4,0},{8,12},{12,8},{14,10},{10,14},{6,2},{2,6},{5,9},{9,5},... | collective-permute-start | bytes 1572872 | tf_op jit(solution)/shard_map/ppermute | solution.py:183
  8.3 14.7 %collective-permute-start.4 = (bf16[1024,256]{1,0:T(8,128)(2,1)S(1)}, bf16[1024,256]{1,0:T(8,128)(2,1)S(1)}, u32[]{:S(2)}, u32[]{:S(2)}) collective-permute-start(bf16[1024,256]{1,0:T(8,128)(2,1)S(1)} %constant_dynamic-update-slice_fusion.refs_0_.refs_2_), channel_id=1, source_target_pairs={{0,4},{4,0},{8,12},{12,8},{14,10},{10,14},{6,2},{2,6},{5,9},{9,5},... | collective-permute-start | bytes 1572872 | tf_op jit(solution)/shard_map/ppermute | solution.py:183
  8.4 3.6 %collective-permute-start.2 = (bf16[1,1024]{1,0:T(2,128)(2,1)S(1)}, bf16[1,1024]{1,0:T(2,128)(2,1)S(1)}, u32[]{:S(2)}, u32[]{:S(2)}) collective-permute-start(bf16[1,1024]{1,0:T(2,128)(2,1)S(1)} %broadcast_in_dim.7.p_own), channel_id=1, source_target_pairs={{0,1},{1,0},{2,3},{3,2},{4,5},{5,4},{6,7},{7,6},{8,9},{9,8},{10,11... | collective-permute-start | bytes 6152 | tf_op jit(solution)/shard_map/ppermute | solution.py:183
  15.6 10.4 %collective-permute-start.9 = (bf16[256,1024]{1,0:T(8,128)(2,1)S(1)}, bf16[256,1024]{1,0:T(8,128)(2,1)S(1)}, u32[]{:S(2)}, u32[]{:S(2)}) collective-permute-start(bf16[256,1024]{1,0:T(8,128)(2,1)S(1)} %collective-permute-done.5.rows), channel_id=1, source_target_pairs={{4,8},{8,4},{12,14},{14,12},{10,6},{6,10},{2,0},{0,2},{1,5},{5,1},... | collective-permute-start | bytes 1572872 | tf_op jit(solution)/shard_map/ppermute | solution.py:183
  23.0 12.4 %collective-permute-start.8 = (bf16[1024,256]{1,0:T(8,128)(2,1)S(1)}, bf16[1024,256]{1,0:T(8,128)(2,1)S(1)}, u32[]{:S(2)}, u32[]{:S(2)}) collective-permute-start(bf16[1024,256]{1,0:T(8,128)(2,1)S(1)} %collective-permute-done.4.refs_4_), channel_id=1, source_target_pairs={{4,8},{8,4},{12,14},{14,12},{10,6},{6,10},{2,0},{0,2},{1,5},{5,1},... | collective-permute-start | bytes 1572872 | tf_op jit(solution)/shard_map/ppermute | solution.py:183
  25.2 13.1 %collective-permute-start.7 = (bf16[256,1024]{1,0:T(8,128)(2,1)S(1)}, bf16[256,1024]{1,0:T(8,128)(2,1)S(1)}, u32[]{:S(2)}, u32[]{:S(2)}) collective-permute-start(bf16[256,1024]{1,0:T(8,128)(2,1)S(1)} %get-tuple-element.44.refs_5_), channel_id=1, source_target_pairs={{0,1},{1,0},{2,3},{3,2},{4,5},{5,4},{6,7},{7,6},{8,9},{9,8},{10,11... | collective-permute-start | bytes 1572872 | tf_op jit(solution)/shard_map/ppermute | solution.py:183
  26.0 13.8 %collective-permute-start.13 = (bf16[256,1024]{1,0:T(8,128)(2,1)S(1)}, bf16[256,1024]{1,0:T(8,128)(2,1)S(1)}, u32[]{:S(2)}, u32[]{:S(2)}) collective-permute-start(bf16[256,1024]{1,0:T(8,128)(2,1)S(1)} %collective-permute-done.9.rows), channel_id=1, source_target_pairs={{0,4},{4,0},{8,12},{12,8},{14,10},{10,14},{6,2},{2,6},{5,9},{9,5},... | collective-permute-start | bytes 1572872 | tf_op jit(solution)/shard_map/ppermute | solution.py:183
  27.9 9.9 %collective-permute-start.6 = (bf16[512,256]{1,0:T(8,128)(2,1)S(1)}, bf16[512,256]{1,0:T(8,128)(2,1)S(1)}, u32[]{:S(2)}, u32[]{:S(2)}) collective-permute-start(bf16[512,256]{1,0:T(8,128)(2,1)S(1)} %slice.21), channel_id=1, source_target_pairs={{0,1},{1,0},{2,3},{3,2},{4,5},{5,4},{6,7},{7,6},{8,9},{9,8},{10,11... | collective-permute-start | bytes 786440 | tf_op jit(solution)/shard_map/ppermute | solution.py:183
  28.2 9.5 %collective-permute-start.3 = (bf16[128,1024]{1,0:T(8,128)(2,1)S(1)}, bf16[128,1024]{1,0:T(8,128)(2,1)S(1)}, u32[]{:S(2)}, u32[]{:S(2)}) collective-permute-start(bf16[128,1024]{1,0:T(8,128)(2,1)S(1)} %get-tuple-element.42.refs_1_), channel_id=1, source_target_pairs={{0,1},{1,0},{2,3},{3,2},{4,5},{5,4},{6,7},{7,6},{8,9},{9,8},{10,11... | collective-permute-start | bytes 786440 | tf_op jit(solution)/shard_map/ppermute | solution.py:183
  35.4 9.5 %collective-permute-start.12 = (bf16[1024,256]{1,0:T(8,128)(2,1)S(1)}, bf16[1024,256]{1,0:T(8,128)(2,1)S(1)}, u32[]{:S(2)}, u32[]{:S(2)}) collective-permute-start(bf16[1024,256]{1,0:T(8,128)(2,1)S(1)} %collective-permute-done.8.refs_1_), channel_id=1, source_target_pairs={{0,4},{4,0},{8,12},{12,8},{14,10},{10,14},{6,2},{2,6},{5,9},{9,5},... | collective-permute-start | bytes 1572872 | tf_op jit(solution)/shard_map/ppermute | solution.py:183
  37.7 2.0 %collective-permute-start.14 = (bf16[128,512]{1,0:T(8,128)(2,1)S(1)}, bf16[128,512]{1,0:T(8,128)(2,1)S(1)}, u32[]{:S(2)}, u32[]{:S(2)}) collective-permute-start(bf16[128,512]{1,0:T(8,128)(2,1)S(1)} %get-tuple-element.49.mine), channel_id=1, source_target_pairs={{0,1},{1,0},{2,3},{3,2},{4,5},{5,4},{6,7},{7,6},{8,9},{9,8},{10,11... | collective-permute-start | bytes 393224 | tf_op jit(solution)/shard_map/ppermute | solution.py:183
  37.7 10.2 %collective-permute-start.11 = (bf16[256,1024]{1,0:T(8,128)(2,1)S(1)}, bf16[256,1024]{1,0:T(8,128)(2,1)S(1)}, u32[]{:S(2)}, u32[]{:S(2)}) collective-permute-start(bf16[256,1024]{1,0:T(8,128)(2,1)S(1)} %get-tuple-element.47.refs_2_), channel_id=1, source_target_pairs={{0,1},{1,0},{2,3},{3,2},{4,5},{5,4},{6,7},{7,6},{8,9},{9,8},{10,11... | collective-permute-start | bytes 1572872 | tf_op jit(solution)/shard_map/ppermute | solution.py:183
  44.1 3.9 %collective-permute-start.16 = (bf16[256,1024]{1,0:T(8,128)(2,1)S(1)}, bf16[256,1024]{1,0:T(8,128)(2,1)S(1)}, u32[]{:S(2)}, u32[]{:S(2)}) collective-permute-start(bf16[256,1024]{1,0:T(8,128)(2,1)S(1)} %get-tuple-element.51.refs_6_), channel_id=1, source_target_pairs={{0,1},{1,0},{2,3},{3,2},{4,5},{5,4},{6,7},{7,6},{8,9},{9,8},{10,11... | collective-permute-start | bytes 1572872 | tf_op jit(solution)/shard_map/ppermute | solution.py:183
  44.2 2.9 %collective-permute-start.10 = (bf16[512,256]{1,0:T(8,128)(2,1)S(1)}, bf16[512,256]{1,0:T(8,128)(2,1)S(1)}, u32[]{:S(2)}, u32[]{:S(2)}) collective-permute-start(bf16[512,256]{1,0:T(8,128)(2,1)S(1)} %slice.22), channel_id=1, source_target_pairs={{0,1},{1,0},{2,3},{3,2},{4,5},{5,4},{6,7},{7,6},{8,9},{9,8},{10,11... | collective-permute-start | bytes 786440 | tf_op jit(solution)/shard_map/ppermute | solution.py:183
  44.9 3.0 %collective-permute-start.15 = (bf16[512,256]{1,0:T(8,128)(2,1)S(1)}, bf16[512,256]{1,0:T(8,128)(2,1)S(1)}, u32[]{:S(2)}, u32[]{:S(2)}) collective-permute-start(bf16[512,256]{1,0:T(8,128)(2,1)S(1)} %slice.23), channel_id=1, source_target_pairs={{0,1},{1,0},{2,3},{3,2},{4,5},{5,4},{6,7},{7,6},{8,9},{9,8},{10,11... | collective-permute-start | bytes 786440 | tf_op jit(solution)/shard_map/ppermute | solution.py:183
  45.0 6.4 %collective-permute-start.18 = (bf16[128,1024]{1,0:T(8,128)(2,1)S(1)}, bf16[128,1024]{1,0:T(8,128)(2,1)S(1)}, u32[]{:S(2)}, u32[]{:S(2)}) collective-permute-start(bf16[128,1024]{1,0:T(8,128)(2,1)S(1)} %slice.25), channel_id=1, source_target_pairs={{4,8},{8,4},{12,14},{14,12},{10,6},{6,10},{2,0},{0,2},{1,5},{5,1},... | collective-permute-start | bytes 786440 | tf_op jit(solution)/shard_map/ppermute | solution.py:183
  47.1 7.8 %collective-permute-start.17 = (bf16[1024,128]{1,0:T(8,128)(2,1)S(1)}, bf16[1024,128]{1,0:T(8,128)(2,1)S(1)}, u32[]{:S(2)}, u32[]{:S(2)}) collective-permute-start(bf16[1024,128]{1,0:T(8,128)(2,1)S(1)} %slice.24), channel_id=1, source_target_pairs={{4,8},{8,4},{12,14},{14,12},{10,6},{6,10},{2,0},{0,2},{1,5},{5,1},... | collective-permute-start | bytes 786440 | tf_op jit(solution)/shard_map/ppermute | solution.py:183
  54.8 1.8 %collective-permute-start.20 = (bf16[128,1024]{1,0:T(8,128)(2,1)S(1)}, bf16[128,1024]{1,0:T(8,128)(2,1)S(1)}, u32[]{:S(2)}, u32[]{:S(2)}) collective-permute-start(bf16[128,1024]{1,0:T(8,128)(2,1)S(1)} %get-tuple-element.54.refs_1_), channel_id=1, source_target_pairs={{0,1},{1,0},{2,3},{3,2},{4,5},{5,4},{6,7},{7,6},{8,9},{9,8},{10,11... | collective-permute-start | bytes 786440 | tf_op jit(solution)/shard_map/ppermute | solution.py:183
  54.9 1.7 %collective-permute-start.19 = (bf16[512,128]{1,0:T(8,128)(2,1)S(1)}, bf16[512,128]{1,0:T(8,128)(2,1)S(1)}, u32[]{:S(2)}, u32[]{:S(2)}) collective-permute-start(bf16[512,128]{1,0:T(8,128)(2,1)S(1)} %slice.28), channel_id=1, source_target_pairs={{0,1},{1,0},{2,3},{3,2},{4,5},{5,4},{6,7},{7,6},{8,9},{9,8},{10,11... | collective-permute-start | bytes 393224 | tf_op jit(solution)/shard_map/ppermute | solution.py:183
  57.6 2.0 %collective-permute-start.21 = (bf16[512,512]{1,0:T(8,128)(2,1)S(1)}, bf16[512,512]{1,0:T(8,128)(2,1)S(1)}, u32[]{:S(2)}, u32[]{:S(2)}) collective-permute-start(bf16[512,512]{1,0:T(8,128)(2,1)S(1)} %get-tuple-element.56.sent), channel_id=1, source_target_pairs={{0,1},{1,0},{2,3},{3,2},{4,5},{5,4},{6,7},{7,6},{8,9},{9,8},{10,11... | collective-permute-start | bytes 1572872 | tf_op jit(solution)/shard_map/ppermute | solution.py:183
  60.4 5.0 %collective-permute-start.23 = (bf16[512,128]{1,0:T(8,128)(2,1)S(1)}, bf16[512,128]{1,0:T(8,128)(2,1)S(1)}, u32[]{:S(2)}, u32[]{:S(2)}) collective-permute-start(bf16[512,128]{1,0:T(8,128)(2,1)S(1)} %far.3), channel_id=1, source_target_pairs={{4,8},{8,4},{12,14},{14,12},{10,6},{6,10},{2,0},{0,2},{1,5},{5,1},... | collective-permute-start | bytes 393224 | tf_op jit(solution)/shard_map/ppermute | solution.py:183
  62.4 5.0 %collective-permute-start.22 = (bf16[512,128]{1,0:T(8,128)(2,1)S(1)}, bf16[512,128]{1,0:T(8,128)(2,1)S(1)}, u32[]{:S(2)}, u32[]{:S(2)}) collective-permute-start(bf16[512,128]{1,0:T(8,128)(2,1)S(1)} %far.2), channel_id=1, source_target_pairs={{4,8},{8,4},{12,14},{14,12},{10,6},{6,10},{2,0},{0,2},{1,5},{5,1},... | collective-permute-start | bytes 393224 | tf_op jit(solution)/shard_map/ppermute | solution.py:183
  68.3 6.4 %collective-permute-start.25 = (bf16[512,256]{1,0:T(8,128)(2,1)S(1)}, bf16[512,256]{1,0:T(8,128)(2,1)S(1)}, u32[]{:S(2)}, u32[]{:S(2)}) collective-permute-start(bf16[512,256]{1,0:T(8,128)(2,1)S(1)} %hop.6), channel_id=1, source_target_pairs={{0,4},{4,0},{8,12},{12,8},{14,10},{10,14},{6,2},{2,6},{5,9},{9,5},... | collective-permute-start | bytes 786440 | tf_op jit(solution)/shard_map/ppermute | solution.py:183
  70.9 7.6 %collective-permute-start.24 = (bf16[512,256]{1,0:T(8,128)(2,1)S(1)}, bf16[512,256]{1,0:T(8,128)(2,1)S(1)}, u32[]{:S(2)}, u32[]{:S(2)}) collective-permute-start(bf16[512,256]{1,0:T(8,128)(2,1)S(1)} %hop.7), channel_id=1, source_target_pairs={{0,4},{4,0},{8,12},{12,8},{14,10},{10,14},{6,2},{2,6},{5,9},{9,5},... | collective-permute-start | bytes 786440 | tf_op jit(solution)/shard_map/ppermute | solution.py:183
  75.6 6.4 %collective-permute-start.27 = (bf16[512,256]{1,0:T(8,128)(2,1)S(1)}, bf16[512,256]{1,0:T(8,128)(2,1)S(1)}, u32[]{:S(2)}, u32[]{:S(2)}) collective-permute-start(bf16[512,256]{1,0:T(8,128)(2,1)S(1)} %hop.8), channel_id=1, source_target_pairs={{4,8},{8,4},{12,14},{14,12},{10,6},{6,10},{2,0},{0,2},{1,5},{5,1},... | collective-permute-start | bytes 786440 | tf_op jit(solution)/shard_map/ppermute | solution.py:183
  79.3 8.2 %collective-permute-start.26 = (bf16[512,256]{1,0:T(8,128)(2,1)S(1)}, bf16[512,256]{1,0:T(8,128)(2,1)S(1)}, u32[]{:S(2)}, u32[]{:S(2)}) collective-permute-start(bf16[512,256]{1,0:T(8,128)(2,1)S(1)} %hop.9), channel_id=1, source_target_pairs={{4,8},{8,4},{12,14},{14,12},{10,6},{6,10},{2,0},{0,2},{1,5},{5,1},... | collective-permute-start | bytes 786440 | tf_op jit(solution)/shard_map/ppermute | solution.py:183
  82.9 7.2 %collective-permute-start.29 = (bf16[512,256]{1,0:T(8,128)(2,1)S(1)}, bf16[512,256]{1,0:T(8,128)(2,1)S(1)}, u32[]{:S(2)}, u32[]{:S(2)}) collective-permute-start(bf16[512,256]{1,0:T(8,128)(2,1)S(1)} %hop.10), channel_id=1, source_target_pairs={{0,4},{4,0},{8,12},{12,8},{14,10},{10,14},{6,2},{2,6},{5,9},{9,5},... | collective-permute-start | bytes 786440 | tf_op jit(solution)/shard_map/ppermute | solution.py:183
  88.4 6.4 %collective-permute-start.28 = (bf16[512,256]{1,0:T(8,128)(2,1)S(1)}, bf16[512,256]{1,0:T(8,128)(2,1)S(1)}, u32[]{:S(2)}, u32[]{:S(2)}) collective-permute-start(bf16[512,256]{1,0:T(8,128)(2,1)S(1)} %hop.11), channel_id=1, source_target_pairs={{0,4},{4,0},{8,12},{12,8},{14,10},{10,14},{6,2},{2,6},{5,9},{9,5},... | collective-permute-start | bytes 786440 | tf_op jit(solution)/shard_map/ppermute | solution.py:183
  90.1 4.8 %collective-permute-start.30 = (bf16[512,256]{1,0:T(8,128)(2,1)S(1)}, bf16[512,256]{1,0:T(8,128)(2,1)S(1)}, u32[]{:S(2)}, u32[]{:S(2)}) collective-permute-start(bf16[512,256]{1,0:T(8,128)(2,1)S(1)} %collective-permute-done.29), channel_id=1, source_target_pairs={{0,1},{1,0},{2,3},{3,2},{4,5},{5,4},{6,7},{7,6},{8,9},{9,8},{10,11... | collective-permute-start | bytes 786440 | tf_op jit(solution)/shard_map/ppermute | solution.py:183
  95.7 6.4 %collective-permute-start.31 = (bf16[512,256]{1,0:T(8,128)(2,1)S(1)}, bf16[512,256]{1,0:T(8,128)(2,1)S(1)}, u32[]{:S(2)}, u32[]{:S(2)}) collective-permute-start(bf16[512,256]{1,0:T(8,128)(2,1)S(1)} %last.1.change), channel_id=1, source_target_pairs={{0,2},{2,0},{1,3},{3,1},{4,6},{6,4},{5,7},{7,5},{8,10},{10,8},{9,1... | collective-permute-start | bytes 786440 | tf_op jit(solution)/shard_map/ppermute | solution.py:183
  (5 other events, 36.0 us)

commit v8 on v7

--- a/solution.py
+++ b/solution.py
@@ -256,9 +256,9 @@
     q3, f3 = block(x3, 2 * part)
     (r3,) = after((r3,), q3)
     r4 = T(r3[:, :part])
+    (x4,) = after((x4,), q3)
+    q4, f4 = block(x4, part)
     begun = begin([(r2, q2), (theirs(r2), C(q2)), (r3, q3), (theirs(r3), C(q3))], begun)
-    (x4,) = after((x4,), begun)
-    q4, f4 = block(x4, part)
     update, sent = call(
         update_kernel, (like((padded, depth), F32), like((padded, depth))), place,
         (begun, r4, q4, theirs(r4), C(q4)), "update", 14,

time: 104 us -> 103 us (level)
  waiting for transfers between devices: 32.5 us -> 31.4 us
    ppermute x32, waiting for transfers between devices: 32.5 us -> 31.4 us  [swap(): lax.ppermute(x, axes, [p for a, b in pairs for p in ((a, b), (b, a))])]
where the time goes in v8:
time: 103 us
  Pallas kernels  37.1 us (36%)
  waiting for transfers between devices  31.4 us (30%)
  starting transfers between devices  29 us (28%)
  local copies, waits for them, and re-layouts  2.56 us (2%)
  other arithmetic  1.24 us (1%)
  between operations  1.15 us (1%)
    pallas_call x21, Pallas kernels, call(): pl.pallas_call(kernel, out_shape=out_shapes, in_specs=[pl.BlockSpec(memor...  37.1 us
    ppermute x32, waiting for transfers between devices, swap(): lax.ppermute(x, axes, [p for a, b in pairs for p in ((a, b), (b, a))])  31.4 us
    ppermute x32, starting transfers between devices, swap(): lax.ppermute(x, axes, [p for a, b in pairs for p in ((a, b), (b, a))])  29 us
    unnamed x11, local copies, waits for them, and re-layouts  2.43 us
  transfers between devices with their start and end apart: 32, of which 16 were waited for; matrix products, arithmetic and copies ran while one was open for 1% of the time, Pallas kernels for 31%

profile of v8, /device:TPU:0, one launch (start us, length us, event | category | flops | bytes accessed | tf_op | source)
XLA Modules:
  0.0 102.5 jit_solution(18289488465804237840)
XLA Ops:
  1.2 1.9 %prepare.1 = (bf16[256,1024]{1,0:T(8,128)(2,1)S(1)}, bf16[512,256]{1,0:T(8,128)(2,1)S(1)}, bf16[512,256]{1,0:T(8,128)(2,1)S(1)}) custom-call(s32[3]{0:T(128)S(1)} %pad_add_fusion.place, bf16[512,1024]{1,0:T(8,128)(2,1)} %inputs.1, s32[1,512]{1,0:T(1,128)} %bitcast.18, f32[500,512]{1,0:T(8,128)} %bitcast.13), custom_call_target="tpu_custom_call" | custom-call | tf_op jit(solution)/shard_map/prepare/pallas_call | solution.py:42
  3.3 2.0 %collective-permute-done = bf16[512,256]{1,0:T(8,128)(2,1)S(1)} collective-permute-done((bf16[512,256]{1,0:T(8,128)(2,1)S(1)}, bf16[512,256]{1,0:T(8,128)(2,1)S(1)}, u32[]{:S(2)}, u32[]{:S(2)}) %collective-permute-start) | collective-permute-done | bytes 262176 | tf_op jit(solution)/shard_map/ppermute | solution.py:183
  5.3 2.9 %collective-permute-start.5 = (bf16[256,1024]{1,0:T(8,128)(2,1)S(1)}, bf16[256,1024]{1,0:T(8,128)(2,1)S(1)}, u32[]{:S(2)}, u32[]{:S(2)}) collective-permute-start(bf16[256,1024]{1,0:T(8,128)(2,1)S(1)} %get-tuple-element.39.rows), channel_id=1, source_target_pairs={{0,4},{4,0},{8,12},{12,8},{14,10},{10,14},{6,2},{2,6},{5,9},{9,5},... | collective-permute-start | bytes 1572872 | tf_op jit(solution)/shard_map/ppermute | solution.py:183
  8.5 2.2 %copy-done.2 = f32[1,512,2048]{2,1,0:T(8,128)S(1)} copy-done((f32[1,512,2048]{2,1,0:T(8,128)S(1)}, f32[1,512,2048]{2,1,0:T(8,128)}, u32[]{:S(2)}) %copy-start.2) | copy-done | bytes 4194328
  10.7 1.4 %split.1 = (bf16[512,2048]{1,0:T(8,128)(2,1)S(1)}, bf16[512,2048]{1,0:T(8,128)(2,1)S(1)}) custom-call(s32[3]{0:T(128)S(1)} %pad_add_fusion.place, f32[512,2048]{1,0:T(8,128)S(1)} %bitcast.16), custom_call_target="tpu_custom_call" | custom-call | tf_op jit(solution)/shard_map/split/pallas_call | solution.py:42
  12.2 3.3 %block.5 = (bf16[128,1024]{1,0:T(8,128)(2,1)S(1)}, bf16[128,512]{1,0:T(8,128)(2,1)S(1)}) custom-call(s32[3]{0:T(128)S(1)} %pad_add_fusion.place, bf16[256,1024]{1,0:T(8,128)(2,1)S(1)} %get-tuple-element.39.rows, bf16[1024,1024]{1,0:T(8,128)(2,1)S(1)} %copy-done, bf16[1024,1024]{1,0:T(8,128)(2,1)S(1)} %collective-permute-done.1.w_other, ...), custom_call_target="tpu_custom_call" | custom-call | tf_op jit(solution)/shard_map/block/pallas_call | solution.py:42
  15.6 2.0 %collective-permute-start.9 = (bf16[256,1024]{1,0:T(8,128)(2,1)S(1)}, bf16[256,1024]{1,0:T(8,128)(2,1)S(1)}, u32[]{:S(2)}, u32[]{:S(2)}) collective-permute-start(bf16[256,1024]{1,0:T(8,128)(2,1)S(1)} %collective-permute-done.5.rows), channel_id=1, source_target_pairs={{4,8},{8,4},{12,14},{14,12},{10,6},{6,10},{2,0},{0,2},{1,5},{5,1},... | collective-permute-start | bytes 1572872 | tf_op jit(solution)/shard_map/ppermute | solution.py:183
  17.6 4.1 %block.6 = (bf16[256,1024]{1,0:T(8,128)(2,1)S(1)}, bf16[256,512]{1,0:T(8,128)(2,1)S(1)}) custom-call(s32[3]{0:T(128)S(1)} %pad_add_fusion.place, bf16[256,1024]{1,0:T(8,128)(2,1)S(1)} %collective-permute-done.5.rows, bf16[1024,1024]{1,0:T(8,128)(2,1)S(1)} %copy-done, bf16[1024,1024]{1,0:T(8,128)(2,1)S(1)} %collective-permute-done.1.w_other, ...), custom_call_target="tpu_custom_call" | custom-call | tf_op jit(solution)/shard_map/block/pallas_call | solution.py:42
  23.0 2.2 %collective-permute-start.8 = (bf16[1024,256]{1,0:T(8,128)(2,1)S(1)}, bf16[1024,256]{1,0:T(8,128)(2,1)S(1)}, u32[]{:S(2)}, u32[]{:S(2)}) collective-permute-start(bf16[1024,256]{1,0:T(8,128)(2,1)S(1)} %collective-permute-done.4.refs_4_), channel_id=1, source_target_pairs={{4,8},{8,4},{12,14},{14,12},{10,6},{6,10},{2,0},{0,2},{1,5},{5,1},... | collective-permute-start | bytes 1572872 | tf_op jit(solution)/shard_map/ppermute | solution.py:183
  26.0 1.8 %collective-permute-start.13 = (bf16[256,1024]{1,0:T(8,128)(2,1)S(1)}, bf16[256,1024]{1,0:T(8,128)(2,1)S(1)}, u32[]{:S(2)}, u32[]{:S(2)}) collective-permute-start(bf16[256,1024]{1,0:T(8,128)(2,1)S(1)} %collective-permute-done.9.rows), channel_id=1, source_target_pairs={{0,4},{4,0},{8,12},{12,8},{14,10},{10,14},{6,2},{2,6},{5,9},{9,5},... | collective-permute-start | bytes 1572872 | tf_op jit(solution)/shard_map/ppermute | solution.py:183
  27.8 4.1 %block.7 = (bf16[256,1024]{1,0:T(8,128)(2,1)S(1)}, bf16[256,512]{1,0:T(8,128)(2,1)S(1)}) custom-call(s32[3]{0:T(128)S(1)} %pad_add_fusion.place, bf16[256,1024]{1,0:T(8,128)(2,1)S(1)} %collective-permute-done.9.rows, bf16[1024,1024]{1,0:T(8,128)(2,1)S(1)} %copy-done, bf16[1024,1024]{1,0:T(8,128)(2,1)S(1)} %collective-permute-done.1.w_other, ...), custom_call_target="tpu_custom_call" | custom-call | tf_op jit(solution)/shard_map/block/pallas_call | solution.py:42
  31.9 3.5 %collective-permute-done.8.refs_1_ = bf16[1024,256]{1,0:T(8,128)(2,1)S(1)} collective-permute-done((bf16[1024,256]{1,0:T(8,128)(2,1)S(1)}, bf16[1024,256]{1,0:T(8,128)(2,1)S(1)}, u32[]{:S(2)}, u32[]{:S(2)}) %collective-permute-start.8) | collective-permute-done | bytes 524320 | tf_op jit(solution)/shard_map/ppermute | solution.py:183
  35.4 2.4 %collective-permute-start.12 = (bf16[1024,256]{1,0:T(8,128)(2,1)S(1)}, bf16[1024,256]{1,0:T(8,128)(2,1)S(1)}, u32[]{:S(2)}, u32[]{:S(2)}) collective-permute-start(bf16[1024,256]{1,0:T(8,128)(2,1)S(1)} %collective-permute-done.8.refs_1_), channel_id=1, source_target_pairs={{0,4},{4,0},{8,12},{12,8},{14,10},{10,14},{6,2},{2,6},{5,9},{9,5},... | collective-permute-start | bytes 1572872 | tf_op jit(solution)/shard_map/ppermute | solution.py:183
  40.0 1.5 %begin.2.refs_0_ = f32[512,512]{1,0:T(8,128)S(1)} custom-call(s32[3]{0:T(128)S(1)} %pad_add_fusion.place, bf16[1024,256]{1,0:T(8,128)(2,1)S(1)} %constant_dynamic-update-slice_fusion.refs_0_.refs_2_, bf16[128,1024]{1,0:T(8,128)(2,1)S(1)} %get-tuple-element.42.refs_1_, bf16[1024,256]{1,0:T(8,128)(2,1)S(1)} %constant_dynamic-update-slice_fusion.refs_0_.refs_2_, ...), custom_call_target="tpu_custom_call" | custom-call | tf_op jit(solution)/shard_map/begin/pallas_call | solution.py:42
  41.5 1.5 %collective-permute-start.18 = (bf16[128,1024]{1,0:T(8,128)(2,1)S(1)}, bf16[128,1024]{1,0:T(8,128)(2,1)S(1)}, u32[]{:S(2)}, u32[]{:S(2)}) collective-permute-start(bf16[128,1024]{1,0:T(8,128)(2,1)S(1)} %slice.25), channel_id=1, source_target_pairs={{4,8},{8,4},{12,14},{14,12},{10,6},{6,10},{2,0},{0,2},{1,5},{5,1},... | collective-permute-start | bytes 786440 | tf_op jit(solution)/shard_map/ppermute | solution.py:183
  43.1 4.2 %block.8 = (bf16[256,1024]{1,0:T(8,128)(2,1)S(1)}, bf16[256,512]{1,0:T(8,128)(2,1)S(1)}) custom-call(s32[3]{0:T(128)S(1)} %pad_add_fusion.place, bf16[256,1024]{1,0:T(8,128)(2,1)S(1)} %collective-permute-done.13.rows, bf16[1024,1024]{1,0:T(8,128)(2,1)S(1)} %copy-done, bf16[1024,1024]{1,0:T(8,128)(2,1)S(1)} %collective-permute-done.1.w_other, ...), custom_call_target="tpu_custom_call" | custom-call | tf_op jit(solution)/shard_map/block/pallas_call | solution.py:42
  48.1 1.4 %collective-permute-start.10 = (bf16[512,256]{1,0:T(8,128)(2,1)S(1)}, bf16[512,256]{1,0:T(8,128)(2,1)S(1)}, u32[]{:S(2)}, u32[]{:S(2)}) collective-permute-start(bf16[512,256]{1,0:T(8,128)(2,1)S(1)} %slice.22), channel_id=1, source_target_pairs={{0,1},{1,0},{2,3},{3,2},{4,5},{5,4},{6,7},{7,6},{8,9},{9,8},{10,11... | collective-permute-start | bytes 786440 | tf_op jit(solution)/shard_map/ppermute | solution.py:183
  49.6 3.3 %block.9 = (bf16[128,1024]{1,0:T(8,128)(2,1)S(1)}, bf16[128,512]{1,0:T(8,128)(2,1)S(1)}) custom-call(s32[3]{0:T(128)S(1)} %pad_add_fusion.place, bf16[128,1024]{1,0:T(8,128)(2,1)S(1)} %collective-permute-done.18.rows, bf16[1024,1024]{1,0:T(8,128)(2,1)S(1)} %copy-done, bf16[1024,1024]{1,0:T(8,128)(2,1)S(1)} %collective-permute-done.1.w_other, ...), custom_call_target="tpu_custom_call" | custom-call | tf_op jit(solution)/shard_map/block/pallas_call | solution.py:42
  54.5 1.8 %begin.3.begun = f32[512,512]{1,0:T(8,128)S(1)} custom-call(s32[3]{0:T(128)S(1)} %pad_add_fusion.place, f32[512,512]{1,0:T(8,128)S(1)} %begin.2.refs_0_, bf16[1024,256]{1,0:T(8,128)(2,1)S(1)} %collective-permute-done.8.refs_1_, bf16[256,1024]{1,0:T(8,128)(2,1)S(1)} %get-tuple-element.47.refs_2_, bf16[512,256]{1,0:T(8,128)(2,1)S(1)} %collective-permute-done.10.refs_3_, ...), custom_call_target="tpu_custom_call" | custom-call | tf_op jit(solution)/shard_map/begin/pallas_call | solution.py:42
  62.2 2.9 %collective-permute-done.23.came = bf16[512,128]{1,0:T(8,128)(2,1)S(1)} collective-permute-done((bf16[512,128]{1,0:T(8,128)(2,1)S(1)}, bf16[512,128]{1,0:T(8,128)(2,1)S(1)}, u32[]{:S(2)}, u32[]{:S(2)}) %collective-permute-start.23) | collective-permute-done | bytes 131104 | tf_op jit(solution)/shard_map/ppermute | solution.py:183
  65.1 1.4 %collective-permute-done.22.came = bf16[512,128]{1,0:T(8,128)(2,1)S(1)} collective-permute-done((bf16[512,128]{1,0:T(8,128)(2,1)S(1)}, bf16[512,128]{1,0:T(8,128)(2,1)S(1)}, u32[]{:S(2)}, u32[]{:S(2)}) %collective-permute-start.22) | collective-permute-done | bytes 131104 | tf_op jit(solution)/shard_map/ppermute | solution.py:183
  67.4 1.8 %collective-permute-start.25 = (bf16[512,256]{1,0:T(8,128)(2,1)S(1)}, bf16[512,256]{1,0:T(8,128)(2,1)S(1)}, u32[]{:S(2)}, u32[]{:S(2)}) collective-permute-start(bf16[512,256]{1,0:T(8,128)(2,1)S(1)} %hop.6), channel_id=1, source_target_pairs={{0,4},{4,0},{8,12},{12,8},{14,10},{10,14},{6,2},{2,6},{5,9},{9,5},... | collective-permute-start | bytes 786440 | tf_op jit(solution)/shard_map/ppermute | solution.py:183
  70.4 3.4 %collective-permute-done.25.came = bf16[512,256]{1,0:T(8,128)(2,1)S(1)} collective-permute-done((bf16[512,256]{1,0:T(8,128)(2,1)S(1)}, bf16[512,256]{1,0:T(8,128)(2,1)S(1)}, u32[]{:S(2)}, u32[]{:S(2)}) %collective-permute-start.25) | collective-permute-done | bytes 262176 | tf_op jit(solution)/shard_map/ppermute | solution.py:183
  76.0 1.4 %collective-permute-done.24.came = bf16[512,256]{1,0:T(8,128)(2,1)S(1)} collective-permute-done((bf16[512,256]{1,0:T(8,128)(2,1)S(1)}, bf16[512,256]{1,0:T(8,128)(2,1)S(1)}, u32[]{:S(2)}, u32[]{:S(2)}) %collective-permute-start.24) | collective-permute-done | bytes 262176 | tf_op jit(solution)/shard_map/ppermute | solution.py:183
  79.5 1.6 %collective-permute-done.27.came = bf16[512,256]{1,0:T(8,128)(2,1)S(1)} collective-permute-done((bf16[512,256]{1,0:T(8,128)(2,1)S(1)}, bf16[512,256]{1,0:T(8,128)(2,1)S(1)}, u32[]{:S(2)}, u32[]{:S(2)}) %collective-permute-start.27) | collective-permute-done | bytes 262176 | tf_op jit(solution)/shard_map/ppermute | solution.py:183
  82.0 1.8 %collective-permute-start.29 = (bf16[512,256]{1,0:T(8,128)(2,1)S(1)}, bf16[512,256]{1,0:T(8,128)(2,1)S(1)}, u32[]{:S(2)}, u32[]{:S(2)}) collective-permute-start(bf16[512,256]{1,0:T(8,128)(2,1)S(1)} %hop.10), channel_id=1, source_target_pairs={{0,4},{4,0},{8,12},{12,8},{14,10},{10,14},{6,2},{2,6},{5,9},{9,5},... | collective-permute-start | bytes 786440 | tf_op jit(solution)/shard_map/ppermute | solution.py:183
  83.8 2.5 %collective-permute-done.26.came = bf16[512,256]{1,0:T(8,128)(2,1)S(1)} collective-permute-done((bf16[512,256]{1,0:T(8,128)(2,1)S(1)}, bf16[512,256]{1,0:T(8,128)(2,1)S(1)}, u32[]{:S(2)}, u32[]{:S(2)}) %collective-permute-start.26) | collective-permute-done | bytes 262176 | tf_op jit(solution)/shard_map/ppermute | solution.py:183
  87.2 1.8 %collective-permute-start.28 = (bf16[512,256]{1,0:T(8,128)(2,1)S(1)}, bf16[512,256]{1,0:T(8,128)(2,1)S(1)}, u32[]{:S(2)}, u32[]{:S(2)}) collective-permute-start(bf16[512,256]{1,0:T(8,128)(2,1)S(1)} %hop.11), channel_id=1, source_target_pairs={{0,4},{4,0},{8,12},{12,8},{14,10},{10,14},{6,2},{2,6},{5,9},{9,5},... | collective-permute-start | bytes 786440 | tf_op jit(solution)/shard_map/ppermute | solution.py:183
  89.0 4.6 %collective-permute-done.28.came = bf16[512,256]{1,0:T(8,128)(2,1)S(1)} collective-permute-done((bf16[512,256]{1,0:T(8,128)(2,1)S(1)}, bf16[512,256]{1,0:T(8,128)(2,1)S(1)}, u32[]{:S(2)}, u32[]{:S(2)}) %collective-permute-start.28) | collective-permute-done | bytes 262176 | tf_op jit(solution)/shard_map/ppermute | solution.py:183
  97.0 1.4 %apply.2.refs_0_ = f32[500,512]{1,0:T(8,128)} custom-call(s32[3]{0:T(128)S(1)} %pad_add_fusion.place, f32[500,512]{1,0:T(8,128)S(1)} %bitcast.14, bf16[512,256]{1,0:T(8,128)(2,1)S(1)} %last.1.change), custom_call_target="tpu_custom_call" | custom-call | tf_op jit(solution)/shard_map/apply/pallas_call | solution.py:42
  98.4 2.6 %collective-permute-done.31.change = bf16[512,256]{1,0:T(8,128)(2,1)S(1)} collective-permute-done((bf16[512,256]{1,0:T(8,128)(2,1)S(1)}, bf16[512,256]{1,0:T(8,128)(2,1)S(1)}, u32[]{:S(2)}, u32[]{:S(2)}) %collective-permute-start.31) | collective-permute-done | bytes 262176 | tf_op jit(solution)/shard_map/ppermute | solution.py:183
  101.0 1.4 %apply.3 = f32[500,512]{1,0:T(8,128)} custom-call(s32[3]{0:T(128)S(1)} %pad_add_fusion.place, f32[500,512]{1,0:T(8,128)S(1)} %bitcast.15, bf16[512,256]{1,0:T(8,128)(2,1)S(1)} %collective-permute-done.31.change, f32[500,512]{1,0:T(8,128)} %apply.2.refs_0_), custom_call_target="tpu_custom_call", output_to_operand_aliasing={{}: (3, {})} | custom-call | tf_op jit(solution)/shard_map/apply/pallas_call | solution.py:42
  (74 shorter events, 25.1 us)
Async XLA Ops:
  0.6 11.4 %collective-permute-start.1 = (bf16[1024,1024]{1,0:T(8,128)(2,1)}, bf16[1024,1024]{1,0:T(8,128)(2,1)S(1)}, u32[]{:S(2)}, u32[]{:S(2)}) collective-permute-start(bf16[1024,1024]{1,0:T(8,128)(2,1)} %w_own.9), channel_id=1, source_target_pairs={{0,1},{1,0},{2,3},{3,2},{4,5},{5,4},{6,7},{7,6},{8,9},{9,8},{10,11... | collective-permute-start | bytes 6291464 | tf_op jit(solution)/shard_map/ppermute | solution.py:183
  3.2 2.2 %collective-permute-start = (bf16[512,256]{1,0:T(8,128)(2,1)S(1)}, bf16[512,256]{1,0:T(8,128)(2,1)S(1)}, u32[]{:S(2)}, u32[]{:S(2)}) collective-permute-start(bf16[512,256]{1,0:T(8,128)(2,1)S(1)} %get-tuple-element.37), channel_id=1, source_target_pairs={{0,1},{1,0},{2,3},{3,2},{4,5},{5,4},{6,7},{7,6},{8,9},{9,8},{10,11... | collective-permute-start | bytes 786440 | tf_op jit(solution)/shard_map/ppermute | solution.py:183
  5.3 10.3 %collective-permute-start.5 = (bf16[256,1024]{1,0:T(8,128)(2,1)S(1)}, bf16[256,1024]{1,0:T(8,128)(2,1)S(1)}, u32[]{:S(2)}, u32[]{:S(2)}) collective-permute-start(bf16[256,1024]{1,0:T(8,128)(2,1)S(1)} %get-tuple-element.39.rows), channel_id=1, source_target_pairs={{0,4},{4,0},{8,12},{12,8},{14,10},{10,14},{6,2},{2,6},{5,9},{9,5},... | collective-permute-start | bytes 1572872 | tf_op jit(solution)/shard_map/ppermute | solution.py:183
  8.3 14.7 %collective-permute-start.4 = (bf16[1024,256]{1,0:T(8,128)(2,1)S(1)}, bf16[1024,256]{1,0:T(8,128)(2,1)S(1)}, u32[]{:S(2)}, u32[]{:S(2)}) collective-permute-start(bf16[1024,256]{1,0:T(8,128)(2,1)S(1)} %constant_dynamic-update-slice_fusion.refs_0_.refs_2_), channel_id=1, source_target_pairs={{0,4},{4,0},{8,12},{12,8},{14,10},{10,14},{6,2},{2,6},{5,9},{9,5},... | collective-permute-start | bytes 1572872 | tf_op jit(solution)/shard_map/ppermute | solution.py:183
  8.4 3.6 %collective-permute-start.2 = (bf16[1,1024]{1,0:T(2,128)(2,1)S(1)}, bf16[1,1024]{1,0:T(2,128)(2,1)S(1)}, u32[]{:S(2)}, u32[]{:S(2)}) collective-permute-start(bf16[1,1024]{1,0:T(2,128)(2,1)S(1)} %broadcast_in_dim.7.p_own), channel_id=1, source_target_pairs={{0,1},{1,0},{2,3},{3,2},{4,5},{5,4},{6,7},{7,6},{8,9},{9,8},{10,11... | collective-permute-start | bytes 6152 | tf_op jit(solution)/shard_map/ppermute | solution.py:183
  15.6 10.4 %collective-permute-start.9 = (bf16[256,1024]{1,0:T(8,128)(2,1)S(1)}, bf16[256,1024]{1,0:T(8,128)(2,1)S(1)}, u32[]{:S(2)}, u32[]{:S(2)}) collective-permute-start(bf16[256,1024]{1,0:T(8,128)(2,1)S(1)} %collective-permute-done.5.rows), channel_id=1, source_target_pairs={{4,8},{8,4},{12,14},{14,12},{10,6},{6,10},{2,0},{0,2},{1,5},{5,1},... | collective-permute-start | bytes 1572872 | tf_op jit(solution)/shard_map/ppermute | solution.py:183
  23.0 12.4 %collective-permute-start.8 = (bf16[1024,256]{1,0:T(8,128)(2,1)S(1)}, bf16[1024,256]{1,0:T(8,128)(2,1)S(1)}, u32[]{:S(2)}, u32[]{:S(2)}) collective-permute-start(bf16[1024,256]{1,0:T(8,128)(2,1)S(1)} %collective-permute-done.4.refs_4_), channel_id=1, source_target_pairs={{4,8},{8,4},{12,14},{14,12},{10,6},{6,10},{2,0},{0,2},{1,5},{5,1},... | collective-permute-start | bytes 1572872 | tf_op jit(solution)/shard_map/ppermute | solution.py:183
  25.2 14.7 %collective-permute-start.7 = (bf16[256,1024]{1,0:T(8,128)(2,1)S(1)}, bf16[256,1024]{1,0:T(8,128)(2,1)S(1)}, u32[]{:S(2)}, u32[]{:S(2)}) collective-permute-start(bf16[256,1024]{1,0:T(8,128)(2,1)S(1)} %get-tuple-element.44.refs_5_), channel_id=1, source_target_pairs={{0,1},{1,0},{2,3},{3,2},{4,5},{5,4},{6,7},{7,6},{8,9},{9,8},{10,11... | collective-permute-start | bytes 1572872 | tf_op jit(solution)/shard_map/ppermute | solution.py:183
  26.0 15.5 %collective-permute-start.13 = (bf16[256,1024]{1,0:T(8,128)(2,1)S(1)}, bf16[256,1024]{1,0:T(8,128)(2,1)S(1)}, u32[]{:S(2)}, u32[]{:S(2)}) collective-permute-start(bf16[256,1024]{1,0:T(8,128)(2,1)S(1)} %collective-permute-done.9.rows), channel_id=1, source_target_pairs={{0,4},{4,0},{8,12},{12,8},{14,10},{10,14},{6,2},{2,6},{5,9},{9,5},... | collective-permute-start | bytes 1572872 | tf_op jit(solution)/shard_map/ppermute | solution.py:183
  35.4 12.0 %collective-permute-start.12 = (bf16[1024,256]{1,0:T(8,128)(2,1)S(1)}, bf16[1024,256]{1,0:T(8,128)(2,1)S(1)}, u32[]{:S(2)}, u32[]{:S(2)}) collective-permute-start(bf16[1024,256]{1,0:T(8,128)(2,1)S(1)} %collective-permute-done.8.refs_1_), channel_id=1, source_target_pairs={{0,4},{4,0},{8,12},{12,8},{14,10},{10,14},{6,2},{2,6},{5,9},{9,5},... | collective-permute-start | bytes 1572872 | tf_op jit(solution)/shard_map/ppermute | solution.py:183
  37.8 1.6 %collective-permute-start.6 = (bf16[512,256]{1,0:T(8,128)(2,1)S(1)}, bf16[512,256]{1,0:T(8,128)(2,1)S(1)}, u32[]{:S(2)}, u32[]{:S(2)}) collective-permute-start(bf16[512,256]{1,0:T(8,128)(2,1)S(1)} %slice.21), channel_id=1, source_target_pairs={{0,1},{1,0},{2,3},{3,2},{4,5},{5,4},{6,7},{7,6},{8,9},{9,8},{10,11... | collective-permute-start | bytes 786440 | tf_op jit(solution)/shard_map/ppermute | solution.py:183
  37.9 1.9 %collective-permute-start.3 = (bf16[128,1024]{1,0:T(8,128)(2,1)S(1)}, bf16[128,1024]{1,0:T(8,128)(2,1)S(1)}, u32[]{:S(2)}, u32[]{:S(2)}) collective-permute-start(bf16[128,1024]{1,0:T(8,128)(2,1)S(1)} %get-tuple-element.42.refs_1_), channel_id=1, source_target_pairs={{0,1},{1,0},{2,3},{3,2},{4,5},{5,4},{6,7},{7,6},{8,9},{9,8},{10,11... | collective-permute-start | bytes 786440 | tf_op jit(solution)/shard_map/ppermute | solution.py:183
  39.4 2.0 %collective-permute-start.14 = (bf16[128,512]{1,0:T(8,128)(2,1)S(1)}, bf16[128,512]{1,0:T(8,128)(2,1)S(1)}, u32[]{:S(2)}, u32[]{:S(2)}) collective-permute-start(bf16[128,512]{1,0:T(8,128)(2,1)S(1)} %get-tuple-element.49.mine), channel_id=1, source_target_pairs={{0,1},{1,0},{2,3},{3,2},{4,5},{5,4},{6,7},{7,6},{8,9},{9,8},{10,11... | collective-permute-start | bytes 393224 | tf_op jit(solution)/shard_map/ppermute | solution.py:183
  39.8 14.6 %collective-permute-start.11 = (bf16[256,1024]{1,0:T(8,128)(2,1)S(1)}, bf16[256,1024]{1,0:T(8,128)(2,1)S(1)}, u32[]{:S(2)}, u32[]{:S(2)}) collective-permute-start(bf16[256,1024]{1,0:T(8,128)(2,1)S(1)} %get-tuple-element.47.refs_2_), channel_id=1, source_target_pairs={{0,1},{1,0},{2,3},{3,2},{4,5},{5,4},{6,7},{7,6},{8,9},{9,8},{10,11... | collective-permute-start | bytes 1572872 | tf_op jit(solution)/shard_map/ppermute | solution.py:183
  41.5 8.0 %collective-permute-start.18 = (bf16[128,1024]{1,0:T(8,128)(2,1)S(1)}, bf16[128,1024]{1,0:T(8,128)(2,1)S(1)}, u32[]{:S(2)}, u32[]{:S(2)}) collective-permute-start(bf16[128,1024]{1,0:T(8,128)(2,1)S(1)} %slice.25), channel_id=1, source_target_pairs={{4,8},{8,4},{12,14},{14,12},{10,6},{6,10},{2,0},{0,2},{1,5},{5,1},... | collective-permute-start | bytes 786440 | tf_op jit(solution)/shard_map/ppermute | solution.py:183
  47.3 7.2 %collective-permute-start.16 = (bf16[256,1024]{1,0:T(8,128)(2,1)S(1)}, bf16[256,1024]{1,0:T(8,128)(2,1)S(1)}, u32[]{:S(2)}, u32[]{:S(2)}) collective-permute-start(bf16[256,1024]{1,0:T(8,128)(2,1)S(1)} %get-tuple-element.51.refs_6_), channel_id=1, source_target_pairs={{0,1},{1,0},{2,3},{3,2},{4,5},{5,4},{6,7},{7,6},{8,9},{9,8},{10,11... | collective-permute-start | bytes 1572872 | tf_op jit(solution)/shard_map/ppermute | solution.py:183
  47.4 6.4 %collective-permute-start.17 = (bf16[1024,128]{1,0:T(8,128)(2,1)S(1)}, bf16[1024,128]{1,0:T(8,128)(2,1)S(1)}, u32[]{:S(2)}, u32[]{:S(2)}) collective-permute-start(bf16[1024,128]{1,0:T(8,128)(2,1)S(1)} %slice.24), channel_id=1, source_target_pairs={{4,8},{8,4},{12,14},{14,12},{10,6},{6,10},{2,0},{0,2},{1,5},{5,1},... | collective-permute-start | bytes 786440 | tf_op jit(solution)/shard_map/ppermute | solution.py:183
  48.1 5.8 %collective-permute-start.10 = (bf16[512,256]{1,0:T(8,128)(2,1)S(1)}, bf16[512,256]{1,0:T(8,128)(2,1)S(1)}, u32[]{:S(2)}, u32[]{:S(2)}) collective-permute-start(bf16[512,256]{1,0:T(8,128)(2,1)S(1)} %slice.22), channel_id=1, source_target_pairs={{0,1},{1,0},{2,3},{3,2},{4,5},{5,4},{6,7},{7,6},{8,9},{9,8},{10,11... | collective-permute-start | bytes 786440 | tf_op jit(solution)/shard_map/ppermute | solution.py:183
  49.5 4.9 %collective-permute-start.15 = (bf16[512,256]{1,0:T(8,128)(2,1)S(1)}, bf16[512,256]{1,0:T(8,128)(2,1)S(1)}, u32[]{:S(2)}, u32[]{:S(2)}) collective-permute-start(bf16[512,256]{1,0:T(8,128)(2,1)S(1)} %slice.23), channel_id=1, source_target_pairs={{0,1},{1,0},{2,3},{3,2},{4,5},{5,4},{6,7},{7,6},{8,9},{9,8},{10,11... | collective-permute-start | bytes 786440 | tf_op jit(solution)/shard_map/ppermute | solution.py:183
  53.9 2.4 %collective-permute-start.20 = (bf16[128,1024]{1,0:T(8,128)(2,1)S(1)}, bf16[128,1024]{1,0:T(8,128)(2,1)S(1)}, u32[]{:S(2)}, u32[]{:S(2)}) collective-permute-start(bf16[128,1024]{1,0:T(8,128)(2,1)S(1)} %get-tuple-element.54.refs_1_), channel_id=1, source_target_pairs={{0,1},{1,0},{2,3},{3,2},{4,5},{5,4},{6,7},{7,6},{8,9},{9,8},{10,11... | collective-permute-start | bytes 786440 | tf_op jit(solution)/shard_map/ppermute | solution.py:183
  53.9 2.4 %collective-permute-start.19 = (bf16[512,128]{1,0:T(8,128)(2,1)S(1)}, bf16[512,128]{1,0:T(8,128)(2,1)S(1)}, u32[]{:S(2)}, u32[]{:S(2)}) collective-permute-start(bf16[512,128]{1,0:T(8,128)(2,1)S(1)} %slice.28), channel_id=1, source_target_pairs={{0,1},{1,0},{2,3},{3,2},{4,5},{5,4},{6,7},{7,6},{8,9},{9,8},{10,11... | collective-permute-start | bytes 393224 | tf_op jit(solution)/shard_map/ppermute | solution.py:183
  57.3 2.0 %collective-permute-start.21 = (bf16[512,512]{1,0:T(8,128)(2,1)S(1)}, bf16[512,512]{1,0:T(8,128)(2,1)S(1)}, u32[]{:S(2)}, u32[]{:S(2)}) collective-permute-start(bf16[512,512]{1,0:T(8,128)(2,1)S(1)} %get-tuple-element.56.sent), channel_id=1, source_target_pairs={{0,1},{1,0},{2,3},{3,2},{4,5},{5,4},{6,7},{7,6},{8,9},{9,8},{10,11... | collective-permute-start | bytes 1572872 | tf_op jit(solution)/shard_map/ppermute | solution.py:183
  60.1 5.0 %collective-permute-start.23 = (bf16[512,128]{1,0:T(8,128)(2,1)S(1)}, bf16[512,128]{1,0:T(8,128)(2,1)S(1)}, u32[]{:S(2)}, u32[]{:S(2)}) collective-permute-start(bf16[512,128]{1,0:T(8,128)(2,1)S(1)} %far.3), channel_id=1, source_target_pairs={{4,8},{8,4},{12,14},{14,12},{10,6},{6,10},{2,0},{0,2},{1,5},{5,1},... | collective-permute-start | bytes 393224 | tf_op jit(solution)/shard_map/ppermute | solution.py:183
  60.9 5.6 %collective-permute-start.22 = (bf16[512,128]{1,0:T(8,128)(2,1)S(1)}, bf16[512,128]{1,0:T(8,128)(2,1)S(1)}, u32[]{:S(2)}, u32[]{:S(2)}) collective-permute-start(bf16[512,128]{1,0:T(8,128)(2,1)S(1)} %far.2), channel_id=1, source_target_pairs={{4,8},{8,4},{12,14},{14,12},{10,6},{6,10},{2,0},{0,2},{1,5},{5,1},... | collective-permute-start | bytes 393224 | tf_op jit(solution)/shard_map/ppermute | solution.py:183
  67.4 6.4 %collective-permute-start.25 = (bf16[512,256]{1,0:T(8,128)(2,1)S(1)}, bf16[512,256]{1,0:T(8,128)(2,1)S(1)}, u32[]{:S(2)}, u32[]{:S(2)}) collective-permute-start(bf16[512,256]{1,0:T(8,128)(2,1)S(1)} %hop.6), channel_id=1, source_target_pairs={{0,4},{4,0},{8,12},{12,8},{14,10},{10,14},{6,2},{2,6},{5,9},{9,5},... | collective-permute-start | bytes 786440 | tf_op jit(solution)/shard_map/ppermute | solution.py:183
  70.1 7.4 %collective-permute-start.24 = (bf16[512,256]{1,0:T(8,128)(2,1)S(1)}, bf16[512,256]{1,0:T(8,128)(2,1)S(1)}, u32[]{:S(2)}, u32[]{:S(2)}) collective-permute-start(bf16[512,256]{1,0:T(8,128)(2,1)S(1)} %hop.7), channel_id=1, source_target_pairs={{0,4},{4,0},{8,12},{12,8},{14,10},{10,14},{6,2},{2,6},{5,9},{9,5},... | collective-permute-start | bytes 786440 | tf_op jit(solution)/shard_map/ppermute | solution.py:183
  74.7 6.4 %collective-permute-start.27 = (bf16[512,256]{1,0:T(8,128)(2,1)S(1)}, bf16[512,256]{1,0:T(8,128)(2,1)S(1)}, u32[]{:S(2)}, u32[]{:S(2)}) collective-permute-start(bf16[512,256]{1,0:T(8,128)(2,1)S(1)} %hop.8), channel_id=1, source_target_pairs={{4,8},{8,4},{12,14},{14,12},{10,6},{6,10},{2,0},{0,2},{1,5},{5,1},... | collective-permute-start | bytes 786440 | tf_op jit(solution)/shard_map/ppermute | solution.py:183
  78.3 8.0 %collective-permute-start.26 = (bf16[512,256]{1,0:T(8,128)(2,1)S(1)}, bf16[512,256]{1,0:T(8,128)(2,1)S(1)}, u32[]{:S(2)}, u32[]{:S(2)}) collective-permute-start(bf16[512,256]{1,0:T(8,128)(2,1)S(1)} %hop.9), channel_id=1, source_target_pairs={{4,8},{8,4},{12,14},{14,12},{10,6},{6,10},{2,0},{0,2},{1,5},{5,1},... | collective-permute-start | bytes 786440 | tf_op jit(solution)/shard_map/ppermute | solution.py:183
  82.0 7.0 %collective-permute-start.29 = (bf16[512,256]{1,0:T(8,128)(2,1)S(1)}, bf16[512,256]{1,0:T(8,128)(2,1)S(1)}, u32[]{:S(2)}, u32[]{:S(2)}) collective-permute-start(bf16[512,256]{1,0:T(8,128)(2,1)S(1)} %hop.10), channel_id=1, source_target_pairs={{0,4},{4,0},{8,12},{12,8},{14,10},{10,14},{6,2},{2,6},{5,9},{9,5},... | collective-permute-start | bytes 786440 | tf_op jit(solution)/shard_map/ppermute | solution.py:183
  87.2 6.4 %collective-permute-start.28 = (bf16[512,256]{1,0:T(8,128)(2,1)S(1)}, bf16[512,256]{1,0:T(8,128)(2,1)S(1)}, u32[]{:S(2)}, u32[]{:S(2)}) collective-permute-start(bf16[512,256]{1,0:T(8,128)(2,1)S(1)} %hop.11), channel_id=1, source_target_pairs={{0,4},{4,0},{8,12},{12,8},{14,10},{10,14},{6,2},{2,6},{5,9},{9,5},... | collective-permute-start | bytes 786440 | tf_op jit(solution)/shard_map/ppermute | solution.py:183
  89.0 4.6 %collective-permute-start.30 = (bf16[512,256]{1,0:T(8,128)(2,1)S(1)}, bf16[512,256]{1,0:T(8,128)(2,1)S(1)}, u32[]{:S(2)}, u32[]{:S(2)}) collective-permute-start(bf16[512,256]{1,0:T(8,128)(2,1)S(1)} %collective-permute-done.29), channel_id=1, source_target_pairs={{0,1},{1,0},{2,3},{3,2},{4,5},{5,4},{6,7},{7,6},{8,9},{9,8},{10,11... | collective-permute-start | bytes 786440 | tf_op jit(solution)/shard_map/ppermute | solution.py:183
  94.5 6.4 %collective-permute-start.31 = (bf16[512,256]{1,0:T(8,128)(2,1)S(1)}, bf16[512,256]{1,0:T(8,128)(2,1)S(1)}, u32[]{:S(2)}, u32[]{:S(2)}) collective-permute-start(bf16[512,256]{1,0:T(8,128)(2,1)S(1)} %last.1.change), channel_id=1, source_target_pairs={{0,2},{2,0},{1,3},{3,1},{4,6},{6,4},{5,7},{7,5},{8,10},{10,8},{9,1... | collective-permute-start | bytes 786440 | tf_op jit(solution)/shard_map/ppermute | solution.py:183
  (5 other events, 35.9 us)

commit v9 on v8

--- a/solution.py
+++ b/solution.py
@@ -146,24 +146,34 @@
     sent[...] = total.astype(BF16)
 
 
-def far_kernel(place, sent, feats, out):
-    out[...] = dot_nt(sent[...], feats[...]).astype(BF16)
-
-
-def hop_kernel(place, sent, feats, came, out):
-    total = dot_nt(sent[...], feats[...])
-    size = came.shape[1]
-    out[:, :size] = (total[:, :size] + came[...].astype(F32)).astype(BF16)
+def far_kernel(place, sent, sent_other, feats, out):
+    size = sent.shape[0]
+    for i, update in enumerate((sent, sent_other)):
+        out[i * size:(i + 1) * size] = dot_nt(update[...], feats[...]).astype(BF16)
+
+
+def change_kernel(n_feats, place, *refs):
+    count = (len(refs) - n_feats) // 2
+    feats, updates, outs = refs[:n_feats], refs[n_feats:n_feats + count], refs[n_feats + count:]
+    rows = feats[0][...] if n_feats == 1 else jnp.concatenate([f[...] for f in feats], axis=0)
+    for update, out in zip(updates, outs):
+        out[...] = dot_nt(update[...], rows)
+
+
+def hop_kernel(half, place, change, came, out):
+    size, there = came.shape[1], slice(half * out.shape[0], (half + 1) * out.shape[0])
+    there = there if came.shape[0] > out.shape[0] else slice(None)
+    out[:, :size] = (change[:, :size] + came[there].astype(F32)).astype(BF16)
     if size < out.shape[1]:
-        out[:, size:] = total[:, size:].astype(BF16)
-
-
-def last_kernel(place, sent, mine, theirs, came, given, out):
-    part = mine.shape[0]
-    total = dot_nt(sent[...], jnp.concatenate([mine[...], theirs[...]], axis=0)) + came[...].astype(F32)
+        out[:, size:] = change[:, size:].astype(BF16)
+
+
+def last_kernel(place, change, came, given, out):
+    part = out.shape[1] // 2
     for i in (0, 1):
         at, there = slice(i * part, (i + 1) * part), slice((1 - i) * part, (2 - i) * part)
-        out[:, at] = (total[:, at] + given[:, there].astype(F32)).astype(BF16)
+        total = change[:, at] + came[:, at].astype(F32) + given[:, there].astype(F32)
+        out[:, at] = total.astype(BF16)
 
 
 def apply_kernel(which, place, predictions, change, *refs):
@@ -264,20 +274,29 @@
         (begun, r4, q4, theirs(r4), C(q4)), "update", 14,
     )
 
-    piece, whole = like((padded, part)), like((padded, 2 * part))
-    far = lambda u: call(far_kernel, piece, place, (u, f4), "far", 6)
-    hop = lambda u, feats, came: call(hop_kernel, whole, place, (u, feats, came), "hop", 6)
-    first = far(sent)
-    sent_other, first = after((C(sent), first), first)
-    first, second = T(first), T(far(sent_other))
-    (second,) = after((second,), first)
-    for way, feats in ((S, f3), (T, f2), (S, f1)):
-        second_sum = hop(sent_other, feats, second)
+    whole, wide = like((padded, 2 * part)), like((padded, 2 * part), F32)
+    sent_other = C(sent)
+
+    def changes(feats, *updates):
+        return call(
+            functools.partial(change_kernel, len(feats)), (wide,) * len(updates), place,
+            (*feats, *updates), "change", 8,
+        )
+
+    hop = lambda half, own, came: call(functools.partial(hop_kernel, half), whole, place, (own, came), "hop", 4)
+    first = T(call(far_kernel, like((2 * padded, part)), place, (sent, sent_other, f4), "far", 6))
+    ahead = changes((f3,), sent, sent_other)
+    (first,) = after((first,), *ahead)
+    second = first
+    for way, feats in ((S, (f2,)), (T, (f1,)), (S, (f0, f0_other))):
+        second_sum = hop(1, ahead[1], second)
         (first,) = after((first,), second_sum)
-        first_sum = hop(sent, feats, first)
+        first_sum = hop(0, ahead[0], first)
         second, first = way(second_sum), way(first_sum)
-        (second,) = after((second,), first_sum)
-    own = call(last_kernel, whole, place, (sent, f0, f0_other, first, C(second)), "last", 6)
+        updates = after((sent, sent_other), first_sum)
+        ahead = changes(feats, *updates[:1 if len(feats) == 2 else 2])
+        (second,) = after((second,), first_sum, *ahead)
+    own = call(last_kernel, whole, place, (ahead[0], first, C(second)), "last", 4)
     new = None
     for i in (0, 1):
         change = swap(own, "blocks", [(0, 1)]) if i else own

time: 103 us -> 102 us (level)
  starting transfers between devices: 29 us -> 27.5 us
  Pallas kernels: 37.1 us -> 38.4 us
    ppermute x32 -> x31, starting transfers between devices: 29 us -> 27.5 us  [swap(): lax.ppermute(x, axes, [p for a, b in pairs for p in ((a, b), (b, a))])]
    pallas_call x21 -> x24, Pallas kernels: 37.1 us -> 38.4 us  [call(): pl.pallas_call(kernel, out_shape=out_shapes, in_specs=[pl.BlockSpec(memor...]
    ppermute x32 -> x31, waiting for transfers between devices: 31.4 us -> 31.3 us  [swap(): lax.ppermute(x, axes, [p for a, b in pairs for p in ((a, b), (b, a))])]
  transfers between devices with their start and end apart: 32 -> 31, of which waited for: 16 -> 15; matrix products, arithmetic and copies ran while one was open for 1% -> 1% of each run, Pallas kernels for 31% -> 33%
where the time goes in v9:
time: 102 us
  Pallas kernels  38.4 us (38%)
  waiting for transfers between devices  31.3 us (31%)
  starting transfers between devices  27.5 us (27%)
  local copies, waits for them, and re-layouts  2.56 us (3%)
  other arithmetic  1.24 us (1%)
  between operations  1.18 us (1%)
    pallas_call x24, Pallas kernels, call(): pl.pallas_call(kernel, out_shape=out_shapes, in_specs=[pl.BlockSpec(memor...  38.4 us
    ppermute x31, waiting for transfers between devices, swap(): lax.ppermute(x, axes, [p for a, b in pairs for p in ((a, b), (b, a))])  31.3 us
    ppermute x31, starting transfers between devices, swap(): lax.ppermute(x, axes, [p for a, b in pairs for p in ((a, b), (b, a))])  27.5 us
    unnamed x11, local copies, waits for them, and re-layouts  2.43 us
  transfers between devices with their start and end apart: 31, of which 15 were waited for; matrix products, arithmetic and copies ran while one was open for 1% of the time, Pallas kernels for 33%

profile of v9, /device:TPU:0, one launch (start us, length us, event | category | flops | bytes accessed | tf_op | source)
XLA Modules:
  0.0 102.2 jit_solution(15608332753964971490)
XLA Ops:
  1.2 1.9 %prepare.1 = (bf16[256,1024]{1,0:T(8,128)(2,1)S(1)}, bf16[512,256]{1,0:T(8,128)(2,1)S(1)}, bf16[512,256]{1,0:T(8,128)(2,1)S(1)}) custom-call(s32[3]{0:T(128)S(1)} %pad_add_fusion.place, bf16[512,1024]{1,0:T(8,128)(2,1)} %inputs.1, s32[1,512]{1,0:T(1,128)} %bitcast.18, f32[500,512]{1,0:T(8,128)} %bitcast.13), custom_call_target="tpu_custom_call" | custom-call | tf_op jit(solution)/shard_map/prepare/pallas_call | solution.py:42
  3.3 2.0 %collective-permute-done = bf16[512,256]{1,0:T(8,128)(2,1)S(1)} collective-permute-done((bf16[512,256]{1,0:T(8,128)(2,1)S(1)}, bf16[512,256]{1,0:T(8,128)(2,1)S(1)}, u32[]{:S(2)}, u32[]{:S(2)}) %collective-permute-start) | collective-permute-done | bytes 262176 | tf_op jit(solution)/shard_map/ppermute | solution.py:193
  5.3 2.9 %collective-permute-start.5 = (bf16[256,1024]{1,0:T(8,128)(2,1)S(1)}, bf16[256,1024]{1,0:T(8,128)(2,1)S(1)}, u32[]{:S(2)}, u32[]{:S(2)}) collective-permute-start(bf16[256,1024]{1,0:T(8,128)(2,1)S(1)} %get-tuple-element.48.rows), channel_id=1, source_target_pairs={{0,4},{4,0},{8,12},{12,8},{14,10},{10,14},{6,2},{2,6},{5,9},{9,5},... | collective-permute-start | bytes 1572872 | tf_op jit(solution)/shard_map/ppermute | solution.py:193
  8.5 2.2 %copy-done.2 = f32[1,512,2048]{2,1,0:T(8,128)S(1)} copy-done((f32[1,512,2048]{2,1,0:T(8,128)S(1)}, f32[1,512,2048]{2,1,0:T(8,128)}, u32[]{:S(2)}) %copy-start.2) | copy-done | bytes 4194328
  10.7 1.4 %split.1 = (bf16[512,2048]{1,0:T(8,128)(2,1)S(1)}, bf16[512,2048]{1,0:T(8,128)(2,1)S(1)}) custom-call(s32[3]{0:T(128)S(1)} %pad_add_fusion.place, f32[512,2048]{1,0:T(8,128)S(1)} %bitcast.16), custom_call_target="tpu_custom_call" | custom-call | tf_op jit(solution)/shard_map/split/pallas_call | solution.py:42
  12.2 3.3 %block.5 = (bf16[128,1024]{1,0:T(8,128)(2,1)S(1)}, bf16[128,512]{1,0:T(8,128)(2,1)S(1)}) custom-call(s32[3]{0:T(128)S(1)} %pad_add_fusion.place, bf16[256,1024]{1,0:T(8,128)(2,1)S(1)} %get-tuple-element.48.rows, bf16[1024,1024]{1,0:T(8,128)(2,1)S(1)} %copy-done, bf16[1024,1024]{1,0:T(8,128)(2,1)S(1)} %collective-permute-done.1.w_other, ...), custom_call_target="tpu_custom_call" | custom-call | tf_op jit(solution)/shard_map/block/pallas_call | solution.py:42
  15.6 2.0 %collective-permute-start.9 = (bf16[256,1024]{1,0:T(8,128)(2,1)S(1)}, bf16[256,1024]{1,0:T(8,128)(2,1)S(1)}, u32[]{:S(2)}, u32[]{:S(2)}) collective-permute-start(bf16[256,1024]{1,0:T(8,128)(2,1)S(1)} %collective-permute-done.5.rows), channel_id=1, source_target_pairs={{4,8},{8,4},{12,14},{14,12},{10,6},{6,10},{2,0},{0,2},{1,5},{5,1},... | collective-permute-start | bytes 1572872 | tf_op jit(solution)/shard_map/ppermute | solution.py:193
  17.6 4.1 %block.6 = (bf16[256,1024]{1,0:T(8,128)(2,1)S(1)}, bf16[256,512]{1,0:T(8,128)(2,1)S(1)}) custom-call(s32[3]{0:T(128)S(1)} %pad_add_fusion.place, bf16[256,1024]{1,0:T(8,128)(2,1)S(1)} %collective-permute-done.5.rows, bf16[1024,1024]{1,0:T(8,128)(2,1)S(1)} %copy-done, bf16[1024,1024]{1,0:T(8,128)(2,1)S(1)} %collective-permute-done.1.w_other, ...), custom_call_target="tpu_custom_call" | custom-call | tf_op jit(solution)/shard_map/block/pallas_call | solution.py:42
  21.7 1.3 %collective-permute-done.4.refs_4_ = bf16[1024,256]{1,0:T(8,128)(2,1)S(1)} collective-permute-done((bf16[1024,256]{1,0:T(8,128)(2,1)S(1)}, bf16[1024,256]{1,0:T(8,128)(2,1)S(1)}, u32[]{:S(2)}, u32[]{:S(2)}) %collective-permute-start.4) | collective-permute-done | bytes 524320 | tf_op jit(solution)/shard_map/ppermute | solution.py:193
  23.0 2.2 %collective-permute-start.8 = (bf16[1024,256]{1,0:T(8,128)(2,1)S(1)}, bf16[1024,256]{1,0:T(8,128)(2,1)S(1)}, u32[]{:S(2)}, u32[]{:S(2)}) collective-permute-start(bf16[1024,256]{1,0:T(8,128)(2,1)S(1)} %collective-permute-done.4.refs_4_), channel_id=1, source_target_pairs={{4,8},{8,4},{12,14},{14,12},{10,6},{6,10},{2,0},{0,2},{1,5},{5,1},... | collective-permute-start | bytes 1572872 | tf_op jit(solution)/shard_map/ppermute | solution.py:193
  26.0 1.8 %collective-permute-start.13 = (bf16[256,1024]{1,0:T(8,128)(2,1)S(1)}, bf16[256,1024]{1,0:T(8,128)(2,1)S(1)}, u32[]{:S(2)}, u32[]{:S(2)}) collective-permute-start(bf16[256,1024]{1,0:T(8,128)(2,1)S(1)} %collective-permute-done.9.rows), channel_id=1, source_target_pairs={{0,4},{4,0},{8,12},{12,8},{14,10},{10,14},{6,2},{2,6},{5,9},{9,5},... | collective-permute-start | bytes 1572872 | tf_op jit(solution)/shard_map/ppermute | solution.py:193
  27.8 4.1 %block.7 = (bf16[256,1024]{1,0:T(8,128)(2,1)S(1)}, bf16[256,512]{1,0:T(8,128)(2,1)S(1)}) custom-call(s32[3]{0:T(128)S(1)} %pad_add_fusion.place, bf16[256,1024]{1,0:T(8,128)(2,1)S(1)} %collective-permute-done.9.rows, bf16[1024,1024]{1,0:T(8,128)(2,1)S(1)} %copy-done, bf16[1024,1024]{1,0:T(8,128)(2,1)S(1)} %collective-permute-done.1.w_other, ...), custom_call_target="tpu_custom_call" | custom-call | tf_op jit(solution)/shard_map/block/pallas_call | solution.py:42
  31.9 3.5 %collective-permute-done.8.refs_1_ = bf16[1024,256]{1,0:T(8,128)(2,1)S(1)} collective-permute-done((bf16[1024,256]{1,0:T(8,128)(2,1)S(1)}, bf16[1024,256]{1,0:T(8,128)(2,1)S(1)}, u32[]{:S(2)}, u32[]{:S(2)}) %collective-permute-start.8) | collective-permute-done | bytes 524320 | tf_op jit(solution)/shard_map/ppermute | solution.py:193
  35.4 2.4 %collective-permute-start.12 = (bf16[1024,256]{1,0:T(8,128)(2,1)S(1)}, bf16[1024,256]{1,0:T(8,128)(2,1)S(1)}, u32[]{:S(2)}, u32[]{:S(2)}) collective-permute-start(bf16[1024,256]{1,0:T(8,128)(2,1)S(1)} %collective-permute-done.8.refs_1_), channel_id=1, source_target_pairs={{0,4},{4,0},{8,12},{12,8},{14,10},{10,14},{6,2},{2,6},{5,9},{9,5},... | collective-permute-start | bytes 1572872 | tf_op jit(solution)/shard_map/ppermute | solution.py:193
  40.0 1.5 %begin.2.refs_0_ = f32[512,512]{1,0:T(8,128)S(1)} custom-call(s32[3]{0:T(128)S(1)} %pad_add_fusion.place, bf16[1024,256]{1,0:T(8,128)(2,1)S(1)} %constant_dynamic-update-slice_fusion.refs_0_.refs_2_, bf16[128,1024]{1,0:T(8,128)(2,1)S(1)} %get-tuple-element.51.refs_1_, bf16[1024,256]{1,0:T(8,128)(2,1)S(1)} %constant_dynamic-update-slice_fusion.refs_0_.refs_2_, ...), custom_call_target="tpu_custom_call" | custom-call | tf_op jit(solution)/shard_map/begin/pallas_call | solution.py:42
  41.5 1.5 %collective-permute-start.18 = (bf16[128,1024]{1,0:T(8,128)(2,1)S(1)}, bf16[128,1024]{1,0:T(8,128)(2,1)S(1)}, u32[]{:S(2)}, u32[]{:S(2)}) collective-permute-start(bf16[128,1024]{1,0:T(8,128)(2,1)S(1)} %slice.25), channel_id=1, source_target_pairs={{4,8},{8,4},{12,14},{14,12},{10,6},{6,10},{2,0},{0,2},{1,5},{5,1},... | collective-permute-start | bytes 786440 | tf_op jit(solution)/shard_map/ppermute | solution.py:193
  43.1 4.2 %block.8 = (bf16[256,1024]{1,0:T(8,128)(2,1)S(1)}, bf16[256,512]{1,0:T(8,128)(2,1)S(1)}) custom-call(s32[3]{0:T(128)S(1)} %pad_add_fusion.place, bf16[256,1024]{1,0:T(8,128)(2,1)S(1)} %collective-permute-done.13.rows, bf16[1024,1024]{1,0:T(8,128)(2,1)S(1)} %copy-done, bf16[1024,1024]{1,0:T(8,128)(2,1)S(1)} %collective-permute-done.1.w_other, ...), custom_call_target="tpu_custom_call" | custom-call | tf_op jit(solution)/shard_map/block/pallas_call | solution.py:42
  48.1 1.4 %collective-permute-start.10 = (bf16[512,256]{1,0:T(8,128)(2,1)S(1)}, bf16[512,256]{1,0:T(8,128)(2,1)S(1)}, u32[]{:S(2)}, u32[]{:S(2)}) collective-permute-start(bf16[512,256]{1,0:T(8,128)(2,1)S(1)} %slice.22), channel_id=1, source_target_pairs={{0,1},{1,0},{2,3},{3,2},{4,5},{5,4},{6,7},{7,6},{8,9},{9,8},{10,11... | collective-permute-start | bytes 786440 | tf_op jit(solution)/shard_map/ppermute | solution.py:193
  49.6 3.3 %block.9 = (bf16[128,1024]{1,0:T(8,128)(2,1)S(1)}, bf16[128,512]{1,0:T(8,128)(2,1)S(1)}) custom-call(s32[3]{0:T(128)S(1)} %pad_add_fusion.place, bf16[128,1024]{1,0:T(8,128)(2,1)S(1)} %collective-permute-done.18.rows, bf16[1024,1024]{1,0:T(8,128)(2,1)S(1)} %copy-done, bf16[1024,1024]{1,0:T(8,128)(2,1)S(1)} %collective-permute-done.1.w_other, ...), custom_call_target="tpu_custom_call" | custom-call | tf_op jit(solution)/shard_map/block/pallas_call | solution.py:42
  54.5 1.8 %begin.3.begun = f32[512,512]{1,0:T(8,128)S(1)} custom-call(s32[3]{0:T(128)S(1)} %pad_add_fusion.place, f32[512,512]{1,0:T(8,128)S(1)} %begin.2.refs_0_, bf16[1024,256]{1,0:T(8,128)(2,1)S(1)} %collective-permute-done.8.refs_1_, bf16[256,1024]{1,0:T(8,128)(2,1)S(1)} %get-tuple-element.56.refs_2_, bf16[512,256]{1,0:T(8,128)(2,1)S(1)} %collective-permute-done.10.refs_3_, ...), custom_call_target="tpu_custom_call" | custom-call | tf_op jit(solution)/shard_map/begin/pallas_call | solution.py:42
  57.4 1.9 %collective-permute-done.21.refs_2_.sent_other = bf16[512,512]{1,0:T(8,128)(2,1)S(1)} collective-permute-done((bf16[512,512]{1,0:T(8,128)(2,1)S(1)}, bf16[512,512]{1,0:T(8,128)(2,1)S(1)}, u32[]{:S(2)}, u32[]{:S(2)}) %collective-permute-start.21) | collective-permute-done | bytes 524320 | tf_op jit(solution)/shard_map/ppermute | solution.py:193
  62.1 4.6 %collective-permute-done.22.came = bf16[1024,128]{1,0:T(8,128)(2,1)S(1)} collective-permute-done((bf16[1024,128]{1,0:T(8,128)(2,1)S(1)}, bf16[1024,128]{1,0:T(8,128)(2,1)S(1)}, u32[]{:S(2)}, u32[]{:S(2)}) %collective-permute-start.22) | collective-permute-done | bytes 262176 | tf_op jit(solution)/shard_map/ppermute | solution.py:193
  67.3 1.8 %collective-permute-start.24 = (bf16[512,256]{1,0:T(8,128)(2,1)S(1)}, bf16[512,256]{1,0:T(8,128)(2,1)S(1)}, u32[]{:S(2)}, u32[]{:S(2)}) collective-permute-start(bf16[512,256]{1,0:T(8,128)(2,1)S(1)} %hop.6), channel_id=1, source_target_pairs={{0,4},{4,0},{8,12},{12,8},{14,10},{10,14},{6,2},{2,6},{5,9},{9,5},... | collective-permute-start | bytes 786440 | tf_op jit(solution)/shard_map/ppermute | solution.py:193
  71.0 2.7 %collective-permute-done.24.came = bf16[512,256]{1,0:T(8,128)(2,1)S(1)} collective-permute-done((bf16[512,256]{1,0:T(8,128)(2,1)S(1)}, bf16[512,256]{1,0:T(8,128)(2,1)S(1)}, u32[]{:S(2)}, u32[]{:S(2)}) %collective-permute-start.24) | collective-permute-done | bytes 262176 | tf_op jit(solution)/shard_map/ppermute | solution.py:193
  75.6 2.0 %collective-permute-done.23.came = bf16[512,256]{1,0:T(8,128)(2,1)S(1)} collective-permute-done((bf16[512,256]{1,0:T(8,128)(2,1)S(1)}, bf16[512,256]{1,0:T(8,128)(2,1)S(1)}, u32[]{:S(2)}, u32[]{:S(2)}) %collective-permute-start.23) | collective-permute-done | bytes 262176 | tf_op jit(solution)/shard_map/ppermute | solution.py:193
  81.3 1.8 %collective-permute-start.28 = (bf16[512,256]{1,0:T(8,128)(2,1)S(1)}, bf16[512,256]{1,0:T(8,128)(2,1)S(1)}, u32[]{:S(2)}, u32[]{:S(2)}) collective-permute-start(bf16[512,256]{1,0:T(8,128)(2,1)S(1)} %hop.10), channel_id=1, source_target_pairs={{0,4},{4,0},{8,12},{12,8},{14,10},{10,14},{6,2},{2,6},{5,9},{9,5},... | collective-permute-start | bytes 786440 | tf_op jit(solution)/shard_map/ppermute | solution.py:193
  83.1 3.4 %collective-permute-done.25.came = bf16[512,256]{1,0:T(8,128)(2,1)S(1)} collective-permute-done((bf16[512,256]{1,0:T(8,128)(2,1)S(1)}, bf16[512,256]{1,0:T(8,128)(2,1)S(1)}, u32[]{:S(2)}, u32[]{:S(2)}) %collective-permute-start.25) | collective-permute-done | bytes 262176 | tf_op jit(solution)/shard_map/ppermute | solution.py:193
  87.1 1.8 %collective-permute-start.27 = (bf16[512,256]{1,0:T(8,128)(2,1)S(1)}, bf16[512,256]{1,0:T(8,128)(2,1)S(1)}, u32[]{:S(2)}, u32[]{:S(2)}) collective-permute-start(bf16[512,256]{1,0:T(8,128)(2,1)S(1)} %hop.11), channel_id=1, source_target_pairs={{0,4},{4,0},{8,12},{12,8},{14,10},{10,14},{6,2},{2,6},{5,9},{9,5},... | collective-permute-start | bytes 786440 | tf_op jit(solution)/shard_map/ppermute | solution.py:193
  89.9 3.7 %collective-permute-done.27.came = bf16[512,256]{1,0:T(8,128)(2,1)S(1)} collective-permute-done((bf16[512,256]{1,0:T(8,128)(2,1)S(1)}, bf16[512,256]{1,0:T(8,128)(2,1)S(1)}, u32[]{:S(2)}, u32[]{:S(2)}) %collective-permute-start.27) | collective-permute-done | bytes 262176 | tf_op jit(solution)/shard_map/ppermute | solution.py:193
  96.6 1.4 %apply.2.refs_0_ = f32[500,512]{1,0:T(8,128)} custom-call(s32[3]{0:T(128)S(1)} %pad_add_fusion.place, f32[500,512]{1,0:T(8,128)S(1)} %bitcast.14, bf16[512,256]{1,0:T(8,128)(2,1)S(1)} %last.1.change), custom_call_target="tpu_custom_call" | custom-call | tf_op jit(solution)/shard_map/apply/pallas_call | solution.py:42
  98.0 2.6 %collective-permute-done.30.change = bf16[512,256]{1,0:T(8,128)(2,1)S(1)} collective-permute-done((bf16[512,256]{1,0:T(8,128)(2,1)S(1)}, bf16[512,256]{1,0:T(8,128)(2,1)S(1)}, u32[]{:S(2)}, u32[]{:S(2)}) %collective-permute-start.30) | collective-permute-done | bytes 262176 | tf_op jit(solution)/shard_map/ppermute | solution.py:193
  100.6 1.4 %apply.3 = f32[500,512]{1,0:T(8,128)} custom-call(s32[3]{0:T(128)S(1)} %pad_add_fusion.place, f32[500,512]{1,0:T(8,128)S(1)} %bitcast.15, bf16[512,256]{1,0:T(8,128)(2,1)S(1)} %collective-permute-done.30.change, f32[500,512]{1,0:T(8,128)} %apply.2.refs_0_), custom_call_target="tpu_custom_call", output_to_operand_aliasing={{}: (3, {})} | custom-call | tf_op jit(solution)/shard_map/apply/pallas_call | solution.py:42
  (75 shorter events, 23.1 us)
Async XLA Ops:
  0.6 11.4 %collective-permute-start.1 = (bf16[1024,1024]{1,0:T(8,128)(2,1)}, bf16[1024,1024]{1,0:T(8,128)(2,1)S(1)}, u32[]{:S(2)}, u32[]{:S(2)}) collective-permute-start(bf16[1024,1024]{1,0:T(8,128)(2,1)} %w_own.9), channel_id=1, source_target_pairs={{0,1},{1,0},{2,3},{3,2},{4,5},{5,4},{6,7},{7,6},{8,9},{9,8},{10,11... | collective-permute-start | bytes 6291464 | tf_op jit(solution)/shard_map/ppermute | solution.py:193
  3.2 2.2 %collective-permute-start = (bf16[512,256]{1,0:T(8,128)(2,1)S(1)}, bf16[512,256]{1,0:T(8,128)(2,1)S(1)}, u32[]{:S(2)}, u32[]{:S(2)}) collective-permute-start(bf16[512,256]{1,0:T(8,128)(2,1)S(1)} %get-tuple-element.46), channel_id=1, source_target_pairs={{0,1},{1,0},{2,3},{3,2},{4,5},{5,4},{6,7},{7,6},{8,9},{9,8},{10,11... | collective-permute-start | bytes 786440 | tf_op jit(solution)/shard_map/ppermute | solution.py:193
  5.3 10.3 %collective-permute-start.5 = (bf16[256,1024]{1,0:T(8,128)(2,1)S(1)}, bf16[256,1024]{1,0:T(8,128)(2,1)S(1)}, u32[]{:S(2)}, u32[]{:S(2)}) collective-permute-start(bf16[256,1024]{1,0:T(8,128)(2,1)S(1)} %get-tuple-element.48.rows), channel_id=1, source_target_pairs={{0,4},{4,0},{8,12},{12,8},{14,10},{10,14},{6,2},{2,6},{5,9},{9,5},... | collective-permute-start | bytes 1572872 | tf_op jit(solution)/shard_map/ppermute | solution.py:193
  8.3 14.7 %collective-permute-start.4 = (bf16[1024,256]{1,0:T(8,128)(2,1)S(1)}, bf16[1024,256]{1,0:T(8,128)(2,1)S(1)}, u32[]{:S(2)}, u32[]{:S(2)}) collective-permute-start(bf16[1024,256]{1,0:T(8,128)(2,1)S(1)} %constant_dynamic-update-slice_fusion.refs_0_.refs_2_), channel_id=1, source_target_pairs={{0,4},{4,0},{8,12},{12,8},{14,10},{10,14},{6,2},{2,6},{5,9},{9,5},... | collective-permute-start | bytes 1572872 | tf_op jit(solution)/shard_map/ppermute | solution.py:193
  8.4 3.6 %collective-permute-start.2 = (bf16[1,1024]{1,0:T(2,128)(2,1)S(1)}, bf16[1,1024]{1,0:T(2,128)(2,1)S(1)}, u32[]{:S(2)}, u32[]{:S(2)}) collective-permute-start(bf16[1,1024]{1,0:T(2,128)(2,1)S(1)} %broadcast_in_dim.7.p_own), channel_id=1, source_target_pairs={{0,1},{1,0},{2,3},{3,2},{4,5},{5,4},{6,7},{7,6},{8,9},{9,8},{10,11... | collective-permute-start | bytes 6152 | tf_op jit(solution)/shard_map/ppermute | solution.py:193
  15.6 10.4 %collective-permute-start.9 = (bf16[256,1024]{1,0:T(8,128)(2,1)S(1)}, bf16[256,1024]{1,0:T(8,128)(2,1)S(1)}, u32[]{:S(2)}, u32[]{:S(2)}) collective-permute-start(bf16[256,1024]{1,0:T(8,128)(2,1)S(1)} %collective-permute-done.5.rows), channel_id=1, source_target_pairs={{4,8},{8,4},{12,14},{14,12},{10,6},{6,10},{2,0},{0,2},{1,5},{5,1},... | collective-permute-start | bytes 1572872 | tf_op jit(solution)/shard_map/ppermute | solution.py:193
  23.0 12.4 %collective-permute-start.8 = (bf16[1024,256]{1,0:T(8,128)(2,1)S(1)}, bf16[1024,256]{1,0:T(8,128)(2,1)S(1)}, u32[]{:S(2)}, u32[]{:S(2)}) collective-permute-start(bf16[1024,256]{1,0:T(8,128)(2,1)S(1)} %collective-permute-done.4.refs_4_), channel_id=1, source_target_pairs={{4,8},{8,4},{12,14},{14,12},{10,6},{6,10},{2,0},{0,2},{1,5},{5,1},... | collective-permute-start | bytes 1572872 | tf_op jit(solution)/shard_map/ppermute | solution.py:193
  25.2 14.7 %collective-permute-start.7 = (bf16[256,1024]{1,0:T(8,128)(2,1)S(1)}, bf16[256,1024]{1,0:T(8,128)(2,1)S(1)}, u32[]{:S(2)}, u32[]{:S(2)}) collective-permute-start(bf16[256,1024]{1,0:T(8,128)(2,1)S(1)} %get-tuple-element.53.refs_5_), channel_id=1, source_target_pairs={{0,1},{1,0},{2,3},{3,2},{4,5},{5,4},{6,7},{7,6},{8,9},{9,8},{10,11... | collective-permute-start | bytes 1572872 | tf_op jit(solution)/shard_map/ppermute | solution.py:193
  26.0 15.5 %collective-permute-start.13 = (bf16[256,1024]{1,0:T(8,128)(2,1)S(1)}, bf16[256,1024]{1,0:T(8,128)(2,1)S(1)}, u32[]{:S(2)}, u32[]{:S(2)}) collective-permute-start(bf16[256,1024]{1,0:T(8,128)(2,1)S(1)} %collective-permute-done.9.rows), channel_id=1, source_target_pairs={{0,4},{4,0},{8,12},{12,8},{14,10},{10,14},{6,2},{2,6},{5,9},{9,5},... | collective-permute-start | bytes 1572872 | tf_op jit(solution)/shard_map/ppermute | solution.py:193
  35.4 12.0 %collective-permute-start.12 = (bf16[1024,256]{1,0:T(8,128)(2,1)S(1)}, bf16[1024,256]{1,0:T(8,128)(2,1)S(1)}, u32[]{:S(2)}, u32[]{:S(2)}) collective-permute-start(bf16[1024,256]{1,0:T(8,128)(2,1)S(1)} %collective-permute-done.8.refs_1_), channel_id=1, source_target_pairs={{0,4},{4,0},{8,12},{12,8},{14,10},{10,14},{6,2},{2,6},{5,9},{9,5},... | collective-permute-start | bytes 1572872 | tf_op jit(solution)/shard_map/ppermute | solution.py:193
  37.8 1.6 %collective-permute-start.6 = (bf16[512,256]{1,0:T(8,128)(2,1)S(1)}, bf16[512,256]{1,0:T(8,128)(2,1)S(1)}, u32[]{:S(2)}, u32[]{:S(2)}) collective-permute-start(bf16[512,256]{1,0:T(8,128)(2,1)S(1)} %slice.21), channel_id=1, source_target_pairs={{0,1},{1,0},{2,3},{3,2},{4,5},{5,4},{6,7},{7,6},{8,9},{9,8},{10,11... | collective-permute-start | bytes 786440 | tf_op jit(solution)/shard_map/ppermute | solution.py:193
  37.9 1.9 %collective-permute-start.3 = (bf16[128,1024]{1,0:T(8,128)(2,1)S(1)}, bf16[128,1024]{1,0:T(8,128)(2,1)S(1)}, u32[]{:S(2)}, u32[]{:S(2)}) collective-permute-start(bf16[128,1024]{1,0:T(8,128)(2,1)S(1)} %get-tuple-element.51.refs_1_), channel_id=1, source_target_pairs={{0,1},{1,0},{2,3},{3,2},{4,5},{5,4},{6,7},{7,6},{8,9},{9,8},{10,11... | collective-permute-start | bytes 786440 | tf_op jit(solution)/shard_map/ppermute | solution.py:193
  39.4 2.0 %collective-permute-start.14 = (bf16[128,512]{1,0:T(8,128)(2,1)S(1)}, bf16[128,512]{1,0:T(8,128)(2,1)S(1)}, u32[]{:S(2)}, u32[]{:S(2)}) collective-permute-start(bf16[128,512]{1,0:T(8,128)(2,1)S(1)} %get-tuple-element.58.refs_0_), channel_id=1, source_target_pairs={{0,1},{1,0},{2,3},{3,2},{4,5},{5,4},{6,7},{7,6},{8,9},{9,8},{10,11... | collective-permute-start | bytes 393224 | tf_op jit(solution)/shard_map/ppermute | solution.py:193
  39.8 14.6 %collective-permute-start.11 = (bf16[256,1024]{1,0:T(8,128)(2,1)S(1)}, bf16[256,1024]{1,0:T(8,128)(2,1)S(1)}, u32[]{:S(2)}, u32[]{:S(2)}) collective-permute-start(bf16[256,1024]{1,0:T(8,128)(2,1)S(1)} %get-tuple-element.56.refs_2_), channel_id=1, source_target_pairs={{0,1},{1,0},{2,3},{3,2},{4,5},{5,4},{6,7},{7,6},{8,9},{9,8},{10,11... | collective-permute-start | bytes 1572872 | tf_op jit(solution)/shard_map/ppermute | solution.py:193
  41.5 8.0 %collective-permute-start.18 = (bf16[128,1024]{1,0:T(8,128)(2,1)S(1)}, bf16[128,1024]{1,0:T(8,128)(2,1)S(1)}, u32[]{:S(2)}, u32[]{:S(2)}) collective-permute-start(bf16[128,1024]{1,0:T(8,128)(2,1)S(1)} %slice.25), channel_id=1, source_target_pairs={{4,8},{8,4},{12,14},{14,12},{10,6},{6,10},{2,0},{0,2},{1,5},{5,1},... | collective-permute-start | bytes 786440 | tf_op jit(solution)/shard_map/ppermute | solution.py:193
  47.3 7.2 %collective-permute-start.16 = (bf16[256,1024]{1,0:T(8,128)(2,1)S(1)}, bf16[256,1024]{1,0:T(8,128)(2,1)S(1)}, u32[]{:S(2)}, u32[]{:S(2)}) collective-permute-start(bf16[256,1024]{1,0:T(8,128)(2,1)S(1)} %get-tuple-element.60.refs_6_), channel_id=1, source_target_pairs={{0,1},{1,0},{2,3},{3,2},{4,5},{5,4},{6,7},{7,6},{8,9},{9,8},{10,11... | collective-permute-start | bytes 1572872 | tf_op jit(solution)/shard_map/ppermute | solution.py:193
  47.4 6.4 %collective-permute-start.17 = (bf16[1024,128]{1,0:T(8,128)(2,1)S(1)}, bf16[1024,128]{1,0:T(8,128)(2,1)S(1)}, u32[]{:S(2)}, u32[]{:S(2)}) collective-permute-start(bf16[1024,128]{1,0:T(8,128)(2,1)S(1)} %slice.24), channel_id=1, source_target_pairs={{4,8},{8,4},{12,14},{14,12},{10,6},{6,10},{2,0},{0,2},{1,5},{5,1},... | collective-permute-start | bytes 786440 | tf_op jit(solution)/shard_map/ppermute | solution.py:193
  48.1 5.8 %collective-permute-start.10 = (bf16[512,256]{1,0:T(8,128)(2,1)S(1)}, bf16[512,256]{1,0:T(8,128)(2,1)S(1)}, u32[]{:S(2)}, u32[]{:S(2)}) collective-permute-start(bf16[512,256]{1,0:T(8,128)(2,1)S(1)} %slice.22), channel_id=1, source_target_pairs={{0,1},{1,0},{2,3},{3,2},{4,5},{5,4},{6,7},{7,6},{8,9},{9,8},{10,11... | collective-permute-start | bytes 786440 | tf_op jit(solution)/shard_map/ppermute | solution.py:193
  49.5 5.0 %collective-permute-start.15 = (bf16[512,256]{1,0:T(8,128)(2,1)S(1)}, bf16[512,256]{1,0:T(8,128)(2,1)S(1)}, u32[]{:S(2)}, u32[]{:S(2)}) collective-permute-start(bf16[512,256]{1,0:T(8,128)(2,1)S(1)} %slice.23), channel_id=1, source_target_pairs={{0,1},{1,0},{2,3},{3,2},{4,5},{5,4},{6,7},{7,6},{8,9},{9,8},{10,11... | collective-permute-start | bytes 786440 | tf_op jit(solution)/shard_map/ppermute | solution.py:193
  53.9 2.4 %collective-permute-start.20 = (bf16[128,1024]{1,0:T(8,128)(2,1)S(1)}, bf16[128,1024]{1,0:T(8,128)(2,1)S(1)}, u32[]{:S(2)}, u32[]{:S(2)}) collective-permute-start(bf16[128,1024]{1,0:T(8,128)(2,1)S(1)} %get-tuple-element.63.refs_1_), channel_id=1, source_target_pairs={{0,1},{1,0},{2,3},{3,2},{4,5},{5,4},{6,7},{7,6},{8,9},{9,8},{10,11... | collective-permute-start | bytes 786440 | tf_op jit(solution)/shard_map/ppermute | solution.py:193
  53.9 2.4 %collective-permute-start.19 = (bf16[512,128]{1,0:T(8,128)(2,1)S(1)}, bf16[512,128]{1,0:T(8,128)(2,1)S(1)}, u32[]{:S(2)}, u32[]{:S(2)}) collective-permute-start(bf16[512,128]{1,0:T(8,128)(2,1)S(1)} %slice.28), channel_id=1, source_target_pairs={{0,1},{1,0},{2,3},{3,2},{4,5},{5,4},{6,7},{7,6},{8,9},{9,8},{10,11... | collective-permute-start | bytes 393224 | tf_op jit(solution)/shard_map/ppermute | solution.py:193
  57.3 2.0 %collective-permute-start.21 = (bf16[512,512]{1,0:T(8,128)(2,1)S(1)}, bf16[512,512]{1,0:T(8,128)(2,1)S(1)}, u32[]{:S(2)}, u32[]{:S(2)}) collective-permute-start(bf16[512,512]{1,0:T(8,128)(2,1)S(1)} %get-tuple-element.86.refs_1_.sent.refs_2_), channel_id=1, source_target_pairs={{0,1},{1,0},{2,3},{3,2},{4,5},{5,4},{6,7},{7,6},{8,9},{9,8},{10,11... | collective-permute-start | bytes 1572872 | tf_op jit(solution)/shard_map/ppermute | solution.py:193
  60.2 6.4 %collective-permute-start.22 = (bf16[1024,128]{1,0:T(8,128)(2,1)S(1)}, bf16[1024,128]{1,0:T(8,128)(2,1)S(1)}, u32[]{:S(2)}, u32[]{:S(2)}) collective-permute-start(bf16[1024,128]{1,0:T(8,128)(2,1)S(1)} %far.1), channel_id=1, source_target_pairs={{4,8},{8,4},{12,14},{14,12},{10,6},{6,10},{2,0},{0,2},{1,5},{5,1},... | collective-permute-start | bytes 786440 | tf_op jit(solution)/shard_map/ppermute | solution.py:193
  67.3 6.4 %collective-permute-start.24 = (bf16[512,256]{1,0:T(8,128)(2,1)S(1)}, bf16[512,256]{1,0:T(8,128)(2,1)S(1)}, u32[]{:S(2)}, u32[]{:S(2)}) collective-permute-start(bf16[512,256]{1,0:T(8,128)(2,1)S(1)} %hop.6), channel_id=1, source_target_pairs={{0,4},{4,0},{8,12},{12,8},{14,10},{10,14},{6,2},{2,6},{5,9},{9,5},... | collective-permute-start | bytes 786440 | tf_op jit(solution)/shard_map/ppermute | solution.py:193
  69.6 7.9 %collective-permute-start.23 = (bf16[512,256]{1,0:T(8,128)(2,1)S(1)}, bf16[512,256]{1,0:T(8,128)(2,1)S(1)}, u32[]{:S(2)}, u32[]{:S(2)}) collective-permute-start(bf16[512,256]{1,0:T(8,128)(2,1)S(1)} %hop.7), channel_id=1, source_target_pairs={{0,4},{4,0},{8,12},{12,8},{14,10},{10,14},{6,2},{2,6},{5,9},{9,5},... | collective-permute-start | bytes 786440 | tf_op jit(solution)/shard_map/ppermute | solution.py:193
  74.3 6.4 %collective-permute-start.26 = (bf16[512,256]{1,0:T(8,128)(2,1)S(1)}, bf16[512,256]{1,0:T(8,128)(2,1)S(1)}, u32[]{:S(2)}, u32[]{:S(2)}) collective-permute-start(bf16[512,256]{1,0:T(8,128)(2,1)S(1)} %hop.8), channel_id=1, source_target_pairs={{4,8},{8,4},{12,14},{14,12},{10,6},{6,10},{2,0},{0,2},{1,5},{5,1},... | collective-permute-start | bytes 786440 | tf_op jit(solution)/shard_map/ppermute | solution.py:193
  78.2 8.3 %collective-permute-start.25 = (bf16[512,256]{1,0:T(8,128)(2,1)S(1)}, bf16[512,256]{1,0:T(8,128)(2,1)S(1)}, u32[]{:S(2)}, u32[]{:S(2)}) collective-permute-start(bf16[512,256]{1,0:T(8,128)(2,1)S(1)} %hop.9), channel_id=1, source_target_pairs={{4,8},{8,4},{12,14},{14,12},{10,6},{6,10},{2,0},{0,2},{1,5},{5,1},... | collective-permute-start | bytes 786440 | tf_op jit(solution)/shard_map/ppermute | solution.py:193
  81.3 14.1 %copy-start.3 = (f32[512,500]{0,1:T(8,128)S(1)}, f32[512,500]{0,1:T(8,128)}, u32[]{:S(2)}) copy-start(f32[512,500]{0,1:T(8,128)} %param.13) | copy-start | bytes 3072004
  81.3 8.4 %collective-permute-start.28 = (bf16[512,256]{1,0:T(8,128)(2,1)S(1)}, bf16[512,256]{1,0:T(8,128)(2,1)S(1)}, u32[]{:S(2)}, u32[]{:S(2)}) collective-permute-start(bf16[512,256]{1,0:T(8,128)(2,1)S(1)} %hop.10), channel_id=1, source_target_pairs={{0,4},{4,0},{8,12},{12,8},{14,10},{10,14},{6,2},{2,6},{5,9},{9,5},... | collective-permute-start | bytes 786440 | tf_op jit(solution)/shard_map/ppermute | solution.py:193
  87.1 6.4 %collective-permute-start.27 = (bf16[512,256]{1,0:T(8,128)(2,1)S(1)}, bf16[512,256]{1,0:T(8,128)(2,1)S(1)}, u32[]{:S(2)}, u32[]{:S(2)}) collective-permute-start(bf16[512,256]{1,0:T(8,128)(2,1)S(1)} %hop.11), channel_id=1, source_target_pairs={{0,4},{4,0},{8,12},{12,8},{14,10},{10,14},{6,2},{2,6},{5,9},{9,5},... | collective-permute-start | bytes 786440 | tf_op jit(solution)/shard_map/ppermute | solution.py:193
  89.8 3.8 %collective-permute-start.29 = (bf16[512,256]{1,0:T(8,128)(2,1)S(1)}, bf16[512,256]{1,0:T(8,128)(2,1)S(1)}, u32[]{:S(2)}, u32[]{:S(2)}) collective-permute-start(bf16[512,256]{1,0:T(8,128)(2,1)S(1)} %collective-permute-done.28), channel_id=1, source_target_pairs={{0,1},{1,0},{2,3},{3,2},{4,5},{5,4},{6,7},{7,6},{8,9},{9,8},{10,11... | collective-permute-start | bytes 786440 | tf_op jit(solution)/shard_map/ppermute | solution.py:193
  94.2 6.4 %collective-permute-start.30 = (bf16[512,256]{1,0:T(8,128)(2,1)S(1)}, bf16[512,256]{1,0:T(8,128)(2,1)S(1)}, u32[]{:S(2)}, u32[]{:S(2)}) collective-permute-start(bf16[512,256]{1,0:T(8,128)(2,1)S(1)} %last.1.change), channel_id=1, source_target_pairs={{0,2},{2,0},{1,3},{3,1},{4,6},{6,4},{5,7},{7,5},{8,10},{10,8},{9,1... | collective-permute-start | bytes 786440 | tf_op jit(solution)/shard_map/ppermute | solution.py:193
  (4 other events, 18.4 us)

commit v10 on v8

--- a/solution.py
+++ b/solution.py
@@ -146,24 +146,26 @@
     sent[...] = total.astype(BF16)
 
 
-def far_kernel(place, sent, feats, out):
-    out[...] = dot_nt(sent[...], feats[...]).astype(BF16)
-
-
-def hop_kernel(place, sent, feats, came, out):
-    total = dot_nt(sent[...], feats[...])
-    size = came.shape[1]
-    out[:, :size] = (total[:, :size] + came[...].astype(F32)).astype(BF16)
-    if size < out.shape[1]:
-        out[:, size:] = total[:, size:].astype(BF16)
-
-
-def last_kernel(place, sent, mine, theirs, came, given, out):
-    part = mine.shape[0]
-    total = dot_nt(sent[...], jnp.concatenate([mine[...], theirs[...]], axis=0)) + came[...].astype(F32)
+def start_kernel(n_feats, place, sent, *refs):
+    rows = refs[0][...] if n_feats == 1 else jnp.concatenate([f[...] for f in refs[:n_feats]], axis=0)
+    refs[-1][...] = dot_nt(sent[...], rows).astype(BF16)
+
+
+def change_kernel(n_feats, place, sent, *refs):
+    rows = refs[0][...] if n_feats == 1 else jnp.concatenate([f[...] for f in refs[:n_feats]], axis=0)
+    refs[-1][...] = dot_nt(sent[...], rows)
+
+
+def hop_kernel(place, change, came, out):
+    out[...] = (change[...] + came[...].astype(F32)).astype(BF16)
+
+
+def last_kernel(place, change, came, given, out):
+    part = out.shape[1] // 2
     for i in (0, 1):
         at, there = slice(i * part, (i + 1) * part), slice((1 - i) * part, (2 - i) * part)
-        out[:, at] = (total[:, at] + given[:, there].astype(F32)).astype(BF16)
+        total = change[:, at] + came[:, at].astype(F32) + given[:, there].astype(F32)
+        out[:, at] = total.astype(BF16)
 
 
 def apply_kernel(which, place, predictions, change, *refs):
@@ -258,26 +260,43 @@
     r4 = T(r3[:, :part])
     (x4,) = after((x4,), q3)
     q4, f4 = block(x4, part)
+    f4_other = C(f4)
     begun = begin([(r2, q2), (theirs(r2), C(q2)), (r3, q3), (theirs(r3), C(q3))], begun)
+    (begun,) = after((begun,), f4_other)
     update, sent = call(
         update_kernel, (like((padded, depth), F32), like((padded, depth))), place,
         (begun, r4, q4, theirs(r4), C(q4)), "update", 14,
     )
 
-    piece, whole = like((padded, part)), like((padded, 2 * part))
-    far = lambda u: call(far_kernel, piece, place, (u, f4), "far", 6)
-    hop = lambda u, feats, came: call(hop_kernel, whole, place, (u, feats, came), "hop", 6)
-    first = far(sent)
-    sent_other, first = after((C(sent), first), first)
-    first, second = T(first), T(far(sent_other))
-    (second,) = after((second,), first)
-    for way, feats in ((S, f3), (T, f2), (S, f1)):
-        second_sum = hop(sent_other, feats, second)
-        (first,) = after((first,), second_sum)
-        first_sum = hop(sent, feats, first)
-        second, first = way(second_sum), way(first_sum)
-        (second,) = after((second,), first_sum)
-    own = call(last_kernel, whole, place, (sent, f0, f0_other, first, C(second)), "last", 6)
+    whole, wide = like((padded, 2 * part)), like((padded, 2 * part), F32)
+
+    def product(kernel, out, update, *feats):
+        kernel = functools.partial(kernel, len(feats))
+        return call(kernel, out, place, (update, *feats), "change", 6)
+
+    hop = lambda ahead, came: call(hop_kernel, whole, place, (ahead, came), "hop", 4)
+    first = product(start_kernel, whole, sent, f4, f4_other)
+    (sent_other,) = after((C(sent),), first)
+    first = T(first)
+    second = product(start_kernel, whole, sent_other, f3)
+    ahead = product(change_kernel, wide, after((sent,), second)[0], f3)
+    second = S(second)
+    (first,) = after((first,), ahead)
+    for way, feats, later in ((S, f2, f2), (T, f1, f1)):
+        total = hop(ahead, first)
+        first = way(total)
+        ahead = product(change_kernel, wide, after((sent_other,), total)[0], feats)
+        (second,) = after((second,), ahead)
+        total = hop(ahead, second)
+        second = (T if way is S else S)(total)
+        ahead = product(change_kernel, wide, after((sent,), total)[0], later)
+        (first,) = after((first,), ahead)
+    total = hop(ahead, first)
+    first = S(total)
+    ahead = product(change_kernel, wide, after((sent,), total)[0], f0, f0_other)
+    given = C(after((second,), ahead)[0])
+    (first,) = after((first,), given)
+    own = call(last_kernel, whole, place, (ahead, first, given), "last", 4)
     new = None
     for i in (0, 1):
         change = swap(own, "blocks", [(0, 1)]) if i else own

time: 103 us -> 101 us (0.981)
  waiting for transfers between devices: 31.4 us -> 22.7 us
  starting transfers between devices: 29 us -> 33.1 us
  Pallas kernels: 37.1 us -> 39.9 us
    ppermute x32, waiting for transfers between devices: 31.4 us -> 22.7 us  [swap(): lax.ppermute(x, axes, [p for a, b in pairs for p in ((a, b), (b, a))])]
    ppermute x32, starting transfers between devices: 29 us -> 33.1 us  [swap(): lax.ppermute(x, axes, [p for a, b in pairs for p in ((a, b), (b, a))])]
    pallas_call x21 -> x26, Pallas kernels: 37.1 us -> 39.9 us  [call(): pl.pallas_call(kernel, out_shape=out_shapes, in_specs=[pl.BlockSpec(memor...]
  transfers between devices with their start and end apart: 32 -> 32, of which waited for: 16 -> 12; matrix products, arithmetic and copies ran while one was open for 1% -> 1% of each run, Pallas kernels for 31% -> 37%
where the time goes in v10:
time: 101 us
  Pallas kernels  39.9 us (40%)
  starting transfers between devices  33.1 us (33%)
  waiting for transfers between devices  22.7 us (22%)
  local copies, waits for them, and re-layouts  2.56 us (3%)
  other arithmetic  1.24 us (1%)
  between operations  1.22 us (1%)
    pallas_call x26, Pallas kernels, call(): pl.pallas_call(kernel, out_shape=out_shapes, in_specs=[pl.BlockSpec(memor...  39.9 us
    ppermute x32, starting transfers between devices, swap(): lax.ppermute(x, axes, [p for a, b in pairs for p in ((a, b), (b, a))])  33.1 us
    ppermute x32, waiting for transfers between devices, swap(): lax.ppermute(x, axes, [p for a, b in pairs for p in ((a, b), (b, a))])  22.7 us
    unnamed x11, local copies, waits for them, and re-layouts  2.43 us
  transfers between devices with their start and end apart: 32, of which 12 were waited for; matrix products, arithmetic and copies ran while one was open for 1% of the time, Pallas kernels for 37%

profile of v10, /device:TPU:0, one launch (start us, length us, event | category | flops | bytes accessed | tf_op | source)
XLA Modules:
  0.0 100.7 jit_solution(1415409951380046475)
XLA Ops:
  1.2 1.9 %prepare.1 = (bf16[256,1024]{1,0:T(8,128)(2,1)S(1)}, bf16[512,256]{1,0:T(8,128)(2,1)S(1)}, bf16[512,256]{1,0:T(8,128)(2,1)S(1)}) custom-call(s32[3]{0:T(128)S(1)} %pad_add_fusion.place, bf16[512,1024]{1,0:T(8,128)(2,1)} %inputs.1, s32[1,512]{1,0:T(1,128)} %bitcast.18, f32[500,512]{1,0:T(8,128)} %bitcast.13), custom_call_target="tpu_custom_call" | custom-call | tf_op jit(solution)/shard_map/prepare/pallas_call | solution.py:42
  3.3 2.0 %collective-permute-done = bf16[512,256]{1,0:T(8,128)(2,1)S(1)} collective-permute-done((bf16[512,256]{1,0:T(8,128)(2,1)S(1)}, bf16[512,256]{1,0:T(8,128)(2,1)S(1)}, u32[]{:S(2)}, u32[]{:S(2)}) %collective-permute-start) | collective-permute-done | bytes 262176 | tf_op jit(solution)/shard_map/ppermute | solution.py:185
  5.3 2.9 %collective-permute-start.5 = (bf16[256,1024]{1,0:T(8,128)(2,1)S(1)}, bf16[256,1024]{1,0:T(8,128)(2,1)S(1)}, u32[]{:S(2)}, u32[]{:S(2)}) collective-permute-start(bf16[256,1024]{1,0:T(8,128)(2,1)S(1)} %get-tuple-element.45.rows), channel_id=1, source_target_pairs={{0,4},{4,0},{8,12},{12,8},{14,10},{10,14},{6,2},{2,6},{5,9},{9,5},... | collective-permute-start | bytes 1572872 | tf_op jit(solution)/shard_map/ppermute | solution.py:185
  8.5 2.2 %copy-done.2 = f32[1,512,2048]{2,1,0:T(8,128)S(1)} copy-done((f32[1,512,2048]{2,1,0:T(8,128)S(1)}, f32[1,512,2048]{2,1,0:T(8,128)}, u32[]{:S(2)}) %copy-start.2) | copy-done | bytes 4194328
  12.3 3.3 %block.5 = (bf16[128,1024]{1,0:T(8,128)(2,1)S(1)}, bf16[128,512]{1,0:T(8,128)(2,1)S(1)}) custom-call(s32[3]{0:T(128)S(1)} %pad_add_fusion.place, bf16[256,1024]{1,0:T(8,128)(2,1)S(1)} %get-tuple-element.45.rows, bf16[1024,1024]{1,0:T(8,128)(2,1)S(1)} %copy-done, bf16[1024,1024]{1,0:T(8,128)(2,1)S(1)} %collective-permute-done.1.w_other, ...), custom_call_target="tpu_custom_call" | custom-call | tf_op jit(solution)/shard_map/block/pallas_call | solution.py:42
  15.6 2.0 %collective-permute-start.9 = (bf16[256,1024]{1,0:T(8,128)(2,1)S(1)}, bf16[256,1024]{1,0:T(8,128)(2,1)S(1)}, u32[]{:S(2)}, u32[]{:S(2)}) collective-permute-start(bf16[256,1024]{1,0:T(8,128)(2,1)S(1)} %collective-permute-done.5.rows), channel_id=1, source_target_pairs={{4,8},{8,4},{12,14},{14,12},{10,6},{6,10},{2,0},{0,2},{1,5},{5,1},... | collective-permute-start | bytes 1572872 | tf_op jit(solution)/shard_map/ppermute | solution.py:185
  17.6 4.1 %block.6 = (bf16[256,1024]{1,0:T(8,128)(2,1)S(1)}, bf16[256,512]{1,0:T(8,128)(2,1)S(1)}) custom-call(s32[3]{0:T(128)S(1)} %pad_add_fusion.place, bf16[256,1024]{1,0:T(8,128)(2,1)S(1)} %collective-permute-done.5.rows, bf16[1024,1024]{1,0:T(8,128)(2,1)S(1)} %copy-done, bf16[1024,1024]{1,0:T(8,128)(2,1)S(1)} %collective-permute-done.1.w_other, ...), custom_call_target="tpu_custom_call" | custom-call | tf_op jit(solution)/shard_map/block/pallas_call | solution.py:42
  23.0 2.2 %collective-permute-start.8 = (bf16[1024,256]{1,0:T(8,128)(2,1)S(1)}, bf16[1024,256]{1,0:T(8,128)(2,1)S(1)}, u32[]{:S(2)}, u32[]{:S(2)}) collective-permute-start(bf16[1024,256]{1,0:T(8,128)(2,1)S(1)} %collective-permute-done.4.refs_4_), channel_id=1, source_target_pairs={{4,8},{8,4},{12,14},{14,12},{10,6},{6,10},{2,0},{0,2},{1,5},{5,1},... | collective-permute-start | bytes 1572872 | tf_op jit(solution)/shard_map/ppermute | solution.py:185
  26.0 1.8 %collective-permute-start.13 = (bf16[256,1024]{1,0:T(8,128)(2,1)S(1)}, bf16[256,1024]{1,0:T(8,128)(2,1)S(1)}, u32[]{:S(2)}, u32[]{:S(2)}) collective-permute-start(bf16[256,1024]{1,0:T(8,128)(2,1)S(1)} %collective-permute-done.9.rows), channel_id=1, source_target_pairs={{0,4},{4,0},{8,12},{12,8},{14,10},{10,14},{6,2},{2,6},{5,9},{9,5},... | collective-permute-start | bytes 1572872 | tf_op jit(solution)/shard_map/ppermute | solution.py:185
  28.2 4.1 %block.7 = (bf16[256,1024]{1,0:T(8,128)(2,1)S(1)}, bf16[256,512]{1,0:T(8,128)(2,1)S(1)}) custom-call(s32[3]{0:T(128)S(1)} %pad_add_fusion.place, bf16[256,1024]{1,0:T(8,128)(2,1)S(1)} %collective-permute-done.9.rows, bf16[1024,1024]{1,0:T(8,128)(2,1)S(1)} %copy-done, bf16[1024,1024]{1,0:T(8,128)(2,1)S(1)} %collective-permute-done.1.w_other, ...), custom_call_target="tpu_custom_call" | custom-call | tf_op jit(solution)/shard_map/block/pallas_call | solution.py:42
  32.3 3.1 %collective-permute-done.8.refs_1_ = bf16[1024,256]{1,0:T(8,128)(2,1)S(1)} collective-permute-done((bf16[1024,256]{1,0:T(8,128)(2,1)S(1)}, bf16[1024,256]{1,0:T(8,128)(2,1)S(1)}, u32[]{:S(2)}, u32[]{:S(2)}) %collective-permute-start.8) | collective-permute-done | bytes 524320 | tf_op jit(solution)/shard_map/ppermute | solution.py:185
  35.4 2.4 %collective-permute-start.12 = (bf16[1024,256]{1,0:T(8,128)(2,1)S(1)}, bf16[1024,256]{1,0:T(8,128)(2,1)S(1)}, u32[]{:S(2)}, u32[]{:S(2)}) collective-permute-start(bf16[1024,256]{1,0:T(8,128)(2,1)S(1)} %collective-permute-done.8.refs_1_), channel_id=1, source_target_pairs={{0,4},{4,0},{8,12},{12,8},{14,10},{10,14},{6,2},{2,6},{5,9},{9,5},... | collective-permute-start | bytes 1572872 | tf_op jit(solution)/shard_map/ppermute | solution.py:185
  39.4 1.5 %begin.2.refs_0_ = f32[512,512]{1,0:T(8,128)S(1)} custom-call(s32[3]{0:T(128)S(1)} %pad_add_fusion.place, bf16[1024,256]{1,0:T(8,128)(2,1)S(1)} %constant_dynamic-update-slice_fusion.refs_0_.refs_2_, bf16[128,1024]{1,0:T(8,128)(2,1)S(1)} %get-tuple-element.48.refs_1_, bf16[1024,256]{1,0:T(8,128)(2,1)S(1)} %constant_dynamic-update-slice_fusion.refs_0_.refs_2_, ...), custom_call_target="tpu_custom_call" | custom-call | tf_op jit(solution)/shard_map/begin/pallas_call | solution.py:42
  41.0 1.6 %collective-permute-start.17 = (bf16[128,1024]{1,0:T(8,128)(2,1)S(1)}, bf16[128,1024]{1,0:T(8,128)(2,1)S(1)}, u32[]{:S(2)}, u32[]{:S(2)}) collective-permute-start(bf16[128,1024]{1,0:T(8,128)(2,1)S(1)} %slice.24), channel_id=1, source_target_pairs={{4,8},{8,4},{12,14},{14,12},{10,6},{6,10},{2,0},{0,2},{1,5},{5,1},... | collective-permute-start | bytes 786440 | tf_op jit(solution)/shard_map/ppermute | solution.py:185
  42.5 4.2 %block.8 = (bf16[256,1024]{1,0:T(8,128)(2,1)S(1)}, bf16[256,512]{1,0:T(8,128)(2,1)S(1)}) custom-call(s32[3]{0:T(128)S(1)} %pad_add_fusion.place, bf16[256,1024]{1,0:T(8,128)(2,1)S(1)} %collective-permute-done.13.rows, bf16[1024,1024]{1,0:T(8,128)(2,1)S(1)} %copy-done, bf16[1024,1024]{1,0:T(8,128)(2,1)S(1)} %collective-permute-done.1.w_other, ...), custom_call_target="tpu_custom_call" | custom-call | tf_op jit(solution)/shard_map/block/pallas_call | solution.py:42
  49.1 3.3 %block.9 = (bf16[128,1024]{1,0:T(8,128)(2,1)S(1)}, bf16[128,512]{1,0:T(8,128)(2,1)S(1)}) custom-call(s32[3]{0:T(128)S(1)} %pad_add_fusion.place, bf16[128,1024]{1,0:T(8,128)(2,1)S(1)} %collective-permute-done.17.rows, bf16[1024,1024]{1,0:T(8,128)(2,1)S(1)} %copy-done, bf16[1024,1024]{1,0:T(8,128)(2,1)S(1)} %collective-permute-done.1.w_other, ...), custom_call_target="tpu_custom_call" | custom-call | tf_op jit(solution)/shard_map/block/pallas_call | solution.py:42
  52.5 1.4 %collective-permute-done.19.refs_0_ = bf16[1024,128]{1,0:T(8,128)(2,1)S(1)} collective-permute-done((bf16[1024,128]{1,0:T(8,128)(2,1)S(1)}, bf16[1024,128]{1,0:T(8,128)(2,1)S(1)}, u32[]{:S(2)}, u32[]{:S(2)}) %collective-permute-start.19) | collective-permute-done | bytes 262176 | tf_op jit(solution)/shard_map/ppermute | solution.py:185
  54.5 1.8 %begin.3.begun = f32[512,512]{1,0:T(8,128)S(1)} custom-call(s32[3]{0:T(128)S(1)} %pad_add_fusion.place, f32[512,512]{1,0:T(8,128)S(1)} %begin.2.refs_0_, bf16[1024,256]{1,0:T(8,128)(2,1)S(1)} %collective-permute-done.8.refs_1_, bf16[256,1024]{1,0:T(8,128)(2,1)S(1)} %get-tuple-element.53.refs_2_, bf16[512,256]{1,0:T(8,128)(2,1)S(1)} %collective-permute-done.10.refs_3_, ...), custom_call_target="tpu_custom_call" | custom-call | tf_op jit(solution)/shard_map/begin/pallas_call | solution.py:42
  60.2 1.9 %collective-permute-start.24 = (bf16[512,256]{1,0:T(8,128)(2,1)S(1)}, bf16[512,256]{1,0:T(8,128)(2,1)S(1)}, u32[]{:S(2)}, u32[]{:S(2)}) collective-permute-start(bf16[512,256]{1,0:T(8,128)(2,1)S(1)} %change.9), channel_id=1, source_target_pairs={{0,4},{4,0},{8,12},{12,8},{14,10},{10,14},{6,2},{2,6},{5,9},{9,5},... | collective-permute-start | bytes 786440 | tf_op jit(solution)/shard_map/ppermute | solution.py:185
  63.0 2.5 %collective-permute-done.23.came = bf16[512,256]{1,0:T(8,128)(2,1)S(1)} collective-permute-done((bf16[512,256]{1,0:T(8,128)(2,1)S(1)}, bf16[512,256]{1,0:T(8,128)(2,1)S(1)}, u32[]{:S(2)}, u32[]{:S(2)}) %collective-permute-start.23) | collective-permute-done | bytes 262176 | tf_op jit(solution)/shard_map/ppermute | solution.py:185
  66.1 2.4 %collective-permute-start.25 = (bf16[512,256]{1,0:T(8,128)(2,1)S(1)}, bf16[512,256]{1,0:T(8,128)(2,1)S(1)}, u32[]{:S(2)}, u32[]{:S(2)}) collective-permute-start(bf16[512,256]{1,0:T(8,128)(2,1)S(1)} %hop.5), channel_id=1, source_target_pairs={{0,4},{4,0},{8,12},{12,8},{14,10},{10,14},{6,2},{2,6},{5,9},{9,5},... | collective-permute-start | bytes 786440 | tf_op jit(solution)/shard_map/ppermute | solution.py:185
  69.9 1.6 %collective-permute-start.26 = (bf16[512,256]{1,0:T(8,128)(2,1)S(1)}, bf16[512,256]{1,0:T(8,128)(2,1)S(1)}, u32[]{:S(2)}, u32[]{:S(2)}) collective-permute-start(bf16[512,256]{1,0:T(8,128)(2,1)S(1)} %hop.6), channel_id=1, source_target_pairs={{4,8},{8,4},{12,14},{14,12},{10,6},{6,10},{2,0},{0,2},{1,5},{5,1},... | collective-permute-start | bytes 786440 | tf_op jit(solution)/shard_map/ppermute | solution.py:185
  72.3 2.4 %collective-permute-done.25.came = bf16[512,256]{1,0:T(8,128)(2,1)S(1)} collective-permute-done((bf16[512,256]{1,0:T(8,128)(2,1)S(1)}, bf16[512,256]{1,0:T(8,128)(2,1)S(1)}, u32[]{:S(2)}, u32[]{:S(2)}) %collective-permute-start.25) | collective-permute-done | bytes 262176 | tf_op jit(solution)/shard_map/ppermute | solution.py:185
  75.3 1.4 %collective-permute-start.27 = (bf16[512,256]{1,0:T(8,128)(2,1)S(1)}, bf16[512,256]{1,0:T(8,128)(2,1)S(1)}, u32[]{:S(2)}, u32[]{:S(2)}) collective-permute-start(bf16[512,256]{1,0:T(8,128)(2,1)S(1)} %hop.7), channel_id=1, source_target_pairs={{4,8},{8,4},{12,14},{14,12},{10,6},{6,10},{2,0},{0,2},{1,5},{5,1},... | collective-permute-start | bytes 786440 | tf_op jit(solution)/shard_map/ppermute | solution.py:185
  78.1 3.2 %collective-permute-start.29 = (bf16[512,256]{1,0:T(8,128)(2,1)S(1)}, bf16[512,256]{1,0:T(8,128)(2,1)S(1)}, u32[]{:S(2)}, u32[]{:S(2)}) collective-permute-start(bf16[512,256]{1,0:T(8,128)(2,1)S(1)} %hop.8), channel_id=1, source_target_pairs={{0,4},{4,0},{8,12},{12,8},{14,10},{10,14},{6,2},{2,6},{5,9},{9,5},... | collective-permute-start | bytes 786440 | tf_op jit(solution)/shard_map/ppermute | solution.py:185
  82.2 2.3 %collective-permute-done.27.came = bf16[512,256]{1,0:T(8,128)(2,1)S(1)} collective-permute-done((bf16[512,256]{1,0:T(8,128)(2,1)S(1)}, bf16[512,256]{1,0:T(8,128)(2,1)S(1)}, u32[]{:S(2)}, u32[]{:S(2)}) %collective-permute-start.27) | collective-permute-done | bytes 262176 | tf_op jit(solution)/shard_map/ppermute | solution.py:185
  85.1 2.5 %collective-permute-start.28 = (bf16[512,256]{1,0:T(8,128)(2,1)S(1)}, bf16[512,256]{1,0:T(8,128)(2,1)S(1)}, u32[]{:S(2)}, u32[]{:S(2)}) collective-permute-start(bf16[512,256]{1,0:T(8,128)(2,1)S(1)} %hop.9), channel_id=1, source_target_pairs={{0,4},{4,0},{8,12},{12,8},{14,10},{10,14},{6,2},{2,6},{5,9},{9,5},... | collective-permute-start | bytes 786440 | tf_op jit(solution)/shard_map/ppermute | solution.py:185
  88.5 3.4 %collective-permute-done.28.came = bf16[512,256]{1,0:T(8,128)(2,1)S(1)} collective-permute-done((bf16[512,256]{1,0:T(8,128)(2,1)S(1)}, bf16[512,256]{1,0:T(8,128)(2,1)S(1)}, u32[]{:S(2)}, u32[]{:S(2)}) %collective-permute-start.28) | collective-permute-done | bytes 262176 | tf_op jit(solution)/shard_map/ppermute | solution.py:185
  92.6 1.6 %collective-permute-start.31 = (bf16[512,256]{1,0:T(8,128)(2,1)S(1)}, bf16[512,256]{1,0:T(8,128)(2,1)S(1)}, u32[]{:S(2)}, u32[]{:S(2)}) collective-permute-start(bf16[512,256]{1,0:T(8,128)(2,1)S(1)} %last.1.change), channel_id=1, source_target_pairs={{0,2},{2,0},{1,3},{3,1},{4,6},{6,4},{5,7},{7,5},{8,10},{10,8},{9,1... | collective-permute-start | bytes 786440 | tf_op jit(solution)/shard_map/ppermute | solution.py:185
  95.3 1.4 %apply.2.refs_0_ = f32[500,512]{1,0:T(8,128)} custom-call(s32[3]{0:T(128)S(1)} %pad_add_fusion.place, f32[500,512]{1,0:T(8,128)S(1)} %bitcast.14, bf16[512,256]{1,0:T(8,128)(2,1)S(1)} %last.1.change), custom_call_target="tpu_custom_call" | custom-call | tf_op jit(solution)/shard_map/apply/pallas_call | solution.py:42
  96.7 2.4 %collective-permute-done.31.change = bf16[512,256]{1,0:T(8,128)(2,1)S(1)} collective-permute-done((bf16[512,256]{1,0:T(8,128)(2,1)S(1)}, bf16[512,256]{1,0:T(8,128)(2,1)S(1)}, u32[]{:S(2)}, u32[]{:S(2)}) %collective-permute-start.31) | collective-permute-done | bytes 262176 | tf_op jit(solution)/shard_map/ppermute | solution.py:185
  99.1 1.4 %apply.3 = f32[500,512]{1,0:T(8,128)} custom-call(s32[3]{0:T(128)S(1)} %pad_add_fusion.place, f32[500,512]{1,0:T(8,128)S(1)} %bitcast.15, bf16[512,256]{1,0:T(8,128)(2,1)S(1)} %collective-permute-done.31.change, f32[500,512]{1,0:T(8,128)} %apply.2.refs_0_), custom_call_target="tpu_custom_call", output_to_operand_aliasing={{}: (3, {})} | custom-call | tf_op jit(solution)/shard_map/apply/pallas_call | solution.py:42
  (79 shorter events, 23.4 us)
Async XLA Ops:
  0.6 11.4 %collective-permute-start.1 = (bf16[1024,1024]{1,0:T(8,128)(2,1)}, bf16[1024,1024]{1,0:T(8,128)(2,1)S(1)}, u32[]{:S(2)}, u32[]{:S(2)}) collective-permute-start(bf16[1024,1024]{1,0:T(8,128)(2,1)} %w_own.9), channel_id=1, source_target_pairs={{0,1},{1,0},{2,3},{3,2},{4,5},{5,4},{6,7},{7,6},{8,9},{9,8},{10,11... | collective-permute-start | bytes 6291464 | tf_op jit(solution)/shard_map/ppermute | solution.py:185
  3.2 2.2 %collective-permute-start = (bf16[512,256]{1,0:T(8,128)(2,1)S(1)}, bf16[512,256]{1,0:T(8,128)(2,1)S(1)}, u32[]{:S(2)}, u32[]{:S(2)}) collective-permute-start(bf16[512,256]{1,0:T(8,128)(2,1)S(1)} %get-tuple-element.43), channel_id=1, source_target_pairs={{0,1},{1,0},{2,3},{3,2},{4,5},{5,4},{6,7},{7,6},{8,9},{9,8},{10,11... | collective-permute-start | bytes 786440 | tf_op jit(solution)/shard_map/ppermute | solution.py:185
  5.3 10.3 %collective-permute-start.5 = (bf16[256,1024]{1,0:T(8,128)(2,1)S(1)}, bf16[256,1024]{1,0:T(8,128)(2,1)S(1)}, u32[]{:S(2)}, u32[]{:S(2)}) collective-permute-start(bf16[256,1024]{1,0:T(8,128)(2,1)S(1)} %get-tuple-element.45.rows), channel_id=1, source_target_pairs={{0,4},{4,0},{8,12},{12,8},{14,10},{10,14},{6,2},{2,6},{5,9},{9,5},... | collective-permute-start | bytes 1572872 | tf_op jit(solution)/shard_map/ppermute | solution.py:185
  8.3 14.7 %collective-permute-start.4 = (bf16[1024,256]{1,0:T(8,128)(2,1)S(1)}, bf16[1024,256]{1,0:T(8,128)(2,1)S(1)}, u32[]{:S(2)}, u32[]{:S(2)}) collective-permute-start(bf16[1024,256]{1,0:T(8,128)(2,1)S(1)} %constant_dynamic-update-slice_fusion.refs_0_.refs_2_), channel_id=1, source_target_pairs={{0,4},{4,0},{8,12},{12,8},{14,10},{10,14},{6,2},{2,6},{5,9},{9,5},... | collective-permute-start | bytes 1572872 | tf_op jit(solution)/shard_map/ppermute | solution.py:185
  8.4 3.6 %collective-permute-start.2 = (bf16[1,1024]{1,0:T(2,128)(2,1)S(1)}, bf16[1,1024]{1,0:T(2,128)(2,1)S(1)}, u32[]{:S(2)}, u32[]{:S(2)}) collective-permute-start(bf16[1,1024]{1,0:T(2,128)(2,1)S(1)} %broadcast_in_dim.7.p_own), channel_id=1, source_target_pairs={{0,1},{1,0},{2,3},{3,2},{4,5},{5,4},{6,7},{7,6},{8,9},{9,8},{10,11... | collective-permute-start | bytes 6152 | tf_op jit(solution)/shard_map/ppermute | solution.py:185
  15.6 10.4 %collective-permute-start.9 = (bf16[256,1024]{1,0:T(8,128)(2,1)S(1)}, bf16[256,1024]{1,0:T(8,128)(2,1)S(1)}, u32[]{:S(2)}, u32[]{:S(2)}) collective-permute-start(bf16[256,1024]{1,0:T(8,128)(2,1)S(1)} %collective-permute-done.5.rows), channel_id=1, source_target_pairs={{4,8},{8,4},{12,14},{14,12},{10,6},{6,10},{2,0},{0,2},{1,5},{5,1},... | collective-permute-start | bytes 1572872 | tf_op jit(solution)/shard_map/ppermute | solution.py:185
  23.0 12.4 %collective-permute-start.8 = (bf16[1024,256]{1,0:T(8,128)(2,1)S(1)}, bf16[1024,256]{1,0:T(8,128)(2,1)S(1)}, u32[]{:S(2)}, u32[]{:S(2)}) collective-permute-start(bf16[1024,256]{1,0:T(8,128)(2,1)S(1)} %collective-permute-done.4.refs_4_), channel_id=1, source_target_pairs={{4,8},{8,4},{12,14},{14,12},{10,6},{6,10},{2,0},{0,2},{1,5},{5,1},... | collective-permute-start | bytes 1572872 | tf_op jit(solution)/shard_map/ppermute | solution.py:185
  25.2 14.2 %collective-permute-start.7 = (bf16[256,1024]{1,0:T(8,128)(2,1)S(1)}, bf16[256,1024]{1,0:T(8,128)(2,1)S(1)}, u32[]{:S(2)}, u32[]{:S(2)}) collective-permute-start(bf16[256,1024]{1,0:T(8,128)(2,1)S(1)} %get-tuple-element.50.refs_5_), channel_id=1, source_target_pairs={{0,1},{1,0},{2,3},{3,2},{4,5},{5,4},{6,7},{7,6},{8,9},{9,8},{10,11... | collective-permute-start | bytes 1572872 | tf_op jit(solution)/shard_map/ppermute | solution.py:185
  26.0 14.9 %collective-permute-start.13 = (bf16[256,1024]{1,0:T(8,128)(2,1)S(1)}, bf16[256,1024]{1,0:T(8,128)(2,1)S(1)}, u32[]{:S(2)}, u32[]{:S(2)}) collective-permute-start(bf16[256,1024]{1,0:T(8,128)(2,1)S(1)} %collective-permute-done.9.rows), channel_id=1, source_target_pairs={{0,4},{4,0},{8,12},{12,8},{14,10},{10,14},{6,2},{2,6},{5,9},{9,5},... | collective-permute-start | bytes 1572872 | tf_op jit(solution)/shard_map/ppermute | solution.py:185
  27.9 9.9 %collective-permute-start.6 = (bf16[512,256]{1,0:T(8,128)(2,1)S(1)}, bf16[512,256]{1,0:T(8,128)(2,1)S(1)}, u32[]{:S(2)}, u32[]{:S(2)}) collective-permute-start(bf16[512,256]{1,0:T(8,128)(2,1)S(1)} %slice.21), channel_id=1, source_target_pairs={{0,1},{1,0},{2,3},{3,2},{4,5},{5,4},{6,7},{7,6},{8,9},{9,8},{10,11... | collective-permute-start | bytes 786440 | tf_op jit(solution)/shard_map/ppermute | solution.py:185
  35.4 12.1 %collective-permute-start.12 = (bf16[1024,256]{1,0:T(8,128)(2,1)S(1)}, bf16[1024,256]{1,0:T(8,128)(2,1)S(1)}, u32[]{:S(2)}, u32[]{:S(2)}) collective-permute-start(bf16[1024,256]{1,0:T(8,128)(2,1)S(1)} %collective-permute-done.8.refs_1_), channel_id=1, source_target_pairs={{0,4},{4,0},{8,12},{12,8},{14,10},{10,14},{6,2},{2,6},{5,9},{9,5},... | collective-permute-start | bytes 1572872 | tf_op jit(solution)/shard_map/ppermute | solution.py:185
  37.7 1.5 %collective-permute-start.3 = (bf16[128,1024]{1,0:T(8,128)(2,1)S(1)}, bf16[128,1024]{1,0:T(8,128)(2,1)S(1)}, u32[]{:S(2)}, u32[]{:S(2)}) collective-permute-start(bf16[128,1024]{1,0:T(8,128)(2,1)S(1)} %get-tuple-element.48.refs_1_), channel_id=1, source_target_pairs={{0,1},{1,0},{2,3},{3,2},{4,5},{5,4},{6,7},{7,6},{8,9},{9,8},{10,11... | collective-permute-start | bytes 786440 | tf_op jit(solution)/shard_map/ppermute | solution.py:185
  37.7 3.2 %collective-permute-start.14 = (bf16[128,512]{1,0:T(8,128)(2,1)S(1)}, bf16[128,512]{1,0:T(8,128)(2,1)S(1)}, u32[]{:S(2)}, u32[]{:S(2)}) collective-permute-start(bf16[128,512]{1,0:T(8,128)(2,1)S(1)} %get-tuple-element.55.refs_0_), channel_id=1, source_target_pairs={{0,1},{1,0},{2,3},{3,2},{4,5},{5,4},{6,7},{7,6},{8,9},{9,8},{10,11... | collective-permute-start | bytes 393224 | tf_op jit(solution)/shard_map/ppermute | solution.py:185
  39.3 14.7 %collective-permute-start.11 = (bf16[256,1024]{1,0:T(8,128)(2,1)S(1)}, bf16[256,1024]{1,0:T(8,128)(2,1)S(1)}, u32[]{:S(2)}, u32[]{:S(2)}) collective-permute-start(bf16[256,1024]{1,0:T(8,128)(2,1)S(1)} %get-tuple-element.53.refs_2_), channel_id=1, source_target_pairs={{0,1},{1,0},{2,3},{3,2},{4,5},{5,4},{6,7},{7,6},{8,9},{9,8},{10,11... | collective-permute-start | bytes 1572872 | tf_op jit(solution)/shard_map/ppermute | solution.py:185
  41.0 7.4 %collective-permute-start.17 = (bf16[128,1024]{1,0:T(8,128)(2,1)S(1)}, bf16[128,1024]{1,0:T(8,128)(2,1)S(1)}, u32[]{:S(2)}, u32[]{:S(2)}) collective-permute-start(bf16[128,1024]{1,0:T(8,128)(2,1)S(1)} %slice.24), channel_id=1, source_target_pairs={{4,8},{8,4},{12,14},{14,12},{10,6},{6,10},{2,0},{0,2},{1,5},{5,1},... | collective-permute-start | bytes 786440 | tf_op jit(solution)/shard_map/ppermute | solution.py:185
  46.8 7.7 %collective-permute-start.16 = (bf16[256,1024]{1,0:T(8,128)(2,1)S(1)}, bf16[256,1024]{1,0:T(8,128)(2,1)S(1)}, u32[]{:S(2)}, u32[]{:S(2)}) collective-permute-start(bf16[256,1024]{1,0:T(8,128)(2,1)S(1)} %get-tuple-element.57.refs_6_), channel_id=1, source_target_pairs={{0,1},{1,0},{2,3},{3,2},{4,5},{5,4},{6,7},{7,6},{8,9},{9,8},{10,11... | collective-permute-start | bytes 1572872 | tf_op jit(solution)/shard_map/ppermute | solution.py:185
  46.9 5.6 %collective-permute-start.10 = (bf16[512,256]{1,0:T(8,128)(2,1)S(1)}, bf16[512,256]{1,0:T(8,128)(2,1)S(1)}, u32[]{:S(2)}, u32[]{:S(2)}) collective-permute-start(bf16[512,256]{1,0:T(8,128)(2,1)S(1)} %slice.22), channel_id=1, source_target_pairs={{0,1},{1,0},{2,3},{3,2},{4,5},{5,4},{6,7},{7,6},{8,9},{9,8},{10,11... | collective-permute-start | bytes 786440 | tf_op jit(solution)/shard_map/ppermute | solution.py:185
  47.5 6.4 %collective-permute-start.19 = (bf16[1024,128]{1,0:T(8,128)(2,1)S(1)}, bf16[1024,128]{1,0:T(8,128)(2,1)S(1)}, u32[]{:S(2)}, u32[]{:S(2)}) collective-permute-start(bf16[1024,128]{1,0:T(8,128)(2,1)S(1)} %slice.25), channel_id=1, source_target_pairs={{4,8},{8,4},{12,14},{14,12},{10,6},{6,10},{2,0},{0,2},{1,5},{5,1},... | collective-permute-start | bytes 786440 | tf_op jit(solution)/shard_map/ppermute | solution.py:185
  48.4 6.1 %collective-permute-start.15 = (bf16[512,256]{1,0:T(8,128)(2,1)S(1)}, bf16[512,256]{1,0:T(8,128)(2,1)S(1)}, u32[]{:S(2)}, u32[]{:S(2)}) collective-permute-start(bf16[512,256]{1,0:T(8,128)(2,1)S(1)} %slice.23), channel_id=1, source_target_pairs={{0,1},{1,0},{2,3},{3,2},{4,5},{5,4},{6,7},{7,6},{8,9},{9,8},{10,11... | collective-permute-start | bytes 786440 | tf_op jit(solution)/shard_map/ppermute | solution.py:185
  52.5 3.9 %collective-permute-start.21 = (bf16[128,1024]{1,0:T(8,128)(2,1)S(1)}, bf16[128,1024]{1,0:T(8,128)(2,1)S(1)}, u32[]{:S(2)}, u32[]{:S(2)}) collective-permute-start(bf16[128,1024]{1,0:T(8,128)(2,1)S(1)} %get-tuple-element.62.refs_1_), channel_id=1, source_target_pairs={{0,1},{1,0},{2,3},{3,2},{4,5},{5,4},{6,7},{7,6},{8,9},{9,8},{10,11... | collective-permute-start | bytes 786440 | tf_op jit(solution)/shard_map/ppermute | solution.py:185
  53.9 2.4 %collective-permute-start.18 = (bf16[128,512]{1,0:T(8,128)(2,1)S(1)}, bf16[128,512]{1,0:T(8,128)(2,1)S(1)}, u32[]{:S(2)}, u32[]{:S(2)}) collective-permute-start(bf16[128,512]{1,0:T(8,128)(2,1)S(1)} %get-tuple-element.60.refs_0_), channel_id=1, source_target_pairs={{0,1},{1,0},{2,3},{3,2},{4,5},{5,4},{6,7},{7,6},{8,9},{9,8},{10,11... | collective-permute-start | bytes 393224 | tf_op jit(solution)/shard_map/ppermute | solution.py:185
  54.0 2.4 %collective-permute-start.20 = (bf16[512,128]{1,0:T(8,128)(2,1)S(1)}, bf16[512,128]{1,0:T(8,128)(2,1)S(1)}, u32[]{:S(2)}, u32[]{:S(2)}) collective-permute-start(bf16[512,128]{1,0:T(8,128)(2,1)S(1)} %slice.28), channel_id=1, source_target_pairs={{0,1},{1,0},{2,3},{3,2},{4,5},{5,4},{6,7},{7,6},{8,9},{9,8},{10,11... | collective-permute-start | bytes 393224 | tf_op jit(solution)/shard_map/ppermute | solution.py:185
  57.3 2.0 %collective-permute-start.22 = (bf16[512,512]{1,0:T(8,128)(2,1)S(1)}, bf16[512,512]{1,0:T(8,128)(2,1)S(1)}, u32[]{:S(2)}, u32[]{:S(2)}) collective-permute-start(bf16[512,512]{1,0:T(8,128)(2,1)S(1)} %get-tuple-element.79.sent), channel_id=1, source_target_pairs={{0,1},{1,0},{2,3},{3,2},{4,5},{5,4},{6,7},{7,6},{8,9},{9,8},{10,11... | collective-permute-start | bytes 1572872 | tf_op jit(solution)/shard_map/ppermute | solution.py:185
  58.3 7.2 %collective-permute-start.23 = (bf16[512,256]{1,0:T(8,128)(2,1)S(1)}, bf16[512,256]{1,0:T(8,128)(2,1)S(1)}, u32[]{:S(2)}, u32[]{:S(2)}) collective-permute-start(bf16[512,256]{1,0:T(8,128)(2,1)S(1)} %change.8), channel_id=1, source_target_pairs={{4,8},{8,4},{12,14},{14,12},{10,6},{6,10},{2,0},{0,2},{1,5},{5,1},... | collective-permute-start | bytes 786440 | tf_op jit(solution)/shard_map/ppermute | solution.py:185
  60.2 9.1 %collective-permute-start.24 = (bf16[512,256]{1,0:T(8,128)(2,1)S(1)}, bf16[512,256]{1,0:T(8,128)(2,1)S(1)}, u32[]{:S(2)}, u32[]{:S(2)}) collective-permute-start(bf16[512,256]{1,0:T(8,128)(2,1)S(1)} %change.9), channel_id=1, source_target_pairs={{0,4},{4,0},{8,12},{12,8},{14,10},{10,14},{6,2},{2,6},{5,9},{9,5},... | collective-permute-start | bytes 786440 | tf_op jit(solution)/shard_map/ppermute | solution.py:185
  66.1 8.6 %collective-permute-start.25 = (bf16[512,256]{1,0:T(8,128)(2,1)S(1)}, bf16[512,256]{1,0:T(8,128)(2,1)S(1)}, u32[]{:S(2)}, u32[]{:S(2)}) collective-permute-start(bf16[512,256]{1,0:T(8,128)(2,1)S(1)} %hop.5), channel_id=1, source_target_pairs={{0,4},{4,0},{8,12},{12,8},{14,10},{10,14},{6,2},{2,6},{5,9},{9,5},... | collective-permute-start | bytes 786440 | tf_op jit(solution)/shard_map/ppermute | solution.py:185
  69.9 7.6 %collective-permute-start.26 = (bf16[512,256]{1,0:T(8,128)(2,1)S(1)}, bf16[512,256]{1,0:T(8,128)(2,1)S(1)}, u32[]{:S(2)}, u32[]{:S(2)}) collective-permute-start(bf16[512,256]{1,0:T(8,128)(2,1)S(1)} %hop.6), channel_id=1, source_target_pairs={{4,8},{8,4},{12,14},{14,12},{10,6},{6,10},{2,0},{0,2},{1,5},{5,1},... | collective-permute-start | bytes 786440 | tf_op jit(solution)/shard_map/ppermute | solution.py:185
  75.3 9.2 %collective-permute-start.27 = (bf16[512,256]{1,0:T(8,128)(2,1)S(1)}, bf16[512,256]{1,0:T(8,128)(2,1)S(1)}, u32[]{:S(2)}, u32[]{:S(2)}) collective-permute-start(bf16[512,256]{1,0:T(8,128)(2,1)S(1)} %hop.7), channel_id=1, source_target_pairs={{4,8},{8,4},{12,14},{14,12},{10,6},{6,10},{2,0},{0,2},{1,5},{5,1},... | collective-permute-start | bytes 786440 | tf_op jit(solution)/shard_map/ppermute | solution.py:185
  78.1 10.3 %collective-permute-start.29 = (bf16[512,256]{1,0:T(8,128)(2,1)S(1)}, bf16[512,256]{1,0:T(8,128)(2,1)S(1)}, u32[]{:S(2)}, u32[]{:S(2)}) collective-permute-start(bf16[512,256]{1,0:T(8,128)(2,1)S(1)} %hop.8), channel_id=1, source_target_pairs={{0,4},{4,0},{8,12},{12,8},{14,10},{10,14},{6,2},{2,6},{5,9},{9,5},... | collective-permute-start | bytes 786440 | tf_op jit(solution)/shard_map/ppermute | solution.py:185
  85.1 6.9 %collective-permute-start.28 = (bf16[512,256]{1,0:T(8,128)(2,1)S(1)}, bf16[512,256]{1,0:T(8,128)(2,1)S(1)}, u32[]{:S(2)}, u32[]{:S(2)}) collective-permute-start(bf16[512,256]{1,0:T(8,128)(2,1)S(1)} %hop.9), channel_id=1, source_target_pairs={{0,4},{4,0},{8,12},{12,8},{14,10},{10,14},{6,2},{2,6},{5,9},{9,5},... | collective-permute-start | bytes 786440 | tf_op jit(solution)/shard_map/ppermute | solution.py:185
  88.5 3.5 %collective-permute-start.30 = (bf16[512,256]{1,0:T(8,128)(2,1)S(1)}, bf16[512,256]{1,0:T(8,128)(2,1)S(1)}, u32[]{:S(2)}, u32[]{:S(2)}) collective-permute-start(bf16[512,256]{1,0:T(8,128)(2,1)S(1)} %collective-permute-done.29), channel_id=1, source_target_pairs={{0,1},{1,0},{2,3},{3,2},{4,5},{5,4},{6,7},{7,6},{8,9},{9,8},{10,11... | collective-permute-start | bytes 786440 | tf_op jit(solution)/shard_map/ppermute | solution.py:185
  92.6 6.5 %collective-permute-start.31 = (bf16[512,256]{1,0:T(8,128)(2,1)S(1)}, bf16[512,256]{1,0:T(8,128)(2,1)S(1)}, u32[]{:S(2)}, u32[]{:S(2)}) collective-permute-start(bf16[512,256]{1,0:T(8,128)(2,1)S(1)} %last.1.change), channel_id=1, source_target_pairs={{0,2},{2,0},{1,3},{3,1},{4,6},{6,4},{5,7},{7,5},{8,10},{10,8},{9,1... | collective-permute-start | bytes 786440 | tf_op jit(solution)/shard_map/ppermute | solution.py:185
  (5 other events, 30.4 us)

commit v11 on v10

--- a/solution.py
+++ b/solution.py
@@ -146,14 +146,12 @@
     sent[...] = total.astype(BF16)
 
 
-def start_kernel(n_feats, place, sent, *refs):
-    rows = refs[0][...] if n_feats == 1 else jnp.concatenate([f[...] for f in refs[:n_feats]], axis=0)
-    refs[-1][...] = dot_nt(sent[...], rows).astype(BF16)
-
-
-def change_kernel(n_feats, place, sent, *refs):
-    rows = refs[0][...] if n_feats == 1 else jnp.concatenate([f[...] for f in refs[:n_feats]], axis=0)
-    refs[-1][...] = dot_nt(sent[...], rows)
+def change_kernel(counts, place, sent, *refs):
+    at = 0
+    for count, out in zip(counts, refs[sum(counts):]):
+        rows = refs[at][...] if count == 1 else jnp.concatenate([f[...] for f in refs[at:at + count]], axis=0)
+        out[...] = dot_nt(sent[...], rows).astype(out.dtype)
+        at += count
 
 
 def hop_kernel(place, change, came, out):
@@ -270,32 +268,32 @@
 
     whole, wide = like((padded, 2 * part)), like((padded, 2 * part), F32)
 
-    def product(kernel, out, update, *feats):
-        kernel = functools.partial(kernel, len(feats))
-        return call(kernel, out, place, (update, *feats), "change", 6)
+    def changes(update, blocks, outs):
+        counts = tuple(len(f) for f in blocks)
+        return call(
+            functools.partial(change_kernel, counts), outs, place, (update, *[f for b in blocks for f in b]), "change", 8
+        )
 
     hop = lambda ahead, came: call(hop_kernel, whole, place, (ahead, came), "hop", 4)
-    first = product(start_kernel, whole, sent, f4, f4_other)
+    (first,) = changes(sent, [(f4, f4_other)], (whole,))
     (sent_other,) = after((C(sent),), first)
+    ahead = changes(after((sent,), first)[0], [(f3,), (f2,), (f1,), (f0, f0_other)], (wide,) * 4)
     first = T(first)
-    second = product(start_kernel, whole, sent_other, f3)
-    ahead = product(change_kernel, wide, after((sent,), second)[0], f3)
+    (sent_other,) = after((sent_other,), *ahead)
+    second, *behind = changes(sent_other, [(f3,), (f2,), (f1,)], (whole, wide, wide))
+    (first,) = after((first,), second)
     second = S(second)
-    (first,) = after((first,), ahead)
-    for way, feats, later in ((S, f2, f2), (T, f1, f1)):
-        total = hop(ahead, first)
+    for i, (way, back) in enumerate(((S, T), (T, S), (S, None))):
+        total = hop(ahead[i], first)
         first = way(total)
-        ahead = product(change_kernel, wide, after((sent_other,), total)[0], feats)
-        (second,) = after((second,), ahead)
-        total = hop(ahead, second)
-        second = (T if way is S else S)(total)
-        ahead = product(change_kernel, wide, after((sent,), total)[0], later)
-        (first,) = after((first,), ahead)
-    total = hop(ahead, first)
-    first = S(total)
-    ahead = product(change_kernel, wide, after((sent,), total)[0], f0, f0_other)
-    given = C(after((second,), ahead)[0])
+        (second,) = after((second,), total)
+        if back:
+            total = hop(behind[i], second)
+            second = back(total)
+            (first,) = after((first,), total)
+    given = C(second)
     (first,) = after((first,), given)
+    ahead = ahead[3]
     own = call(last_kernel, whole, place, (ahead, first, given), "last", 4)
     new = None
     for i in (0, 1):

time: 101 us -> 98.3 us (0.973); the launches traced: 101 us -> 96.8 us
  Pallas kernels: 39.9 us -> 36.2 us
  starting transfers between devices: 33.1 us -> 31.6 us
  waiting for transfers between devices: 22.7 us -> 24 us
    pallas_call x26 -> x21, Pallas kernels: 39.9 us -> 36.2 us  [call(): pl.pallas_call(kernel, out_shape=out_shapes, in_specs=[pl.BlockSpec(memor...]
    ppermute x32, starting transfers between devices: 33.1 us -> 31.6 us  [swap(): lax.ppermute(x, axes, [p for a, b in pairs for p in ((a, b), (b, a))])]
    ppermute x32, waiting for transfers between devices: 22.7 us -> 24 us  [swap(): lax.ppermute(x, axes, [p for a, b in pairs for p in ((a, b), (b, a))])]
  transfers between devices with their start and end apart: 32 -> 32, of which waited for: 12 -> 13; matrix products, arithmetic and copies ran while one was open for 1% -> 1% of each run, Pallas kernels for 37% -> 34%
where the time goes in v11:
time: 98.3 us; the launch traced here: 96.8 us
  Pallas kernels  36.2 us (37%)
  starting transfers between devices  31.6 us (32%)
  waiting for transfers between devices  24 us (24%)
  local copies, waits for them, and re-layouts  2.56 us (3%)
  other arithmetic  1.24 us (1%)
  between operations  1.16 us (1%)
    pallas_call x21, Pallas kernels, call(): pl.pallas_call(kernel, out_shape=out_shapes, in_specs=[pl.BlockSpec(memor...  36.2 us
    ppermute x32, starting transfers between devices, swap(): lax.ppermute(x, axes, [p for a, b in pairs for p in ((a, b), (b, a))])  31.6 us
    ppermute x32, waiting for transfers between devices, swap(): lax.ppermute(x, axes, [p for a, b in pairs for p in ((a, b), (b, a))])  24 us
    unnamed x11, local copies, waits for them, and re-layouts  2.43 us
  transfers between devices with their start and end apart: 32, of which 13 were waited for; matrix products, arithmetic and copies ran while one was open for 1% of the time, Pallas kernels for 34%

profile of v11, /device:TPU:0, one launch (start us, length us, event | category | flops | bytes accessed | tf_op | source)
XLA Modules:
  0.0 96.8 jit_solution(856288633882983165)
XLA Ops:
  1.2 1.9 %prepare.1 = (bf16[256,1024]{1,0:T(8,128)(2,1)S(1)}, bf16[512,256]{1,0:T(8,128)(2,1)S(1)}, bf16[512,256]{1,0:T(8,128)(2,1)S(1)}) custom-call(s32[3]{0:T(128)S(1)} %pad_add_fusion.place, bf16[512,1024]{1,0:T(8,128)(2,1)} %inputs.1, s32[1,512]{1,0:T(1,128)} %bitcast.18, f32[500,512]{1,0:T(8,128)} %bitcast.13), custom_call_target="tpu_custom_call" | custom-call | tf_op jit(solution)/shard_map/prepare/pallas_call | solution.py:42
  3.3 2.0 %collective-permute-done = bf16[512,256]{1,0:T(8,128)(2,1)S(1)} collective-permute-done((bf16[512,256]{1,0:T(8,128)(2,1)S(1)}, bf16[512,256]{1,0:T(8,128)(2,1)S(1)}, u32[]{:S(2)}, u32[]{:S(2)}) %collective-permute-start) | collective-permute-done | bytes 262176 | tf_op jit(solution)/shard_map/ppermute | solution.py:183
  5.3 2.9 %collective-permute-start.5 = (bf16[256,1024]{1,0:T(8,128)(2,1)S(1)}, bf16[256,1024]{1,0:T(8,128)(2,1)S(1)}, u32[]{:S(2)}, u32[]{:S(2)}) collective-permute-start(bf16[256,1024]{1,0:T(8,128)(2,1)S(1)} %get-tuple-element.48.rows), channel_id=1, source_target_pairs={{0,4},{4,0},{8,12},{12,8},{14,10},{10,14},{6,2},{2,6},{5,9},{9,5},... | collective-permute-start | bytes 1572872 | tf_op jit(solution)/shard_map/ppermute | solution.py:183
  8.5 2.2 %copy-done.2 = f32[1,512,2048]{2,1,0:T(8,128)S(1)} copy-done((f32[1,512,2048]{2,1,0:T(8,128)S(1)}, f32[1,512,2048]{2,1,0:T(8,128)}, u32[]{:S(2)}) %copy-start.2) | copy-done | bytes 4194328
  10.7 1.4 %split.1 = (bf16[512,2048]{1,0:T(8,128)(2,1)S(1)}, bf16[512,2048]{1,0:T(8,128)(2,1)S(1)}) custom-call(s32[3]{0:T(128)S(1)} %pad_add_fusion.place, f32[512,2048]{1,0:T(8,128)S(1)} %bitcast.16), custom_call_target="tpu_custom_call" | custom-call | tf_op jit(solution)/shard_map/split/pallas_call | solution.py:42
  12.3 3.3 %block.5 = (bf16[128,1024]{1,0:T(8,128)(2,1)S(1)}, bf16[128,512]{1,0:T(8,128)(2,1)S(1)}) custom-call(s32[3]{0:T(128)S(1)} %pad_add_fusion.place, bf16[256,1024]{1,0:T(8,128)(2,1)S(1)} %get-tuple-element.48.rows, bf16[1024,1024]{1,0:T(8,128)(2,1)S(1)} %copy-done, bf16[1024,1024]{1,0:T(8,128)(2,1)S(1)} %collective-permute-done.1.w_other, ...), custom_call_target="tpu_custom_call" | custom-call | tf_op jit(solution)/shard_map/block/pallas_call | solution.py:42
  15.6 2.0 %collective-permute-start.9 = (bf16[256,1024]{1,0:T(8,128)(2,1)S(1)}, bf16[256,1024]{1,0:T(8,128)(2,1)S(1)}, u32[]{:S(2)}, u32[]{:S(2)}) collective-permute-start(bf16[256,1024]{1,0:T(8,128)(2,1)S(1)} %collective-permute-done.5.rows), channel_id=1, source_target_pairs={{4,8},{8,4},{12,14},{14,12},{10,6},{6,10},{2,0},{0,2},{1,5},{5,1},... | collective-permute-start | bytes 1572872 | tf_op jit(solution)/shard_map/ppermute | solution.py:183
  17.6 4.1 %block.6 = (bf16[256,1024]{1,0:T(8,128)(2,1)S(1)}, bf16[256,512]{1,0:T(8,128)(2,1)S(1)}) custom-call(s32[3]{0:T(128)S(1)} %pad_add_fusion.place, bf16[256,1024]{1,0:T(8,128)(2,1)S(1)} %collective-permute-done.5.rows, bf16[1024,1024]{1,0:T(8,128)(2,1)S(1)} %copy-done, bf16[1024,1024]{1,0:T(8,128)(2,1)S(1)} %collective-permute-done.1.w_other, ...), custom_call_target="tpu_custom_call" | custom-call | tf_op jit(solution)/shard_map/block/pallas_call | solution.py:42
  21.7 1.3 %collective-permute-done.4.refs_4_ = bf16[1024,256]{1,0:T(8,128)(2,1)S(1)} collective-permute-done((bf16[1024,256]{1,0:T(8,128)(2,1)S(1)}, bf16[1024,256]{1,0:T(8,128)(2,1)S(1)}, u32[]{:S(2)}, u32[]{:S(2)}) %collective-permute-start.4) | collective-permute-done | bytes 524320 | tf_op jit(solution)/shard_map/ppermute | solution.py:183
  23.0 2.2 %collective-permute-start.8 = (bf16[1024,256]{1,0:T(8,128)(2,1)S(1)}, bf16[1024,256]{1,0:T(8,128)(2,1)S(1)}, u32[]{:S(2)}, u32[]{:S(2)}) collective-permute-start(bf16[1024,256]{1,0:T(8,128)(2,1)S(1)} %collective-permute-done.4.refs_4_), channel_id=1, source_target_pairs={{4,8},{8,4},{12,14},{14,12},{10,6},{6,10},{2,0},{0,2},{1,5},{5,1},... | collective-permute-start | bytes 1572872 | tf_op jit(solution)/shard_map/ppermute | solution.py:183
  26.0 1.8 %collective-permute-start.13 = (bf16[256,1024]{1,0:T(8,128)(2,1)S(1)}, bf16[256,1024]{1,0:T(8,128)(2,1)S(1)}, u32[]{:S(2)}, u32[]{:S(2)}) collective-permute-start(bf16[256,1024]{1,0:T(8,128)(2,1)S(1)} %collective-permute-done.9.rows), channel_id=1, source_target_pairs={{0,4},{4,0},{8,12},{12,8},{14,10},{10,14},{6,2},{2,6},{5,9},{9,5},... | collective-permute-start | bytes 1572872 | tf_op jit(solution)/shard_map/ppermute | solution.py:183
  28.2 4.1 %block.7 = (bf16[256,1024]{1,0:T(8,128)(2,1)S(1)}, bf16[256,512]{1,0:T(8,128)(2,1)S(1)}) custom-call(s32[3]{0:T(128)S(1)} %pad_add_fusion.place, bf16[256,1024]{1,0:T(8,128)(2,1)S(1)} %collective-permute-done.9.rows, bf16[1024,1024]{1,0:T(8,128)(2,1)S(1)} %copy-done, bf16[1024,1024]{1,0:T(8,128)(2,1)S(1)} %collective-permute-done.1.w_other, ...), custom_call_target="tpu_custom_call" | custom-call | tf_op jit(solution)/shard_map/block/pallas_call | solution.py:42
  32.3 3.1 %collective-permute-done.8.refs_1_ = bf16[1024,256]{1,0:T(8,128)(2,1)S(1)} collective-permute-done((bf16[1024,256]{1,0:T(8,128)(2,1)S(1)}, bf16[1024,256]{1,0:T(8,128)(2,1)S(1)}, u32[]{:S(2)}, u32[]{:S(2)}) %collective-permute-start.8) | collective-permute-done | bytes 524320 | tf_op jit(solution)/shard_map/ppermute | solution.py:183
  35.4 2.4 %collective-permute-start.12 = (bf16[1024,256]{1,0:T(8,128)(2,1)S(1)}, bf16[1024,256]{1,0:T(8,128)(2,1)S(1)}, u32[]{:S(2)}, u32[]{:S(2)}) collective-permute-start(bf16[1024,256]{1,0:T(8,128)(2,1)S(1)} %collective-permute-done.8.refs_1_), channel_id=1, source_target_pairs={{0,4},{4,0},{8,12},{12,8},{14,10},{10,14},{6,2},{2,6},{5,9},{9,5},... | collective-permute-start | bytes 1572872 | tf_op jit(solution)/shard_map/ppermute | solution.py:183
  39.4 1.5 %begin.2.refs_0_ = f32[512,512]{1,0:T(8,128)S(1)} custom-call(s32[3]{0:T(128)S(1)} %pad_add_fusion.place, bf16[1024,256]{1,0:T(8,128)(2,1)S(1)} %constant_dynamic-update-slice_fusion.refs_0_.refs_2_, bf16[128,1024]{1,0:T(8,128)(2,1)S(1)} %get-tuple-element.51.refs_1_, bf16[1024,256]{1,0:T(8,128)(2,1)S(1)} %constant_dynamic-update-slice_fusion.refs_0_.refs_2_, ...), custom_call_target="tpu_custom_call" | custom-call | tf_op jit(solution)/shard_map/begin/pallas_call | solution.py:42
  41.0 1.6 %collective-permute-start.17 = (bf16[128,1024]{1,0:T(8,128)(2,1)S(1)}, bf16[128,1024]{1,0:T(8,128)(2,1)S(1)}, u32[]{:S(2)}, u32[]{:S(2)}) collective-permute-start(bf16[128,1024]{1,0:T(8,128)(2,1)S(1)} %slice.24), channel_id=1, source_target_pairs={{4,8},{8,4},{12,14},{14,12},{10,6},{6,10},{2,0},{0,2},{1,5},{5,1},... | collective-permute-start | bytes 786440 | tf_op jit(solution)/shard_map/ppermute | solution.py:183
  42.5 4.2 %block.8 = (bf16[256,1024]{1,0:T(8,128)(2,1)S(1)}, bf16[256,512]{1,0:T(8,128)(2,1)S(1)}) custom-call(s32[3]{0:T(128)S(1)} %pad_add_fusion.place, bf16[256,1024]{1,0:T(8,128)(2,1)S(1)} %collective-permute-done.13.rows, bf16[1024,1024]{1,0:T(8,128)(2,1)S(1)} %copy-done, bf16[1024,1024]{1,0:T(8,128)(2,1)S(1)} %collective-permute-done.1.w_other, ...), custom_call_target="tpu_custom_call" | custom-call | tf_op jit(solution)/shard_map/block/pallas_call | solution.py:42
  49.1 3.3 %block.9 = (bf16[128,1024]{1,0:T(8,128)(2,1)S(1)}, bf16[128,512]{1,0:T(8,128)(2,1)S(1)}) custom-call(s32[3]{0:T(128)S(1)} %pad_add_fusion.place, bf16[128,1024]{1,0:T(8,128)(2,1)S(1)} %collective-permute-done.17.rows, bf16[1024,1024]{1,0:T(8,128)(2,1)S(1)} %copy-done, bf16[1024,1024]{1,0:T(8,128)(2,1)S(1)} %collective-permute-done.1.w_other, ...), custom_call_target="tpu_custom_call" | custom-call | tf_op jit(solution)/shard_map/block/pallas_call | solution.py:42
  52.5 1.4 %collective-permute-done.19.refs_0_ = bf16[1024,128]{1,0:T(8,128)(2,1)S(1)} collective-permute-done((bf16[1024,128]{1,0:T(8,128)(2,1)S(1)}, bf16[1024,128]{1,0:T(8,128)(2,1)S(1)}, u32[]{:S(2)}, u32[]{:S(2)}) %collective-permute-start.19) | collective-permute-done | bytes 262176 | tf_op jit(solution)/shard_map/ppermute | solution.py:183
  54.5 1.8 %begin.3.begun = f32[512,512]{1,0:T(8,128)S(1)} custom-call(s32[3]{0:T(128)S(1)} %pad_add_fusion.place, f32[512,512]{1,0:T(8,128)S(1)} %begin.2.refs_0_, bf16[1024,256]{1,0:T(8,128)(2,1)S(1)} %collective-permute-done.8.refs_1_, bf16[256,1024]{1,0:T(8,128)(2,1)S(1)} %get-tuple-element.56.refs_2_, bf16[512,256]{1,0:T(8,128)(2,1)S(1)} %collective-permute-done.10.refs_3_, ...), custom_call_target="tpu_custom_call" | custom-call | tf_op jit(solution)/shard_map/begin/pallas_call | solution.py:42
  61.6 1.8 %collective-permute-start.25 = (bf16[512,256]{1,0:T(8,128)(2,1)S(1)}, bf16[512,256]{1,0:T(8,128)(2,1)S(1)}, u32[]{:S(2)}, u32[]{:S(2)}) collective-permute-start(bf16[512,256]{1,0:T(8,128)(2,1)S(1)} %get-tuple-element.78), channel_id=1, source_target_pairs={{0,4},{4,0},{8,12},{12,8},{14,10},{10,14},{6,2},{2,6},{5,9},{9,5},... | collective-permute-start | bytes 786440 | tf_op jit(solution)/shard_map/ppermute | solution.py:183
  63.4 1.3 %collective-permute-done.22.came = bf16[512,256]{1,0:T(8,128)(2,1)S(1)} collective-permute-done((bf16[512,256]{1,0:T(8,128)(2,1)S(1)}, bf16[512,256]{1,0:T(8,128)(2,1)S(1)}, u32[]{:S(2)}, u32[]{:S(2)}) %collective-permute-start.22) | collective-permute-done | bytes 262176 | tf_op jit(solution)/shard_map/ppermute | solution.py:183
  65.3 1.9 %collective-permute-start.24 = (bf16[512,256]{1,0:T(8,128)(2,1)S(1)}, bf16[512,256]{1,0:T(8,128)(2,1)S(1)}, u32[]{:S(2)}, u32[]{:S(2)}) collective-permute-start(bf16[512,256]{1,0:T(8,128)(2,1)S(1)} %hop.5), channel_id=1, source_target_pairs={{0,4},{4,0},{8,12},{12,8},{14,10},{10,14},{6,2},{2,6},{5,9},{9,5},... | collective-permute-start | bytes 786440 | tf_op jit(solution)/shard_map/ppermute | solution.py:183
  69.9 2.1 %collective-permute-done.24.came = bf16[512,256]{1,0:T(8,128)(2,1)S(1)} collective-permute-done((bf16[512,256]{1,0:T(8,128)(2,1)S(1)}, bf16[512,256]{1,0:T(8,128)(2,1)S(1)}, u32[]{:S(2)}, u32[]{:S(2)}) %collective-permute-start.24) | collective-permute-done | bytes 262176 | tf_op jit(solution)/shard_map/ppermute | solution.py:183
  75.7 2.1 %collective-permute-start.29 = (bf16[512,256]{1,0:T(8,128)(2,1)S(1)}, bf16[512,256]{1,0:T(8,128)(2,1)S(1)}, u32[]{:S(2)}, u32[]{:S(2)}) collective-permute-start(bf16[512,256]{1,0:T(8,128)(2,1)S(1)} %hop.8), channel_id=1, source_target_pairs={{0,4},{4,0},{8,12},{12,8},{14,10},{10,14},{6,2},{2,6},{5,9},{9,5},... | collective-permute-start | bytes 786440 | tf_op jit(solution)/shard_map/ppermute | solution.py:183
  77.9 2.2 %collective-permute-done.26.came = bf16[512,256]{1,0:T(8,128)(2,1)S(1)} collective-permute-done((bf16[512,256]{1,0:T(8,128)(2,1)S(1)}, bf16[512,256]{1,0:T(8,128)(2,1)S(1)}, u32[]{:S(2)}, u32[]{:S(2)}) %collective-permute-start.26) | collective-permute-done | bytes 262176 | tf_op jit(solution)/shard_map/ppermute | solution.py:183
  80.7 3.1 %collective-permute-start.28 = (bf16[512,256]{1,0:T(8,128)(2,1)S(1)}, bf16[512,256]{1,0:T(8,128)(2,1)S(1)}, u32[]{:S(2)}, u32[]{:S(2)}) collective-permute-start(bf16[512,256]{1,0:T(8,128)(2,1)S(1)} %hop.9), channel_id=1, source_target_pairs={{0,4},{4,0},{8,12},{12,8},{14,10},{10,14},{6,2},{2,6},{5,9},{9,5},... | collective-permute-start | bytes 786440 | tf_op jit(solution)/shard_map/ppermute | solution.py:183
  83.8 4.3 %collective-permute-done.28.came = bf16[512,256]{1,0:T(8,128)(2,1)S(1)} collective-permute-done((bf16[512,256]{1,0:T(8,128)(2,1)S(1)}, bf16[512,256]{1,0:T(8,128)(2,1)S(1)}, u32[]{:S(2)}, u32[]{:S(2)}) %collective-permute-start.28) | collective-permute-done | bytes 262176 | tf_op jit(solution)/shard_map/ppermute | solution.py:183
  88.8 1.6 %collective-permute-start.31 = (bf16[512,256]{1,0:T(8,128)(2,1)S(1)}, bf16[512,256]{1,0:T(8,128)(2,1)S(1)}, u32[]{:S(2)}, u32[]{:S(2)}) collective-permute-start(bf16[512,256]{1,0:T(8,128)(2,1)S(1)} %last.1.change), channel_id=1, source_target_pairs={{0,2},{2,0},{1,3},{3,1},{4,6},{6,4},{5,7},{7,5},{8,10},{10,8},{9,1... | collective-permute-start | bytes 786440 | tf_op jit(solution)/shard_map/ppermute | solution.py:183
  91.5 1.4 %apply.2.refs_0_ = f32[500,512]{1,0:T(8,128)} custom-call(s32[3]{0:T(128)S(1)} %pad_add_fusion.place, f32[500,512]{1,0:T(8,128)S(1)} %bitcast.14, bf16[512,256]{1,0:T(8,128)(2,1)S(1)} %last.1.change), custom_call_target="tpu_custom_call" | custom-call | tf_op jit(solution)/shard_map/apply/pallas_call | solution.py:42
  92.9 2.3 %collective-permute-done.31.change = bf16[512,256]{1,0:T(8,128)(2,1)S(1)} collective-permute-done((bf16[512,256]{1,0:T(8,128)(2,1)S(1)}, bf16[512,256]{1,0:T(8,128)(2,1)S(1)}, u32[]{:S(2)}, u32[]{:S(2)}) %collective-permute-start.31) | collective-permute-done | bytes 262176 | tf_op jit(solution)/shard_map/ppermute | solution.py:183
  95.2 1.4 %apply.3 = f32[500,512]{1,0:T(8,128)} custom-call(s32[3]{0:T(128)S(1)} %pad_add_fusion.place, f32[500,512]{1,0:T(8,128)S(1)} %bitcast.15, bf16[512,256]{1,0:T(8,128)(2,1)S(1)} %collective-permute-done.31.change, f32[500,512]{1,0:T(8,128)} %apply.2.refs_0_), custom_call_target="tpu_custom_call", output_to_operand_aliasing={{}: (3, {})} | custom-call | tf_op jit(solution)/shard_map/apply/pallas_call | solution.py:42
  (74 shorter events, 21.6 us)
Async XLA Ops:
  0.6 11.4 %collective-permute-start.1 = (bf16[1024,1024]{1,0:T(8,128)(2,1)}, bf16[1024,1024]{1,0:T(8,128)(2,1)S(1)}, u32[]{:S(2)}, u32[]{:S(2)}) collective-permute-start(bf16[1024,1024]{1,0:T(8,128)(2,1)} %w_own.9), channel_id=1, source_target_pairs={{0,1},{1,0},{2,3},{3,2},{4,5},{5,4},{6,7},{7,6},{8,9},{9,8},{10,11... | collective-permute-start | bytes 6291464 | tf_op jit(solution)/shard_map/ppermute | solution.py:183
  3.2 2.2 %collective-permute-start = (bf16[512,256]{1,0:T(8,128)(2,1)S(1)}, bf16[512,256]{1,0:T(8,128)(2,1)S(1)}, u32[]{:S(2)}, u32[]{:S(2)}) collective-permute-start(bf16[512,256]{1,0:T(8,128)(2,1)S(1)} %get-tuple-element.46), channel_id=1, source_target_pairs={{0,1},{1,0},{2,3},{3,2},{4,5},{5,4},{6,7},{7,6},{8,9},{9,8},{10,11... | collective-permute-start | bytes 786440 | tf_op jit(solution)/shard_map/ppermute | solution.py:183
  5.3 10.3 %collective-permute-start.5 = (bf16[256,1024]{1,0:T(8,128)(2,1)S(1)}, bf16[256,1024]{1,0:T(8,128)(2,1)S(1)}, u32[]{:S(2)}, u32[]{:S(2)}) collective-permute-start(bf16[256,1024]{1,0:T(8,128)(2,1)S(1)} %get-tuple-element.48.rows), channel_id=1, source_target_pairs={{0,4},{4,0},{8,12},{12,8},{14,10},{10,14},{6,2},{2,6},{5,9},{9,5},... | collective-permute-start | bytes 1572872 | tf_op jit(solution)/shard_map/ppermute | solution.py:183
  8.3 14.7 %collective-permute-start.4 = (bf16[1024,256]{1,0:T(8,128)(2,1)S(1)}, bf16[1024,256]{1,0:T(8,128)(2,1)S(1)}, u32[]{:S(2)}, u32[]{:S(2)}) collective-permute-start(bf16[1024,256]{1,0:T(8,128)(2,1)S(1)} %constant_dynamic-update-slice_fusion.refs_0_.refs_2_), channel_id=1, source_target_pairs={{0,4},{4,0},{8,12},{12,8},{14,10},{10,14},{6,2},{2,6},{5,9},{9,5},... | collective-permute-start | bytes 1572872 | tf_op jit(solution)/shard_map/ppermute | solution.py:183
  8.4 3.6 %collective-permute-start.2 = (bf16[1,1024]{1,0:T(2,128)(2,1)S(1)}, bf16[1,1024]{1,0:T(2,128)(2,1)S(1)}, u32[]{:S(2)}, u32[]{:S(2)}) collective-permute-start(bf16[1,1024]{1,0:T(2,128)(2,1)S(1)} %broadcast_in_dim.7.p_own), channel_id=1, source_target_pairs={{0,1},{1,0},{2,3},{3,2},{4,5},{5,4},{6,7},{7,6},{8,9},{9,8},{10,11... | collective-permute-start | bytes 6152 | tf_op jit(solution)/shard_map/ppermute | solution.py:183
  15.6 10.4 %collective-permute-start.9 = (bf16[256,1024]{1,0:T(8,128)(2,1)S(1)}, bf16[256,1024]{1,0:T(8,128)(2,1)S(1)}, u32[]{:S(2)}, u32[]{:S(2)}) collective-permute-start(bf16[256,1024]{1,0:T(8,128)(2,1)S(1)} %collective-permute-done.5.rows), channel_id=1, source_target_pairs={{4,8},{8,4},{12,14},{14,12},{10,6},{6,10},{2,0},{0,2},{1,5},{5,1},... | collective-permute-start | bytes 1572872 | tf_op jit(solution)/shard_map/ppermute | solution.py:183
  23.0 12.4 %collective-permute-start.8 = (bf16[1024,256]{1,0:T(8,128)(2,1)S(1)}, bf16[1024,256]{1,0:T(8,128)(2,1)S(1)}, u32[]{:S(2)}, u32[]{:S(2)}) collective-permute-start(bf16[1024,256]{1,0:T(8,128)(2,1)S(1)} %collective-permute-done.4.refs_4_), channel_id=1, source_target_pairs={{4,8},{8,4},{12,14},{14,12},{10,6},{6,10},{2,0},{0,2},{1,5},{5,1},... | collective-permute-start | bytes 1572872 | tf_op jit(solution)/shard_map/ppermute | solution.py:183
  25.2 14.2 %collective-permute-start.7 = (bf16[256,1024]{1,0:T(8,128)(2,1)S(1)}, bf16[256,1024]{1,0:T(8,128)(2,1)S(1)}, u32[]{:S(2)}, u32[]{:S(2)}) collective-permute-start(bf16[256,1024]{1,0:T(8,128)(2,1)S(1)} %get-tuple-element.53.refs_5_), channel_id=1, source_target_pairs={{0,1},{1,0},{2,3},{3,2},{4,5},{5,4},{6,7},{7,6},{8,9},{9,8},{10,11... | collective-permute-start | bytes 1572872 | tf_op jit(solution)/shard_map/ppermute | solution.py:183
  26.0 14.9 %collective-permute-start.13 = (bf16[256,1024]{1,0:T(8,128)(2,1)S(1)}, bf16[256,1024]{1,0:T(8,128)(2,1)S(1)}, u32[]{:S(2)}, u32[]{:S(2)}) collective-permute-start(bf16[256,1024]{1,0:T(8,128)(2,1)S(1)} %collective-permute-done.9.rows), channel_id=1, source_target_pairs={{0,4},{4,0},{8,12},{12,8},{14,10},{10,14},{6,2},{2,6},{5,9},{9,5},... | collective-permute-start | bytes 1572872 | tf_op jit(solution)/shard_map/ppermute | solution.py:183
  27.9 9.9 %collective-permute-start.6 = (bf16[512,256]{1,0:T(8,128)(2,1)S(1)}, bf16[512,256]{1,0:T(8,128)(2,1)S(1)}, u32[]{:S(2)}, u32[]{:S(2)}) collective-permute-start(bf16[512,256]{1,0:T(8,128)(2,1)S(1)} %slice.21), channel_id=1, source_target_pairs={{0,1},{1,0},{2,3},{3,2},{4,5},{5,4},{6,7},{7,6},{8,9},{9,8},{10,11... | collective-permute-start | bytes 786440 | tf_op jit(solution)/shard_map/ppermute | solution.py:183
  35.4 12.1 %collective-permute-start.12 = (bf16[1024,256]{1,0:T(8,128)(2,1)S(1)}, bf16[1024,256]{1,0:T(8,128)(2,1)S(1)}, u32[]{:S(2)}, u32[]{:S(2)}) collective-permute-start(bf16[1024,256]{1,0:T(8,128)(2,1)S(1)} %collective-permute-done.8.refs_1_), channel_id=1, source_target_pairs={{0,4},{4,0},{8,12},{12,8},{14,10},{10,14},{6,2},{2,6},{5,9},{9,5},... | collective-permute-start | bytes 1572872 | tf_op jit(solution)/shard_map/ppermute | solution.py:183
  37.7 1.5 %collective-permute-start.3 = (bf16[128,1024]{1,0:T(8,128)(2,1)S(1)}, bf16[128,1024]{1,0:T(8,128)(2,1)S(1)}, u32[]{:S(2)}, u32[]{:S(2)}) collective-permute-start(bf16[128,1024]{1,0:T(8,128)(2,1)S(1)} %get-tuple-element.51.refs_1_), channel_id=1, source_target_pairs={{0,1},{1,0},{2,3},{3,2},{4,5},{5,4},{6,7},{7,6},{8,9},{9,8},{10,11... | collective-permute-start | bytes 786440 | tf_op jit(solution)/shard_map/ppermute | solution.py:183
  37.7 3.2 %collective-permute-start.14 = (bf16[128,512]{1,0:T(8,128)(2,1)S(1)}, bf16[128,512]{1,0:T(8,128)(2,1)S(1)}, u32[]{:S(2)}, u32[]{:S(2)}) collective-permute-start(bf16[128,512]{1,0:T(8,128)(2,1)S(1)} %get-tuple-element.58.refs_3_), channel_id=1, source_target_pairs={{0,1},{1,0},{2,3},{3,2},{4,5},{5,4},{6,7},{7,6},{8,9},{9,8},{10,11... | collective-permute-start | bytes 393224 | tf_op jit(solution)/shard_map/ppermute | solution.py:183
  39.3 14.7 %collective-permute-start.11 = (bf16[256,1024]{1,0:T(8,128)(2,1)S(1)}, bf16[256,1024]{1,0:T(8,128)(2,1)S(1)}, u32[]{:S(2)}, u32[]{:S(2)}) collective-permute-start(bf16[256,1024]{1,0:T(8,128)(2,1)S(1)} %get-tuple-element.56.refs_2_), channel_id=1, source_target_pairs={{0,1},{1,0},{2,3},{3,2},{4,5},{5,4},{6,7},{7,6},{8,9},{9,8},{10,11... | collective-permute-start | bytes 1572872 | tf_op jit(solution)/shard_map/ppermute | solution.py:183
  41.0 7.4 %collective-permute-start.17 = (bf16[128,1024]{1,0:T(8,128)(2,1)S(1)}, bf16[128,1024]{1,0:T(8,128)(2,1)S(1)}, u32[]{:S(2)}, u32[]{:S(2)}) collective-permute-start(bf16[128,1024]{1,0:T(8,128)(2,1)S(1)} %slice.24), channel_id=1, source_target_pairs={{4,8},{8,4},{12,14},{14,12},{10,6},{6,10},{2,0},{0,2},{1,5},{5,1},... | collective-permute-start | bytes 786440 | tf_op jit(solution)/shard_map/ppermute | solution.py:183
  46.8 7.7 %collective-permute-start.16 = (bf16[256,1024]{1,0:T(8,128)(2,1)S(1)}, bf16[256,1024]{1,0:T(8,128)(2,1)S(1)}, u32[]{:S(2)}, u32[]{:S(2)}) collective-permute-start(bf16[256,1024]{1,0:T(8,128)(2,1)S(1)} %get-tuple-element.60.refs_6_), channel_id=1, source_target_pairs={{0,1},{1,0},{2,3},{3,2},{4,5},{5,4},{6,7},{7,6},{8,9},{9,8},{10,11... | collective-permute-start | bytes 1572872 | tf_op jit(solution)/shard_map/ppermute | solution.py:183
  46.9 5.6 %collective-permute-start.10 = (bf16[512,256]{1,0:T(8,128)(2,1)S(1)}, bf16[512,256]{1,0:T(8,128)(2,1)S(1)}, u32[]{:S(2)}, u32[]{:S(2)}) collective-permute-start(bf16[512,256]{1,0:T(8,128)(2,1)S(1)} %slice.22), channel_id=1, source_target_pairs={{0,1},{1,0},{2,3},{3,2},{4,5},{5,4},{6,7},{7,6},{8,9},{9,8},{10,11... | collective-permute-start | bytes 786440 | tf_op jit(solution)/shard_map/ppermute | solution.py:183
  47.5 6.4 %collective-permute-start.19 = (bf16[1024,128]{1,0:T(8,128)(2,1)S(1)}, bf16[1024,128]{1,0:T(8,128)(2,1)S(1)}, u32[]{:S(2)}, u32[]{:S(2)}) collective-permute-start(bf16[1024,128]{1,0:T(8,128)(2,1)S(1)} %slice.25), channel_id=1, source_target_pairs={{4,8},{8,4},{12,14},{14,12},{10,6},{6,10},{2,0},{0,2},{1,5},{5,1},... | collective-permute-start | bytes 786440 | tf_op jit(solution)/shard_map/ppermute | solution.py:183
  48.4 6.1 %collective-permute-start.15 = (bf16[512,256]{1,0:T(8,128)(2,1)S(1)}, bf16[512,256]{1,0:T(8,128)(2,1)S(1)}, u32[]{:S(2)}, u32[]{:S(2)}) collective-permute-start(bf16[512,256]{1,0:T(8,128)(2,1)S(1)} %slice.23), channel_id=1, source_target_pairs={{0,1},{1,0},{2,3},{3,2},{4,5},{5,4},{6,7},{7,6},{8,9},{9,8},{10,11... | collective-permute-start | bytes 786440 | tf_op jit(solution)/shard_map/ppermute | solution.py:183
  52.5 3.9 %collective-permute-start.21 = (bf16[128,1024]{1,0:T(8,128)(2,1)S(1)}, bf16[128,1024]{1,0:T(8,128)(2,1)S(1)}, u32[]{:S(2)}, u32[]{:S(2)}) collective-permute-start(bf16[128,1024]{1,0:T(8,128)(2,1)S(1)} %get-tuple-element.65.refs_1_), channel_id=1, source_target_pairs={{0,1},{1,0},{2,3},{3,2},{4,5},{5,4},{6,7},{7,6},{8,9},{9,8},{10,11... | collective-permute-start | bytes 786440 | tf_op jit(solution)/shard_map/ppermute | solution.py:183
  53.9 2.4 %collective-permute-start.18 = (bf16[128,512]{1,0:T(8,128)(2,1)S(1)}, bf16[128,512]{1,0:T(8,128)(2,1)S(1)}, u32[]{:S(2)}, u32[]{:S(2)}) collective-permute-start(bf16[128,512]{1,0:T(8,128)(2,1)S(1)} %get-tuple-element.63.refs_0_), channel_id=1, source_target_pairs={{0,1},{1,0},{2,3},{3,2},{4,5},{5,4},{6,7},{7,6},{8,9},{9,8},{10,11... | collective-permute-start | bytes 393224 | tf_op jit(solution)/shard_map/ppermute | solution.py:183
  54.0 2.4 %collective-permute-start.20 = (bf16[512,128]{1,0:T(8,128)(2,1)S(1)}, bf16[512,128]{1,0:T(8,128)(2,1)S(1)}, u32[]{:S(2)}, u32[]{:S(2)}) collective-permute-start(bf16[512,128]{1,0:T(8,128)(2,1)S(1)} %slice.28), channel_id=1, source_target_pairs={{0,1},{1,0},{2,3},{3,2},{4,5},{5,4},{6,7},{7,6},{8,9},{9,8},{10,11... | collective-permute-start | bytes 393224 | tf_op jit(solution)/shard_map/ppermute | solution.py:183
  57.3 3.1 %collective-permute-start.23 = (bf16[512,512]{1,0:T(8,128)(2,1)S(1)}, bf16[512,512]{1,0:T(8,128)(2,1)S(1)}, u32[]{:S(2)}, u32[]{:S(2)}) collective-permute-start(bf16[512,512]{1,0:T(8,128)(2,1)S(1)} %get-tuple-element.68.sent), channel_id=1, source_target_pairs={{0,1},{1,0},{2,3},{3,2},{4,5},{5,4},{6,7},{7,6},{8,9},{9,8},{10,11... | collective-permute-start | bytes 1572872 | tf_op jit(solution)/shard_map/ppermute | solution.py:183
  58.3 6.4 %collective-permute-start.22 = (bf16[512,256]{1,0:T(8,128)(2,1)S(1)}, bf16[512,256]{1,0:T(8,128)(2,1)S(1)}, u32[]{:S(2)}, u32[]{:S(2)}) collective-permute-start(bf16[512,256]{1,0:T(8,128)(2,1)S(1)} %change.3), channel_id=1, source_target_pairs={{4,8},{8,4},{12,14},{14,12},{10,6},{6,10},{2,0},{0,2},{1,5},{5,1},... | collective-permute-start | bytes 786440 | tf_op jit(solution)/shard_map/ppermute | solution.py:183
  61.6 6.4 %collective-permute-start.25 = (bf16[512,256]{1,0:T(8,128)(2,1)S(1)}, bf16[512,256]{1,0:T(8,128)(2,1)S(1)}, u32[]{:S(2)}, u32[]{:S(2)}) collective-permute-start(bf16[512,256]{1,0:T(8,128)(2,1)S(1)} %get-tuple-element.78), channel_id=1, source_target_pairs={{0,4},{4,0},{8,12},{12,8},{14,10},{10,14},{6,2},{2,6},{5,9},{9,5},... | collective-permute-start | bytes 786440 | tf_op jit(solution)/shard_map/ppermute | solution.py:183
  65.3 6.7 %collective-permute-start.24 = (bf16[512,256]{1,0:T(8,128)(2,1)S(1)}, bf16[512,256]{1,0:T(8,128)(2,1)S(1)}, u32[]{:S(2)}, u32[]{:S(2)}) collective-permute-start(bf16[512,256]{1,0:T(8,128)(2,1)S(1)} %hop.5), channel_id=1, source_target_pairs={{0,4},{4,0},{8,12},{12,8},{14,10},{10,14},{6,2},{2,6},{5,9},{9,5},... | collective-permute-start | bytes 786440 | tf_op jit(solution)/shard_map/ppermute | solution.py:183
  68.7 6.4 %collective-permute-start.27 = (bf16[512,256]{1,0:T(8,128)(2,1)S(1)}, bf16[512,256]{1,0:T(8,128)(2,1)S(1)}, u32[]{:S(2)}, u32[]{:S(2)}) collective-permute-start(bf16[512,256]{1,0:T(8,128)(2,1)S(1)} %hop.6), channel_id=1, source_target_pairs={{4,8},{8,4},{12,14},{14,12},{10,6},{6,10},{2,0},{0,2},{1,5},{5,1},... | collective-permute-start | bytes 786440 | tf_op jit(solution)/shard_map/ppermute | solution.py:183
  72.6 7.5 %collective-permute-start.26 = (bf16[512,256]{1,0:T(8,128)(2,1)S(1)}, bf16[512,256]{1,0:T(8,128)(2,1)S(1)}, u32[]{:S(2)}, u32[]{:S(2)}) collective-permute-start(bf16[512,256]{1,0:T(8,128)(2,1)S(1)} %hop.7), channel_id=1, source_target_pairs={{4,8},{8,4},{12,14},{14,12},{10,6},{6,10},{2,0},{0,2},{1,5},{5,1},... | collective-permute-start | bytes 786440 | tf_op jit(solution)/shard_map/ppermute | solution.py:183
  75.7 8.1 %collective-permute-start.29 = (bf16[512,256]{1,0:T(8,128)(2,1)S(1)}, bf16[512,256]{1,0:T(8,128)(2,1)S(1)}, u32[]{:S(2)}, u32[]{:S(2)}) collective-permute-start(bf16[512,256]{1,0:T(8,128)(2,1)S(1)} %hop.8), channel_id=1, source_target_pairs={{0,4},{4,0},{8,12},{12,8},{14,10},{10,14},{6,2},{2,6},{5,9},{9,5},... | collective-permute-start | bytes 786440 | tf_op jit(solution)/shard_map/ppermute | solution.py:183
  80.7 7.5 %collective-permute-start.28 = (bf16[512,256]{1,0:T(8,128)(2,1)S(1)}, bf16[512,256]{1,0:T(8,128)(2,1)S(1)}, u32[]{:S(2)}, u32[]{:S(2)}) collective-permute-start(bf16[512,256]{1,0:T(8,128)(2,1)S(1)} %hop.9), channel_id=1, source_target_pairs={{0,4},{4,0},{8,12},{12,8},{14,10},{10,14},{6,2},{2,6},{5,9},{9,5},... | collective-permute-start | bytes 786440 | tf_op jit(solution)/shard_map/ppermute | solution.py:183
  83.8 4.4 %collective-permute-start.30 = (bf16[512,256]{1,0:T(8,128)(2,1)S(1)}, bf16[512,256]{1,0:T(8,128)(2,1)S(1)}, u32[]{:S(2)}, u32[]{:S(2)}) collective-permute-start(bf16[512,256]{1,0:T(8,128)(2,1)S(1)} %collective-permute-done.29), channel_id=1, source_target_pairs={{0,1},{1,0},{2,3},{3,2},{4,5},{5,4},{6,7},{7,6},{8,9},{9,8},{10,11... | collective-permute-start | bytes 786440 | tf_op jit(solution)/shard_map/ppermute | solution.py:183
  88.8 6.4 %collective-permute-start.31 = (bf16[512,256]{1,0:T(8,128)(2,1)S(1)}, bf16[512,256]{1,0:T(8,128)(2,1)S(1)}, u32[]{:S(2)}, u32[]{:S(2)}) collective-permute-start(bf16[512,256]{1,0:T(8,128)(2,1)S(1)} %last.1.change), channel_id=1, source_target_pairs={{0,2},{2,0},{1,3},{3,1},{4,6},{6,4},{5,7},{7,5},{8,10},{10,8},{9,1... | collective-permute-start | bytes 786440 | tf_op jit(solution)/shard_map/ppermute | solution.py:183
  (5 other events, 44.1 us)

commit v12 on v11

--- a/solution.py
+++ b/solution.py
@@ -243,15 +243,15 @@
     q1, f1 = block(x1, 2 * part)
     (r1,) = after((r1,), q1)
     r2 = T(r1)
-    (x2,) = after((x2,), q1)
+    theirs = lambda r: C(r[padded:])
+    q0_other, f0_other = C(q0), C(f0)
+    (x2,) = after((x2,), q1, q0_other, f0_other)
     x3 = S(x2)
     q2, f2 = block(x2, 2 * part)
-    (r2,) = after((r2,), q2)
+    begun = begin([(r0, q0), (r0, q0_other), (r1, q1), (theirs(r1), C(q1))])
+    (r2,) = after((r2,), q2, begun)
     r3 = S(r2)
-    theirs = lambda r: C(r[padded:])
-    q0_other, f0_other = C(q0), C(f0)
-    begun = begin([(r0, q0), (r0, q0_other), (r1, q1), (theirs(r1), C(q1))])
-    (x3,) = after((x3,), begun, f0_other)
+    (x3,) = after((x3,), begun)
     x4 = T(x3[:part])
     q3, f3 = block(x3, 2 * part)
     (r3,) = after((r3,), q3)

time: 98.3 us -> 98.6 us (level)
  waiting for transfers between devices: 24 us -> 21.9 us
  starting transfers between devices: 31.6 us -> 33.6 us
    ppermute x32, waiting for transfers between devices: 24 us -> 21.9 us  [swap(): lax.ppermute(x, axes, [p for a, b in pairs for p in ((a, b), (b, a))])]
    ppermute x32, starting transfers between devices: 31.6 us -> 33.6 us  [swap(): lax.ppermute(x, axes, [p for a, b in pairs for p in ((a, b), (b, a))])]
  transfers between devices with their start and end apart: 32 -> 32, of which waited for: 13 -> 15; matrix products, arithmetic and copies ran while one was open for 1% -> 1% of each run, Pallas kernels for 34% -> 34%
where the time goes in v12:
time: 98.6 us; the launch traced here: 96.7 us
  Pallas kernels  36.3 us (37%)
  starting transfers between devices  33.6 us (34%)
  waiting for transfers between devices  21.9 us (22%)
  local copies, waits for them, and re-layouts  2.56 us (3%)
  other arithmetic  1.24 us (1%)
  between operations  1.16 us (1%)
    pallas_call x21, Pallas kernels, call(): pl.pallas_call(kernel, out_shape=out_shapes, in_specs=[pl.BlockSpec(memor...  36.3 us
    ppermute x32, starting transfers between devices, swap(): lax.ppermute(x, axes, [p for a, b in pairs for p in ((a, b), (b, a))])  33.6 us
    ppermute x32, waiting for transfers between devices, swap(): lax.ppermute(x, axes, [p for a, b in pairs for p in ((a, b), (b, a))])  21.9 us
    unnamed x11, local copies, waits for them, and re-layouts  2.43 us
  transfers between devices with their start and end apart: 32, of which 15 were waited for; matrix products, arithmetic and copies ran while one was open for 1% of the time, Pallas kernels for 34%

profile of v12, /device:TPU:0, one launch (start us, length us, event | category | flops | bytes accessed | tf_op | source)
XLA Modules:
  0.0 96.7 jit_solution(15471928352495424402)
XLA Ops:
  1.2 1.9 %prepare.1 = (bf16[256,1024]{1,0:T(8,128)(2,1)S(1)}, bf16[512,256]{1,0:T(8,128)(2,1)S(1)}, bf16[512,256]{1,0:T(8,128)(2,1)S(1)}) custom-call(s32[3]{0:T(128)S(1)} %pad_add_fusion.place, bf16[512,1024]{1,0:T(8,128)(2,1)} %inputs.1, s32[1,512]{1,0:T(1,128)} %bitcast.18, f32[500,512]{1,0:T(8,128)} %bitcast.13), custom_call_target="tpu_custom_call" | custom-call | tf_op jit(solution)/shard_map/prepare/pallas_call | solution.py:42
  3.3 2.0 %collective-permute-done = bf16[512,256]{1,0:T(8,128)(2,1)S(1)} collective-permute-done((bf16[512,256]{1,0:T(8,128)(2,1)S(1)}, bf16[512,256]{1,0:T(8,128)(2,1)S(1)}, u32[]{:S(2)}, u32[]{:S(2)}) %collective-permute-start) | collective-permute-done | bytes 262176 | tf_op jit(solution)/shard_map/ppermute | solution.py:183
  5.3 2.9 %collective-permute-start.5 = (bf16[256,1024]{1,0:T(8,128)(2,1)S(1)}, bf16[256,1024]{1,0:T(8,128)(2,1)S(1)}, u32[]{:S(2)}, u32[]{:S(2)}) collective-permute-start(bf16[256,1024]{1,0:T(8,128)(2,1)S(1)} %get-tuple-element.48.rows), channel_id=1, source_target_pairs={{0,4},{4,0},{8,12},{12,8},{14,10},{10,14},{6,2},{2,6},{5,9},{9,5},... | collective-permute-start | bytes 1572872 | tf_op jit(solution)/shard_map/ppermute | solution.py:183
  8.5 2.2 %copy-done.2 = f32[1,512,2048]{2,1,0:T(8,128)S(1)} copy-done((f32[1,512,2048]{2,1,0:T(8,128)S(1)}, f32[1,512,2048]{2,1,0:T(8,128)}, u32[]{:S(2)}) %copy-start.2) | copy-done | bytes 4194328
  12.3 3.3 %block.5 = (bf16[128,1024]{1,0:T(8,128)(2,1)S(1)}, bf16[128,512]{1,0:T(8,128)(2,1)S(1)}) custom-call(s32[3]{0:T(128)S(1)} %pad_add_fusion.place, bf16[256,1024]{1,0:T(8,128)(2,1)S(1)} %get-tuple-element.48.rows, bf16[1024,1024]{1,0:T(8,128)(2,1)S(1)} %copy-done, bf16[1024,1024]{1,0:T(8,128)(2,1)S(1)} %collective-permute-done.1.w_other, ...), custom_call_target="tpu_custom_call" | custom-call | tf_op jit(solution)/shard_map/block/pallas_call | solution.py:42
  15.6 2.0 %collective-permute-start.9 = (bf16[256,1024]{1,0:T(8,128)(2,1)S(1)}, bf16[256,1024]{1,0:T(8,128)(2,1)S(1)}, u32[]{:S(2)}, u32[]{:S(2)}) collective-permute-start(bf16[256,1024]{1,0:T(8,128)(2,1)S(1)} %collective-permute-done.5.rows), channel_id=1, source_target_pairs={{4,8},{8,4},{12,14},{14,12},{10,6},{6,10},{2,0},{0,2},{1,5},{5,1},... | collective-permute-start | bytes 1572872 | tf_op jit(solution)/shard_map/ppermute | solution.py:183
  17.6 4.1 %block.6 = (bf16[256,1024]{1,0:T(8,128)(2,1)S(1)}, bf16[256,512]{1,0:T(8,128)(2,1)S(1)}) custom-call(s32[3]{0:T(128)S(1)} %pad_add_fusion.place, bf16[256,1024]{1,0:T(8,128)(2,1)S(1)} %collective-permute-done.5.rows, bf16[1024,1024]{1,0:T(8,128)(2,1)S(1)} %copy-done, bf16[1024,1024]{1,0:T(8,128)(2,1)S(1)} %collective-permute-done.1.w_other, ...), custom_call_target="tpu_custom_call" | custom-call | tf_op jit(solution)/shard_map/block/pallas_call | solution.py:42
  23.0 2.2 %collective-permute-start.8 = (bf16[1024,256]{1,0:T(8,128)(2,1)S(1)}, bf16[1024,256]{1,0:T(8,128)(2,1)S(1)}, u32[]{:S(2)}, u32[]{:S(2)}) collective-permute-start(bf16[1024,256]{1,0:T(8,128)(2,1)S(1)} %collective-permute-done.4.refs_4_), channel_id=1, source_target_pairs={{4,8},{8,4},{12,14},{14,12},{10,6},{6,10},{2,0},{0,2},{1,5},{5,1},... | collective-permute-start | bytes 1572872 | tf_op jit(solution)/shard_map/ppermute | solution.py:183
  26.9 1.7 %collective-permute-start.14 = (bf16[256,1024]{1,0:T(8,128)(2,1)S(1)}, bf16[256,1024]{1,0:T(8,128)(2,1)S(1)}, u32[]{:S(2)}, u32[]{:S(2)}) collective-permute-start(bf16[256,1024]{1,0:T(8,128)(2,1)S(1)} %collective-permute-done.9.rows), channel_id=1, source_target_pairs={{0,4},{4,0},{8,12},{12,8},{14,10},{10,14},{6,2},{2,6},{5,9},{9,5},... | collective-permute-start | bytes 1572872 | tf_op jit(solution)/shard_map/ppermute | solution.py:183
  28.6 4.1 %block.7 = (bf16[256,1024]{1,0:T(8,128)(2,1)S(1)}, bf16[256,512]{1,0:T(8,128)(2,1)S(1)}) custom-call(s32[3]{0:T(128)S(1)} %pad_add_fusion.place, bf16[256,1024]{1,0:T(8,128)(2,1)S(1)} %collective-permute-done.9.rows, bf16[1024,1024]{1,0:T(8,128)(2,1)S(1)} %copy-done, bf16[1024,1024]{1,0:T(8,128)(2,1)S(1)} %collective-permute-done.1.w_other, ...), custom_call_target="tpu_custom_call" | custom-call | tf_op jit(solution)/shard_map/block/pallas_call | solution.py:42
  32.7 1.5 %begin.2.refs_0_ = f32[512,512]{1,0:T(8,128)S(1)} custom-call(s32[3]{0:T(128)S(1)} %pad_add_fusion.place, bf16[1024,256]{1,0:T(8,128)(2,1)S(1)} %constant_dynamic-update-slice_fusion.refs_0_.refs_2_, bf16[128,1024]{1,0:T(8,128)(2,1)S(1)} %get-tuple-element.51.refs_1_, bf16[1024,256]{1,0:T(8,128)(2,1)S(1)} %constant_dynamic-update-slice_fusion.refs_0_.refs_2_, ...), custom_call_target="tpu_custom_call" | custom-call | tf_op jit(solution)/shard_map/begin/pallas_call | solution.py:42
  35.2 2.1 %collective-permute-start.13 = (bf16[1024,256]{1,0:T(8,128)(2,1)S(1)}, bf16[1024,256]{1,0:T(8,128)(2,1)S(1)}, u32[]{:S(2)}, u32[]{:S(2)}) collective-permute-start(bf16[1024,256]{1,0:T(8,128)(2,1)S(1)} %collective-permute-done.8.refs_1_), channel_id=1, source_target_pairs={{0,4},{4,0},{8,12},{12,8},{14,10},{10,14},{6,2},{2,6},{5,9},{9,5},... | collective-permute-start | bytes 1572872 | tf_op jit(solution)/shard_map/ppermute | solution.py:183
  37.9 2.0 %collective-permute-start.17 = (bf16[128,1024]{1,0:T(8,128)(2,1)S(1)}, bf16[128,1024]{1,0:T(8,128)(2,1)S(1)}, u32[]{:S(2)}, u32[]{:S(2)}) collective-permute-start(bf16[128,1024]{1,0:T(8,128)(2,1)S(1)} %slice.24), channel_id=1, source_target_pairs={{4,8},{8,4},{12,14},{14,12},{10,6},{6,10},{2,0},{0,2},{1,5},{5,1},... | collective-permute-start | bytes 786440 | tf_op jit(solution)/shard_map/ppermute | solution.py:183
  39.9 4.3 %block.8 = (bf16[256,1024]{1,0:T(8,128)(2,1)S(1)}, bf16[256,512]{1,0:T(8,128)(2,1)S(1)}) custom-call(s32[3]{0:T(128)S(1)} %pad_add_fusion.place, bf16[256,1024]{1,0:T(8,128)(2,1)S(1)} %collective-permute-done.14.rows, bf16[1024,1024]{1,0:T(8,128)(2,1)S(1)} %copy-done, bf16[1024,1024]{1,0:T(8,128)(2,1)S(1)} %collective-permute-done.1.w_other, ...), custom_call_target="tpu_custom_call" | custom-call | tf_op jit(solution)/shard_map/block/pallas_call | solution.py:42
  44.8 2.5 %collective-permute-done.13.refs_5_ = bf16[1024,256]{1,0:T(8,128)(2,1)S(1)} collective-permute-done((bf16[1024,256]{1,0:T(8,128)(2,1)S(1)}, bf16[1024,256]{1,0:T(8,128)(2,1)S(1)}, u32[]{:S(2)}, u32[]{:S(2)}) %collective-permute-start.13) | collective-permute-done | bytes 524320 | tf_op jit(solution)/shard_map/ppermute | solution.py:183
  47.3 2.4 %collective-permute-start.19 = (bf16[1024,128]{1,0:T(8,128)(2,1)S(1)}, bf16[1024,128]{1,0:T(8,128)(2,1)S(1)}, u32[]{:S(2)}, u32[]{:S(2)}) collective-permute-start(bf16[1024,128]{1,0:T(8,128)(2,1)S(1)} %slice.25), channel_id=1, source_target_pairs={{4,8},{8,4},{12,14},{14,12},{10,6},{6,10},{2,0},{0,2},{1,5},{5,1},... | collective-permute-start | bytes 786440 | tf_op jit(solution)/shard_map/ppermute | solution.py:183
  49.9 3.3 %block.9 = (bf16[128,1024]{1,0:T(8,128)(2,1)S(1)}, bf16[128,512]{1,0:T(8,128)(2,1)S(1)}) custom-call(s32[3]{0:T(128)S(1)} %pad_add_fusion.place, bf16[128,1024]{1,0:T(8,128)(2,1)S(1)} %collective-permute-done.17.rows, bf16[1024,1024]{1,0:T(8,128)(2,1)S(1)} %copy-done, bf16[1024,1024]{1,0:T(8,128)(2,1)S(1)} %collective-permute-done.1.w_other, ...), custom_call_target="tpu_custom_call" | custom-call | tf_op jit(solution)/shard_map/block/pallas_call | solution.py:42
  54.7 1.8 %begin.3.begun = f32[512,512]{1,0:T(8,128)S(1)} custom-call(s32[3]{0:T(128)S(1)} %pad_add_fusion.place, f32[512,512]{1,0:T(8,128)S(1)} %begin.2.refs_0_, bf16[1024,256]{1,0:T(8,128)(2,1)S(1)} %collective-permute-done.8.refs_1_, bf16[256,1024]{1,0:T(8,128)(2,1)S(1)} %get-tuple-element.57.refs_2_, bf16[512,256]{1,0:T(8,128)(2,1)S(1)} %collective-permute-done.11.refs_3_, ...), custom_call_target="tpu_custom_call" | custom-call | tf_op jit(solution)/shard_map/begin/pallas_call | solution.py:42
  58.5 2.1 %collective-permute-start.22 = (bf16[512,256]{1,0:T(8,128)(2,1)S(1)}, bf16[512,256]{1,0:T(8,128)(2,1)S(1)}, u32[]{:S(2)}, u32[]{:S(2)}) collective-permute-start(bf16[512,256]{1,0:T(8,128)(2,1)S(1)} %change.3), channel_id=1, source_target_pairs={{4,8},{8,4},{12,14},{14,12},{10,6},{6,10},{2,0},{0,2},{1,5},{5,1},... | collective-permute-start | bytes 786440 | tf_op jit(solution)/shard_map/ppermute | solution.py:183
  63.0 1.7 %collective-permute-start.25 = (bf16[512,256]{1,0:T(8,128)(2,1)S(1)}, bf16[512,256]{1,0:T(8,128)(2,1)S(1)}, u32[]{:S(2)}, u32[]{:S(2)}) collective-permute-start(bf16[512,256]{1,0:T(8,128)(2,1)S(1)} %get-tuple-element.78), channel_id=1, source_target_pairs={{0,4},{4,0},{8,12},{12,8},{14,10},{10,14},{6,2},{2,6},{5,9},{9,5},... | collective-permute-start | bytes 786440 | tf_op jit(solution)/shard_map/ppermute | solution.py:183
  65.5 1.7 %collective-permute-start.24 = (bf16[512,256]{1,0:T(8,128)(2,1)S(1)}, bf16[512,256]{1,0:T(8,128)(2,1)S(1)}, u32[]{:S(2)}, u32[]{:S(2)}) collective-permute-start(bf16[512,256]{1,0:T(8,128)(2,1)S(1)} %hop.5), channel_id=1, source_target_pairs={{0,4},{4,0},{8,12},{12,8},{14,10},{10,14},{6,2},{2,6},{5,9},{9,5},... | collective-permute-start | bytes 786440 | tf_op jit(solution)/shard_map/ppermute | solution.py:183
  67.3 2.2 %collective-permute-done.25.came = bf16[512,256]{1,0:T(8,128)(2,1)S(1)} collective-permute-done((bf16[512,256]{1,0:T(8,128)(2,1)S(1)}, bf16[512,256]{1,0:T(8,128)(2,1)S(1)}, u32[]{:S(2)}, u32[]{:S(2)}) %collective-permute-start.25) | collective-permute-done | bytes 262176 | tf_op jit(solution)/shard_map/ppermute | solution.py:183
  71.3 1.5 %collective-permute-done.24.came = bf16[512,256]{1,0:T(8,128)(2,1)S(1)} collective-permute-done((bf16[512,256]{1,0:T(8,128)(2,1)S(1)}, bf16[512,256]{1,0:T(8,128)(2,1)S(1)}, u32[]{:S(2)}, u32[]{:S(2)}) %collective-permute-start.24) | collective-permute-done | bytes 262176 | tf_op jit(solution)/shard_map/ppermute | solution.py:183
  73.3 1.9 %collective-permute-start.26 = (bf16[512,256]{1,0:T(8,128)(2,1)S(1)}, bf16[512,256]{1,0:T(8,128)(2,1)S(1)}, u32[]{:S(2)}, u32[]{:S(2)}) collective-permute-start(bf16[512,256]{1,0:T(8,128)(2,1)S(1)} %hop.7), channel_id=1, source_target_pairs={{4,8},{8,4},{12,14},{14,12},{10,6},{6,10},{2,0},{0,2},{1,5},{5,1},... | collective-permute-start | bytes 786440 | tf_op jit(solution)/shard_map/ppermute | solution.py:183
  77.1 1.7 %collective-permute-start.29 = (bf16[512,256]{1,0:T(8,128)(2,1)S(1)}, bf16[512,256]{1,0:T(8,128)(2,1)S(1)}, u32[]{:S(2)}, u32[]{:S(2)}) collective-permute-start(bf16[512,256]{1,0:T(8,128)(2,1)S(1)} %hop.8), channel_id=1, source_target_pairs={{0,4},{4,0},{8,12},{12,8},{14,10},{10,14},{6,2},{2,6},{5,9},{9,5},... | collective-permute-start | bytes 786440 | tf_op jit(solution)/shard_map/ppermute | solution.py:183
  78.8 2.2 %collective-permute-done.26.came = bf16[512,256]{1,0:T(8,128)(2,1)S(1)} collective-permute-done((bf16[512,256]{1,0:T(8,128)(2,1)S(1)}, bf16[512,256]{1,0:T(8,128)(2,1)S(1)}, u32[]{:S(2)}, u32[]{:S(2)}) %collective-permute-start.26) | collective-permute-done | bytes 262176 | tf_op jit(solution)/shard_map/ppermute | solution.py:183
  81.6 2.0 %collective-permute-start.28 = (bf16[512,256]{1,0:T(8,128)(2,1)S(1)}, bf16[512,256]{1,0:T(8,128)(2,1)S(1)}, u32[]{:S(2)}, u32[]{:S(2)}) collective-permute-start(bf16[512,256]{1,0:T(8,128)(2,1)S(1)} %hop.9), channel_id=1, source_target_pairs={{0,4},{4,0},{8,12},{12,8},{14,10},{10,14},{6,2},{2,6},{5,9},{9,5},... | collective-permute-start | bytes 786440 | tf_op jit(solution)/shard_map/ppermute | solution.py:183
  83.6 4.5 %collective-permute-done.28.came = bf16[512,256]{1,0:T(8,128)(2,1)S(1)} collective-permute-done((bf16[512,256]{1,0:T(8,128)(2,1)S(1)}, bf16[512,256]{1,0:T(8,128)(2,1)S(1)}, u32[]{:S(2)}, u32[]{:S(2)}) %collective-permute-start.28) | collective-permute-done | bytes 262176 | tf_op jit(solution)/shard_map/ppermute | solution.py:183
  88.7 2.1 %collective-permute-start.31 = (bf16[512,256]{1,0:T(8,128)(2,1)S(1)}, bf16[512,256]{1,0:T(8,128)(2,1)S(1)}, u32[]{:S(2)}, u32[]{:S(2)}) collective-permute-start(bf16[512,256]{1,0:T(8,128)(2,1)S(1)} %last.1.change), channel_id=1, source_target_pairs={{0,2},{2,0},{1,3},{3,1},{4,6},{6,4},{5,7},{7,5},{8,10},{10,8},{9,1... | collective-permute-start | bytes 786440 | tf_op jit(solution)/shard_map/ppermute | solution.py:183
  91.9 1.4 %apply.2.refs_0_ = f32[500,512]{1,0:T(8,128)} custom-call(s32[3]{0:T(128)S(1)} %pad_add_fusion.place, f32[500,512]{1,0:T(8,128)S(1)} %bitcast.14, bf16[512,256]{1,0:T(8,128)(2,1)S(1)} %last.1.change), custom_call_target="tpu_custom_call" | custom-call | tf_op jit(solution)/shard_map/apply/pallas_call | solution.py:42
  93.3 1.8 %collective-permute-done.31.change = bf16[512,256]{1,0:T(8,128)(2,1)S(1)} collective-permute-done((bf16[512,256]{1,0:T(8,128)(2,1)S(1)}, bf16[512,256]{1,0:T(8,128)(2,1)S(1)}, u32[]{:S(2)}, u32[]{:S(2)}) %collective-permute-start.31) | collective-permute-done | bytes 262176 | tf_op jit(solution)/shard_map/ppermute | solution.py:183
  95.1 1.4 %apply.3 = f32[500,512]{1,0:T(8,128)} custom-call(s32[3]{0:T(128)S(1)} %pad_add_fusion.place, f32[500,512]{1,0:T(8,128)S(1)} %bitcast.15, bf16[512,256]{1,0:T(8,128)(2,1)S(1)} %collective-permute-done.31.change, f32[500,512]{1,0:T(8,128)} %apply.2.refs_0_), custom_call_target="tpu_custom_call", output_to_operand_aliasing={{}: (3, {})} | custom-call | tf_op jit(solution)/shard_map/apply/pallas_call | solution.py:42
  (74 shorter events, 21.0 us)
Async XLA Ops:
  0.6 11.4 %collective-permute-start.1 = (bf16[1024,1024]{1,0:T(8,128)(2,1)}, bf16[1024,1024]{1,0:T(8,128)(2,1)S(1)}, u32[]{:S(2)}, u32[]{:S(2)}) collective-permute-start(bf16[1024,1024]{1,0:T(8,128)(2,1)} %w_own.9), channel_id=1, source_target_pairs={{0,1},{1,0},{2,3},{3,2},{4,5},{5,4},{6,7},{7,6},{8,9},{9,8},{10,11... | collective-permute-start | bytes 6291464 | tf_op jit(solution)/shard_map/ppermute | solution.py:183
  3.2 2.2 %collective-permute-start = (bf16[512,256]{1,0:T(8,128)(2,1)S(1)}, bf16[512,256]{1,0:T(8,128)(2,1)S(1)}, u32[]{:S(2)}, u32[]{:S(2)}) collective-permute-start(bf16[512,256]{1,0:T(8,128)(2,1)S(1)} %get-tuple-element.46), channel_id=1, source_target_pairs={{0,1},{1,0},{2,3},{3,2},{4,5},{5,4},{6,7},{7,6},{8,9},{9,8},{10,11... | collective-permute-start | bytes 786440 | tf_op jit(solution)/shard_map/ppermute | solution.py:183
  5.3 10.3 %collective-permute-start.5 = (bf16[256,1024]{1,0:T(8,128)(2,1)S(1)}, bf16[256,1024]{1,0:T(8,128)(2,1)S(1)}, u32[]{:S(2)}, u32[]{:S(2)}) collective-permute-start(bf16[256,1024]{1,0:T(8,128)(2,1)S(1)} %get-tuple-element.48.rows), channel_id=1, source_target_pairs={{0,4},{4,0},{8,12},{12,8},{14,10},{10,14},{6,2},{2,6},{5,9},{9,5},... | collective-permute-start | bytes 1572872 | tf_op jit(solution)/shard_map/ppermute | solution.py:183
  8.3 14.7 %collective-permute-start.4 = (bf16[1024,256]{1,0:T(8,128)(2,1)S(1)}, bf16[1024,256]{1,0:T(8,128)(2,1)S(1)}, u32[]{:S(2)}, u32[]{:S(2)}) collective-permute-start(bf16[1024,256]{1,0:T(8,128)(2,1)S(1)} %constant_dynamic-update-slice_fusion.refs_0_.refs_2_), channel_id=1, source_target_pairs={{0,4},{4,0},{8,12},{12,8},{14,10},{10,14},{6,2},{2,6},{5,9},{9,5},... | collective-permute-start | bytes 1572872 | tf_op jit(solution)/shard_map/ppermute | solution.py:183
  8.4 3.6 %collective-permute-start.2 = (bf16[1,1024]{1,0:T(2,128)(2,1)S(1)}, bf16[1,1024]{1,0:T(2,128)(2,1)S(1)}, u32[]{:S(2)}, u32[]{:S(2)}) collective-permute-start(bf16[1,1024]{1,0:T(2,128)(2,1)S(1)} %broadcast_in_dim.7.p_own), channel_id=1, source_target_pairs={{0,1},{1,0},{2,3},{3,2},{4,5},{5,4},{6,7},{7,6},{8,9},{9,8},{10,11... | collective-permute-start | bytes 6152 | tf_op jit(solution)/shard_map/ppermute | solution.py:183
  15.6 11.3 %collective-permute-start.9 = (bf16[256,1024]{1,0:T(8,128)(2,1)S(1)}, bf16[256,1024]{1,0:T(8,128)(2,1)S(1)}, u32[]{:S(2)}, u32[]{:S(2)}) collective-permute-start(bf16[256,1024]{1,0:T(8,128)(2,1)S(1)} %collective-permute-done.5.rows), channel_id=1, source_target_pairs={{4,8},{8,4},{12,14},{14,12},{10,6},{6,10},{2,0},{0,2},{1,5},{5,1},... | collective-permute-start | bytes 1572872 | tf_op jit(solution)/shard_map/ppermute | solution.py:183
  21.7 11.0 %collective-permute-start.7 = (bf16[256,1024]{1,0:T(8,128)(2,1)S(1)}, bf16[256,1024]{1,0:T(8,128)(2,1)S(1)}, u32[]{:S(2)}, u32[]{:S(2)}) collective-permute-start(bf16[256,1024]{1,0:T(8,128)(2,1)S(1)} %get-tuple-element.53.refs_5_), channel_id=1, source_target_pairs={{0,1},{1,0},{2,3},{3,2},{4,5},{5,4},{6,7},{7,6},{8,9},{9,8},{10,11... | collective-permute-start | bytes 1572872 | tf_op jit(solution)/shard_map/ppermute | solution.py:183
  23.0 12.2 %collective-permute-start.8 = (bf16[1024,256]{1,0:T(8,128)(2,1)S(1)}, bf16[1024,256]{1,0:T(8,128)(2,1)S(1)}, u32[]{:S(2)}, u32[]{:S(2)}) collective-permute-start(bf16[1024,256]{1,0:T(8,128)(2,1)S(1)} %collective-permute-done.4.refs_4_), channel_id=1, source_target_pairs={{4,8},{8,4},{12,14},{14,12},{10,6},{6,10},{2,0},{0,2},{1,5},{5,1},... | collective-permute-start | bytes 1572872 | tf_op jit(solution)/shard_map/ppermute | solution.py:183
  25.2 1.3 %collective-permute-start.10 = (bf16[128,512]{1,0:T(8,128)(2,1)S(1)}, bf16[128,512]{1,0:T(8,128)(2,1)S(1)}, u32[]{:S(2)}, u32[]{:S(2)}) collective-permute-start(bf16[128,512]{1,0:T(8,128)(2,1)S(1)} %get-tuple-element.55.refs_3_), channel_id=1, source_target_pairs={{0,1},{1,0},{2,3},{3,2},{4,5},{5,4},{6,7},{7,6},{8,9},{9,8},{10,11... | collective-permute-start | bytes 393224 | tf_op jit(solution)/shard_map/ppermute | solution.py:183
  25.2 1.7 %collective-permute-start.3 = (bf16[128,1024]{1,0:T(8,128)(2,1)S(1)}, bf16[128,1024]{1,0:T(8,128)(2,1)S(1)}, u32[]{:S(2)}, u32[]{:S(2)}) collective-permute-start(bf16[128,1024]{1,0:T(8,128)(2,1)S(1)} %get-tuple-element.51.refs_1_), channel_id=1, source_target_pairs={{0,1},{1,0},{2,3},{3,2},{4,5},{5,4},{6,7},{7,6},{8,9},{9,8},{10,11... | collective-permute-start | bytes 786440 | tf_op jit(solution)/shard_map/ppermute | solution.py:183
  26.5 6.1 %collective-permute-start.6 = (bf16[512,256]{1,0:T(8,128)(2,1)S(1)}, bf16[512,256]{1,0:T(8,128)(2,1)S(1)}, u32[]{:S(2)}, u32[]{:S(2)}) collective-permute-start(bf16[512,256]{1,0:T(8,128)(2,1)S(1)} %slice.21), channel_id=1, source_target_pairs={{0,1},{1,0},{2,3},{3,2},{4,5},{5,4},{6,7},{7,6},{8,9},{9,8},{10,11... | collective-permute-start | bytes 786440 | tf_op jit(solution)/shard_map/ppermute | solution.py:183
  26.9 11.0 %collective-permute-start.14 = (bf16[256,1024]{1,0:T(8,128)(2,1)S(1)}, bf16[256,1024]{1,0:T(8,128)(2,1)S(1)}, u32[]{:S(2)}, u32[]{:S(2)}) collective-permute-start(bf16[256,1024]{1,0:T(8,128)(2,1)S(1)} %collective-permute-done.9.rows), channel_id=1, source_target_pairs={{0,4},{4,0},{8,12},{12,8},{14,10},{10,14},{6,2},{2,6},{5,9},{9,5},... | collective-permute-start | bytes 1572872 | tf_op jit(solution)/shard_map/ppermute | solution.py:183
  35.2 12.1 %collective-permute-start.13 = (bf16[1024,256]{1,0:T(8,128)(2,1)S(1)}, bf16[1024,256]{1,0:T(8,128)(2,1)S(1)}, u32[]{:S(2)}, u32[]{:S(2)}) collective-permute-start(bf16[1024,256]{1,0:T(8,128)(2,1)S(1)} %collective-permute-done.8.refs_1_), channel_id=1, source_target_pairs={{0,4},{4,0},{8,12},{12,8},{14,10},{10,14},{6,2},{2,6},{5,9},{9,5},... | collective-permute-start | bytes 1572872 | tf_op jit(solution)/shard_map/ppermute | solution.py:183
  37.3 16.8 %collective-permute-start.12 = (bf16[256,1024]{1,0:T(8,128)(2,1)S(1)}, bf16[256,1024]{1,0:T(8,128)(2,1)S(1)}, u32[]{:S(2)}, u32[]{:S(2)}) collective-permute-start(bf16[256,1024]{1,0:T(8,128)(2,1)S(1)} %get-tuple-element.57.refs_2_), channel_id=1, source_target_pairs={{0,1},{1,0},{2,3},{3,2},{4,5},{5,4},{6,7},{7,6},{8,9},{9,8},{10,11... | collective-permute-start | bytes 1572872 | tf_op jit(solution)/shard_map/ppermute | solution.py:183
  37.9 11.9 %collective-permute-start.17 = (bf16[128,1024]{1,0:T(8,128)(2,1)S(1)}, bf16[128,1024]{1,0:T(8,128)(2,1)S(1)}, u32[]{:S(2)}, u32[]{:S(2)}) collective-permute-start(bf16[128,1024]{1,0:T(8,128)(2,1)S(1)} %slice.24), channel_id=1, source_target_pairs={{4,8},{8,4},{12,14},{14,12},{10,6},{6,10},{2,0},{0,2},{1,5},{5,1},... | collective-permute-start | bytes 786440 | tf_op jit(solution)/shard_map/ppermute | solution.py:183
  44.2 10.5 %collective-permute-start.16 = (bf16[256,1024]{1,0:T(8,128)(2,1)S(1)}, bf16[256,1024]{1,0:T(8,128)(2,1)S(1)}, u32[]{:S(2)}, u32[]{:S(2)}) collective-permute-start(bf16[256,1024]{1,0:T(8,128)(2,1)S(1)} %get-tuple-element.60.refs_6_), channel_id=1, source_target_pairs={{0,1},{1,0},{2,3},{3,2},{4,5},{5,4},{6,7},{7,6},{8,9},{9,8},{10,11... | collective-permute-start | bytes 1572872 | tf_op jit(solution)/shard_map/ppermute | solution.py:183
  44.3 8.9 %collective-permute-start.11 = (bf16[512,256]{1,0:T(8,128)(2,1)S(1)}, bf16[512,256]{1,0:T(8,128)(2,1)S(1)}, u32[]{:S(2)}, u32[]{:S(2)}) collective-permute-start(bf16[512,256]{1,0:T(8,128)(2,1)S(1)} %slice.22), channel_id=1, source_target_pairs={{0,1},{1,0},{2,3},{3,2},{4,5},{5,4},{6,7},{7,6},{8,9},{9,8},{10,11... | collective-permute-start | bytes 786440 | tf_op jit(solution)/shard_map/ppermute | solution.py:183
  47.3 6.8 %collective-permute-start.19 = (bf16[1024,128]{1,0:T(8,128)(2,1)S(1)}, bf16[1024,128]{1,0:T(8,128)(2,1)S(1)}, u32[]{:S(2)}, u32[]{:S(2)}) collective-permute-start(bf16[1024,128]{1,0:T(8,128)(2,1)S(1)} %slice.25), channel_id=1, source_target_pairs={{4,8},{8,4},{12,14},{14,12},{10,6},{6,10},{2,0},{0,2},{1,5},{5,1},... | collective-permute-start | bytes 786440 | tf_op jit(solution)/shard_map/ppermute | solution.py:183
  49.8 4.9 %collective-permute-start.15 = (bf16[512,256]{1,0:T(8,128)(2,1)S(1)}, bf16[512,256]{1,0:T(8,128)(2,1)S(1)}, u32[]{:S(2)}, u32[]{:S(2)}) collective-permute-start(bf16[512,256]{1,0:T(8,128)(2,1)S(1)} %slice.23), channel_id=1, source_target_pairs={{0,1},{1,0},{2,3},{3,2},{4,5},{5,4},{6,7},{7,6},{8,9},{9,8},{10,11... | collective-permute-start | bytes 786440 | tf_op jit(solution)/shard_map/ppermute | solution.py:183
  53.2 3.3 %collective-permute-start.21 = (bf16[128,1024]{1,0:T(8,128)(2,1)S(1)}, bf16[128,1024]{1,0:T(8,128)(2,1)S(1)}, u32[]{:S(2)}, u32[]{:S(2)}) collective-permute-start(bf16[128,1024]{1,0:T(8,128)(2,1)S(1)} %get-tuple-element.65.refs_1_), channel_id=1, source_target_pairs={{0,1},{1,0},{2,3},{3,2},{4,5},{5,4},{6,7},{7,6},{8,9},{9,8},{10,11... | collective-permute-start | bytes 786440 | tf_op jit(solution)/shard_map/ppermute | solution.py:183
  54.1 2.4 %collective-permute-start.18 = (bf16[128,512]{1,0:T(8,128)(2,1)S(1)}, bf16[128,512]{1,0:T(8,128)(2,1)S(1)}, u32[]{:S(2)}, u32[]{:S(2)}) collective-permute-start(bf16[128,512]{1,0:T(8,128)(2,1)S(1)} %get-tuple-element.63.refs_0_), channel_id=1, source_target_pairs={{0,1},{1,0},{2,3},{3,2},{4,5},{5,4},{6,7},{7,6},{8,9},{9,8},{10,11... | collective-permute-start | bytes 393224 | tf_op jit(solution)/shard_map/ppermute | solution.py:183
  54.1 2.4 %collective-permute-start.20 = (bf16[512,128]{1,0:T(8,128)(2,1)S(1)}, bf16[512,128]{1,0:T(8,128)(2,1)S(1)}, u32[]{:S(2)}, u32[]{:S(2)}) collective-permute-start(bf16[512,128]{1,0:T(8,128)(2,1)S(1)} %slice.28), channel_id=1, source_target_pairs={{0,1},{1,0},{2,3},{3,2},{4,5},{5,4},{6,7},{7,6},{8,9},{9,8},{10,11... | collective-permute-start | bytes 393224 | tf_op jit(solution)/shard_map/ppermute | solution.py:183
  57.5 4.3 %collective-permute-start.23 = (bf16[512,512]{1,0:T(8,128)(2,1)S(1)}, bf16[512,512]{1,0:T(8,128)(2,1)S(1)}, u32[]{:S(2)}, u32[]{:S(2)}) collective-permute-start(bf16[512,512]{1,0:T(8,128)(2,1)S(1)} %get-tuple-element.68.sent), channel_id=1, source_target_pairs={{0,1},{1,0},{2,3},{3,2},{4,5},{5,4},{6,7},{7,6},{8,9},{9,8},{10,11... | collective-permute-start | bytes 1572872 | tf_op jit(solution)/shard_map/ppermute | solution.py:183
  58.5 6.4 %collective-permute-start.22 = (bf16[512,256]{1,0:T(8,128)(2,1)S(1)}, bf16[512,256]{1,0:T(8,128)(2,1)S(1)}, u32[]{:S(2)}, u32[]{:S(2)}) collective-permute-start(bf16[512,256]{1,0:T(8,128)(2,1)S(1)} %change.3), channel_id=1, source_target_pairs={{4,8},{8,4},{12,14},{14,12},{10,6},{6,10},{2,0},{0,2},{1,5},{5,1},... | collective-permute-start | bytes 786440 | tf_op jit(solution)/shard_map/ppermute | solution.py:183
  63.0 6.4 %collective-permute-start.25 = (bf16[512,256]{1,0:T(8,128)(2,1)S(1)}, bf16[512,256]{1,0:T(8,128)(2,1)S(1)}, u32[]{:S(2)}, u32[]{:S(2)}) collective-permute-start(bf16[512,256]{1,0:T(8,128)(2,1)S(1)} %get-tuple-element.78), channel_id=1, source_target_pairs={{0,4},{4,0},{8,12},{12,8},{14,10},{10,14},{6,2},{2,6},{5,9},{9,5},... | collective-permute-start | bytes 786440 | tf_op jit(solution)/shard_map/ppermute | solution.py:183
  65.5 7.2 %collective-permute-start.24 = (bf16[512,256]{1,0:T(8,128)(2,1)S(1)}, bf16[512,256]{1,0:T(8,128)(2,1)S(1)}, u32[]{:S(2)}, u32[]{:S(2)}) collective-permute-start(bf16[512,256]{1,0:T(8,128)(2,1)S(1)} %hop.5), channel_id=1, source_target_pairs={{0,4},{4,0},{8,12},{12,8},{14,10},{10,14},{6,2},{2,6},{5,9},{9,5},... | collective-permute-start | bytes 786440 | tf_op jit(solution)/shard_map/ppermute | solution.py:183
  70.1 6.4 %collective-permute-start.27 = (bf16[512,256]{1,0:T(8,128)(2,1)S(1)}, bf16[512,256]{1,0:T(8,128)(2,1)S(1)}, u32[]{:S(2)}, u32[]{:S(2)}) collective-permute-start(bf16[512,256]{1,0:T(8,128)(2,1)S(1)} %hop.6), channel_id=1, source_target_pairs={{4,8},{8,4},{12,14},{14,12},{10,6},{6,10},{2,0},{0,2},{1,5},{5,1},... | collective-permute-start | bytes 786440 | tf_op jit(solution)/shard_map/ppermute | solution.py:183
  73.3 7.7 %collective-permute-start.26 = (bf16[512,256]{1,0:T(8,128)(2,1)S(1)}, bf16[512,256]{1,0:T(8,128)(2,1)S(1)}, u32[]{:S(2)}, u32[]{:S(2)}) collective-permute-start(bf16[512,256]{1,0:T(8,128)(2,1)S(1)} %hop.7), channel_id=1, source_target_pairs={{4,8},{8,4},{12,14},{14,12},{10,6},{6,10},{2,0},{0,2},{1,5},{5,1},... | collective-permute-start | bytes 786440 | tf_op jit(solution)/shard_map/ppermute | solution.py:183
  77.1 6.5 %collective-permute-start.29 = (bf16[512,256]{1,0:T(8,128)(2,1)S(1)}, bf16[512,256]{1,0:T(8,128)(2,1)S(1)}, u32[]{:S(2)}, u32[]{:S(2)}) collective-permute-start(bf16[512,256]{1,0:T(8,128)(2,1)S(1)} %hop.8), channel_id=1, source_target_pairs={{0,4},{4,0},{8,12},{12,8},{14,10},{10,14},{6,2},{2,6},{5,9},{9,5},... | collective-permute-start | bytes 786440 | tf_op jit(solution)/shard_map/ppermute | solution.py:183
  81.6 6.4 %collective-permute-start.28 = (bf16[512,256]{1,0:T(8,128)(2,1)S(1)}, bf16[512,256]{1,0:T(8,128)(2,1)S(1)}, u32[]{:S(2)}, u32[]{:S(2)}) collective-permute-start(bf16[512,256]{1,0:T(8,128)(2,1)S(1)} %hop.9), channel_id=1, source_target_pairs={{0,4},{4,0},{8,12},{12,8},{14,10},{10,14},{6,2},{2,6},{5,9},{9,5},... | collective-permute-start | bytes 786440 | tf_op jit(solution)/shard_map/ppermute | solution.py:183
  83.6 4.5 %collective-permute-start.30 = (bf16[512,256]{1,0:T(8,128)(2,1)S(1)}, bf16[512,256]{1,0:T(8,128)(2,1)S(1)}, u32[]{:S(2)}, u32[]{:S(2)}) collective-permute-start(bf16[512,256]{1,0:T(8,128)(2,1)S(1)} %collective-permute-done.29), channel_id=1, source_target_pairs={{0,1},{1,0},{2,3},{3,2},{4,5},{5,4},{6,7},{7,6},{8,9},{9,8},{10,11... | collective-permute-start | bytes 786440 | tf_op jit(solution)/shard_map/ppermute | solution.py:183
  88.7 6.4 %collective-permute-start.31 = (bf16[512,256]{1,0:T(8,128)(2,1)S(1)}, bf16[512,256]{1,0:T(8,128)(2,1)S(1)}, u32[]{:S(2)}, u32[]{:S(2)}) collective-permute-start(bf16[512,256]{1,0:T(8,128)(2,1)S(1)} %last.1.change), channel_id=1, source_target_pairs={{0,2},{2,0},{1,3},{3,1},{4,6},{6,4},{5,7},{7,5},{8,10},{10,8},{9,1... | collective-permute-start | bytes 786440 | tf_op jit(solution)/shard_map/ppermute | solution.py:183
  (5 other events, 42.6 us)

commit v13 on v12

--- a/solution.py
+++ b/solution.py
@@ -92,23 +92,23 @@
     return high, (x - high.astype(F32)).astype(BF16)
 
 
-def split_kernel(place, x, high, low):
-    high[...], low[...] = high_low(x[...])
+def round_kernel(place, x, out):
+    out[...] = x[...].astype(BF16)
 
 
 TILE = 512
 
 
-def block_kernel(place, rows, w_own, w_other, p_own, p_other, high, low, out, own_slice, feats):
+def block_kernel(place, rows, w_own, w_other, p_own, p_other, inverse, out, own_slice, feats):
     inputs = rows[:feats.shape[0]]
-    half, depth = w_own.shape[1], high.shape[0]
+    half, depth = w_own.shape[1], inverse.shape[0]
     total = None
     for i, (weights, phases) in enumerate(((w_own, p_own), (w_other, p_other))):
         for k in range(0, half, TILE):
             at = pl.ds(pl.multiple_of((place[2] ^ i) * half + k, TILE), TILE)
             tile = cosine(dot(inputs, weights[:, k:k + TILE]), phases[:, k:k + TILE]).astype(BF16)
             feats[:, at] = tile
-            product = dot_nt(tile, high[:, at]) + dot_nt(tile, low[:, at])
+            product = dot_nt(tile, inverse[:, at])
             total = product if total is None else total + product
     out[:, :depth], out[:, depth:] = high_low(total)
     own_slice[...] = feats[:, lanes(place[0], depth)]
@@ -219,15 +219,13 @@
     weights = (projection, C(projection))
     phases = phases[None, :]
     phases = (phases, C(phases))
-    inverse = call(
-        split_kernel, (like(inverse_blocks.shape[1:]),) * 2, place, (inverse_blocks[0],), "split", 14
-    )
+    inverse = call(round_kernel, like(inverse_blocks.shape[1:]), place, (inverse_blocks[0],), "round", 10)
 
     def block(rows, size):
         scratch = (pltpu.VMEM((size, 2 * projection.shape[1]), BF16),)
         return call(
             block_kernel, (like((size, 2 * depth)), like((size, depth))), place,
-            (rows, *weights, *phases, *inverse), "block", 16, scratch,
+            (rows, *weights, *phases, inverse), "block", 16, scratch,
         )
 
     def begin(pairs, *earlier):

time: 98.6 us -> 100 us (1.014)
  waiting for transfers between devices: 21.9 us -> 30.3 us
  Pallas kernels: 36.3 us -> 31.7 us
  starting transfers between devices: 33.6 us -> 31.5 us
    ppermute x32, waiting for transfers between devices: 21.9 us -> 30.3 us  [swap(): lax.ppermute(x, axes, [p for a, b in pairs for p in ((a, b), (b, a))])]
    pallas_call x21, Pallas kernels: 36.3 us -> 31.7 us  [call(): pl.pallas_call(kernel, out_shape=out_shapes, in_specs=[pl.BlockSpec(memor...]
    ppermute x32, starting transfers between devices: 33.6 us -> 31.5 us  [swap(): lax.ppermute(x, axes, [p for a, b in pairs for p in ((a, b), (b, a))])]
  transfers between devices with their start and end apart: 32 -> 32, of which waited for: 15 -> 15; matrix products, arithmetic and copies ran while one was open for 1% -> 1% of each run, Pallas kernels for 34% -> 29%
where the time goes in v13:
time: 100 us; the launch traced here: 99 us
  Pallas kernels  31.7 us (32%)
  starting transfers between devices  31.5 us (32%)
  waiting for transfers between devices  30.3 us (30%)
  local copies, waits for them, and re-layouts  3.16 us (3%)
  other arithmetic  1.24 us (1%)
  between operations  1.14 us (1%)
    pallas_call x21, Pallas kernels, call(): pl.pallas_call(kernel, out_shape=out_shapes, in_specs=[pl.BlockSpec(memor...  31.7 us
    ppermute x32, starting transfers between devices, swap(): lax.ppermute(x, axes, [p for a, b in pairs for p in ((a, b), (b, a))])  31.5 us
    ppermute x32, waiting for transfers between devices, swap(): lax.ppermute(x, axes, [p for a, b in pairs for p in ((a, b), (b, a))])  30.3 us
    unnamed x11, local copies, waits for them, and re-layouts  3.04 us
  transfers between devices with their start and end apart: 32, of which 15 were waited for; matrix products, arithmetic and copies ran while one was open for 1% of the time, Pallas kernels for 29%

profile of v13, /device:TPU:0, one launch (start us, length us, event | category | flops | bytes accessed | tf_op | source)
XLA Modules:
  0.0 99.0 jit_solution(4560553536644248263)
XLA Ops:
  1.2 1.9 %prepare.1 = (bf16[256,1024]{1,0:T(8,128)(2,1)S(1)}, bf16[512,256]{1,0:T(8,128)(2,1)S(1)}, bf16[512,256]{1,0:T(8,128)(2,1)S(1)}) custom-call(s32[3]{0:T(128)S(1)} %pad_add_fusion.place, bf16[512,1024]{1,0:T(8,128)(2,1)} %inputs.1, s32[1,512]{1,0:T(1,128)} %bitcast.18, f32[500,512]{1,0:T(8,128)} %bitcast.13), custom_call_target="tpu_custom_call" | custom-call | tf_op jit(solution)/shard_map/prepare/pallas_call | solution.py:42
  3.3 2.0 %collective-permute-done = bf16[512,256]{1,0:T(8,128)(2,1)S(1)} collective-permute-done((bf16[512,256]{1,0:T(8,128)(2,1)S(1)}, bf16[512,256]{1,0:T(8,128)(2,1)S(1)}, u32[]{:S(2)}, u32[]{:S(2)}) %collective-permute-start) | collective-permute-done | bytes 262176 | tf_op jit(solution)/shard_map/ppermute | solution.py:183
  5.3 2.9 %collective-permute-start.5 = (bf16[256,1024]{1,0:T(8,128)(2,1)S(1)}, bf16[256,1024]{1,0:T(8,128)(2,1)S(1)}, u32[]{:S(2)}, u32[]{:S(2)}) collective-permute-start(bf16[256,1024]{1,0:T(8,128)(2,1)S(1)} %get-tuple-element.46.rows), channel_id=1, source_target_pairs={{0,4},{4,0},{8,12},{12,8},{14,10},{10,14},{6,2},{2,6},{5,9},{9,5},... | collective-permute-start | bytes 1572872 | tf_op jit(solution)/shard_map/ppermute | solution.py:183
  8.5 2.2 %copy-done.2 = f32[1,512,2048]{2,1,0:T(8,128)S(1)} copy-done((f32[1,512,2048]{2,1,0:T(8,128)S(1)}, f32[1,512,2048]{2,1,0:T(8,128)}, u32[]{:S(2)}) %copy-start.2) | copy-done | bytes 4194328
  12.3 2.4 %block.5 = (bf16[128,1024]{1,0:T(8,128)(2,1)S(1)}, bf16[128,512]{1,0:T(8,128)(2,1)S(1)}) custom-call(s32[3]{0:T(128)S(1)} %pad_add_fusion.place, bf16[256,1024]{1,0:T(8,128)(2,1)S(1)} %get-tuple-element.46.rows, bf16[1024,1024]{1,0:T(8,128)(2,1)S(1)} %copy-done, bf16[1024,1024]{1,0:T(8,128)(2,1)S(1)} %collective-permute-done.1.w_other, ...), custom_call_target="tpu_custom_call" | custom-call | tf_op jit(solution)/shard_map/block/pallas_call | solution.py:42
  15.4 1.9 %collective-permute-start.9 = (bf16[256,1024]{1,0:T(8,128)(2,1)S(1)}, bf16[256,1024]{1,0:T(8,128)(2,1)S(1)}, u32[]{:S(2)}, u32[]{:S(2)}) collective-permute-start(bf16[256,1024]{1,0:T(8,128)(2,1)S(1)} %collective-permute-done.5.rows), channel_id=1, source_target_pairs={{4,8},{8,4},{12,14},{14,12},{10,6},{6,10},{2,0},{0,2},{1,5},{5,1},... | collective-permute-start | bytes 1572872 | tf_op jit(solution)/shard_map/ppermute | solution.py:183
  17.4 3.4 %block.6 = (bf16[256,1024]{1,0:T(8,128)(2,1)S(1)}, bf16[256,512]{1,0:T(8,128)(2,1)S(1)}) custom-call(s32[3]{0:T(128)S(1)} %pad_add_fusion.place, bf16[256,1024]{1,0:T(8,128)(2,1)S(1)} %collective-permute-done.5.rows, bf16[1024,1024]{1,0:T(8,128)(2,1)S(1)} %copy-done, bf16[1024,1024]{1,0:T(8,128)(2,1)S(1)} %collective-permute-done.1.w_other, ...), custom_call_target="tpu_custom_call" | custom-call | tf_op jit(solution)/shard_map/block/pallas_call | solution.py:42
  20.8 3.1 %collective-permute-done.4.refs_4_ = bf16[1024,256]{1,0:T(8,128)(2,1)S(1)} collective-permute-done((bf16[1024,256]{1,0:T(8,128)(2,1)S(1)}, bf16[1024,256]{1,0:T(8,128)(2,1)S(1)}, u32[]{:S(2)}, u32[]{:S(2)}) %collective-permute-start.4) | collective-permute-done | bytes 524320 | tf_op jit(solution)/shard_map/ppermute | solution.py:183
  23.9 2.2 %collective-permute-start.8 = (bf16[1024,256]{1,0:T(8,128)(2,1)S(1)}, bf16[1024,256]{1,0:T(8,128)(2,1)S(1)}, u32[]{:S(2)}, u32[]{:S(2)}) collective-permute-start(bf16[1024,256]{1,0:T(8,128)(2,1)S(1)} %collective-permute-done.4.refs_4_), channel_id=1, source_target_pairs={{4,8},{8,4},{12,14},{14,12},{10,6},{6,10},{2,0},{0,2},{1,5},{5,1},... | collective-permute-start | bytes 1572872 | tf_op jit(solution)/shard_map/ppermute | solution.py:183
  27.8 1.6 %collective-permute-start.14 = (bf16[256,1024]{1,0:T(8,128)(2,1)S(1)}, bf16[256,1024]{1,0:T(8,128)(2,1)S(1)}, u32[]{:S(2)}, u32[]{:S(2)}) collective-permute-start(bf16[256,1024]{1,0:T(8,128)(2,1)S(1)} %collective-permute-done.9.rows), channel_id=1, source_target_pairs={{0,4},{4,0},{8,12},{12,8},{14,10},{10,14},{6,2},{2,6},{5,9},{9,5},... | collective-permute-start | bytes 1572872 | tf_op jit(solution)/shard_map/ppermute | solution.py:183
  29.5 3.4 %block.7 = (bf16[256,1024]{1,0:T(8,128)(2,1)S(1)}, bf16[256,512]{1,0:T(8,128)(2,1)S(1)}) custom-call(s32[3]{0:T(128)S(1)} %pad_add_fusion.place, bf16[256,1024]{1,0:T(8,128)(2,1)S(1)} %collective-permute-done.9.rows, bf16[1024,1024]{1,0:T(8,128)(2,1)S(1)} %copy-done, bf16[1024,1024]{1,0:T(8,128)(2,1)S(1)} %collective-permute-done.1.w_other, ...), custom_call_target="tpu_custom_call" | custom-call | tf_op jit(solution)/shard_map/block/pallas_call | solution.py:42
  32.9 1.5 %begin.2.refs_0_ = f32[512,512]{1,0:T(8,128)S(1)} custom-call(s32[3]{0:T(128)S(1)} %pad_add_fusion.place, bf16[1024,256]{1,0:T(8,128)(2,1)S(1)} %constant_dynamic-update-slice_fusion.refs_0_.refs_2_, bf16[128,1024]{1,0:T(8,128)(2,1)S(1)} %get-tuple-element.47.refs_1_, bf16[1024,256]{1,0:T(8,128)(2,1)S(1)} %constant_dynamic-update-slice_fusion.refs_0_.refs_2_, ...), custom_call_target="tpu_custom_call" | custom-call | tf_op jit(solution)/shard_map/begin/pallas_call | solution.py:42
  34.4 2.6 %collective-permute-done.8.refs_1_ = bf16[1024,256]{1,0:T(8,128)(2,1)S(1)} collective-permute-done((bf16[1024,256]{1,0:T(8,128)(2,1)S(1)}, bf16[1024,256]{1,0:T(8,128)(2,1)S(1)}, u32[]{:S(2)}, u32[]{:S(2)}) %collective-permute-start.8) | collective-permute-done | bytes 524320 | tf_op jit(solution)/shard_map/ppermute | solution.py:183
  37.0 1.4 %collective-permute-start.13 = (bf16[1024,256]{1,0:T(8,128)(2,1)S(1)}, bf16[1024,256]{1,0:T(8,128)(2,1)S(1)}, u32[]{:S(2)}, u32[]{:S(2)}) collective-permute-start(bf16[1024,256]{1,0:T(8,128)(2,1)S(1)} %collective-permute-done.8.refs_1_), channel_id=1, source_target_pairs={{0,4},{4,0},{8,12},{12,8},{14,10},{10,14},{6,2},{2,6},{5,9},{9,5},... | collective-permute-start | bytes 1572872 | tf_op jit(solution)/shard_map/ppermute | solution.py:183
  38.5 1.6 %collective-permute-start.17 = (bf16[128,1024]{1,0:T(8,128)(2,1)S(1)}, bf16[128,1024]{1,0:T(8,128)(2,1)S(1)}, u32[]{:S(2)}, u32[]{:S(2)}) collective-permute-start(bf16[128,1024]{1,0:T(8,128)(2,1)S(1)} %slice.24), channel_id=1, source_target_pairs={{4,8},{8,4},{12,14},{14,12},{10,6},{6,10},{2,0},{0,2},{1,5},{5,1},... | collective-permute-start | bytes 786440 | tf_op jit(solution)/shard_map/ppermute | solution.py:183
  40.1 3.4 %block.8 = (bf16[256,1024]{1,0:T(8,128)(2,1)S(1)}, bf16[256,512]{1,0:T(8,128)(2,1)S(1)}) custom-call(s32[3]{0:T(128)S(1)} %pad_add_fusion.place, bf16[256,1024]{1,0:T(8,128)(2,1)S(1)} %collective-permute-done.14.rows, bf16[1024,1024]{1,0:T(8,128)(2,1)S(1)} %copy-done, bf16[1024,1024]{1,0:T(8,128)(2,1)S(1)} %collective-permute-done.1.w_other, ...), custom_call_target="tpu_custom_call" | custom-call | tf_op jit(solution)/shard_map/block/pallas_call | solution.py:42
  44.1 4.8 %collective-permute-done.13.refs_5_ = bf16[1024,256]{1,0:T(8,128)(2,1)S(1)} collective-permute-done((bf16[1024,256]{1,0:T(8,128)(2,1)S(1)}, bf16[1024,256]{1,0:T(8,128)(2,1)S(1)}, u32[]{:S(2)}, u32[]{:S(2)}) %collective-permute-start.13) | collective-permute-done | bytes 524320 | tf_op jit(solution)/shard_map/ppermute | solution.py:183
  49.0 2.5 %collective-permute-start.19 = (bf16[1024,128]{1,0:T(8,128)(2,1)S(1)}, bf16[1024,128]{1,0:T(8,128)(2,1)S(1)}, u32[]{:S(2)}, u32[]{:S(2)}) collective-permute-start(bf16[1024,128]{1,0:T(8,128)(2,1)S(1)} %slice.25), channel_id=1, source_target_pairs={{4,8},{8,4},{12,14},{14,12},{10,6},{6,10},{2,0},{0,2},{1,5},{5,1},... | collective-permute-start | bytes 786440 | tf_op jit(solution)/shard_map/ppermute | solution.py:183
  51.7 2.6 %block.9 = (bf16[128,1024]{1,0:T(8,128)(2,1)S(1)}, bf16[128,512]{1,0:T(8,128)(2,1)S(1)}) custom-call(s32[3]{0:T(128)S(1)} %pad_add_fusion.place, bf16[128,1024]{1,0:T(8,128)(2,1)S(1)} %collective-permute-done.17.rows, bf16[1024,1024]{1,0:T(8,128)(2,1)S(1)} %copy-done, bf16[1024,1024]{1,0:T(8,128)(2,1)S(1)} %collective-permute-done.1.w_other, ...), custom_call_target="tpu_custom_call" | custom-call | tf_op jit(solution)/shard_map/block/pallas_call | solution.py:42
  56.5 1.8 %begin.3.begun = f32[512,512]{1,0:T(8,128)S(1)} custom-call(s32[3]{0:T(128)S(1)} %pad_add_fusion.place, f32[512,512]{1,0:T(8,128)S(1)} %begin.2.refs_0_, bf16[1024,256]{1,0:T(8,128)(2,1)S(1)} %collective-permute-done.8.refs_1_, bf16[256,1024]{1,0:T(8,128)(2,1)S(1)} %get-tuple-element.53.refs_2_, bf16[512,256]{1,0:T(8,128)(2,1)S(1)} %collective-permute-done.11.refs_3_, ...), custom_call_target="tpu_custom_call" | custom-call | tf_op jit(solution)/shard_map/begin/pallas_call | solution.py:42
  60.3 2.1 %collective-permute-start.22 = (bf16[512,256]{1,0:T(8,128)(2,1)S(1)}, bf16[512,256]{1,0:T(8,128)(2,1)S(1)}, u32[]{:S(2)}, u32[]{:S(2)}) collective-permute-start(bf16[512,256]{1,0:T(8,128)(2,1)S(1)} %change.3), channel_id=1, source_target_pairs={{4,8},{8,4},{12,14},{14,12},{10,6},{6,10},{2,0},{0,2},{1,5},{5,1},... | collective-permute-start | bytes 786440 | tf_op jit(solution)/shard_map/ppermute | solution.py:183
  64.8 1.5 %collective-permute-start.25 = (bf16[512,256]{1,0:T(8,128)(2,1)S(1)}, bf16[512,256]{1,0:T(8,128)(2,1)S(1)}, u32[]{:S(2)}, u32[]{:S(2)}) collective-permute-start(bf16[512,256]{1,0:T(8,128)(2,1)S(1)} %get-tuple-element.74), channel_id=1, source_target_pairs={{0,4},{4,0},{8,12},{12,8},{14,10},{10,14},{6,2},{2,6},{5,9},{9,5},... | collective-permute-start | bytes 786440 | tf_op jit(solution)/shard_map/ppermute | solution.py:183
  67.3 1.5 %collective-permute-start.24 = (bf16[512,256]{1,0:T(8,128)(2,1)S(1)}, bf16[512,256]{1,0:T(8,128)(2,1)S(1)}, u32[]{:S(2)}, u32[]{:S(2)}) collective-permute-start(bf16[512,256]{1,0:T(8,128)(2,1)S(1)} %hop.5), channel_id=1, source_target_pairs={{0,4},{4,0},{8,12},{12,8},{14,10},{10,14},{6,2},{2,6},{5,9},{9,5},... | collective-permute-start | bytes 786440 | tf_op jit(solution)/shard_map/ppermute | solution.py:183
  68.8 2.4 %collective-permute-done.25.came = bf16[512,256]{1,0:T(8,128)(2,1)S(1)} collective-permute-done((bf16[512,256]{1,0:T(8,128)(2,1)S(1)}, bf16[512,256]{1,0:T(8,128)(2,1)S(1)}, u32[]{:S(2)}, u32[]{:S(2)}) %collective-permute-start.25) | collective-permute-done | bytes 262176 | tf_op jit(solution)/shard_map/ppermute | solution.py:183
  72.9 1.9 %collective-permute-done.24.came = bf16[512,256]{1,0:T(8,128)(2,1)S(1)} collective-permute-done((bf16[512,256]{1,0:T(8,128)(2,1)S(1)}, bf16[512,256]{1,0:T(8,128)(2,1)S(1)}, u32[]{:S(2)}, u32[]{:S(2)}) %collective-permute-start.24) | collective-permute-done | bytes 262176 | tf_op jit(solution)/shard_map/ppermute | solution.py:183
  75.4 2.0 %collective-permute-start.26 = (bf16[512,256]{1,0:T(8,128)(2,1)S(1)}, bf16[512,256]{1,0:T(8,128)(2,1)S(1)}, u32[]{:S(2)}, u32[]{:S(2)}) collective-permute-start(bf16[512,256]{1,0:T(8,128)(2,1)S(1)} %hop.7), channel_id=1, source_target_pairs={{4,8},{8,4},{12,14},{14,12},{10,6},{6,10},{2,0},{0,2},{1,5},{5,1},... | collective-permute-start | bytes 786440 | tf_op jit(solution)/shard_map/ppermute | solution.py:183
  78.9 1.5 %collective-permute-start.29 = (bf16[512,256]{1,0:T(8,128)(2,1)S(1)}, bf16[512,256]{1,0:T(8,128)(2,1)S(1)}, u32[]{:S(2)}, u32[]{:S(2)}) collective-permute-start(bf16[512,256]{1,0:T(8,128)(2,1)S(1)} %hop.8), channel_id=1, source_target_pairs={{0,4},{4,0},{8,12},{12,8},{14,10},{10,14},{6,2},{2,6},{5,9},{9,5},... | collective-permute-start | bytes 786440 | tf_op jit(solution)/shard_map/ppermute | solution.py:183
  80.4 2.8 %collective-permute-done.26.came = bf16[512,256]{1,0:T(8,128)(2,1)S(1)} collective-permute-done((bf16[512,256]{1,0:T(8,128)(2,1)S(1)}, bf16[512,256]{1,0:T(8,128)(2,1)S(1)}, u32[]{:S(2)}, u32[]{:S(2)}) %collective-permute-start.26) | collective-permute-done | bytes 262176 | tf_op jit(solution)/shard_map/ppermute | solution.py:183
  83.9 1.9 %collective-permute-start.28 = (bf16[512,256]{1,0:T(8,128)(2,1)S(1)}, bf16[512,256]{1,0:T(8,128)(2,1)S(1)}, u32[]{:S(2)}, u32[]{:S(2)}) collective-permute-start(bf16[512,256]{1,0:T(8,128)(2,1)S(1)} %hop.9), channel_id=1, source_target_pairs={{0,4},{4,0},{8,12},{12,8},{14,10},{10,14},{6,2},{2,6},{5,9},{9,5},... | collective-permute-start | bytes 786440 | tf_op jit(solution)/shard_map/ppermute | solution.py:183
  85.8 4.5 %collective-permute-done.28.came = bf16[512,256]{1,0:T(8,128)(2,1)S(1)} collective-permute-done((bf16[512,256]{1,0:T(8,128)(2,1)S(1)}, bf16[512,256]{1,0:T(8,128)(2,1)S(1)}, u32[]{:S(2)}, u32[]{:S(2)}) %collective-permute-start.28) | collective-permute-done | bytes 262176 | tf_op jit(solution)/shard_map/ppermute | solution.py:183
  90.9 2.1 %collective-permute-start.31 = (bf16[512,256]{1,0:T(8,128)(2,1)S(1)}, bf16[512,256]{1,0:T(8,128)(2,1)S(1)}, u32[]{:S(2)}, u32[]{:S(2)}) collective-permute-start(bf16[512,256]{1,0:T(8,128)(2,1)S(1)} %last.1.change), channel_id=1, source_target_pairs={{0,2},{2,0},{1,3},{3,1},{4,6},{6,4},{5,7},{7,5},{8,10},{10,8},{9,1... | collective-permute-start | bytes 786440 | tf_op jit(solution)/shard_map/ppermute | solution.py:183
  95.7 1.8 %collective-permute-done.31.change = bf16[512,256]{1,0:T(8,128)(2,1)S(1)} collective-permute-done((bf16[512,256]{1,0:T(8,128)(2,1)S(1)}, bf16[512,256]{1,0:T(8,128)(2,1)S(1)}, u32[]{:S(2)}, u32[]{:S(2)}) %collective-permute-start.31) | collective-permute-done | bytes 262176 | tf_op jit(solution)/shard_map/ppermute | solution.py:183
  (74 shorter events, 22.4 us)
Async XLA Ops:
  0.6 10.8 %collective-permute-start.1 = (bf16[1024,1024]{1,0:T(8,128)(2,1)}, bf16[1024,1024]{1,0:T(8,128)(2,1)S(1)}, u32[]{:S(2)}, u32[]{:S(2)}) collective-permute-start(bf16[1024,1024]{1,0:T(8,128)(2,1)} %w_own.9), channel_id=1, source_target_pairs={{0,1},{1,0},{2,3},{3,2},{4,5},{5,4},{6,7},{7,6},{8,9},{9,8},{10,11... | collective-permute-start | bytes 6291464 | tf_op jit(solution)/shard_map/ppermute | solution.py:183
  3.2 2.2 %collective-permute-start = (bf16[512,256]{1,0:T(8,128)(2,1)S(1)}, bf16[512,256]{1,0:T(8,128)(2,1)S(1)}, u32[]{:S(2)}, u32[]{:S(2)}) collective-permute-start(bf16[512,256]{1,0:T(8,128)(2,1)S(1)} %get-tuple-element.44), channel_id=1, source_target_pairs={{0,1},{1,0},{2,3},{3,2},{4,5},{5,4},{6,7},{7,6},{8,9},{9,8},{10,11... | collective-permute-start | bytes 786440 | tf_op jit(solution)/shard_map/ppermute | solution.py:183
  5.3 10.1 %collective-permute-start.5 = (bf16[256,1024]{1,0:T(8,128)(2,1)S(1)}, bf16[256,1024]{1,0:T(8,128)(2,1)S(1)}, u32[]{:S(2)}, u32[]{:S(2)}) collective-permute-start(bf16[256,1024]{1,0:T(8,128)(2,1)S(1)} %get-tuple-element.46.rows), channel_id=1, source_target_pairs={{0,4},{4,0},{8,12},{12,8},{14,10},{10,14},{6,2},{2,6},{5,9},{9,5},... | collective-permute-start | bytes 1572872 | tf_op jit(solution)/shard_map/ppermute | solution.py:183
  8.3 15.6 %collective-permute-start.4 = (bf16[1024,256]{1,0:T(8,128)(2,1)S(1)}, bf16[1024,256]{1,0:T(8,128)(2,1)S(1)}, u32[]{:S(2)}, u32[]{:S(2)}) collective-permute-start(bf16[1024,256]{1,0:T(8,128)(2,1)S(1)} %constant_dynamic-update-slice_fusion.refs_0_.refs_2_), channel_id=1, source_target_pairs={{0,4},{4,0},{8,12},{12,8},{14,10},{10,14},{6,2},{2,6},{5,9},{9,5},... | collective-permute-start | bytes 1572872 | tf_op jit(solution)/shard_map/ppermute | solution.py:183
  8.4 3.0 %collective-permute-start.2 = (bf16[1,1024]{1,0:T(2,128)(2,1)S(1)}, bf16[1,1024]{1,0:T(2,128)(2,1)S(1)}, u32[]{:S(2)}, u32[]{:S(2)}) collective-permute-start(bf16[1,1024]{1,0:T(2,128)(2,1)S(1)} %broadcast_in_dim.7.p_own), channel_id=1, source_target_pairs={{0,1},{1,0},{2,3},{3,2},{4,5},{5,4},{6,7},{7,6},{8,9},{9,8},{10,11... | collective-permute-start | bytes 6152 | tf_op jit(solution)/shard_map/ppermute | solution.py:183
  15.4 12.4 %collective-permute-start.9 = (bf16[256,1024]{1,0:T(8,128)(2,1)S(1)}, bf16[256,1024]{1,0:T(8,128)(2,1)S(1)}, u32[]{:S(2)}, u32[]{:S(2)}) collective-permute-start(bf16[256,1024]{1,0:T(8,128)(2,1)S(1)} %collective-permute-done.5.rows), channel_id=1, source_target_pairs={{4,8},{8,4},{12,14},{14,12},{10,6},{6,10},{2,0},{0,2},{1,5},{5,1},... | collective-permute-start | bytes 1572872 | tf_op jit(solution)/shard_map/ppermute | solution.py:183
  20.7 12.1 %collective-permute-start.7 = (bf16[256,1024]{1,0:T(8,128)(2,1)S(1)}, bf16[256,1024]{1,0:T(8,128)(2,1)S(1)}, u32[]{:S(2)}, u32[]{:S(2)}) collective-permute-start(bf16[256,1024]{1,0:T(8,128)(2,1)S(1)} %get-tuple-element.49.refs_5_), channel_id=1, source_target_pairs={{0,1},{1,0},{2,3},{3,2},{4,5},{5,4},{6,7},{7,6},{8,9},{9,8},{10,11... | collective-permute-start | bytes 1572872 | tf_op jit(solution)/shard_map/ppermute | solution.py:183
  23.9 13.1 %collective-permute-start.8 = (bf16[1024,256]{1,0:T(8,128)(2,1)S(1)}, bf16[1024,256]{1,0:T(8,128)(2,1)S(1)}, u32[]{:S(2)}, u32[]{:S(2)}) collective-permute-start(bf16[1024,256]{1,0:T(8,128)(2,1)S(1)} %collective-permute-done.4.refs_4_), channel_id=1, source_target_pairs={{4,8},{8,4},{12,14},{14,12},{10,6},{6,10},{2,0},{0,2},{1,5},{5,1},... | collective-permute-start | bytes 1572872 | tf_op jit(solution)/shard_map/ppermute | solution.py:183
  26.1 1.3 %collective-permute-start.10 = (bf16[128,512]{1,0:T(8,128)(2,1)S(1)}, bf16[128,512]{1,0:T(8,128)(2,1)S(1)}, u32[]{:S(2)}, u32[]{:S(2)}) collective-permute-start(bf16[128,512]{1,0:T(8,128)(2,1)S(1)} %get-tuple-element.51.refs_3_), channel_id=1, source_target_pairs={{0,1},{1,0},{2,3},{3,2},{4,5},{5,4},{6,7},{7,6},{8,9},{9,8},{10,11... | collective-permute-start | bytes 393224 | tf_op jit(solution)/shard_map/ppermute | solution.py:183
  26.1 1.7 %collective-permute-start.3 = (bf16[128,1024]{1,0:T(8,128)(2,1)S(1)}, bf16[128,1024]{1,0:T(8,128)(2,1)S(1)}, u32[]{:S(2)}, u32[]{:S(2)}) collective-permute-start(bf16[128,1024]{1,0:T(8,128)(2,1)S(1)} %get-tuple-element.47.refs_1_), channel_id=1, source_target_pairs={{0,1},{1,0},{2,3},{3,2},{4,5},{5,4},{6,7},{7,6},{8,9},{9,8},{10,11... | collective-permute-start | bytes 786440 | tf_op jit(solution)/shard_map/ppermute | solution.py:183
  27.5 5.4 %collective-permute-start.6 = (bf16[512,256]{1,0:T(8,128)(2,1)S(1)}, bf16[512,256]{1,0:T(8,128)(2,1)S(1)}, u32[]{:S(2)}, u32[]{:S(2)}) collective-permute-start(bf16[512,256]{1,0:T(8,128)(2,1)S(1)} %slice.21), channel_id=1, source_target_pairs={{0,1},{1,0},{2,3},{3,2},{4,5},{5,4},{6,7},{7,6},{8,9},{9,8},{10,11... | collective-permute-start | bytes 786440 | tf_op jit(solution)/shard_map/ppermute | solution.py:183
  27.8 10.6 %collective-permute-start.14 = (bf16[256,1024]{1,0:T(8,128)(2,1)S(1)}, bf16[256,1024]{1,0:T(8,128)(2,1)S(1)}, u32[]{:S(2)}, u32[]{:S(2)}) collective-permute-start(bf16[256,1024]{1,0:T(8,128)(2,1)S(1)} %collective-permute-done.9.rows), channel_id=1, source_target_pairs={{0,4},{4,0},{8,12},{12,8},{14,10},{10,14},{6,2},{2,6},{5,9},{9,5},... | collective-permute-start | bytes 1572872 | tf_op jit(solution)/shard_map/ppermute | solution.py:183
  37.0 12.0 %collective-permute-start.13 = (bf16[1024,256]{1,0:T(8,128)(2,1)S(1)}, bf16[1024,256]{1,0:T(8,128)(2,1)S(1)}, u32[]{:S(2)}, u32[]{:S(2)}) collective-permute-start(bf16[1024,256]{1,0:T(8,128)(2,1)S(1)} %collective-permute-done.8.refs_1_), channel_id=1, source_target_pairs={{0,4},{4,0},{8,12},{12,8},{14,10},{10,14},{6,2},{2,6},{5,9},{9,5},... | collective-permute-start | bytes 1572872 | tf_op jit(solution)/shard_map/ppermute | solution.py:183
  38.5 17.5 %collective-permute-start.12 = (bf16[256,1024]{1,0:T(8,128)(2,1)S(1)}, bf16[256,1024]{1,0:T(8,128)(2,1)S(1)}, u32[]{:S(2)}, u32[]{:S(2)}) collective-permute-start(bf16[256,1024]{1,0:T(8,128)(2,1)S(1)} %get-tuple-element.53.refs_2_), channel_id=1, source_target_pairs={{0,1},{1,0},{2,3},{3,2},{4,5},{5,4},{6,7},{7,6},{8,9},{9,8},{10,11... | collective-permute-start | bytes 1572872 | tf_op jit(solution)/shard_map/ppermute | solution.py:183
  38.5 13.1 %collective-permute-start.17 = (bf16[128,1024]{1,0:T(8,128)(2,1)S(1)}, bf16[128,1024]{1,0:T(8,128)(2,1)S(1)}, u32[]{:S(2)}, u32[]{:S(2)}) collective-permute-start(bf16[128,1024]{1,0:T(8,128)(2,1)S(1)} %slice.24), channel_id=1, source_target_pairs={{4,8},{8,4},{12,14},{14,12},{10,6},{6,10},{2,0},{0,2},{1,5},{5,1},... | collective-permute-start | bytes 786440 | tf_op jit(solution)/shard_map/ppermute | solution.py:183
  43.4 13.1 %collective-permute-start.16 = (bf16[256,1024]{1,0:T(8,128)(2,1)S(1)}, bf16[256,1024]{1,0:T(8,128)(2,1)S(1)}, u32[]{:S(2)}, u32[]{:S(2)}) collective-permute-start(bf16[256,1024]{1,0:T(8,128)(2,1)S(1)} %get-tuple-element.56.refs_6_), channel_id=1, source_target_pairs={{0,1},{1,0},{2,3},{3,2},{4,5},{5,4},{6,7},{7,6},{8,9},{9,8},{10,11... | collective-permute-start | bytes 1572872 | tf_op jit(solution)/shard_map/ppermute | solution.py:183
  44.1 10.2 %collective-permute-start.11 = (bf16[512,256]{1,0:T(8,128)(2,1)S(1)}, bf16[512,256]{1,0:T(8,128)(2,1)S(1)}, u32[]{:S(2)}, u32[]{:S(2)}) collective-permute-start(bf16[512,256]{1,0:T(8,128)(2,1)S(1)} %slice.22), channel_id=1, source_target_pairs={{0,1},{1,0},{2,3},{3,2},{4,5},{5,4},{6,7},{7,6},{8,9},{9,8},{10,11... | collective-permute-start | bytes 786440 | tf_op jit(solution)/shard_map/ppermute | solution.py:183
  49.0 6.9 %collective-permute-start.19 = (bf16[1024,128]{1,0:T(8,128)(2,1)S(1)}, bf16[1024,128]{1,0:T(8,128)(2,1)S(1)}, u32[]{:S(2)}, u32[]{:S(2)}) collective-permute-start(bf16[1024,128]{1,0:T(8,128)(2,1)S(1)} %slice.25), channel_id=1, source_target_pairs={{4,8},{8,4},{12,14},{14,12},{10,6},{6,10},{2,0},{0,2},{1,5},{5,1},... | collective-permute-start | bytes 786440 | tf_op jit(solution)/shard_map/ppermute | solution.py:183
  51.6 4.9 %collective-permute-start.15 = (bf16[512,256]{1,0:T(8,128)(2,1)S(1)}, bf16[512,256]{1,0:T(8,128)(2,1)S(1)}, u32[]{:S(2)}, u32[]{:S(2)}) collective-permute-start(bf16[512,256]{1,0:T(8,128)(2,1)S(1)} %slice.23), channel_id=1, source_target_pairs={{0,1},{1,0},{2,3},{3,2},{4,5},{5,4},{6,7},{7,6},{8,9},{9,8},{10,11... | collective-permute-start | bytes 786440 | tf_op jit(solution)/shard_map/ppermute | solution.py:183
  54.3 4.1 %collective-permute-start.21 = (bf16[128,1024]{1,0:T(8,128)(2,1)S(1)}, bf16[128,1024]{1,0:T(8,128)(2,1)S(1)}, u32[]{:S(2)}, u32[]{:S(2)}) collective-permute-start(bf16[128,1024]{1,0:T(8,128)(2,1)S(1)} %get-tuple-element.61.refs_1_), channel_id=1, source_target_pairs={{0,1},{1,0},{2,3},{3,2},{4,5},{5,4},{6,7},{7,6},{8,9},{9,8},{10,11... | collective-permute-start | bytes 786440 | tf_op jit(solution)/shard_map/ppermute | solution.py:183
  55.9 2.4 %collective-permute-start.18 = (bf16[128,512]{1,0:T(8,128)(2,1)S(1)}, bf16[128,512]{1,0:T(8,128)(2,1)S(1)}, u32[]{:S(2)}, u32[]{:S(2)}) collective-permute-start(bf16[128,512]{1,0:T(8,128)(2,1)S(1)} %get-tuple-element.59.refs_0_), channel_id=1, source_target_pairs={{0,1},{1,0},{2,3},{3,2},{4,5},{5,4},{6,7},{7,6},{8,9},{9,8},{10,11... | collective-permute-start | bytes 393224 | tf_op jit(solution)/shard_map/ppermute | solution.py:183
  55.9 2.4 %collective-permute-start.20 = (bf16[512,128]{1,0:T(8,128)(2,1)S(1)}, bf16[512,128]{1,0:T(8,128)(2,1)S(1)}, u32[]{:S(2)}, u32[]{:S(2)}) collective-permute-start(bf16[512,128]{1,0:T(8,128)(2,1)S(1)} %slice.28), channel_id=1, source_target_pairs={{0,1},{1,0},{2,3},{3,2},{4,5},{5,4},{6,7},{7,6},{8,9},{9,8},{10,11... | collective-permute-start | bytes 393224 | tf_op jit(solution)/shard_map/ppermute | solution.py:183
  59.3 4.3 %collective-permute-start.23 = (bf16[512,512]{1,0:T(8,128)(2,1)S(1)}, bf16[512,512]{1,0:T(8,128)(2,1)S(1)}, u32[]{:S(2)}, u32[]{:S(2)}) collective-permute-start(bf16[512,512]{1,0:T(8,128)(2,1)S(1)} %get-tuple-element.64.sent), channel_id=1, source_target_pairs={{0,1},{1,0},{2,3},{3,2},{4,5},{5,4},{6,7},{7,6},{8,9},{9,8},{10,11... | collective-permute-start | bytes 1572872 | tf_op jit(solution)/shard_map/ppermute | solution.py:183
  60.3 6.4 %collective-permute-start.22 = (bf16[512,256]{1,0:T(8,128)(2,1)S(1)}, bf16[512,256]{1,0:T(8,128)(2,1)S(1)}, u32[]{:S(2)}, u32[]{:S(2)}) collective-permute-start(bf16[512,256]{1,0:T(8,128)(2,1)S(1)} %change.3), channel_id=1, source_target_pairs={{4,8},{8,4},{12,14},{14,12},{10,6},{6,10},{2,0},{0,2},{1,5},{5,1},... | collective-permute-start | bytes 786440 | tf_op jit(solution)/shard_map/ppermute | solution.py:183
  64.8 6.4 %collective-permute-start.25 = (bf16[512,256]{1,0:T(8,128)(2,1)S(1)}, bf16[512,256]{1,0:T(8,128)(2,1)S(1)}, u32[]{:S(2)}, u32[]{:S(2)}) collective-permute-start(bf16[512,256]{1,0:T(8,128)(2,1)S(1)} %get-tuple-element.74), channel_id=1, source_target_pairs={{0,4},{4,0},{8,12},{12,8},{14,10},{10,14},{6,2},{2,6},{5,9},{9,5},... | collective-permute-start | bytes 786440 | tf_op jit(solution)/shard_map/ppermute | solution.py:183
  67.3 7.4 %collective-permute-start.24 = (bf16[512,256]{1,0:T(8,128)(2,1)S(1)}, bf16[512,256]{1,0:T(8,128)(2,1)S(1)}, u32[]{:S(2)}, u32[]{:S(2)}) collective-permute-start(bf16[512,256]{1,0:T(8,128)(2,1)S(1)} %hop.5), channel_id=1, source_target_pairs={{0,4},{4,0},{8,12},{12,8},{14,10},{10,14},{6,2},{2,6},{5,9},{9,5},... | collective-permute-start | bytes 786440 | tf_op jit(solution)/shard_map/ppermute | solution.py:183
  71.9 6.4 %collective-permute-start.27 = (bf16[512,256]{1,0:T(8,128)(2,1)S(1)}, bf16[512,256]{1,0:T(8,128)(2,1)S(1)}, u32[]{:S(2)}, u32[]{:S(2)}) collective-permute-start(bf16[512,256]{1,0:T(8,128)(2,1)S(1)} %hop.6), channel_id=1, source_target_pairs={{4,8},{8,4},{12,14},{14,12},{10,6},{6,10},{2,0},{0,2},{1,5},{5,1},... | collective-permute-start | bytes 786440 | tf_op jit(solution)/shard_map/ppermute | solution.py:183
  75.4 7.9 %collective-permute-start.26 = (bf16[512,256]{1,0:T(8,128)(2,1)S(1)}, bf16[512,256]{1,0:T(8,128)(2,1)S(1)}, u32[]{:S(2)}, u32[]{:S(2)}) collective-permute-start(bf16[512,256]{1,0:T(8,128)(2,1)S(1)} %hop.7), channel_id=1, source_target_pairs={{4,8},{8,4},{12,14},{14,12},{10,6},{6,10},{2,0},{0,2},{1,5},{5,1},... | collective-permute-start | bytes 786440 | tf_op jit(solution)/shard_map/ppermute | solution.py:183
  78.9 6.9 %collective-permute-start.29 = (bf16[512,256]{1,0:T(8,128)(2,1)S(1)}, bf16[512,256]{1,0:T(8,128)(2,1)S(1)}, u32[]{:S(2)}, u32[]{:S(2)}) collective-permute-start(bf16[512,256]{1,0:T(8,128)(2,1)S(1)} %hop.8), channel_id=1, source_target_pairs={{0,4},{4,0},{8,12},{12,8},{14,10},{10,14},{6,2},{2,6},{5,9},{9,5},... | collective-permute-start | bytes 786440 | tf_op jit(solution)/shard_map/ppermute | solution.py:183
  83.9 6.4 %collective-permute-start.28 = (bf16[512,256]{1,0:T(8,128)(2,1)S(1)}, bf16[512,256]{1,0:T(8,128)(2,1)S(1)}, u32[]{:S(2)}, u32[]{:S(2)}) collective-permute-start(bf16[512,256]{1,0:T(8,128)(2,1)S(1)} %hop.9), channel_id=1, source_target_pairs={{0,4},{4,0},{8,12},{12,8},{14,10},{10,14},{6,2},{2,6},{5,9},{9,5},... | collective-permute-start | bytes 786440 | tf_op jit(solution)/shard_map/ppermute | solution.py:183
  85.8 4.5 %collective-permute-start.30 = (bf16[512,256]{1,0:T(8,128)(2,1)S(1)}, bf16[512,256]{1,0:T(8,128)(2,1)S(1)}, u32[]{:S(2)}, u32[]{:S(2)}) collective-permute-start(bf16[512,256]{1,0:T(8,128)(2,1)S(1)} %collective-permute-done.29), channel_id=1, source_target_pairs={{0,1},{1,0},{2,3},{3,2},{4,5},{5,4},{6,7},{7,6},{8,9},{9,8},{10,11... | collective-permute-start | bytes 786440 | tf_op jit(solution)/shard_map/ppermute | solution.py:183
  90.9 6.5 %collective-permute-start.31 = (bf16[512,256]{1,0:T(8,128)(2,1)S(1)}, bf16[512,256]{1,0:T(8,128)(2,1)S(1)}, u32[]{:S(2)}, u32[]{:S(2)}) collective-permute-start(bf16[512,256]{1,0:T(8,128)(2,1)S(1)} %last.1.change), channel_id=1, source_target_pairs={{0,2},{2,0},{1,3},{3,1},{4,6},{6,4},{5,7},{7,5},{8,10},{10,8},{9,1... | collective-permute-start | bytes 786440 | tf_op jit(solution)/shard_map/ppermute | solution.py:183
  (5 other events, 43.2 us)

commit v14 on v13

--- a/solution.py
+++ b/solution.py
@@ -237,27 +237,27 @@
     x1, r1 = S(x0), S(r0)
     q0, f0 = block(x0, part)
     (x1,) = after((x1,), q0)
-    x2 = T(x1)
-    q1, f1 = block(x1, 2 * part)
-    (r1,) = after((r1,), q1)
-    r2 = T(r1)
     theirs = lambda r: C(r[padded:])
+
+    def onward(way, rows, residual, size, begun, earlier):
+        q, f = block(rows, size)
+        (rows,) = after((rows,), q)
+        further = way(rows[:part] if way is last else rows)
+        q_other = C(q)
+        (residual,) = after((residual,), q_other)
+        further_residual = way(residual[:, :part] if way is last else residual)
+        begun = begin([*earlier, (residual, q), (theirs(residual), q_other)], *begun)
+        return q, f, further, further_residual, begun
+
+    last = lambda x: T(x)
     q0_other, f0_other = C(q0), C(f0)
-    (x2,) = after((x2,), q1, q0_other, f0_other)
-    x3 = S(x2)
-    q2, f2 = block(x2, 2 * part)
-    begun = begin([(r0, q0), (r0, q0_other), (r1, q1), (theirs(r1), C(q1))])
-    (r2,) = after((r2,), q2, begun)
-    r3 = S(r2)
+    q1, f1, x2, r2, begun = onward(T, x1, r1, 2 * part, (), [(r0, q0), (r0, q0_other)])
+    (x2,) = after((x2,), begun, f0_other)
+    q2, f2, x3, r3, begun = onward(S, x2, r2, 2 * part, (begun,), [])
     (x3,) = after((x3,), begun)
-    x4 = T(x3[:part])
-    q3, f3 = block(x3, 2 * part)
-    (r3,) = after((r3,), q3)
-    r4 = T(r3[:, :part])
-    (x4,) = after((x4,), q3)
+    q3, f3, x4, r4, begun = onward(last, x3, r3, 2 * part, (begun,), [])
     q4, f4 = block(x4, part)
     f4_other = C(f4)
-    begun = begin([(r2, q2), (theirs(r2), C(q2)), (r3, q3), (theirs(r3), C(q3))], begun)
     (begun,) = after((begun,), f4_other)
     update, sent = call(
         update_kernel, (like((padded, depth), F32), like((padded, depth))), place,

time: 100 us -> 98.7 us (0.987)
  waiting for transfers between devices: 30.3 us -> 25 us
  starting transfers between devices: 31.5 us -> 35.2 us
    ppermute x32, waiting for transfers between devices: 30.3 us -> 25 us  [swap(): lax.ppermute(x, axes, [p for a, b in pairs for p in ((a, b), (b, a))])]
    ppermute x32, starting transfers between devices: 31.5 us -> 35.2 us  [swap(): lax.ppermute(x, axes, [p for a, b in pairs for p in ((a, b), (b, a))])]
    pallas_call x21 -> x22, Pallas kernels: 31.7 us -> 32.4 us  [call(): pl.pallas_call(kernel, out_shape=out_shapes, in_specs=[pl.BlockSpec(memor...]
  transfers between devices with their start and end apart: 32 -> 32, of which waited for: 15 -> 14; matrix products, arithmetic and copies ran while one was open for 1% -> 1% of each run, Pallas kernels for 29% -> 30%
where the time goes in v14:
time: 98.7 us; the launch traced here: 97.3 us
  starting transfers between devices  35.2 us (36%)
  Pallas kernels  32.4 us (33%)
  waiting for transfers between devices  25 us (25%)
  local copies, waits for them, and re-layouts  2.35 us (2%)
  other arithmetic  1.24 us (1%)
  between operations  1.13 us (1%)
    ppermute x32, starting transfers between devices, swap(): lax.ppermute(x, axes, [p for a, b in pairs for p in ((a, b), (b, a))])  35.2 us
    pallas_call x22, Pallas kernels, call(): pl.pallas_call(kernel, out_shape=out_shapes, in_specs=[pl.BlockSpec(memor...  32.4 us
    ppermute x32, waiting for transfers between devices, swap(): lax.ppermute(x, axes, [p for a, b in pairs for p in ((a, b), (b, a))])  25 us
    unnamed x11, local copies, waits for them, and re-layouts  2.22 us
  transfers between devices with their start and end apart: 32, of which 14 were waited for; matrix products, arithmetic and copies ran while one was open for 1% of the time, Pallas kernels for 30%

profile of v14, /device:TPU:0, one launch (start us, length us, event | category | flops | bytes accessed | tf_op | source)
XLA Modules:
  0.0 97.3 jit_solution(2373530567796081560)
XLA Ops:
  1.2 1.9 %prepare.1 = (bf16[256,1024]{1,0:T(8,128)(2,1)S(1)}, bf16[512,256]{1,0:T(8,128)(2,1)S(1)}, bf16[512,256]{1,0:T(8,128)(2,1)S(1)}) custom-call(s32[3]{0:T(128)S(1)} %pad_add_fusion.place, bf16[512,1024]{1,0:T(8,128)(2,1)} %inputs.1, s32[1,512]{1,0:T(1,128)} %bitcast.18, f32[500,512]{1,0:T(8,128)} %bitcast.13), custom_call_target="tpu_custom_call" | custom-call | tf_op jit(solution)/shard_map/prepare/pallas_call | solution.py:42
  3.3 2.0 %collective-permute-done = bf16[512,256]{1,0:T(8,128)(2,1)S(1)} collective-permute-done((bf16[512,256]{1,0:T(8,128)(2,1)S(1)}, bf16[512,256]{1,0:T(8,128)(2,1)S(1)}, u32[]{:S(2)}, u32[]{:S(2)}) %collective-permute-start) | collective-permute-done | bytes 262176 | tf_op jit(solution)/shard_map/ppermute | solution.py:183
  5.3 2.9 %collective-permute-start.5 = (bf16[256,1024]{1,0:T(8,128)(2,1)S(1)}, bf16[256,1024]{1,0:T(8,128)(2,1)S(1)}, u32[]{:S(2)}, u32[]{:S(2)}) collective-permute-start(bf16[256,1024]{1,0:T(8,128)(2,1)S(1)} %get-tuple-element.48.rows), channel_id=1, source_target_pairs={{0,4},{4,0},{8,12},{12,8},{14,10},{10,14},{6,2},{2,6},{5,9},{9,5},... | collective-permute-start | bytes 1572872 | tf_op jit(solution)/shard_map/ppermute | solution.py:183
  8.4 2.2 %copy-done.2 = f32[1,512,2048]{2,1,0:T(8,128)S(1)} copy-done((f32[1,512,2048]{2,1,0:T(8,128)S(1)}, f32[1,512,2048]{2,1,0:T(8,128)}, u32[]{:S(2)}) %copy-start.2) | copy-done | bytes 4194328
  11.3 1.5 %collective-permute-start.4 = (bf16[1024,256]{1,0:T(8,128)(2,1)S(1)}, bf16[1024,256]{1,0:T(8,128)(2,1)S(1)}, u32[]{:S(2)}, u32[]{:S(2)}) collective-permute-start(bf16[1024,256]{1,0:T(8,128)(2,1)S(1)} %constant_dynamic-update-slice_fusion.refs_0_.refs_2_), channel_id=1, source_target_pairs={{0,4},{4,0},{8,12},{12,8},{14,10},{10,14},{6,2},{2,6},{5,9},{9,5},... | collective-permute-start | bytes 1572872 | tf_op jit(solution)/shard_map/ppermute | solution.py:183
  12.8 2.4 %block.5 = (bf16[128,1024]{1,0:T(8,128)(2,1)S(1)}, bf16[128,512]{1,0:T(8,128)(2,1)S(1)}) custom-call(s32[3]{0:T(128)S(1)} %pad_add_fusion.place, bf16[256,1024]{1,0:T(8,128)(2,1)S(1)} %get-tuple-element.48.rows, bf16[1024,1024]{1,0:T(8,128)(2,1)S(1)} %copy-done, bf16[1024,1024]{1,0:T(8,128)(2,1)S(1)} %collective-permute-done.1.w_other, ...), custom_call_target="tpu_custom_call" | custom-call | tf_op jit(solution)/shard_map/block/pallas_call | solution.py:42
  15.4 3.4 %block.6 = (bf16[256,1024]{1,0:T(8,128)(2,1)S(1)}, bf16[256,512]{1,0:T(8,128)(2,1)S(1)}) custom-call(s32[3]{0:T(128)S(1)} %pad_add_fusion.place, bf16[256,1024]{1,0:T(8,128)(2,1)S(1)} %collective-permute-done.5.rows, bf16[1024,1024]{1,0:T(8,128)(2,1)S(1)} %copy-done, bf16[1024,1024]{1,0:T(8,128)(2,1)S(1)} %collective-permute-done.1.w_other, ...), custom_call_target="tpu_custom_call" | custom-call | tf_op jit(solution)/shard_map/block/pallas_call | solution.py:42
  19.0 1.9 %collective-permute-start.9 = (bf16[256,1024]{1,0:T(8,128)(2,1)S(1)}, bf16[256,1024]{1,0:T(8,128)(2,1)S(1)}, u32[]{:S(2)}, u32[]{:S(2)}) collective-permute-start(bf16[256,1024]{1,0:T(8,128)(2,1)S(1)} %collective-permute-done.5.rows), channel_id=1, source_target_pairs={{4,8},{8,4},{12,14},{14,12},{10,6},{6,10},{2,0},{0,2},{1,5},{5,1},... | collective-permute-start | bytes 1572872 | tf_op jit(solution)/shard_map/ppermute | solution.py:183
  21.7 1.9 %collective-permute-start.8 = (bf16[1024,256]{1,0:T(8,128)(2,1)S(1)}, bf16[1024,256]{1,0:T(8,128)(2,1)S(1)}, u32[]{:S(2)}, u32[]{:S(2)}) collective-permute-start(bf16[1024,256]{1,0:T(8,128)(2,1)S(1)} %collective-permute-done.4.refs_4_), channel_id=1, source_target_pairs={{4,8},{8,4},{12,14},{14,12},{10,6},{6,10},{2,0},{0,2},{1,5},{5,1},... | collective-permute-start | bytes 1572872 | tf_op jit(solution)/shard_map/ppermute | solution.py:183
  23.6 1.5 %begin.3.refs_0_ = f32[512,512]{1,0:T(8,128)S(1)} custom-call(s32[3]{0:T(128)S(1)} %pad_add_fusion.place, bf16[1024,256]{1,0:T(8,128)(2,1)S(1)} %constant_dynamic-update-slice_fusion.refs_0_.refs_2_, bf16[128,1024]{1,0:T(8,128)(2,1)S(1)} %get-tuple-element.49.refs_1_, bf16[1024,256]{1,0:T(8,128)(2,1)S(1)} %constant_dynamic-update-slice_fusion.refs_0_.refs_2_, ...), custom_call_target="tpu_custom_call" | custom-call | tf_op jit(solution)/shard_map/begin/pallas_call | solution.py:42
  25.1 3.1 %collective-permute-done.9.rows = bf16[256,1024]{1,0:T(8,128)(2,1)S(1)} collective-permute-done((bf16[256,1024]{1,0:T(8,128)(2,1)S(1)}, bf16[256,1024]{1,0:T(8,128)(2,1)S(1)}, u32[]{:S(2)}, u32[]{:S(2)}) %collective-permute-start.9) | collective-permute-done | bytes 524320 | tf_op jit(solution)/shard_map/ppermute | solution.py:183
  28.2 3.4 %block.7 = (bf16[256,1024]{1,0:T(8,128)(2,1)S(1)}, bf16[256,512]{1,0:T(8,128)(2,1)S(1)}) custom-call(s32[3]{0:T(128)S(1)} %pad_add_fusion.place, bf16[256,1024]{1,0:T(8,128)(2,1)S(1)} %collective-permute-done.9.rows, bf16[1024,1024]{1,0:T(8,128)(2,1)S(1)} %copy-done, bf16[1024,1024]{1,0:T(8,128)(2,1)S(1)} %collective-permute-done.1.w_other, ...), custom_call_target="tpu_custom_call" | custom-call | tf_op jit(solution)/shard_map/block/pallas_call | solution.py:42
  31.6 2.0 %collective-permute-start.14 = (bf16[256,1024]{1,0:T(8,128)(2,1)S(1)}, bf16[256,1024]{1,0:T(8,128)(2,1)S(1)}, u32[]{:S(2)}, u32[]{:S(2)}) collective-permute-start(bf16[256,1024]{1,0:T(8,128)(2,1)S(1)} %collective-permute-done.9.rows), channel_id=1, source_target_pairs={{0,4},{4,0},{8,12},{12,8},{14,10},{10,14},{6,2},{2,6},{5,9},{9,5},... | collective-permute-start | bytes 1572872 | tf_op jit(solution)/shard_map/ppermute | solution.py:183
  33.9 2.0 %collective-permute-start.13 = (bf16[1024,256]{1,0:T(8,128)(2,1)S(1)}, bf16[1024,256]{1,0:T(8,128)(2,1)S(1)}, u32[]{:S(2)}, u32[]{:S(2)}) collective-permute-start(bf16[1024,256]{1,0:T(8,128)(2,1)S(1)} %collective-permute-done.8.refs_1_), channel_id=1, source_target_pairs={{0,4},{4,0},{8,12},{12,8},{14,10},{10,14},{6,2},{2,6},{5,9},{9,5},... | collective-permute-start | bytes 1572872 | tf_op jit(solution)/shard_map/ppermute | solution.py:183
  37.2 3.7 %collective-permute-done.14.rows = bf16[256,1024]{1,0:T(8,128)(2,1)S(1)} collective-permute-done((bf16[256,1024]{1,0:T(8,128)(2,1)S(1)}, bf16[256,1024]{1,0:T(8,128)(2,1)S(1)}, u32[]{:S(2)}, u32[]{:S(2)}) %collective-permute-start.14) | collective-permute-done | bytes 524320 | tf_op jit(solution)/shard_map/ppermute | solution.py:183
  40.9 3.4 %block.8 = (bf16[256,1024]{1,0:T(8,128)(2,1)S(1)}, bf16[256,512]{1,0:T(8,128)(2,1)S(1)}) custom-call(s32[3]{0:T(128)S(1)} %pad_add_fusion.place, bf16[256,1024]{1,0:T(8,128)(2,1)S(1)} %collective-permute-done.14.rows, bf16[1024,1024]{1,0:T(8,128)(2,1)S(1)} %copy-done, bf16[1024,1024]{1,0:T(8,128)(2,1)S(1)} %collective-permute-done.1.w_other, ...), custom_call_target="tpu_custom_call" | custom-call | tf_op jit(solution)/shard_map/block/pallas_call | solution.py:42
  44.3 1.9 %collective-permute-start.17 = (bf16[128,1024]{1,0:T(8,128)(2,1)S(1)}, bf16[128,1024]{1,0:T(8,128)(2,1)S(1)}, u32[]{:S(2)}, u32[]{:S(2)}) collective-permute-start(bf16[128,1024]{1,0:T(8,128)(2,1)S(1)} %slice.24), channel_id=1, source_target_pairs={{4,8},{8,4},{12,14},{14,12},{10,6},{6,10},{2,0},{0,2},{1,5},{5,1},... | collective-permute-start | bytes 786440 | tf_op jit(solution)/shard_map/ppermute | solution.py:183
  46.5 1.9 %collective-permute-start.19 = (bf16[1024,128]{1,0:T(8,128)(2,1)S(1)}, bf16[1024,128]{1,0:T(8,128)(2,1)S(1)}, u32[]{:S(2)}, u32[]{:S(2)}) collective-permute-start(bf16[1024,128]{1,0:T(8,128)(2,1)S(1)} %slice.25), channel_id=1, source_target_pairs={{4,8},{8,4},{12,14},{14,12},{10,6},{6,10},{2,0},{0,2},{1,5},{5,1},... | collective-permute-start | bytes 786440 | tf_op jit(solution)/shard_map/ppermute | solution.py:183
  48.5 2.2 %collective-permute-done.17.rows = bf16[128,1024]{1,0:T(8,128)(2,1)S(1)} collective-permute-done((bf16[128,1024]{1,0:T(8,128)(2,1)S(1)}, bf16[128,1024]{1,0:T(8,128)(2,1)S(1)}, u32[]{:S(2)}, u32[]{:S(2)}) %collective-permute-start.17) | collective-permute-done | bytes 262176 | tf_op jit(solution)/shard_map/ppermute | solution.py:183
  50.8 2.6 %block.9 = (bf16[128,1024]{1,0:T(8,128)(2,1)S(1)}, bf16[128,512]{1,0:T(8,128)(2,1)S(1)}) custom-call(s32[3]{0:T(128)S(1)} %pad_add_fusion.place, bf16[128,1024]{1,0:T(8,128)(2,1)S(1)} %collective-permute-done.17.rows, bf16[1024,1024]{1,0:T(8,128)(2,1)S(1)} %copy-done, bf16[1024,1024]{1,0:T(8,128)(2,1)S(1)} %collective-permute-done.1.w_other, ...), custom_call_target="tpu_custom_call" | custom-call | tf_op jit(solution)/shard_map/block/pallas_call | solution.py:42
  57.8 1.9 %collective-permute-start.22 = (bf16[512,256]{1,0:T(8,128)(2,1)S(1)}, bf16[512,256]{1,0:T(8,128)(2,1)S(1)}, u32[]{:S(2)}, u32[]{:S(2)}) collective-permute-start(bf16[512,256]{1,0:T(8,128)(2,1)S(1)} %change.3), channel_id=1, source_target_pairs={{4,8},{8,4},{12,14},{14,12},{10,6},{6,10},{2,0},{0,2},{1,5},{5,1},... | collective-permute-start | bytes 786440 | tf_op jit(solution)/shard_map/ppermute | solution.py:183
  62.2 1.7 %collective-permute-start.25 = (bf16[512,256]{1,0:T(8,128)(2,1)S(1)}, bf16[512,256]{1,0:T(8,128)(2,1)S(1)}, u32[]{:S(2)}, u32[]{:S(2)}) collective-permute-start(bf16[512,256]{1,0:T(8,128)(2,1)S(1)} %get-tuple-element.78), channel_id=1, source_target_pairs={{0,4},{4,0},{8,12},{12,8},{14,10},{10,14},{6,2},{2,6},{5,9},{9,5},... | collective-permute-start | bytes 786440 | tf_op jit(solution)/shard_map/ppermute | solution.py:183
  64.8 2.0 %collective-permute-start.24 = (bf16[512,256]{1,0:T(8,128)(2,1)S(1)}, bf16[512,256]{1,0:T(8,128)(2,1)S(1)}, u32[]{:S(2)}, u32[]{:S(2)}) collective-permute-start(bf16[512,256]{1,0:T(8,128)(2,1)S(1)} %hop.5), channel_id=1, source_target_pairs={{0,4},{4,0},{8,12},{12,8},{14,10},{10,14},{6,2},{2,6},{5,9},{9,5},... | collective-permute-start | bytes 786440 | tf_op jit(solution)/shard_map/ppermute | solution.py:183
  66.8 1.7 %collective-permute-done.25.came = bf16[512,256]{1,0:T(8,128)(2,1)S(1)} collective-permute-done((bf16[512,256]{1,0:T(8,128)(2,1)S(1)}, bf16[512,256]{1,0:T(8,128)(2,1)S(1)}, u32[]{:S(2)}, u32[]{:S(2)}) %collective-permute-start.25) | collective-permute-done | bytes 262176 | tf_op jit(solution)/shard_map/ppermute | solution.py:183
  70.4 1.4 %collective-permute-done.24.came = bf16[512,256]{1,0:T(8,128)(2,1)S(1)} collective-permute-done((bf16[512,256]{1,0:T(8,128)(2,1)S(1)}, bf16[512,256]{1,0:T(8,128)(2,1)S(1)}, u32[]{:S(2)}, u32[]{:S(2)}) %collective-permute-start.24) | collective-permute-done | bytes 262176 | tf_op jit(solution)/shard_map/ppermute | solution.py:183
  72.4 2.0 %collective-permute-start.26 = (bf16[512,256]{1,0:T(8,128)(2,1)S(1)}, bf16[512,256]{1,0:T(8,128)(2,1)S(1)}, u32[]{:S(2)}, u32[]{:S(2)}) collective-permute-start(bf16[512,256]{1,0:T(8,128)(2,1)S(1)} %hop.7), channel_id=1, source_target_pairs={{4,8},{8,4},{12,14},{14,12},{10,6},{6,10},{2,0},{0,2},{1,5},{5,1},... | collective-permute-start | bytes 786440 | tf_op jit(solution)/shard_map/ppermute | solution.py:183
  76.2 1.8 %collective-permute-start.29 = (bf16[512,256]{1,0:T(8,128)(2,1)S(1)}, bf16[512,256]{1,0:T(8,128)(2,1)S(1)}, u32[]{:S(2)}, u32[]{:S(2)}) collective-permute-start(bf16[512,256]{1,0:T(8,128)(2,1)S(1)} %hop.8), channel_id=1, source_target_pairs={{0,4},{4,0},{8,12},{12,8},{14,10},{10,14},{6,2},{2,6},{5,9},{9,5},... | collective-permute-start | bytes 786440 | tf_op jit(solution)/shard_map/ppermute | solution.py:183
  78.0 2.0 %collective-permute-done.26.came = bf16[512,256]{1,0:T(8,128)(2,1)S(1)} collective-permute-done((bf16[512,256]{1,0:T(8,128)(2,1)S(1)}, bf16[512,256]{1,0:T(8,128)(2,1)S(1)}, u32[]{:S(2)}, u32[]{:S(2)}) %collective-permute-start.26) | collective-permute-done | bytes 262176 | tf_op jit(solution)/shard_map/ppermute | solution.py:183
  80.7 3.7 %collective-permute-start.28 = (bf16[512,256]{1,0:T(8,128)(2,1)S(1)}, bf16[512,256]{1,0:T(8,128)(2,1)S(1)}, u32[]{:S(2)}, u32[]{:S(2)}) collective-permute-start(bf16[512,256]{1,0:T(8,128)(2,1)S(1)} %hop.9), channel_id=1, source_target_pairs={{0,4},{4,0},{8,12},{12,8},{14,10},{10,14},{6,2},{2,6},{5,9},{9,5},... | collective-permute-start | bytes 786440 | tf_op jit(solution)/shard_map/ppermute | solution.py:183
  84.4 4.3 %collective-permute-done.28.came = bf16[512,256]{1,0:T(8,128)(2,1)S(1)} collective-permute-done((bf16[512,256]{1,0:T(8,128)(2,1)S(1)}, bf16[512,256]{1,0:T(8,128)(2,1)S(1)}, u32[]{:S(2)}, u32[]{:S(2)}) %collective-permute-start.28) | collective-permute-done | bytes 262176 | tf_op jit(solution)/shard_map/ppermute | solution.py:183
  89.4 1.6 %collective-permute-start.31 = (bf16[512,256]{1,0:T(8,128)(2,1)S(1)}, bf16[512,256]{1,0:T(8,128)(2,1)S(1)}, u32[]{:S(2)}, u32[]{:S(2)}) collective-permute-start(bf16[512,256]{1,0:T(8,128)(2,1)S(1)} %last.1.change), channel_id=1, source_target_pairs={{0,2},{2,0},{1,3},{3,1},{4,6},{6,4},{5,7},{7,5},{8,10},{10,8},{9,1... | collective-permute-start | bytes 786440 | tf_op jit(solution)/shard_map/ppermute | solution.py:183
  93.5 2.3 %collective-permute-done.31.change = bf16[512,256]{1,0:T(8,128)(2,1)S(1)} collective-permute-done((bf16[512,256]{1,0:T(8,128)(2,1)S(1)}, bf16[512,256]{1,0:T(8,128)(2,1)S(1)}, u32[]{:S(2)}, u32[]{:S(2)}) %collective-permute-start.31) | collective-permute-done | bytes 262176 | tf_op jit(solution)/shard_map/ppermute | solution.py:183
  (75 shorter events, 21.8 us)
Async XLA Ops:
  0.6 12.2 %collective-permute-start.1 = (bf16[1024,1024]{1,0:T(8,128)(2,1)}, bf16[1024,1024]{1,0:T(8,128)(2,1)S(1)}, u32[]{:S(2)}, u32[]{:S(2)}) collective-permute-start(bf16[1024,1024]{1,0:T(8,128)(2,1)} %w_own.9), channel_id=1, source_target_pairs={{0,1},{1,0},{2,3},{3,2},{4,5},{5,4},{6,7},{7,6},{8,9},{9,8},{10,11... | collective-permute-start | bytes 6291464 | tf_op jit(solution)/shard_map/ppermute | solution.py:183
  3.2 2.2 %collective-permute-start = (bf16[512,256]{1,0:T(8,128)(2,1)S(1)}, bf16[512,256]{1,0:T(8,128)(2,1)S(1)}, u32[]{:S(2)}, u32[]{:S(2)}) collective-permute-start(bf16[512,256]{1,0:T(8,128)(2,1)S(1)} %get-tuple-element.46), channel_id=1, source_target_pairs={{0,1},{1,0},{2,3},{3,2},{4,5},{5,4},{6,7},{7,6},{8,9},{9,8},{10,11... | collective-permute-start | bytes 786440 | tf_op jit(solution)/shard_map/ppermute | solution.py:183
  5.3 10.1 %collective-permute-start.5 = (bf16[256,1024]{1,0:T(8,128)(2,1)S(1)}, bf16[256,1024]{1,0:T(8,128)(2,1)S(1)}, u32[]{:S(2)}, u32[]{:S(2)}) collective-permute-start(bf16[256,1024]{1,0:T(8,128)(2,1)S(1)} %get-tuple-element.48.rows), channel_id=1, source_target_pairs={{0,4},{4,0},{8,12},{12,8},{14,10},{10,14},{6,2},{2,6},{5,9},{9,5},... | collective-permute-start | bytes 1572872 | tf_op jit(solution)/shard_map/ppermute | solution.py:183
  8.3 4.6 %collective-permute-start.2 = (bf16[1,1024]{1,0:T(2,128)(2,1)S(1)}, bf16[1,1024]{1,0:T(2,128)(2,1)S(1)}, u32[]{:S(2)}, u32[]{:S(2)}) collective-permute-start(bf16[1,1024]{1,0:T(2,128)(2,1)S(1)} %broadcast_in_dim.7.p_own), channel_id=1, source_target_pairs={{0,1},{1,0},{2,3},{3,2},{4,5},{5,4},{6,7},{7,6},{8,9},{9,8},{10,11... | collective-permute-start | bytes 6152 | tf_op jit(solution)/shard_map/ppermute | solution.py:183
  11.3 9.8 %collective-permute-start.4 = (bf16[1024,256]{1,0:T(8,128)(2,1)S(1)}, bf16[1024,256]{1,0:T(8,128)(2,1)S(1)}, u32[]{:S(2)}, u32[]{:S(2)}) collective-permute-start(bf16[1024,256]{1,0:T(8,128)(2,1)S(1)} %constant_dynamic-update-slice_fusion.refs_0_.refs_2_), channel_id=1, source_target_pairs={{0,4},{4,0},{8,12},{12,8},{14,10},{10,14},{6,2},{2,6},{5,9},{9,5},... | collective-permute-start | bytes 1572872 | tf_op jit(solution)/shard_map/ppermute | solution.py:183
  18.8 2.3 %collective-permute-start.6 = (bf16[256,1024]{1,0:T(8,128)(2,1)S(1)}, bf16[256,1024]{1,0:T(8,128)(2,1)S(1)}, u32[]{:S(2)}, u32[]{:S(2)}) collective-permute-start(bf16[256,1024]{1,0:T(8,128)(2,1)S(1)} %get-tuple-element.51.refs_5_), channel_id=1, source_target_pairs={{0,1},{1,0},{2,3},{3,2},{4,5},{5,4},{6,7},{7,6},{8,9},{9,8},{10,11... | collective-permute-start | bytes 1572872 | tf_op jit(solution)/shard_map/ppermute | solution.py:183
  19.0 9.2 %collective-permute-start.9 = (bf16[256,1024]{1,0:T(8,128)(2,1)S(1)}, bf16[256,1024]{1,0:T(8,128)(2,1)S(1)}, u32[]{:S(2)}, u32[]{:S(2)}) collective-permute-start(bf16[256,1024]{1,0:T(8,128)(2,1)S(1)} %collective-permute-done.5.rows), channel_id=1, source_target_pairs={{4,8},{8,4},{12,14},{14,12},{10,6},{6,10},{2,0},{0,2},{1,5},{5,1},... | collective-permute-start | bytes 1572872 | tf_op jit(solution)/shard_map/ppermute | solution.py:183
  20.9 2.7 %collective-permute-start.3 = (bf16[128,1024]{1,0:T(8,128)(2,1)S(1)}, bf16[128,1024]{1,0:T(8,128)(2,1)S(1)}, u32[]{:S(2)}, u32[]{:S(2)}) collective-permute-start(bf16[128,1024]{1,0:T(8,128)(2,1)S(1)} %get-tuple-element.49.refs_1_), channel_id=1, source_target_pairs={{0,1},{1,0},{2,3},{3,2},{4,5},{5,4},{6,7},{7,6},{8,9},{9,8},{10,11... | collective-permute-start | bytes 786440 | tf_op jit(solution)/shard_map/ppermute | solution.py:183
  21.1 2.4 %collective-permute-start.7 = (bf16[512,256]{1,0:T(8,128)(2,1)S(1)}, bf16[512,256]{1,0:T(8,128)(2,1)S(1)}, u32[]{:S(2)}, u32[]{:S(2)}) collective-permute-start(bf16[512,256]{1,0:T(8,128)(2,1)S(1)} %slice.21), channel_id=1, source_target_pairs={{0,1},{1,0},{2,3},{3,2},{4,5},{5,4},{6,7},{7,6},{8,9},{9,8},{10,11... | collective-permute-start | bytes 786440 | tf_op jit(solution)/shard_map/ppermute | solution.py:183
  21.5 3.6 %collective-permute-start.10 = (bf16[128,512]{1,0:T(8,128)(2,1)S(1)}, bf16[128,512]{1,0:T(8,128)(2,1)S(1)}, u32[]{:S(2)}, u32[]{:S(2)}) collective-permute-start(bf16[128,512]{1,0:T(8,128)(2,1)S(1)} %get-tuple-element.54.refs_3_), channel_id=1, source_target_pairs={{0,1},{1,0},{2,3},{3,2},{4,5},{5,4},{6,7},{7,6},{8,9},{9,8},{10,11... | collective-permute-start | bytes 393224 | tf_op jit(solution)/shard_map/ppermute | solution.py:183
  21.7 12.1 %collective-permute-start.8 = (bf16[1024,256]{1,0:T(8,128)(2,1)S(1)}, bf16[1024,256]{1,0:T(8,128)(2,1)S(1)}, u32[]{:S(2)}, u32[]{:S(2)}) collective-permute-start(bf16[1024,256]{1,0:T(8,128)(2,1)S(1)} %collective-permute-done.4.refs_4_), channel_id=1, source_target_pairs={{4,8},{8,4},{12,14},{14,12},{10,6},{6,10},{2,0},{0,2},{1,5},{5,1},... | collective-permute-start | bytes 1572872 | tf_op jit(solution)/shard_map/ppermute | solution.py:183
  31.6 2.3 %collective-permute-start.11 = (bf16[256,1024]{1,0:T(8,128)(2,1)S(1)}, bf16[256,1024]{1,0:T(8,128)(2,1)S(1)}, u32[]{:S(2)}, u32[]{:S(2)}) collective-permute-start(bf16[256,1024]{1,0:T(8,128)(2,1)S(1)} %get-tuple-element.56.refs_2_), channel_id=1, source_target_pairs={{0,1},{1,0},{2,3},{3,2},{4,5},{5,4},{6,7},{7,6},{8,9},{9,8},{10,11... | collective-permute-start | bytes 1572872 | tf_op jit(solution)/shard_map/ppermute | solution.py:183
  31.6 9.2 %collective-permute-start.14 = (bf16[256,1024]{1,0:T(8,128)(2,1)S(1)}, bf16[256,1024]{1,0:T(8,128)(2,1)S(1)}, u32[]{:S(2)}, u32[]{:S(2)}) collective-permute-start(bf16[256,1024]{1,0:T(8,128)(2,1)S(1)} %collective-permute-done.9.rows), channel_id=1, source_target_pairs={{0,4},{4,0},{8,12},{12,8},{14,10},{10,14},{6,2},{2,6},{5,9},{9,5},... | collective-permute-start | bytes 1572872 | tf_op jit(solution)/shard_map/ppermute | solution.py:183
  33.8 2.1 %collective-permute-start.12 = (bf16[512,256]{1,0:T(8,128)(2,1)S(1)}, bf16[512,256]{1,0:T(8,128)(2,1)S(1)}, u32[]{:S(2)}, u32[]{:S(2)}) collective-permute-start(bf16[512,256]{1,0:T(8,128)(2,1)S(1)} %slice.22), channel_id=1, source_target_pairs={{0,1},{1,0},{2,3},{3,2},{4,5},{5,4},{6,7},{7,6},{8,9},{9,8},{10,11... | collective-permute-start | bytes 786440 | tf_op jit(solution)/shard_map/ppermute | solution.py:183
  33.9 12.6 %collective-permute-start.13 = (bf16[1024,256]{1,0:T(8,128)(2,1)S(1)}, bf16[1024,256]{1,0:T(8,128)(2,1)S(1)}, u32[]{:S(2)}, u32[]{:S(2)}) collective-permute-start(bf16[1024,256]{1,0:T(8,128)(2,1)S(1)} %collective-permute-done.8.refs_1_), channel_id=1, source_target_pairs={{0,4},{4,0},{8,12},{12,8},{14,10},{10,14},{6,2},{2,6},{5,9},{9,5},... | collective-permute-start | bytes 1572872 | tf_op jit(solution)/shard_map/ppermute | solution.py:183
  44.2 2.3 %collective-permute-start.15 = (bf16[256,1024]{1,0:T(8,128)(2,1)S(1)}, bf16[256,1024]{1,0:T(8,128)(2,1)S(1)}, u32[]{:S(2)}, u32[]{:S(2)}) collective-permute-start(bf16[256,1024]{1,0:T(8,128)(2,1)S(1)} %get-tuple-element.60.refs_2_), channel_id=1, source_target_pairs={{0,1},{1,0},{2,3},{3,2},{4,5},{5,4},{6,7},{7,6},{8,9},{9,8},{10,11... | collective-permute-start | bytes 1572872 | tf_op jit(solution)/shard_map/ppermute | solution.py:183
  44.3 6.4 %collective-permute-start.17 = (bf16[128,1024]{1,0:T(8,128)(2,1)S(1)}, bf16[128,1024]{1,0:T(8,128)(2,1)S(1)}, u32[]{:S(2)}, u32[]{:S(2)}) collective-permute-start(bf16[128,1024]{1,0:T(8,128)(2,1)S(1)} %slice.24), channel_id=1, source_target_pairs={{4,8},{8,4},{12,14},{14,12},{10,6},{6,10},{2,0},{0,2},{1,5},{5,1},... | collective-permute-start | bytes 786440 | tf_op jit(solution)/shard_map/ppermute | solution.py:183
  46.5 7.5 %collective-permute-start.19 = (bf16[1024,128]{1,0:T(8,128)(2,1)S(1)}, bf16[1024,128]{1,0:T(8,128)(2,1)S(1)}, u32[]{:S(2)}, u32[]{:S(2)}) collective-permute-start(bf16[1024,128]{1,0:T(8,128)(2,1)S(1)} %slice.25), channel_id=1, source_target_pairs={{4,8},{8,4},{12,14},{14,12},{10,6},{6,10},{2,0},{0,2},{1,5},{5,1},... | collective-permute-start | bytes 786440 | tf_op jit(solution)/shard_map/ppermute | solution.py:183
  48.5 5.7 %collective-permute-start.16 = (bf16[512,256]{1,0:T(8,128)(2,1)S(1)}, bf16[512,256]{1,0:T(8,128)(2,1)S(1)}, u32[]{:S(2)}, u32[]{:S(2)}) collective-permute-start(bf16[512,256]{1,0:T(8,128)(2,1)S(1)} %slice.23), channel_id=1, source_target_pairs={{0,1},{1,0},{2,3},{3,2},{4,5},{5,4},{6,7},{7,6},{8,9},{9,8},{10,11... | collective-permute-start | bytes 786440 | tf_op jit(solution)/shard_map/ppermute | solution.py:183
  53.4 2.0 %collective-permute-start.21 = (bf16[128,1024]{1,0:T(8,128)(2,1)S(1)}, bf16[128,1024]{1,0:T(8,128)(2,1)S(1)}, u32[]{:S(2)}, u32[]{:S(2)}) collective-permute-start(bf16[128,1024]{1,0:T(8,128)(2,1)S(1)} %get-tuple-element.65.refs_1_), channel_id=1, source_target_pairs={{0,1},{1,0},{2,3},{3,2},{4,5},{5,4},{6,7},{7,6},{8,9},{9,8},{10,11... | collective-permute-start | bytes 786440 | tf_op jit(solution)/shard_map/ppermute | solution.py:183
  53.5 1.9 %collective-permute-start.18 = (bf16[128,512]{1,0:T(8,128)(2,1)S(1)}, bf16[128,512]{1,0:T(8,128)(2,1)S(1)}, u32[]{:S(2)}, u32[]{:S(2)}) collective-permute-start(bf16[128,512]{1,0:T(8,128)(2,1)S(1)} %get-tuple-element.63.refs_0_), channel_id=1, source_target_pairs={{0,1},{1,0},{2,3},{3,2},{4,5},{5,4},{6,7},{7,6},{8,9},{9,8},{10,11... | collective-permute-start | bytes 393224 | tf_op jit(solution)/shard_map/ppermute | solution.py:183
  54.0 1.4 %collective-permute-start.20 = (bf16[512,128]{1,0:T(8,128)(2,1)S(1)}, bf16[512,128]{1,0:T(8,128)(2,1)S(1)}, u32[]{:S(2)}, u32[]{:S(2)}) collective-permute-start(bf16[512,128]{1,0:T(8,128)(2,1)S(1)} %slice.28), channel_id=1, source_target_pairs={{0,1},{1,0},{2,3},{3,2},{4,5},{5,4},{6,7},{7,6},{8,9},{9,8},{10,11... | collective-permute-start | bytes 393224 | tf_op jit(solution)/shard_map/ppermute | solution.py:183
  56.4 4.6 %collective-permute-start.23 = (bf16[512,512]{1,0:T(8,128)(2,1)S(1)}, bf16[512,512]{1,0:T(8,128)(2,1)S(1)}, u32[]{:S(2)}, u32[]{:S(2)}) collective-permute-start(bf16[512,512]{1,0:T(8,128)(2,1)S(1)} %get-tuple-element.68.sent), channel_id=1, source_target_pairs={{0,1},{1,0},{2,3},{3,2},{4,5},{5,4},{6,7},{7,6},{8,9},{9,8},{10,11... | collective-permute-start | bytes 1572872 | tf_op jit(solution)/shard_map/ppermute | solution.py:183
  57.8 6.4 %collective-permute-start.22 = (bf16[512,256]{1,0:T(8,128)(2,1)S(1)}, bf16[512,256]{1,0:T(8,128)(2,1)S(1)}, u32[]{:S(2)}, u32[]{:S(2)}) collective-permute-start(bf16[512,256]{1,0:T(8,128)(2,1)S(1)} %change.3), channel_id=1, source_target_pairs={{4,8},{8,4},{12,14},{14,12},{10,6},{6,10},{2,0},{0,2},{1,5},{5,1},... | collective-permute-start | bytes 786440 | tf_op jit(solution)/shard_map/ppermute | solution.py:183
  62.2 6.4 %collective-permute-start.25 = (bf16[512,256]{1,0:T(8,128)(2,1)S(1)}, bf16[512,256]{1,0:T(8,128)(2,1)S(1)}, u32[]{:S(2)}, u32[]{:S(2)}) collective-permute-start(bf16[512,256]{1,0:T(8,128)(2,1)S(1)} %get-tuple-element.78), channel_id=1, source_target_pairs={{0,4},{4,0},{8,12},{12,8},{14,10},{10,14},{6,2},{2,6},{5,9},{9,5},... | collective-permute-start | bytes 786440 | tf_op jit(solution)/shard_map/ppermute | solution.py:183
  64.8 7.0 %collective-permute-start.24 = (bf16[512,256]{1,0:T(8,128)(2,1)S(1)}, bf16[512,256]{1,0:T(8,128)(2,1)S(1)}, u32[]{:S(2)}, u32[]{:S(2)}) collective-permute-start(bf16[512,256]{1,0:T(8,128)(2,1)S(1)} %hop.5), channel_id=1, source_target_pairs={{0,4},{4,0},{8,12},{12,8},{14,10},{10,14},{6,2},{2,6},{5,9},{9,5},... | collective-permute-start | bytes 786440 | tf_op jit(solution)/shard_map/ppermute | solution.py:183
  69.2 6.4 %collective-permute-start.27 = (bf16[512,256]{1,0:T(8,128)(2,1)S(1)}, bf16[512,256]{1,0:T(8,128)(2,1)S(1)}, u32[]{:S(2)}, u32[]{:S(2)}) collective-permute-start(bf16[512,256]{1,0:T(8,128)(2,1)S(1)} %hop.6), channel_id=1, source_target_pairs={{4,8},{8,4},{12,14},{14,12},{10,6},{6,10},{2,0},{0,2},{1,5},{5,1},... | collective-permute-start | bytes 786440 | tf_op jit(solution)/shard_map/ppermute | solution.py:183
  72.4 7.7 %collective-permute-start.26 = (bf16[512,256]{1,0:T(8,128)(2,1)S(1)}, bf16[512,256]{1,0:T(8,128)(2,1)S(1)}, u32[]{:S(2)}, u32[]{:S(2)}) collective-permute-start(bf16[512,256]{1,0:T(8,128)(2,1)S(1)} %hop.7), channel_id=1, source_target_pairs={{4,8},{8,4},{12,14},{14,12},{10,6},{6,10},{2,0},{0,2},{1,5},{5,1},... | collective-permute-start | bytes 786440 | tf_op jit(solution)/shard_map/ppermute | solution.py:183
  76.2 8.1 %collective-permute-start.29 = (bf16[512,256]{1,0:T(8,128)(2,1)S(1)}, bf16[512,256]{1,0:T(8,128)(2,1)S(1)}, u32[]{:S(2)}, u32[]{:S(2)}) collective-permute-start(bf16[512,256]{1,0:T(8,128)(2,1)S(1)} %hop.8), channel_id=1, source_target_pairs={{0,4},{4,0},{8,12},{12,8},{14,10},{10,14},{6,2},{2,6},{5,9},{9,5},... | collective-permute-start | bytes 786440 | tf_op jit(solution)/shard_map/ppermute | solution.py:183
  80.7 8.0 %collective-permute-start.28 = (bf16[512,256]{1,0:T(8,128)(2,1)S(1)}, bf16[512,256]{1,0:T(8,128)(2,1)S(1)}, u32[]{:S(2)}, u32[]{:S(2)}) collective-permute-start(bf16[512,256]{1,0:T(8,128)(2,1)S(1)} %hop.9), channel_id=1, source_target_pairs={{0,4},{4,0},{8,12},{12,8},{14,10},{10,14},{6,2},{2,6},{5,9},{9,5},... | collective-permute-start | bytes 786440 | tf_op jit(solution)/shard_map/ppermute | solution.py:183
  84.4 4.4 %collective-permute-start.30 = (bf16[512,256]{1,0:T(8,128)(2,1)S(1)}, bf16[512,256]{1,0:T(8,128)(2,1)S(1)}, u32[]{:S(2)}, u32[]{:S(2)}) collective-permute-start(bf16[512,256]{1,0:T(8,128)(2,1)S(1)} %collective-permute-done.29), channel_id=1, source_target_pairs={{0,1},{1,0},{2,3},{3,2},{4,5},{5,4},{6,7},{7,6},{8,9},{9,8},{10,11... | collective-permute-start | bytes 786440 | tf_op jit(solution)/shard_map/ppermute | solution.py:183
  89.4 6.4 %collective-permute-start.31 = (bf16[512,256]{1,0:T(8,128)(2,1)S(1)}, bf16[512,256]{1,0:T(8,128)(2,1)S(1)}, u32[]{:S(2)}, u32[]{:S(2)}) collective-permute-start(bf16[512,256]{1,0:T(8,128)(2,1)S(1)} %last.1.change), channel_id=1, source_target_pairs={{0,2},{2,0},{1,3},{3,1},{4,6},{6,4},{5,7},{7,5},{8,10},{10,8},{9,1... | collective-permute-start | bytes 786440 | tf_op jit(solution)/shard_map/ppermute | solution.py:183
  (5 other events, 45.3 us)

commit v15 on v14

--- a/solution.py
+++ b/solution.py
@@ -96,7 +96,7 @@
     out[...] = x[...].astype(BF16)
 
 
-TILE = 512
+TILE = 1024
 
 
 def block_kernel(place, rows, w_own, w_other, p_own, p_other, inverse, out, own_slice, feats):

time: 98.7 us -> 99.4 us (level)
  Pallas kernels: 32.4 us -> 33.4 us
  starting transfers between devices: 35.2 us -> 34.2 us
    ppermute x32, starting transfers between devices: 35.2 us -> 34.2 us  [swap(): lax.ppermute(x, axes, [p for a, b in pairs for p in ((a, b), (b, a))])]
  transfers between devices with their start and end apart: 32 -> 32, of which waited for: 14 -> 11; matrix products, arithmetic and copies ran while one was open for 1% -> 1% of each run, Pallas kernels for 30% -> 31%
where the time goes in v15:
time: 99.4 us; the launch traced here: 98 us
  starting transfers between devices  34.2 us (34%)
  Pallas kernels  33.4 us (34%)
  waiting for transfers between devices  25.7 us (26%)
  local copies, waits for them, and re-layouts  2.35 us (2%)
  other arithmetic  1.24 us (1%)
  between operations  1.12 us (1%)
    ppermute x32, starting transfers between devices, swap(): lax.ppermute(x, axes, [p for a, b in pairs for p in ((a, b), (b, a))])  34.2 us
    pallas_call x22, Pallas kernels, call(): pl.pallas_call(kernel, out_shape=out_shapes, in_specs=[pl.BlockSpec(memor...  33.4 us
    ppermute x32, waiting for transfers between devices, swap(): lax.ppermute(x, axes, [p for a, b in pairs for p in ((a, b), (b, a))])  25.7 us
    unnamed x11, local copies, waits for them, and re-layouts  2.22 us
  transfers between devices with their start and end apart: 32, of which 11 were waited for; matrix products, arithmetic and copies ran while one was open for 1% of the time, Pallas kernels for 31%

profile of v15, /device:TPU:0, one launch (start us, length us, event | category | flops | bytes accessed | tf_op | source)
XLA Modules:
  0.0 98.0 jit_solution(8126750109013345195)
XLA Ops:
  1.2 1.9 %prepare.1 = (bf16[256,1024]{1,0:T(8,128)(2,1)S(1)}, bf16[512,256]{1,0:T(8,128)(2,1)S(1)}, bf16[512,256]{1,0:T(8,128)(2,1)S(1)}) custom-call(s32[3]{0:T(128)S(1)} %pad_add_fusion.place, bf16[512,1024]{1,0:T(8,128)(2,1)} %inputs.1, s32[1,512]{1,0:T(1,128)} %bitcast.18, f32[500,512]{1,0:T(8,128)} %bitcast.13), custom_call_target="tpu_custom_call" | custom-call | tf_op jit(solution)/shard_map/prepare/pallas_call | solution.py:42
  3.3 2.0 %collective-permute-done = bf16[512,256]{1,0:T(8,128)(2,1)S(1)} collective-permute-done((bf16[512,256]{1,0:T(8,128)(2,1)S(1)}, bf16[512,256]{1,0:T(8,128)(2,1)S(1)}, u32[]{:S(2)}, u32[]{:S(2)}) %collective-permute-start) | collective-permute-done | bytes 262176 | tf_op jit(solution)/shard_map/ppermute | solution.py:183
  5.3 2.9 %collective-permute-start.5 = (bf16[256,1024]{1,0:T(8,128)(2,1)S(1)}, bf16[256,1024]{1,0:T(8,128)(2,1)S(1)}, u32[]{:S(2)}, u32[]{:S(2)}) collective-permute-start(bf16[256,1024]{1,0:T(8,128)(2,1)S(1)} %get-tuple-element.48.rows), channel_id=1, source_target_pairs={{0,4},{4,0},{8,12},{12,8},{14,10},{10,14},{6,2},{2,6},{5,9},{9,5},... | collective-permute-start | bytes 1572872 | tf_op jit(solution)/shard_map/ppermute | solution.py:183
  8.4 2.2 %copy-done.2 = f32[1,512,2048]{2,1,0:T(8,128)S(1)} copy-done((f32[1,512,2048]{2,1,0:T(8,128)S(1)}, f32[1,512,2048]{2,1,0:T(8,128)}, u32[]{:S(2)}) %copy-start.2) | copy-done | bytes 4194328
  11.3 1.5 %collective-permute-start.4 = (bf16[1024,256]{1,0:T(8,128)(2,1)S(1)}, bf16[1024,256]{1,0:T(8,128)(2,1)S(1)}, u32[]{:S(2)}, u32[]{:S(2)}) collective-permute-start(bf16[1024,256]{1,0:T(8,128)(2,1)S(1)} %constant_dynamic-update-slice_fusion.refs_0_.refs_2_), channel_id=1, source_target_pairs={{0,4},{4,0},{8,12},{12,8},{14,10},{10,14},{6,2},{2,6},{5,9},{9,5},... | collective-permute-start | bytes 1572872 | tf_op jit(solution)/shard_map/ppermute | solution.py:183
  12.8 2.5 %block.5 = (bf16[128,1024]{1,0:T(8,128)(2,1)S(1)}, bf16[128,512]{1,0:T(8,128)(2,1)S(1)}) custom-call(s32[3]{0:T(128)S(1)} %pad_add_fusion.place, bf16[256,1024]{1,0:T(8,128)(2,1)S(1)} %get-tuple-element.48.rows, bf16[1024,1024]{1,0:T(8,128)(2,1)S(1)} %copy-done, bf16[1024,1024]{1,0:T(8,128)(2,1)S(1)} %collective-permute-done.1.w_other, ...), custom_call_target="tpu_custom_call" | custom-call | tf_op jit(solution)/shard_map/block/pallas_call | solution.py:42
  15.4 3.6 %block.6 = (bf16[256,1024]{1,0:T(8,128)(2,1)S(1)}, bf16[256,512]{1,0:T(8,128)(2,1)S(1)}) custom-call(s32[3]{0:T(128)S(1)} %pad_add_fusion.place, bf16[256,1024]{1,0:T(8,128)(2,1)S(1)} %collective-permute-done.5.rows, bf16[1024,1024]{1,0:T(8,128)(2,1)S(1)} %copy-done, bf16[1024,1024]{1,0:T(8,128)(2,1)S(1)} %collective-permute-done.1.w_other, ...), custom_call_target="tpu_custom_call" | custom-call | tf_op jit(solution)/shard_map/block/pallas_call | solution.py:42
  19.4 1.8 %collective-permute-start.9 = (bf16[256,1024]{1,0:T(8,128)(2,1)S(1)}, bf16[256,1024]{1,0:T(8,128)(2,1)S(1)}, u32[]{:S(2)}, u32[]{:S(2)}) collective-permute-start(bf16[256,1024]{1,0:T(8,128)(2,1)S(1)} %collective-permute-done.5.rows), channel_id=1, source_target_pairs={{4,8},{8,4},{12,14},{14,12},{10,6},{6,10},{2,0},{0,2},{1,5},{5,1},... | collective-permute-start | bytes 1572872 | tf_op jit(solution)/shard_map/ppermute | solution.py:183
  21.9 1.6 %collective-permute-start.8 = (bf16[1024,256]{1,0:T(8,128)(2,1)S(1)}, bf16[1024,256]{1,0:T(8,128)(2,1)S(1)}, u32[]{:S(2)}, u32[]{:S(2)}) collective-permute-start(bf16[1024,256]{1,0:T(8,128)(2,1)S(1)} %collective-permute-done.4.refs_4_), channel_id=1, source_target_pairs={{4,8},{8,4},{12,14},{14,12},{10,6},{6,10},{2,0},{0,2},{1,5},{5,1},... | collective-permute-start | bytes 1572872 | tf_op jit(solution)/shard_map/ppermute | solution.py:183
  23.6 1.5 %begin.3.refs_0_ = f32[512,512]{1,0:T(8,128)S(1)} custom-call(s32[3]{0:T(128)S(1)} %pad_add_fusion.place, bf16[1024,256]{1,0:T(8,128)(2,1)S(1)} %constant_dynamic-update-slice_fusion.refs_0_.refs_2_, bf16[128,1024]{1,0:T(8,128)(2,1)S(1)} %get-tuple-element.49.refs_1_, bf16[1024,256]{1,0:T(8,128)(2,1)S(1)} %constant_dynamic-update-slice_fusion.refs_0_.refs_2_, ...), custom_call_target="tpu_custom_call" | custom-call | tf_op jit(solution)/shard_map/begin/pallas_call | solution.py:42
  25.1 3.4 %collective-permute-done.9.rows = bf16[256,1024]{1,0:T(8,128)(2,1)S(1)} collective-permute-done((bf16[256,1024]{1,0:T(8,128)(2,1)S(1)}, bf16[256,1024]{1,0:T(8,128)(2,1)S(1)}, u32[]{:S(2)}, u32[]{:S(2)}) %collective-permute-start.9) | collective-permute-done | bytes 524320 | tf_op jit(solution)/shard_map/ppermute | solution.py:183
  28.5 3.6 %block.7 = (bf16[256,1024]{1,0:T(8,128)(2,1)S(1)}, bf16[256,512]{1,0:T(8,128)(2,1)S(1)}) custom-call(s32[3]{0:T(128)S(1)} %pad_add_fusion.place, bf16[256,1024]{1,0:T(8,128)(2,1)S(1)} %collective-permute-done.9.rows, bf16[1024,1024]{1,0:T(8,128)(2,1)S(1)} %copy-done, bf16[1024,1024]{1,0:T(8,128)(2,1)S(1)} %collective-permute-done.1.w_other, ...), custom_call_target="tpu_custom_call" | custom-call | tf_op jit(solution)/shard_map/block/pallas_call | solution.py:42
  32.2 1.9 %collective-permute-start.14 = (bf16[256,1024]{1,0:T(8,128)(2,1)S(1)}, bf16[256,1024]{1,0:T(8,128)(2,1)S(1)}, u32[]{:S(2)}, u32[]{:S(2)}) collective-permute-start(bf16[256,1024]{1,0:T(8,128)(2,1)S(1)} %collective-permute-done.9.rows), channel_id=1, source_target_pairs={{0,4},{4,0},{8,12},{12,8},{14,10},{10,14},{6,2},{2,6},{5,9},{9,5},... | collective-permute-start | bytes 1572872 | tf_op jit(solution)/shard_map/ppermute | solution.py:183
  34.3 1.8 %collective-permute-start.13 = (bf16[1024,256]{1,0:T(8,128)(2,1)S(1)}, bf16[1024,256]{1,0:T(8,128)(2,1)S(1)}, u32[]{:S(2)}, u32[]{:S(2)}) collective-permute-start(bf16[1024,256]{1,0:T(8,128)(2,1)S(1)} %collective-permute-done.8.refs_1_), channel_id=1, source_target_pairs={{0,4},{4,0},{8,12},{12,8},{14,10},{10,14},{6,2},{2,6},{5,9},{9,5},... | collective-permute-start | bytes 1572872 | tf_op jit(solution)/shard_map/ppermute | solution.py:183
  37.4 4.0 %collective-permute-done.14.rows = bf16[256,1024]{1,0:T(8,128)(2,1)S(1)} collective-permute-done((bf16[256,1024]{1,0:T(8,128)(2,1)S(1)}, bf16[256,1024]{1,0:T(8,128)(2,1)S(1)}, u32[]{:S(2)}, u32[]{:S(2)}) %collective-permute-start.14) | collective-permute-done | bytes 524320 | tf_op jit(solution)/shard_map/ppermute | solution.py:183
  41.5 3.8 %block.8 = (bf16[256,1024]{1,0:T(8,128)(2,1)S(1)}, bf16[256,512]{1,0:T(8,128)(2,1)S(1)}) custom-call(s32[3]{0:T(128)S(1)} %pad_add_fusion.place, bf16[256,1024]{1,0:T(8,128)(2,1)S(1)} %collective-permute-done.14.rows, bf16[1024,1024]{1,0:T(8,128)(2,1)S(1)} %copy-done, bf16[1024,1024]{1,0:T(8,128)(2,1)S(1)} %collective-permute-done.1.w_other, ...), custom_call_target="tpu_custom_call" | custom-call | tf_op jit(solution)/shard_map/block/pallas_call | solution.py:42
  45.4 1.8 %collective-permute-start.17 = (bf16[128,1024]{1,0:T(8,128)(2,1)S(1)}, bf16[128,1024]{1,0:T(8,128)(2,1)S(1)}, u32[]{:S(2)}, u32[]{:S(2)}) collective-permute-start(bf16[128,1024]{1,0:T(8,128)(2,1)S(1)} %slice.24), channel_id=1, source_target_pairs={{4,8},{8,4},{12,14},{14,12},{10,6},{6,10},{2,0},{0,2},{1,5},{5,1},... | collective-permute-start | bytes 786440 | tf_op jit(solution)/shard_map/ppermute | solution.py:183
  47.3 1.8 %collective-permute-start.19 = (bf16[1024,128]{1,0:T(8,128)(2,1)S(1)}, bf16[1024,128]{1,0:T(8,128)(2,1)S(1)}, u32[]{:S(2)}, u32[]{:S(2)}) collective-permute-start(bf16[1024,128]{1,0:T(8,128)(2,1)S(1)} %slice.25), channel_id=1, source_target_pairs={{4,8},{8,4},{12,14},{14,12},{10,6},{6,10},{2,0},{0,2},{1,5},{5,1},... | collective-permute-start | bytes 786440 | tf_op jit(solution)/shard_map/ppermute | solution.py:183
  49.2 2.6 %collective-permute-done.17.rows = bf16[128,1024]{1,0:T(8,128)(2,1)S(1)} collective-permute-done((bf16[128,1024]{1,0:T(8,128)(2,1)S(1)}, bf16[128,1024]{1,0:T(8,128)(2,1)S(1)}, u32[]{:S(2)}, u32[]{:S(2)}) %collective-permute-start.17) | collective-permute-done | bytes 262176 | tf_op jit(solution)/shard_map/ppermute | solution.py:183
  51.8 2.5 %block.9 = (bf16[128,1024]{1,0:T(8,128)(2,1)S(1)}, bf16[128,512]{1,0:T(8,128)(2,1)S(1)}) custom-call(s32[3]{0:T(128)S(1)} %pad_add_fusion.place, bf16[128,1024]{1,0:T(8,128)(2,1)S(1)} %collective-permute-done.17.rows, bf16[1024,1024]{1,0:T(8,128)(2,1)S(1)} %copy-done, bf16[1024,1024]{1,0:T(8,128)(2,1)S(1)} %collective-permute-done.1.w_other, ...), custom_call_target="tpu_custom_call" | custom-call | tf_op jit(solution)/shard_map/block/pallas_call | solution.py:42
  58.7 1.8 %collective-permute-start.22 = (bf16[512,256]{1,0:T(8,128)(2,1)S(1)}, bf16[512,256]{1,0:T(8,128)(2,1)S(1)}, u32[]{:S(2)}, u32[]{:S(2)}) collective-permute-start(bf16[512,256]{1,0:T(8,128)(2,1)S(1)} %change.3), channel_id=1, source_target_pairs={{4,8},{8,4},{12,14},{14,12},{10,6},{6,10},{2,0},{0,2},{1,5},{5,1},... | collective-permute-start | bytes 786440 | tf_op jit(solution)/shard_map/ppermute | solution.py:183
  63.0 1.7 %collective-permute-start.25 = (bf16[512,256]{1,0:T(8,128)(2,1)S(1)}, bf16[512,256]{1,0:T(8,128)(2,1)S(1)}, u32[]{:S(2)}, u32[]{:S(2)}) collective-permute-start(bf16[512,256]{1,0:T(8,128)(2,1)S(1)} %get-tuple-element.78), channel_id=1, source_target_pairs={{0,4},{4,0},{8,12},{12,8},{14,10},{10,14},{6,2},{2,6},{5,9},{9,5},... | collective-permute-start | bytes 786440 | tf_op jit(solution)/shard_map/ppermute | solution.py:183
  65.8 1.9 %collective-permute-start.24 = (bf16[512,256]{1,0:T(8,128)(2,1)S(1)}, bf16[512,256]{1,0:T(8,128)(2,1)S(1)}, u32[]{:S(2)}, u32[]{:S(2)}) collective-permute-start(bf16[512,256]{1,0:T(8,128)(2,1)S(1)} %hop.5), channel_id=1, source_target_pairs={{0,4},{4,0},{8,12},{12,8},{14,10},{10,14},{6,2},{2,6},{5,9},{9,5},... | collective-permute-start | bytes 786440 | tf_op jit(solution)/shard_map/ppermute | solution.py:183
  67.7 1.8 %collective-permute-done.25.came = bf16[512,256]{1,0:T(8,128)(2,1)S(1)} collective-permute-done((bf16[512,256]{1,0:T(8,128)(2,1)S(1)}, bf16[512,256]{1,0:T(8,128)(2,1)S(1)}, u32[]{:S(2)}, u32[]{:S(2)}) %collective-permute-start.25) | collective-permute-done | bytes 262176 | tf_op jit(solution)/shard_map/ppermute | solution.py:183
  71.2 1.4 %collective-permute-done.24.came = bf16[512,256]{1,0:T(8,128)(2,1)S(1)} collective-permute-done((bf16[512,256]{1,0:T(8,128)(2,1)S(1)}, bf16[512,256]{1,0:T(8,128)(2,1)S(1)}, u32[]{:S(2)}, u32[]{:S(2)}) %collective-permute-start.24) | collective-permute-done | bytes 262176 | tf_op jit(solution)/shard_map/ppermute | solution.py:183
  73.3 2.0 %collective-permute-start.26 = (bf16[512,256]{1,0:T(8,128)(2,1)S(1)}, bf16[512,256]{1,0:T(8,128)(2,1)S(1)}, u32[]{:S(2)}, u32[]{:S(2)}) collective-permute-start(bf16[512,256]{1,0:T(8,128)(2,1)S(1)} %hop.7), channel_id=1, source_target_pairs={{4,8},{8,4},{12,14},{14,12},{10,6},{6,10},{2,0},{0,2},{1,5},{5,1},... | collective-permute-start | bytes 786440 | tf_op jit(solution)/shard_map/ppermute | solution.py:183
  77.1 1.7 %collective-permute-start.29 = (bf16[512,256]{1,0:T(8,128)(2,1)S(1)}, bf16[512,256]{1,0:T(8,128)(2,1)S(1)}, u32[]{:S(2)}, u32[]{:S(2)}) collective-permute-start(bf16[512,256]{1,0:T(8,128)(2,1)S(1)} %hop.8), channel_id=1, source_target_pairs={{0,4},{4,0},{8,12},{12,8},{14,10},{10,14},{6,2},{2,6},{5,9},{9,5},... | collective-permute-start | bytes 786440 | tf_op jit(solution)/shard_map/ppermute | solution.py:183
  78.8 2.1 %collective-permute-done.26.came = bf16[512,256]{1,0:T(8,128)(2,1)S(1)} collective-permute-done((bf16[512,256]{1,0:T(8,128)(2,1)S(1)}, bf16[512,256]{1,0:T(8,128)(2,1)S(1)}, u32[]{:S(2)}, u32[]{:S(2)}) %collective-permute-start.26) | collective-permute-done | bytes 262176 | tf_op jit(solution)/shard_map/ppermute | solution.py:183
  81.5 3.5 %collective-permute-start.28 = (bf16[512,256]{1,0:T(8,128)(2,1)S(1)}, bf16[512,256]{1,0:T(8,128)(2,1)S(1)}, u32[]{:S(2)}, u32[]{:S(2)}) collective-permute-start(bf16[512,256]{1,0:T(8,128)(2,1)S(1)} %hop.9), channel_id=1, source_target_pairs={{0,4},{4,0},{8,12},{12,8},{14,10},{10,14},{6,2},{2,6},{5,9},{9,5},... | collective-permute-start | bytes 786440 | tf_op jit(solution)/shard_map/ppermute | solution.py:183
  85.0 4.3 %collective-permute-done.28.came = bf16[512,256]{1,0:T(8,128)(2,1)S(1)} collective-permute-done((bf16[512,256]{1,0:T(8,128)(2,1)S(1)}, bf16[512,256]{1,0:T(8,128)(2,1)S(1)}, u32[]{:S(2)}, u32[]{:S(2)}) %collective-permute-start.28) | collective-permute-done | bytes 262176 | tf_op jit(solution)/shard_map/ppermute | solution.py:183
  90.0 1.7 %collective-permute-start.31 = (bf16[512,256]{1,0:T(8,128)(2,1)S(1)}, bf16[512,256]{1,0:T(8,128)(2,1)S(1)}, u32[]{:S(2)}, u32[]{:S(2)}) collective-permute-start(bf16[512,256]{1,0:T(8,128)(2,1)S(1)} %last.1.change), channel_id=1, source_target_pairs={{0,2},{2,0},{1,3},{3,1},{4,6},{6,4},{5,7},{7,5},{8,10},{10,8},{9,1... | collective-permute-start | bytes 786440 | tf_op jit(solution)/shard_map/ppermute | solution.py:183
  94.2 2.2 %collective-permute-done.31.change = bf16[512,256]{1,0:T(8,128)(2,1)S(1)} collective-permute-done((bf16[512,256]{1,0:T(8,128)(2,1)S(1)}, bf16[512,256]{1,0:T(8,128)(2,1)S(1)}, u32[]{:S(2)}, u32[]{:S(2)}) %collective-permute-start.31) | collective-permute-done | bytes 262176 | tf_op jit(solution)/shard_map/ppermute | solution.py:183
  (75 shorter events, 21.7 us)
Async XLA Ops:
  0.6 12.2 %collective-permute-start.1 = (bf16[1024,1024]{1,0:T(8,128)(2,1)}, bf16[1024,1024]{1,0:T(8,128)(2,1)S(1)}, u32[]{:S(2)}, u32[]{:S(2)}) collective-permute-start(bf16[1024,1024]{1,0:T(8,128)(2,1)} %w_own.9), channel_id=1, source_target_pairs={{0,1},{1,0},{2,3},{3,2},{4,5},{5,4},{6,7},{7,6},{8,9},{9,8},{10,11... | collective-permute-start | bytes 6291464 | tf_op jit(solution)/shard_map/ppermute | solution.py:183
  3.2 2.2 %collective-permute-start = (bf16[512,256]{1,0:T(8,128)(2,1)S(1)}, bf16[512,256]{1,0:T(8,128)(2,1)S(1)}, u32[]{:S(2)}, u32[]{:S(2)}) collective-permute-start(bf16[512,256]{1,0:T(8,128)(2,1)S(1)} %get-tuple-element.46), channel_id=1, source_target_pairs={{0,1},{1,0},{2,3},{3,2},{4,5},{5,4},{6,7},{7,6},{8,9},{9,8},{10,11... | collective-permute-start | bytes 786440 | tf_op jit(solution)/shard_map/ppermute | solution.py:183
  5.3 10.1 %collective-permute-start.5 = (bf16[256,1024]{1,0:T(8,128)(2,1)S(1)}, bf16[256,1024]{1,0:T(8,128)(2,1)S(1)}, u32[]{:S(2)}, u32[]{:S(2)}) collective-permute-start(bf16[256,1024]{1,0:T(8,128)(2,1)S(1)} %get-tuple-element.48.rows), channel_id=1, source_target_pairs={{0,4},{4,0},{8,12},{12,8},{14,10},{10,14},{6,2},{2,6},{5,9},{9,5},... | collective-permute-start | bytes 1572872 | tf_op jit(solution)/shard_map/ppermute | solution.py:183
  8.3 4.6 %collective-permute-start.2 = (bf16[1,1024]{1,0:T(2,128)(2,1)S(1)}, bf16[1,1024]{1,0:T(2,128)(2,1)S(1)}, u32[]{:S(2)}, u32[]{:S(2)}) collective-permute-start(bf16[1,1024]{1,0:T(2,128)(2,1)S(1)} %broadcast_in_dim.7.p_own), channel_id=1, source_target_pairs={{0,1},{1,0},{2,3},{3,2},{4,5},{5,4},{6,7},{7,6},{8,9},{9,8},{10,11... | collective-permute-start | bytes 6152 | tf_op jit(solution)/shard_map/ppermute | solution.py:183
  11.3 10.0 %collective-permute-start.4 = (bf16[1024,256]{1,0:T(8,128)(2,1)S(1)}, bf16[1024,256]{1,0:T(8,128)(2,1)S(1)}, u32[]{:S(2)}, u32[]{:S(2)}) collective-permute-start(bf16[1024,256]{1,0:T(8,128)(2,1)S(1)} %constant_dynamic-update-slice_fusion.refs_0_.refs_2_), channel_id=1, source_target_pairs={{0,4},{4,0},{8,12},{12,8},{14,10},{10,14},{6,2},{2,6},{5,9},{9,5},... | collective-permute-start | bytes 1572872 | tf_op jit(solution)/shard_map/ppermute | solution.py:183
  19.0 2.3 %collective-permute-start.6 = (bf16[256,1024]{1,0:T(8,128)(2,1)S(1)}, bf16[256,1024]{1,0:T(8,128)(2,1)S(1)}, u32[]{:S(2)}, u32[]{:S(2)}) collective-permute-start(bf16[256,1024]{1,0:T(8,128)(2,1)S(1)} %get-tuple-element.51.refs_5_), channel_id=1, source_target_pairs={{0,1},{1,0},{2,3},{3,2},{4,5},{5,4},{6,7},{7,6},{8,9},{9,8},{10,11... | collective-permute-start | bytes 1572872 | tf_op jit(solution)/shard_map/ppermute | solution.py:183
  19.4 9.2 %collective-permute-start.9 = (bf16[256,1024]{1,0:T(8,128)(2,1)S(1)}, bf16[256,1024]{1,0:T(8,128)(2,1)S(1)}, u32[]{:S(2)}, u32[]{:S(2)}) collective-permute-start(bf16[256,1024]{1,0:T(8,128)(2,1)S(1)} %collective-permute-done.5.rows), channel_id=1, source_target_pairs={{4,8},{8,4},{12,14},{14,12},{10,6},{6,10},{2,0},{0,2},{1,5},{5,1},... | collective-permute-start | bytes 1572872 | tf_op jit(solution)/shard_map/ppermute | solution.py:183
  21.1 2.5 %collective-permute-start.3 = (bf16[128,1024]{1,0:T(8,128)(2,1)S(1)}, bf16[128,1024]{1,0:T(8,128)(2,1)S(1)}, u32[]{:S(2)}, u32[]{:S(2)}) collective-permute-start(bf16[128,1024]{1,0:T(8,128)(2,1)S(1)} %get-tuple-element.49.refs_1_), channel_id=1, source_target_pairs={{0,1},{1,0},{2,3},{3,2},{4,5},{5,4},{6,7},{7,6},{8,9},{9,8},{10,11... | collective-permute-start | bytes 786440 | tf_op jit(solution)/shard_map/ppermute | solution.py:183
  21.4 2.2 %collective-permute-start.7 = (bf16[512,256]{1,0:T(8,128)(2,1)S(1)}, bf16[512,256]{1,0:T(8,128)(2,1)S(1)}, u32[]{:S(2)}, u32[]{:S(2)}) collective-permute-start(bf16[512,256]{1,0:T(8,128)(2,1)S(1)} %slice.21), channel_id=1, source_target_pairs={{0,1},{1,0},{2,3},{3,2},{4,5},{5,4},{6,7},{7,6},{8,9},{9,8},{10,11... | collective-permute-start | bytes 786440 | tf_op jit(solution)/shard_map/ppermute | solution.py:183
  21.7 3.4 %collective-permute-start.10 = (bf16[128,512]{1,0:T(8,128)(2,1)S(1)}, bf16[128,512]{1,0:T(8,128)(2,1)S(1)}, u32[]{:S(2)}, u32[]{:S(2)}) collective-permute-start(bf16[128,512]{1,0:T(8,128)(2,1)S(1)} %get-tuple-element.54.refs_3_), channel_id=1, source_target_pairs={{0,1},{1,0},{2,3},{3,2},{4,5},{5,4},{6,7},{7,6},{8,9},{9,8},{10,11... | collective-permute-start | bytes 393224 | tf_op jit(solution)/shard_map/ppermute | solution.py:183
  21.9 12.2 %collective-permute-start.8 = (bf16[1024,256]{1,0:T(8,128)(2,1)S(1)}, bf16[1024,256]{1,0:T(8,128)(2,1)S(1)}, u32[]{:S(2)}, u32[]{:S(2)}) collective-permute-start(bf16[1024,256]{1,0:T(8,128)(2,1)S(1)} %collective-permute-done.4.refs_4_), channel_id=1, source_target_pairs={{4,8},{8,4},{12,14},{14,12},{10,6},{6,10},{2,0},{0,2},{1,5},{5,1},... | collective-permute-start | bytes 1572872 | tf_op jit(solution)/shard_map/ppermute | solution.py:183
  32.1 2.0 %collective-permute-start.11 = (bf16[256,1024]{1,0:T(8,128)(2,1)S(1)}, bf16[256,1024]{1,0:T(8,128)(2,1)S(1)}, u32[]{:S(2)}, u32[]{:S(2)}) collective-permute-start(bf16[256,1024]{1,0:T(8,128)(2,1)S(1)} %get-tuple-element.56.refs_2_), channel_id=1, source_target_pairs={{0,1},{1,0},{2,3},{3,2},{4,5},{5,4},{6,7},{7,6},{8,9},{9,8},{10,11... | collective-permute-start | bytes 1572872 | tf_op jit(solution)/shard_map/ppermute | solution.py:183
  32.2 9.2 %collective-permute-start.14 = (bf16[256,1024]{1,0:T(8,128)(2,1)S(1)}, bf16[256,1024]{1,0:T(8,128)(2,1)S(1)}, u32[]{:S(2)}, u32[]{:S(2)}) collective-permute-start(bf16[256,1024]{1,0:T(8,128)(2,1)S(1)} %collective-permute-done.9.rows), channel_id=1, source_target_pairs={{0,4},{4,0},{8,12},{12,8},{14,10},{10,14},{6,2},{2,6},{5,9},{9,5},... | collective-permute-start | bytes 1572872 | tf_op jit(solution)/shard_map/ppermute | solution.py:183
  34.2 2.0 %collective-permute-start.12 = (bf16[512,256]{1,0:T(8,128)(2,1)S(1)}, bf16[512,256]{1,0:T(8,128)(2,1)S(1)}, u32[]{:S(2)}, u32[]{:S(2)}) collective-permute-start(bf16[512,256]{1,0:T(8,128)(2,1)S(1)} %slice.22), channel_id=1, source_target_pairs={{0,1},{1,0},{2,3},{3,2},{4,5},{5,4},{6,7},{7,6},{8,9},{9,8},{10,11... | collective-permute-start | bytes 786440 | tf_op jit(solution)/shard_map/ppermute | solution.py:183
  34.3 12.9 %collective-permute-start.13 = (bf16[1024,256]{1,0:T(8,128)(2,1)S(1)}, bf16[1024,256]{1,0:T(8,128)(2,1)S(1)}, u32[]{:S(2)}, u32[]{:S(2)}) collective-permute-start(bf16[1024,256]{1,0:T(8,128)(2,1)S(1)} %collective-permute-done.8.refs_1_), channel_id=1, source_target_pairs={{0,4},{4,0},{8,12},{12,8},{14,10},{10,14},{6,2},{2,6},{5,9},{9,5},... | collective-permute-start | bytes 1572872 | tf_op jit(solution)/shard_map/ppermute | solution.py:183
  45.3 2.0 %collective-permute-start.15 = (bf16[256,1024]{1,0:T(8,128)(2,1)S(1)}, bf16[256,1024]{1,0:T(8,128)(2,1)S(1)}, u32[]{:S(2)}, u32[]{:S(2)}) collective-permute-start(bf16[256,1024]{1,0:T(8,128)(2,1)S(1)} %get-tuple-element.60.refs_2_), channel_id=1, source_target_pairs={{0,1},{1,0},{2,3},{3,2},{4,5},{5,4},{6,7},{7,6},{8,9},{9,8},{10,11... | collective-permute-start | bytes 1572872 | tf_op jit(solution)/shard_map/ppermute | solution.py:183
  45.4 6.4 %collective-permute-start.17 = (bf16[128,1024]{1,0:T(8,128)(2,1)S(1)}, bf16[128,1024]{1,0:T(8,128)(2,1)S(1)}, u32[]{:S(2)}, u32[]{:S(2)}) collective-permute-start(bf16[128,1024]{1,0:T(8,128)(2,1)S(1)} %slice.24), channel_id=1, source_target_pairs={{4,8},{8,4},{12,14},{14,12},{10,6},{6,10},{2,0},{0,2},{1,5},{5,1},... | collective-permute-start | bytes 786440 | tf_op jit(solution)/shard_map/ppermute | solution.py:183
  47.3 7.7 %collective-permute-start.19 = (bf16[1024,128]{1,0:T(8,128)(2,1)S(1)}, bf16[1024,128]{1,0:T(8,128)(2,1)S(1)}, u32[]{:S(2)}, u32[]{:S(2)}) collective-permute-start(bf16[1024,128]{1,0:T(8,128)(2,1)S(1)} %slice.25), channel_id=1, source_target_pairs={{4,8},{8,4},{12,14},{14,12},{10,6},{6,10},{2,0},{0,2},{1,5},{5,1},... | collective-permute-start | bytes 786440 | tf_op jit(solution)/shard_map/ppermute | solution.py:183
  49.1 6.0 %collective-permute-start.16 = (bf16[512,256]{1,0:T(8,128)(2,1)S(1)}, bf16[512,256]{1,0:T(8,128)(2,1)S(1)}, u32[]{:S(2)}, u32[]{:S(2)}) collective-permute-start(bf16[512,256]{1,0:T(8,128)(2,1)S(1)} %slice.23), channel_id=1, source_target_pairs={{0,1},{1,0},{2,3},{3,2},{4,5},{5,4},{6,7},{7,6},{8,9},{9,8},{10,11... | collective-permute-start | bytes 786440 | tf_op jit(solution)/shard_map/ppermute | solution.py:183
  54.4 2.0 %collective-permute-start.21 = (bf16[128,1024]{1,0:T(8,128)(2,1)S(1)}, bf16[128,1024]{1,0:T(8,128)(2,1)S(1)}, u32[]{:S(2)}, u32[]{:S(2)}) collective-permute-start(bf16[128,1024]{1,0:T(8,128)(2,1)S(1)} %get-tuple-element.65.refs_1_), channel_id=1, source_target_pairs={{0,1},{1,0},{2,3},{3,2},{4,5},{5,4},{6,7},{7,6},{8,9},{9,8},{10,11... | collective-permute-start | bytes 786440 | tf_op jit(solution)/shard_map/ppermute | solution.py:183
  54.4 1.9 %collective-permute-start.18 = (bf16[128,512]{1,0:T(8,128)(2,1)S(1)}, bf16[128,512]{1,0:T(8,128)(2,1)S(1)}, u32[]{:S(2)}, u32[]{:S(2)}) collective-permute-start(bf16[128,512]{1,0:T(8,128)(2,1)S(1)} %get-tuple-element.63.refs_0_), channel_id=1, source_target_pairs={{0,1},{1,0},{2,3},{3,2},{4,5},{5,4},{6,7},{7,6},{8,9},{9,8},{10,11... | collective-permute-start | bytes 393224 | tf_op jit(solution)/shard_map/ppermute | solution.py:183
  54.9 1.4 %collective-permute-start.20 = (bf16[512,128]{1,0:T(8,128)(2,1)S(1)}, bf16[512,128]{1,0:T(8,128)(2,1)S(1)}, u32[]{:S(2)}, u32[]{:S(2)}) collective-permute-start(bf16[512,128]{1,0:T(8,128)(2,1)S(1)} %slice.28), channel_id=1, source_target_pairs={{0,1},{1,0},{2,3},{3,2},{4,5},{5,4},{6,7},{7,6},{8,9},{9,8},{10,11... | collective-permute-start | bytes 393224 | tf_op jit(solution)/shard_map/ppermute | solution.py:183
  57.4 4.5 %collective-permute-start.23 = (bf16[512,512]{1,0:T(8,128)(2,1)S(1)}, bf16[512,512]{1,0:T(8,128)(2,1)S(1)}, u32[]{:S(2)}, u32[]{:S(2)}) collective-permute-start(bf16[512,512]{1,0:T(8,128)(2,1)S(1)} %get-tuple-element.68.sent), channel_id=1, source_target_pairs={{0,1},{1,0},{2,3},{3,2},{4,5},{5,4},{6,7},{7,6},{8,9},{9,8},{10,11... | collective-permute-start | bytes 1572872 | tf_op jit(solution)/shard_map/ppermute | solution.py:183
  58.7 6.4 %collective-permute-start.22 = (bf16[512,256]{1,0:T(8,128)(2,1)S(1)}, bf16[512,256]{1,0:T(8,128)(2,1)S(1)}, u32[]{:S(2)}, u32[]{:S(2)}) collective-permute-start(bf16[512,256]{1,0:T(8,128)(2,1)S(1)} %change.3), channel_id=1, source_target_pairs={{4,8},{8,4},{12,14},{14,12},{10,6},{6,10},{2,0},{0,2},{1,5},{5,1},... | collective-permute-start | bytes 786440 | tf_op jit(solution)/shard_map/ppermute | solution.py:183
  63.0 6.4 %collective-permute-start.25 = (bf16[512,256]{1,0:T(8,128)(2,1)S(1)}, bf16[512,256]{1,0:T(8,128)(2,1)S(1)}, u32[]{:S(2)}, u32[]{:S(2)}) collective-permute-start(bf16[512,256]{1,0:T(8,128)(2,1)S(1)} %get-tuple-element.78), channel_id=1, source_target_pairs={{0,4},{4,0},{8,12},{12,8},{14,10},{10,14},{6,2},{2,6},{5,9},{9,5},... | collective-permute-start | bytes 786440 | tf_op jit(solution)/shard_map/ppermute | solution.py:183
  65.8 6.9 %collective-permute-start.24 = (bf16[512,256]{1,0:T(8,128)(2,1)S(1)}, bf16[512,256]{1,0:T(8,128)(2,1)S(1)}, u32[]{:S(2)}, u32[]{:S(2)}) collective-permute-start(bf16[512,256]{1,0:T(8,128)(2,1)S(1)} %hop.5), channel_id=1, source_target_pairs={{0,4},{4,0},{8,12},{12,8},{14,10},{10,14},{6,2},{2,6},{5,9},{9,5},... | collective-permute-start | bytes 786440 | tf_op jit(solution)/shard_map/ppermute | solution.py:183
  70.0 6.4 %collective-permute-start.27 = (bf16[512,256]{1,0:T(8,128)(2,1)S(1)}, bf16[512,256]{1,0:T(8,128)(2,1)S(1)}, u32[]{:S(2)}, u32[]{:S(2)}) collective-permute-start(bf16[512,256]{1,0:T(8,128)(2,1)S(1)} %hop.6), channel_id=1, source_target_pairs={{4,8},{8,4},{12,14},{14,12},{10,6},{6,10},{2,0},{0,2},{1,5},{5,1},... | collective-permute-start | bytes 786440 | tf_op jit(solution)/shard_map/ppermute | solution.py:183
  73.3 7.7 %collective-permute-start.26 = (bf16[512,256]{1,0:T(8,128)(2,1)S(1)}, bf16[512,256]{1,0:T(8,128)(2,1)S(1)}, u32[]{:S(2)}, u32[]{:S(2)}) collective-permute-start(bf16[512,256]{1,0:T(8,128)(2,1)S(1)} %hop.7), channel_id=1, source_target_pairs={{4,8},{8,4},{12,14},{14,12},{10,6},{6,10},{2,0},{0,2},{1,5},{5,1},... | collective-permute-start | bytes 786440 | tf_op jit(solution)/shard_map/ppermute | solution.py:183
  77.1 8.0 %collective-permute-start.29 = (bf16[512,256]{1,0:T(8,128)(2,1)S(1)}, bf16[512,256]{1,0:T(8,128)(2,1)S(1)}, u32[]{:S(2)}, u32[]{:S(2)}) collective-permute-start(bf16[512,256]{1,0:T(8,128)(2,1)S(1)} %hop.8), channel_id=1, source_target_pairs={{0,4},{4,0},{8,12},{12,8},{14,10},{10,14},{6,2},{2,6},{5,9},{9,5},... | collective-permute-start | bytes 786440 | tf_op jit(solution)/shard_map/ppermute | solution.py:183
  81.5 7.8 %collective-permute-start.28 = (bf16[512,256]{1,0:T(8,128)(2,1)S(1)}, bf16[512,256]{1,0:T(8,128)(2,1)S(1)}, u32[]{:S(2)}, u32[]{:S(2)}) collective-permute-start(bf16[512,256]{1,0:T(8,128)(2,1)S(1)} %hop.9), channel_id=1, source_target_pairs={{0,4},{4,0},{8,12},{12,8},{14,10},{10,14},{6,2},{2,6},{5,9},{9,5},... | collective-permute-start | bytes 786440 | tf_op jit(solution)/shard_map/ppermute | solution.py:183
  85.0 4.4 %collective-permute-start.30 = (bf16[512,256]{1,0:T(8,128)(2,1)S(1)}, bf16[512,256]{1,0:T(8,128)(2,1)S(1)}, u32[]{:S(2)}, u32[]{:S(2)}) collective-permute-start(bf16[512,256]{1,0:T(8,128)(2,1)S(1)} %collective-permute-done.29), channel_id=1, source_target_pairs={{0,1},{1,0},{2,3},{3,2},{4,5},{5,4},{6,7},{7,6},{8,9},{9,8},{10,11... | collective-permute-start | bytes 786440 | tf_op jit(solution)/shard_map/ppermute | solution.py:183
  90.0 6.4 %collective-permute-start.31 = (bf16[512,256]{1,0:T(8,128)(2,1)S(1)}, bf16[512,256]{1,0:T(8,128)(2,1)S(1)}, u32[]{:S(2)}, u32[]{:S(2)}) collective-permute-start(bf16[512,256]{1,0:T(8,128)(2,1)S(1)} %last.1.change), channel_id=1, source_target_pairs={{0,2},{2,0},{1,3},{3,1},{4,6},{6,4},{5,7},{7,5},{8,10},{10,8},{9,1... | collective-permute-start | bytes 786440 | tf_op jit(solution)/shard_map/ppermute | solution.py:183
  (5 other events, 45.1 us)

commit v16 on v14

--- a/solution.py
+++ b/solution.py
@@ -114,6 +114,20 @@
     own_slice[...] = feats[:, lanes(place[0], depth)]
 
 
+def features_kernel(place, rows, w_own, w_other, p_own, p_other, feats, own_slice):
+    half = w_own.shape[1]
+    for i, (weights, phases) in enumerate(((w_own, p_own), (w_other, p_other))):
+        for k in range(0, half, TILE):
+            at = pl.ds(pl.multiple_of((place[2] ^ i) * half + k, TILE), TILE)
+            feats[:, at] = cosine(dot(rows[...], weights[:, k:k + TILE]), phases[:, k:k + TILE]).astype(BF16)
+    own_slice[...] = feats[:, lanes(place[0], own_slice.shape[1])]
+
+
+def meet_kernel(place, feats, inverse, out):
+    depth = inverse.shape[0]
+    out[:, :depth], out[:, depth:] = high_low(dot_nt(feats[...], inverse[...]))
+
+
 def product_of(refs, classes):
     total, short = None, None
     for residual, q in zip(refs[::2], refs[1::2]):
@@ -240,11 +254,15 @@
     theirs = lambda r: C(r[padded:])
 
     def onward(way, rows, residual, size, begun, earlier):
-        q, f = block(rows, size)
-        (rows,) = after((rows,), q)
+        feats, f = call(
+            features_kernel, (like((size, inverse.shape[1])), like((size, depth))), place,
+            (rows, *weights, *phases), "features", 14,
+        )
+        (rows,) = after((rows,), f)
         further = way(rows[:part] if way is last else rows)
+        q = call(meet_kernel, like((size, 2 * depth)), place, (feats, inverse), "meet", 14)
+        (residual,) = after((residual,), q)
         q_other = C(q)
-        (residual,) = after((residual,), q_other)
         further_residual = way(residual[:, :part] if way is last else residual)
         begun = begin([*earlier, (residual, q), (theirs(residual), q_other)], *begun)
         return q, f, further, further_residual, begun
@@ -252,10 +270,13 @@
     last = lambda x: T(x)
     q0_other, f0_other = C(q0), C(f0)
     q1, f1, x2, r2, begun = onward(T, x1, r1, 2 * part, (), [(r0, q0), (r0, q0_other)])
-    (x2,) = after((x2,), begun, f0_other)
+    (x2,) = after((x2,), q1, f0_other)
+    (r2,) = after((r2,), begun)
     q2, f2, x3, r3, begun = onward(S, x2, r2, 2 * part, (begun,), [])
-    (x3,) = after((x3,), begun)
+    (x3,) = after((x3,), q2)
+    (r3,) = after((r3,), begun)
     q3, f3, x4, r4, begun = onward(last, x3, r3, 2 * part, (begun,), [])
+    (x4,) = after((x4,), q3)
     q4, f4 = block(x4, part)
     f4_other = C(f4)
     (begun,) = after((begun,), f4_other)

time: 98.7 us -> 98.2 us (level)
  starting transfers between devices: 35.2 us -> 31.7 us
  Pallas kernels: 32.4 us -> 34.7 us
    ppermute x32, starting transfers between devices: 35.2 us -> 31.7 us  [swap(): lax.ppermute(x, axes, [p for a, b in pairs for p in ((a, b), (b, a))])]
    pallas_call x22 -> x25, Pallas kernels: 32.4 us -> 34.7 us  [call(): pl.pallas_call(kernel, out_shape=out_shapes, in_specs=[pl.BlockSpec(memor...]
  transfers between devices with their start and end apart: 32 -> 32, of which waited for: 14 -> 14; matrix products, arithmetic and copies ran while one was open for 1% -> 1% of each run, Pallas kernels for 30% -> 33%
where the time goes in v16:
time: 98.2 us; the launch traced here: 96.8 us
  Pallas kernels  34.7 us (35%)
  starting transfers between devices  31.7 us (32%)
  waiting for transfers between devices  24.8 us (25%)
  local copies, waits for them, and re-layouts  3.16 us (3%)
  other arithmetic  1.24 us (1%)
  between operations  1.21 us (1%)
    pallas_call x25, Pallas kernels, call(): pl.pallas_call(kernel, out_shape=out_shapes, in_specs=[pl.BlockSpec(memor...  34.7 us
    ppermute x32, starting transfers between devices, swap(): lax.ppermute(x, axes, [p for a, b in pairs for p in ((a, b), (b, a))])  31.7 us
    ppermute x32, waiting for transfers between devices, swap(): lax.ppermute(x, axes, [p for a, b in pairs for p in ((a, b), (b, a))])  24.8 us
    unnamed x11, local copies, waits for them, and re-layouts  3.04 us
  transfers between devices with their start and end apart: 32, of which 14 were waited for; matrix products, arithmetic and copies ran while one was open for 1% of the time, Pallas kernels for 33%

profile of v16, /device:TPU:0, one launch (start us, length us, event | category | flops | bytes accessed | tf_op | source)
XLA Modules:
  0.0 96.8 jit_solution(16480671012779238943)
XLA Ops:
  1.2 1.9 %prepare.1 = (bf16[256,1024]{1,0:T(8,128)(2,1)S(1)}, bf16[512,256]{1,0:T(8,128)(2,1)S(1)}, bf16[512,256]{1,0:T(8,128)(2,1)S(1)}) custom-call(s32[3]{0:T(128)S(1)} %pad_add_fusion.place, bf16[512,1024]{1,0:T(8,128)(2,1)} %inputs.1, s32[1,512]{1,0:T(1,128)} %bitcast.18, f32[500,512]{1,0:T(8,128)} %bitcast.13), custom_call_target="tpu_custom_call" | custom-call | tf_op jit(solution)/shard_map/prepare/pallas_call | solution.py:42
  3.3 2.0 %collective-permute-done = bf16[512,256]{1,0:T(8,128)(2,1)S(1)} collective-permute-done((bf16[512,256]{1,0:T(8,128)(2,1)S(1)}, bf16[512,256]{1,0:T(8,128)(2,1)S(1)}, u32[]{:S(2)}, u32[]{:S(2)}) %collective-permute-start) | collective-permute-done | bytes 262176 | tf_op jit(solution)/shard_map/ppermute | solution.py:197
  5.3 2.9 %collective-permute-start.5 = (bf16[256,1024]{1,0:T(8,128)(2,1)S(1)}, bf16[256,1024]{1,0:T(8,128)(2,1)S(1)}, u32[]{:S(2)}, u32[]{:S(2)}) collective-permute-start(bf16[256,1024]{1,0:T(8,128)(2,1)S(1)} %get-tuple-element.51.rows), channel_id=1, source_target_pairs={{0,4},{4,0},{8,12},{12,8},{14,10},{10,14},{6,2},{2,6},{5,9},{9,5},... | collective-permute-start | bytes 1572872 | tf_op jit(solution)/shard_map/ppermute | solution.py:197
  8.5 2.2 %copy-done.2 = f32[1,512,2048]{2,1,0:T(8,128)S(1)} copy-done((f32[1,512,2048]{2,1,0:T(8,128)S(1)}, f32[1,512,2048]{2,1,0:T(8,128)}, u32[]{:S(2)}) %copy-start.2) | copy-done | bytes 4194328
  12.3 2.4 %block.2 = (bf16[128,1024]{1,0:T(8,128)(2,1)S(1)}, bf16[128,512]{1,0:T(8,128)(2,1)S(1)}) custom-call(s32[3]{0:T(128)S(1)} %pad_add_fusion.place, bf16[256,1024]{1,0:T(8,128)(2,1)S(1)} %get-tuple-element.51.rows, bf16[1024,1024]{1,0:T(8,128)(2,1)S(1)} %copy-done, bf16[1024,1024]{1,0:T(8,128)(2,1)S(1)} %collective-permute-done.1.w_other, ...), custom_call_target="tpu_custom_call" | custom-call | tf_op jit(solution)/shard_map/block/pallas_call | solution.py:42
  15.4 2.8 %features.3 = (bf16[256,2048]{1,0:T(8,128)(2,1)S(1)}, bf16[256,512]{1,0:T(8,128)(2,1)S(1)}) custom-call(s32[3]{0:T(128)S(1)} %pad_add_fusion.place, bf16[256,1024]{1,0:T(8,128)(2,1)S(1)} %collective-permute-done.5.rows, bf16[1024,1024]{1,0:T(8,128)(2,1)S(1)} %copy-done, bf16[1024,1024]{1,0:T(8,128)(2,1)S(1)} %collective-permute-done.1.w_other, ...), custom_call_target="tpu_custom_call" | custom-call | tf_op jit(solution)/shard_map/features/pallas_call | solution.py:42
  18.3 2.0 %collective-permute-start.9 = (bf16[256,1024]{1,0:T(8,128)(2,1)S(1)}, bf16[256,1024]{1,0:T(8,128)(2,1)S(1)}, u32[]{:S(2)}, u32[]{:S(2)}) collective-permute-start(bf16[256,1024]{1,0:T(8,128)(2,1)S(1)} %collective-permute-done.5.rows), channel_id=1, source_target_pairs={{4,8},{8,4},{12,14},{14,12},{10,6},{6,10},{2,0},{0,2},{1,5},{5,1},... | collective-permute-start | bytes 1572872 | tf_op jit(solution)/shard_map/ppermute | solution.py:197
  21.7 1.6 %collective-permute-start.8 = (bf16[1024,256]{1,0:T(8,128)(2,1)S(1)}, bf16[1024,256]{1,0:T(8,128)(2,1)S(1)}, u32[]{:S(2)}, u32[]{:S(2)}) collective-permute-start(bf16[1024,256]{1,0:T(8,128)(2,1)S(1)} %collective-permute-done.4.refs_4_), channel_id=1, source_target_pairs={{4,8},{8,4},{12,14},{14,12},{10,6},{6,10},{2,0},{0,2},{1,5},{5,1},... | collective-permute-start | bytes 1572872 | tf_op jit(solution)/shard_map/ppermute | solution.py:197
  24.9 2.6 %collective-permute-done.9.rows = bf16[256,1024]{1,0:T(8,128)(2,1)S(1)} collective-permute-done((bf16[256,1024]{1,0:T(8,128)(2,1)S(1)}, bf16[256,1024]{1,0:T(8,128)(2,1)S(1)}, u32[]{:S(2)}, u32[]{:S(2)}) %collective-permute-start.9) | collective-permute-done | bytes 524320 | tf_op jit(solution)/shard_map/ppermute | solution.py:197
  27.5 2.8 %features.4 = (bf16[256,2048]{1,0:T(8,128)(2,1)S(1)}, bf16[256,512]{1,0:T(8,128)(2,1)S(1)}) custom-call(s32[3]{0:T(128)S(1)} %pad_add_fusion.place, bf16[256,1024]{1,0:T(8,128)(2,1)S(1)} %collective-permute-done.9.rows, bf16[1024,1024]{1,0:T(8,128)(2,1)S(1)} %copy-done, bf16[1024,1024]{1,0:T(8,128)(2,1)S(1)} %collective-permute-done.1.w_other, ...), custom_call_target="tpu_custom_call" | custom-call | tf_op jit(solution)/shard_map/features/pallas_call | solution.py:42
  30.4 2.1 %collective-permute-start.14 = (bf16[256,1024]{1,0:T(8,128)(2,1)S(1)}, bf16[256,1024]{1,0:T(8,128)(2,1)S(1)}, u32[]{:S(2)}, u32[]{:S(2)}) collective-permute-start(bf16[256,1024]{1,0:T(8,128)(2,1)S(1)} %collective-permute-done.9.rows), channel_id=1, source_target_pairs={{0,4},{4,0},{8,12},{12,8},{14,10},{10,14},{6,2},{2,6},{5,9},{9,5},... | collective-permute-start | bytes 1572872 | tf_op jit(solution)/shard_map/ppermute | solution.py:197
  33.8 1.5 %begin.3.refs_0_ = f32[512,512]{1,0:T(8,128)S(1)} custom-call(s32[3]{0:T(128)S(1)} %pad_add_fusion.place, bf16[1024,256]{1,0:T(8,128)(2,1)S(1)} %constant_dynamic-update-slice_fusion.refs_0_.refs_2_, bf16[128,1024]{1,0:T(8,128)(2,1)S(1)} %get-tuple-element.52.refs_1_, bf16[1024,256]{1,0:T(8,128)(2,1)S(1)} %constant_dynamic-update-slice_fusion.refs_0_.refs_2_, ...), custom_call_target="tpu_custom_call" | custom-call | tf_op jit(solution)/shard_map/begin/pallas_call | solution.py:42
  37.2 2.4 %collective-permute-done.14.rows = bf16[256,1024]{1,0:T(8,128)(2,1)S(1)} collective-permute-done((bf16[256,1024]{1,0:T(8,128)(2,1)S(1)}, bf16[256,1024]{1,0:T(8,128)(2,1)S(1)}, u32[]{:S(2)}, u32[]{:S(2)}) %collective-permute-start.14) | collective-permute-done | bytes 524320 | tf_op jit(solution)/shard_map/ppermute | solution.py:197
  39.6 2.8 %features.5 = (bf16[256,2048]{1,0:T(8,128)(2,1)S(1)}, bf16[256,512]{1,0:T(8,128)(2,1)S(1)}) custom-call(s32[3]{0:T(128)S(1)} %pad_add_fusion.place, bf16[256,1024]{1,0:T(8,128)(2,1)S(1)} %collective-permute-done.14.rows, bf16[1024,1024]{1,0:T(8,128)(2,1)S(1)} %copy-done, bf16[1024,1024]{1,0:T(8,128)(2,1)S(1)} %collective-permute-done.1.w_other, ...), custom_call_target="tpu_custom_call" | custom-call | tf_op jit(solution)/shard_map/features/pallas_call | solution.py:42
  42.5 1.3 %meet.5.refs_2_ = bf16[256,1024]{1,0:T(8,128)(2,1)S(1)} custom-call(s32[3]{0:T(128)S(1)} %pad_add_fusion.place, bf16[256,2048]{1,0:T(8,128)(2,1)S(1)} %get-tuple-element.67.feats, bf16[512,2048]{1,0:T(8,128)(2,1)S(1)} %round.1.inverse), custom_call_target="tpu_custom_call" | custom-call | tf_op jit(solution)/shard_map/meet/pallas_call | solution.py:42
  43.9 2.0 %collective-permute-start.17 = (bf16[128,1024]{1,0:T(8,128)(2,1)S(1)}, bf16[128,1024]{1,0:T(8,128)(2,1)S(1)}, u32[]{:S(2)}, u32[]{:S(2)}) collective-permute-start(bf16[128,1024]{1,0:T(8,128)(2,1)S(1)} %slice.24), channel_id=1, source_target_pairs={{4,8},{8,4},{12,14},{14,12},{10,6},{6,10},{2,0},{0,2},{1,5},{5,1},... | collective-permute-start | bytes 786440 | tf_op jit(solution)/shard_map/ppermute | solution.py:197
  47.6 2.7 %collective-permute-done.17.rows = bf16[128,1024]{1,0:T(8,128)(2,1)S(1)} collective-permute-done((bf16[128,1024]{1,0:T(8,128)(2,1)S(1)}, bf16[128,1024]{1,0:T(8,128)(2,1)S(1)}, u32[]{:S(2)}, u32[]{:S(2)}) %collective-permute-start.17) | collective-permute-done | bytes 262176 | tf_op jit(solution)/shard_map/ppermute | solution.py:197
  50.3 2.6 %block.3 = (bf16[128,1024]{1,0:T(8,128)(2,1)S(1)}, bf16[128,512]{1,0:T(8,128)(2,1)S(1)}) custom-call(s32[3]{0:T(128)S(1)} %pad_add_fusion.place, bf16[128,1024]{1,0:T(8,128)(2,1)S(1)} %collective-permute-done.17.rows, bf16[1024,1024]{1,0:T(8,128)(2,1)S(1)} %copy-done, bf16[1024,1024]{1,0:T(8,128)(2,1)S(1)} %collective-permute-done.1.w_other, ...), custom_call_target="tpu_custom_call" | custom-call | tf_op jit(solution)/shard_map/block/pallas_call | solution.py:42
  57.4 1.9 %collective-permute-start.22 = (bf16[512,256]{1,0:T(8,128)(2,1)S(1)}, bf16[512,256]{1,0:T(8,128)(2,1)S(1)}, u32[]{:S(2)}, u32[]{:S(2)}) collective-permute-start(bf16[512,256]{1,0:T(8,128)(2,1)S(1)} %change.3), channel_id=1, source_target_pairs={{4,8},{8,4},{12,14},{14,12},{10,6},{6,10},{2,0},{0,2},{1,5},{5,1},... | collective-permute-start | bytes 786440 | tf_op jit(solution)/shard_map/ppermute | solution.py:197
  61.7 1.7 %collective-permute-start.25 = (bf16[512,256]{1,0:T(8,128)(2,1)S(1)}, bf16[512,256]{1,0:T(8,128)(2,1)S(1)}, u32[]{:S(2)}, u32[]{:S(2)}) collective-permute-start(bf16[512,256]{1,0:T(8,128)(2,1)S(1)} %get-tuple-element.84), channel_id=1, source_target_pairs={{0,4},{4,0},{8,12},{12,8},{14,10},{10,14},{6,2},{2,6},{5,9},{9,5},... | collective-permute-start | bytes 786440 | tf_op jit(solution)/shard_map/ppermute | solution.py:197
  64.4 2.0 %collective-permute-start.24 = (bf16[512,256]{1,0:T(8,128)(2,1)S(1)}, bf16[512,256]{1,0:T(8,128)(2,1)S(1)}, u32[]{:S(2)}, u32[]{:S(2)}) collective-permute-start(bf16[512,256]{1,0:T(8,128)(2,1)S(1)} %hop.5), channel_id=1, source_target_pairs={{0,4},{4,0},{8,12},{12,8},{14,10},{10,14},{6,2},{2,6},{5,9},{9,5},... | collective-permute-start | bytes 786440 | tf_op jit(solution)/shard_map/ppermute | solution.py:197
  66.4 1.7 %collective-permute-done.25.came = bf16[512,256]{1,0:T(8,128)(2,1)S(1)} collective-permute-done((bf16[512,256]{1,0:T(8,128)(2,1)S(1)}, bf16[512,256]{1,0:T(8,128)(2,1)S(1)}, u32[]{:S(2)}, u32[]{:S(2)}) %collective-permute-start.25) | collective-permute-done | bytes 262176 | tf_op jit(solution)/shard_map/ppermute | solution.py:197
  70.0 1.4 %collective-permute-done.24.came = bf16[512,256]{1,0:T(8,128)(2,1)S(1)} collective-permute-done((bf16[512,256]{1,0:T(8,128)(2,1)S(1)}, bf16[512,256]{1,0:T(8,128)(2,1)S(1)}, u32[]{:S(2)}, u32[]{:S(2)}) %collective-permute-start.24) | collective-permute-done | bytes 262176 | tf_op jit(solution)/shard_map/ppermute | solution.py:197
  72.0 2.0 %collective-permute-start.26 = (bf16[512,256]{1,0:T(8,128)(2,1)S(1)}, bf16[512,256]{1,0:T(8,128)(2,1)S(1)}, u32[]{:S(2)}, u32[]{:S(2)}) collective-permute-start(bf16[512,256]{1,0:T(8,128)(2,1)S(1)} %hop.7), channel_id=1, source_target_pairs={{4,8},{8,4},{12,14},{14,12},{10,6},{6,10},{2,0},{0,2},{1,5},{5,1},... | collective-permute-start | bytes 786440 | tf_op jit(solution)/shard_map/ppermute | solution.py:197
  75.8 1.7 %collective-permute-start.29 = (bf16[512,256]{1,0:T(8,128)(2,1)S(1)}, bf16[512,256]{1,0:T(8,128)(2,1)S(1)}, u32[]{:S(2)}, u32[]{:S(2)}) collective-permute-start(bf16[512,256]{1,0:T(8,128)(2,1)S(1)} %hop.8), channel_id=1, source_target_pairs={{0,4},{4,0},{8,12},{12,8},{14,10},{10,14},{6,2},{2,6},{5,9},{9,5},... | collective-permute-start | bytes 786440 | tf_op jit(solution)/shard_map/ppermute | solution.py:197
  77.6 2.1 %collective-permute-done.26.came = bf16[512,256]{1,0:T(8,128)(2,1)S(1)} collective-permute-done((bf16[512,256]{1,0:T(8,128)(2,1)S(1)}, bf16[512,256]{1,0:T(8,128)(2,1)S(1)}, u32[]{:S(2)}, u32[]{:S(2)}) %collective-permute-start.26) | collective-permute-done | bytes 262176 | tf_op jit(solution)/shard_map/ppermute | solution.py:197
  80.2 3.6 %collective-permute-start.28 = (bf16[512,256]{1,0:T(8,128)(2,1)S(1)}, bf16[512,256]{1,0:T(8,128)(2,1)S(1)}, u32[]{:S(2)}, u32[]{:S(2)}) collective-permute-start(bf16[512,256]{1,0:T(8,128)(2,1)S(1)} %hop.9), channel_id=1, source_target_pairs={{0,4},{4,0},{8,12},{12,8},{14,10},{10,14},{6,2},{2,6},{5,9},{9,5},... | collective-permute-start | bytes 786440 | tf_op jit(solution)/shard_map/ppermute | solution.py:197
  83.8 4.3 %collective-permute-done.28.came = bf16[512,256]{1,0:T(8,128)(2,1)S(1)} collective-permute-done((bf16[512,256]{1,0:T(8,128)(2,1)S(1)}, bf16[512,256]{1,0:T(8,128)(2,1)S(1)}, u32[]{:S(2)}, u32[]{:S(2)}) %collective-permute-start.28) | collective-permute-done | bytes 262176 | tf_op jit(solution)/shard_map/ppermute | solution.py:197
  88.8 1.7 %collective-permute-start.31 = (bf16[512,256]{1,0:T(8,128)(2,1)S(1)}, bf16[512,256]{1,0:T(8,128)(2,1)S(1)}, u32[]{:S(2)}, u32[]{:S(2)}) collective-permute-start(bf16[512,256]{1,0:T(8,128)(2,1)S(1)} %last.1.change), channel_id=1, source_target_pairs={{0,2},{2,0},{1,3},{3,1},{4,6},{6,4},{5,7},{7,5},{8,10},{10,8},{9,1... | collective-permute-start | bytes 786440 | tf_op jit(solution)/shard_map/ppermute | solution.py:197
  91.7 1.4 %apply.2.refs_0_ = f32[500,512]{1,0:T(8,128)} custom-call(s32[3]{0:T(128)S(1)} %pad_add_fusion.place, f32[500,512]{1,0:T(8,128)S(1)} %bitcast.14, bf16[512,256]{1,0:T(8,128)(2,1)S(1)} %last.1.change), custom_call_target="tpu_custom_call" | custom-call | tf_op jit(solution)/shard_map/apply/pallas_call | solution.py:42
  93.0 2.2 %collective-permute-done.31.change = bf16[512,256]{1,0:T(8,128)(2,1)S(1)} collective-permute-done((bf16[512,256]{1,0:T(8,128)(2,1)S(1)}, bf16[512,256]{1,0:T(8,128)(2,1)S(1)}, u32[]{:S(2)}, u32[]{:S(2)}) %collective-permute-start.31) | collective-permute-done | bytes 262176 | tf_op jit(solution)/shard_map/ppermute | solution.py:197
  95.3 1.4 %apply.3 = f32[500,512]{1,0:T(8,128)} custom-call(s32[3]{0:T(128)S(1)} %pad_add_fusion.place, f32[500,512]{1,0:T(8,128)S(1)} %bitcast.15, bf16[512,256]{1,0:T(8,128)(2,1)S(1)} %collective-permute-done.31.change, f32[500,512]{1,0:T(8,128)} %apply.2.refs_0_), custom_call_target="tpu_custom_call", output_to_operand_aliasing={{}: (3, {})} | custom-call | tf_op jit(solution)/shard_map/apply/pallas_call | solution.py:42
  (78 shorter events, 25.5 us)
Async XLA Ops:
  0.6 10.8 %collective-permute-start.1 = (bf16[1024,1024]{1,0:T(8,128)(2,1)}, bf16[1024,1024]{1,0:T(8,128)(2,1)S(1)}, u32[]{:S(2)}, u32[]{:S(2)}) collective-permute-start(bf16[1024,1024]{1,0:T(8,128)(2,1)} %w_own.9), channel_id=1, source_target_pairs={{0,1},{1,0},{2,3},{3,2},{4,5},{5,4},{6,7},{7,6},{8,9},{9,8},{10,11... | collective-permute-start | bytes 6291464 | tf_op jit(solution)/shard_map/ppermute | solution.py:197
  3.2 2.2 %collective-permute-start = (bf16[512,256]{1,0:T(8,128)(2,1)S(1)}, bf16[512,256]{1,0:T(8,128)(2,1)S(1)}, u32[]{:S(2)}, u32[]{:S(2)}) collective-permute-start(bf16[512,256]{1,0:T(8,128)(2,1)S(1)} %get-tuple-element.49), channel_id=1, source_target_pairs={{0,1},{1,0},{2,3},{3,2},{4,5},{5,4},{6,7},{7,6},{8,9},{9,8},{10,11... | collective-permute-start | bytes 786440 | tf_op jit(solution)/shard_map/ppermute | solution.py:197
  5.3 10.1 %collective-permute-start.5 = (bf16[256,1024]{1,0:T(8,128)(2,1)S(1)}, bf16[256,1024]{1,0:T(8,128)(2,1)S(1)}, u32[]{:S(2)}, u32[]{:S(2)}) collective-permute-start(bf16[256,1024]{1,0:T(8,128)(2,1)S(1)} %get-tuple-element.51.rows), channel_id=1, source_target_pairs={{0,4},{4,0},{8,12},{12,8},{14,10},{10,14},{6,2},{2,6},{5,9},{9,5},... | collective-permute-start | bytes 1572872 | tf_op jit(solution)/shard_map/ppermute | solution.py:197
  8.3 13.3 %collective-permute-start.4 = (bf16[1024,256]{1,0:T(8,128)(2,1)S(1)}, bf16[1024,256]{1,0:T(8,128)(2,1)S(1)}, u32[]{:S(2)}, u32[]{:S(2)}) collective-permute-start(bf16[1024,256]{1,0:T(8,128)(2,1)S(1)} %constant_dynamic-update-slice_fusion.refs_0_.refs_2_), channel_id=1, source_target_pairs={{0,4},{4,0},{8,12},{12,8},{14,10},{10,14},{6,2},{2,6},{5,9},{9,5},... | collective-permute-start | bytes 1572872 | tf_op jit(solution)/shard_map/ppermute | solution.py:197
  8.4 3.0 %collective-permute-start.2 = (bf16[1,1024]{1,0:T(2,128)(2,1)S(1)}, bf16[1,1024]{1,0:T(2,128)(2,1)S(1)}, u32[]{:S(2)}, u32[]{:S(2)}) collective-permute-start(bf16[1,1024]{1,0:T(2,128)(2,1)S(1)} %broadcast_in_dim.7.p_own), channel_id=1, source_target_pairs={{0,1},{1,0},{2,3},{3,2},{4,5},{5,4},{6,7},{7,6},{8,9},{9,8},{10,11... | collective-permute-start | bytes 6152 | tf_op jit(solution)/shard_map/ppermute | solution.py:197
  18.3 9.2 %collective-permute-start.9 = (bf16[256,1024]{1,0:T(8,128)(2,1)S(1)}, bf16[256,1024]{1,0:T(8,128)(2,1)S(1)}, u32[]{:S(2)}, u32[]{:S(2)}) collective-permute-start(bf16[256,1024]{1,0:T(8,128)(2,1)S(1)} %collective-permute-done.5.rows), channel_id=1, source_target_pairs={{4,8},{8,4},{12,14},{14,12},{10,6},{6,10},{2,0},{0,2},{1,5},{5,1},... | collective-permute-start | bytes 1572872 | tf_op jit(solution)/shard_map/ppermute | solution.py:197
  21.6 12.2 %collective-permute-start.7 = (bf16[256,1024]{1,0:T(8,128)(2,1)S(1)}, bf16[256,1024]{1,0:T(8,128)(2,1)S(1)}, u32[]{:S(2)}, u32[]{:S(2)}) collective-permute-start(bf16[256,1024]{1,0:T(8,128)(2,1)S(1)} %meet.3.refs_5_), channel_id=1, source_target_pairs={{0,1},{1,0},{2,3},{3,2},{4,5},{5,4},{6,7},{7,6},{8,9},{9,8},{10,11... | collective-permute-start | bytes 1572872 | tf_op jit(solution)/shard_map/ppermute | solution.py:197
  21.7 13.6 %collective-permute-start.8 = (bf16[1024,256]{1,0:T(8,128)(2,1)S(1)}, bf16[1024,256]{1,0:T(8,128)(2,1)S(1)}, u32[]{:S(2)}, u32[]{:S(2)}) collective-permute-start(bf16[1024,256]{1,0:T(8,128)(2,1)S(1)} %collective-permute-done.4.refs_4_), channel_id=1, source_target_pairs={{4,8},{8,4},{12,14},{14,12},{10,6},{6,10},{2,0},{0,2},{1,5},{5,1},... | collective-permute-start | bytes 1572872 | tf_op jit(solution)/shard_map/ppermute | solution.py:197
  23.2 1.3 %collective-permute-start.10 = (bf16[128,512]{1,0:T(8,128)(2,1)S(1)}, bf16[128,512]{1,0:T(8,128)(2,1)S(1)}, u32[]{:S(2)}, u32[]{:S(2)}) collective-permute-start(bf16[128,512]{1,0:T(8,128)(2,1)S(1)} %get-tuple-element.59.refs_3_), channel_id=1, source_target_pairs={{0,1},{1,0},{2,3},{3,2},{4,5},{5,4},{6,7},{7,6},{8,9},{9,8},{10,11... | collective-permute-start | bytes 393224 | tf_op jit(solution)/shard_map/ppermute | solution.py:197
  23.6 10.2 %collective-permute-start.6 = (bf16[512,256]{1,0:T(8,128)(2,1)S(1)}, bf16[512,256]{1,0:T(8,128)(2,1)S(1)}, u32[]{:S(2)}, u32[]{:S(2)}) collective-permute-start(bf16[512,256]{1,0:T(8,128)(2,1)S(1)} %slice.21), channel_id=1, source_target_pairs={{0,1},{1,0},{2,3},{3,2},{4,5},{5,4},{6,7},{7,6},{8,9},{9,8},{10,11... | collective-permute-start | bytes 786440 | tf_op jit(solution)/shard_map/ppermute | solution.py:197
  24.6 9.2 %collective-permute-start.3 = (bf16[128,1024]{1,0:T(8,128)(2,1)S(1)}, bf16[128,1024]{1,0:T(8,128)(2,1)S(1)}, u32[]{:S(2)}, u32[]{:S(2)}) collective-permute-start(bf16[128,1024]{1,0:T(8,128)(2,1)S(1)} %get-tuple-element.52.refs_1_), channel_id=1, source_target_pairs={{0,1},{1,0},{2,3},{3,2},{4,5},{5,4},{6,7},{7,6},{8,9},{9,8},{10,11... | collective-permute-start | bytes 786440 | tf_op jit(solution)/shard_map/ppermute | solution.py:197
  30.4 9.3 %collective-permute-start.14 = (bf16[256,1024]{1,0:T(8,128)(2,1)S(1)}, bf16[256,1024]{1,0:T(8,128)(2,1)S(1)}, u32[]{:S(2)}, u32[]{:S(2)}) collective-permute-start(bf16[256,1024]{1,0:T(8,128)(2,1)S(1)} %collective-permute-done.9.rows), channel_id=1, source_target_pairs={{0,4},{4,0},{8,12},{12,8},{14,10},{10,14},{6,2},{2,6},{5,9},{9,5},... | collective-permute-start | bytes 1572872 | tf_op jit(solution)/shard_map/ppermute | solution.py:197
  35.3 10.6 %collective-permute-start.12 = (bf16[256,1024]{1,0:T(8,128)(2,1)S(1)}, bf16[256,1024]{1,0:T(8,128)(2,1)S(1)}, u32[]{:S(2)}, u32[]{:S(2)}) collective-permute-start(bf16[256,1024]{1,0:T(8,128)(2,1)S(1)} %meet.4.refs_2_), channel_id=1, source_target_pairs={{0,1},{1,0},{2,3},{3,2},{4,5},{5,4},{6,7},{7,6},{8,9},{9,8},{10,11... | collective-permute-start | bytes 1572872 | tf_op jit(solution)/shard_map/ppermute | solution.py:197
  35.4 11.7 %collective-permute-start.13 = (bf16[1024,256]{1,0:T(8,128)(2,1)S(1)}, bf16[1024,256]{1,0:T(8,128)(2,1)S(1)}, u32[]{:S(2)}, u32[]{:S(2)}) collective-permute-start(bf16[1024,256]{1,0:T(8,128)(2,1)S(1)} %collective-permute-done.8.refs_1_), channel_id=1, source_target_pairs={{0,4},{4,0},{8,12},{12,8},{14,10},{10,14},{6,2},{2,6},{5,9},{9,5},... | collective-permute-start | bytes 1572872 | tf_op jit(solution)/shard_map/ppermute | solution.py:197
  36.0 9.9 %collective-permute-start.11 = (bf16[512,256]{1,0:T(8,128)(2,1)S(1)}, bf16[512,256]{1,0:T(8,128)(2,1)S(1)}, u32[]{:S(2)}, u32[]{:S(2)}) collective-permute-start(bf16[512,256]{1,0:T(8,128)(2,1)S(1)} %slice.22), channel_id=1, source_target_pairs={{0,1},{1,0},{2,3},{3,2},{4,5},{5,4},{6,7},{7,6},{8,9},{9,8},{10,11... | collective-permute-start | bytes 786440 | tf_op jit(solution)/shard_map/ppermute | solution.py:197
  43.8 9.9 %collective-permute-start.16 = (bf16[256,1024]{1,0:T(8,128)(2,1)S(1)}, bf16[256,1024]{1,0:T(8,128)(2,1)S(1)}, u32[]{:S(2)}, u32[]{:S(2)}) collective-permute-start(bf16[256,1024]{1,0:T(8,128)(2,1)S(1)} %meet.5.refs_2_), channel_id=1, source_target_pairs={{0,1},{1,0},{2,3},{3,2},{4,5},{5,4},{6,7},{7,6},{8,9},{9,8},{10,11... | collective-permute-start | bytes 1572872 | tf_op jit(solution)/shard_map/ppermute | solution.py:197
  43.9 6.4 %collective-permute-start.17 = (bf16[128,1024]{1,0:T(8,128)(2,1)S(1)}, bf16[128,1024]{1,0:T(8,128)(2,1)S(1)}, u32[]{:S(2)}, u32[]{:S(2)}) collective-permute-start(bf16[128,1024]{1,0:T(8,128)(2,1)S(1)} %slice.24), channel_id=1, source_target_pairs={{4,8},{8,4},{12,14},{14,12},{10,6},{6,10},{2,0},{0,2},{1,5},{5,1},... | collective-permute-start | bytes 786440 | tf_op jit(solution)/shard_map/ppermute | solution.py:197
  47.2 6.4 %collective-permute-start.19 = (bf16[1024,128]{1,0:T(8,128)(2,1)S(1)}, bf16[1024,128]{1,0:T(8,128)(2,1)S(1)}, u32[]{:S(2)}, u32[]{:S(2)}) collective-permute-start(bf16[1024,128]{1,0:T(8,128)(2,1)S(1)} %slice.25), channel_id=1, source_target_pairs={{4,8},{8,4},{12,14},{14,12},{10,6},{6,10},{2,0},{0,2},{1,5},{5,1},... | collective-permute-start | bytes 786440 | tf_op jit(solution)/shard_map/ppermute | solution.py:197
  47.3 6.3 %collective-permute-start.15 = (bf16[512,256]{1,0:T(8,128)(2,1)S(1)}, bf16[512,256]{1,0:T(8,128)(2,1)S(1)}, u32[]{:S(2)}, u32[]{:S(2)}) collective-permute-start(bf16[512,256]{1,0:T(8,128)(2,1)S(1)} %slice.23), channel_id=1, source_target_pairs={{0,1},{1,0},{2,3},{3,2},{4,5},{5,4},{6,7},{7,6},{8,9},{9,8},{10,11... | collective-permute-start | bytes 786440 | tf_op jit(solution)/shard_map/ppermute | solution.py:197
  52.9 2.1 %collective-permute-start.21 = (bf16[128,1024]{1,0:T(8,128)(2,1)S(1)}, bf16[128,1024]{1,0:T(8,128)(2,1)S(1)}, u32[]{:S(2)}, u32[]{:S(2)}) collective-permute-start(bf16[128,1024]{1,0:T(8,128)(2,1)S(1)} %get-tuple-element.74.refs_1_), channel_id=1, source_target_pairs={{0,1},{1,0},{2,3},{3,2},{4,5},{5,4},{6,7},{7,6},{8,9},{9,8},{10,11... | collective-permute-start | bytes 786440 | tf_op jit(solution)/shard_map/ppermute | solution.py:197
  53.0 1.9 %collective-permute-start.18 = (bf16[128,512]{1,0:T(8,128)(2,1)S(1)}, bf16[128,512]{1,0:T(8,128)(2,1)S(1)}, u32[]{:S(2)}, u32[]{:S(2)}) collective-permute-start(bf16[128,512]{1,0:T(8,128)(2,1)S(1)} %get-tuple-element.72.refs_0_), channel_id=1, source_target_pairs={{0,1},{1,0},{2,3},{3,2},{4,5},{5,4},{6,7},{7,6},{8,9},{9,8},{10,11... | collective-permute-start | bytes 393224 | tf_op jit(solution)/shard_map/ppermute | solution.py:197
  53.6 1.4 %collective-permute-start.20 = (bf16[512,128]{1,0:T(8,128)(2,1)S(1)}, bf16[512,128]{1,0:T(8,128)(2,1)S(1)}, u32[]{:S(2)}, u32[]{:S(2)}) collective-permute-start(bf16[512,128]{1,0:T(8,128)(2,1)S(1)} %slice.28), channel_id=1, source_target_pairs={{0,1},{1,0},{2,3},{3,2},{4,5},{5,4},{6,7},{7,6},{8,9},{9,8},{10,11... | collective-permute-start | bytes 393224 | tf_op jit(solution)/shard_map/ppermute | solution.py:197
  56.0 4.6 %collective-permute-start.23 = (bf16[512,512]{1,0:T(8,128)(2,1)S(1)}, bf16[512,512]{1,0:T(8,128)(2,1)S(1)}, u32[]{:S(2)}, u32[]{:S(2)}) collective-permute-start(bf16[512,512]{1,0:T(8,128)(2,1)S(1)} %get-tuple-element.77.sent), channel_id=1, source_target_pairs={{0,1},{1,0},{2,3},{3,2},{4,5},{5,4},{6,7},{7,6},{8,9},{9,8},{10,11... | collective-permute-start | bytes 1572872 | tf_op jit(solution)/shard_map/ppermute | solution.py:197
  57.4 6.4 %collective-permute-start.22 = (bf16[512,256]{1,0:T(8,128)(2,1)S(1)}, bf16[512,256]{1,0:T(8,128)(2,1)S(1)}, u32[]{:S(2)}, u32[]{:S(2)}) collective-permute-start(bf16[512,256]{1,0:T(8,128)(2,1)S(1)} %change.3), channel_id=1, source_target_pairs={{4,8},{8,4},{12,14},{14,12},{10,6},{6,10},{2,0},{0,2},{1,5},{5,1},... | collective-permute-start | bytes 786440 | tf_op jit(solution)/shard_map/ppermute | solution.py:197
  61.7 6.4 %collective-permute-start.25 = (bf16[512,256]{1,0:T(8,128)(2,1)S(1)}, bf16[512,256]{1,0:T(8,128)(2,1)S(1)}, u32[]{:S(2)}, u32[]{:S(2)}) collective-permute-start(bf16[512,256]{1,0:T(8,128)(2,1)S(1)} %get-tuple-element.84), channel_id=1, source_target_pairs={{0,4},{4,0},{8,12},{12,8},{14,10},{10,14},{6,2},{2,6},{5,9},{9,5},... | collective-permute-start | bytes 786440 | tf_op jit(solution)/shard_map/ppermute | solution.py:197
  64.4 7.0 %collective-permute-start.24 = (bf16[512,256]{1,0:T(8,128)(2,1)S(1)}, bf16[512,256]{1,0:T(8,128)(2,1)S(1)}, u32[]{:S(2)}, u32[]{:S(2)}) collective-permute-start(bf16[512,256]{1,0:T(8,128)(2,1)S(1)} %hop.5), channel_id=1, source_target_pairs={{0,4},{4,0},{8,12},{12,8},{14,10},{10,14},{6,2},{2,6},{5,9},{9,5},... | collective-permute-start | bytes 786440 | tf_op jit(solution)/shard_map/ppermute | solution.py:197
  68.8 6.4 %collective-permute-start.27 = (bf16[512,256]{1,0:T(8,128)(2,1)S(1)}, bf16[512,256]{1,0:T(8,128)(2,1)S(1)}, u32[]{:S(2)}, u32[]{:S(2)}) collective-permute-start(bf16[512,256]{1,0:T(8,128)(2,1)S(1)} %hop.6), channel_id=1, source_target_pairs={{4,8},{8,4},{12,14},{14,12},{10,6},{6,10},{2,0},{0,2},{1,5},{5,1},... | collective-permute-start | bytes 786440 | tf_op jit(solution)/shard_map/ppermute | solution.py:197
  72.0 7.6 %collective-permute-start.26 = (bf16[512,256]{1,0:T(8,128)(2,1)S(1)}, bf16[512,256]{1,0:T(8,128)(2,1)S(1)}, u32[]{:S(2)}, u32[]{:S(2)}) collective-permute-start(bf16[512,256]{1,0:T(8,128)(2,1)S(1)} %hop.7), channel_id=1, source_target_pairs={{4,8},{8,4},{12,14},{14,12},{10,6},{6,10},{2,0},{0,2},{1,5},{5,1},... | collective-permute-start | bytes 786440 | tf_op jit(solution)/shard_map/ppermute | solution.py:197
  75.8 8.0 %collective-permute-start.29 = (bf16[512,256]{1,0:T(8,128)(2,1)S(1)}, bf16[512,256]{1,0:T(8,128)(2,1)S(1)}, u32[]{:S(2)}, u32[]{:S(2)}) collective-permute-start(bf16[512,256]{1,0:T(8,128)(2,1)S(1)} %hop.8), channel_id=1, source_target_pairs={{0,4},{4,0},{8,12},{12,8},{14,10},{10,14},{6,2},{2,6},{5,9},{9,5},... | collective-permute-start | bytes 786440 | tf_op jit(solution)/shard_map/ppermute | solution.py:197
  80.2 7.9 %collective-permute-start.28 = (bf16[512,256]{1,0:T(8,128)(2,1)S(1)}, bf16[512,256]{1,0:T(8,128)(2,1)S(1)}, u32[]{:S(2)}, u32[]{:S(2)}) collective-permute-start(bf16[512,256]{1,0:T(8,128)(2,1)S(1)} %hop.9), channel_id=1, source_target_pairs={{0,4},{4,0},{8,12},{12,8},{14,10},{10,14},{6,2},{2,6},{5,9},{9,5},... | collective-permute-start | bytes 786440 | tf_op jit(solution)/shard_map/ppermute | solution.py:197
  83.8 4.4 %collective-permute-start.30 = (bf16[512,256]{1,0:T(8,128)(2,1)S(1)}, bf16[512,256]{1,0:T(8,128)(2,1)S(1)}, u32[]{:S(2)}, u32[]{:S(2)}) collective-permute-start(bf16[512,256]{1,0:T(8,128)(2,1)S(1)} %collective-permute-done.29), channel_id=1, source_target_pairs={{0,1},{1,0},{2,3},{3,2},{4,5},{5,4},{6,7},{7,6},{8,9},{9,8},{10,11... | collective-permute-start | bytes 786440 | tf_op jit(solution)/shard_map/ppermute | solution.py:197
  88.8 6.4 %collective-permute-start.31 = (bf16[512,256]{1,0:T(8,128)(2,1)S(1)}, bf16[512,256]{1,0:T(8,128)(2,1)S(1)}, u32[]{:S(2)}, u32[]{:S(2)}) collective-permute-start(bf16[512,256]{1,0:T(8,128)(2,1)S(1)} %last.1.change), channel_id=1, source_target_pairs={{0,2},{2,0},{1,3},{3,1},{4,6},{6,4},{5,7},{7,5},{8,10},{10,8},{9,1... | collective-permute-start | bytes 786440 | tf_op jit(solution)/shard_map/ppermute | solution.py:197
  (5 other events, 44.7 us)

commit v17 on v16

--- a/solution.py
+++ b/solution.py
@@ -168,10 +168,6 @@
         at += count
 
 
-def hop_kernel(place, change, came, out):
-    out[...] = (change[...] + came[...].astype(F32)).astype(BF16)
-
-
 def last_kernel(place, change, came, given, out):
     part = out.shape[1] // 2
     for i in (0, 1):
@@ -293,7 +289,7 @@
             functools.partial(change_kernel, counts), outs, place, (update, *[f for b in blocks for f in b]), "change", 8
         )
 
-    hop = lambda ahead, came: call(hop_kernel, whole, place, (ahead, came), "hop", 4)
+    hop = lambda ahead, came: (ahead + came.astype(F32)).astype(BF16)
     (first,) = changes(sent, [(f4, f4_other)], (whole,))
     (sent_other,) = after((C(sent),), first)
     ahead = changes(after((sent,), first)[0], [(f3,), (f2,), (f1,), (f0, f0_other)], (wide,) * 4)

time: 98.2 us -> 96.6 us (0.984)
  waiting for transfers between devices: 24.8 us -> 28.7 us
  Pallas kernels: 34.7 us -> 31.8 us
  starting transfers between devices: 31.7 us -> 29.2 us
    ppermute x32, waiting for transfers between devices: 24.8 us -> 28.7 us  [swap(): lax.ppermute(x, axes, [p for a, b in pairs for p in ((a, b), (b, a))])]
    pallas_call x25 -> x20, Pallas kernels: 34.7 us -> 31.8 us  [call(): pl.pallas_call(kernel, out_shape=out_shapes, in_specs=[pl.BlockSpec(memor...]
    ppermute x32, starting transfers between devices: 31.7 us -> 29.2 us  [swap(): lax.ppermute(x, axes, [p for a, b in pairs for p in ((a, b), (b, a))])]
  transfers between devices with their start and end apart: 32 -> 32, of which waited for: 14 -> 14; matrix products, arithmetic and copies ran while one was open for 1% -> 2% of each run, Pallas kernels for 33% -> 30%
where the time goes in v17:
time: 96.6 us; the launch traced here: 95.5 us
  Pallas kernels  31.8 us (33%)
  starting transfers between devices  29.2 us (30%)
  waiting for transfers between devices  28.7 us (30%)
  local copies, waits for them, and re-layouts  3.16 us (3%)
  other arithmetic  1.54 us (2%)
  between operations  1.19 us (1%)
    pallas_call x20, Pallas kernels, call(): pl.pallas_call(kernel, out_shape=out_shapes, in_specs=[pl.BlockSpec(memor...  31.8 us
    ppermute x32, starting transfers between devices, swap(): lax.ppermute(x, axes, [p for a, b in pairs for p in ((a, b), (b, a))])  29.2 us
    ppermute x32, waiting for transfers between devices, swap(): lax.ppermute(x, axes, [p for a, b in pairs for p in ((a, b), (b, a))])  28.7 us
    unnamed x11, local copies, waits for them, and re-layouts  3.04 us
  transfers between devices with their start and end apart: 32, of which 14 were waited for; matrix products, arithmetic and copies ran while one was open for 2% of the time, Pallas kernels for 30%

profile of v17, /device:TPU:0, one launch (start us, length us, event | category | flops | bytes accessed | tf_op | source)
XLA Modules:
  0.0 95.5 jit_solution(11622924230790027810)
XLA Ops:
  1.2 1.9 %prepare.1 = (bf16[256,1024]{1,0:T(8,128)(2,1)S(1)}, bf16[512,256]{1,0:T(8,128)(2,1)S(1)}, bf16[512,256]{1,0:T(8,128)(2,1)S(1)}) custom-call(s32[3]{0:T(128)S(1)} %pad_add_fusion.place, bf16[512,1024]{1,0:T(8,128)(2,1)} %inputs.1, s32[1,512]{1,0:T(1,128)} %bitcast.18, f32[500,512]{1,0:T(8,128)} %bitcast.13), custom_call_target="tpu_custom_call" | custom-call | tf_op jit(solution)/shard_map/prepare/pallas_call | solution.py:42
  3.3 2.0 %collective-permute-done = bf16[512,256]{1,0:T(8,128)(2,1)S(1)} collective-permute-done((bf16[512,256]{1,0:T(8,128)(2,1)S(1)}, bf16[512,256]{1,0:T(8,128)(2,1)S(1)}, u32[]{:S(2)}, u32[]{:S(2)}) %collective-permute-start) | collective-permute-done | bytes 262176 | tf_op jit(solution)/shard_map/ppermute | solution.py:193
  5.3 2.9 %collective-permute-start.5 = (bf16[256,1024]{1,0:T(8,128)(2,1)S(1)}, bf16[256,1024]{1,0:T(8,128)(2,1)S(1)}, u32[]{:S(2)}, u32[]{:S(2)}) collective-permute-start(bf16[256,1024]{1,0:T(8,128)(2,1)S(1)} %get-tuple-element.51.rows), channel_id=1, source_target_pairs={{0,4},{4,0},{8,12},{12,8},{14,10},{10,14},{6,2},{2,6},{5,9},{9,5},... | collective-permute-start | bytes 1572872 | tf_op jit(solution)/shard_map/ppermute | solution.py:193
  8.5 2.2 %copy-done.2 = f32[1,512,2048]{2,1,0:T(8,128)S(1)} copy-done((f32[1,512,2048]{2,1,0:T(8,128)S(1)}, f32[1,512,2048]{2,1,0:T(8,128)}, u32[]{:S(2)}) %copy-start.2) | copy-done | bytes 4194328
  12.3 2.4 %block.2 = (bf16[128,1024]{1,0:T(8,128)(2,1)S(1)}, bf16[128,512]{1,0:T(8,128)(2,1)S(1)}) custom-call(s32[3]{0:T(128)S(1)} %pad_add_fusion.place, bf16[256,1024]{1,0:T(8,128)(2,1)S(1)} %get-tuple-element.51.rows, bf16[1024,1024]{1,0:T(8,128)(2,1)S(1)} %copy-done, bf16[1024,1024]{1,0:T(8,128)(2,1)S(1)} %collective-permute-done.1.w_other, ...), custom_call_target="tpu_custom_call" | custom-call | tf_op jit(solution)/shard_map/block/pallas_call | solution.py:42
  15.4 2.8 %features.3 = (bf16[256,2048]{1,0:T(8,128)(2,1)S(1)}, bf16[256,512]{1,0:T(8,128)(2,1)S(1)}) custom-call(s32[3]{0:T(128)S(1)} %pad_add_fusion.place, bf16[256,1024]{1,0:T(8,128)(2,1)S(1)} %collective-permute-done.5.rows, bf16[1024,1024]{1,0:T(8,128)(2,1)S(1)} %copy-done, bf16[1024,1024]{1,0:T(8,128)(2,1)S(1)} %collective-permute-done.1.w_other, ...), custom_call_target="tpu_custom_call" | custom-call | tf_op jit(solution)/shard_map/features/pallas_call | solution.py:42
  18.3 2.0 %collective-permute-start.9 = (bf16[256,1024]{1,0:T(8,128)(2,1)S(1)}, bf16[256,1024]{1,0:T(8,128)(2,1)S(1)}, u32[]{:S(2)}, u32[]{:S(2)}) collective-permute-start(bf16[256,1024]{1,0:T(8,128)(2,1)S(1)} %collective-permute-done.5.rows), channel_id=1, source_target_pairs={{4,8},{8,4},{12,14},{14,12},{10,6},{6,10},{2,0},{0,2},{1,5},{5,1},... | collective-permute-start | bytes 1572872 | tf_op jit(solution)/shard_map/ppermute | solution.py:193
  21.7 1.6 %collective-permute-start.8 = (bf16[1024,256]{1,0:T(8,128)(2,1)S(1)}, bf16[1024,256]{1,0:T(8,128)(2,1)S(1)}, u32[]{:S(2)}, u32[]{:S(2)}) collective-permute-start(bf16[1024,256]{1,0:T(8,128)(2,1)S(1)} %collective-permute-done.4.refs_4_), channel_id=1, source_target_pairs={{4,8},{8,4},{12,14},{14,12},{10,6},{6,10},{2,0},{0,2},{1,5},{5,1},... | collective-permute-start | bytes 1572872 | tf_op jit(solution)/shard_map/ppermute | solution.py:193
  24.9 2.6 %collective-permute-done.9.rows = bf16[256,1024]{1,0:T(8,128)(2,1)S(1)} collective-permute-done((bf16[256,1024]{1,0:T(8,128)(2,1)S(1)}, bf16[256,1024]{1,0:T(8,128)(2,1)S(1)}, u32[]{:S(2)}, u32[]{:S(2)}) %collective-permute-start.9) | collective-permute-done | bytes 524320 | tf_op jit(solution)/shard_map/ppermute | solution.py:193
  27.5 2.8 %features.4 = (bf16[256,2048]{1,0:T(8,128)(2,1)S(1)}, bf16[256,512]{1,0:T(8,128)(2,1)S(1)}) custom-call(s32[3]{0:T(128)S(1)} %pad_add_fusion.place, bf16[256,1024]{1,0:T(8,128)(2,1)S(1)} %collective-permute-done.9.rows, bf16[1024,1024]{1,0:T(8,128)(2,1)S(1)} %copy-done, bf16[1024,1024]{1,0:T(8,128)(2,1)S(1)} %collective-permute-done.1.w_other, ...), custom_call_target="tpu_custom_call" | custom-call | tf_op jit(solution)/shard_map/features/pallas_call | solution.py:42
  30.4 2.1 %collective-permute-start.14 = (bf16[256,1024]{1,0:T(8,128)(2,1)S(1)}, bf16[256,1024]{1,0:T(8,128)(2,1)S(1)}, u32[]{:S(2)}, u32[]{:S(2)}) collective-permute-start(bf16[256,1024]{1,0:T(8,128)(2,1)S(1)} %collective-permute-done.9.rows), channel_id=1, source_target_pairs={{0,4},{4,0},{8,12},{12,8},{14,10},{10,14},{6,2},{2,6},{5,9},{9,5},... | collective-permute-start | bytes 1572872 | tf_op jit(solution)/shard_map/ppermute | solution.py:193
  33.8 1.5 %begin.3.refs_0_ = f32[512,512]{1,0:T(8,128)S(1)} custom-call(s32[3]{0:T(128)S(1)} %pad_add_fusion.place, bf16[1024,256]{1,0:T(8,128)(2,1)S(1)} %constant_dynamic-update-slice_fusion.refs_0_.refs_2_, bf16[128,1024]{1,0:T(8,128)(2,1)S(1)} %get-tuple-element.52.refs_1_, bf16[1024,256]{1,0:T(8,128)(2,1)S(1)} %constant_dynamic-update-slice_fusion.refs_0_.refs_2_, ...), custom_call_target="tpu_custom_call" | custom-call | tf_op jit(solution)/shard_map/begin/pallas_call | solution.py:42
  37.2 2.4 %collective-permute-done.14.rows = bf16[256,1024]{1,0:T(8,128)(2,1)S(1)} collective-permute-done((bf16[256,1024]{1,0:T(8,128)(2,1)S(1)}, bf16[256,1024]{1,0:T(8,128)(2,1)S(1)}, u32[]{:S(2)}, u32[]{:S(2)}) %collective-permute-start.14) | collective-permute-done | bytes 524320 | tf_op jit(solution)/shard_map/ppermute | solution.py:193
  39.6 2.8 %features.5 = (bf16[256,2048]{1,0:T(8,128)(2,1)S(1)}, bf16[256,512]{1,0:T(8,128)(2,1)S(1)}) custom-call(s32[3]{0:T(128)S(1)} %pad_add_fusion.place, bf16[256,1024]{1,0:T(8,128)(2,1)S(1)} %collective-permute-done.14.rows, bf16[1024,1024]{1,0:T(8,128)(2,1)S(1)} %copy-done, bf16[1024,1024]{1,0:T(8,128)(2,1)S(1)} %collective-permute-done.1.w_other, ...), custom_call_target="tpu_custom_call" | custom-call | tf_op jit(solution)/shard_map/features/pallas_call | solution.py:42
  42.5 1.3 %meet.5.refs_2_ = bf16[256,1024]{1,0:T(8,128)(2,1)S(1)} custom-call(s32[3]{0:T(128)S(1)} %pad_add_fusion.place, bf16[256,2048]{1,0:T(8,128)(2,1)S(1)} %get-tuple-element.67.feats, bf16[512,2048]{1,0:T(8,128)(2,1)S(1)} %round.1.inverse), custom_call_target="tpu_custom_call" | custom-call | tf_op jit(solution)/shard_map/meet/pallas_call | solution.py:42
  43.9 2.0 %collective-permute-start.17 = (bf16[128,1024]{1,0:T(8,128)(2,1)S(1)}, bf16[128,1024]{1,0:T(8,128)(2,1)S(1)}, u32[]{:S(2)}, u32[]{:S(2)}) collective-permute-start(bf16[128,1024]{1,0:T(8,128)(2,1)S(1)} %slice.24), channel_id=1, source_target_pairs={{4,8},{8,4},{12,14},{14,12},{10,6},{6,10},{2,0},{0,2},{1,5},{5,1},... | collective-permute-start | bytes 786440 | tf_op jit(solution)/shard_map/ppermute | solution.py:193
  47.6 2.7 %collective-permute-done.17.rows = bf16[128,1024]{1,0:T(8,128)(2,1)S(1)} collective-permute-done((bf16[128,1024]{1,0:T(8,128)(2,1)S(1)}, bf16[128,1024]{1,0:T(8,128)(2,1)S(1)}, u32[]{:S(2)}, u32[]{:S(2)}) %collective-permute-start.17) | collective-permute-done | bytes 262176 | tf_op jit(solution)/shard_map/ppermute | solution.py:193
  50.3 2.6 %block.3 = (bf16[128,1024]{1,0:T(8,128)(2,1)S(1)}, bf16[128,512]{1,0:T(8,128)(2,1)S(1)}) custom-call(s32[3]{0:T(128)S(1)} %pad_add_fusion.place, bf16[128,1024]{1,0:T(8,128)(2,1)S(1)} %collective-permute-done.17.rows, bf16[1024,1024]{1,0:T(8,128)(2,1)S(1)} %copy-done, bf16[1024,1024]{1,0:T(8,128)(2,1)S(1)} %collective-permute-done.1.w_other, ...), custom_call_target="tpu_custom_call" | custom-call | tf_op jit(solution)/shard_map/block/pallas_call | solution.py:42
  57.4 1.9 %collective-permute-start.22 = (bf16[512,256]{1,0:T(8,128)(2,1)S(1)}, bf16[512,256]{1,0:T(8,128)(2,1)S(1)}, u32[]{:S(2)}, u32[]{:S(2)}) collective-permute-start(bf16[512,256]{1,0:T(8,128)(2,1)S(1)} %change.3), channel_id=1, source_target_pairs={{4,8},{8,4},{12,14},{14,12},{10,6},{6,10},{2,0},{0,2},{1,5},{5,1},... | collective-permute-start | bytes 786440 | tf_op jit(solution)/shard_map/ppermute | solution.py:193
  61.7 1.7 %collective-permute-start.25 = (bf16[512,256]{1,0:T(8,128)(2,1)S(1)}, bf16[512,256]{1,0:T(8,128)(2,1)S(1)}, u32[]{:S(2)}, u32[]{:S(2)}) collective-permute-start(bf16[512,256]{1,0:T(8,128)(2,1)S(1)} %get-tuple-element.84), channel_id=1, source_target_pairs={{0,4},{4,0},{8,12},{12,8},{14,10},{10,14},{6,2},{2,6},{5,9},{9,5},... | collective-permute-start | bytes 786440 | tf_op jit(solution)/shard_map/ppermute | solution.py:193
  63.9 2.0 %collective-permute-start.24 = (bf16[512,256]{1,0:T(8,128)(2,1)S(1)}, bf16[512,256]{1,0:T(8,128)(2,1)S(1)}, u32[]{:S(2)}, u32[]{:S(2)}) collective-permute-start(bf16[512,256]{1,0:T(8,128)(2,1)S(1)} %add_convert_fusion.4), channel_id=1, source_target_pairs={{0,4},{4,0},{8,12},{12,8},{14,10},{10,14},{6,2},{2,6},{5,9},{9,5},... | collective-permute-start | bytes 786440 | tf_op jit(solution)/shard_map/ppermute | solution.py:193
  65.9 2.3 %collective-permute-done.25 = bf16[512,256]{1,0:T(8,128)(2,1)S(1)} collective-permute-done((bf16[512,256]{1,0:T(8,128)(2,1)S(1)}, bf16[512,256]{1,0:T(8,128)(2,1)S(1)}, u32[]{:S(2)}, u32[]{:S(2)}) %collective-permute-start.25) | collective-permute-done | bytes 262176 | tf_op jit(solution)/shard_map/ppermute | solution.py:193
  69.5 2.4 %collective-permute-done.24 = bf16[512,256]{1,0:T(8,128)(2,1)S(1)} collective-permute-done((bf16[512,256]{1,0:T(8,128)(2,1)S(1)}, bf16[512,256]{1,0:T(8,128)(2,1)S(1)}, u32[]{:S(2)}, u32[]{:S(2)}) %collective-permute-start.24) | collective-permute-done | bytes 262176 | tf_op jit(solution)/shard_map/ppermute | solution.py:193
  73.0 1.7 %collective-permute-done.27 = bf16[512,256]{1,0:T(8,128)(2,1)S(1)} collective-permute-done((bf16[512,256]{1,0:T(8,128)(2,1)S(1)}, bf16[512,256]{1,0:T(8,128)(2,1)S(1)}, u32[]{:S(2)}, u32[]{:S(2)}) %collective-permute-start.27) | collective-permute-done | bytes 262176 | tf_op jit(solution)/shard_map/ppermute | solution.py:193
  74.8 1.7 %collective-permute-start.29 = (bf16[512,256]{1,0:T(8,128)(2,1)S(1)}, bf16[512,256]{1,0:T(8,128)(2,1)S(1)}, u32[]{:S(2)}, u32[]{:S(2)}) collective-permute-start(bf16[512,256]{1,0:T(8,128)(2,1)S(1)} %add_convert_fusion.1), channel_id=1, source_target_pairs={{0,4},{4,0},{8,12},{12,8},{14,10},{10,14},{6,2},{2,6},{5,9},{9,5},... | collective-permute-start | bytes 786440 | tf_op jit(solution)/shard_map/ppermute | solution.py:193
  76.5 3.7 %collective-permute-done.26 = bf16[512,256]{1,0:T(8,128)(2,1)S(1)} collective-permute-done((bf16[512,256]{1,0:T(8,128)(2,1)S(1)}, bf16[512,256]{1,0:T(8,128)(2,1)S(1)}, u32[]{:S(2)}, u32[]{:S(2)}) %collective-permute-start.26) | collective-permute-done | bytes 262176 | tf_op jit(solution)/shard_map/ppermute | solution.py:193
  80.3 2.2 %collective-permute-start.28 = (bf16[512,256]{1,0:T(8,128)(2,1)S(1)}, bf16[512,256]{1,0:T(8,128)(2,1)S(1)}, u32[]{:S(2)}, u32[]{:S(2)}) collective-permute-start(bf16[512,256]{1,0:T(8,128)(2,1)S(1)} %add_convert_fusion), channel_id=1, source_target_pairs={{0,4},{4,0},{8,12},{12,8},{14,10},{10,14},{6,2},{2,6},{5,9},{9,5},... | collective-permute-start | bytes 786440 | tf_op jit(solution)/shard_map/ppermute | solution.py:193
  82.5 4.3 %collective-permute-done.28.came = bf16[512,256]{1,0:T(8,128)(2,1)S(1)} collective-permute-done((bf16[512,256]{1,0:T(8,128)(2,1)S(1)}, bf16[512,256]{1,0:T(8,128)(2,1)S(1)}, u32[]{:S(2)}, u32[]{:S(2)}) %collective-permute-start.28) | collective-permute-done | bytes 262176 | tf_op jit(solution)/shard_map/ppermute | solution.py:193
  87.5 1.6 %collective-permute-start.31 = (bf16[512,256]{1,0:T(8,128)(2,1)S(1)}, bf16[512,256]{1,0:T(8,128)(2,1)S(1)}, u32[]{:S(2)}, u32[]{:S(2)}) collective-permute-start(bf16[512,256]{1,0:T(8,128)(2,1)S(1)} %last.1.change), channel_id=1, source_target_pairs={{0,2},{2,0},{1,3},{3,1},{4,6},{6,4},{5,7},{7,5},{8,10},{10,8},{9,1... | collective-permute-start | bytes 786440 | tf_op jit(solution)/shard_map/ppermute | solution.py:193
  90.2 1.4 %apply.2.refs_0_ = f32[500,512]{1,0:T(8,128)} custom-call(s32[3]{0:T(128)S(1)} %pad_add_fusion.place, f32[500,512]{1,0:T(8,128)S(1)} %bitcast.14, bf16[512,256]{1,0:T(8,128)(2,1)S(1)} %last.1.change), custom_call_target="tpu_custom_call" | custom-call | tf_op jit(solution)/shard_map/apply/pallas_call | solution.py:42
  91.6 2.3 %collective-permute-done.31.change = bf16[512,256]{1,0:T(8,128)(2,1)S(1)} collective-permute-done((bf16[512,256]{1,0:T(8,128)(2,1)S(1)}, bf16[512,256]{1,0:T(8,128)(2,1)S(1)}, u32[]{:S(2)}, u32[]{:S(2)}) %collective-permute-start.31) | collective-permute-done | bytes 262176 | tf_op jit(solution)/shard_map/ppermute | solution.py:193
  93.9 1.4 %apply.3 = f32[500,512]{1,0:T(8,128)} custom-call(s32[3]{0:T(128)S(1)} %pad_add_fusion.place, f32[500,512]{1,0:T(8,128)S(1)} %bitcast.15, bf16[512,256]{1,0:T(8,128)(2,1)S(1)} %collective-permute-done.31.change, f32[500,512]{1,0:T(8,128)} %apply.2.refs_0_), custom_call_target="tpu_custom_call", output_to_operand_aliasing={{}: (3, {})} | custom-call | tf_op jit(solution)/shard_map/apply/pallas_call | solution.py:42
  (78 shorter events, 22.6 us)
Async XLA Ops:
  0.6 10.8 %collective-permute-start.1 = (bf16[1024,1024]{1,0:T(8,128)(2,1)}, bf16[1024,1024]{1,0:T(8,128)(2,1)S(1)}, u32[]{:S(2)}, u32[]{:S(2)}) collective-permute-start(bf16[1024,1024]{1,0:T(8,128)(2,1)} %w_own.9), channel_id=1, source_target_pairs={{0,1},{1,0},{2,3},{3,2},{4,5},{5,4},{6,7},{7,6},{8,9},{9,8},{10,11... | collective-permute-start | bytes 6291464 | tf_op jit(solution)/shard_map/ppermute | solution.py:193
  3.2 2.2 %collective-permute-start = (bf16[512,256]{1,0:T(8,128)(2,1)S(1)}, bf16[512,256]{1,0:T(8,128)(2,1)S(1)}, u32[]{:S(2)}, u32[]{:S(2)}) collective-permute-start(bf16[512,256]{1,0:T(8,128)(2,1)S(1)} %get-tuple-element.49), channel_id=1, source_target_pairs={{0,1},{1,0},{2,3},{3,2},{4,5},{5,4},{6,7},{7,6},{8,9},{9,8},{10,11... | collective-permute-start | bytes 786440 | tf_op jit(solution)/shard_map/ppermute | solution.py:193
  5.3 10.1 %collective-permute-start.5 = (bf16[256,1024]{1,0:T(8,128)(2,1)S(1)}, bf16[256,1024]{1,0:T(8,128)(2,1)S(1)}, u32[]{:S(2)}, u32[]{:S(2)}) collective-permute-start(bf16[256,1024]{1,0:T(8,128)(2,1)S(1)} %get-tuple-element.51.rows), channel_id=1, source_target_pairs={{0,4},{4,0},{8,12},{12,8},{14,10},{10,14},{6,2},{2,6},{5,9},{9,5},... | collective-permute-start | bytes 1572872 | tf_op jit(solution)/shard_map/ppermute | solution.py:193
  8.3 13.3 %collective-permute-start.4 = (bf16[1024,256]{1,0:T(8,128)(2,1)S(1)}, bf16[1024,256]{1,0:T(8,128)(2,1)S(1)}, u32[]{:S(2)}, u32[]{:S(2)}) collective-permute-start(bf16[1024,256]{1,0:T(8,128)(2,1)S(1)} %constant_dynamic-update-slice_fusion.refs_0_.refs_2_), channel_id=1, source_target_pairs={{0,4},{4,0},{8,12},{12,8},{14,10},{10,14},{6,2},{2,6},{5,9},{9,5},... | collective-permute-start | bytes 1572872 | tf_op jit(solution)/shard_map/ppermute | solution.py:193
  8.4 3.0 %collective-permute-start.2 = (bf16[1,1024]{1,0:T(2,128)(2,1)S(1)}, bf16[1,1024]{1,0:T(2,128)(2,1)S(1)}, u32[]{:S(2)}, u32[]{:S(2)}) collective-permute-start(bf16[1,1024]{1,0:T(2,128)(2,1)S(1)} %broadcast_in_dim.7.p_own), channel_id=1, source_target_pairs={{0,1},{1,0},{2,3},{3,2},{4,5},{5,4},{6,7},{7,6},{8,9},{9,8},{10,11... | collective-permute-start | bytes 6152 | tf_op jit(solution)/shard_map/ppermute | solution.py:193
  18.3 9.2 %collective-permute-start.9 = (bf16[256,1024]{1,0:T(8,128)(2,1)S(1)}, bf16[256,1024]{1,0:T(8,128)(2,1)S(1)}, u32[]{:S(2)}, u32[]{:S(2)}) collective-permute-start(bf16[256,1024]{1,0:T(8,128)(2,1)S(1)} %collective-permute-done.5.rows), channel_id=1, source_target_pairs={{4,8},{8,4},{12,14},{14,12},{10,6},{6,10},{2,0},{0,2},{1,5},{5,1},... | collective-permute-start | bytes 1572872 | tf_op jit(solution)/shard_map/ppermute | solution.py:193
  21.6 12.2 %collective-permute-start.7 = (bf16[256,1024]{1,0:T(8,128)(2,1)S(1)}, bf16[256,1024]{1,0:T(8,128)(2,1)S(1)}, u32[]{:S(2)}, u32[]{:S(2)}) collective-permute-start(bf16[256,1024]{1,0:T(8,128)(2,1)S(1)} %meet.3.refs_5_), channel_id=1, source_target_pairs={{0,1},{1,0},{2,3},{3,2},{4,5},{5,4},{6,7},{7,6},{8,9},{9,8},{10,11... | collective-permute-start | bytes 1572872 | tf_op jit(solution)/shard_map/ppermute | solution.py:193
  21.7 13.6 %collective-permute-start.8 = (bf16[1024,256]{1,0:T(8,128)(2,1)S(1)}, bf16[1024,256]{1,0:T(8,128)(2,1)S(1)}, u32[]{:S(2)}, u32[]{:S(2)}) collective-permute-start(bf16[1024,256]{1,0:T(8,128)(2,1)S(1)} %collective-permute-done.4.refs_4_), channel_id=1, source_target_pairs={{4,8},{8,4},{12,14},{14,12},{10,6},{6,10},{2,0},{0,2},{1,5},{5,1},... | collective-permute-start | bytes 1572872 | tf_op jit(solution)/shard_map/ppermute | solution.py:193
  23.2 1.3 %collective-permute-start.10 = (bf16[128,512]{1,0:T(8,128)(2,1)S(1)}, bf16[128,512]{1,0:T(8,128)(2,1)S(1)}, u32[]{:S(2)}, u32[]{:S(2)}) collective-permute-start(bf16[128,512]{1,0:T(8,128)(2,1)S(1)} %get-tuple-element.59.refs_3_), channel_id=1, source_target_pairs={{0,1},{1,0},{2,3},{3,2},{4,5},{5,4},{6,7},{7,6},{8,9},{9,8},{10,11... | collective-permute-start | bytes 393224 | tf_op jit(solution)/shard_map/ppermute | solution.py:193
  23.6 10.2 %collective-permute-start.6 = (bf16[512,256]{1,0:T(8,128)(2,1)S(1)}, bf16[512,256]{1,0:T(8,128)(2,1)S(1)}, u32[]{:S(2)}, u32[]{:S(2)}) collective-permute-start(bf16[512,256]{1,0:T(8,128)(2,1)S(1)} %slice.21), channel_id=1, source_target_pairs={{0,1},{1,0},{2,3},{3,2},{4,5},{5,4},{6,7},{7,6},{8,9},{9,8},{10,11... | collective-permute-start | bytes 786440 | tf_op jit(solution)/shard_map/ppermute | solution.py:193
  24.6 9.2 %collective-permute-start.3 = (bf16[128,1024]{1,0:T(8,128)(2,1)S(1)}, bf16[128,1024]{1,0:T(8,128)(2,1)S(1)}, u32[]{:S(2)}, u32[]{:S(2)}) collective-permute-start(bf16[128,1024]{1,0:T(8,128)(2,1)S(1)} %get-tuple-element.52.refs_1_), channel_id=1, source_target_pairs={{0,1},{1,0},{2,3},{3,2},{4,5},{5,4},{6,7},{7,6},{8,9},{9,8},{10,11... | collective-permute-start | bytes 786440 | tf_op jit(solution)/shard_map/ppermute | solution.py:193
  30.4 9.3 %collective-permute-start.14 = (bf16[256,1024]{1,0:T(8,128)(2,1)S(1)}, bf16[256,1024]{1,0:T(8,128)(2,1)S(1)}, u32[]{:S(2)}, u32[]{:S(2)}) collective-permute-start(bf16[256,1024]{1,0:T(8,128)(2,1)S(1)} %collective-permute-done.9.rows), channel_id=1, source_target_pairs={{0,4},{4,0},{8,12},{12,8},{14,10},{10,14},{6,2},{2,6},{5,9},{9,5},... | collective-permute-start | bytes 1572872 | tf_op jit(solution)/shard_map/ppermute | solution.py:193
  35.3 10.6 %collective-permute-start.12 = (bf16[256,1024]{1,0:T(8,128)(2,1)S(1)}, bf16[256,1024]{1,0:T(8,128)(2,1)S(1)}, u32[]{:S(2)}, u32[]{:S(2)}) collective-permute-start(bf16[256,1024]{1,0:T(8,128)(2,1)S(1)} %meet.4.refs_2_), channel_id=1, source_target_pairs={{0,1},{1,0},{2,3},{3,2},{4,5},{5,4},{6,7},{7,6},{8,9},{9,8},{10,11... | collective-permute-start | bytes 1572872 | tf_op jit(solution)/shard_map/ppermute | solution.py:193
  35.4 11.7 %collective-permute-start.13 = (bf16[1024,256]{1,0:T(8,128)(2,1)S(1)}, bf16[1024,256]{1,0:T(8,128)(2,1)S(1)}, u32[]{:S(2)}, u32[]{:S(2)}) collective-permute-start(bf16[1024,256]{1,0:T(8,128)(2,1)S(1)} %collective-permute-done.8.refs_1_), channel_id=1, source_target_pairs={{0,4},{4,0},{8,12},{12,8},{14,10},{10,14},{6,2},{2,6},{5,9},{9,5},... | collective-permute-start | bytes 1572872 | tf_op jit(solution)/shard_map/ppermute | solution.py:193
  36.0 9.9 %collective-permute-start.11 = (bf16[512,256]{1,0:T(8,128)(2,1)S(1)}, bf16[512,256]{1,0:T(8,128)(2,1)S(1)}, u32[]{:S(2)}, u32[]{:S(2)}) collective-permute-start(bf16[512,256]{1,0:T(8,128)(2,1)S(1)} %slice.22), channel_id=1, source_target_pairs={{0,1},{1,0},{2,3},{3,2},{4,5},{5,4},{6,7},{7,6},{8,9},{9,8},{10,11... | collective-permute-start | bytes 786440 | tf_op jit(solution)/shard_map/ppermute | solution.py:193
  43.8 9.9 %collective-permute-start.16 = (bf16[256,1024]{1,0:T(8,128)(2,1)S(1)}, bf16[256,1024]{1,0:T(8,128)(2,1)S(1)}, u32[]{:S(2)}, u32[]{:S(2)}) collective-permute-start(bf16[256,1024]{1,0:T(8,128)(2,1)S(1)} %meet.5.refs_2_), channel_id=1, source_target_pairs={{0,1},{1,0},{2,3},{3,2},{4,5},{5,4},{6,7},{7,6},{8,9},{9,8},{10,11... | collective-permute-start | bytes 1572872 | tf_op jit(solution)/shard_map/ppermute | solution.py:193
  43.9 6.4 %collective-permute-start.17 = (bf16[128,1024]{1,0:T(8,128)(2,1)S(1)}, bf16[128,1024]{1,0:T(8,128)(2,1)S(1)}, u32[]{:S(2)}, u32[]{:S(2)}) collective-permute-start(bf16[128,1024]{1,0:T(8,128)(2,1)S(1)} %slice.24), channel_id=1, source_target_pairs={{4,8},{8,4},{12,14},{14,12},{10,6},{6,10},{2,0},{0,2},{1,5},{5,1},... | collective-permute-start | bytes 786440 | tf_op jit(solution)/shard_map/ppermute | solution.py:193
  47.2 6.4 %collective-permute-start.19 = (bf16[1024,128]{1,0:T(8,128)(2,1)S(1)}, bf16[1024,128]{1,0:T(8,128)(2,1)S(1)}, u32[]{:S(2)}, u32[]{:S(2)}) collective-permute-start(bf16[1024,128]{1,0:T(8,128)(2,1)S(1)} %slice.25), channel_id=1, source_target_pairs={{4,8},{8,4},{12,14},{14,12},{10,6},{6,10},{2,0},{0,2},{1,5},{5,1},... | collective-permute-start | bytes 786440 | tf_op jit(solution)/shard_map/ppermute | solution.py:193
  47.3 6.3 %collective-permute-start.15 = (bf16[512,256]{1,0:T(8,128)(2,1)S(1)}, bf16[512,256]{1,0:T(8,128)(2,1)S(1)}, u32[]{:S(2)}, u32[]{:S(2)}) collective-permute-start(bf16[512,256]{1,0:T(8,128)(2,1)S(1)} %slice.23), channel_id=1, source_target_pairs={{0,1},{1,0},{2,3},{3,2},{4,5},{5,4},{6,7},{7,6},{8,9},{9,8},{10,11... | collective-permute-start | bytes 786440 | tf_op jit(solution)/shard_map/ppermute | solution.py:193
  52.9 2.1 %collective-permute-start.21 = (bf16[128,1024]{1,0:T(8,128)(2,1)S(1)}, bf16[128,1024]{1,0:T(8,128)(2,1)S(1)}, u32[]{:S(2)}, u32[]{:S(2)}) collective-permute-start(bf16[128,1024]{1,0:T(8,128)(2,1)S(1)} %get-tuple-element.74.refs_1_), channel_id=1, source_target_pairs={{0,1},{1,0},{2,3},{3,2},{4,5},{5,4},{6,7},{7,6},{8,9},{9,8},{10,11... | collective-permute-start | bytes 786440 | tf_op jit(solution)/shard_map/ppermute | solution.py:193
  53.0 1.9 %collective-permute-start.18 = (bf16[128,512]{1,0:T(8,128)(2,1)S(1)}, bf16[128,512]{1,0:T(8,128)(2,1)S(1)}, u32[]{:S(2)}, u32[]{:S(2)}) collective-permute-start(bf16[128,512]{1,0:T(8,128)(2,1)S(1)} %get-tuple-element.72.refs_0_), channel_id=1, source_target_pairs={{0,1},{1,0},{2,3},{3,2},{4,5},{5,4},{6,7},{7,6},{8,9},{9,8},{10,11... | collective-permute-start | bytes 393224 | tf_op jit(solution)/shard_map/ppermute | solution.py:193
  53.6 1.4 %collective-permute-start.20 = (bf16[512,128]{1,0:T(8,128)(2,1)S(1)}, bf16[512,128]{1,0:T(8,128)(2,1)S(1)}, u32[]{:S(2)}, u32[]{:S(2)}) collective-permute-start(bf16[512,128]{1,0:T(8,128)(2,1)S(1)} %slice.28), channel_id=1, source_target_pairs={{0,1},{1,0},{2,3},{3,2},{4,5},{5,4},{6,7},{7,6},{8,9},{9,8},{10,11... | collective-permute-start | bytes 393224 | tf_op jit(solution)/shard_map/ppermute | solution.py:193
  56.0 4.6 %collective-permute-start.23 = (bf16[512,512]{1,0:T(8,128)(2,1)S(1)}, bf16[512,512]{1,0:T(8,128)(2,1)S(1)}, u32[]{:S(2)}, u32[]{:S(2)}) collective-permute-start(bf16[512,512]{1,0:T(8,128)(2,1)S(1)} %get-tuple-element.77.sent), channel_id=1, source_target_pairs={{0,1},{1,0},{2,3},{3,2},{4,5},{5,4},{6,7},{7,6},{8,9},{9,8},{10,11... | collective-permute-start | bytes 1572872 | tf_op jit(solution)/shard_map/ppermute | solution.py:193
  57.4 6.4 %collective-permute-start.22 = (bf16[512,256]{1,0:T(8,128)(2,1)S(1)}, bf16[512,256]{1,0:T(8,128)(2,1)S(1)}, u32[]{:S(2)}, u32[]{:S(2)}) collective-permute-start(bf16[512,256]{1,0:T(8,128)(2,1)S(1)} %change.3), channel_id=1, source_target_pairs={{4,8},{8,4},{12,14},{14,12},{10,6},{6,10},{2,0},{0,2},{1,5},{5,1},... | collective-permute-start | bytes 786440 | tf_op jit(solution)/shard_map/ppermute | solution.py:193
  61.7 6.4 %collective-permute-start.25 = (bf16[512,256]{1,0:T(8,128)(2,1)S(1)}, bf16[512,256]{1,0:T(8,128)(2,1)S(1)}, u32[]{:S(2)}, u32[]{:S(2)}) collective-permute-start(bf16[512,256]{1,0:T(8,128)(2,1)S(1)} %get-tuple-element.84), channel_id=1, source_target_pairs={{0,4},{4,0},{8,12},{12,8},{14,10},{10,14},{6,2},{2,6},{5,9},{9,5},... | collective-permute-start | bytes 786440 | tf_op jit(solution)/shard_map/ppermute | solution.py:193
  63.9 8.0 %collective-permute-start.24 = (bf16[512,256]{1,0:T(8,128)(2,1)S(1)}, bf16[512,256]{1,0:T(8,128)(2,1)S(1)}, u32[]{:S(2)}, u32[]{:S(2)}) collective-permute-start(bf16[512,256]{1,0:T(8,128)(2,1)S(1)} %add_convert_fusion.4), channel_id=1, source_target_pairs={{0,4},{4,0},{8,12},{12,8},{14,10},{10,14},{6,2},{2,6},{5,9},{9,5},... | collective-permute-start | bytes 786440 | tf_op jit(solution)/shard_map/ppermute | solution.py:193
  68.3 6.4 %collective-permute-start.27 = (bf16[512,256]{1,0:T(8,128)(2,1)S(1)}, bf16[512,256]{1,0:T(8,128)(2,1)S(1)}, u32[]{:S(2)}, u32[]{:S(2)}) collective-permute-start(bf16[512,256]{1,0:T(8,128)(2,1)S(1)} %add_convert_fusion.3), channel_id=1, source_target_pairs={{4,8},{8,4},{12,14},{14,12},{10,6},{6,10},{2,0},{0,2},{1,5},{5,1},... | collective-permute-start | bytes 786440 | tf_op jit(solution)/shard_map/ppermute | solution.py:193
  72.0 8.2 %collective-permute-start.26 = (bf16[512,256]{1,0:T(8,128)(2,1)S(1)}, bf16[512,256]{1,0:T(8,128)(2,1)S(1)}, u32[]{:S(2)}, u32[]{:S(2)}) collective-permute-start(bf16[512,256]{1,0:T(8,128)(2,1)S(1)} %add_convert_fusion.2), channel_id=1, source_target_pairs={{4,8},{8,4},{12,14},{14,12},{10,6},{6,10},{2,0},{0,2},{1,5},{5,1},... | collective-permute-start | bytes 786440 | tf_op jit(solution)/shard_map/ppermute | solution.py:193
  74.8 7.7 %collective-permute-start.29 = (bf16[512,256]{1,0:T(8,128)(2,1)S(1)}, bf16[512,256]{1,0:T(8,128)(2,1)S(1)}, u32[]{:S(2)}, u32[]{:S(2)}) collective-permute-start(bf16[512,256]{1,0:T(8,128)(2,1)S(1)} %add_convert_fusion.1), channel_id=1, source_target_pairs={{0,4},{4,0},{8,12},{12,8},{14,10},{10,14},{6,2},{2,6},{5,9},{9,5},... | collective-permute-start | bytes 786440 | tf_op jit(solution)/shard_map/ppermute | solution.py:193
  80.3 6.6 %collective-permute-start.28 = (bf16[512,256]{1,0:T(8,128)(2,1)S(1)}, bf16[512,256]{1,0:T(8,128)(2,1)S(1)}, u32[]{:S(2)}, u32[]{:S(2)}) collective-permute-start(bf16[512,256]{1,0:T(8,128)(2,1)S(1)} %add_convert_fusion), channel_id=1, source_target_pairs={{0,4},{4,0},{8,12},{12,8},{14,10},{10,14},{6,2},{2,6},{5,9},{9,5},... | collective-permute-start | bytes 786440 | tf_op jit(solution)/shard_map/ppermute | solution.py:193
  82.5 4.4 %collective-permute-start.30 = (bf16[512,256]{1,0:T(8,128)(2,1)S(1)}, bf16[512,256]{1,0:T(8,128)(2,1)S(1)}, u32[]{:S(2)}, u32[]{:S(2)}) collective-permute-start(bf16[512,256]{1,0:T(8,128)(2,1)S(1)} %collective-permute-done.29), channel_id=1, source_target_pairs={{0,1},{1,0},{2,3},{3,2},{4,5},{5,4},{6,7},{7,6},{8,9},{9,8},{10,11... | collective-permute-start | bytes 786440 | tf_op jit(solution)/shard_map/ppermute | solution.py:193
  87.5 6.4 %collective-permute-start.31 = (bf16[512,256]{1,0:T(8,128)(2,1)S(1)}, bf16[512,256]{1,0:T(8,128)(2,1)S(1)}, u32[]{:S(2)}, u32[]{:S(2)}) collective-permute-start(bf16[512,256]{1,0:T(8,128)(2,1)S(1)} %last.1.change), channel_id=1, source_target_pairs={{0,2},{2,0},{1,3},{3,1},{4,6},{6,4},{5,7},{7,5},{8,10},{10,8},{9,1... | collective-permute-start | bytes 786440 | tf_op jit(solution)/shard_map/ppermute | solution.py:193
  (5 other events, 42.3 us)

commit v18 on v17

--- a/solution.py
+++ b/solution.py
@@ -160,20 +160,15 @@
     sent[...] = total.astype(BF16)
 
 
-def change_kernel(counts, place, sent, *refs):
+def change_kernel(counts, turned, place, sent, *refs):
     at = 0
     for count, out in zip(counts, refs[sum(counts):]):
         rows = refs[at][...] if count == 1 else jnp.concatenate([f[...] for f in refs[at:at + count]], axis=0)
+        if turned:
+            part = rows.shape[0] // 2
+            rows = jnp.concatenate([rows[part:], rows[:part]], axis=0)
         out[...] = dot_nt(sent[...], rows).astype(out.dtype)
         at += count
-
-
-def last_kernel(place, change, came, given, out):
-    part = out.shape[1] // 2
-    for i in (0, 1):
-        at, there = slice(i * part, (i + 1) * part), slice((1 - i) * part, (2 - i) * part)
-        total = change[:, at] + came[:, at].astype(F32) + given[:, there].astype(F32)
-        out[:, at] = total.astype(BF16)
 
 
 def apply_kernel(which, place, predictions, change, *refs):
@@ -283,10 +278,10 @@
 
     whole, wide = like((padded, 2 * part)), like((padded, 2 * part), F32)
 
-    def changes(update, blocks, outs):
+    def changes(update, blocks, outs, turned=False):
         counts = tuple(len(f) for f in blocks)
         return call(
-            functools.partial(change_kernel, counts), outs, place, (update, *[f for b in blocks for f in b]), "change", 8
+            functools.partial(change_kernel, counts, turned), outs, place, (update, *[f for b in blocks for f in b]), "change", 8
         )
 
     hop = lambda ahead, came: (ahead + came.astype(F32)).astype(BF16)
@@ -295,7 +290,7 @@
     ahead = changes(after((sent,), first)[0], [(f3,), (f2,), (f1,), (f0, f0_other)], (wide,) * 4)
     first = T(first)
     (sent_other,) = after((sent_other,), *ahead)
-    second, *behind = changes(sent_other, [(f3,), (f2,), (f1,)], (whole, wide, wide))
+    second, *behind = changes(sent_other, [(f3,), (f2,), (f1,)], (whole, wide, wide), True)
     (first,) = after((first,), second)
     second = S(second)
     for i, (way, back) in enumerate(((S, T), (T, S), (S, None))):
@@ -308,8 +303,7 @@
             (first,) = after((first,), total)
     given = C(second)
     (first,) = after((first,), given)
-    ahead = ahead[3]
-    own = call(last_kernel, whole, place, (ahead, first, given), "last", 4)
+    own = (ahead[3] + first.astype(F32) + given.astype(F32)).astype(BF16)
     new = None
     for i in (0, 1):
         change = swap(own, "blocks", [(0, 1)]) if i else own

time: 96.6 us -> 96.1 us (level)
    pallas_call x20 -> x19, Pallas kernels: 31.8 us -> 31.1 us  [call(): pl.pallas_call(kernel, out_shape=out_shapes, in_specs=[pl.BlockSpec(memor...]
where the time goes in v18:
time: 96.1 us; the launch traced here: 94.9 us
  Pallas kernels  31.1 us (32%)
  starting transfers between devices  29.2 us (30%)
  waiting for transfers between devices  28.7 us (30%)
  local copies, waits for them, and re-layouts  3.16 us (3%)
  other arithmetic  1.62 us (2%)
  between operations  1.19 us (1%)
    pallas_call x19, Pallas kernels, call(): pl.pallas_call(kernel, out_shape=out_shapes, in_specs=[pl.BlockSpec(memor...  31.1 us
    ppermute x32, starting transfers between devices, swap(): lax.ppermute(x, axes, [p for a, b in pairs for p in ((a, b), (b, a))])  29.2 us
    ppermute x32, waiting for transfers between devices, swap(): lax.ppermute(x, axes, [p for a, b in pairs for p in ((a, b), (b, a))])  28.7 us
    unnamed x11, local copies, waits for them, and re-layouts  3.04 us
  transfers between devices with their start and end apart: 32, of which 14 were waited for; matrix products, arithmetic and copies ran while one was open for 2% of the time, Pallas kernels for 30%

profile of v18, /device:TPU:0, one launch (start us, length us, event | category | flops | bytes accessed | tf_op | source)
XLA Modules:
  0.0 94.9 jit_solution(9863787501202377614)
XLA Ops:
  1.2 1.9 %prepare.1 = (bf16[256,1024]{1,0:T(8,128)(2,1)S(1)}, bf16[512,256]{1,0:T(8,128)(2,1)S(1)}, bf16[512,256]{1,0:T(8,128)(2,1)S(1)}) custom-call(s32[3]{0:T(128)S(1)} %pad_add_fusion.place, bf16[512,1024]{1,0:T(8,128)(2,1)} %inputs.1, s32[1,512]{1,0:T(1,128)} %bitcast.18, f32[500,512]{1,0:T(8,128)} %bitcast.13), custom_call_target="tpu_custom_call" | custom-call | tf_op jit(solution)/shard_map/prepare/pallas_call | solution.py:42
  3.3 2.0 %collective-permute-done = bf16[512,256]{1,0:T(8,128)(2,1)S(1)} collective-permute-done((bf16[512,256]{1,0:T(8,128)(2,1)S(1)}, bf16[512,256]{1,0:T(8,128)(2,1)S(1)}, u32[]{:S(2)}, u32[]{:S(2)}) %collective-permute-start) | collective-permute-done | bytes 262176 | tf_op jit(solution)/shard_map/ppermute | solution.py:188
  5.3 2.9 %collective-permute-start.5 = (bf16[256,1024]{1,0:T(8,128)(2,1)S(1)}, bf16[256,1024]{1,0:T(8,128)(2,1)S(1)}, u32[]{:S(2)}, u32[]{:S(2)}) collective-permute-start(bf16[256,1024]{1,0:T(8,128)(2,1)S(1)} %get-tuple-element.51.rows), channel_id=1, source_target_pairs={{0,4},{4,0},{8,12},{12,8},{14,10},{10,14},{6,2},{2,6},{5,9},{9,5},... | collective-permute-start | bytes 1572872 | tf_op jit(solution)/shard_map/ppermute | solution.py:188
  8.5 2.2 %copy-done.2 = f32[1,512,2048]{2,1,0:T(8,128)S(1)} copy-done((f32[1,512,2048]{2,1,0:T(8,128)S(1)}, f32[1,512,2048]{2,1,0:T(8,128)}, u32[]{:S(2)}) %copy-start.2) | copy-done | bytes 4194328
  12.3 2.4 %block.2 = (bf16[128,1024]{1,0:T(8,128)(2,1)S(1)}, bf16[128,512]{1,0:T(8,128)(2,1)S(1)}) custom-call(s32[3]{0:T(128)S(1)} %pad_add_fusion.place, bf16[256,1024]{1,0:T(8,128)(2,1)S(1)} %get-tuple-element.51.rows, bf16[1024,1024]{1,0:T(8,128)(2,1)S(1)} %copy-done, bf16[1024,1024]{1,0:T(8,128)(2,1)S(1)} %collective-permute-done.1.w_other, ...), custom_call_target="tpu_custom_call" | custom-call | tf_op jit(solution)/shard_map/block/pallas_call | solution.py:42
  15.4 2.8 %features.3 = (bf16[256,2048]{1,0:T(8,128)(2,1)S(1)}, bf16[256,512]{1,0:T(8,128)(2,1)S(1)}) custom-call(s32[3]{0:T(128)S(1)} %pad_add_fusion.place, bf16[256,1024]{1,0:T(8,128)(2,1)S(1)} %collective-permute-done.5.rows, bf16[1024,1024]{1,0:T(8,128)(2,1)S(1)} %copy-done, bf16[1024,1024]{1,0:T(8,128)(2,1)S(1)} %collective-permute-done.1.w_other, ...), custom_call_target="tpu_custom_call" | custom-call | tf_op jit(solution)/shard_map/features/pallas_call | solution.py:42
  18.3 2.0 %collective-permute-start.9 = (bf16[256,1024]{1,0:T(8,128)(2,1)S(1)}, bf16[256,1024]{1,0:T(8,128)(2,1)S(1)}, u32[]{:S(2)}, u32[]{:S(2)}) collective-permute-start(bf16[256,1024]{1,0:T(8,128)(2,1)S(1)} %collective-permute-done.5.rows), channel_id=1, source_target_pairs={{4,8},{8,4},{12,14},{14,12},{10,6},{6,10},{2,0},{0,2},{1,5},{5,1},... | collective-permute-start | bytes 1572872 | tf_op jit(solution)/shard_map/ppermute | solution.py:188
  21.7 1.6 %collective-permute-start.8 = (bf16[1024,256]{1,0:T(8,128)(2,1)S(1)}, bf16[1024,256]{1,0:T(8,128)(2,1)S(1)}, u32[]{:S(2)}, u32[]{:S(2)}) collective-permute-start(bf16[1024,256]{1,0:T(8,128)(2,1)S(1)} %collective-permute-done.4.refs_4_), channel_id=1, source_target_pairs={{4,8},{8,4},{12,14},{14,12},{10,6},{6,10},{2,0},{0,2},{1,5},{5,1},... | collective-permute-start | bytes 1572872 | tf_op jit(solution)/shard_map/ppermute | solution.py:188
  24.9 2.6 %collective-permute-done.9.rows = bf16[256,1024]{1,0:T(8,128)(2,1)S(1)} collective-permute-done((bf16[256,1024]{1,0:T(8,128)(2,1)S(1)}, bf16[256,1024]{1,0:T(8,128)(2,1)S(1)}, u32[]{:S(2)}, u32[]{:S(2)}) %collective-permute-start.9) | collective-permute-done | bytes 524320 | tf_op jit(solution)/shard_map/ppermute | solution.py:188
  27.5 2.8 %features.4 = (bf16[256,2048]{1,0:T(8,128)(2,1)S(1)}, bf16[256,512]{1,0:T(8,128)(2,1)S(1)}) custom-call(s32[3]{0:T(128)S(1)} %pad_add_fusion.place, bf16[256,1024]{1,0:T(8,128)(2,1)S(1)} %collective-permute-done.9.rows, bf16[1024,1024]{1,0:T(8,128)(2,1)S(1)} %copy-done, bf16[1024,1024]{1,0:T(8,128)(2,1)S(1)} %collective-permute-done.1.w_other, ...), custom_call_target="tpu_custom_call" | custom-call | tf_op jit(solution)/shard_map/features/pallas_call | solution.py:42
  30.4 2.1 %collective-permute-start.14 = (bf16[256,1024]{1,0:T(8,128)(2,1)S(1)}, bf16[256,1024]{1,0:T(8,128)(2,1)S(1)}, u32[]{:S(2)}, u32[]{:S(2)}) collective-permute-start(bf16[256,1024]{1,0:T(8,128)(2,1)S(1)} %collective-permute-done.9.rows), channel_id=1, source_target_pairs={{0,4},{4,0},{8,12},{12,8},{14,10},{10,14},{6,2},{2,6},{5,9},{9,5},... | collective-permute-start | bytes 1572872 | tf_op jit(solution)/shard_map/ppermute | solution.py:188
  33.8 1.5 %begin.3.refs_0_ = f32[512,512]{1,0:T(8,128)S(1)} custom-call(s32[3]{0:T(128)S(1)} %pad_add_fusion.place, bf16[1024,256]{1,0:T(8,128)(2,1)S(1)} %constant_dynamic-update-slice_fusion.refs_0_.refs_2_, bf16[128,1024]{1,0:T(8,128)(2,1)S(1)} %get-tuple-element.52.refs_1_, bf16[1024,256]{1,0:T(8,128)(2,1)S(1)} %constant_dynamic-update-slice_fusion.refs_0_.refs_2_, ...), custom_call_target="tpu_custom_call" | custom-call | tf_op jit(solution)/shard_map/begin/pallas_call | solution.py:42
  37.2 2.4 %collective-permute-done.14.rows = bf16[256,1024]{1,0:T(8,128)(2,1)S(1)} collective-permute-done((bf16[256,1024]{1,0:T(8,128)(2,1)S(1)}, bf16[256,1024]{1,0:T(8,128)(2,1)S(1)}, u32[]{:S(2)}, u32[]{:S(2)}) %collective-permute-start.14) | collective-permute-done | bytes 524320 | tf_op jit(solution)/shard_map/ppermute | solution.py:188
  39.6 2.8 %features.5 = (bf16[256,2048]{1,0:T(8,128)(2,1)S(1)}, bf16[256,512]{1,0:T(8,128)(2,1)S(1)}) custom-call(s32[3]{0:T(128)S(1)} %pad_add_fusion.place, bf16[256,1024]{1,0:T(8,128)(2,1)S(1)} %collective-permute-done.14.rows, bf16[1024,1024]{1,0:T(8,128)(2,1)S(1)} %copy-done, bf16[1024,1024]{1,0:T(8,128)(2,1)S(1)} %collective-permute-done.1.w_other, ...), custom_call_target="tpu_custom_call" | custom-call | tf_op jit(solution)/shard_map/features/pallas_call | solution.py:42
  42.5 1.3 %meet.5.refs_2_ = bf16[256,1024]{1,0:T(8,128)(2,1)S(1)} custom-call(s32[3]{0:T(128)S(1)} %pad_add_fusion.place, bf16[256,2048]{1,0:T(8,128)(2,1)S(1)} %get-tuple-element.67.feats, bf16[512,2048]{1,0:T(8,128)(2,1)S(1)} %round.1.inverse), custom_call_target="tpu_custom_call" | custom-call | tf_op jit(solution)/shard_map/meet/pallas_call | solution.py:42
  43.9 2.0 %collective-permute-start.17 = (bf16[128,1024]{1,0:T(8,128)(2,1)S(1)}, bf16[128,1024]{1,0:T(8,128)(2,1)S(1)}, u32[]{:S(2)}, u32[]{:S(2)}) collective-permute-start(bf16[128,1024]{1,0:T(8,128)(2,1)S(1)} %slice.24), channel_id=1, source_target_pairs={{4,8},{8,4},{12,14},{14,12},{10,6},{6,10},{2,0},{0,2},{1,5},{5,1},... | collective-permute-start | bytes 786440 | tf_op jit(solution)/shard_map/ppermute | solution.py:188
  47.6 2.7 %collective-permute-done.17.rows = bf16[128,1024]{1,0:T(8,128)(2,1)S(1)} collective-permute-done((bf16[128,1024]{1,0:T(8,128)(2,1)S(1)}, bf16[128,1024]{1,0:T(8,128)(2,1)S(1)}, u32[]{:S(2)}, u32[]{:S(2)}) %collective-permute-start.17) | collective-permute-done | bytes 262176 | tf_op jit(solution)/shard_map/ppermute | solution.py:188
  50.3 2.6 %block.3 = (bf16[128,1024]{1,0:T(8,128)(2,1)S(1)}, bf16[128,512]{1,0:T(8,128)(2,1)S(1)}) custom-call(s32[3]{0:T(128)S(1)} %pad_add_fusion.place, bf16[128,1024]{1,0:T(8,128)(2,1)S(1)} %collective-permute-done.17.rows, bf16[1024,1024]{1,0:T(8,128)(2,1)S(1)} %copy-done, bf16[1024,1024]{1,0:T(8,128)(2,1)S(1)} %collective-permute-done.1.w_other, ...), custom_call_target="tpu_custom_call" | custom-call | tf_op jit(solution)/shard_map/block/pallas_call | solution.py:42
  57.4 1.9 %collective-permute-start.22 = (bf16[512,256]{1,0:T(8,128)(2,1)S(1)}, bf16[512,256]{1,0:T(8,128)(2,1)S(1)}, u32[]{:S(2)}, u32[]{:S(2)}) collective-permute-start(bf16[512,256]{1,0:T(8,128)(2,1)S(1)} %change.3), channel_id=1, source_target_pairs={{4,8},{8,4},{12,14},{14,12},{10,6},{6,10},{2,0},{0,2},{1,5},{5,1},... | collective-permute-start | bytes 786440 | tf_op jit(solution)/shard_map/ppermute | solution.py:188
  61.7 1.7 %collective-permute-start.25 = (bf16[512,256]{1,0:T(8,128)(2,1)S(1)}, bf16[512,256]{1,0:T(8,128)(2,1)S(1)}, u32[]{:S(2)}, u32[]{:S(2)}) collective-permute-start(bf16[512,256]{1,0:T(8,128)(2,1)S(1)} %get-tuple-element.84), channel_id=1, source_target_pairs={{0,4},{4,0},{8,12},{12,8},{14,10},{10,14},{6,2},{2,6},{5,9},{9,5},... | collective-permute-start | bytes 786440 | tf_op jit(solution)/shard_map/ppermute | solution.py:188
  63.9 2.0 %collective-permute-start.24 = (bf16[512,256]{1,0:T(8,128)(2,1)S(1)}, bf16[512,256]{1,0:T(8,128)(2,1)S(1)}, u32[]{:S(2)}, u32[]{:S(2)}) collective-permute-start(bf16[512,256]{1,0:T(8,128)(2,1)S(1)} %add_convert_fusion.5), channel_id=1, source_target_pairs={{0,4},{4,0},{8,12},{12,8},{14,10},{10,14},{6,2},{2,6},{5,9},{9,5},... | collective-permute-start | bytes 786440 | tf_op jit(solution)/shard_map/ppermute | solution.py:188
  65.9 2.3 %collective-permute-done.25 = bf16[512,256]{1,0:T(8,128)(2,1)S(1)} collective-permute-done((bf16[512,256]{1,0:T(8,128)(2,1)S(1)}, bf16[512,256]{1,0:T(8,128)(2,1)S(1)}, u32[]{:S(2)}, u32[]{:S(2)}) %collective-permute-start.25) | collective-permute-done | bytes 262176 | tf_op jit(solution)/shard_map/ppermute | solution.py:188
  69.5 2.4 %collective-permute-done.24 = bf16[512,256]{1,0:T(8,128)(2,1)S(1)} collective-permute-done((bf16[512,256]{1,0:T(8,128)(2,1)S(1)}, bf16[512,256]{1,0:T(8,128)(2,1)S(1)}, u32[]{:S(2)}, u32[]{:S(2)}) %collective-permute-start.24) | collective-permute-done | bytes 262176 | tf_op jit(solution)/shard_map/ppermute | solution.py:188
  73.0 1.7 %collective-permute-done.27 = bf16[512,256]{1,0:T(8,128)(2,1)S(1)} collective-permute-done((bf16[512,256]{1,0:T(8,128)(2,1)S(1)}, bf16[512,256]{1,0:T(8,128)(2,1)S(1)}, u32[]{:S(2)}, u32[]{:S(2)}) %collective-permute-start.27) | collective-permute-done | bytes 262176 | tf_op jit(solution)/shard_map/ppermute | solution.py:188
  74.8 1.7 %collective-permute-start.29 = (bf16[512,256]{1,0:T(8,128)(2,1)S(1)}, bf16[512,256]{1,0:T(8,128)(2,1)S(1)}, u32[]{:S(2)}, u32[]{:S(2)}) collective-permute-start(bf16[512,256]{1,0:T(8,128)(2,1)S(1)} %add_convert_fusion.2), channel_id=1, source_target_pairs={{0,4},{4,0},{8,12},{12,8},{14,10},{10,14},{6,2},{2,6},{5,9},{9,5},... | collective-permute-start | bytes 786440 | tf_op jit(solution)/shard_map/ppermute | solution.py:188
  76.5 3.7 %collective-permute-done.26 = bf16[512,256]{1,0:T(8,128)(2,1)S(1)} collective-permute-done((bf16[512,256]{1,0:T(8,128)(2,1)S(1)}, bf16[512,256]{1,0:T(8,128)(2,1)S(1)}, u32[]{:S(2)}, u32[]{:S(2)}) %collective-permute-start.26) | collective-permute-done | bytes 262176 | tf_op jit(solution)/shard_map/ppermute | solution.py:188
  80.3 2.2 %collective-permute-start.28 = (bf16[512,256]{1,0:T(8,128)(2,1)S(1)}, bf16[512,256]{1,0:T(8,128)(2,1)S(1)}, u32[]{:S(2)}, u32[]{:S(2)}) collective-permute-start(bf16[512,256]{1,0:T(8,128)(2,1)S(1)} %add_convert_fusion.1), channel_id=1, source_target_pairs={{0,4},{4,0},{8,12},{12,8},{14,10},{10,14},{6,2},{2,6},{5,9},{9,5},... | collective-permute-start | bytes 786440 | tf_op jit(solution)/shard_map/ppermute | solution.py:188
  82.5 4.3 %collective-permute-done.28 = bf16[512,256]{1,0:T(8,128)(2,1)S(1)} collective-permute-done((bf16[512,256]{1,0:T(8,128)(2,1)S(1)}, bf16[512,256]{1,0:T(8,128)(2,1)S(1)}, u32[]{:S(2)}, u32[]{:S(2)}) %collective-permute-start.28) | collective-permute-done | bytes 262176 | tf_op jit(solution)/shard_map/ppermute | solution.py:188
  86.9 1.6 %collective-permute-start.31 = (bf16[512,256]{1,0:T(8,128)(2,1)S(1)}, bf16[512,256]{1,0:T(8,128)(2,1)S(1)}, u32[]{:S(2)}, u32[]{:S(2)}) collective-permute-start(bf16[512,256]{1,0:T(8,128)(2,1)S(1)} %add_convert_fusion.change), channel_id=1, source_target_pairs={{0,2},{2,0},{1,3},{3,1},{4,6},{6,4},{5,7},{7,5},{8,10},{10,8},{9,1... | collective-permute-start | bytes 786440 | tf_op jit(solution)/shard_map/ppermute | solution.py:188
  89.7 1.4 %apply.2.refs_0_ = f32[500,512]{1,0:T(8,128)} custom-call(s32[3]{0:T(128)S(1)} %pad_add_fusion.place, f32[500,512]{1,0:T(8,128)S(1)} %bitcast.14, bf16[512,256]{1,0:T(8,128)(2,1)S(1)} %add_convert_fusion.change), custom_call_target="tpu_custom_call" | custom-call | tf_op jit(solution)/shard_map/apply/pallas_call | solution.py:42
  91.1 2.3 %collective-permute-done.31.change = bf16[512,256]{1,0:T(8,128)(2,1)S(1)} collective-permute-done((bf16[512,256]{1,0:T(8,128)(2,1)S(1)}, bf16[512,256]{1,0:T(8,128)(2,1)S(1)}, u32[]{:S(2)}, u32[]{:S(2)}) %collective-permute-start.31) | collective-permute-done | bytes 262176 | tf_op jit(solution)/shard_map/ppermute | solution.py:188
  93.4 1.4 %apply.3 = f32[500,512]{1,0:T(8,128)} custom-call(s32[3]{0:T(128)S(1)} %pad_add_fusion.place, f32[500,512]{1,0:T(8,128)S(1)} %bitcast.15, bf16[512,256]{1,0:T(8,128)(2,1)S(1)} %collective-permute-done.31.change, f32[500,512]{1,0:T(8,128)} %apply.2.refs_0_), custom_call_target="tpu_custom_call", output_to_operand_aliasing={{}: (3, {})} | custom-call | tf_op jit(solution)/shard_map/apply/pallas_call | solution.py:42
  (78 shorter events, 22.0 us)
Async XLA Ops:
  0.6 10.8 %collective-permute-start.1 = (bf16[1024,1024]{1,0:T(8,128)(2,1)}, bf16[1024,1024]{1,0:T(8,128)(2,1)S(1)}, u32[]{:S(2)}, u32[]{:S(2)}) collective-permute-start(bf16[1024,1024]{1,0:T(8,128)(2,1)} %w_own.9), channel_id=1, source_target_pairs={{0,1},{1,0},{2,3},{3,2},{4,5},{5,4},{6,7},{7,6},{8,9},{9,8},{10,11... | collective-permute-start | bytes 6291464 | tf_op jit(solution)/shard_map/ppermute | solution.py:188
  3.2 2.2 %collective-permute-start = (bf16[512,256]{1,0:T(8,128)(2,1)S(1)}, bf16[512,256]{1,0:T(8,128)(2,1)S(1)}, u32[]{:S(2)}, u32[]{:S(2)}) collective-permute-start(bf16[512,256]{1,0:T(8,128)(2,1)S(1)} %get-tuple-element.49), channel_id=1, source_target_pairs={{0,1},{1,0},{2,3},{3,2},{4,5},{5,4},{6,7},{7,6},{8,9},{9,8},{10,11... | collective-permute-start | bytes 786440 | tf_op jit(solution)/shard_map/ppermute | solution.py:188
  5.3 10.1 %collective-permute-start.5 = (bf16[256,1024]{1,0:T(8,128)(2,1)S(1)}, bf16[256,1024]{1,0:T(8,128)(2,1)S(1)}, u32[]{:S(2)}, u32[]{:S(2)}) collective-permute-start(bf16[256,1024]{1,0:T(8,128)(2,1)S(1)} %get-tuple-element.51.rows), channel_id=1, source_target_pairs={{0,4},{4,0},{8,12},{12,8},{14,10},{10,14},{6,2},{2,6},{5,9},{9,5},... | collective-permute-start | bytes 1572872 | tf_op jit(solution)/shard_map/ppermute | solution.py:188
  8.3 13.3 %collective-permute-start.4 = (bf16[1024,256]{1,0:T(8,128)(2,1)S(1)}, bf16[1024,256]{1,0:T(8,128)(2,1)S(1)}, u32[]{:S(2)}, u32[]{:S(2)}) collective-permute-start(bf16[1024,256]{1,0:T(8,128)(2,1)S(1)} %constant_dynamic-update-slice_fusion.refs_0_.refs_2_), channel_id=1, source_target_pairs={{0,4},{4,0},{8,12},{12,8},{14,10},{10,14},{6,2},{2,6},{5,9},{9,5},... | collective-permute-start | bytes 1572872 | tf_op jit(solution)/shard_map/ppermute | solution.py:188
  8.4 3.0 %collective-permute-start.2 = (bf16[1,1024]{1,0:T(2,128)(2,1)S(1)}, bf16[1,1024]{1,0:T(2,128)(2,1)S(1)}, u32[]{:S(2)}, u32[]{:S(2)}) collective-permute-start(bf16[1,1024]{1,0:T(2,128)(2,1)S(1)} %broadcast_in_dim.7.p_own), channel_id=1, source_target_pairs={{0,1},{1,0},{2,3},{3,2},{4,5},{5,4},{6,7},{7,6},{8,9},{9,8},{10,11... | collective-permute-start | bytes 6152 | tf_op jit(solution)/shard_map/ppermute | solution.py:188
  18.3 9.2 %collective-permute-start.9 = (bf16[256,1024]{1,0:T(8,128)(2,1)S(1)}, bf16[256,1024]{1,0:T(8,128)(2,1)S(1)}, u32[]{:S(2)}, u32[]{:S(2)}) collective-permute-start(bf16[256,1024]{1,0:T(8,128)(2,1)S(1)} %collective-permute-done.5.rows), channel_id=1, source_target_pairs={{4,8},{8,4},{12,14},{14,12},{10,6},{6,10},{2,0},{0,2},{1,5},{5,1},... | collective-permute-start | bytes 1572872 | tf_op jit(solution)/shard_map/ppermute | solution.py:188
  21.6 12.2 %collective-permute-start.7 = (bf16[256,1024]{1,0:T(8,128)(2,1)S(1)}, bf16[256,1024]{1,0:T(8,128)(2,1)S(1)}, u32[]{:S(2)}, u32[]{:S(2)}) collective-permute-start(bf16[256,1024]{1,0:T(8,128)(2,1)S(1)} %meet.3.refs_5_), channel_id=1, source_target_pairs={{0,1},{1,0},{2,3},{3,2},{4,5},{5,4},{6,7},{7,6},{8,9},{9,8},{10,11... | collective-permute-start | bytes 1572872 | tf_op jit(solution)/shard_map/ppermute | solution.py:188
  21.7 13.6 %collective-permute-start.8 = (bf16[1024,256]{1,0:T(8,128)(2,1)S(1)}, bf16[1024,256]{1,0:T(8,128)(2,1)S(1)}, u32[]{:S(2)}, u32[]{:S(2)}) collective-permute-start(bf16[1024,256]{1,0:T(8,128)(2,1)S(1)} %collective-permute-done.4.refs_4_), channel_id=1, source_target_pairs={{4,8},{8,4},{12,14},{14,12},{10,6},{6,10},{2,0},{0,2},{1,5},{5,1},... | collective-permute-start | bytes 1572872 | tf_op jit(solution)/shard_map/ppermute | solution.py:188
  23.2 1.3 %collective-permute-start.10 = (bf16[128,512]{1,0:T(8,128)(2,1)S(1)}, bf16[128,512]{1,0:T(8,128)(2,1)S(1)}, u32[]{:S(2)}, u32[]{:S(2)}) collective-permute-start(bf16[128,512]{1,0:T(8,128)(2,1)S(1)} %get-tuple-element.59.refs_3_), channel_id=1, source_target_pairs={{0,1},{1,0},{2,3},{3,2},{4,5},{5,4},{6,7},{7,6},{8,9},{9,8},{10,11... | collective-permute-start | bytes 393224 | tf_op jit(solution)/shard_map/ppermute | solution.py:188
  23.6 10.2 %collective-permute-start.6 = (bf16[512,256]{1,0:T(8,128)(2,1)S(1)}, bf16[512,256]{1,0:T(8,128)(2,1)S(1)}, u32[]{:S(2)}, u32[]{:S(2)}) collective-permute-start(bf16[512,256]{1,0:T(8,128)(2,1)S(1)} %slice.21), channel_id=1, source_target_pairs={{0,1},{1,0},{2,3},{3,2},{4,5},{5,4},{6,7},{7,6},{8,9},{9,8},{10,11... | collective-permute-start | bytes 786440 | tf_op jit(solution)/shard_map/ppermute | solution.py:188
  24.6 9.2 %collective-permute-start.3 = (bf16[128,1024]{1,0:T(8,128)(2,1)S(1)}, bf16[128,1024]{1,0:T(8,128)(2,1)S(1)}, u32[]{:S(2)}, u32[]{:S(2)}) collective-permute-start(bf16[128,1024]{1,0:T(8,128)(2,1)S(1)} %get-tuple-element.52.refs_1_), channel_id=1, source_target_pairs={{0,1},{1,0},{2,3},{3,2},{4,5},{5,4},{6,7},{7,6},{8,9},{9,8},{10,11... | collective-permute-start | bytes 786440 | tf_op jit(solution)/shard_map/ppermute | solution.py:188
  30.4 9.3 %collective-permute-start.14 = (bf16[256,1024]{1,0:T(8,128)(2,1)S(1)}, bf16[256,1024]{1,0:T(8,128)(2,1)S(1)}, u32[]{:S(2)}, u32[]{:S(2)}) collective-permute-start(bf16[256,1024]{1,0:T(8,128)(2,1)S(1)} %collective-permute-done.9.rows), channel_id=1, source_target_pairs={{0,4},{4,0},{8,12},{12,8},{14,10},{10,14},{6,2},{2,6},{5,9},{9,5},... | collective-permute-start | bytes 1572872 | tf_op jit(solution)/shard_map/ppermute | solution.py:188
  35.3 10.6 %collective-permute-start.12 = (bf16[256,1024]{1,0:T(8,128)(2,1)S(1)}, bf16[256,1024]{1,0:T(8,128)(2,1)S(1)}, u32[]{:S(2)}, u32[]{:S(2)}) collective-permute-start(bf16[256,1024]{1,0:T(8,128)(2,1)S(1)} %meet.4.refs_2_), channel_id=1, source_target_pairs={{0,1},{1,0},{2,3},{3,2},{4,5},{5,4},{6,7},{7,6},{8,9},{9,8},{10,11... | collective-permute-start | bytes 1572872 | tf_op jit(solution)/shard_map/ppermute | solution.py:188
  35.4 11.7 %collective-permute-start.13 = (bf16[1024,256]{1,0:T(8,128)(2,1)S(1)}, bf16[1024,256]{1,0:T(8,128)(2,1)S(1)}, u32[]{:S(2)}, u32[]{:S(2)}) collective-permute-start(bf16[1024,256]{1,0:T(8,128)(2,1)S(1)} %collective-permute-done.8.refs_1_), channel_id=1, source_target_pairs={{0,4},{4,0},{8,12},{12,8},{14,10},{10,14},{6,2},{2,6},{5,9},{9,5},... | collective-permute-start | bytes 1572872 | tf_op jit(solution)/shard_map/ppermute | solution.py:188
  36.0 9.9 %collective-permute-start.11 = (bf16[512,256]{1,0:T(8,128)(2,1)S(1)}, bf16[512,256]{1,0:T(8,128)(2,1)S(1)}, u32[]{:S(2)}, u32[]{:S(2)}) collective-permute-start(bf16[512,256]{1,0:T(8,128)(2,1)S(1)} %slice.22), channel_id=1, source_target_pairs={{0,1},{1,0},{2,3},{3,2},{4,5},{5,4},{6,7},{7,6},{8,9},{9,8},{10,11... | collective-permute-start | bytes 786440 | tf_op jit(solution)/shard_map/ppermute | solution.py:188
  43.8 9.9 %collective-permute-start.16 = (bf16[256,1024]{1,0:T(8,128)(2,1)S(1)}, bf16[256,1024]{1,0:T(8,128)(2,1)S(1)}, u32[]{:S(2)}, u32[]{:S(2)}) collective-permute-start(bf16[256,1024]{1,0:T(8,128)(2,1)S(1)} %meet.5.refs_2_), channel_id=1, source_target_pairs={{0,1},{1,0},{2,3},{3,2},{4,5},{5,4},{6,7},{7,6},{8,9},{9,8},{10,11... | collective-permute-start | bytes 1572872 | tf_op jit(solution)/shard_map/ppermute | solution.py:188
  43.9 6.4 %collective-permute-start.17 = (bf16[128,1024]{1,0:T(8,128)(2,1)S(1)}, bf16[128,1024]{1,0:T(8,128)(2,1)S(1)}, u32[]{:S(2)}, u32[]{:S(2)}) collective-permute-start(bf16[128,1024]{1,0:T(8,128)(2,1)S(1)} %slice.24), channel_id=1, source_target_pairs={{4,8},{8,4},{12,14},{14,12},{10,6},{6,10},{2,0},{0,2},{1,5},{5,1},... | collective-permute-start | bytes 786440 | tf_op jit(solution)/shard_map/ppermute | solution.py:188
  47.2 6.4 %collective-permute-start.19 = (bf16[1024,128]{1,0:T(8,128)(2,1)S(1)}, bf16[1024,128]{1,0:T(8,128)(2,1)S(1)}, u32[]{:S(2)}, u32[]{:S(2)}) collective-permute-start(bf16[1024,128]{1,0:T(8,128)(2,1)S(1)} %slice.25), channel_id=1, source_target_pairs={{4,8},{8,4},{12,14},{14,12},{10,6},{6,10},{2,0},{0,2},{1,5},{5,1},... | collective-permute-start | bytes 786440 | tf_op jit(solution)/shard_map/ppermute | solution.py:188
  47.3 6.3 %collective-permute-start.15 = (bf16[512,256]{1,0:T(8,128)(2,1)S(1)}, bf16[512,256]{1,0:T(8,128)(2,1)S(1)}, u32[]{:S(2)}, u32[]{:S(2)}) collective-permute-start(bf16[512,256]{1,0:T(8,128)(2,1)S(1)} %slice.23), channel_id=1, source_target_pairs={{0,1},{1,0},{2,3},{3,2},{4,5},{5,4},{6,7},{7,6},{8,9},{9,8},{10,11... | collective-permute-start | bytes 786440 | tf_op jit(solution)/shard_map/ppermute | solution.py:188
  52.9 2.1 %collective-permute-start.21 = (bf16[128,1024]{1,0:T(8,128)(2,1)S(1)}, bf16[128,1024]{1,0:T(8,128)(2,1)S(1)}, u32[]{:S(2)}, u32[]{:S(2)}) collective-permute-start(bf16[128,1024]{1,0:T(8,128)(2,1)S(1)} %get-tuple-element.74.refs_1_), channel_id=1, source_target_pairs={{0,1},{1,0},{2,3},{3,2},{4,5},{5,4},{6,7},{7,6},{8,9},{9,8},{10,11... | collective-permute-start | bytes 786440 | tf_op jit(solution)/shard_map/ppermute | solution.py:188
  53.0 1.9 %collective-permute-start.18 = (bf16[128,512]{1,0:T(8,128)(2,1)S(1)}, bf16[128,512]{1,0:T(8,128)(2,1)S(1)}, u32[]{:S(2)}, u32[]{:S(2)}) collective-permute-start(bf16[128,512]{1,0:T(8,128)(2,1)S(1)} %get-tuple-element.72.refs_0_), channel_id=1, source_target_pairs={{0,1},{1,0},{2,3},{3,2},{4,5},{5,4},{6,7},{7,6},{8,9},{9,8},{10,11... | collective-permute-start | bytes 393224 | tf_op jit(solution)/shard_map/ppermute | solution.py:188
  53.6 1.4 %collective-permute-start.20 = (bf16[512,128]{1,0:T(8,128)(2,1)S(1)}, bf16[512,128]{1,0:T(8,128)(2,1)S(1)}, u32[]{:S(2)}, u32[]{:S(2)}) collective-permute-start(bf16[512,128]{1,0:T(8,128)(2,1)S(1)} %slice.28), channel_id=1, source_target_pairs={{0,1},{1,0},{2,3},{3,2},{4,5},{5,4},{6,7},{7,6},{8,9},{9,8},{10,11... | collective-permute-start | bytes 393224 | tf_op jit(solution)/shard_map/ppermute | solution.py:188
  56.0 4.6 %collective-permute-start.23 = (bf16[512,512]{1,0:T(8,128)(2,1)S(1)}, bf16[512,512]{1,0:T(8,128)(2,1)S(1)}, u32[]{:S(2)}, u32[]{:S(2)}) collective-permute-start(bf16[512,512]{1,0:T(8,128)(2,1)S(1)} %get-tuple-element.77.sent), channel_id=1, source_target_pairs={{0,1},{1,0},{2,3},{3,2},{4,5},{5,4},{6,7},{7,6},{8,9},{9,8},{10,11... | collective-permute-start | bytes 1572872 | tf_op jit(solution)/shard_map/ppermute | solution.py:188
  57.4 6.4 %collective-permute-start.22 = (bf16[512,256]{1,0:T(8,128)(2,1)S(1)}, bf16[512,256]{1,0:T(8,128)(2,1)S(1)}, u32[]{:S(2)}, u32[]{:S(2)}) collective-permute-start(bf16[512,256]{1,0:T(8,128)(2,1)S(1)} %change.3), channel_id=1, source_target_pairs={{4,8},{8,4},{12,14},{14,12},{10,6},{6,10},{2,0},{0,2},{1,5},{5,1},... | collective-permute-start | bytes 786440 | tf_op jit(solution)/shard_map/ppermute | solution.py:188
  61.7 6.4 %collective-permute-start.25 = (bf16[512,256]{1,0:T(8,128)(2,1)S(1)}, bf16[512,256]{1,0:T(8,128)(2,1)S(1)}, u32[]{:S(2)}, u32[]{:S(2)}) collective-permute-start(bf16[512,256]{1,0:T(8,128)(2,1)S(1)} %get-tuple-element.84), channel_id=1, source_target_pairs={{0,4},{4,0},{8,12},{12,8},{14,10},{10,14},{6,2},{2,6},{5,9},{9,5},... | collective-permute-start | bytes 786440 | tf_op jit(solution)/shard_map/ppermute | solution.py:188
  63.9 8.0 %collective-permute-start.24 = (bf16[512,256]{1,0:T(8,128)(2,1)S(1)}, bf16[512,256]{1,0:T(8,128)(2,1)S(1)}, u32[]{:S(2)}, u32[]{:S(2)}) collective-permute-start(bf16[512,256]{1,0:T(8,128)(2,1)S(1)} %add_convert_fusion.5), channel_id=1, source_target_pairs={{0,4},{4,0},{8,12},{12,8},{14,10},{10,14},{6,2},{2,6},{5,9},{9,5},... | collective-permute-start | bytes 786440 | tf_op jit(solution)/shard_map/ppermute | solution.py:188
  68.3 6.4 %collective-permute-start.27 = (bf16[512,256]{1,0:T(8,128)(2,1)S(1)}, bf16[512,256]{1,0:T(8,128)(2,1)S(1)}, u32[]{:S(2)}, u32[]{:S(2)}) collective-permute-start(bf16[512,256]{1,0:T(8,128)(2,1)S(1)} %add_convert_fusion.4), channel_id=1, source_target_pairs={{4,8},{8,4},{12,14},{14,12},{10,6},{6,10},{2,0},{0,2},{1,5},{5,1},... | collective-permute-start | bytes 786440 | tf_op jit(solution)/shard_map/ppermute | solution.py:188
  72.0 8.2 %collective-permute-start.26 = (bf16[512,256]{1,0:T(8,128)(2,1)S(1)}, bf16[512,256]{1,0:T(8,128)(2,1)S(1)}, u32[]{:S(2)}, u32[]{:S(2)}) collective-permute-start(bf16[512,256]{1,0:T(8,128)(2,1)S(1)} %add_convert_fusion.3), channel_id=1, source_target_pairs={{4,8},{8,4},{12,14},{14,12},{10,6},{6,10},{2,0},{0,2},{1,5},{5,1},... | collective-permute-start | bytes 786440 | tf_op jit(solution)/shard_map/ppermute | solution.py:188
  74.8 7.7 %collective-permute-start.29 = (bf16[512,256]{1,0:T(8,128)(2,1)S(1)}, bf16[512,256]{1,0:T(8,128)(2,1)S(1)}, u32[]{:S(2)}, u32[]{:S(2)}) collective-permute-start(bf16[512,256]{1,0:T(8,128)(2,1)S(1)} %add_convert_fusion.2), channel_id=1, source_target_pairs={{0,4},{4,0},{8,12},{12,8},{14,10},{10,14},{6,2},{2,6},{5,9},{9,5},... | collective-permute-start | bytes 786440 | tf_op jit(solution)/shard_map/ppermute | solution.py:188
  80.3 6.6 %collective-permute-start.28 = (bf16[512,256]{1,0:T(8,128)(2,1)S(1)}, bf16[512,256]{1,0:T(8,128)(2,1)S(1)}, u32[]{:S(2)}, u32[]{:S(2)}) collective-permute-start(bf16[512,256]{1,0:T(8,128)(2,1)S(1)} %add_convert_fusion.1), channel_id=1, source_target_pairs={{0,4},{4,0},{8,12},{12,8},{14,10},{10,14},{6,2},{2,6},{5,9},{9,5},... | collective-permute-start | bytes 786440 | tf_op jit(solution)/shard_map/ppermute | solution.py:188
  82.5 4.4 %collective-permute-start.30 = (bf16[512,256]{1,0:T(8,128)(2,1)S(1)}, bf16[512,256]{1,0:T(8,128)(2,1)S(1)}, u32[]{:S(2)}, u32[]{:S(2)}) collective-permute-start(bf16[512,256]{1,0:T(8,128)(2,1)S(1)} %collective-permute-done.29), channel_id=1, source_target_pairs={{0,1},{1,0},{2,3},{3,2},{4,5},{5,4},{6,7},{7,6},{8,9},{9,8},{10,11... | collective-permute-start | bytes 786440 | tf_op jit(solution)/shard_map/ppermute | solution.py:188
  86.9 6.4 %collective-permute-start.31 = (bf16[512,256]{1,0:T(8,128)(2,1)S(1)}, bf16[512,256]{1,0:T(8,128)(2,1)S(1)}, u32[]{:S(2)}, u32[]{:S(2)}) collective-permute-start(bf16[512,256]{1,0:T(8,128)(2,1)S(1)} %add_convert_fusion.change), channel_id=1, source_target_pairs={{0,2},{2,0},{1,3},{3,1},{4,6},{6,4},{5,7},{7,5},{8,10},{10,8},{9,1... | collective-permute-start | bytes 786440 | tf_op jit(solution)/shard_map/ppermute | solution.py:188
  (5 other events, 41.2 us)

commit v19 on v18

--- a/solution.py
+++ b/solution.py
@@ -285,7 +285,7 @@
         )
 
     hop = lambda ahead, came: (ahead + came.astype(F32)).astype(BF16)
-    (first,) = changes(sent, [(f4, f4_other)], (whole,))
+    first = dot_nt(sent, jnp.concatenate([f4, f4_other], axis=0)).astype(BF16)
     (sent_other,) = after((C(sent),), first)
     ahead = changes(after((sent,), first)[0], [(f3,), (f2,), (f1,), (f0, f0_other)], (wide,) * 4)
     first = T(first)

time: 96.1 us -> 95.5 us (level)
    pallas_call x19 -> x18, Pallas kernels: 31.1 us -> 30.3 us  [call(): pl.pallas_call(kernel, out_shape=out_shapes, in_specs=[pl.BlockSpec(memor...]
where the time goes in v19:
time: 95.5 us; the launch traced here: 94.4 us
  Pallas kernels  30.3 us (32%)
  starting transfers between devices  29.1 us (30%)
  waiting for transfers between devices  28.7 us (30%)
  local copies, waits for them, and re-layouts  3.16 us (3%)
  other arithmetic  1.63 us (2%)
  between operations  1.2 us (1%)
    pallas_call x18, Pallas kernels, call(): pl.pallas_call(kernel, out_shape=out_shapes, in_specs=[pl.BlockSpec(memor...  30.3 us
    ppermute x32, starting transfers between devices, swap(): lax.ppermute(x, axes, [p for a, b in pairs for p in ((a, b), (b, a))])  29.1 us
    ppermute x32, waiting for transfers between devices, swap(): lax.ppermute(x, axes, [p for a, b in pairs for p in ((a, b), (b, a))])  28.7 us
    unnamed x11, local copies, waits for them, and re-layouts  3.04 us
  transfers between devices with their start and end apart: 32, of which 14 were waited for; matrix products, arithmetic and copies ran while one was open for 2% of the time, Pallas kernels for 30%

profile of v19, /device:TPU:0, one launch (start us, length us, event | category | flops | bytes accessed | tf_op | source)
XLA Modules:
  0.0 94.4 jit_solution(4058734253747300058)
XLA Ops:
  1.2 1.9 %prepare.1 = (bf16[256,1024]{1,0:T(8,128)(2,1)S(1)}, bf16[512,256]{1,0:T(8,128)(2,1)S(1)}, bf16[512,256]{1,0:T(8,128)(2,1)S(1)}) custom-call(s32[3]{0:T(128)S(1)} %pad_add_fusion.place, bf16[512,1024]{1,0:T(8,128)(2,1)} %inputs.1, s32[1,512]{1,0:T(1,128)} %bitcast.19, f32[500,512]{1,0:T(8,128)} %bitcast.14), custom_call_target="tpu_custom_call" | custom-call | tf_op jit(solution)/shard_map/prepare/pallas_call | solution.py:42
  3.3 2.0 %collective-permute-done = bf16[512,256]{1,0:T(8,128)(2,1)S(1)} collective-permute-done((bf16[512,256]{1,0:T(8,128)(2,1)S(1)}, bf16[512,256]{1,0:T(8,128)(2,1)S(1)}, u32[]{:S(2)}, u32[]{:S(2)}) %collective-permute-start) | collective-permute-done | bytes 262176 | tf_op jit(solution)/shard_map/ppermute | solution.py:188
  5.3 2.9 %collective-permute-start.5 = (bf16[256,1024]{1,0:T(8,128)(2,1)S(1)}, bf16[256,1024]{1,0:T(8,128)(2,1)S(1)}, u32[]{:S(2)}, u32[]{:S(2)}) collective-permute-start(bf16[256,1024]{1,0:T(8,128)(2,1)S(1)} %get-tuple-element.51.rows), channel_id=1, source_target_pairs={{0,4},{4,0},{8,12},{12,8},{14,10},{10,14},{6,2},{2,6},{5,9},{9,5},... | collective-permute-start | bytes 1572872 | tf_op jit(solution)/shard_map/ppermute | solution.py:188
  8.5 2.2 %copy-done.2 = f32[1,512,2048]{2,1,0:T(8,128)S(1)} copy-done((f32[1,512,2048]{2,1,0:T(8,128)S(1)}, f32[1,512,2048]{2,1,0:T(8,128)}, u32[]{:S(2)}) %copy-start.2) | copy-done | bytes 4194328
  12.3 2.4 %block.2 = (bf16[128,1024]{1,0:T(8,128)(2,1)S(1)}, bf16[128,512]{1,0:T(8,128)(2,1)S(1)}) custom-call(s32[3]{0:T(128)S(1)} %pad_add_fusion.place, bf16[256,1024]{1,0:T(8,128)(2,1)S(1)} %get-tuple-element.51.rows, bf16[1024,1024]{1,0:T(8,128)(2,1)S(1)} %copy-done, bf16[1024,1024]{1,0:T(8,128)(2,1)S(1)} %collective-permute-done.1.w_other, ...), custom_call_target="tpu_custom_call" | custom-call | tf_op jit(solution)/shard_map/block/pallas_call | solution.py:42
  15.4 2.8 %features.3 = (bf16[256,2048]{1,0:T(8,128)(2,1)S(1)}, bf16[256,512]{1,0:T(8,128)(2,1)S(1)}) custom-call(s32[3]{0:T(128)S(1)} %pad_add_fusion.place, bf16[256,1024]{1,0:T(8,128)(2,1)S(1)} %collective-permute-done.5.rows, bf16[1024,1024]{1,0:T(8,128)(2,1)S(1)} %copy-done, bf16[1024,1024]{1,0:T(8,128)(2,1)S(1)} %collective-permute-done.1.w_other, ...), custom_call_target="tpu_custom_call" | custom-call | tf_op jit(solution)/shard_map/features/pallas_call | solution.py:42
  18.3 2.0 %collective-permute-start.9 = (bf16[256,1024]{1,0:T(8,128)(2,1)S(1)}, bf16[256,1024]{1,0:T(8,128)(2,1)S(1)}, u32[]{:S(2)}, u32[]{:S(2)}) collective-permute-start(bf16[256,1024]{1,0:T(8,128)(2,1)S(1)} %collective-permute-done.5.rows), channel_id=1, source_target_pairs={{4,8},{8,4},{12,14},{14,12},{10,6},{6,10},{2,0},{0,2},{1,5},{5,1},... | collective-permute-start | bytes 1572872 | tf_op jit(solution)/shard_map/ppermute | solution.py:188
  21.7 1.6 %collective-permute-start.8 = (bf16[1024,256]{1,0:T(8,128)(2,1)S(1)}, bf16[1024,256]{1,0:T(8,128)(2,1)S(1)}, u32[]{:S(2)}, u32[]{:S(2)}) collective-permute-start(bf16[1024,256]{1,0:T(8,128)(2,1)S(1)} %collective-permute-done.4.refs_4_), channel_id=1, source_target_pairs={{4,8},{8,4},{12,14},{14,12},{10,6},{6,10},{2,0},{0,2},{1,5},{5,1},... | collective-permute-start | bytes 1572872 | tf_op jit(solution)/shard_map/ppermute | solution.py:188
  24.9 2.6 %collective-permute-done.9.rows = bf16[256,1024]{1,0:T(8,128)(2,1)S(1)} collective-permute-done((bf16[256,1024]{1,0:T(8,128)(2,1)S(1)}, bf16[256,1024]{1,0:T(8,128)(2,1)S(1)}, u32[]{:S(2)}, u32[]{:S(2)}) %collective-permute-start.9) | collective-permute-done | bytes 524320 | tf_op jit(solution)/shard_map/ppermute | solution.py:188
  27.5 2.8 %features.4 = (bf16[256,2048]{1,0:T(8,128)(2,1)S(1)}, bf16[256,512]{1,0:T(8,128)(2,1)S(1)}) custom-call(s32[3]{0:T(128)S(1)} %pad_add_fusion.place, bf16[256,1024]{1,0:T(8,128)(2,1)S(1)} %collective-permute-done.9.rows, bf16[1024,1024]{1,0:T(8,128)(2,1)S(1)} %copy-done, bf16[1024,1024]{1,0:T(8,128)(2,1)S(1)} %collective-permute-done.1.w_other, ...), custom_call_target="tpu_custom_call" | custom-call | tf_op jit(solution)/shard_map/features/pallas_call | solution.py:42
  30.4 2.1 %collective-permute-start.14 = (bf16[256,1024]{1,0:T(8,128)(2,1)S(1)}, bf16[256,1024]{1,0:T(8,128)(2,1)S(1)}, u32[]{:S(2)}, u32[]{:S(2)}) collective-permute-start(bf16[256,1024]{1,0:T(8,128)(2,1)S(1)} %collective-permute-done.9.rows), channel_id=1, source_target_pairs={{0,4},{4,0},{8,12},{12,8},{14,10},{10,14},{6,2},{2,6},{5,9},{9,5},... | collective-permute-start | bytes 1572872 | tf_op jit(solution)/shard_map/ppermute | solution.py:188
  33.8 1.5 %begin.3.refs_0_ = f32[512,512]{1,0:T(8,128)S(1)} custom-call(s32[3]{0:T(128)S(1)} %pad_add_fusion.place, bf16[1024,256]{1,0:T(8,128)(2,1)S(1)} %constant_dynamic-update-slice_fusion.refs_0_.refs_2_, bf16[128,1024]{1,0:T(8,128)(2,1)S(1)} %get-tuple-element.52.refs_1_, bf16[1024,256]{1,0:T(8,128)(2,1)S(1)} %constant_dynamic-update-slice_fusion.refs_0_.refs_2_, ...), custom_call_target="tpu_custom_call" | custom-call | tf_op jit(solution)/shard_map/begin/pallas_call | solution.py:42
  37.2 2.4 %collective-permute-done.14.rows = bf16[256,1024]{1,0:T(8,128)(2,1)S(1)} collective-permute-done((bf16[256,1024]{1,0:T(8,128)(2,1)S(1)}, bf16[256,1024]{1,0:T(8,128)(2,1)S(1)}, u32[]{:S(2)}, u32[]{:S(2)}) %collective-permute-start.14) | collective-permute-done | bytes 524320 | tf_op jit(solution)/shard_map/ppermute | solution.py:188
  39.6 2.8 %features.5 = (bf16[256,2048]{1,0:T(8,128)(2,1)S(1)}, bf16[256,512]{1,0:T(8,128)(2,1)S(1)}) custom-call(s32[3]{0:T(128)S(1)} %pad_add_fusion.place, bf16[256,1024]{1,0:T(8,128)(2,1)S(1)} %collective-permute-done.14.rows, bf16[1024,1024]{1,0:T(8,128)(2,1)S(1)} %copy-done, bf16[1024,1024]{1,0:T(8,128)(2,1)S(1)} %collective-permute-done.1.w_other, ...), custom_call_target="tpu_custom_call" | custom-call | tf_op jit(solution)/shard_map/features/pallas_call | solution.py:42
  42.5 1.3 %meet.5.refs_2_ = bf16[256,1024]{1,0:T(8,128)(2,1)S(1)} custom-call(s32[3]{0:T(128)S(1)} %pad_add_fusion.place, bf16[256,2048]{1,0:T(8,128)(2,1)S(1)} %get-tuple-element.67.feats, bf16[512,2048]{1,0:T(8,128)(2,1)S(1)} %round.1.inverse), custom_call_target="tpu_custom_call" | custom-call | tf_op jit(solution)/shard_map/meet/pallas_call | solution.py:42
  43.9 2.0 %collective-permute-start.17 = (bf16[128,1024]{1,0:T(8,128)(2,1)S(1)}, bf16[128,1024]{1,0:T(8,128)(2,1)S(1)}, u32[]{:S(2)}, u32[]{:S(2)}) collective-permute-start(bf16[128,1024]{1,0:T(8,128)(2,1)S(1)} %slice.24), channel_id=1, source_target_pairs={{4,8},{8,4},{12,14},{14,12},{10,6},{6,10},{2,0},{0,2},{1,5},{5,1},... | collective-permute-start | bytes 786440 | tf_op jit(solution)/shard_map/ppermute | solution.py:188
  47.6 2.7 %collective-permute-done.17.rows = bf16[128,1024]{1,0:T(8,128)(2,1)S(1)} collective-permute-done((bf16[128,1024]{1,0:T(8,128)(2,1)S(1)}, bf16[128,1024]{1,0:T(8,128)(2,1)S(1)}, u32[]{:S(2)}, u32[]{:S(2)}) %collective-permute-start.17) | collective-permute-done | bytes 262176 | tf_op jit(solution)/shard_map/ppermute | solution.py:188
  50.3 2.6 %block.3 = (bf16[128,1024]{1,0:T(8,128)(2,1)S(1)}, bf16[128,512]{1,0:T(8,128)(2,1)S(1)}) custom-call(s32[3]{0:T(128)S(1)} %pad_add_fusion.place, bf16[128,1024]{1,0:T(8,128)(2,1)S(1)} %collective-permute-done.17.rows, bf16[1024,1024]{1,0:T(8,128)(2,1)S(1)} %copy-done, bf16[1024,1024]{1,0:T(8,128)(2,1)S(1)} %collective-permute-done.1.w_other, ...), custom_call_target="tpu_custom_call" | custom-call | tf_op jit(solution)/shard_map/block/pallas_call | solution.py:42
  56.9 1.9 %collective-permute-start.22 = (bf16[512,256]{1,0:T(8,128)(2,1)S(1)}, bf16[512,256]{1,0:T(8,128)(2,1)S(1)}, u32[]{:S(2)}, u32[]{:S(2)}) collective-permute-start(bf16[512,256]{1,0:T(8,128)(2,1)S(1)} %convolution_convert_fusion), channel_id=1, source_target_pairs={{4,8},{8,4},{12,14},{14,12},{10,6},{6,10},{2,0},{0,2},{1,5},{5,1},... | collective-permute-start | bytes 786440 | tf_op jit(solution)/shard_map/ppermute | solution.py:188
  61.2 1.7 %collective-permute-start.25 = (bf16[512,256]{1,0:T(8,128)(2,1)S(1)}, bf16[512,256]{1,0:T(8,128)(2,1)S(1)}, u32[]{:S(2)}, u32[]{:S(2)}) collective-permute-start(bf16[512,256]{1,0:T(8,128)(2,1)S(1)} %get-tuple-element.84), channel_id=1, source_target_pairs={{0,4},{4,0},{8,12},{12,8},{14,10},{10,14},{6,2},{2,6},{5,9},{9,5},... | collective-permute-start | bytes 786440 | tf_op jit(solution)/shard_map/ppermute | solution.py:188
  63.4 2.0 %collective-permute-start.24 = (bf16[512,256]{1,0:T(8,128)(2,1)S(1)}, bf16[512,256]{1,0:T(8,128)(2,1)S(1)}, u32[]{:S(2)}, u32[]{:S(2)}) collective-permute-start(bf16[512,256]{1,0:T(8,128)(2,1)S(1)} %add_convert_fusion.5), channel_id=1, source_target_pairs={{0,4},{4,0},{8,12},{12,8},{14,10},{10,14},{6,2},{2,6},{5,9},{9,5},... | collective-permute-start | bytes 786440 | tf_op jit(solution)/shard_map/ppermute | solution.py:188
  65.4 2.3 %collective-permute-done.25 = bf16[512,256]{1,0:T(8,128)(2,1)S(1)} collective-permute-done((bf16[512,256]{1,0:T(8,128)(2,1)S(1)}, bf16[512,256]{1,0:T(8,128)(2,1)S(1)}, u32[]{:S(2)}, u32[]{:S(2)}) %collective-permute-start.25) | collective-permute-done | bytes 262176 | tf_op jit(solution)/shard_map/ppermute | solution.py:188
  68.9 2.5 %collective-permute-done.24 = bf16[512,256]{1,0:T(8,128)(2,1)S(1)} collective-permute-done((bf16[512,256]{1,0:T(8,128)(2,1)S(1)}, bf16[512,256]{1,0:T(8,128)(2,1)S(1)}, u32[]{:S(2)}, u32[]{:S(2)}) %collective-permute-start.24) | collective-permute-done | bytes 262176 | tf_op jit(solution)/shard_map/ppermute | solution.py:188
  72.4 1.7 %collective-permute-done.27 = bf16[512,256]{1,0:T(8,128)(2,1)S(1)} collective-permute-done((bf16[512,256]{1,0:T(8,128)(2,1)S(1)}, bf16[512,256]{1,0:T(8,128)(2,1)S(1)}, u32[]{:S(2)}, u32[]{:S(2)}) %collective-permute-start.27) | collective-permute-done | bytes 262176 | tf_op jit(solution)/shard_map/ppermute | solution.py:188
  74.2 1.7 %collective-permute-start.29 = (bf16[512,256]{1,0:T(8,128)(2,1)S(1)}, bf16[512,256]{1,0:T(8,128)(2,1)S(1)}, u32[]{:S(2)}, u32[]{:S(2)}) collective-permute-start(bf16[512,256]{1,0:T(8,128)(2,1)S(1)} %add_convert_fusion.2), channel_id=1, source_target_pairs={{0,4},{4,0},{8,12},{12,8},{14,10},{10,14},{6,2},{2,6},{5,9},{9,5},... | collective-permute-start | bytes 786440 | tf_op jit(solution)/shard_map/ppermute | solution.py:188
  76.0 3.8 %collective-permute-done.26 = bf16[512,256]{1,0:T(8,128)(2,1)S(1)} collective-permute-done((bf16[512,256]{1,0:T(8,128)(2,1)S(1)}, bf16[512,256]{1,0:T(8,128)(2,1)S(1)}, u32[]{:S(2)}, u32[]{:S(2)}) %collective-permute-start.26) | collective-permute-done | bytes 262176 | tf_op jit(solution)/shard_map/ppermute | solution.py:188
  79.8 2.2 %collective-permute-start.28 = (bf16[512,256]{1,0:T(8,128)(2,1)S(1)}, bf16[512,256]{1,0:T(8,128)(2,1)S(1)}, u32[]{:S(2)}, u32[]{:S(2)}) collective-permute-start(bf16[512,256]{1,0:T(8,128)(2,1)S(1)} %add_convert_fusion.1), channel_id=1, source_target_pairs={{0,4},{4,0},{8,12},{12,8},{14,10},{10,14},{6,2},{2,6},{5,9},{9,5},... | collective-permute-start | bytes 786440 | tf_op jit(solution)/shard_map/ppermute | solution.py:188
  82.0 4.3 %collective-permute-done.28 = bf16[512,256]{1,0:T(8,128)(2,1)S(1)} collective-permute-done((bf16[512,256]{1,0:T(8,128)(2,1)S(1)}, bf16[512,256]{1,0:T(8,128)(2,1)S(1)}, u32[]{:S(2)}, u32[]{:S(2)}) %collective-permute-start.28) | collective-permute-done | bytes 262176 | tf_op jit(solution)/shard_map/ppermute | solution.py:188
  86.4 1.6 %collective-permute-start.31 = (bf16[512,256]{1,0:T(8,128)(2,1)S(1)}, bf16[512,256]{1,0:T(8,128)(2,1)S(1)}, u32[]{:S(2)}, u32[]{:S(2)}) collective-permute-start(bf16[512,256]{1,0:T(8,128)(2,1)S(1)} %add_convert_fusion.change), channel_id=1, source_target_pairs={{0,2},{2,0},{1,3},{3,1},{4,6},{6,4},{5,7},{7,5},{8,10},{10,8},{9,1... | collective-permute-start | bytes 786440 | tf_op jit(solution)/shard_map/ppermute | solution.py:188
  89.1 1.4 %apply.2.refs_0_ = f32[500,512]{1,0:T(8,128)} custom-call(s32[3]{0:T(128)S(1)} %pad_add_fusion.place, f32[500,512]{1,0:T(8,128)S(1)} %bitcast.15, bf16[512,256]{1,0:T(8,128)(2,1)S(1)} %add_convert_fusion.change), custom_call_target="tpu_custom_call" | custom-call | tf_op jit(solution)/shard_map/apply/pallas_call | solution.py:42
  90.5 2.3 %collective-permute-done.31.change = bf16[512,256]{1,0:T(8,128)(2,1)S(1)} collective-permute-done((bf16[512,256]{1,0:T(8,128)(2,1)S(1)}, bf16[512,256]{1,0:T(8,128)(2,1)S(1)}, u32[]{:S(2)}, u32[]{:S(2)}) %collective-permute-start.31) | collective-permute-done | bytes 262176 | tf_op jit(solution)/shard_map/ppermute | solution.py:188
  92.9 1.4 %apply.3 = f32[500,512]{1,0:T(8,128)} custom-call(s32[3]{0:T(128)S(1)} %pad_add_fusion.place, f32[500,512]{1,0:T(8,128)S(1)} %bitcast.16, bf16[512,256]{1,0:T(8,128)(2,1)S(1)} %collective-permute-done.31.change, f32[500,512]{1,0:T(8,128)} %apply.2.refs_0_), custom_call_target="tpu_custom_call", output_to_operand_aliasing={{}: (3, {})} | custom-call | tf_op jit(solution)/shard_map/apply/pallas_call | solution.py:42
  (78 shorter events, 21.4 us)
Async XLA Ops:
  0.6 10.8 %collective-permute-start.1 = (bf16[1024,1024]{1,0:T(8,128)(2,1)}, bf16[1024,1024]{1,0:T(8,128)(2,1)S(1)}, u32[]{:S(2)}, u32[]{:S(2)}) collective-permute-start(bf16[1024,1024]{1,0:T(8,128)(2,1)} %w_own.9), channel_id=1, source_target_pairs={{0,1},{1,0},{2,3},{3,2},{4,5},{5,4},{6,7},{7,6},{8,9},{9,8},{10,11... | collective-permute-start | bytes 6291464 | tf_op jit(solution)/shard_map/ppermute | solution.py:188
  3.2 2.2 %collective-permute-start = (bf16[512,256]{1,0:T(8,128)(2,1)S(1)}, bf16[512,256]{1,0:T(8,128)(2,1)S(1)}, u32[]{:S(2)}, u32[]{:S(2)}) collective-permute-start(bf16[512,256]{1,0:T(8,128)(2,1)S(1)} %get-tuple-element.49), channel_id=1, source_target_pairs={{0,1},{1,0},{2,3},{3,2},{4,5},{5,4},{6,7},{7,6},{8,9},{9,8},{10,11... | collective-permute-start | bytes 786440 | tf_op jit(solution)/shard_map/ppermute | solution.py:188
  5.3 10.1 %collective-permute-start.5 = (bf16[256,1024]{1,0:T(8,128)(2,1)S(1)}, bf16[256,1024]{1,0:T(8,128)(2,1)S(1)}, u32[]{:S(2)}, u32[]{:S(2)}) collective-permute-start(bf16[256,1024]{1,0:T(8,128)(2,1)S(1)} %get-tuple-element.51.rows), channel_id=1, source_target_pairs={{0,4},{4,0},{8,12},{12,8},{14,10},{10,14},{6,2},{2,6},{5,9},{9,5},... | collective-permute-start | bytes 1572872 | tf_op jit(solution)/shard_map/ppermute | solution.py:188
  8.3 13.3 %collective-permute-start.4 = (bf16[1024,256]{1,0:T(8,128)(2,1)S(1)}, bf16[1024,256]{1,0:T(8,128)(2,1)S(1)}, u32[]{:S(2)}, u32[]{:S(2)}) collective-permute-start(bf16[1024,256]{1,0:T(8,128)(2,1)S(1)} %constant_dynamic-update-slice_fusion.refs_0_.refs_2_), channel_id=1, source_target_pairs={{0,4},{4,0},{8,12},{12,8},{14,10},{10,14},{6,2},{2,6},{5,9},{9,5},... | collective-permute-start | bytes 1572872 | tf_op jit(solution)/shard_map/ppermute | solution.py:188
  8.4 3.0 %collective-permute-start.2 = (bf16[1,1024]{1,0:T(2,128)(2,1)S(1)}, bf16[1,1024]{1,0:T(2,128)(2,1)S(1)}, u32[]{:S(2)}, u32[]{:S(2)}) collective-permute-start(bf16[1,1024]{1,0:T(2,128)(2,1)S(1)} %broadcast_in_dim.7.p_own), channel_id=1, source_target_pairs={{0,1},{1,0},{2,3},{3,2},{4,5},{5,4},{6,7},{7,6},{8,9},{9,8},{10,11... | collective-permute-start | bytes 6152 | tf_op jit(solution)/shard_map/ppermute | solution.py:188
  18.3 9.2 %collective-permute-start.9 = (bf16[256,1024]{1,0:T(8,128)(2,1)S(1)}, bf16[256,1024]{1,0:T(8,128)(2,1)S(1)}, u32[]{:S(2)}, u32[]{:S(2)}) collective-permute-start(bf16[256,1024]{1,0:T(8,128)(2,1)S(1)} %collective-permute-done.5.rows), channel_id=1, source_target_pairs={{4,8},{8,4},{12,14},{14,12},{10,6},{6,10},{2,0},{0,2},{1,5},{5,1},... | collective-permute-start | bytes 1572872 | tf_op jit(solution)/shard_map/ppermute | solution.py:188
  21.6 12.2 %collective-permute-start.7 = (bf16[256,1024]{1,0:T(8,128)(2,1)S(1)}, bf16[256,1024]{1,0:T(8,128)(2,1)S(1)}, u32[]{:S(2)}, u32[]{:S(2)}) collective-permute-start(bf16[256,1024]{1,0:T(8,128)(2,1)S(1)} %meet.3.refs_5_), channel_id=1, source_target_pairs={{0,1},{1,0},{2,3},{3,2},{4,5},{5,4},{6,7},{7,6},{8,9},{9,8},{10,11... | collective-permute-start | bytes 1572872 | tf_op jit(solution)/shard_map/ppermute | solution.py:188
  21.7 13.6 %collective-permute-start.8 = (bf16[1024,256]{1,0:T(8,128)(2,1)S(1)}, bf16[1024,256]{1,0:T(8,128)(2,1)S(1)}, u32[]{:S(2)}, u32[]{:S(2)}) collective-permute-start(bf16[1024,256]{1,0:T(8,128)(2,1)S(1)} %collective-permute-done.4.refs_4_), channel_id=1, source_target_pairs={{4,8},{8,4},{12,14},{14,12},{10,6},{6,10},{2,0},{0,2},{1,5},{5,1},... | collective-permute-start | bytes 1572872 | tf_op jit(solution)/shard_map/ppermute | solution.py:188
  23.2 1.3 %collective-permute-start.10 = (bf16[128,512]{1,0:T(8,128)(2,1)S(1)}, bf16[128,512]{1,0:T(8,128)(2,1)S(1)}, u32[]{:S(2)}, u32[]{:S(2)}) collective-permute-start(bf16[128,512]{1,0:T(8,128)(2,1)S(1)} %get-tuple-element.59.refs_3_), channel_id=1, source_target_pairs={{0,1},{1,0},{2,3},{3,2},{4,5},{5,4},{6,7},{7,6},{8,9},{9,8},{10,11... | collective-permute-start | bytes 393224 | tf_op jit(solution)/shard_map/ppermute | solution.py:188
  23.6 10.2 %collective-permute-start.6 = (bf16[512,256]{1,0:T(8,128)(2,1)S(1)}, bf16[512,256]{1,0:T(8,128)(2,1)S(1)}, u32[]{:S(2)}, u32[]{:S(2)}) collective-permute-start(bf16[512,256]{1,0:T(8,128)(2,1)S(1)} %slice.21), channel_id=1, source_target_pairs={{0,1},{1,0},{2,3},{3,2},{4,5},{5,4},{6,7},{7,6},{8,9},{9,8},{10,11... | collective-permute-start | bytes 786440 | tf_op jit(solution)/shard_map/ppermute | solution.py:188
  24.6 9.2 %collective-permute-start.3 = (bf16[128,1024]{1,0:T(8,128)(2,1)S(1)}, bf16[128,1024]{1,0:T(8,128)(2,1)S(1)}, u32[]{:S(2)}, u32[]{:S(2)}) collective-permute-start(bf16[128,1024]{1,0:T(8,128)(2,1)S(1)} %get-tuple-element.52.refs_1_), channel_id=1, source_target_pairs={{0,1},{1,0},{2,3},{3,2},{4,5},{5,4},{6,7},{7,6},{8,9},{9,8},{10,11... | collective-permute-start | bytes 786440 | tf_op jit(solution)/shard_map/ppermute | solution.py:188
  30.4 9.3 %collective-permute-start.14 = (bf16[256,1024]{1,0:T(8,128)(2,1)S(1)}, bf16[256,1024]{1,0:T(8,128)(2,1)S(1)}, u32[]{:S(2)}, u32[]{:S(2)}) collective-permute-start(bf16[256,1024]{1,0:T(8,128)(2,1)S(1)} %collective-permute-done.9.rows), channel_id=1, source_target_pairs={{0,4},{4,0},{8,12},{12,8},{14,10},{10,14},{6,2},{2,6},{5,9},{9,5},... | collective-permute-start | bytes 1572872 | tf_op jit(solution)/shard_map/ppermute | solution.py:188
  35.3 10.6 %collective-permute-start.12 = (bf16[256,1024]{1,0:T(8,128)(2,1)S(1)}, bf16[256,1024]{1,0:T(8,128)(2,1)S(1)}, u32[]{:S(2)}, u32[]{:S(2)}) collective-permute-start(bf16[256,1024]{1,0:T(8,128)(2,1)S(1)} %meet.4.refs_2_), channel_id=1, source_target_pairs={{0,1},{1,0},{2,3},{3,2},{4,5},{5,4},{6,7},{7,6},{8,9},{9,8},{10,11... | collective-permute-start | bytes 1572872 | tf_op jit(solution)/shard_map/ppermute | solution.py:188
  35.4 11.7 %collective-permute-start.13 = (bf16[1024,256]{1,0:T(8,128)(2,1)S(1)}, bf16[1024,256]{1,0:T(8,128)(2,1)S(1)}, u32[]{:S(2)}, u32[]{:S(2)}) collective-permute-start(bf16[1024,256]{1,0:T(8,128)(2,1)S(1)} %collective-permute-done.8.refs_1_), channel_id=1, source_target_pairs={{0,4},{4,0},{8,12},{12,8},{14,10},{10,14},{6,2},{2,6},{5,9},{9,5},... | collective-permute-start | bytes 1572872 | tf_op jit(solution)/shard_map/ppermute | solution.py:188
  36.0 9.9 %collective-permute-start.11 = (bf16[512,256]{1,0:T(8,128)(2,1)S(1)}, bf16[512,256]{1,0:T(8,128)(2,1)S(1)}, u32[]{:S(2)}, u32[]{:S(2)}) collective-permute-start(bf16[512,256]{1,0:T(8,128)(2,1)S(1)} %slice.22), channel_id=1, source_target_pairs={{0,1},{1,0},{2,3},{3,2},{4,5},{5,4},{6,7},{7,6},{8,9},{9,8},{10,11... | collective-permute-start | bytes 786440 | tf_op jit(solution)/shard_map/ppermute | solution.py:188
  43.8 9.9 %collective-permute-start.16 = (bf16[256,1024]{1,0:T(8,128)(2,1)S(1)}, bf16[256,1024]{1,0:T(8,128)(2,1)S(1)}, u32[]{:S(2)}, u32[]{:S(2)}) collective-permute-start(bf16[256,1024]{1,0:T(8,128)(2,1)S(1)} %meet.5.refs_2_), channel_id=1, source_target_pairs={{0,1},{1,0},{2,3},{3,2},{4,5},{5,4},{6,7},{7,6},{8,9},{9,8},{10,11... | collective-permute-start | bytes 1572872 | tf_op jit(solution)/shard_map/ppermute | solution.py:188
  43.9 6.4 %collective-permute-start.17 = (bf16[128,1024]{1,0:T(8,128)(2,1)S(1)}, bf16[128,1024]{1,0:T(8,128)(2,1)S(1)}, u32[]{:S(2)}, u32[]{:S(2)}) collective-permute-start(bf16[128,1024]{1,0:T(8,128)(2,1)S(1)} %slice.24), channel_id=1, source_target_pairs={{4,8},{8,4},{12,14},{14,12},{10,6},{6,10},{2,0},{0,2},{1,5},{5,1},... | collective-permute-start | bytes 786440 | tf_op jit(solution)/shard_map/ppermute | solution.py:188
  47.2 6.4 %collective-permute-start.19 = (bf16[1024,128]{1,0:T(8,128)(2,1)S(1)}, bf16[1024,128]{1,0:T(8,128)(2,1)S(1)}, u32[]{:S(2)}, u32[]{:S(2)}) collective-permute-start(bf16[1024,128]{1,0:T(8,128)(2,1)S(1)} %slice.25), channel_id=1, source_target_pairs={{4,8},{8,4},{12,14},{14,12},{10,6},{6,10},{2,0},{0,2},{1,5},{5,1},... | collective-permute-start | bytes 786440 | tf_op jit(solution)/shard_map/ppermute | solution.py:188
  47.3 6.3 %collective-permute-start.15 = (bf16[512,256]{1,0:T(8,128)(2,1)S(1)}, bf16[512,256]{1,0:T(8,128)(2,1)S(1)}, u32[]{:S(2)}, u32[]{:S(2)}) collective-permute-start(bf16[512,256]{1,0:T(8,128)(2,1)S(1)} %slice.23), channel_id=1, source_target_pairs={{0,1},{1,0},{2,3},{3,2},{4,5},{5,4},{6,7},{7,6},{8,9},{9,8},{10,11... | collective-permute-start | bytes 786440 | tf_op jit(solution)/shard_map/ppermute | solution.py:188
  52.9 2.1 %collective-permute-start.21 = (bf16[128,1024]{1,0:T(8,128)(2,1)S(1)}, bf16[128,1024]{1,0:T(8,128)(2,1)S(1)}, u32[]{:S(2)}, u32[]{:S(2)}) collective-permute-start(bf16[128,1024]{1,0:T(8,128)(2,1)S(1)} %get-tuple-element.74.refs_1_), channel_id=1, source_target_pairs={{0,1},{1,0},{2,3},{3,2},{4,5},{5,4},{6,7},{7,6},{8,9},{9,8},{10,11... | collective-permute-start | bytes 786440 | tf_op jit(solution)/shard_map/ppermute | solution.py:188
  53.0 1.9 %collective-permute-start.18 = (bf16[128,512]{1,0:T(8,128)(2,1)S(1)}, bf16[128,512]{1,0:T(8,128)(2,1)S(1)}, u32[]{:S(2)}, u32[]{:S(2)}) collective-permute-start(bf16[128,512]{1,0:T(8,128)(2,1)S(1)} %get-tuple-element.72), channel_id=1, source_target_pairs={{0,1},{1,0},{2,3},{3,2},{4,5},{5,4},{6,7},{7,6},{8,9},{9,8},{10,11... | collective-permute-start | bytes 393224 | tf_op jit(solution)/shard_map/ppermute | solution.py:188
  53.6 1.4 %collective-permute-start.20 = (bf16[512,128]{1,0:T(8,128)(2,1)S(1)}, bf16[512,128]{1,0:T(8,128)(2,1)S(1)}, u32[]{:S(2)}, u32[]{:S(2)}) collective-permute-start(bf16[512,128]{1,0:T(8,128)(2,1)S(1)} %slice.28), channel_id=1, source_target_pairs={{0,1},{1,0},{2,3},{3,2},{4,5},{5,4},{6,7},{7,6},{8,9},{9,8},{10,11... | collective-permute-start | bytes 393224 | tf_op jit(solution)/shard_map/ppermute | solution.py:188
  56.0 4.0 %collective-permute-start.23 = (bf16[512,512]{1,0:T(8,128)(2,1)S(1)}, bf16[512,512]{1,0:T(8,128)(2,1)S(1)}, u32[]{:S(2)}, u32[]{:S(2)}) collective-permute-start(bf16[512,512]{1,0:T(8,128)(2,1)S(1)} %get-tuple-element.77.sent), channel_id=1, source_target_pairs={{0,1},{1,0},{2,3},{3,2},{4,5},{5,4},{6,7},{7,6},{8,9},{9,8},{10,11... | collective-permute-start | bytes 1572872 | tf_op jit(solution)/shard_map/ppermute | solution.py:188
  56.9 6.4 %collective-permute-start.22 = (bf16[512,256]{1,0:T(8,128)(2,1)S(1)}, bf16[512,256]{1,0:T(8,128)(2,1)S(1)}, u32[]{:S(2)}, u32[]{:S(2)}) collective-permute-start(bf16[512,256]{1,0:T(8,128)(2,1)S(1)} %convolution_convert_fusion), channel_id=1, source_target_pairs={{4,8},{8,4},{12,14},{14,12},{10,6},{6,10},{2,0},{0,2},{1,5},{5,1},... | collective-permute-start | bytes 786440 | tf_op jit(solution)/shard_map/ppermute | solution.py:188
  61.2 6.4 %collective-permute-start.25 = (bf16[512,256]{1,0:T(8,128)(2,1)S(1)}, bf16[512,256]{1,0:T(8,128)(2,1)S(1)}, u32[]{:S(2)}, u32[]{:S(2)}) collective-permute-start(bf16[512,256]{1,0:T(8,128)(2,1)S(1)} %get-tuple-element.84), channel_id=1, source_target_pairs={{0,4},{4,0},{8,12},{12,8},{14,10},{10,14},{6,2},{2,6},{5,9},{9,5},... | collective-permute-start | bytes 786440 | tf_op jit(solution)/shard_map/ppermute | solution.py:188
  63.4 8.0 %collective-permute-start.24 = (bf16[512,256]{1,0:T(8,128)(2,1)S(1)}, bf16[512,256]{1,0:T(8,128)(2,1)S(1)}, u32[]{:S(2)}, u32[]{:S(2)}) collective-permute-start(bf16[512,256]{1,0:T(8,128)(2,1)S(1)} %add_convert_fusion.5), channel_id=1, source_target_pairs={{0,4},{4,0},{8,12},{12,8},{14,10},{10,14},{6,2},{2,6},{5,9},{9,5},... | collective-permute-start | bytes 786440 | tf_op jit(solution)/shard_map/ppermute | solution.py:188
  67.7 6.4 %collective-permute-start.27 = (bf16[512,256]{1,0:T(8,128)(2,1)S(1)}, bf16[512,256]{1,0:T(8,128)(2,1)S(1)}, u32[]{:S(2)}, u32[]{:S(2)}) collective-permute-start(bf16[512,256]{1,0:T(8,128)(2,1)S(1)} %add_convert_fusion.4), channel_id=1, source_target_pairs={{4,8},{8,4},{12,14},{14,12},{10,6},{6,10},{2,0},{0,2},{1,5},{5,1},... | collective-permute-start | bytes 786440 | tf_op jit(solution)/shard_map/ppermute | solution.py:188
  71.5 8.3 %collective-permute-start.26 = (bf16[512,256]{1,0:T(8,128)(2,1)S(1)}, bf16[512,256]{1,0:T(8,128)(2,1)S(1)}, u32[]{:S(2)}, u32[]{:S(2)}) collective-permute-start(bf16[512,256]{1,0:T(8,128)(2,1)S(1)} %add_convert_fusion.3), channel_id=1, source_target_pairs={{4,8},{8,4},{12,14},{14,12},{10,6},{6,10},{2,0},{0,2},{1,5},{5,1},... | collective-permute-start | bytes 786440 | tf_op jit(solution)/shard_map/ppermute | solution.py:188
  74.2 7.8 %collective-permute-start.29 = (bf16[512,256]{1,0:T(8,128)(2,1)S(1)}, bf16[512,256]{1,0:T(8,128)(2,1)S(1)}, u32[]{:S(2)}, u32[]{:S(2)}) collective-permute-start(bf16[512,256]{1,0:T(8,128)(2,1)S(1)} %add_convert_fusion.2), channel_id=1, source_target_pairs={{0,4},{4,0},{8,12},{12,8},{14,10},{10,14},{6,2},{2,6},{5,9},{9,5},... | collective-permute-start | bytes 786440 | tf_op jit(solution)/shard_map/ppermute | solution.py:188
  79.8 6.5 %collective-permute-start.28 = (bf16[512,256]{1,0:T(8,128)(2,1)S(1)}, bf16[512,256]{1,0:T(8,128)(2,1)S(1)}, u32[]{:S(2)}, u32[]{:S(2)}) collective-permute-start(bf16[512,256]{1,0:T(8,128)(2,1)S(1)} %add_convert_fusion.1), channel_id=1, source_target_pairs={{0,4},{4,0},{8,12},{12,8},{14,10},{10,14},{6,2},{2,6},{5,9},{9,5},... | collective-permute-start | bytes 786440 | tf_op jit(solution)/shard_map/ppermute | solution.py:188
  82.0 4.4 %collective-permute-start.30 = (bf16[512,256]{1,0:T(8,128)(2,1)S(1)}, bf16[512,256]{1,0:T(8,128)(2,1)S(1)}, u32[]{:S(2)}, u32[]{:S(2)}) collective-permute-start(bf16[512,256]{1,0:T(8,128)(2,1)S(1)} %collective-permute-done.29), channel_id=1, source_target_pairs={{0,1},{1,0},{2,3},{3,2},{4,5},{5,4},{6,7},{7,6},{8,9},{9,8},{10,11... | collective-permute-start | bytes 786440 | tf_op jit(solution)/shard_map/ppermute | solution.py:188
  86.4 6.4 %collective-permute-start.31 = (bf16[512,256]{1,0:T(8,128)(2,1)S(1)}, bf16[512,256]{1,0:T(8,128)(2,1)S(1)}, u32[]{:S(2)}, u32[]{:S(2)}) collective-permute-start(bf16[512,256]{1,0:T(8,128)(2,1)S(1)} %add_convert_fusion.change), channel_id=1, source_target_pairs={{0,2},{2,0},{1,3},{3,1},{4,6},{6,4},{5,7},{7,5},{8,10},{10,8},{9,1... | collective-permute-start | bytes 786440 | tf_op jit(solution)/shard_map/ppermute | solution.py:188
  (5 other events, 41.2 us)

commit v20 on v19

--- a/solution.py
+++ b/solution.py
@@ -153,13 +153,6 @@
     out[...] = pieces[0][...] + total if earlier else total
 
 
-def update_kernel(place, begun, *refs):
-    *pieces, update, sent = refs
-    total = DAMPING * (begun[...] + product_of(pieces, begun.shape[0]))
-    update[...] = total
-    sent[...] = total.astype(BF16)
-
-
 def change_kernel(counts, turned, place, sent, *refs):
     at = 0
     for count, out in zip(counts, refs[sum(counts):]):
@@ -271,10 +264,10 @@
     q4, f4 = block(x4, part)
     f4_other = C(f4)
     (begun,) = after((begun,), f4_other)
-    update, sent = call(
-        update_kernel, (like((padded, depth), F32), like((padded, depth))), place,
-        (begun, r4, q4, theirs(r4), C(q4)), "update", 14,
-    )
+    ends = [(r4[:padded], q4), (theirs(r4), C(q4))]
+    total = dot(*[jnp.concatenate(side, axis=1 - i) for i, side in enumerate(zip(*ends))])
+    update = DAMPING * (begun + (total[:, :depth] + total[:, depth:]))
+    sent = update.astype(BF16)
 
     whole, wide = like((padded, 2 * part)), like((padded, 2 * part), F32)
 

time: 95.5 us -> 95.1 us (level)
  starting transfers between devices: 29.1 us -> 32.3 us
  waiting for transfers between devices: 28.7 us -> 26 us
  Pallas kernels: 30.3 us -> 29.3 us
    ppermute x32, starting transfers between devices: 29.1 us -> 32.3 us  [swap(): lax.ppermute(x, axes, [p for a, b in pairs for p in ((a, b), (b, a))])]
    ppermute x32, waiting for transfers between devices: 28.7 us -> 26 us  [swap(): lax.ppermute(x, axes, [p for a, b in pairs for p in ((a, b), (b, a))])]
    pallas_call x18 -> x17, Pallas kernels: 30.3 us -> 29.3 us  [call(): pl.pallas_call(kernel, out_shape=out_shapes, in_specs=[pl.BlockSpec(memor...]
  transfers between devices with their start and end apart: 32 -> 32, of which waited for: 14 -> 14; matrix products, arithmetic and copies ran while one was open for 2% -> 2% of each run, Pallas kernels for 30% -> 29%
where the time goes in v20:
time: 95.1 us; the launch traced here: 94.7 us
  starting transfers between devices  32.3 us (34%)
  Pallas kernels  29.3 us (31%)
  waiting for transfers between devices  26 us (27%)
  local copies, waits for them, and re-layouts  3.17 us (3%)
  other arithmetic  2.01 us (2%)
  between operations  1.2 us (1%)
    ppermute x32, starting transfers between devices, swap(): lax.ppermute(x, axes, [p for a, b in pairs for p in ((a, b), (b, a))])  32.3 us
    pallas_call x17, Pallas kernels, call(): pl.pallas_call(kernel, out_shape=out_shapes, in_specs=[pl.BlockSpec(memor...  29.3 us
    ppermute x32, waiting for transfers between devices, swap(): lax.ppermute(x, axes, [p for a, b in pairs for p in ((a, b), (b, a))])  26 us
    unnamed x11, local copies, waits for them, and re-layouts  3.04 us
  transfers between devices with their start and end apart: 32, of which 14 were waited for; matrix products, arithmetic and copies ran while one was open for 2% of the time, Pallas kernels for 29%

profile of v20, /device:TPU:0, one launch (start us, length us, event | category | flops | bytes accessed | tf_op | source)
XLA Modules:
  0.0 94.7 jit_solution(12230699089963548878)
XLA Ops:
  1.2 1.9 %prepare.1 = (bf16[256,1024]{1,0:T(8,128)(2,1)S(1)}, bf16[512,256]{1,0:T(8,128)(2,1)S(1)}, bf16[512,256]{1,0:T(8,128)(2,1)S(1)}) custom-call(s32[3]{0:T(128)S(1)} %pad_add_fusion.place, bf16[512,1024]{1,0:T(8,128)(2,1)} %inputs.1, s32[1,512]{1,0:T(1,128)} %bitcast.17, f32[500,512]{1,0:T(8,128)} %bitcast.12), custom_call_target="tpu_custom_call" | custom-call | tf_op jit(solution)/shard_map/prepare/pallas_call | solution.py:42
  3.3 2.0 %collective-permute-done = bf16[512,256]{1,0:T(8,128)(2,1)S(1)} collective-permute-done((bf16[512,256]{1,0:T(8,128)(2,1)S(1)}, bf16[512,256]{1,0:T(8,128)(2,1)S(1)}, u32[]{:S(2)}, u32[]{:S(2)}) %collective-permute-start) | collective-permute-done | bytes 262176 | tf_op jit(solution)/shard_map/ppermute | solution.py:181
  5.3 2.9 %collective-permute-start.5 = (bf16[256,1024]{1,0:T(8,128)(2,1)S(1)}, bf16[256,1024]{1,0:T(8,128)(2,1)S(1)}, u32[]{:S(2)}, u32[]{:S(2)}) collective-permute-start(bf16[256,1024]{1,0:T(8,128)(2,1)S(1)} %get-tuple-element.49.rows), channel_id=1, source_target_pairs={{0,4},{4,0},{8,12},{12,8},{14,10},{10,14},{6,2},{2,6},{5,9},{9,5},... | collective-permute-start | bytes 1572872 | tf_op jit(solution)/shard_map/ppermute | solution.py:181
  8.5 2.2 %copy-done.2 = f32[1,512,2048]{2,1,0:T(8,128)S(1)} copy-done((f32[1,512,2048]{2,1,0:T(8,128)S(1)}, f32[1,512,2048]{2,1,0:T(8,128)}, u32[]{:S(2)}) %copy-start.2) | copy-done | bytes 4194328
  12.2 2.4 %block.2 = (bf16[128,1024]{1,0:T(8,128)(2,1)S(1)}, bf16[128,512]{1,0:T(8,128)(2,1)S(1)}) custom-call(s32[3]{0:T(128)S(1)} %pad_add_fusion.place, bf16[256,1024]{1,0:T(8,128)(2,1)S(1)} %get-tuple-element.49.rows, bf16[1024,1024]{1,0:T(8,128)(2,1)S(1)} %copy-done, bf16[1024,1024]{1,0:T(8,128)(2,1)S(1)} %collective-permute-done.1.w_other, ...), custom_call_target="tpu_custom_call" | custom-call | tf_op jit(solution)/shard_map/block/pallas_call | solution.py:42
  15.4 2.8 %features.3 = (bf16[256,2048]{1,0:T(8,128)(2,1)S(1)}, bf16[256,512]{1,0:T(8,128)(2,1)S(1)}) custom-call(s32[3]{0:T(128)S(1)} %pad_add_fusion.place, bf16[256,1024]{1,0:T(8,128)(2,1)S(1)} %collective-permute-done.5.rows, bf16[1024,1024]{1,0:T(8,128)(2,1)S(1)} %copy-done, bf16[1024,1024]{1,0:T(8,128)(2,1)S(1)} %collective-permute-done.1.w_other, ...), custom_call_target="tpu_custom_call" | custom-call | tf_op jit(solution)/shard_map/features/pallas_call | solution.py:42
  18.3 2.0 %collective-permute-start.9 = (bf16[256,1024]{1,0:T(8,128)(2,1)S(1)}, bf16[256,1024]{1,0:T(8,128)(2,1)S(1)}, u32[]{:S(2)}, u32[]{:S(2)}) collective-permute-start(bf16[256,1024]{1,0:T(8,128)(2,1)S(1)} %collective-permute-done.5.rows), channel_id=1, source_target_pairs={{4,8},{8,4},{12,14},{14,12},{10,6},{6,10},{2,0},{0,2},{1,5},{5,1},... | collective-permute-start | bytes 1572872 | tf_op jit(solution)/shard_map/ppermute | solution.py:181
  20.3 1.3 %meet.3.refs_5_ = bf16[256,1024]{1,0:T(8,128)(2,1)S(1)} custom-call(s32[3]{0:T(128)S(1)} %pad_add_fusion.place, bf16[256,2048]{1,0:T(8,128)(2,1)S(1)} %get-tuple-element.52.feats, bf16[512,2048]{1,0:T(8,128)(2,1)S(1)} %round.1.inverse), custom_call_target="tpu_custom_call" | custom-call | tf_op jit(solution)/shard_map/meet/pallas_call | solution.py:42
  21.7 1.6 %collective-permute-start.8 = (bf16[1024,256]{1,0:T(8,128)(2,1)S(1)}, bf16[1024,256]{1,0:T(8,128)(2,1)S(1)}, u32[]{:S(2)}, u32[]{:S(2)}) collective-permute-start(bf16[1024,256]{1,0:T(8,128)(2,1)S(1)} %collective-permute-done.4.refs_4_), channel_id=1, source_target_pairs={{4,8},{8,4},{12,14},{14,12},{10,6},{6,10},{2,0},{0,2},{1,5},{5,1},... | collective-permute-start | bytes 1572872 | tf_op jit(solution)/shard_map/ppermute | solution.py:181
  24.9 2.6 %collective-permute-done.9.rows = bf16[256,1024]{1,0:T(8,128)(2,1)S(1)} collective-permute-done((bf16[256,1024]{1,0:T(8,128)(2,1)S(1)}, bf16[256,1024]{1,0:T(8,128)(2,1)S(1)}, u32[]{:S(2)}, u32[]{:S(2)}) %collective-permute-start.9) | collective-permute-done | bytes 524320 | tf_op jit(solution)/shard_map/ppermute | solution.py:181
  27.5 2.8 %features.4 = (bf16[256,2048]{1,0:T(8,128)(2,1)S(1)}, bf16[256,512]{1,0:T(8,128)(2,1)S(1)}) custom-call(s32[3]{0:T(128)S(1)} %pad_add_fusion.place, bf16[256,1024]{1,0:T(8,128)(2,1)S(1)} %collective-permute-done.9.rows, bf16[1024,1024]{1,0:T(8,128)(2,1)S(1)} %copy-done, bf16[1024,1024]{1,0:T(8,128)(2,1)S(1)} %collective-permute-done.1.w_other, ...), custom_call_target="tpu_custom_call" | custom-call | tf_op jit(solution)/shard_map/features/pallas_call | solution.py:42
  30.4 2.1 %collective-permute-start.14 = (bf16[256,1024]{1,0:T(8,128)(2,1)S(1)}, bf16[256,1024]{1,0:T(8,128)(2,1)S(1)}, u32[]{:S(2)}, u32[]{:S(2)}) collective-permute-start(bf16[256,1024]{1,0:T(8,128)(2,1)S(1)} %collective-permute-done.9.rows), channel_id=1, source_target_pairs={{0,4},{4,0},{8,12},{12,8},{14,10},{10,14},{6,2},{2,6},{5,9},{9,5},... | collective-permute-start | bytes 1572872 | tf_op jit(solution)/shard_map/ppermute | solution.py:181
  33.8 1.5 %begin.3.refs_0_ = f32[512,512]{1,0:T(8,128)S(1)} custom-call(s32[3]{0:T(128)S(1)} %pad_add_fusion.place, bf16[1024,256]{1,0:T(8,128)(2,1)S(1)} %constant_dynamic-update-slice_fusion.refs_0_.refs_2_, bf16[128,1024]{1,0:T(8,128)(2,1)S(1)} %get-tuple-element.50.refs_1_, bf16[1024,256]{1,0:T(8,128)(2,1)S(1)} %constant_dynamic-update-slice_fusion.refs_0_.refs_2_, ...), custom_call_target="tpu_custom_call" | custom-call | tf_op jit(solution)/shard_map/begin/pallas_call | solution.py:42
  37.2 2.4 %collective-permute-done.14.rows = bf16[256,1024]{1,0:T(8,128)(2,1)S(1)} collective-permute-done((bf16[256,1024]{1,0:T(8,128)(2,1)S(1)}, bf16[256,1024]{1,0:T(8,128)(2,1)S(1)}, u32[]{:S(2)}, u32[]{:S(2)}) %collective-permute-start.14) | collective-permute-done | bytes 524320 | tf_op jit(solution)/shard_map/ppermute | solution.py:181
  39.6 2.8 %features.5 = (bf16[256,2048]{1,0:T(8,128)(2,1)S(1)}, bf16[256,512]{1,0:T(8,128)(2,1)S(1)}) custom-call(s32[3]{0:T(128)S(1)} %pad_add_fusion.place, bf16[256,1024]{1,0:T(8,128)(2,1)S(1)} %collective-permute-done.14.rows, bf16[1024,1024]{1,0:T(8,128)(2,1)S(1)} %copy-done, bf16[1024,1024]{1,0:T(8,128)(2,1)S(1)} %collective-permute-done.1.w_other, ...), custom_call_target="tpu_custom_call" | custom-call | tf_op jit(solution)/shard_map/features/pallas_call | solution.py:42
  42.5 2.0 %collective-permute-start.17 = (bf16[128,1024]{1,0:T(8,128)(2,1)S(1)}, bf16[128,1024]{1,0:T(8,128)(2,1)S(1)}, u32[]{:S(2)}, u32[]{:S(2)}) collective-permute-start(bf16[128,1024]{1,0:T(8,128)(2,1)S(1)} %slice.33), channel_id=1, source_target_pairs={{4,8},{8,4},{12,14},{14,12},{10,6},{6,10},{2,0},{0,2},{1,5},{5,1},... | collective-permute-start | bytes 786440 | tf_op jit(solution)/shard_map/ppermute | solution.py:181
  48.9 2.6 %block.3 = (bf16[128,1024]{1,0:T(8,128)(2,1)S(1)}, bf16[128,512]{1,0:T(8,128)(2,1)S(1)}) custom-call(s32[3]{0:T(128)S(1)} %pad_add_fusion.place, bf16[128,1024]{1,0:T(8,128)(2,1)S(1)} %collective-permute-done.17.rows, bf16[1024,1024]{1,0:T(8,128)(2,1)S(1)} %copy-done, bf16[1024,1024]{1,0:T(8,128)(2,1)S(1)} %collective-permute-done.1.w_other, ...), custom_call_target="tpu_custom_call" | custom-call | tf_op jit(solution)/shard_map/block/pallas_call | solution.py:42
  52.2 1.4 %collective-permute-done.19 = bf16[1024,128]{1,0:T(8,128)(2,1)S(1)} collective-permute-done((bf16[1024,128]{1,0:T(8,128)(2,1)S(1)}, bf16[1024,128]{1,0:T(8,128)(2,1)S(1)}, u32[]{:S(2)}, u32[]{:S(2)}) %collective-permute-start.19) | collective-permute-done | bytes 262176 | tf_op jit(solution)/shard_map/ppermute | solution.py:181
  60.0 1.7 %collective-permute-start.25 = (bf16[512,256]{1,0:T(8,128)(2,1)S(1)}, bf16[512,256]{1,0:T(8,128)(2,1)S(1)}, u32[]{:S(2)}, u32[]{:S(2)}) collective-permute-start(bf16[512,256]{1,0:T(8,128)(2,1)S(1)} %get-tuple-element.80), channel_id=1, source_target_pairs={{0,4},{4,0},{8,12},{12,8},{14,10},{10,14},{6,2},{2,6},{5,9},{9,5},... | collective-permute-start | bytes 786440 | tf_op jit(solution)/shard_map/ppermute | solution.py:181
  61.7 1.4 %collective-permute-done.22 = bf16[512,256]{1,0:T(8,128)(2,1)S(1)} collective-permute-done((bf16[512,256]{1,0:T(8,128)(2,1)S(1)}, bf16[512,256]{1,0:T(8,128)(2,1)S(1)}, u32[]{:S(2)}, u32[]{:S(2)}) %collective-permute-start.22) | collective-permute-done | bytes 262176 | tf_op jit(solution)/shard_map/ppermute | solution.py:181
  63.2 1.8 %collective-permute-start.24 = (bf16[512,256]{1,0:T(8,128)(2,1)S(1)}, bf16[512,256]{1,0:T(8,128)(2,1)S(1)}, u32[]{:S(2)}, u32[]{:S(2)}) collective-permute-start(bf16[512,256]{1,0:T(8,128)(2,1)S(1)} %add_convert_fusion.5), channel_id=1, source_target_pairs={{0,4},{4,0},{8,12},{12,8},{14,10},{10,14},{6,2},{2,6},{5,9},{9,5},... | collective-permute-start | bytes 786440 | tf_op jit(solution)/shard_map/ppermute | solution.py:181
  65.0 1.5 %collective-permute-done.25 = bf16[512,256]{1,0:T(8,128)(2,1)S(1)} collective-permute-done((bf16[512,256]{1,0:T(8,128)(2,1)S(1)}, bf16[512,256]{1,0:T(8,128)(2,1)S(1)}, u32[]{:S(2)}, u32[]{:S(2)}) %collective-permute-start.25) | collective-permute-done | bytes 262176 | tf_op jit(solution)/shard_map/ppermute | solution.py:181
  67.8 2.4 %collective-permute-done.24 = bf16[512,256]{1,0:T(8,128)(2,1)S(1)} collective-permute-done((bf16[512,256]{1,0:T(8,128)(2,1)S(1)}, bf16[512,256]{1,0:T(8,128)(2,1)S(1)}, u32[]{:S(2)}, u32[]{:S(2)}) %collective-permute-start.24) | collective-permute-done | bytes 262176 | tf_op jit(solution)/shard_map/ppermute | solution.py:181
  70.3 2.4 %collective-permute-start.26 = (bf16[512,256]{1,0:T(8,128)(2,1)S(1)}, bf16[512,256]{1,0:T(8,128)(2,1)S(1)}, u32[]{:S(2)}, u32[]{:S(2)}) collective-permute-start(bf16[512,256]{1,0:T(8,128)(2,1)S(1)} %add_convert_fusion.3), channel_id=1, source_target_pairs={{4,8},{8,4},{12,14},{14,12},{10,6},{6,10},{2,0},{0,2},{1,5},{5,1},... | collective-permute-start | bytes 786440 | tf_op jit(solution)/shard_map/ppermute | solution.py:181
  73.0 1.9 %collective-permute-start.29 = (bf16[512,256]{1,0:T(8,128)(2,1)S(1)}, bf16[512,256]{1,0:T(8,128)(2,1)S(1)}, u32[]{:S(2)}, u32[]{:S(2)}) collective-permute-start(bf16[512,256]{1,0:T(8,128)(2,1)S(1)} %add_convert_fusion.2), channel_id=1, source_target_pairs={{0,4},{4,0},{8,12},{12,8},{14,10},{10,14},{6,2},{2,6},{5,9},{9,5},... | collective-permute-start | bytes 786440 | tf_op jit(solution)/shard_map/ppermute | solution.py:181
  74.9 4.0 %collective-permute-done.26 = bf16[512,256]{1,0:T(8,128)(2,1)S(1)} collective-permute-done((bf16[512,256]{1,0:T(8,128)(2,1)S(1)}, bf16[512,256]{1,0:T(8,128)(2,1)S(1)}, u32[]{:S(2)}, u32[]{:S(2)}) %collective-permute-start.26) | collective-permute-done | bytes 262176 | tf_op jit(solution)/shard_map/ppermute | solution.py:181
  78.9 2.5 %collective-permute-start.28 = (bf16[512,256]{1,0:T(8,128)(2,1)S(1)}, bf16[512,256]{1,0:T(8,128)(2,1)S(1)}, u32[]{:S(2)}, u32[]{:S(2)}) collective-permute-start(bf16[512,256]{1,0:T(8,128)(2,1)S(1)} %add_convert_fusion.1), channel_id=1, source_target_pairs={{0,4},{4,0},{8,12},{12,8},{14,10},{10,14},{6,2},{2,6},{5,9},{9,5},... | collective-permute-start | bytes 786440 | tf_op jit(solution)/shard_map/ppermute | solution.py:181
  81.4 4.3 %collective-permute-done.28 = bf16[512,256]{1,0:T(8,128)(2,1)S(1)} collective-permute-done((bf16[512,256]{1,0:T(8,128)(2,1)S(1)}, bf16[512,256]{1,0:T(8,128)(2,1)S(1)}, u32[]{:S(2)}, u32[]{:S(2)}) %collective-permute-start.28) | collective-permute-done | bytes 262176 | tf_op jit(solution)/shard_map/ppermute | solution.py:181
  85.9 2.9 %collective-permute-start.31 = (bf16[512,256]{1,0:T(8,128)(2,1)S(1)}, bf16[512,256]{1,0:T(8,128)(2,1)S(1)}, u32[]{:S(2)}, u32[]{:S(2)}) collective-permute-start(bf16[512,256]{1,0:T(8,128)(2,1)S(1)} %add_convert_fusion.change), channel_id=1, source_target_pairs={{0,2},{2,0},{1,3},{3,1},{4,6},{6,4},{5,7},{7,5},{8,10},{10,8},{9,1... | collective-permute-start | bytes 786440 | tf_op jit(solution)/shard_map/ppermute | solution.py:181
  90.0 1.4 %apply.2.refs_0_ = f32[500,512]{1,0:T(8,128)} custom-call(s32[3]{0:T(128)S(1)} %pad_add_fusion.place, f32[500,512]{1,0:T(8,128)S(1)} %bitcast.13, bf16[512,256]{1,0:T(8,128)(2,1)S(1)} %add_convert_fusion.change), custom_call_target="tpu_custom_call" | custom-call | tf_op jit(solution)/shard_map/apply/pallas_call | solution.py:42
  91.4 1.8 %collective-permute-done.31.change = bf16[512,256]{1,0:T(8,128)(2,1)S(1)} collective-permute-done((bf16[512,256]{1,0:T(8,128)(2,1)S(1)}, bf16[512,256]{1,0:T(8,128)(2,1)S(1)}, u32[]{:S(2)}, u32[]{:S(2)}) %collective-permute-start.31) | collective-permute-done | bytes 262176 | tf_op jit(solution)/shard_map/ppermute | solution.py:181
  93.2 1.4 %apply.3 = f32[500,512]{1,0:T(8,128)} custom-call(s32[3]{0:T(128)S(1)} %pad_add_fusion.place, f32[500,512]{1,0:T(8,128)S(1)} %bitcast.14, bf16[512,256]{1,0:T(8,128)(2,1)S(1)} %collective-permute-done.31.change, f32[500,512]{1,0:T(8,128)} %apply.2.refs_0_), custom_call_target="tpu_custom_call", output_to_operand_aliasing={{}: (3, {})} | custom-call | tf_op jit(solution)/shard_map/apply/pallas_call | solution.py:42
  (79 shorter events, 22.5 us)
Async XLA Ops:
  0.6 10.8 %collective-permute-start.1 = (bf16[1024,1024]{1,0:T(8,128)(2,1)}, bf16[1024,1024]{1,0:T(8,128)(2,1)S(1)}, u32[]{:S(2)}, u32[]{:S(2)}) collective-permute-start(bf16[1024,1024]{1,0:T(8,128)(2,1)} %w_own.9), channel_id=1, source_target_pairs={{0,1},{1,0},{2,3},{3,2},{4,5},{5,4},{6,7},{7,6},{8,9},{9,8},{10,11... | collective-permute-start | bytes 6291464 | tf_op jit(solution)/shard_map/ppermute | solution.py:181
  3.2 2.2 %collective-permute-start = (bf16[512,256]{1,0:T(8,128)(2,1)S(1)}, bf16[512,256]{1,0:T(8,128)(2,1)S(1)}, u32[]{:S(2)}, u32[]{:S(2)}) collective-permute-start(bf16[512,256]{1,0:T(8,128)(2,1)S(1)} %get-tuple-element.47), channel_id=1, source_target_pairs={{0,1},{1,0},{2,3},{3,2},{4,5},{5,4},{6,7},{7,6},{8,9},{9,8},{10,11... | collective-permute-start | bytes 786440 | tf_op jit(solution)/shard_map/ppermute | solution.py:181
  5.3 10.1 %collective-permute-start.5 = (bf16[256,1024]{1,0:T(8,128)(2,1)S(1)}, bf16[256,1024]{1,0:T(8,128)(2,1)S(1)}, u32[]{:S(2)}, u32[]{:S(2)}) collective-permute-start(bf16[256,1024]{1,0:T(8,128)(2,1)S(1)} %get-tuple-element.49.rows), channel_id=1, source_target_pairs={{0,4},{4,0},{8,12},{12,8},{14,10},{10,14},{6,2},{2,6},{5,9},{9,5},... | collective-permute-start | bytes 1572872 | tf_op jit(solution)/shard_map/ppermute | solution.py:181
  8.3 13.4 %collective-permute-start.4 = (bf16[1024,256]{1,0:T(8,128)(2,1)S(1)}, bf16[1024,256]{1,0:T(8,128)(2,1)S(1)}, u32[]{:S(2)}, u32[]{:S(2)}) collective-permute-start(bf16[1024,256]{1,0:T(8,128)(2,1)S(1)} %constant_dynamic-update-slice_fusion.refs_0_.refs_2_), channel_id=1, source_target_pairs={{0,4},{4,0},{8,12},{12,8},{14,10},{10,14},{6,2},{2,6},{5,9},{9,5},... | collective-permute-start | bytes 1572872 | tf_op jit(solution)/shard_map/ppermute | solution.py:181
  8.4 3.0 %collective-permute-start.2 = (bf16[1,1024]{1,0:T(2,128)(2,1)S(1)}, bf16[1,1024]{1,0:T(2,128)(2,1)S(1)}, u32[]{:S(2)}, u32[]{:S(2)}) collective-permute-start(bf16[1,1024]{1,0:T(2,128)(2,1)S(1)} %broadcast_in_dim.7.p_own), channel_id=1, source_target_pairs={{0,1},{1,0},{2,3},{3,2},{4,5},{5,4},{6,7},{7,6},{8,9},{9,8},{10,11... | collective-permute-start | bytes 6152 | tf_op jit(solution)/shard_map/ppermute | solution.py:181
  18.3 9.2 %collective-permute-start.9 = (bf16[256,1024]{1,0:T(8,128)(2,1)S(1)}, bf16[256,1024]{1,0:T(8,128)(2,1)S(1)}, u32[]{:S(2)}, u32[]{:S(2)}) collective-permute-start(bf16[256,1024]{1,0:T(8,128)(2,1)S(1)} %collective-permute-done.5.rows), channel_id=1, source_target_pairs={{4,8},{8,4},{12,14},{14,12},{10,6},{6,10},{2,0},{0,2},{1,5},{5,1},... | collective-permute-start | bytes 1572872 | tf_op jit(solution)/shard_map/ppermute | solution.py:181
  21.6 12.2 %collective-permute-start.7 = (bf16[256,1024]{1,0:T(8,128)(2,1)S(1)}, bf16[256,1024]{1,0:T(8,128)(2,1)S(1)}, u32[]{:S(2)}, u32[]{:S(2)}) collective-permute-start(bf16[256,1024]{1,0:T(8,128)(2,1)S(1)} %meet.3.refs_5_), channel_id=1, source_target_pairs={{0,1},{1,0},{2,3},{3,2},{4,5},{5,4},{6,7},{7,6},{8,9},{9,8},{10,11... | collective-permute-start | bytes 1572872 | tf_op jit(solution)/shard_map/ppermute | solution.py:181
  21.7 13.6 %collective-permute-start.8 = (bf16[1024,256]{1,0:T(8,128)(2,1)S(1)}, bf16[1024,256]{1,0:T(8,128)(2,1)S(1)}, u32[]{:S(2)}, u32[]{:S(2)}) collective-permute-start(bf16[1024,256]{1,0:T(8,128)(2,1)S(1)} %collective-permute-done.4.refs_4_), channel_id=1, source_target_pairs={{4,8},{8,4},{12,14},{14,12},{10,6},{6,10},{2,0},{0,2},{1,5},{5,1},... | collective-permute-start | bytes 1572872 | tf_op jit(solution)/shard_map/ppermute | solution.py:181
  23.3 1.3 %collective-permute-start.10 = (bf16[128,512]{1,0:T(8,128)(2,1)S(1)}, bf16[128,512]{1,0:T(8,128)(2,1)S(1)}, u32[]{:S(2)}, u32[]{:S(2)}) collective-permute-start(bf16[128,512]{1,0:T(8,128)(2,1)S(1)} %get-tuple-element.57.refs_3_), channel_id=1, source_target_pairs={{0,1},{1,0},{2,3},{3,2},{4,5},{5,4},{6,7},{7,6},{8,9},{9,8},{10,11... | collective-permute-start | bytes 393224 | tf_op jit(solution)/shard_map/ppermute | solution.py:181
  23.6 10.2 %collective-permute-start.6 = (bf16[512,256]{1,0:T(8,128)(2,1)S(1)}, bf16[512,256]{1,0:T(8,128)(2,1)S(1)}, u32[]{:S(2)}, u32[]{:S(2)}) collective-permute-start(bf16[512,256]{1,0:T(8,128)(2,1)S(1)} %slice.30), channel_id=1, source_target_pairs={{0,1},{1,0},{2,3},{3,2},{4,5},{5,4},{6,7},{7,6},{8,9},{9,8},{10,11... | collective-permute-start | bytes 786440 | tf_op jit(solution)/shard_map/ppermute | solution.py:181
  24.6 9.1 %collective-permute-start.3 = (bf16[128,1024]{1,0:T(8,128)(2,1)S(1)}, bf16[128,1024]{1,0:T(8,128)(2,1)S(1)}, u32[]{:S(2)}, u32[]{:S(2)}) collective-permute-start(bf16[128,1024]{1,0:T(8,128)(2,1)S(1)} %get-tuple-element.50.refs_1_), channel_id=1, source_target_pairs={{0,1},{1,0},{2,3},{3,2},{4,5},{5,4},{6,7},{7,6},{8,9},{9,8},{10,11... | collective-permute-start | bytes 786440 | tf_op jit(solution)/shard_map/ppermute | solution.py:181
  30.4 9.3 %collective-permute-start.14 = (bf16[256,1024]{1,0:T(8,128)(2,1)S(1)}, bf16[256,1024]{1,0:T(8,128)(2,1)S(1)}, u32[]{:S(2)}, u32[]{:S(2)}) collective-permute-start(bf16[256,1024]{1,0:T(8,128)(2,1)S(1)} %collective-permute-done.9.rows), channel_id=1, source_target_pairs={{0,4},{4,0},{8,12},{12,8},{14,10},{10,14},{6,2},{2,6},{5,9},{9,5},... | collective-permute-start | bytes 1572872 | tf_op jit(solution)/shard_map/ppermute | solution.py:181
  35.3 10.5 %collective-permute-start.12 = (bf16[256,1024]{1,0:T(8,128)(2,1)S(1)}, bf16[256,1024]{1,0:T(8,128)(2,1)S(1)}, u32[]{:S(2)}, u32[]{:S(2)}) collective-permute-start(bf16[256,1024]{1,0:T(8,128)(2,1)S(1)} %meet.4.refs_2_), channel_id=1, source_target_pairs={{0,1},{1,0},{2,3},{3,2},{4,5},{5,4},{6,7},{7,6},{8,9},{9,8},{10,11... | collective-permute-start | bytes 1572872 | tf_op jit(solution)/shard_map/ppermute | solution.py:181
  35.4 11.7 %collective-permute-start.13 = (bf16[1024,256]{1,0:T(8,128)(2,1)S(1)}, bf16[1024,256]{1,0:T(8,128)(2,1)S(1)}, u32[]{:S(2)}, u32[]{:S(2)}) collective-permute-start(bf16[1024,256]{1,0:T(8,128)(2,1)S(1)} %collective-permute-done.8.refs_1_), channel_id=1, source_target_pairs={{0,4},{4,0},{8,12},{12,8},{14,10},{10,14},{6,2},{2,6},{5,9},{9,5},... | collective-permute-start | bytes 1572872 | tf_op jit(solution)/shard_map/ppermute | solution.py:181
  36.0 9.8 %collective-permute-start.11 = (bf16[512,256]{1,0:T(8,128)(2,1)S(1)}, bf16[512,256]{1,0:T(8,128)(2,1)S(1)}, u32[]{:S(2)}, u32[]{:S(2)}) collective-permute-start(bf16[512,256]{1,0:T(8,128)(2,1)S(1)} %slice.31), channel_id=1, source_target_pairs={{0,1},{1,0},{2,3},{3,2},{4,5},{5,4},{6,7},{7,6},{8,9},{9,8},{10,11... | collective-permute-start | bytes 786440 | tf_op jit(solution)/shard_map/ppermute | solution.py:181
  42.5 6.4 %collective-permute-start.17 = (bf16[128,1024]{1,0:T(8,128)(2,1)S(1)}, bf16[128,1024]{1,0:T(8,128)(2,1)S(1)}, u32[]{:S(2)}, u32[]{:S(2)}) collective-permute-start(bf16[128,1024]{1,0:T(8,128)(2,1)S(1)} %slice.33), channel_id=1, source_target_pairs={{4,8},{8,4},{12,14},{14,12},{10,6},{6,10},{2,0},{0,2},{1,5},{5,1},... | collective-permute-start | bytes 786440 | tf_op jit(solution)/shard_map/ppermute | solution.py:181
  47.1 6.4 %collective-permute-start.19 = (bf16[1024,128]{1,0:T(8,128)(2,1)S(1)}, bf16[1024,128]{1,0:T(8,128)(2,1)S(1)}, u32[]{:S(2)}, u32[]{:S(2)}) collective-permute-start(bf16[1024,128]{1,0:T(8,128)(2,1)S(1)} %slice.34), channel_id=1, source_target_pairs={{4,8},{8,4},{12,14},{14,12},{10,6},{6,10},{2,0},{0,2},{1,5},{5,1},... | collective-permute-start | bytes 786440 | tf_op jit(solution)/shard_map/ppermute | solution.py:181
  48.0 5.6 %collective-permute-start.16 = (bf16[256,1024]{1,0:T(8,128)(2,1)S(1)}, bf16[256,1024]{1,0:T(8,128)(2,1)S(1)}, u32[]{:S(2)}, u32[]{:S(2)}) collective-permute-start(bf16[256,1024]{1,0:T(8,128)(2,1)S(1)} %meet.5.refs_2_), channel_id=1, source_target_pairs={{0,1},{1,0},{2,3},{3,2},{4,5},{5,4},{6,7},{7,6},{8,9},{9,8},{10,11... | collective-permute-start | bytes 1572872 | tf_op jit(solution)/shard_map/ppermute | solution.py:181
  48.0 5.6 %collective-permute-start.15 = (bf16[512,256]{1,0:T(8,128)(2,1)S(1)}, bf16[512,256]{1,0:T(8,128)(2,1)S(1)}, u32[]{:S(2)}, u32[]{:S(2)}) collective-permute-start(bf16[512,256]{1,0:T(8,128)(2,1)S(1)} %slice.32), channel_id=1, source_target_pairs={{0,1},{1,0},{2,3},{3,2},{4,5},{5,4},{6,7},{7,6},{8,9},{9,8},{10,11... | collective-permute-start | bytes 786440 | tf_op jit(solution)/shard_map/ppermute | solution.py:181
  51.6 3.4 %collective-permute-start.21 = (bf16[128,1024]{1,0:T(8,128)(2,1)S(1)}, bf16[128,1024]{1,0:T(8,128)(2,1)S(1)}, u32[]{:S(2)}, u32[]{:S(2)}) collective-permute-start(bf16[128,1024]{1,0:T(8,128)(2,1)S(1)} %get-tuple-element.72), channel_id=1, source_target_pairs={{0,1},{1,0},{2,3},{3,2},{4,5},{5,4},{6,7},{7,6},{8,9},{9,8},{10,11... | collective-permute-start | bytes 786440 | tf_op jit(solution)/shard_map/ppermute | solution.py:181
  51.7 3.3 %collective-permute-start.18 = (bf16[128,512]{1,0:T(8,128)(2,1)S(1)}, bf16[128,512]{1,0:T(8,128)(2,1)S(1)}, u32[]{:S(2)}, u32[]{:S(2)}) collective-permute-start(bf16[128,512]{1,0:T(8,128)(2,1)S(1)} %get-tuple-element.70), channel_id=1, source_target_pairs={{0,1},{1,0},{2,3},{3,2},{4,5},{5,4},{6,7},{7,6},{8,9},{9,8},{10,11... | collective-permute-start | bytes 393224 | tf_op jit(solution)/shard_map/ppermute | solution.py:181
  53.5 1.4 %collective-permute-start.20 = (bf16[512,128]{1,0:T(8,128)(2,1)S(1)}, bf16[512,128]{1,0:T(8,128)(2,1)S(1)}, u32[]{:S(2)}, u32[]{:S(2)}) collective-permute-start(bf16[512,128]{1,0:T(8,128)(2,1)S(1)} %get-tuple-element.93), channel_id=1, source_target_pairs={{0,1},{1,0},{2,3},{3,2},{4,5},{5,4},{6,7},{7,6},{8,9},{9,8},{10,11... | collective-permute-start | bytes 393224 | tf_op jit(solution)/shard_map/ppermute | solution.py:181
  55.8 3.0 %collective-permute-start.23 = (bf16[512,512]{1,0:T(8,128)(2,1)S(1)}, bf16[512,512]{1,0:T(8,128)(2,1)S(1)}, u32[]{:S(2)}, u32[]{:S(2)}) collective-permute-start(bf16[512,512]{1,0:T(8,128)(2,1)S(1)} %get-tuple-element.73.sent), channel_id=1, source_target_pairs={{0,1},{1,0},{2,3},{3,2},{4,5},{5,4},{6,7},{7,6},{8,9},{9,8},{10,11... | collective-permute-start | bytes 1572872 | tf_op jit(solution)/shard_map/ppermute | solution.py:181
  56.7 6.4 %collective-permute-start.22 = (bf16[512,256]{1,0:T(8,128)(2,1)S(1)}, bf16[512,256]{1,0:T(8,128)(2,1)S(1)}, u32[]{:S(2)}, u32[]{:S(2)}) collective-permute-start(bf16[512,256]{1,0:T(8,128)(2,1)S(1)} %convolution_convert_fusion), channel_id=1, source_target_pairs={{4,8},{8,4},{12,14},{14,12},{10,6},{6,10},{2,0},{0,2},{1,5},{5,1},... | collective-permute-start | bytes 786440 | tf_op jit(solution)/shard_map/ppermute | solution.py:181
  60.0 6.4 %collective-permute-start.25 = (bf16[512,256]{1,0:T(8,128)(2,1)S(1)}, bf16[512,256]{1,0:T(8,128)(2,1)S(1)}, u32[]{:S(2)}, u32[]{:S(2)}) collective-permute-start(bf16[512,256]{1,0:T(8,128)(2,1)S(1)} %get-tuple-element.80), channel_id=1, source_target_pairs={{0,4},{4,0},{8,12},{12,8},{14,10},{10,14},{6,2},{2,6},{5,9},{9,5},... | collective-permute-start | bytes 786440 | tf_op jit(solution)/shard_map/ppermute | solution.py:181
  63.2 7.0 %collective-permute-start.24 = (bf16[512,256]{1,0:T(8,128)(2,1)S(1)}, bf16[512,256]{1,0:T(8,128)(2,1)S(1)}, u32[]{:S(2)}, u32[]{:S(2)}) collective-permute-start(bf16[512,256]{1,0:T(8,128)(2,1)S(1)} %add_convert_fusion.5), channel_id=1, source_target_pairs={{0,4},{4,0},{8,12},{12,8},{14,10},{10,14},{6,2},{2,6},{5,9},{9,5},... | collective-permute-start | bytes 786440 | tf_op jit(solution)/shard_map/ppermute | solution.py:181
  66.5 6.4 %collective-permute-start.27 = (bf16[512,256]{1,0:T(8,128)(2,1)S(1)}, bf16[512,256]{1,0:T(8,128)(2,1)S(1)}, u32[]{:S(2)}, u32[]{:S(2)}) collective-permute-start(bf16[512,256]{1,0:T(8,128)(2,1)S(1)} %add_convert_fusion.4), channel_id=1, source_target_pairs={{4,8},{8,4},{12,14},{14,12},{10,6},{6,10},{2,0},{0,2},{1,5},{5,1},... | collective-permute-start | bytes 786440 | tf_op jit(solution)/shard_map/ppermute | solution.py:181
  70.3 8.6 %collective-permute-start.26 = (bf16[512,256]{1,0:T(8,128)(2,1)S(1)}, bf16[512,256]{1,0:T(8,128)(2,1)S(1)}, u32[]{:S(2)}, u32[]{:S(2)}) collective-permute-start(bf16[512,256]{1,0:T(8,128)(2,1)S(1)} %add_convert_fusion.3), channel_id=1, source_target_pairs={{4,8},{8,4},{12,14},{14,12},{10,6},{6,10},{2,0},{0,2},{1,5},{5,1},... | collective-permute-start | bytes 786440 | tf_op jit(solution)/shard_map/ppermute | solution.py:181
  73.0 8.4 %collective-permute-start.29 = (bf16[512,256]{1,0:T(8,128)(2,1)S(1)}, bf16[512,256]{1,0:T(8,128)(2,1)S(1)}, u32[]{:S(2)}, u32[]{:S(2)}) collective-permute-start(bf16[512,256]{1,0:T(8,128)(2,1)S(1)} %add_convert_fusion.2), channel_id=1, source_target_pairs={{0,4},{4,0},{8,12},{12,8},{14,10},{10,14},{6,2},{2,6},{5,9},{9,5},... | collective-permute-start | bytes 786440 | tf_op jit(solution)/shard_map/ppermute | solution.py:181
  78.9 6.8 %collective-permute-start.28 = (bf16[512,256]{1,0:T(8,128)(2,1)S(1)}, bf16[512,256]{1,0:T(8,128)(2,1)S(1)}, u32[]{:S(2)}, u32[]{:S(2)}) collective-permute-start(bf16[512,256]{1,0:T(8,128)(2,1)S(1)} %add_convert_fusion.1), channel_id=1, source_target_pairs={{0,4},{4,0},{8,12},{12,8},{14,10},{10,14},{6,2},{2,6},{5,9},{9,5},... | collective-permute-start | bytes 786440 | tf_op jit(solution)/shard_map/ppermute | solution.py:181
  81.4 4.4 %collective-permute-start.30 = (bf16[512,256]{1,0:T(8,128)(2,1)S(1)}, bf16[512,256]{1,0:T(8,128)(2,1)S(1)}, u32[]{:S(2)}, u32[]{:S(2)}) collective-permute-start(bf16[512,256]{1,0:T(8,128)(2,1)S(1)} %collective-permute-done.29), channel_id=1, source_target_pairs={{0,1},{1,0},{2,3},{3,2},{4,5},{5,4},{6,7},{7,6},{8,9},{9,8},{10,11... | collective-permute-start | bytes 786440 | tf_op jit(solution)/shard_map/ppermute | solution.py:181
  85.9 7.3 %collective-permute-start.31 = (bf16[512,256]{1,0:T(8,128)(2,1)S(1)}, bf16[512,256]{1,0:T(8,128)(2,1)S(1)}, u32[]{:S(2)}, u32[]{:S(2)}) collective-permute-start(bf16[512,256]{1,0:T(8,128)(2,1)S(1)} %add_convert_fusion.change), channel_id=1, source_target_pairs={{0,2},{2,0},{1,3},{3,1},{4,6},{6,4},{5,7},{7,5},{8,10},{10,8},{9,1... | collective-permute-start | bytes 786440 | tf_op jit(solution)/shard_map/ppermute | solution.py:181
  (5 other events, 44.9 us)
